TPU v7x, 32 devices: a whole 2x2x4 slice. The times are simulated.
32 devices in a mesh: dp: 8 (over z, y), tensor: 4 (over x, core).
Axes of the slice: x: 2, y: 2, z: 4, core: 2. Of those that a mesh axis runs over, the one named last changes fastest.
Arguments:
- stream_in: float32 [20480, 1024], P(('dp', 'tensor')), may hold values from -27 to 27
- segment_ids: int32 [20480], P('dp'), may hold values from 0 to 103, as said below
- parent_ids: int32 [20480], P('dp'), may hold values from 0 to 95, as said below
- norm_gain_attn: float32 [1024], replicated, may hold values from 0.5 to 1.5
- norm_shift_attn: float32 [1024], replicated, may hold values from -1 to 1
- norm_gain_mlp: float32 [1024], replicated, may hold values from 0.5 to 1.5
- norm_shift_mlp: float32 [1024], replicated, may hold values from -1 to 1
- qkv_weight: float32 [1024, 3072], P('dp', 'tensor'), may hold values from -0.1875 to 0.1875
- qkv_bias: float32 [3072], replicated, may hold values from -1 to 1
- dense_weight: float32 [1024, 1024], P('tensor', 'dp'), may hold values from -3 to 3
- dense_bias: float32 [1024], replicated, may hold values from -1 to 1
- fc_weight: float32 [1024, 4096], P('dp', 'tensor'), may hold values from -0.1875 to 0.1875
- fc_bias: float32 [4096], replicated, may hold values from -1 to 1
- out_weight: float32 [4096, 1024], P('tensor', 'dp'), may hold values from -0.125 to 0.125
- out_bias: float32 [1024], replicated, may hold values from -1 to 1
- out_grad: bfloat16 [20480, 1024], P(('dp', 'tensor')), may hold values from -6 to 6
Outputs:
- output: float32 [20480, 1024], P(('dp', 'tensor'))
- stream_grad: float32 [20480, 1024], P(('dp', 'tensor'))
- gain_attn_grad: float32 [1024], replicated
- shift_attn_grad: float32 [1024], replicated
- gain_mlp_grad: float32 [1024], replicated
- shift_mlp_grad: float32 [1024], replicated
- qkv_weight_grad: float32 [1024, 3072], P('dp', 'tensor')
- qkv_bias_grad: float32 [3072], replicated
- dense_weight_grad: float32 [1024, 1024], P('tensor', 'dp')
- dense_bias_grad: float32 [1024], replicated
- fc_weight_grad: float32 [1024, 4096], P('dp', 'tensor')
- fc_bias_grad: float32 [4096], replicated
- out_weight_grad: float32 [4096, 1024], P('tensor', 'dp')
- out_bias_grad: float32 [1024], replicated
- root_squares: float32 [3], replicated
Inputs may be any that keep to these rules, and one draw needn't show every extreme that they name: `segment_ids`: each tree is 2560 consecutive tokens: its trunk of 1024 tokens first, then 128-token branches and leaves in an order that varies; 4 branches with 2 leaves each; segment numbers are distinct across trees. `parent_ids`: A branch's parent is its tree's trunk, a leaf's parent a branch of the same tree.
All inputs are finite; a program needn't handle non-finite values.
Results may differ from a plain program's by a relative error of at most 0.012.
The roundings to bfloat16 on the way count: a program that leaves them out, or rounds other values in their place, can miss the bound.
Values may be sent and summed in bfloat16 or wider, within the bound.
No kernel may reach another device: no remote copies, remote signals or barrier semaphores. Data moves between devices by JAX's collectives and lax.ppermute only.
A program may use at most 320 MiB of HBM per device.

v0:
```python
import jax
import jax.numpy as jnp
from jax import lax
from jax.sharding import PartitionSpec as P

HD = 64
ROT = 16
TRUNK = 1024
SEG = 128
TREE = 2560


eps_norm = 1e-05
masked_score = -1e30


def contract_first(left, right):
    return lax.dot_general(
        left, right, (((0,), (0,)), ((), ())), preferred_element_type=jnp.float32
    )


def contract_last(left, right):
    return lax.dot_general(
        left, right, (((1,), (1,)), ((), ())), preferred_element_type=jnp.float32
    )


def group_products(left, right, groups):
    rows = left.shape[0]
    inner = left.shape[1] // groups
    parts = jnp.einsum(
        "rgc,gcd->grd",
        left.reshape(rows, groups, inner),
        right.reshape(groups, inner, right.shape[1]),
        preferred_element_type=jnp.float32,
    )
    return jnp.sum(parts.astype(jnp.bfloat16).astype(jnp.float32), axis=0)


def position_tables(segments, parents):
    token_count = segments.shape[0]
    index_all = jnp.arange(token_count, dtype=jnp.int32) % TREE
    root_ids = jnp.repeat(segments.reshape(token_count // TREE, TREE)[:, 0], TREE)
    depth_shift = jnp.where(parents == root_ids, 0, SEG)
    places = jnp.where(
        index_all < TRUNK, index_all, TRUNK + (index_all - TRUNK) % SEG + depth_shift
    )
    half_rot = ROT // 2
    inverse_freq = 10000.0 ** (-(jnp.arange(half_rot, dtype=jnp.float32) * 2.0 / ROT))
    angles = places.astype(jnp.float32)[:, None] * inverse_freq[None, :]
    cosine_table = jnp.concatenate([jnp.cos(angles), jnp.cos(angles)], axis=1)
    sine_table = jnp.concatenate([jnp.sin(angles), jnp.sin(angles)], axis=1)
    return (cosine_table, sine_table, root_ids)


def rotate_forward(field, cosine_table, sine_table):
    half_rot = ROT // 2
    turned_part = field[..., :ROT]
    first_half = turned_part[..., :half_rot]
    second_half = turned_part[..., half_rot:]
    swapped = jnp.concatenate([-second_half, first_half], axis=-1)
    turned = turned_part * cosine_table[:, None, :] + swapped * sine_table[:, None, :]
    return jnp.concatenate([turned, field[..., ROT:]], axis=-1)


def rotate_backward(gradient, cosine_table, sine_table):
    half_rot = ROT // 2
    turned_part = gradient[..., :ROT]
    with_cosine = turned_part * cosine_table[:, None, :]
    with_sine = turned_part * sine_table[:, None, :]
    back = with_cosine + jnp.concatenate(
        [with_sine[..., half_rot:], -with_sine[..., :half_rot]], axis=-1
    )
    return jnp.concatenate([back, gradient[..., ROT:]], axis=-1)


def visible(seg_rows, parent_rows, root_rows, index_rows, seg_cols, index_cols):
    same_seg = (seg_cols[None, :] == seg_rows[:, None]) & (
        index_cols[None, :] <= index_rows[:, None]
    )
    upper_seg = (seg_cols[None, :] == parent_rows[:, None]) & (parent_rows != seg_rows)[:, None]
    rooted_seg = (seg_cols[None, :] == root_rows[:, None]) & (root_rows != seg_rows)[:, None]
    return same_seg | upper_seg | rooted_seg


def block_size():
    return 512


def key_limit(row_end):
    return row_end if row_end <= TRUNK else TREE


def tree_scores(
    queries, key_rows, seg_tree, parent_tree, root_tree, row_start, block_rows, key_end
):
    index_tree = jnp.arange(TREE, dtype=jnp.int32)
    row_end = row_start + block_rows
    allowed = visible(
        seg_tree[row_start:row_end],
        parent_tree[row_start:row_end],
        root_tree[row_start:row_end],
        index_tree[row_start:row_end],
        seg_tree[:key_end],
        index_tree[:key_end],
    )
    raw_scores = jnp.einsum(
        "qhd,khd->hqk",
        queries[row_start:row_end],
        key_rows[:key_end],
        preferred_element_type=jnp.float32,
    )
    return jnp.where(allowed[None], raw_scores * HD ** (-0.5), masked_score)


def forward_tree(pieces):
    queries, key_rows, values, seg_tree, parent_tree, root_tree = pieces
    block_rows = block_size()
    context_parts = []
    total_parts = []
    for block_index in range(TREE // block_rows):
        row_start = block_index * block_rows
        key_end = key_limit(row_start + block_rows)
        scores = tree_scores(
            queries, key_rows, seg_tree, parent_tree, root_tree, row_start, block_rows, key_end
        )
        row_max = jnp.max(scores, axis=-1, keepdims=True)
        exp_total = jnp.sum(jnp.exp(scores - row_max), axis=-1, keepdims=True)
        log_total = row_max + jnp.log(exp_total)
        soft_low = jnp.exp(scores - log_total).astype(jnp.bfloat16)
        context_parts.append(
            jnp.einsum(
                "hqk,khd->qhd", soft_low, values[:key_end], preferred_element_type=jnp.float32
            )
        )
        total_parts.append(log_total[..., 0])
    return (jnp.concatenate(context_parts, axis=0), jnp.concatenate(total_parts, axis=1))


def backward_tree(pieces):
    queries, key_rows, values, seg_tree, parent_tree, root_tree, log_totals, grad_context = pieces
    block_rows = block_size()
    key_grad = jnp.zeros(key_rows.shape, jnp.float32)
    value_grad = jnp.zeros(values.shape, jnp.float32)
    query_parts = []
    for block_index in range(TREE // block_rows):
        row_start = block_index * block_rows
        row_end = row_start + block_rows
        key_end = key_limit(row_end)
        scores = tree_scores(
            queries, key_rows, seg_tree, parent_tree, root_tree, row_start, block_rows, key_end
        )
        soft_full = jnp.exp(scores - log_totals[:, row_start:row_end, None])
        soft_low = soft_full.astype(jnp.bfloat16)
        grad_rows = grad_context[row_start:row_end]
        value_grad = value_grad.at[:key_end].add(
            jnp.einsum("hqk,qhd->khd", soft_low, grad_rows, preferred_element_type=jnp.float32)
        )
        soft_grad = jnp.einsum(
            "qhd,khd->hqk", grad_rows, values[:key_end], preferred_element_type=jnp.float32
        )
        row_delta = jnp.sum(soft_full * soft_grad, axis=-1, keepdims=True)
        score_grad = (soft_full * (soft_grad - row_delta) * HD ** (-0.5)).astype(jnp.bfloat16)
        query_parts.append(
            jnp.einsum(
                "hqk,khd->qhd", score_grad, key_rows[:key_end], preferred_element_type=jnp.float32
            )
        )
        key_grad = key_grad.at[:key_end].add(
            jnp.einsum(
                "hqk,qhd->khd",
                score_grad,
                queries[row_start:row_end],
                preferred_element_type=jnp.float32,
            )
        )
    return (jnp.concatenate(query_parts, axis=0), key_grad, value_grad)


def local(
    stream_in,
    segment_ids,
    parent_ids,
    norm_gain_attn,
    norm_shift_attn,
    norm_gain_mlp,
    norm_shift_mlp,
    qkv_weight,
    qkv_bias,
    dense_weight,
    dense_bias,
    fc_weight,
    fc_bias,
    out_weight,
    out_bias,
    out_grad,
):
    tensor_rank = lax.axis_index("tensor")
    rows_local = stream_in.shape[0]
    group_rows = segment_ids.shape[0]
    qkv_width = qkv_weight.shape[1]
    heads_local = qkv_width // (3 * HD)
    ff_local = fc_weight.shape[1]
    tree_count = group_rows // TREE
    row_mean = jnp.mean(stream_in, axis=-1, keepdims=True)
    centred = stream_in - row_mean
    row_var = jnp.mean(centred * centred, axis=-1, keepdims=True)
    inv_std = lax.rsqrt(row_var + eps_norm)
    normalized = centred * inv_std
    sent_norm = normalized.astype(jnp.bfloat16)
    sent_group = lax.all_gather(sent_norm, "tensor", axis=0, tiled=True)
    qkv_whole, fc_whole, dense_whole, out_whole = (
        lax.all_gather(qkv_weight.astype(jnp.bfloat16), "dp", axis=0, tiled=True),
        lax.all_gather(fc_weight.astype(jnp.bfloat16), "dp", axis=0, tiled=True),
        lax.all_gather(dense_weight.astype(jnp.bfloat16), "dp", axis=1, tiled=True),
        lax.all_gather(out_weight.astype(jnp.bfloat16), "dp", axis=1, tiled=True),
    )
    sent_float = sent_group.astype(jnp.float32)
    normed_attn = (sent_float * norm_gain_attn + norm_shift_attn).astype(jnp.bfloat16)
    normed_mlp = (sent_float * norm_gain_mlp + norm_shift_mlp).astype(jnp.bfloat16)
    qkv_bias_local = lax.dynamic_slice_in_dim(qkv_bias, tensor_rank * qkv_width, qkv_width)
    fc_bias_local = lax.dynamic_slice_in_dim(fc_bias, tensor_rank * ff_local, ff_local)
    qkv = jnp.dot(normed_attn, qkv_whole, preferred_element_type=jnp.float32) + qkv_bias_local
    qkv = qkv.reshape(group_rows, heads_local, 3, HD)
    cosine_table, sine_table, root_ids = position_tables(segment_ids, parent_ids)
    queries = rotate_forward(qkv[:, :, 0], cosine_table, sine_table).astype(jnp.bfloat16)
    key_rows = rotate_forward(qkv[:, :, 1], cosine_table, sine_table).astype(jnp.bfloat16)
    values = qkv[:, :, 2].astype(jnp.bfloat16)
    tree_shape = (tree_count, TREE, heads_local, HD)
    tree_pieces = (
        queries.reshape(tree_shape),
        key_rows.reshape(tree_shape),
        values.reshape(tree_shape),
        segment_ids.reshape(tree_count, TREE),
        parent_ids.reshape(tree_count, TREE),
        root_ids.reshape(tree_count, TREE),
    )
    context, log_totals = lax.map(forward_tree, tree_pieces)
    context_low = context.reshape(group_rows, heads_local * HD).astype(jnp.bfloat16)
    hidden = jnp.dot(normed_mlp, fc_whole, preferred_element_type=jnp.float32) + fc_bias_local
    activated = jax.nn.gelu(hidden, approximate=False).astype(jnp.bfloat16)
    context_own, activated_own = (
        lax.all_to_all(context_low, "tensor", split_axis=0, concat_axis=1, tiled=True),
        lax.all_to_all(activated, "tensor", split_axis=0, concat_axis=1, tiled=True),
    )
    dense_every, out_every = (
        lax.all_gather(dense_whole, "tensor", axis=0, tiled=True),
        lax.all_gather(out_whole, "tensor", axis=0, tiled=True),
    )
    group_count = lax.axis_size("tensor")
    attn_sum = group_products(context_own, dense_every, group_count)
    mlp_sum = group_products(activated_own, out_every, group_count)
    attn_out = attn_sum + dense_bias
    mlp_out = mlp_sum + out_bias
    output = stream_in + attn_out + mlp_out
    grad_group = lax.all_gather(out_grad, "tensor", axis=0, tiled=True)
    grad_activated = contract_last(grad_group, out_whole)
    out_weight_part = contract_first(activated, grad_group)
    hidden_primal, gelu_pullback = jax.vjp(
        lambda field: jax.nn.gelu(field, approximate=False), hidden
    )
    grad_hidden = gelu_pullback(grad_activated)[0].astype(jnp.bfloat16)
    fc_bias_part = jnp.sum(grad_hidden.astype(jnp.float32), axis=0)
    fc_weight_part = contract_first(normed_mlp, grad_hidden)
    grad_normed_mlp = contract_last(grad_hidden, fc_whole)
    grad_context = contract_last(grad_group, dense_whole).astype(jnp.bfloat16)
    dense_weight_part = contract_first(context_low, grad_group)
    query_grad, key_grad, value_grad = lax.map(
        backward_tree, tree_pieces + (log_totals, grad_context.reshape(tree_shape))
    )
    query_grad = rotate_backward(
        query_grad.reshape(group_rows, heads_local, HD), cosine_table, sine_table
    )
    key_grad = rotate_backward(
        key_grad.reshape(group_rows, heads_local, HD), cosine_table, sine_table
    )
    value_grad = value_grad.reshape(group_rows, heads_local, HD)
    grad_qkv = jnp.stack([query_grad, key_grad, value_grad], axis=2).reshape(group_rows, qkv_width)
    grad_qkv = grad_qkv.astype(jnp.bfloat16)
    qkv_bias_part = jnp.sum(grad_qkv.astype(jnp.float32), axis=0)
    qkv_weight_part = contract_first(normed_attn, grad_qkv)
    grad_normed_attn = contract_last(grad_qkv, qkv_whole)
    gain_attn_part = jnp.sum(grad_normed_attn * sent_float, axis=0)
    shift_attn_part = jnp.sum(grad_normed_attn, axis=0)
    gain_mlp_part = jnp.sum(grad_normed_mlp * sent_float, axis=0)
    shift_mlp_part = jnp.sum(grad_normed_mlp, axis=0)
    grad_sent_part = grad_normed_attn * norm_gain_attn + grad_normed_mlp * norm_gain_mlp
    grad_sent = lax.psum_scatter(
        grad_sent_part.astype(jnp.bfloat16), "tensor", scatter_dimension=0, tiled=True
    ).astype(jnp.float32)
    mean_grad = jnp.mean(grad_sent, axis=-1, keepdims=True)
    mean_cross = jnp.mean(grad_sent * normalized, axis=-1, keepdims=True)
    stream_grad = out_grad.astype(jnp.float32) + inv_std * (
        grad_sent - mean_grad - normalized * mean_cross
    )
    qkv_weight_grad, fc_weight_grad, dense_weight_grad, out_weight_grad = (
        lax.psum_scatter(
            qkv_weight_part.astype(jnp.bfloat16), "dp", scatter_dimension=0, tiled=True
        ).astype(jnp.float32),
        lax.psum_scatter(
            fc_weight_part.astype(jnp.bfloat16), "dp", scatter_dimension=0, tiled=True
        ).astype(jnp.float32),
        lax.psum_scatter(
            dense_weight_part.astype(jnp.bfloat16), "dp", scatter_dimension=1, tiled=True
        ).astype(jnp.float32),
        lax.psum_scatter(
            out_weight_part.astype(jnp.bfloat16), "dp", scatter_dimension=1, tiled=True
        ).astype(jnp.float32),
    )
    residual_part = jnp.sum(out_grad.astype(jnp.float32), axis=0)
    qkv_bias_spread = lax.dynamic_update_slice(
        jnp.zeros(qkv_bias.shape, jnp.float32), qkv_bias_part, (tensor_rank * qkv_width,)
    )
    fc_bias_spread = lax.dynamic_update_slice(
        jnp.zeros(fc_bias.shape, jnp.float32), fc_bias_part, (tensor_rank * ff_local,)
    )
    (
        gain_attn_grad,
        shift_attn_grad,
        gain_mlp_grad,
        shift_mlp_grad,
        residual_grad,
        qkv_bias_grad,
        fc_bias_grad,
        output_square,
        attn_square,
        mlp_square,
    ) = lax.psum(
        (
            gain_attn_part,
            shift_attn_part,
            gain_mlp_part,
            shift_mlp_part,
            residual_part,
            qkv_bias_spread,
            fc_bias_spread,
            jnp.sum(output * output),
            jnp.sum(attn_out * attn_out),
            jnp.sum(mlp_out * mlp_out),
        ),
        ("dp", "tensor"),
    )
    count_all = float(
        rows_local * lax.axis_size("dp") * lax.axis_size("tensor") * stream_in.shape[1]
    )
    root_squares = jnp.sqrt(jnp.stack([output_square, attn_square, mlp_square]) / count_all)
    return (
        output,
        stream_grad,
        gain_attn_grad,
        shift_attn_grad,
        gain_mlp_grad,
        shift_mlp_grad,
        qkv_weight_grad,
        qkv_bias_grad,
        dense_weight_grad,
        residual_grad,
        fc_weight_grad,
        fc_bias_grad,
        out_weight_grad,
        residual_grad,
        root_squares,
    )


def solution(mesh):
    placed = (
        P(("dp", "tensor"), None),
        P("dp"),
        P("dp"),
        P(),
        P(),
        P(),
        P(),
        P("dp", "tensor"),
        P(),
        P("tensor", "dp"),
        P(),
        P("dp", "tensor"),
        P(),
        P("tensor", "dp"),
        P(),
        P(("dp", "tensor"), None),
    )
    return jax.shard_map(
        local,
        mesh=mesh,
        in_specs=placed,
        out_specs=(
            P(("dp", "tensor"), None),
            P(("dp", "tensor"), None),
            P(),
            P(),
            P(),
            P(),
            P("dp", "tensor"),
            P(),
            P("tensor", "dp"),
            P(),
            P("dp", "tensor"),
            P(),
            P("tensor", "dp"),
            P(),
            P(),
        ),
        check_vma=False,
    )
```

profile of v0, /device:TPU:0, one launch (start us, length us, event | category | flops | bytes accessed | tf_op | source)
XLA Modules:
  0.0 1078.6 jit_solution(15230396105723233312)
XLA Ops:
  18.3 33.0 %all_gather.26 = bf16[256,1024]{1,0:T(8,128)(2,1)} all-gather(bf16[256,128]{1,0:T(8,128)(2,1)S(1)} %convert_element_type.175), channel_id=1, replica_groups=mesh['dp'=8,'tensor'=4] {'dp'}, dimensions={1}, use_global_device_ids=true | all-gather | bytes 589824 | tf_op jit(solution)/shard_map/all_gather | solution.py:216
  59.7 9.0 fusion.112
  68.8 34.1 %all-gather.8.cloned.1.call-done = bf16[2560,1024]{1,0:T(8,128)(2,1)} async-done(((bf16[640,1024]{1,0:T(8,128)(2,1)}), bf16[2560,1024]{1,0:T(8,128)(2,1)}) %all-gather.8.cloned.1.call-update) | async-done | bytes 5242896 | tf_op jit(solution)/shard_map/all_gather | solution.py:212
  102.9 6.9 convolution_add_fusion
  109.8 2.5 copy.67
  116.5 28.5 %all-gather.20.cloned.1.call-done = bf16[2560,1024]{1,0:T(8,128)(2,1)} async-done(((bf16[640,1024]{1,0:T(8,128)(2,1)}), bf16[2560,1024]{1,0:T(8,128)(2,1)}) %all-gather.20.cloned.1.call-update) | async-done | bytes 5242896 | tf_op jit(solution)/shard_map/all_gather | solution.py:257
  145.0 4.3 convolution_convert_fusion
  155.1 3.9 fusion.253
  161.0 8.7 fusion.207
  169.7 9.8 fusion.204
  179.4 4.3 fusion.213
  185.6 5.5 fusion.248
  192.8 3.2 copy-done.2
  196.0 2.4 exponential_reduce_fusion.3
  198.5 18.0 %fusion.218 = f32[2560,4,64]{0,2,1:T(8,128)} fusion(f32[2560,4,64]{0,2,1:T(8,128)} %fusion.204, f32[4,512,1024]{2,1,0:T(8,128)} %fusion.248, f32[4,512,1024]{2,1,0:T(8,128)} %copy-done.2, f32[4,512]{1,0:T(4,128)S(1)} %log_add_fusion.3, pred[512,1024]{1,0:T(8,128)(4,1)S(1)} %and_or_fusion, bf16[2560,4,48]{0,2,1:T(8,128)(2,1)S(1)} %slice.741, ...), kind=kOutput, calls=%fused_computation.211 | convolution fusion | flops 292555776 | bytes 36454400 | tf_op jit(solution)/shard_map/while/body/eval_jaxpr/hqk,khd->qhd/dot_general | solution.py:166
  216.6 23.2 %fusion.197 = f32[2560,4,64]{0,2,1:T(8,128)} fusion(f32[2560,4,64]{0,2,1:T(8,128)} %scatter-add.14, f32[4,512,1024]{2,1,0:T(8,128)} %fusion.248, f32[4,512,1024]{2,1,0:T(8,128)} %copy-done.2, f32[4,512]{1,0:T(4,128)S(1)} %log_add_fusion.3, pred[512,1024]{1,0:T(8,128)(4,1)S(1)} %and_or_fusion, bf16[2560,4,48]{0,2,1:T(8,128)(2,1)S(1)} %slice.742, ...), kind=kOutput, calls=%fused_computation.187 | convolution fusion | flops 292293632 | bytes 38027264 | tf_op jit(solution)/shard_map/while/body/eval_jaxpr/hqk,qhd->khd/dot_general | solution.py:171
  239.8 10.1 fusion.247
  249.9 9.0 fusion.246
  258.8 8.6 fusion.245
  267.5 5.6 fusion.10
  273.1 7.3 exponential_reduce_fusion
  280.5 5.5 fusion.8
  286.0 7.1 exponential_reduce_fusion.2
  293.5 5.5 fusion.9
  299.0 7.1 exponential_reduce_fusion.1
  306.5 40.6 %fusion.140 = f32[2560,4,64]{0,2,1:T(8,128)} fusion(f32[4,512,2560]{2,1,0:T(8,128)} %fusion.246, f32[4,512,2560]{2,1,0:T(8,128)} %copy-done.4, f32[4,512]{1,0:T(4,128)S(1)} %log_add_fusion.1, pred[512,2560]{1,0:T(8,128)(4,1)} %get-tuple-element.354, bf16[2560,4,48]{0,2,1:T(8,128)(2,1)S(1)} %slice.742, bf16[2560,4,16]{0,2,1:T(8,128)(2,1)S(1)} %get-tuple-element.341), kind=kOutput, calls=%fused_computation.132 | convolution fusion | flops 729289216 | bytes 90456064 | tf_op jit(solution)/shard_map/while/body/eval_jaxpr/hqk,qhd->khd/dot_general | solution.py:171
  347.1 38.3 %fusion.236 = f32[2560,4,64]{0,2,1:T(8,128)} fusion(f32[2560,4,64]{0,2,1:T(8,128)} %fusion.218, f32[4,512,2560]{2,1,0:T(8,128)} %fusion.247, f32[4,512,2560]{2,1,0:T(8,128)} %copy-done.5, f32[4,512]{1,0:T(4,128)S(1)} %log_add_fusion.2, pred[512,2560]{1,0:T(8,128)(4,1)} %get-tuple-element.353, bf16[2560,4,48]{0,2,1:T(8,128)(2,1)S(1)} %slice.741, ...), kind=kOutput, calls=%fused_computation.217 | convolution fusion | flops 731386368 | bytes 88358912 | tf_op jit(solution)/shard_map/while/body/eval_jaxpr/hqk,khd->qhd/dot_general | solution.py:166
  385.4 37.8 %fusion.230 = f32[2560,4,64]{0,2,1:T(8,128)} fusion(f32[2560,4,64]{0,2,1:T(8,128)} %fusion.236, f32[4,512,2560]{2,1,0:T(8,128)} %fusion.246, f32[4,512,2560]{2,1,0:T(8,128)} %copy-done.4, f32[4,512]{1,0:T(4,128)S(1)} %log_add_fusion.1, pred[512,2560]{1,0:T(8,128)(4,1)} %get-tuple-element.354, bf16[2560,4,48]{0,2,1:T(8,128)(2,1)S(1)} %slice.741, ...), kind=kOutput, calls=%fused_computation.215 | convolution fusion | flops 731386368 | bytes 88358912 | tf_op jit(solution)/shard_map/while/body/eval_jaxpr/hqk,khd->qhd/dot_general | solution.py:166
  423.2 40.6 %fusion.137 = f32[2560,4,64]{0,2,1:T(8,128)} fusion(bf16[512,4,64]{0,2,1:T(8,128)(2,1)S(1)} %copy-done.43, f32[4,512,2560]{2,1,0:T(8,128)} %fusion.245, f32[4,512,2560]{2,1,0:T(8,128)} %copy-done.3, f32[4,512]{1,0:T(4,128)S(1)} %log_add_fusion, pred[512,2560]{1,0:T(8,128)(4,1)} %get-tuple-element.352), kind=kOutput, calls=%fused_computation.131 | convolution fusion | flops 728764928 | bytes 46145536 | tf_op jit(solution)/shard_map/while/body/eval_jaxpr/hqk,qhd->khd/dot_general | solution.py:171
  463.8 37.8 %fusion.224 = f32[2560,4,64]{0,2,1:T(8,128)} fusion(f32[2560,4,64]{0,2,1:T(8,128)} %fusion.230, f32[4,512,2560]{2,1,0:T(8,128)} %fusion.245, f32[4,512,2560]{2,1,0:T(8,128)} %copy-done.3, f32[4,512]{1,0:T(4,128)S(1)} %log_add_fusion, pred[512,2560]{1,0:T(8,128)(4,1)} %get-tuple-element.352, bf16[2560,4,48]{0,2,1:T(8,128)(2,1)S(1)} %slice.741, ...), kind=kOutput, calls=%fused_computation.213 | convolution fusion | flops 731386368 | bytes 88358912 | tf_op jit(solution)/shard_map/while/body/eval_jaxpr/hqk,khd->qhd/dot_general | solution.py:166
  501.7 41.5 %fusion.156 = f32[2560,4,64]{0,2,1:T(8,128)} fusion(f32[2560,4,64]{0,2,1:T(8,128)} %fusion.137, f32[2560,4,64]{0,2,1:T(8,128)} %fusion.140, f32[2560,4,64]{0,2,1:T(8,128)} %fusion.197, f32[4,512,2560]{2,1,0:T(8,128)} %fusion.247, f32[4,512,2560]{2,1,0:T(8,128)} %copy-done.5, f32[4,512]{1,0:T(4,128)S(1)} %log_add_fusion.2, ...), kind=kOutput, calls=%fused_computation.143 | convolution fusion | flops 731255296 | bytes 98320384 | tf_op jit(solution)/shard_map/while/body/eval_jaxpr/hqk,qhd->khd/dot_general | solution.py:171
  543.2 2.7 slice.646
  545.9 2.6 slice.642
  548.5 2.4 slice_multiply_fusion.3
  551.3 5.0 fusion.193
  557.3 2.3 fusion.214
  559.7 11.7 %fusion.149 = f32[2560,4,64]{0,2,1:T(8,128)} fusion(f32[2560,4,64]{0,2,1:T(8,128)S(1)} %fusion.193, bf16[512,4,64]{0,2,1:T(8,128)(2,1)S(1)} %bitcast.184, f32[4,512,2560]{2,1,0:T(8,128)} %copy-done.5, f32[4,512]{1,0:T(4,128)S(1)} %log_add_fusion.2, pred[512,2560]{1,0:T(8,128)(4,1)S(1)} %copy-done.13), kind=kOutput, calls=%fused_computation.140 | convolution fusion | flops 692715520 | bytes 27795456 | tf_op jit(solution)/shard_map/while/body/eval_jaxpr/hqk,qhd->khd/dot_general | solution.py:158
  571.4 9.8 fusion.212
  581.3 10.4 fusion.211
  591.7 9.8 fusion.210
  602.7 2.3 convolution_convert_fusion.2
  610.6 10.2 fusion.148
  620.8 10.4 fusion.147
  635.1 9.2 fusion.186
  644.4 11.2 %fusion.161 = f32[2560,1024]{1,0:T(8,128)} fusion(bf16[1024,1024]{1,0:T(8,128)(2,1)} %all-gather.14.cloned.1.call-done, bf16[2560,1024]{1,0:T(8,128)(2,1)} %all-gather.8.cloned.1.call-done, f32[1024]{0:T(1024)S(1)} %copy-done.60, f32[1024]{0:T(1024)S(1)} %copy-done.63), kind=kOutput, calls=%fused_computation.145 | convolution fusion | flops 5379194880 | bytes 17833984 | tf_op jit(solution)/shard_map/dot_general | solution.py:241
  655.6 33.9 %convert_reduce_fusion = (f32[1024]{0:T(1024)S(1)}, bf16[2560,1024]{1,0:T(8,128)(2,1)}, f32[2560,1024]{1,0:T(8,128)}) fusion(f32[2560,1024]{1,0:T(8,128)} %fusion.161, f32[1024]{0:T(1024)S(1)} %copy-done.51, bf16[2560,1024]{1,0:T(8,128)(2,1)} %all-gather.20.cloned.1.call-done, bf16[1024,1024]{1,0:T(8,128)(2,1)} %all-gather.16.cloned.1.call-done), kind=kOutput, calls=%fused_computation.47 | convolution fusion | flops 5565316096 | bytes 33562624 | tf_op jit(solution)/shard_map/dot_general | solution.py:24
  689.6 12.3 %multiply_convert_fusion.3 = bf16[2560,1024]{1,0:T(8,128)(2,1)} fusion(f32[2560,1024]{1,0:T(8,128)} %get-tuple-element.316, f32[2560,1024]{1,0:T(8,128)} %fusion.161, f32[1024]{0:T(1024)S(1)} %copy-done.51), kind=kLoop, calls=%fused_computation.51 | loop fusion | flops 10485760 | bytes 26218496 | tf_op jit(solution)/shard_map/convert_element_type | solution.py:242
  701.8 9.4 convolution_convert_fusion.1
  711.2 2.6 copy.64
  713.9 10.2 fusion.183
  724.8 7.2 fusion.336
  732.1 15.2 %fusion.328 = (f32[1024]{0:T(1024)S(1)}, f32[1024]{0:T(1024)S(1)}, bf16[2560,1024]{1,0:T(8,128)(2,1)}, f32[1024]{0:T(1024)S(1)}, f32[1024]{0:T(1024)S(1)}) fusion(bf16[2560,1024]{1,0:T(8,128)(2,1)} %all-gather.8.cloned.1.call-done, f32[1024]{0:T(1024)S(1)} %copy-done.63, f32[2560,1024]{1,0:T(8,128)S(1)} %fusion.336, f32[1024]{0:T(1024)S(1)} %copy-done.62, ...), kind=kOutput, calls=%fused_computation.332 | convolution fusion | flops 5397540864 | bytes 28336128 | tf_op jit(solution)/shard_map/dot_general | solution.py:24
  750.4 19.7 %all_to_all.29 = bf16[4,640,256]{2,1,0:T(8,128)(2,1)S(1)} all-to-all(bf16[4,640,256]{2,1,0:T(8,128)(2,1)S(1)} %copy.52), channel_id=1, replica_groups=mesh['dp'=8,'tensor'=4] {'tensor'}, dimensions={0} | all-to-all | bytes 2621440 | tf_op jit(solution)/shard_map/all_to_all | solution.py:244
  770.1 5.3 all-to-all-start.1
  776.1 4.8 convert_reduce_fusion.2
  784.2 50.7 %reduce-scatter.18.cloned.1.call-done = bf16[128,1024]{1,0:T(8,128)(2,1)} async-done(((bf16[1024,1024]{1,0:T(8,128)(2,1)}), bf16[128,1024]{1,0:T(8,128)(2,1)}) %reduce-scatter.18.cloned.1.call-update) | async-done | bytes 262160
  836.9 69.0 %reduce-scatter.14.cloned.1.call-done = bf16[128,1024]{1,0:T(8,128)(2,1)} async-done(((bf16[1024,1024]{1,0:T(8,128)(2,1)}), bf16[128,1024]{1,0:T(8,128)(2,1)}) %reduce-scatter.14.cloned.1.call-update) | async-done | bytes 262160 | tf_op jit(solution)/shard_map/reduce_scatter | solution.py:301
  907.6 57.1 %all-gather.18.cloned.1.call-done = bf16[4096,1024]{1,0:T(8,128)(2,1)} async-done(((bf16[1024,1024]{1,0:T(8,128)(2,1)}), bf16[4096,1024]{1,0:T(8,128)(2,1)}) %all-gather.18.cloned.1.call-update) | async-done | bytes 8388624 | tf_op jit(solution)/shard_map/all_gather | solution.py:249
  964.7 11.9 %convert_reduce_fusion.1 = f32[640,1024]{1,0:T(8,128)} fusion(bf16[4,1024,1024]{2,1,0:T(8,128)(2,1)} %bitcast.191, bf16[4,640,1024]{2,1,0:T(8,128)(2,1)} %all-to-all-done.1), kind=kOutput, calls=%fused_computation.50 | convolution fusion | flops 5375918080 | bytes 16252928 | tf_op jit(solution)/shard_map/rgc,gcd->grd/dot_general | solution.py:32
  976.6 41.9 %reduce-scatter.10.cloned.1.call-done = bf16[640,1024]{1,0:T(8,128)(2,1)} async-done(((bf16[2560,1024]{1,0:T(8,128)(2,1)}), bf16[640,1024]{1,0:T(8,128)(2,1)}) %reduce-scatter.10.cloned.1.call-update) | async-done | bytes 1310736 | tf_op jit(solution)/shard_map/reduce_scatter | solution.py:289
  1018.5 2.4 convert_reduce_fusion.4
  1021.0 6.7 multiply_reduce_fusion.7
  1027.6 40.9 %all-reduce.2 = (f32[1024]{0:T(1024)}, f32[1024]{0:T(1024)}, f32[1024]{0:T(1024)}, f32[1024]{0:T(1024)}, f32[3072]{0:T(1024)}, /*index=5*/f32[1024]{0:T(1024)S(1...) all-reduce(f32[1024]{0:T(1024)S(1)} %get-tuple-element.320, ...), channel_id=1, replica_groups=mesh['dp'=8,'tensor'=4] {'dp','tensor'}, use_global_device_ids=true, to_apply=%region_23.24 | all-reduce | flops 12291 | bytes 98328 | tf_op jit(solution)/shard_map/psum | solution.py:329
  1068.5 2.4 fusion.272
  (244 shorter events, 59.7 us)
Async XLA Ops:
  7.2 6.2 copy-start
  7.2 61.6 %all-gather.10.cloned.1.call-start = ((), (), s32[]{:S(2)}) async-start(), calls=%async_computation.8 | async-start | bytes 1769472 | tf_op jit(solution)/shard_map/all_gather | solution.py:214
  9.1 93.8 %all-gather.8.cloned.1.call-start = ((), (), s32[]{:S(2)}) async-start(), calls=%async_computation.7 | async-start | bytes 6553600 | tf_op jit(solution)/shard_map/all_gather | solution.py:212
  11.1 7.1 copy-start.45
  11.1 7.1 copy-start.44
  13.3 38.1 %copy-start.42 = (s32[2560]{0:T(1024)S(1)}, s32[2560]{0:T(1024)}, u32[]{:S(2)}) copy-start(s32[2560]{0:T(1024)} %param.49) | copy-start | bytes 30724
  13.3 40.0 %copy-start.47 = (s32[2560]{0:T(1024)S(1)}, s32[2560]{0:T(1024)}, u32[]{:S(2)}) copy-start(s32[2560]{0:T(1024)} %param.50) | copy-start | bytes 30724
  13.4 44.5 %copy-start.48 = (f32[640]{0:T(1024)}, f32[640]{0:T(1024)S(1)}, u32[]{:S(2)}) copy-start(f32[640]{0:T(1024)S(1)} %add_rsqrt_fusion) | copy-start | bytes 7684
  13.4 44.9 %slice-start.2 = ((s32[2560]{0:T(1024)}), s32[1024]{0:T(1024)S(1)}, s32[]{:S(2)}) async-start(s32[2560]{0:T(1024)} %param.49), calls=%async_computation.21 | async-start | bytes 8192 | tf_op jit(solution)/shard_map/while/body/eval_jaxpr/slice | solution.py:105
  14.8 88.1 %copy-start.58 = (f32[1024]{0:T(1024)S(1)}, f32[1024]{0:T(1024)}, u32[]{:S(2)}) copy-start(f32[1024]{0:T(1024)} %param.52) | copy-start | bytes 12292
  14.8 88.1 %copy-start.61 = (f32[1024]{0:T(1024)S(1)}, f32[1024]{0:T(1024)}, u32[]{:S(2)}) copy-start(f32[1024]{0:T(1024)} %param.51) | copy-start | bytes 12292
  14.8 130.1 %all-gather.20.cloned.1.call-start = ((), (), s32[]{:S(2)}) async-start(), calls=%async_computation.13 | async-start | bytes 6553600 | tf_op jit(solution)/shard_map/all_gather | solution.py:257
  15.6 628.8 %all-gather.14.cloned.1.call-start = ((), (), s32[]{:S(2)}) async-start(), calls=%async_computation.10 | async-start | bytes 2359296 | tf_op jit(solution)/shard_map/all_gather | solution.py:215
  16.4 639.3 %all-gather.16.cloned.1.call-start = ((), (), s32[]{:S(2)}) async-start(), calls=%async_computation.11 | async-start | bytes 2359296 | tf_op jit(solution)/shard_map/all_gather | solution.py:217
  18.2 757.9 %all-gather.12.cloned.1.call-start = ((), (), s32[]{:S(2)}) async-start(), calls=%async_computation.9 | async-start | bytes 2621440 | tf_op jit(solution)/shard_map/all_gather | solution.py:248
  51.3 729.6 %reduce-scatter.16.cloned.1.call-start = ((), (), s32[]{:S(2)}) async-start(), calls=%async_computation.17 | async-start | bytes 589824
  59.7 156.8 %copy-start.14 = (pred[512,1024]{1,0:T(8,128)(4,1)}, pred[512,1024]{1,0:T(8,128)(4,1)S(1)}, u32[]{:S(2)}) copy-start(pred[512,1024]{1,0:T(8,128)(4,1)S(1)} %and_or_fusion) | copy-start | bytes 1572868
  144.9 5.3 copy-start.19
  144.9 5.3 copy-start.21
  144.9 5.3 copy-start.23
  144.9 5.3 copy-start.24
  144.9 5.3 copy-start.25
  145.0 5.3 copy-start.26
  179.4 6.2 copy-start.36
  198.5 18.1 %copy-start.52 = (f32[4,512]{1,0:T(4,128)}, f32[4,512]{1,0:T(4,128)S(1)}, u32[]{:S(2)}) copy-start(f32[4,512]{1,0:T(4,128)S(1)} %log_add_fusion.3) | copy-start | bytes 24580
  216.5 23.2 %copy-start.34 = (bf16[512,256]{0,1:T(8,128)(2,1)S(1)}, bf16[512,256]{0,1:T(8,128)(2,1)}, u32[]{:S(2)}) copy-start(bf16[512,256]{0,1:T(8,128)(2,1)} %get-tuple-element.334) | copy-start | bytes 786436
  239.8 10.1 copy-start.6
  239.8 10.1 copy-start.32
  249.9 9.0 copy-start.30
  258.8 8.7 copy-start.43
  273.1 7.4 copy-start.3
  286.0 7.4 copy-start.5
  299.0 7.4 copy-start.4
  501.7 46.8 %copy-start.22 = (f32[2560,16]{0,1:T(8,128)S(1)}, f32[2560,16]{0,1:T(8,128)}, u32[]{:S(2)}) copy-start(f32[2560,16]{0,1:T(8,128)} %get-tuple-element.391) | copy-start | bytes 491524
  543.1 7.8 copy-start.40
  543.1 8.1 copy-start.15
  543.2 8.1 copy-start.37
  543.2 8.1 copy-start.53
  548.5 7.8 slice-start
  551.2 5.1 slice-start.1
  551.2 5.8 copy-start.7
  551.2 6.1 copy-start.27
  571.4 9.8 copy-start.12
  581.3 10.4 copy-start.11
  581.3 21.4 %slice-start.3 = ((s8[5242880]{0:T(1024)(128)(4,1)}), s8[4194304]{0:T(1024)(128)(4,1)S(1)}, s32[]{:S(2)}) async-start(s8[5242880]{0:T(1024)(128)(4,1)} %bitcast.192), calls=%async_computation.22 | async-start | bytes 8388608
  591.7 11.0 %slice-start.4 = ((s8[5242880]{0:T(1024)(128)(4,1)}), s8[1048576]{0:T(1024)(128)(4,1)S(1)}, s32[]{:S(2)}) async-start(s8[5242880]{0:T(1024)(128)(4,1)} %bitcast.192), calls=%async_computation.23 | async-start | bytes 2097152
  602.7 5.7 copy-start.20
  610.6 10.2 copy-start.31
  635.0 147.5 %reduce-scatter.12.cloned.1.call-start = ((), (), s32[]{:S(2)}) async-start(), calls=%async_computation.15 | async-start | bytes 1769472 | tf_op jit(solution)/shard_map/reduce_scatter | solution.py:298
  635.0 9.3 copy-start.60
  635.1 9.3 copy-start.63
  644.3 11.3 %copy-start.51 = (f32[1024]{0:T(1024)S(1)}, f32[1024]{0:T(1024)}, u32[]{:S(2)}) copy-start(f32[1024]{0:T(1024)} %dynamic_slice.38) | copy-start | bytes 12292
  644.3 190.6 %reduce-scatter.18.cloned.1.call-start = ((), (), s32[]{:S(2)}) async-start(), calls=%async_computation.18 | async-start | bytes 2359296
  713.8 192.0 %reduce-scatter.14.cloned.1.call-start = ((), (), s32[]{:S(2)}) async-start(), calls=%async_computation.16 | async-start | bytes 2359296 | tf_op jit(solution)/shard_map/reduce_scatter | solution.py:301
  724.0 240.6 %all-gather.18.cloned.1.call-start = ((), (), s32[]{:S(2)}) async-start(), calls=%async_computation.12 | async-start | bytes 10485760 | tf_op jit(solution)/shard_map/all_gather | solution.py:249
  724.8 7.3 copy-start.57
  724.8 293.7 %reduce-scatter.10.cloned.1.call-start = ((), (), s32[]{:S(2)}) async-start(), calls=%async_computation.14 | async-start | bytes 6553600 | tf_op jit(solution)/shard_map/reduce_scatter | solution.py:289
  770.1 5.3 copy-start.50
  770.1 137.5 %all-to-all-start.1 = ((bf16[4,640,1024]{2,1,0:T(8,128)(2,1)}), bf16[4,640,1024]{2,1,0:T(8,128)(2,1)}, u32[]{:S(2)}, u32[]{:S(2)}) async-start(bf16[4,640,1024]{2,1,0:T(8,128)(2,1)} %bitcast.173), calls=%async_computation.1 | async-start | bytes 10485760 | tf_op jit(solution)/shard_map/all_to_all | solution.py:245
  964.7 53.8 %copy-start.1 = (f32[640,1024]{1,0:T(8,128)S(1)}, f32[640,1024]{1,0:T(8,128)}, u32[]{:S(2)}) copy-start(f32[640,1024]{1,0:T(8,128)} %param.48) | copy-start | bytes 7864324
  964.7 53.8 %copy-start.46 = (f32[640]{0:T(1024)S(1)}, f32[640]{0:T(1024)}, u32[]{:S(2)}) copy-start(f32[640]{0:T(1024)} %copy-done.45) | copy-start | bytes 7684
  964.7 53.8 %copy-start.49 = (f32[640]{0:T(1024)S(1)}, f32[640]{0:T(1024)}, u32[]{:S(2)}) copy-start(f32[640]{0:T(1024)} %copy-done.48) | copy-start | bytes 7684
  964.7 56.3 %copy-start.55 = (f32[1024]{0:T(1024)S(1)}, f32[1024]{0:T(1024)}, u32[]{:S(2)}) copy-start(f32[1024]{0:T(1024)} %param.62) | copy-start | bytes 12292
  964.7 56.3 %copy-start.56 = (f32[1024]{0:T(1024)S(1)}, f32[1024]{0:T(1024)}, u32[]{:S(2)}) copy-start(f32[1024]{0:T(1024)} %param.58) | copy-start | bytes 12292
  (19 other events, 49.4 us)
Sparse Core Ops, SparseCore 0:
  10.8 50.6 all-gather.9
  63.7 39.1 all-gather.7
  104.5 40.4 all-gather.19
  146.9 49.4 all-gather.13
  198.3 49.5 all-gather.15
  249.3 20.7 all-gather.11
  635.1 61.7 reduce-scatter.15
  700.7 63.8 reduce-scatter.11
  768.2 66.6 reduce-scatter.17
  838.9 66.9 reduce-scatter.13
  907.4 57.2 all-gather.17
  967.1 51.3 reduce-scatter.9
where the time goes:
time: 1080 us
  matrix products  555 us (51%)
  waiting for transfers between devices  283 us (26%)
  blocking collectives  93.6 us (9%)
  other arithmetic  88.5 us (8%)
  local copies, waits for them, and re-layouts  37.3 us (3%)
  between operations  15.5 us (1%)
    dot_general x5, matrix products, backward_tree(): jnp.einsum('hqk,qhd->khd', score_grad, queries[row_start:row_end], prefer...  155 us
    dot_general x5, matrix products, backward_tree(): jnp.einsum('hqk,khd->qhd', score_grad, key_rows[:key_end], preferred_elem...  142 us
    reduce_scatter x1, waiting for transfers between devices, local(): lax.psum_scatter(fc_weight_part.astype(jnp.bfloat16), 'dp', scatter_dimen...  69 us
    dot_general x4, matrix products, contract_last(): lax.dot_general(left, right, (((1,), (1,)), ((), ())), preferred_element_...  60.6 us
    all_gather x1, waiting for transfers between devices, local(): lax.all_gather(out_whole, 'tensor', axis=0, tiled=True)  57.1 us
    unnamed x14, waiting for transfers between devices  52.2 us
    reduce_scatter x1, waiting for transfers between devices, local(): lax.psum_scatter(grad_sent_part.astype(jnp.bfloat16), 'tensor', scatter_d...  41.9 us
    psum x1, blocking collectives, local(): lax.psum((gain_attn_part, shift_attn_part, gain_mlp_part, shift_mlp_part,...  40.9 us
  transfers between devices with their start and end apart: 13, of which 6 were waited for; matrix products, arithmetic and copies ran while one was open for 61% of the time, Pallas kernels for 0%

commit v1 on v0

v1 whole, which is shorter than its diff:
```python
import jax
import jax.numpy as jnp
from jax import lax
from jax.experimental import pallas as pl
from jax.experimental.pallas import tpu as pltpu
from jax.sharding import PartitionSpec as P

HD = 64
ROT = 16
TRUNK = 1024
SEG = 128
TREE = 2560
NB = TREE // SEG
NT = TRUNK // SEG

f32 = jnp.float32
bf16 = jnp.bfloat16
eps_norm = 1e-05
masked_score = -1e30
VMEM_MOST = 62 << 20

TAIL_SLOPE = 0.3
TAIL_COEFS = (
    0.11968663334846497,
    0.11957288533449173,
    0.11022695899009705,
    0.07842729985713959,
    0.09605274349451065,
    -0.07923758029937744,
    0.191569522023201,
    -0.22805799543857574,
    0.1123715341091156,
    -0.02061200700700283,
)


def dot_nn(left, right):
    return lax.dot_general(left, right, (((1,), (0,)), ((), ())), preferred_element_type=f32)


def dot_nt(left, right):
    return lax.dot_general(left, right, (((1,), (1,)), ((), ())), preferred_element_type=f32)


def dot_tn(left, right):
    return lax.dot_general(left, right, (((0,), (0,)), ((), ())), preferred_element_type=f32)


def bits_of(size):
    bits = []
    bit = 1
    while bit < size:
        bits.append(bit)
        bit *= 2
    return bits


def swap(block, axis, bit):
    size = lax.axis_size(axis)
    return lax.ppermute(block, axis, [(i, i ^ bit) for i in range(size)])


def gather_pieces(block, axis, bits):
    pieces = {0: block}
    for bit in bits:
        for j in list(pieces):
            pieces[j | bit] = swap(pieces[j], axis, bit)
    return [pieces[j] for j in range(len(pieces))]


def halving_order(bits):
    if not bits:
        return [0]
    rest = halving_order(bits[1:])
    return [bits[0] ^ j for j in rest] + rest


def scatter_halves(send, keep, axis, bits):
    terms = [keep]
    for at, bit in enumerate(bits):
        got = swap(send, axis, bit)
        terms = [t.astype(f32) for t in terms] + [got.astype(f32)]
        total = sum(terms)
        if at == len(bits) - 1:
            return total[0]
        half = total.shape[0] // 2
        send = total[:half].astype(bf16)
        terms = [total[half:]]
    return terms[0][0].astype(f32)


def scatter_parts(parts, axis, bits):
    parts = dict(enumerate(parts))
    for at, bit in enumerate(bits):
        last = at == len(bits) - 1
        kept = {}
        for j in sorted(parts):
            if not j & bit:
                got = swap(parts[j | bit], axis, bit)
                total = parts[j].astype(f32) + got.astype(f32)
                kept[j] = total if last or j == 0 else total.astype(bf16)
        parts = kept
    return parts[0].astype(f32)


def sum_everywhere(value, axes):
    for axis in axes:
        for bit in bits_of(lax.axis_size(axis)):
            value = value + swap(value, axis, bit)
    return value


def resident(shape):
    zeros = (0,) * len(shape)
    return pl.BlockSpec(shape, lambda *_: zeros, pipeline_mode=pl.Buffered(1))


def own_block(rows, columns):
    return pl.BlockSpec((rows, columns), lambda i, ids, *_: (ids[0] ^ i, 0))


def step_block(rows, columns):
    return pl.BlockSpec((rows, columns), lambda i, *_: (i, 0))


def place_pieces(pieces, where, number):
    rows = pieces[0].shape[0]
    for j, piece in enumerate(pieces):
        where[pl.ds(pl.multiple_of((number ^ j) * rows, rows), rows), :] = piece[...]


def pick_piece(pieces, where, step):
    for j, piece in enumerate(pieces):

        @pl.when(step == j)
        def _(piece=piece):
            where[...] = piece[...]


def store_part(parts, value, step, rows):
    if len(parts) == 1:
        parts[0][pl.ds(pl.multiple_of(step * rows, rows), rows), :] = value
        return
    for j, part in enumerate(parts):

        @pl.when(step == j)
        def _(part=part):
            part[...] = value


def store_halves(send, keep, total, number, order):
    half, rows = send.shape[0], send.shape[1]
    for at, j in enumerate(order):
        where = send if at < half else keep
        block = total[pl.ds(pl.multiple_of((number ^ j) * rows, rows), rows), :]
        where[at % half] = block.astype(bf16)


def halves_shape(size, rows, columns):
    return jax.ShapeDtypeStruct((max(size // 2, 1), rows, columns), bf16)


def call(kernel, name, grid, prefetch, operands, specs, outs, out_specs, scratch, flops, extra=0):
    size = sum(x.size * x.dtype.itemsize for x in list(operands) + list(outs))
    return pl.pallas_call(
        kernel,
        grid_spec=pltpu.PrefetchScalarGridSpec(
            num_scalar_prefetch=len(prefetch),
            grid=grid,
            in_specs=specs,
            out_specs=out_specs,
            scratch_shapes=scratch,
        ),
        out_shape=outs,
        compiler_params=pltpu.CompilerParams(
            dimension_semantics=("arbitrary",) * len(grid), vmem_limit_bytes=VMEM_MOST
        ),
        cost_estimate=pl.CostEstimate(
            flops=int(flops), bytes_accessed=int(size), transcendentals=int(extra)
        ),
        name=name,
    )(*prefetch, *operands)


def shaped(*shape, dtype=bf16):
    return jax.ShapeDtypeStruct(shape, dtype)


def shift_gain(block, gain, shift):
    return (block.astype(f32) * gain[...] + shift[...]).astype(bf16)


def turn(block, cosine, low_sine, high_sine, sign):
    width = block.shape[1]
    step = min(width, 128)
    done = []
    for start in range(0, width, step):
        part = block[:, start : start + step]
        if step == 128:
            left = pltpu.roll(part, step - ROT // 2, 1)
            right = pltpu.roll(part, ROT // 2, 1)
        else:
            left = jnp.concatenate([part[:, ROT // 2 :], part[:, : ROT // 2]], axis=1)
            right = jnp.concatenate([part[:, -ROT // 2 :], part[:, : -ROT // 2]], axis=1)
        moved = left * low_sine[:, :step] + right * high_sine[:, :step]
        done.append(part * cosine[:, :step] + moved * sign)
    return done[0] if len(done) == 1 else jnp.concatenate(done, axis=1)


def project_qkv(ids, info, sent, gain, shift, weight, bias, tables, width):
    groups, pieces = len(sent), len(weight)
    rows, model = sent[0].shape

    def kernel(ids, info, *refs):
        sent_refs, refs = refs[:groups], refs[groups:]
        weight_refs, refs = refs[:pieces], refs[pieces:]
        gain, shift, bias, cos, low, high, q_out, k_out, v_out, whole, block = refs
        step = pl.program_id(0)

        @pl.when(step == 0)
        def _():
            place_pieces(weight_refs, whole, ids[1])

        pick_piece(sent_refs, block, step)
        qkv = dot_nn(shift_gain(block[...], gain, shift), whole[...]) + bias[...]
        first = (ids[0] ^ step) * (rows // SEG)
        for at in range(rows // SEG):
            number = first + at
            table = pl.ds(pl.multiple_of(info[number // NB, number % NB, 4] * SEG, SEG), SEG)
            tabs = (cos[table, :], low[table, :], high[table, :])
            own = slice(at * SEG, (at + 1) * SEG)
            q_out[own, :] = (turn(qkv[own, :width], *tabs, 1.0) * HD**-0.5).astype(bf16)
            k_out[own, :] = turn(qkv[own, width : 2 * width], *tabs, 1.0).astype(bf16)
        v_out[...] = qkv[:, 2 * width :].astype(bf16)

    operands = [*sent, *weight, gain, shift, bias, *tables]
    out = shaped(groups * rows, width)
    return call(
        kernel,
        "project_qkv",
        (groups,),
        [ids, info],
        operands,
        [resident(x.shape) for x in operands],
        [out] * 3,
        [own_block(rows, width)] * 3,
        [pltpu.VMEM((model, 3 * width), bf16), pltpu.VMEM((rows, model), bf16)],
        2 * groups * rows * model * 3 * width,
    )


def project_grad(ids, grad, weight):
    groups, pieces = len(grad), len(weight)
    rows, model = grad[0].shape
    width = weight[0].shape[1]

    def kernel(ids, *refs):
        grad_refs, refs = refs[:groups], refs[groups:]
        weight_refs, (out, whole, block) = refs[:pieces], refs[pieces:]
        step = pl.program_id(0)

        @pl.when(step == 0)
        def _():
            place_pieces(weight_refs, whole, ids[1])

        pick_piece(grad_refs, block, step)
        out[...] = dot_nn(block[...], whole[...]).astype(bf16)

    operands = [*grad, *weight]
    return call(
        kernel,
        "project_grad",
        (groups,),
        [ids],
        operands,
        [resident(x.shape) for x in operands],
        [shaped(groups * rows, width)],
        [own_block(rows, width)],
        [pltpu.VMEM((model, width), bf16), pltpu.VMEM((rows, model), bf16)],
        2 * groups * rows * model * width,
    )[0]


def attention_kernel(
    info, q_ref, do_ref, k_ref, v_ref, cos, low, high, ctx_ref, dq_ref, dk_ref, dv_ref, dk_sum, dv_sum
):
    tree, step = pl.program_id(0), pl.program_id(1)
    width = q_ref.shape[1]
    heads = width // HD
    lane_head = lax.broadcasted_iota(jnp.int32, (SEG, width), 1) // HD

    @pl.when(step == 0)
    def _():
        dk_sum[...] = jnp.zeros_like(dk_sum)
        dv_sum[...] = jnp.zeros_like(dv_sum)

    first, second = info[tree, step, 0], info[tree, step, 1]
    first_rows = pl.ds(pl.multiple_of(first * SEG, SEG), SEG)
    second_rows = pl.ds(pl.multiple_of(second * SEG, SEG), SEG)
    queries, grads = q_ref[...], do_ref[...]
    zero = jnp.zeros_like(queries)
    q_rows = jnp.concatenate([jnp.where(lane_head == h, queries, zero) for h in range(heads)], axis=0)
    g_rows = jnp.concatenate([jnp.where(lane_head == h, grads, zero) for h in range(heads)], axis=0)
    q_turned, g_turned = queries.T, grads.T
    ahead = lax.broadcasted_iota(jnp.int32, (SEG, SEG), 1) - lax.broadcasted_iota(
        jnp.int32, (SEG, SEG), 0
    )
    seen = jnp.concatenate([ahead <= info[tree, step, 2], ahead <= info[tree, step, 3]], axis=1)
    seen = jnp.concatenate([seen] * heads, axis=0)
    k_near = jnp.concatenate([k_ref[first_rows, :], k_ref[second_rows, :]], axis=0)
    v_near = jnp.concatenate([v_ref[first_rows, :], v_ref[second_rows, :]], axis=0)

    def work(pairs):
        count = pairs * 2 * SEG
        near = jnp.where(seen, dot_nt(q_rows, k_near), masked_score)
        most = jnp.max(near, axis=1, keepdims=True)
        if count:
            k_far, v_far = k_ref[0:count, :], v_ref[0:count, :]
            far = dot_nt(q_rows, k_far)
            most = jnp.maximum(most, jnp.max(far, axis=1, keepdims=True))
        near = jnp.exp(near - most)
        total = jnp.sum(near, axis=1, keepdims=True)
        if count:
            far = jnp.exp(far - most)
            total = total + jnp.sum(far, axis=1, keepdims=True)
        scale = 1.0 / total
        near = near * scale
        near_low = near.astype(bf16)
        context = dot_nn(near_low, v_near)
        if count:
            far = far * scale
            far_low = far.astype(bf16)
            context = context + dot_nn(far_low, v_far)
        delta = jnp.sum(context * g_rows.astype(f32), axis=1, keepdims=True)
        near = (near * (dot_nt(g_rows, v_near) - delta)).astype(bf16)
        dq = dot_nn(near, k_near)
        if count:
            far = (far * (dot_nt(g_rows, v_far) - delta)).astype(bf16)
            dq = dq + dot_nn(far, k_far)
        ctx_own, dq_own = context[0:SEG], dq[0:SEG]
        for h in range(1, heads):
            ctx_own = jnp.where(lane_head == h, context[h * SEG : (h + 1) * SEG], ctx_own)
            dq_own = jnp.where(lane_head == h, dq[h * SEG : (h + 1) * SEG], dq_own)
        ctx_ref[...] = ctx_own.astype(bf16)
        dq_ref[...] = turn(dq_own * HD**-0.5, cos, low, high, -1.0).astype(bf16)
        for h in range(heads):
            own = slice(h * SEG, (h + 1) * SEG)
            part = slice(h * HD, (h + 1) * HD)
            dk = dot_nn(q_turned[part], near[own])
            dv = dot_nn(g_turned[part], near_low[own])
            dk_sum[first, part, :] += dk[:, :SEG]
            dv_sum[first, part, :] += dv[:, :SEG]
            dk_sum[second, part, :] += dk[:, SEG:]
            dv_sum[second, part, :] += dv[:, SEG:]
            if count:
                dk = dot_nn(q_turned[part], far[own])
                dv = dot_nn(g_turned[part], far_low[own])
                for j in range(2 * pairs):
                    dk_sum[j, part, :] += dk[:, j * SEG : (j + 1) * SEG]
                    dv_sum[j, part, :] += dv[:, j * SEG : (j + 1) * SEG]

    for pairs in range(NT // 2):

        @pl.when(step // 2 == pairs)
        def _(pairs=pairs):
            work(pairs)

    @pl.when(step >= NT)
    def _():
        work(NT // 2)

    @pl.when(step == NB - 1)
    def _():
        def finish(j, carry):
            rows = pl.ds(pl.multiple_of(j * SEG, SEG), SEG)
            dv_ref[rows, :] = dv_sum[j].T.astype(bf16)
            dk_ref[rows, :] = dk_sum[j].T.astype(bf16)
            return carry

        lax.fori_loop(0, NB, finish, 0)


def attention(info, tables, queries, keys, values, grads):
    total, width = queries.shape
    trees = total // TREE
    table_width = tables[0].shape[1]
    block = pl.BlockSpec((SEG, width), lambda t, b, info: (t * NB + b, 0))
    whole = pl.BlockSpec((TREE, width), lambda t, b, info: (t, 0))
    table = pl.BlockSpec((SEG, table_width), lambda t, b, info: (info[t, b, 4], 0))
    scores = trees * (TREE - TRUNK) * (TRUNK + 2 * SEG) * (width // HD)
    return call(
        attention_kernel,
        "attention",
        (trees, NB),
        [info],
        [queries, grads, keys, values, *tables],
        [block, block, whole, whole, table, table, table],
        [shaped(total, width)] * 4,
        [block, block, whole, whole],
        [pltpu.VMEM((NB, width, SEG), f32), pltpu.VMEM((NB, width, SEG), f32)],
        scores * width * 2 * 6 * 1.3,
        scores,
    )


def project_context(ids, context, grad, weight, order):
    groups, pieces = len(grad), len(weight)
    rows, model = grad[0].shape
    width = context.shape[1]
    parts = groups if groups <= 4 else 1

    def kernel(ids, ctx, *refs):
        grad_refs, refs = refs[:groups], refs[groups:]
        weight_refs, refs = refs[:pieces], refs[pieces:]
        part_refs, refs = refs[:parts], refs[parts:]
        send, keep, whole, block, total = refs
        step = pl.program_id(0)

        @pl.when(step == 0)
        def _():
            place_pieces(weight_refs, whole, ids[1])
            total[...] = jnp.zeros_like(total)

        pick_piece(grad_refs, block, step)
        store_part(part_refs, dot_nt(ctx[...], whole[...]).astype(bf16), step, rows)
        total[...] += dot_tn(block[...], ctx[...])

        @pl.when(step == groups - 1)
        def _():
            store_halves(send, keep, total, ids[1], order)

    operands = [context, *grad, *weight]
    part = shaped(groups * rows // parts, model)
    halves = halves_shape(pieces, model // pieces, width)
    outs = [part] * parts + [halves] * 2
    out = call(
        kernel,
        "project_context",
        (groups,),
        [ids],
        operands,
        [own_block(rows, width)] + [resident(x.shape) for x in operands[1:]],
        outs,
        [resident(x.shape) for x in outs],
        [
            pltpu.VMEM((model, width), bf16),
            pltpu.VMEM((rows, model), bf16),
            pltpu.VMEM((model, width), f32),
        ],
        4 * groups * rows * model * width,
    )
    return split_parts(out[:parts], groups), out[parts], out[parts + 1]


def split_parts(parts, groups):
    if len(parts) == groups:
        return list(parts)
    rows = parts[0].shape[0] // groups
    return [parts[0][j * rows : (j + 1) * rows] for j in range(groups)]


def mlp_forward(ids, sent, gain, shift, fc, bias, out):
    groups, pieces = len(sent), len(fc)
    rows, model = sent[0].shape
    units = fc[0].shape[1]
    parts = groups if groups <= 4 else 1

    def kernel(ids, *refs):
        sent_refs, refs = refs[:groups], refs[groups:]
        fc_refs, refs = refs[:pieces], refs[pieces:]
        out_refs, refs = refs[:pieces], refs[pieces:]
        gain, shift, bias, act_ref, slope_ref = refs[:5]
        part_refs, (fc_whole, out_whole, block) = refs[5 : 5 + parts], refs[5 + parts :]
        step = pl.program_id(0)

        @pl.when(step == 0)
        def _():
            place_pieces(fc_refs, fc_whole, ids[1])
            place_pieces(out_refs, out_whole, ids[1])

        pick_piece(sent_refs, block, step)
        hidden = dot_nn(shift_gain(block[...], gain, shift), fc_whole[...]) + bias[...]
        size = jnp.abs(hidden)
        ratio = 1.0 / (1.0 + TAIL_SLOPE * size)
        tail = jnp.full_like(ratio, TAIL_COEFS[-1])
        for coef in TAIL_COEFS[-2::-1]:
            tail = tail * ratio + coef
        bell = jnp.exp(hidden * hidden * -0.5)
        tail = tail * ratio * bell
        chance = jnp.where(hidden < 0, tail, 1.0 - tail)
        active = (hidden * chance).astype(bf16)
        act_ref[...] = active
        slope_ref[...] = chance + hidden * bell * 0.3989422804014327
        store_part(part_refs, dot_nt(active, out_whole[...]).astype(bf16), step, rows)

    operands = [*sent, *fc, *out, gain, shift, bias]
    part = shaped(groups * rows // parts, model)
    outs = [shaped(groups * rows, units), shaped(groups * rows, units, dtype=f32)] + [part] * parts
    done = call(
        kernel,
        "mlp_forward",
        (groups,),
        [ids],
        operands,
        [resident(x.shape) for x in operands],
        outs,
        [step_block(rows, units)] * 2 + [resident(part.shape)] * parts,
        [
            pltpu.VMEM((model, units), bf16),
            pltpu.VMEM((model, units), bf16),
            pltpu.VMEM((rows, model), bf16),
        ],
        4 * groups * rows * model * units,
    )
    return done[0], done[1], split_parts(done[2:], groups)


def mlp_backward(ids, sent, grad, active, slope, gain, shift, fc, out, fc_order, out_order):
    groups, pieces = len(sent), len(fc)
    rows, model = sent[0].shape
    units = fc[0].shape[1]

    def kernel(ids, act_ref, slope_ref, *refs):
        sent_refs, refs = refs[:groups], refs[groups:]
        grad_refs, refs = refs[:groups], refs[groups:]
        fc_refs, refs = refs[:pieces], refs[pieces:]
        out_refs, refs = refs[:pieces], refs[pieces:]
        gain, shift, back_ref, bias_ref, sums_ref, fc_send, fc_keep, out_send, out_keep = refs[:9]
        fc_whole, out_whole, block, grad_block, fc_total, out_total = refs[9:]
        step = pl.program_id(0)

        @pl.when(step == 0)
        def _():
            place_pieces(fc_refs, fc_whole, ids[1])
            place_pieces(out_refs, out_whole, ids[1])
            fc_total[...] = jnp.zeros_like(fc_total)
            out_total[...] = jnp.zeros_like(out_total)
            bias_ref[...] = jnp.zeros_like(bias_ref)
            sums_ref[...] = jnp.zeros_like(sums_ref)

        pick_piece(sent_refs, block, step)
        pick_piece(grad_refs, grad_block, step)
        hidden = (dot_nn(grad_block[...], out_whole[...]) * slope_ref[...]).astype(bf16)
        bias_ref[0:1, :] += jnp.sum(hidden.astype(f32), axis=0, keepdims=True)
        back = dot_nt(hidden, fc_whole[...])
        back_ref[...] = back
        token = block[...]
        sums_ref[0:1, :] += jnp.sum(back * token.astype(f32), axis=0, keepdims=True)
        sums_ref[1:2, :] += jnp.sum(back, axis=0, keepdims=True)
        fc_total[...] += dot_tn(shift_gain(token, gain, shift), hidden)
        out_total[...] += dot_tn(grad_block[...], act_ref[...])

        @pl.when(step == groups - 1)
        def _():
            store_halves(fc_send, fc_keep, fc_total, ids[1], fc_order)
            store_halves(out_send, out_keep, out_total, ids[1], out_order)

    operands = [active, slope, *sent, *grad, *fc, *out, gain, shift]
    halves = halves_shape(pieces, model // pieces, units)
    outs = [
        shaped(groups * rows, model, dtype=f32),
        shaped(8, units, dtype=f32),
        shaped(8, model, dtype=f32),
    ] + [halves] * 4
    return call(
        kernel,
        "mlp_backward",
        (groups,),
        [ids],
        operands,
        [step_block(rows, units)] * 2 + [resident(x.shape) for x in operands[2:]],
        outs,
        [step_block(rows, model)] + [resident(x.shape) for x in outs[1:]],
        [
            pltpu.VMEM((model, units), bf16),
            pltpu.VMEM((model, units), bf16),
            pltpu.VMEM((rows, model), bf16),
            pltpu.VMEM((rows, model), bf16),
            pltpu.VMEM((model, units), f32),
            pltpu.VMEM((model, units), f32),
        ],
        8 * groups * rows * model * units,
    )


def qkv_backward(ids, info, tables, dq, dk, dv, sent, back_mlp, gain, shift, gain_mlp, weight, order):
    groups, pieces = len(sent), len(weight)
    rows, model = sent[0].shape
    width = dq.shape[1]
    parts = groups if groups <= 4 else 1

    def kernel(ids, info, dq_ref, dk_ref, dv_ref, mlp_ref, *refs):
        sent_refs, refs = refs[:groups], refs[groups:]
        weight_refs, refs = refs[:pieces], refs[pieces:]
        gain, shift, gain_mlp, cos, low, high = refs[:6]
        part_refs, refs = refs[6 : 6 + parts], refs[6 + parts :]
        bias_ref, sums_ref, send, keep, whole, block, total, grads = refs
        step = pl.program_id(0)

        @pl.when(step == 0)
        def _():
            place_pieces(weight_refs, whole, ids[1])
            total[...] = jnp.zeros_like(total)
            bias_ref[...] = jnp.zeros_like(bias_ref)
            sums_ref[...] = jnp.zeros_like(sums_ref)

        pick_piece(sent_refs, block, step)
        grads[:, :width] = dq_ref[...]
        first = (ids[0] ^ step) * (rows // SEG)
        for at in range(rows // SEG):
            number = first + at
            table = pl.ds(pl.multiple_of(info[number // NB, number % NB, 4] * SEG, SEG), SEG)
            own = slice(at * SEG, (at + 1) * SEG)
            turned = turn(dk_ref[own, :], cos[table, :], low[table, :], high[table, :], -1.0)
            grads[own, width : 2 * width] = turned.astype(bf16)
        grads[:, 2 * width :] = dv_ref[...]
        bias_ref[0:1, :] += jnp.sum(grads[...].astype(f32), axis=0, keepdims=True)
        back = dot_nt(grads[...], whole[...])
        token = block[...]
        sums_ref[0:1, :] += jnp.sum(back * token.astype(f32), axis=0, keepdims=True)
        sums_ref[1:2, :] += jnp.sum(back, axis=0, keepdims=True)
        part = (back * gain[...] + mlp_ref[...] * gain_mlp[...]).astype(bf16)
        store_part(part_refs, part, step, rows)
        total[...] += dot_tn(shift_gain(token, gain, shift), grads[...])

        @pl.when(step == groups - 1)
        def _():
            store_halves(send, keep, total, ids[1], order)

    operands = [dq, dk, dv, back_mlp, *sent, *weight, gain, shift, gain_mlp, *tables]
    part = shaped(groups * rows // parts, model)
    halves = halves_shape(pieces, model // pieces, 3 * width)
    outs = (
        [part] * parts
        + [shaped(8, 3 * width, dtype=f32), shaped(8, model, dtype=f32)]
        + [halves] * 2
    )
    done = call(
        kernel,
        "qkv_backward",
        (groups,),
        [ids, info],
        operands,
        [own_block(rows, width)] * 3
        + [step_block(rows, model)]
        + [resident(x.shape) for x in operands[4:]],
        outs,
        [resident(x.shape) for x in outs],
        [
            pltpu.VMEM((model, 3 * width), bf16),
            pltpu.VMEM((rows, model), bf16),
            pltpu.VMEM((model, 3 * width), f32),
            pltpu.VMEM((rows, 3 * width), bf16),
        ],
        4 * groups * rows * model * 3 * width,
    )
    return (split_parts(done[:parts], groups), *done[parts:])


def tree_table(segment_ids, parent_ids):
    trees = segment_ids.shape[0] // TREE
    segment = segment_ids.reshape(trees, NB, SEG)[:, :, 0]
    parent = parent_ids.reshape(trees, NB, SEG)[:, :, 0]
    block = lax.broadcasted_iota(jnp.int32, (trees, NB), 1)
    trunk = block < NT
    leaf = (parent != segment[:, :1]) & ~trunk
    at = lax.broadcasted_iota(jnp.int32, (trees, NB, NB), 2)
    owner = jnp.sum(jnp.where(segment[:, None, :] == parent[:, :, None], at, 0), axis=2)
    odd = block % 2 == 1
    first = jnp.where(trunk, block // 2 * 2, block)
    second = jnp.where(trunk, block // 2 * 2 + 1, jnp.where(leaf, owner, block))
    first_most = jnp.where(trunk & odd, SEG, 0)
    second_most = jnp.where(trunk, jnp.where(odd, 0, -SEG), jnp.where(leaf, SEG, -SEG))
    table = jnp.where(trunk, block, jnp.where(leaf, NT + 1, NT))
    return jnp.stack([first, second, first_most, second_most, table], axis=2).astype(jnp.int32)


def angle_tables():
    places = TRUNK + 2 * SEG
    place = lax.broadcasted_iota(jnp.int32, (places, 2 * HD), 0).astype(f32)
    lane = lax.broadcasted_iota(jnp.int32, (places, 2 * HD), 1) % HD
    half = ROT // 2
    frequency = 10000.0 ** (-((lane % half).astype(f32) * 2.0 / ROT))
    angle = place * frequency
    cosine = jnp.where(lane < ROT, jnp.cos(angle), 1.0)
    sine = jnp.sin(angle)
    low = jnp.where(lane < half, -sine, 0.0)
    high = jnp.where((lane >= half) & (lane < ROT), sine, 0.0)
    return cosine, low, high


def by_kind(array, heads):
    shape = array.shape[:-1]
    array = array.reshape(*shape, heads, 3, HD)
    return jnp.swapaxes(array, -3, -2).reshape(*shape, 3 * heads * HD)


def by_head(array, heads):
    shape = array.shape[:-1]
    array = array.reshape(*shape, 3, heads, HD)
    return jnp.swapaxes(array, -3, -2).reshape(*shape, 3 * heads * HD)


def local(
    stream_in,
    segment_ids,
    parent_ids,
    norm_gain_attn,
    norm_shift_attn,
    norm_gain_mlp,
    norm_shift_mlp,
    qkv_weight,
    qkv_bias,
    dense_weight,
    dense_bias,
    fc_weight,
    fc_bias,
    out_weight,
    out_bias,
    out_grad,
):
    tensor_rank = lax.axis_index("tensor")
    data_rank = lax.axis_index("dp")
    ids = jnp.stack([tensor_rank, data_rank]).astype(jnp.int32)
    rows_local = stream_in.shape[0]
    model = stream_in.shape[1]
    qkv_width = qkv_weight.shape[1]
    heads = qkv_width // (3 * HD)
    width = heads * HD
    units = fc_weight.shape[1]
    tensor_bits = bits_of(lax.axis_size("tensor"))
    far_first = tensor_bits[:0:-1] + tensor_bits[:1]
    data_bits = bits_of(lax.axis_size("dp"))
    rows_first = data_bits[:0:-1] + data_bits[:1]
    columns_first = data_bits[:1] + data_bits[:0:-1]

    row_mean = jnp.mean(stream_in, axis=-1, keepdims=True)
    centred = stream_in - row_mean
    row_var = jnp.mean(centred * centred, axis=-1, keepdims=True)
    inv_std = lax.rsqrt(row_var + eps_norm)
    normalized = centred * inv_std
    sent_norm = normalized.astype(bf16)

    qkv_pieces = gather_pieces(by_kind(qkv_weight.astype(bf16), heads), "dp", rows_first)
    dense_pieces = gather_pieces(dense_weight.astype(bf16).T, "dp", columns_first)
    fc_pieces = gather_pieces(fc_weight.astype(bf16), "dp", rows_first)
    out_pieces = gather_pieces(out_weight.astype(bf16).T, "dp", columns_first)
    sent = gather_pieces(sent_norm, "tensor", far_first)
    first_grad = lax.optimization_barrier((out_grad, sent[-1]))[0]
    grad = gather_pieces(first_grad, "tensor", far_first)

    info = tree_table(segment_ids, parent_ids)
    tables = angle_tables()
    gain_attn, shift_attn = norm_gain_attn[None, :], norm_shift_attn[None, :]
    gain_mlp, shift_mlp = norm_gain_mlp[None, :], norm_shift_mlp[None, :]
    qkv_bias_own = by_kind(
        lax.dynamic_slice_in_dim(qkv_bias, tensor_rank * qkv_width, qkv_width), heads
    )[None, :]
    fc_bias_own = lax.dynamic_slice_in_dim(fc_bias, tensor_rank * units, units)[None, :]

    queries, keys, values = project_qkv(
        ids, info, sent, gain_attn, shift_attn, qkv_pieces, qkv_bias_own, tables, width
    )
    active, slope, mlp_parts = mlp_forward(
        ids, sent, gain_mlp, shift_mlp, fc_pieces, fc_bias_own, out_pieces
    )
    mlp_sum = scatter_parts(mlp_parts, "tensor", tensor_bits)
    grad_context = project_grad(ids, grad, dense_pieces)
    context, dq, dk, dv = attention(info, tables, queries, keys, values, grad_context)
    out_bits, fc_bits = columns_first[::-1], rows_first[::-1]
    attn_parts, dense_send, dense_keep = project_context(
        ids, context, grad, dense_pieces, halving_order(out_bits)
    )
    attn_sum = scatter_parts(attn_parts, "tensor", tensor_bits)
    back_mlp, fc_bias_sums, mlp_sums, fc_send, fc_keep, out_send, out_keep = mlp_backward(
        ids,
        sent,
        grad,
        active,
        slope,
        gain_mlp,
        shift_mlp,
        fc_pieces,
        out_pieces,
        halving_order(fc_bits),
        halving_order(out_bits),
    )
    back_parts, qkv_bias_sums, attn_sums, qkv_send, qkv_keep = qkv_backward(
        ids,
        info,
        tables,
        dq,
        dk,
        dv,
        sent,
        back_mlp,
        gain_attn,
        shift_attn,
        gain_mlp,
        qkv_pieces,
        halving_order(fc_bits),
    )
    grad_sent = scatter_parts(back_parts, "tensor", tensor_bits)

    fc_weight_grad = scatter_halves(fc_send, fc_keep, "dp", fc_bits)
    out_weight_grad = scatter_halves(out_send, out_keep, "dp", out_bits).T
    dense_weight_grad = scatter_halves(dense_send, dense_keep, "dp", out_bits).T
    qkv_weight_grad = by_head(scatter_halves(qkv_send, qkv_keep, "dp", fc_bits), heads)

    attn_out = attn_sum + dense_bias
    mlp_out = mlp_sum + out_bias
    output = stream_in + attn_out + mlp_out

    mean_grad = jnp.mean(grad_sent, axis=-1, keepdims=True)
    mean_cross = jnp.mean(grad_sent * normalized, axis=-1, keepdims=True)
    stream_grad = out_grad.astype(f32) + inv_std * (
        grad_sent - mean_grad - normalized * mean_cross
    )

    residual_part = jnp.sum(out_grad.astype(f32), axis=0)
    squares = jnp.stack([jnp.sum(output * output), jnp.sum(attn_out * attn_out), jnp.sum(mlp_out * mlp_out)])
    count_all = float(rows_local * lax.axis_size("dp") * lax.axis_size("tensor") * model)

    fc_bias_spread = lax.dynamic_update_slice(
        jnp.zeros(fc_bias.shape, f32), fc_bias_sums[0], (tensor_rank * units,)
    )
    early = jnp.concatenate(
        [residual_part, mlp_sums[0], mlp_sums[1], fc_bias_spread, jnp.pad(squares, (0, 125))]
    )
    early = sum_everywhere(early, ("tensor", "dp"))
    qkv_bias_spread = lax.dynamic_update_slice(
        jnp.zeros(qkv_bias.shape, f32), by_head(qkv_bias_sums[0], heads), (tensor_rank * qkv_width,)
    )
    late = jnp.concatenate([attn_sums[0], attn_sums[1], qkv_bias_spread])
    late = sum_everywhere(late, ("tensor", "dp"))

    residual_grad = early[:model]
    gain_mlp_grad = early[model : 2 * model]
    shift_mlp_grad = early[2 * model : 3 * model]
    fc_bias_grad = early[3 * model : 3 * model + fc_bias.shape[0]]
    squares = early[3 * model + fc_bias.shape[0] :][:3]
    gain_attn_grad = late[:model]
    shift_attn_grad = late[model : 2 * model]
    qkv_bias_grad = late[2 * model :]
    root_squares = jnp.sqrt(squares / count_all)
    return (
        output,
        stream_grad,
        gain_attn_grad,
        shift_attn_grad,
        gain_mlp_grad,
        shift_mlp_grad,
        qkv_weight_grad,
        qkv_bias_grad,
        dense_weight_grad,
        residual_grad,
        fc_weight_grad,
        fc_bias_grad,
        out_weight_grad,
        residual_grad,
        root_squares,
    )


def solution(mesh):
    tokens, weights, rows, whole = (
        P(("dp", "tensor"), None),
        P("dp", "tensor"),
        P("tensor", "dp"),
        P(),
    )
    return jax.shard_map(
        local,
        mesh=mesh,
        in_specs=(
            tokens,
            P("dp"),
            P("dp"),
            whole,
            whole,
            whole,
            whole,
            weights,
            whole,
            rows,
            whole,
            weights,
            whole,
            rows,
            whole,
            tokens,
        ),
        out_specs=(
            tokens,
            tokens,
            whole,
            whole,
            whole,
            whole,
            weights,
            whole,
            rows,
            whole,
            weights,
            whole,
            rows,
            whole,
            whole,
        ),
        check_vma=False,
    )
```

time: 1080 us -> 476 us (0.44)
  matrix products: 555 us -> 0 us
  Pallas kernels: 0 us -> 176 us
  waiting for transfers between devices: 283 us -> 171 us
  blocking collectives: 93.6 us -> 0 us
  starting transfers between devices: 5.82 us -> 72.3 us
  other arithmetic: 88.5 us -> 29.6 us
  local copies, waits for them, and re-layouts: 37.3 us -> 20.6 us
  between operations: 15.5 us -> 1.7 us
    dot_general x42 -> x0, matrix products: 555 us -> none  [the longest x5 155 us: backward_tree(): jnp.einsum('hqk,qhd->khd', score_grad, queries[row_start:row_end], prefer...]
    pallas_call x0 -> x7, Pallas kernels: none -> 176 us  [call(): pl.pallas_call(kernel, grid_spec=pltpu.PrefetchScalarGridSpec(num_scalar_...]
    ppermute x0 -> x65, waiting for transfers between devices: none -> 171 us  [swap(): return lax.ppermute(block, axis, [(i, i ^ bit) for i in range(size)])]
    all_gather x7 -> x0, waiting for transfers between devices: 120 us -> none  [the longest x1 57.1 us: local(): lax.all_gather(out_whole, 'tensor', axis=0, tiled=True)]
    reduce_scatter x3 -> x0, waiting for transfers between devices: 111 us -> none  [the longest x1 69 us: local(): lax.psum_scatter(fc_weight_part.astype(jnp.bfloat16), 'dp', scatter_dimen...]
    ppermute x0 -> x65, starting transfers between devices: none -> 72.3 us  [swap(): return lax.ppermute(block, axis, [(i, i ^ bit) for i in range(size)])]
    unnamed x14 -> x0, waiting for transfers between devices: 52.2 us -> none
    psum x1 -> x0, blocking collectives: 40.9 us -> none  [local(): lax.psum((gain_attn_part, shift_attn_part, gain_mlp_part, shift_mlp_part,...]
  transfers between devices with their start and end apart: 13 -> 65, of which waited for: 6 -> 26; matrix products, arithmetic and copies ran while one was open for 61% -> 9% of each run, Pallas kernels for 0% -> 37%
where the time goes in v1:
time: 476 us; the launch traced here: 472 us
  Pallas kernels  176 us (37%)
  waiting for transfers between devices  171 us (36%)
  starting transfers between devices  72.3 us (15%)
  other arithmetic  29.6 us (6%)
  local copies, waits for them, and re-layouts  20.6 us (4%)
    pallas_call x7, Pallas kernels, call(): pl.pallas_call(kernel, grid_spec=pltpu.PrefetchScalarGridSpec(num_scalar_...  176 us
    ppermute x65, waiting for transfers between devices, swap(): return lax.ppermute(block, axis, [(i, i ^ bit) for i in range(size)])  171 us
    ppermute x65, starting transfers between devices, swap(): return lax.ppermute(block, axis, [(i, i ^ bit) for i in range(size)])  72.3 us
  transfers between devices with their start and end apart: 65, of which 26 were waited for; matrix products, arithmetic and copies ran while one was open for 9% of the time, Pallas kernels for 37%

profile of v1, /device:TPU:0, one launch (start us, length us, event | category | flops | bytes accessed | tf_op | source)
XLA Modules:
  0.0 471.7 jit_solution(9164029845220683942)
XLA Ops:
  0.7 2.1 reduce_sum.85
  5.0 2.9 collective-permute-start.1
  7.9 28.9 %collective-permute-done.1.refs_2_ = bf16[640,1024]{1,0:T(8,128)(2,1)} collective-permute-done((bf16[640,1024]{1,0:T(8,128)(2,1)S(1)}, bf16[640,1024]{1,0:T(8,128)(2,1)}, u32[]{:S(2)}, u32[]{:S(2)}) %collective-permute-start.1) | collective-permute-done | bytes 1310752 | tf_op jit(solution)/shard_map/ppermute | solution.py:60
  37.0 1.8 collective-permute-start.13
  38.8 2.6 collective-permute-start.16
  41.4 1.6 collective-permute-start.14
  43.0 1.4 collective-permute-start.17
  45.1 1.5 collective-permute-start.26
  48.0 1.5 collective-permute-start.6
  49.5 1.6 collective-permute-start.4
  51.0 6.9 %collective-permute-done.17.refs_9_ = bf16[128,256]{1,0:T(8,128)(2,1)} collective-permute-done((bf16[128,256]{1,0:T(8,128)(2,1)S(1)}, bf16[128,256]{1,0:T(8,128)(2,1)}, u32[]{:S(2)}, u32[]{:S(2)}) %collective-permute-start.17) | collective-permute-done | bytes 65568 | tf_op jit(solution)/shard_map/ppermute | solution.py:60
  59.2 9.5 %collective-permute-done.6.refs_8_ = bf16[128,768]{1,0:T(8,128)(2,1)} collective-permute-done((bf16[128,768]{1,0:T(8,128)(2,1)S(1)}, bf16[128,768]{1,0:T(8,128)(2,1)}, u32[]{:S(2)}, u32[]{:S(2)}) %collective-permute-start.6) | collective-permute-done | bytes 196640 | tf_op jit(solution)/shard_map/ppermute | solution.py:60
  69.7 3.5 collective-permute-start.33
  74.0 4.0 collective-permute-done.30.refs_13_.refs_17_
  78.0 5.2 %collective-permute-done.24.refs_6_.refs_10_ = bf16[128,1024]{1,0:T(8,128)(2,1)} collective-permute-done((bf16[128,1024]{1,0:T(8,128)(2,1)}, bf16[128,1024]{1,0:T(8,128)(2,1)}, u32[]{:S(2)}, u32[]{:S(2)}) %collective-permute-start.24) | collective-permute-done | bytes 262176 | tf_op jit(solution)/shard_map/ppermute | solution.py:60
  85.3 2.2 collective-permute-start.34
  87.4 7.5 %collective-permute-done.31.refs_14_.refs_18_ = bf16[128,1024]{1,0:T(8,128)(2,1)S(1)} collective-permute-done((bf16[128,1024]{1,0:T(8,128)(2,1)S(1)}, bf16[128,1024]{1,0:T(8,128)(2,1)S(1)}, u32[]{:S(2)}, u32[]{:S(2)}) %collective-permute-start.31) | collective-permute-done | bytes 262176 | tf_op jit(solution)/shard_map/ppermute | solution.py:60
  95.0 1.5 collective-permute-start.11
  96.5 4.1 fusion.10
  101.7 1.7 collective-permute-done.28.refs_10_.refs_14_
  104.5 5.4 %collective-permute-done.27.refs_9_.refs_13_ = bf16[128,1024]{1,0:T(8,128)(2,1)} collective-permute-done((bf16[128,1024]{1,0:T(8,128)(2,1)}, bf16[128,1024]{1,0:T(8,128)(2,1)}, u32[]{:S(2)}, u32[]{:S(2)}) %collective-permute-start.27) | collective-permute-done | bytes 262176 | tf_op jit(solution)/shard_map/ppermute | solution.py:60
  109.9 3.0 collective-permute-done.32.refs_15_.refs_19_
  112.9 1.8 collective-permute-done.25.refs_7_.refs_11_
  120.0 1.4 collective-permute-done.29.refs_11_.refs_15_
  122.1 1.4 collective-permute-start.9
  124.0 29.8 %mlp_forward.1 = (bf16[2560,1024]{1,0:T(8,128)(2,1)}, f32[2560,1024]{1,0:T(8,128)}, bf16[640,1024]{1,0:T(8,128)(2,1)}, bf16[640,1024]{1,0:T(8,128)(2,1)}, bf16[6...) custom-call(s32[2]{0:T(128)} %pad_add_fusion.ids, bf16[640,1024]{1,0:T(8,128)(2,1)} %copy-done.7, ...), custom_call_target="tpu_custom_call" | custom-call | flops 10737418240 | bytes 30420992 | tf_op jit(solution)/shard_map/mlp_forward/pallas_call | solution.py:165
  154.5 1.4 collective-permute-start.18
  156.6 11.8 %project_qkv.1 = (bf16[2560,256]{1,0:T(8,128)(2,1)}, bf16[2560,256]{1,0:T(8,128)(2,1)}, bf16[2560,256]{1,0:T(8,128)(2,1)}) custom-call(s32[2]{0:T(128)} %pad_add_fusion.ids, s32[1,20,5]{2,1,0:T(8,128)} %stack.32.info, bf16[640,1024]{1,0:T(8,128)(2,1)} %copy-done.7, bf16[640,1024]{1,0:T(8,128)(2,1)} %collective-permute-done.refs_1_, ...), custom_call_target="tpu_custom_call" | custom-call | flops 4026531840 | bytes 12725248 | tf_op jit(solution)/shard_map/project_qkv/pallas_call | solution.py:165
  169.2 6.6 %project_grad.1.do_ref = bf16[2560,256]{1,0:T(8,128)(2,1)} custom-call(s32[2]{0:T(128)} %pad_add_fusion.ids, bf16[640,1024]{1,0:T(8,128)(2,1)} %refs_4_, bf16[640,1024]{1,0:T(8,128)(2,1)} %collective-permute-done.10.refs_1_.refs_5_, bf16[640,1024]{1,0:T(8,128)(2,1)} %collective-permute-done.11.refs_2_.refs_6_, ...), custom_call_target="tpu_custom_call" | custom-call | flops 1342177280 | bytes 7077888 | tf_op jit(solution)/shard_map/project_grad/pallas_call | solution.py:165
  175.8 55.2 %attention.1 = (bf16[2560,256]{1,0:T(8,128)(2,1)}, bf16[2560,256]{1,0:T(8,128)(2,1)}, bf16[2560,256]{1,0:T(8,128)(2,1)}, bf16[2560,256]{1,0:T(8,128)(2,1)}) custom-call(s32[1,20,5]{2,1,0:T(8,128)} %stack.32.info, bf16[2560,256]{1,0:T(8,128)(2,1)} %get-tuple-element.50.q_ref, bf16[2560,256]{1,0:T(8,128)(2,1)} %project_grad.1.do_ref, ...), custom_call_target="tpu_custom_call" | custom-call | flops 31406948352 | bytes 12451840 | tf_op jit(solution)/shard_map/attention/pallas_call | solution.py:165
  231.0 37.3 %mlp_backward.1 = (f32[2560,1024]{1,0:T(8,128)}, f32[8,1024]{1,0:T(8,128)}, f32[8,1024]{1,0:T(8,128)}, bf16[4,128,1024]{2,1,0:T(8,128)(2,1)}, bf16[4,128,1024]{2...) custom-call(s32[2]{0:T(128)} %pad_add_fusion.ids, ...), custom_call_target="tpu_custom_call" | custom-call | flops 21474836480 | bytes 45162496 | tf_op jit(solution)/shard_map/mlp_backward/pallas_call | solution.py:165
  268.3 22.5 %qkv_backward.1 = (bf16[640,1024]{1,0:T(8,128)(2,1)}, bf16[640,1024]{1,0:T(8,128)(2,1)}, bf16[640,1024]{1,0:T(8,128)(2,1)}, bf16[640,1024]{1,0:T(8,128)(2,1)}, f...) custom-call(s32[2]{0:T(128)} %pad_add_fusion.ids, ...), custom_call_target="tpu_custom_call" | custom-call | flops 8053063680 | bytes 30085120 | tf_op jit(solution)/shard_map/qkv_backward/pallas_call | solution.py:165
  295.1 2.9 collective-permute-done.44
  298.9 13.0 %project_context.1 = (bf16[640,1024]{1,0:T(8,128)(2,1)}, bf16[640,1024]{1,0:T(8,128)(2,1)}, bf16[640,1024]{1,0:T(8,128)(2,1)}, bf16[640,1024]{1,0:T(8,128)(2,1)}...) custom-call(s32[2]{0:T(128)} %pad_add_fusion.ids, bf16[2560,256]{1,0:T(8,128)(2,1)} %get-tuple-element.54.ctx, ...), custom_call_target="tpu_custom_call" | custom-call | flops 2684354560 | bytes 12845056 | tf_op jit(solution)/shard_map/project_context/pallas_call | solution.py:165
  314.0 2.9 add_convert_fusion.1
  318.2 1.4 collective-permute-start.53
  319.7 2.9 collective-permute-start.47
  322.8 1.4 fusion.37
  325.2 17.1 %collective-permute-done.47 = f32[5120]{0:T(1024)S(1)} collective-permute-done((f32[5120]{0:T(1024)S(1)}, f32[5120]{0:T(1024)S(1)}, u32[]{:S(2)}, u32[]{:S(2)}) %collective-permute-start.47) | collective-permute-done | bytes 20512 | tf_op jit(solution)/shard_map/ppermute | solution.py:60
  342.3 2.1 collective-permute-done.57
  344.5 1.4 collective-permute-start.58
  347.1 1.7 collective-permute-done.58
  349.6 1.4 collective-permute-start.59
  351.0 1.8 add_convert_fusion
  352.8 1.4 collective-permute-start.42
  355.6 3.8 collective-permute-start.54
  359.4 1.8 convert_add_fusion.2
  361.5 2.0 add_convert_fusion.2
  363.5 11.9 %collective-permute-done.59 = bf16[4,128,1024]{2,1,0:T(8,128)(2,1)S(1)} collective-permute-done((bf16[4,128,1024]{2,1,0:T(8,128)(2,1)}, bf16[4,128,1024]{2,1,0:T(8,128)(2,1)S(1)}, u32[]{:S(2)}, u32[]{:S(2)}) %collective-permute-start.59) | collective-permute-done | bytes 1048608 | tf_op jit(solution)/shard_map/ppermute | solution.py:60
  375.4 1.3 collective-permute-start.39
  378.2 6.3 %collective-permute-done.42 = bf16[640,1024]{1,0:T(8,128)(2,1)S(1)} collective-permute-done((bf16[640,1024]{1,0:T(8,128)(2,1)S(1)}, bf16[640,1024]{1,0:T(8,128)(2,1)S(1)}, u32[]{:S(2)}, u32[]{:S(2)}) %collective-permute-start.42) | collective-permute-done | bytes 1310752 | tf_op jit(solution)/shard_map/ppermute | solution.py:60
  384.5 3.4 collective-permute-start.63
  389.4 23.2 %collective-permute-done.39 = bf16[640,1024]{1,0:T(8,128)(2,1)S(1)} collective-permute-done((bf16[640,1024]{1,0:T(8,128)(2,1)S(1)}, bf16[640,1024]{1,0:T(8,128)(2,1)S(1)}, u32[]{:S(2)}, u32[]{:S(2)}) %collective-permute-start.39) | collective-permute-done | bytes 1310752 | tf_op jit(solution)/shard_map/ppermute | solution.py:60
  412.6 3.4 collective-permute-start.55
  416.0 24.0 %collective-permute-done.22 = bf16[640,1024]{1,0:T(8,128)(2,1)S(1)} collective-permute-done((bf16[640,1024]{1,0:T(8,128)(2,1)S(1)}, bf16[640,1024]{1,0:T(8,128)(2,1)S(1)}, u32[]{:S(2)}, u32[]{:S(2)}) %collective-permute-start.22) | collective-permute-done | bytes 1310752 | tf_op jit(solution)/shard_map/ppermute | solution.py:60
  440.0 5.4 %multiply_reduce_fusion.2 = (f32[]{:T(128)}, f32[640,1024]{1,0:T(8,128)}, f32[]{:T(128)}, f32[]{:T(128)}, f32[640,1024]{1,0:T(8,128)}, /*index=5*/f32[1024]{0:T(1024)S(1)}) fusion(f32[1024]{0:T(1024)S(1)} %copy-done.36, bf16[640,1024]{1,0:T(8,128)(2,1)S(1)} %collective-permute-done.39, bf16[640,1024]{1,0:T(8,128)(2,1)S(1)} %collective-permute-done.37, ...), kind=kLoop, calls=%fused_computation.4 | loop fusion | flops 22281212 | bytes 20994060 | tf_op jit(solution)/shard_map/reduce_sum | solution.py:821
  445.5 2.0 constant_dynamic-update-slice_fusion
  449.0 1.4 collective-permute-start.49
  451.3 3.4 collective-permute-start.61
  454.7 1.5 collective-permute-start.50
  457.3 1.3 collective-permute-done.50
  458.7 3.0 collective-permute-start.51
  461.7 1.9 collective-permute-done.51
  463.6 3.7 collective-permute-start.52
  (258 shorter events, 44.2 us)
Async XLA Ops:
  5.0 31.8 %collective-permute-start.1 = (bf16[640,1024]{1,0:T(8,128)(2,1)S(1)}, bf16[640,1024]{1,0:T(8,128)(2,1)}, u32[]{:S(2)}, u32[]{:S(2)}) collective-permute-start(bf16[640,1024]{1,0:T(8,128)(2,1)S(1)} %fusion.refs_0_), channel_id=1, source_target_pairs={{0,2},{1,3},{2,0},{3,1},{4,6},{5,7},{6,4},{7,5},{8,10},{9,11},{10,... | collective-permute-start | bytes 3932168 | tf_op jit(solution)/shard_map/ppermute | solution.py:60
  36.8 37.2 %collective-permute-start.2 = (bf16[640,1024]{1,0:T(8,128)(2,1)}, bf16[640,1024]{1,0:T(8,128)(2,1)}, u32[]{:S(2)}, u32[]{:S(2)}) collective-permute-start(bf16[640,1024]{1,0:T(8,128)(2,1)} %collective-permute-done.1.refs_2_), channel_id=1, source_target_pairs={{0,1},{1,0},{2,3},{3,2},{4,5},{5,4},{6,7},{7,6},{8,9},{9,8},{10,11... | collective-permute-start | bytes 3932168 | tf_op jit(solution)/shard_map/ppermute | solution.py:60
  37.0 6.0 %collective-permute-start.13 = (bf16[128,256]{1,0:T(8,128)(2,1)S(1)}, bf16[128,256]{1,0:T(8,128)(2,1)S(1)}, u32[]{:S(2)}, u32[]{:S(2)}) collective-permute-start(bf16[128,256]{1,0:T(8,128)(2,1)S(1)} %bitcast.53), channel_id=1, source_target_pairs={{0,4},{4,0},{8,12},{12,8},{16,20},{20,16},{24,28},{28,24},{1,5},{5... | collective-permute-start | bytes 196616 | tf_op jit(solution)/shard_map/ppermute | solution.py:60
  38.8 9.2 %collective-permute-start.16 = (bf16[128,256]{1,0:T(8,128)(2,1)S(1)}, bf16[128,256]{1,0:T(8,128)(2,1)S(1)}, u32[]{:S(2)}, u32[]{:S(2)}) collective-permute-start(bf16[128,256]{1,0:T(8,128)(2,1)S(1)} %bitcast.54), channel_id=1, source_target_pairs={{0,16},{4,20},{8,24},{12,28},{16,0},{20,4},{24,8},{28,12},{1,17},{... | collective-permute-start | bytes 196616 | tf_op jit(solution)/shard_map/ppermute | solution.py:60
  41.4 8.1 %collective-permute-start.14 = (bf16[128,256]{1,0:T(8,128)(2,1)S(1)}, bf16[128,256]{1,0:T(8,128)(2,1)}, u32[]{:S(2)}, u32[]{:S(2)}) collective-permute-start(bf16[128,256]{1,0:T(8,128)(2,1)S(1)} %bitcast.55), channel_id=1, source_target_pairs={{0,8},{4,12},{8,0},{12,4},{16,24},{20,28},{24,16},{28,20},{1,9},{5... | collective-permute-start | bytes 196616 | tf_op jit(solution)/shard_map/ppermute | solution.py:60
  43.0 15.0 %collective-permute-start.17 = (bf16[128,256]{1,0:T(8,128)(2,1)S(1)}, bf16[128,256]{1,0:T(8,128)(2,1)}, u32[]{:S(2)}, u32[]{:S(2)}) collective-permute-start(bf16[128,256]{1,0:T(8,128)(2,1)S(1)} %collective-permute-done.13.refs_5_), channel_id=1, source_target_pairs={{0,16},{4,20},{8,24},{12,28},{16,0},{20,4},{24,8},{28,12},{1,17},{... | collective-permute-start | bytes 196616 | tf_op jit(solution)/shard_map/ppermute | solution.py:60
  45.1 28.0 %collective-permute-start.26 = (bf16[128,1024]{1,0:T(8,128)(2,1)}, bf16[128,1024]{1,0:T(8,128)(2,1)}, u32[]{:S(2)}, u32[]{:S(2)}) collective-permute-start(bf16[128,1024]{1,0:T(8,128)(2,1)} %convert_element_type.181.refs_4_.refs_8_), channel_id=1, source_target_pairs={{0,16},{4,20},{8,24},{12,28},{16,0},{20,4},{24,8},{28,12},{1,17},{... | collective-permute-start | bytes 786440 | tf_op jit(solution)/shard_map/ppermute | solution.py:60
  48.0 20.7 %collective-permute-start.6 = (bf16[128,768]{1,0:T(8,128)(2,1)S(1)}, bf16[128,768]{1,0:T(8,128)(2,1)}, u32[]{:S(2)}, u32[]{:S(2)}) collective-permute-start(bf16[128,768]{1,0:T(8,128)(2,1)S(1)} %copy.128.refs_4_), channel_id=1, source_target_pairs={{0,16},{4,20},{8,24},{12,28},{16,0},{20,4},{24,8},{28,12},{1,17},{... | collective-permute-start | bytes 589832 | tf_op jit(solution)/shard_map/ppermute | solution.py:60
  49.5 19.2 %collective-permute-start.4 = (bf16[128,768]{1,0:T(8,128)(2,1)S(1)}, bf16[128,768]{1,0:T(8,128)(2,1)}, u32[]{:S(2)}, u32[]{:S(2)}) collective-permute-start(bf16[128,768]{1,0:T(8,128)(2,1)S(1)} %copy.128.refs_4_), channel_id=1, source_target_pairs={{0,8},{4,12},{8,0},{12,4},{16,24},{20,28},{24,16},{28,20},{1,9},{5... | collective-permute-start | bytes 589832 | tf_op jit(solution)/shard_map/ppermute | solution.py:60
  58.0 11.7 %collective-permute-start.3 = (bf16[128,768]{1,0:T(8,128)(2,1)S(1)}, bf16[128,768]{1,0:T(8,128)(2,1)}, u32[]{:S(2)}, u32[]{:S(2)}) collective-permute-start(bf16[128,768]{1,0:T(8,128)(2,1)S(1)} %copy.128.refs_4_), channel_id=1, source_target_pairs={{0,4},{4,0},{8,12},{12,8},{16,20},{20,16},{24,28},{28,24},{1,5},{5... | collective-permute-start | bytes 589832 | tf_op jit(solution)/shard_map/ppermute | solution.py:60
  68.7 14.5 %collective-permute-start.24 = (bf16[128,1024]{1,0:T(8,128)(2,1)}, bf16[128,1024]{1,0:T(8,128)(2,1)}, u32[]{:S(2)}, u32[]{:S(2)}) collective-permute-start(bf16[128,1024]{1,0:T(8,128)(2,1)} %convert_element_type.181.refs_4_.refs_8_), channel_id=1, source_target_pairs={{0,8},{4,12},{8,0},{12,4},{16,24},{20,28},{24,16},{28,20},{1,9},{5... | collective-permute-start | bytes 786440 | tf_op jit(solution)/shard_map/ppermute | solution.py:60
  68.7 9.3 %collective-permute-start.30 = (bf16[128,1024]{1,0:T(8,128)(2,1)S(1)}, bf16[128,1024]{1,0:T(8,128)(2,1)}, u32[]{:S(2)}, u32[]{:S(2)}) collective-permute-start(bf16[128,1024]{1,0:T(8,128)(2,1)S(1)} %bitcast.58), channel_id=1, source_target_pairs={{0,4},{4,0},{8,12},{12,8},{16,20},{20,16},{24,28},{28,24},{1,5},{5... | collective-permute-start | bytes 786440 | tf_op jit(solution)/shard_map/ppermute | solution.py:60
  69.7 14.7 %collective-permute-start.33 = (bf16[128,1024]{1,0:T(8,128)(2,1)S(1)}, bf16[128,1024]{1,0:T(8,128)(2,1)S(1)}, u32[]{:S(2)}, u32[]{:S(2)}) collective-permute-start(bf16[128,1024]{1,0:T(8,128)(2,1)S(1)} %bitcast.59), channel_id=1, source_target_pairs={{0,16},{4,20},{8,24},{12,28},{16,0},{20,4},{24,8},{28,12},{1,17},{... | collective-permute-start | bytes 786440 | tf_op jit(solution)/shard_map/ppermute | solution.py:60
  73.2 12.1 %collective-permute-start.23 = (bf16[128,1024]{1,0:T(8,128)(2,1)}, bf16[128,1024]{1,0:T(8,128)(2,1)S(1)}, u32[]{:S(2)}, u32[]{:S(2)}) collective-permute-start(bf16[128,1024]{1,0:T(8,128)(2,1)} %convert_element_type.181.refs_4_.refs_8_), channel_id=1, source_target_pairs={{0,4},{4,0},{8,12},{12,8},{16,20},{20,16},{24,28},{28,24},{1,5},{5... | collective-permute-start | bytes 786440 | tf_op jit(solution)/shard_map/ppermute | solution.py:60
  74.0 21.0 %collective-permute-start.31 = (bf16[128,1024]{1,0:T(8,128)(2,1)S(1)}, bf16[128,1024]{1,0:T(8,128)(2,1)S(1)}, u32[]{:S(2)}, u32[]{:S(2)}) collective-permute-start(bf16[128,1024]{1,0:T(8,128)(2,1)S(1)} %bitcast.60), channel_id=1, source_target_pairs={{0,8},{4,12},{8,0},{12,4},{16,24},{20,28},{24,16},{28,20},{1,9},{5... | collective-permute-start | bytes 786440 | tf_op jit(solution)/shard_map/ppermute | solution.py:60
  78.0 45.4 %collective-permute-start = (bf16[640,1024]{1,0:T(8,128)(2,1)S(1)}, bf16[640,1024]{1,0:T(8,128)(2,1)}, u32[]{:S(2)}, u32[]{:S(2)}) collective-permute-start(bf16[640,1024]{1,0:T(8,128)(2,1)S(1)} %copy-done.8), channel_id=1, source_target_pairs={{0,1},{1,0},{2,3},{3,2},{4,5},{5,4},{6,7},{7,6},{8,9},{9,8},{10,11... | collective-permute-start | bytes 3932168 | tf_op jit(solution)/shard_map/ppermute | solution.py:60
  83.2 17.5 %collective-permute-start.8 = (bf16[128,768]{1,0:T(8,128)(2,1)}, bf16[128,768]{1,0:T(8,128)(2,1)S(1)}, u32[]{:S(2)}, u32[]{:S(2)}) collective-permute-start(bf16[128,768]{1,0:T(8,128)(2,1)} %collective-permute-done.6.refs_8_), channel_id=1, source_target_pairs={{0,8},{4,12},{8,0},{12,4},{16,24},{20,28},{24,16},{28,20},{1,9},{5... | collective-permute-start | bytes 589832 | tf_op jit(solution)/shard_map/ppermute | solution.py:60
  84.4 19.0 %collective-permute-start.28 = (bf16[128,1024]{1,0:T(8,128)(2,1)}, bf16[128,1024]{1,0:T(8,128)(2,1)S(1)}, u32[]{:S(2)}, u32[]{:S(2)}) collective-permute-start(bf16[128,1024]{1,0:T(8,128)(2,1)} %collective-permute-done.26.refs_8_.refs_12_), channel_id=1, source_target_pairs={{0,8},{4,12},{8,0},{12,4},{16,24},{20,28},{24,16},{28,20},{1,9},{5... | collective-permute-start | bytes 786440 | tf_op jit(solution)/shard_map/ppermute | solution.py:60
  85.3 18.1 %collective-permute-start.34 = (bf16[128,1024]{1,0:T(8,128)(2,1)}, bf16[128,1024]{1,0:T(8,128)(2,1)S(1)}, u32[]{:S(2)}, u32[]{:S(2)}) collective-permute-start(bf16[128,1024]{1,0:T(8,128)(2,1)} %collective-permute-done.30.refs_13_.refs_17_), channel_id=1, source_target_pairs={{0,16},{4,20},{8,24},{12,28},{16,0},{20,4},{24,8},{28,12},{1,17},{... | collective-permute-start | bytes 786440 | tf_op jit(solution)/shard_map/ppermute | solution.py:60
  95.0 28.5 %collective-permute-start.11 = (bf16[640,1024]{1,0:T(8,128)(2,1)S(1)}, bf16[640,1024]{1,0:T(8,128)(2,1)}, u32[]{:S(2)}, u32[]{:S(2)}) collective-permute-start(bf16[640,1024]{1,0:T(8,128)(2,1)S(1)} %copy-done.2), channel_id=1, source_target_pairs={{0,2},{1,3},{2,0},{3,1},{4,6},{5,7},{6,4},{7,5},{8,10},{9,11},{10,... | collective-permute-start | bytes 3932168 | tf_op jit(solution)/shard_map/ppermute | solution.py:60
  100.7 9.2 %collective-permute-start.27 = (bf16[128,1024]{1,0:T(8,128)(2,1)}, bf16[128,1024]{1,0:T(8,128)(2,1)}, u32[]{:S(2)}, u32[]{:S(2)}) collective-permute-start(bf16[128,1024]{1,0:T(8,128)(2,1)} %collective-permute-done.26.refs_8_.refs_12_), channel_id=1, source_target_pairs={{0,4},{4,0},{8,12},{12,8},{16,20},{20,16},{24,28},{28,24},{1,5},{5... | collective-permute-start | bytes 786440 | tf_op jit(solution)/shard_map/ppermute | solution.py:60
  103.3 9.6 %collective-permute-start.32 = (bf16[128,1024]{1,0:T(8,128)(2,1)}, bf16[128,1024]{1,0:T(8,128)(2,1)}, u32[]{:S(2)}, u32[]{:S(2)}) collective-permute-start(bf16[128,1024]{1,0:T(8,128)(2,1)} %collective-permute-done.30.refs_13_.refs_17_), channel_id=1, source_target_pairs={{0,8},{4,12},{8,0},{12,4},{16,24},{20,28},{24,16},{28,20},{1,9},{5... | collective-permute-start | bytes 786440 | tf_op jit(solution)/shard_map/ppermute | solution.py:60
  103.4 11.4 %collective-permute-start.25 = (bf16[128,1024]{1,0:T(8,128)(2,1)}, bf16[128,1024]{1,0:T(8,128)(2,1)}, u32[]{:S(2)}, u32[]{:S(2)}) collective-permute-start(bf16[128,1024]{1,0:T(8,128)(2,1)} %collective-permute-done.24.refs_6_.refs_10_), channel_id=1, source_target_pairs={{0,4},{4,0},{8,12},{12,8},{16,20},{20,16},{24,28},{28,24},{1,5},{5... | collective-permute-start | bytes 786440 | tf_op jit(solution)/shard_map/ppermute | solution.py:60
  109.9 9.3 %collective-permute-start.35 = (bf16[128,1024]{1,0:T(8,128)(2,1)}, bf16[128,1024]{1,0:T(8,128)(2,1)}, u32[]{:S(2)}, u32[]{:S(2)}) collective-permute-start(bf16[128,1024]{1,0:T(8,128)(2,1)} %copy-done.40), channel_id=1, source_target_pairs={{0,8},{4,12},{8,0},{12,4},{16,24},{20,28},{24,16},{28,20},{1,9},{5... | collective-permute-start | bytes 786440 | tf_op jit(solution)/shard_map/ppermute | solution.py:60
  112.9 8.5 %collective-permute-start.29 = (bf16[128,1024]{1,0:T(8,128)(2,1)}, bf16[128,1024]{1,0:T(8,128)(2,1)}, u32[]{:S(2)}, u32[]{:S(2)}) collective-permute-start(bf16[128,1024]{1,0:T(8,128)(2,1)} %copy-done.43), channel_id=1, source_target_pairs={{0,4},{4,0},{8,12},{12,8},{16,20},{20,16},{24,28},{28,24},{1,5},{5... | collective-permute-start | bytes 786440 | tf_op jit(solution)/shard_map/ppermute | solution.py:60
  114.7 7.3 %collective-permute-start.36 = (bf16[128,1024]{1,0:T(8,128)(2,1)}, bf16[128,1024]{1,0:T(8,128)(2,1)}, u32[]{:S(2)}, u32[]{:S(2)}) collective-permute-start(bf16[128,1024]{1,0:T(8,128)(2,1)} %copy-done.44), channel_id=1, source_target_pairs={{0,8},{4,12},{8,0},{12,4},{16,24},{20,28},{24,16},{28,20},{1,9},{5... | collective-permute-start | bytes 786440 | tf_op jit(solution)/shard_map/ppermute | solution.py:60
  119.3 34.6 %collective-permute-start.7 = (bf16[128,768]{1,0:T(8,128)(2,1)}, bf16[128,768]{1,0:T(8,128)(2,1)}, u32[]{:S(2)}, u32[]{:S(2)}) collective-permute-start(bf16[128,768]{1,0:T(8,128)(2,1)} %collective-permute-done.6.refs_8_), channel_id=1, source_target_pairs={{0,4},{4,0},{8,12},{12,8},{16,20},{20,16},{24,28},{28,24},{1,5},{5... | collective-permute-start | bytes 589832 | tf_op jit(solution)/shard_map/ppermute | solution.py:60
  121.4 33.1 %collective-permute-start.5 = (bf16[128,768]{1,0:T(8,128)(2,1)}, bf16[128,768]{1,0:T(8,128)(2,1)}, u32[]{:S(2)}, u32[]{:S(2)}) collective-permute-start(bf16[128,768]{1,0:T(8,128)(2,1)} %collective-permute-done.4.refs_6_), channel_id=1, source_target_pairs={{0,4},{4,0},{8,12},{12,8},{16,20},{20,16},{24,28},{28,24},{1,5},{5... | collective-permute-start | bytes 589832 | tf_op jit(solution)/shard_map/ppermute | solution.py:60
  122.1 33.9 %collective-permute-start.9 = (bf16[128,768]{1,0:T(8,128)(2,1)}, bf16[128,768]{1,0:T(8,128)(2,1)}, u32[]{:S(2)}, u32[]{:S(2)}) collective-permute-start(bf16[128,768]{1,0:T(8,128)(2,1)} %copy-done.45), channel_id=1, source_target_pairs={{0,4},{4,0},{8,12},{12,8},{16,20},{20,16},{24,28},{28,24},{1,5},{5... | collective-permute-start | bytes 589832 | tf_op jit(solution)/shard_map/ppermute | solution.py:60
  123.5 45.1 %collective-permute-start.10 = (bf16[640,1024]{1,0:T(8,128)(2,1)S(1)}, bf16[640,1024]{1,0:T(8,128)(2,1)}, u32[]{:S(2)}, u32[]{:S(2)}) collective-permute-start(bf16[640,1024]{1,0:T(8,128)(2,1)S(1)} %copy-done.2), channel_id=1, source_target_pairs={{0,1},{1,0},{2,3},{3,2},{4,5},{5,4},{6,7},{7,6},{8,9},{9,8},{10,11... | collective-permute-start | bytes 3932168 | tf_op jit(solution)/shard_map/ppermute | solution.py:60
  123.5 45.1 %collective-permute-start.12 = (bf16[640,1024]{1,0:T(8,128)(2,1)}, bf16[640,1024]{1,0:T(8,128)(2,1)}, u32[]{:S(2)}, u32[]{:S(2)}) collective-permute-start(bf16[640,1024]{1,0:T(8,128)(2,1)} %collective-permute-done.11.refs_2_.refs_6_), channel_id=1, source_target_pairs={{0,1},{1,0},{2,3},{3,2},{4,5},{5,4},{6,7},{7,6},{8,9},{9,8},{10,11... | collective-permute-start | bytes 3932168 | tf_op jit(solution)/shard_map/ppermute | solution.py:60
  153.9 14.6 %collective-permute-start.15 = (bf16[128,256]{1,0:T(8,128)(2,1)S(1)}, bf16[128,256]{1,0:T(8,128)(2,1)S(1)}, u32[]{:S(2)}, u32[]{:S(2)}) collective-permute-start(bf16[128,256]{1,0:T(8,128)(2,1)S(1)} %collective-permute-done.13.refs_5_), channel_id=1, source_target_pairs={{0,8},{4,12},{8,0},{12,4},{16,24},{20,28},{24,16},{28,20},{1,9},{5... | collective-permute-start | bytes 196616 | tf_op jit(solution)/shard_map/ppermute | solution.py:60
  154.5 14.0 %collective-permute-start.18 = (bf16[128,256]{1,0:T(8,128)(2,1)S(1)}, bf16[128,256]{1,0:T(8,128)(2,1)S(1)}, u32[]{:S(2)}, u32[]{:S(2)}) collective-permute-start(bf16[128,256]{1,0:T(8,128)(2,1)S(1)} %collective-permute-done.16.refs_8_), channel_id=1, source_target_pairs={{0,8},{4,12},{8,0},{12,4},{16,24},{20,28},{24,16},{28,20},{1,9},{5... | collective-permute-start | bytes 196616 | tf_op jit(solution)/shard_map/ppermute | solution.py:60
  156.0 12.6 %collective-permute-start.19 = (bf16[128,256]{1,0:T(8,128)(2,1)}, bf16[128,256]{1,0:T(8,128)(2,1)S(1)}, u32[]{:S(2)}, u32[]{:S(2)}) collective-permute-start(bf16[128,256]{1,0:T(8,128)(2,1)} %collective-permute-done.17.refs_9_), channel_id=1, source_target_pairs={{0,8},{4,12},{8,0},{12,4},{16,24},{20,28},{24,16},{28,20},{1,9},{5... | collective-permute-start | bytes 196616 | tf_op jit(solution)/shard_map/ppermute | solution.py:60
  168.4 145.6 %collective-permute-start.38 = (bf16[640,1024]{1,0:T(8,128)(2,1)}, bf16[640,1024]{1,0:T(8,128)(2,1)}, u32[]{:S(2)}, u32[]{:S(2)}) collective-permute-start(bf16[640,1024]{1,0:T(8,128)(2,1)} %get-tuple-element.62), channel_id=1, source_target_pairs={{0,1},{1,0},{2,3},{3,2},{4,5},{5,4},{6,7},{7,6},{8,9},{9,8},{10,11... | collective-permute-start | bytes 3932168 | tf_op jit(solution)/shard_map/ppermute | solution.py:60
  294.2 3.8 collective-permute-start.44
  298.0 15.1 %collective-permute-start.45 = (f32[5120]{0:T(1024)S(1)}, f32[5120]{0:T(1024)S(1)}, u32[]{:S(2)}, u32[]{:S(2)}) collective-permute-start(f32[5120]{0:T(1024)S(1)} %add.256), channel_id=1, source_target_pairs={{0,4},{4,0},{8,12},{12,8},{16,20},{20,16},{24,28},{28,24},{1,5},{5... | collective-permute-start | bytes 61448 | tf_op jit(solution)/shard_map/ppermute | solution.py:60
  311.9 10.8 %collective-permute-start.56 = (bf16[4,128,256]{2,1,0:T(8,128)(2,1)}, bf16[4,128,256]{2,1,0:T(8,128)(2,1)S(1)}, u32[]{:S(2)}, u32[]{:S(2)}) collective-permute-start(bf16[4,128,256]{2,1,0:T(8,128)(2,1)} %get-tuple-element.80), channel_id=1, source_target_pairs={{0,8},{4,12},{8,0},{12,4},{16,24},{20,28},{24,16},{28,20},{1,9},{5... | collective-permute-start | bytes 786440 | tf_op jit(solution)/shard_map/ppermute | solution.py:60
  313.1 36.4 %collective-permute-start.41 = (bf16[640,1024]{1,0:T(8,128)(2,1)}, bf16[640,1024]{1,0:T(8,128)(2,1)}, u32[]{:S(2)}, u32[]{:S(2)}) collective-permute-start(bf16[640,1024]{1,0:T(8,128)(2,1)} %get-tuple-element.72), channel_id=1, source_target_pairs={{0,1},{1,0},{2,3},{3,2},{4,5},{5,4},{6,7},{7,6},{8,9},{9,8},{10,11... | collective-permute-start | bytes 3932168 | tf_op jit(solution)/shard_map/ppermute | solution.py:60
  313.1 6.6 %collective-permute-start.46 = (f32[5120]{0:T(1024)S(1)}, f32[5120]{0:T(1024)S(1)}, u32[]{:S(2)}, u32[]{:S(2)}) collective-permute-start(f32[5120]{0:T(1024)S(1)} %add.257), channel_id=1, source_target_pairs={{0,8},{4,12},{8,0},{12,4},{16,24},{20,28},{24,16},{28,20},{1,9},{5... | collective-permute-start | bytes 61448 | tf_op jit(solution)/shard_map/ppermute | solution.py:60
  316.9 38.7 %collective-permute-start.62 = (bf16[4,128,1024]{2,1,0:T(8,128)(2,1)}, bf16[4,128,1024]{2,1,0:T(8,128)(2,1)}, u32[]{:S(2)}, u32[]{:S(2)}) collective-permute-start(bf16[4,128,1024]{2,1,0:T(8,128)(2,1)} %get-tuple-element.84), channel_id=1, source_target_pairs={{0,8},{4,12},{8,0},{12,4},{16,24},{20,28},{24,16},{28,20},{1,9},{5... | collective-permute-start | bytes 3145736 | tf_op jit(solution)/shard_map/ppermute | solution.py:60
  318.2 34.7 %collective-permute-start.53 = (bf16[4,128,768]{2,1,0:T(8,128)(2,1)}, bf16[4,128,768]{2,1,0:T(8,128)(2,1)}, u32[]{:S(2)}, u32[]{:S(2)}) collective-permute-start(bf16[4,128,768]{2,1,0:T(8,128)(2,1)} %get-tuple-element.78), channel_id=1, source_target_pairs={{0,4},{4,0},{8,12},{12,8},{16,20},{20,16},{24,28},{28,24},{1,5},{5... | collective-permute-start | bytes 2359304 | tf_op jit(solution)/shard_map/ppermute | solution.py:60
  319.7 22.6 %collective-permute-start.47 = (f32[5120]{0:T(1024)S(1)}, f32[5120]{0:T(1024)S(1)}, u32[]{:S(2)}, u32[]{:S(2)}) collective-permute-start(f32[5120]{0:T(1024)S(1)} %add.258), channel_id=1, source_target_pairs={{0,16},{4,20},{8,24},{12,28},{16,0},{20,4},{24,8},{28,12},{1,17},{... | collective-permute-start | bytes 61448 | tf_op jit(solution)/shard_map/ppermute | solution.py:60
  322.7 21.7 %collective-permute-start.57 = (bf16[2,128,256]{2,1,0:T(8,128)(2,1)S(1)}, bf16[2,128,256]{2,1,0:T(8,128)(2,1)S(1)}, u32[]{:S(2)}, u32[]{:S(2)}) collective-permute-start(bf16[2,128,256]{2,1,0:T(8,128)(2,1)S(1)} %slice.203), channel_id=1, source_target_pairs={{0,16},{4,20},{8,24},{12,28},{16,0},{20,4},{24,8},{28,12},{1,17},{... | collective-permute-start | bytes 393224 | tf_op jit(solution)/shard_map/ppermute | solution.py:60
  342.3 18.9 %collective-permute-start.21 = (bf16[640,1024]{1,0:T(8,128)(2,1)}, bf16[640,1024]{1,0:T(8,128)(2,1)}, u32[]{:S(2)}, u32[]{:S(2)}) collective-permute-start(bf16[640,1024]{1,0:T(8,128)(2,1)} %get-tuple-element.58), channel_id=1, source_target_pairs={{0,1},{1,0},{2,3},{3,2},{4,5},{5,4},{6,7},{7,6},{8,9},{9,8},{10,11... | collective-permute-start | bytes 3932168 | tf_op jit(solution)/shard_map/ppermute | solution.py:60
  344.5 4.3 collective-permute-start.58
  348.8 27.9 %collective-permute-start.40 = (bf16[640,1024]{1,0:T(8,128)(2,1)}, bf16[640,1024]{1,0:T(8,128)(2,1)S(1)}, u32[]{:S(2)}, u32[]{:S(2)}) collective-permute-start(bf16[640,1024]{1,0:T(8,128)(2,1)} %get-tuple-element.70), channel_id=1, source_target_pairs={{0,1},{1,0},{2,3},{3,2},{4,5},{5,4},{6,7},{7,6},{8,9},{9,8},{10,11... | collective-permute-start | bytes 3932168 | tf_op jit(solution)/shard_map/ppermute | solution.py:60
  349.6 25.8 %collective-permute-start.59 = (bf16[4,128,1024]{2,1,0:T(8,128)(2,1)}, bf16[4,128,1024]{2,1,0:T(8,128)(2,1)S(1)}, u32[]{:S(2)}, u32[]{:S(2)}) collective-permute-start(bf16[4,128,1024]{2,1,0:T(8,128)(2,1)} %get-tuple-element.82), channel_id=1, source_target_pairs={{0,4},{4,0},{8,12},{12,8},{16,20},{20,16},{24,28},{28,24},{1,5},{5... | collective-permute-start | bytes 3145736 | tf_op jit(solution)/shard_map/ppermute | solution.py:60
  352.8 31.7 %collective-permute-start.42 = (bf16[640,1024]{1,0:T(8,128)(2,1)S(1)}, bf16[640,1024]{1,0:T(8,128)(2,1)S(1)}, u32[]{:S(2)}, u32[]{:S(2)}) collective-permute-start(bf16[640,1024]{1,0:T(8,128)(2,1)S(1)} %add_convert_fusion), channel_id=1, source_target_pairs={{0,2},{1,3},{2,0},{3,1},{4,6},{5,7},{6,4},{7,5},{8,10},{9,11},{10,... | collective-permute-start | bytes 3932168 | tf_op jit(solution)/shard_map/ppermute | solution.py:60
  355.6 21.0 %collective-permute-start.54 = (bf16[2,128,768]{2,1,0:T(8,128)(2,1)S(1)}, bf16[2,128,768]{2,1,0:T(8,128)(2,1)S(1)}, u32[]{:S(2)}, u32[]{:S(2)}) collective-permute-start(bf16[2,128,768]{2,1,0:T(8,128)(2,1)S(1)} %slice.199), channel_id=1, source_target_pairs={{0,8},{4,12},{8,0},{12,4},{16,24},{20,28},{24,16},{28,20},{1,9},{5... | collective-permute-start | bytes 1179656 | tf_op jit(solution)/shard_map/ppermute | solution.py:60
  361.3 27.8 %collective-permute-start.37 = (bf16[640,1024]{1,0:T(8,128)(2,1)S(1)}, bf16[640,1024]{1,0:T(8,128)(2,1)S(1)}, u32[]{:S(2)}, u32[]{:S(2)}) collective-permute-start(bf16[640,1024]{1,0:T(8,128)(2,1)S(1)} %copy-done.38), channel_id=1, source_target_pairs={{0,1},{1,0},{2,3},{3,2},{4,5},{5,4},{6,7},{7,6},{8,9},{9,8},{10,11... | collective-permute-start | bytes 3932168 | tf_op jit(solution)/shard_map/ppermute | solution.py:60
  375.4 37.2 %collective-permute-start.39 = (bf16[640,1024]{1,0:T(8,128)(2,1)S(1)}, bf16[640,1024]{1,0:T(8,128)(2,1)S(1)}, u32[]{:S(2)}, u32[]{:S(2)}) collective-permute-start(bf16[640,1024]{1,0:T(8,128)(2,1)S(1)} %copy-done.11), channel_id=1, source_target_pairs={{0,2},{1,3},{2,0},{3,1},{4,6},{5,7},{6,4},{7,5},{8,10},{9,11},{10,... | collective-permute-start | bytes 3932168 | tf_op jit(solution)/shard_map/ppermute | solution.py:60
  376.7 39.3 %collective-permute-start.20 = (bf16[640,1024]{1,0:T(8,128)(2,1)S(1)}, bf16[640,1024]{1,0:T(8,128)(2,1)S(1)}, u32[]{:S(2)}, u32[]{:S(2)}) collective-permute-start(bf16[640,1024]{1,0:T(8,128)(2,1)S(1)} %copy-done.39), channel_id=1, source_target_pairs={{0,1},{1,0},{2,3},{3,2},{4,5},{5,4},{6,7},{7,6},{8,9},{9,8},{10,11... | collective-permute-start | bytes 3932168 | tf_op jit(solution)/shard_map/ppermute | solution.py:60
  376.7 63.3 %collective-permute-start.22 = (bf16[640,1024]{1,0:T(8,128)(2,1)S(1)}, bf16[640,1024]{1,0:T(8,128)(2,1)S(1)}, u32[]{:S(2)}, u32[]{:S(2)}) collective-permute-start(bf16[640,1024]{1,0:T(8,128)(2,1)S(1)} %add_convert_fusion.2), channel_id=1, source_target_pairs={{0,2},{1,3},{2,0},{3,1},{4,6},{5,7},{6,4},{7,5},{8,10},{9,11},{10,... | collective-permute-start | bytes 3932168 | tf_op jit(solution)/shard_map/ppermute | solution.py:60
  384.5 63.0 %collective-permute-start.63 = (bf16[2,128,1024]{2,1,0:T(8,128)(2,1)S(1)}, bf16[2,128,1024]{2,1,0:T(8,128)(2,1)S(1)}, u32[]{:S(2)}, u32[]{:S(2)}) collective-permute-start(bf16[2,128,1024]{2,1,0:T(8,128)(2,1)S(1)} %slice.197), channel_id=1, source_target_pairs={{0,16},{4,20},{8,24},{12,28},{16,0},{20,4},{24,8},{28,12},{1,17},{... | collective-permute-start | bytes 1572872 | tf_op jit(solution)/shard_map/ppermute | solution.py:60
  389.1 61.3 %collective-permute-start.60 = (bf16[2,128,1024]{2,1,0:T(8,128)(2,1)S(1)}, bf16[2,128,1024]{2,1,0:T(8,128)(2,1)S(1)}, u32[]{:S(2)}, u32[]{:S(2)}) collective-permute-start(bf16[2,128,1024]{2,1,0:T(8,128)(2,1)S(1)} %slice.198), channel_id=1, source_target_pairs={{0,8},{4,12},{8,0},{12,4},{16,24},{20,28},{24,16},{28,20},{1,9},{5... | collective-permute-start | bytes 1572872 | tf_op jit(solution)/shard_map/ppermute | solution.py:60
  412.6 43.6 %collective-permute-start.55 = (bf16[1,128,768]{2,1,0:T(8,128)(2,1)S(1)}, bf16[1,128,768]{2,1,0:T(8,128)(2,1)S(1)}, u32[]{:S(2)}, u32[]{:S(2)}) collective-permute-start(bf16[1,128,768]{2,1,0:T(8,128)(2,1)S(1)} %slice.202), channel_id=1, source_target_pairs={{0,16},{4,20},{8,24},{12,28},{16,0},{20,4},{24,8},{28,12},{1,17},{... | collective-permute-start | bytes 589832 | tf_op jit(solution)/shard_map/ppermute | solution.py:60
  447.5 1.6 collective-permute-start.48
  448.4 13.2 %collective-permute-start.64 = (bf16[1,128,1024]{2,1,0:T(8,128)(2,1)}, bf16[1,128,1024]{2,1,0:T(8,128)(2,1)S(1)}, u32[]{:S(2)}, u32[]{:S(2)}) collective-permute-start(bf16[1,128,1024]{2,1,0:T(8,128)(2,1)} %slice.200), channel_id=1, source_target_pairs={{0,4},{4,0},{8,12},{12,8},{16,20},{20,16},{24,28},{28,24},{1,5},{5... | collective-permute-start | bytes 786440 | tf_op jit(solution)/shard_map/ppermute | solution.py:60
  449.0 5.6 %collective-permute-start.49 = (f32[7296]{0:T(1024)S(1)}, f32[7296]{0:T(1024)S(1)}, u32[]{:S(2)}, u32[]{:S(2)}) collective-permute-start(f32[7296]{0:T(1024)S(1)} %add.260), channel_id=1, source_target_pairs={{0,2},{1,3},{2,0},{3,1},{4,6},{5,7},{6,4},{7,5},{8,10},{9,11},{10,... | collective-permute-start | bytes 87560 | tf_op jit(solution)/shard_map/ppermute | solution.py:60
  451.3 16.0 %collective-permute-start.61 = (bf16[1,128,1024]{2,1,0:T(8,128)(2,1)}, bf16[1,128,1024]{2,1,0:T(8,128)(2,1)S(1)}, u32[]{:S(2)}, u32[]{:S(2)}) collective-permute-start(bf16[1,128,1024]{2,1,0:T(8,128)(2,1)} %slice.201), channel_id=1, source_target_pairs={{0,16},{4,20},{8,24},{12,28},{16,0},{20,4},{24,8},{28,12},{1,17},{... | collective-permute-start | bytes 786440 | tf_op jit(solution)/shard_map/ppermute | solution.py:60
  454.7 4.0 collective-permute-start.50
  458.7 5.0 %collective-permute-start.51 = (f32[7296]{0:T(1024)S(1)}, f32[7296]{0:T(1024)S(1)}, u32[]{:S(2)}, u32[]{:S(2)}) collective-permute-start(f32[7296]{0:T(1024)S(1)} %add.262), channel_id=1, source_target_pairs={{0,8},{4,12},{8,0},{12,4},{16,24},{20,28},{24,16},{28,20},{1,9},{5... | collective-permute-start | bytes 87560 | tf_op jit(solution)/shard_map/ppermute | solution.py:60
  463.6 5.6 %collective-permute-start.52 = (f32[7296]{0:T(1024)S(1)}, f32[7296]{0:T(1024)S(1)}, u32[]{:S(2)}, u32[]{:S(2)}) collective-permute-start(f32[7296]{0:T(1024)S(1)} %add.263), channel_id=1, source_target_pairs={{0,16},{4,20},{8,24},{12,28},{16,0},{20,4},{24,8},{28,12},{1,17},{... | collective-permute-start | bytes 87560 | tf_op jit(solution)/shard_map/ppermute | solution.py:60
  (47 other events, 1329.6 us)

commit v2 on v1

--- a/solution.py
+++ b/solution.py
@@ -60,12 +60,47 @@
     return lax.ppermute(block, axis, [(i, i ^ bit) for i in range(size)])
 
 
-def gather_pieces(block, axis, bits):
-    pieces = {0: block}
-    for bit in bits:
-        for j in list(pieces):
-            pieces[j | bit] = swap(pieces[j], axis, bit)
-    return [pieces[j] for j in range(len(pieces))]
+def tie(*values):
+    return lax.optimization_barrier(values)
+
+
+def gather_far(block, axis, bits):
+    pieces = [block]
+    for bit in bits[1:]:
+        pieces = pieces + [swap(piece, axis, bit) for piece in pieces]
+    return pieces
+
+
+def gather_near(pieces, axis):
+    pieces = [x for piece in pieces for x in (piece, swap(piece, axis, 1))]
+    return pieces
+
+
+class Pack:
+    def __init__(self, block, axis, bits):
+        self.rows, self.axis, self.bits = block.shape[0], axis, list(bits)
+        self.arrays, self.owners = [block], [[0]]
+
+    def double(self):
+        bit = self.bits.pop(0)
+        held = self.arrays[0] if len(self.arrays) == 1 else jnp.concatenate(self.arrays, axis=0)
+        self.owners.append([j ^ bit for owners in self.owners for j in owners])
+        self.arrays.append(swap(held, self.axis, bit))
+
+    def place(self, refs, where, number, columns):
+        for ref, owners in zip(refs, self.owners):
+            for at, j in enumerate(owners):
+                rows = pl.ds(pl.multiple_of((number ^ j) * self.rows, self.rows), self.rows)
+                where[rows, :] = ref[at * self.rows : (at + 1) * self.rows, columns]
+
+
+def tie_packs(*packs, beside=()):
+    flat = tie(*beside, *[x for pack in packs for x in pack.arrays])
+    at = len(beside)
+    for pack in packs:
+        pack.arrays = list(flat[at : at + len(pack.arrays)])
+        at += len(pack.arrays)
+    return list(flat[: len(beside)])
 
 
 def halving_order(bits):
@@ -75,32 +110,39 @@
     return [bits[0] ^ j for j in rest] + rest
 
 
-def scatter_halves(send, keep, axis, bits):
-    terms = [keep]
-    for at, bit in enumerate(bits):
-        got = swap(send, axis, bit)
-        terms = [t.astype(f32) for t in terms] + [got.astype(f32)]
-        total = sum(terms)
-        if at == len(bits) - 1:
-            return total[0]
-        half = total.shape[0] // 2
-        send = total[:half].astype(bf16)
-        terms = [total[half:]]
-    return terms[0][0].astype(f32)
-
-
-def scatter_parts(parts, axis, bits):
-    parts = dict(enumerate(parts))
-    for at, bit in enumerate(bits):
-        last = at == len(bits) - 1
-        kept = {}
-        for j in sorted(parts):
-            if not j & bit:
-                got = swap(parts[j | bit], axis, bit)
-                total = parts[j].astype(f32) + got.astype(f32)
-                kept[j] = total if last or j == 0 else total.astype(bf16)
-        parts = kept
-    return parts[0].astype(f32)
+class Halving:
+    def __init__(self, send, keep, axis, bits):
+        self.send, self.terms, self.axis, self.bits = send, [keep], axis, list(bits)
+
+    def swap(self):
+        self.got = swap(self.send, self.axis, self.bits.pop(0))
+
+    def add(self):
+        total = sum([x.astype(f32) for x in self.terms] + [self.got.astype(f32)])
+        if self.bits:
+            half = total.shape[0] // 2
+            self.send = total[:half].astype(bf16)
+            self.terms = [total[half:]]
+        else:
+            self.total = total[0]
+
+    def most(self):
+        while len(self.bits) > 1:
+            self.swap()
+            self.add()
+
+    def finish(self):
+        while self.bits:
+            self.swap()
+            self.add()
+        return self.total
+
+
+def tie_halves(values, *halvings):
+    flat = tie(*values, *[x.got for x in halvings])
+    for x, got in zip(halvings, flat[len(values) :]):
+        x.got = got
+    return flat[: len(values)]
 
 
 def sum_everywhere(value, axes):
@@ -116,48 +158,60 @@
 
 
 def own_block(rows, columns):
-    return pl.BlockSpec((rows, columns), lambda i, ids, *_: (ids[0] ^ i, 0))
+    return pl.BlockSpec((rows, columns), lambda i, ids, *_: (ids[0] ^ ids[2 + i], 0))
 
 
 def step_block(rows, columns):
     return pl.BlockSpec((rows, columns), lambda i, *_: (i, 0))
 
 
-def place_pieces(pieces, where, number):
-    rows = pieces[0].shape[0]
-    for j, piece in enumerate(pieces):
-        where[pl.ds(pl.multiple_of((number ^ j) * rows, rows), rows), :] = piece[...]
+def half_blocks(groups, rows, columns):
+    half = groups // 2
+    shape = (pl.Squeezed(), rows, columns)
+    return [
+        pl.BlockSpec(shape, lambda i, *_: (jnp.minimum(i, half - 1), 0, 0)),
+        pl.BlockSpec(shape, lambda i, *_: (jnp.maximum(i - half, 0), 0, 0)),
+    ]
+
+
+def store_half(send, keep, value, step, groups):
+    @pl.when(step < groups // 2)
+    def _():
+        send[...] = value
+
+    @pl.when(step >= groups // 2)
+    def _():
+        keep[...] = value
+
+
+class Tokens:
+    def __init__(self, pieces, order):
+        self.groups, (self.rows, self.model) = len(pieces), pieces[0].shape
+        if self.groups <= 4:
+            self.arrays = [pieces[j] for j in order]
+            self.specs = [resident(x.shape) for x in pieces]
+        else:
+            self.arrays = [jnp.concatenate([pieces[j] for j in order], axis=0)]
+            self.specs = [step_block(self.rows, self.model)]
 
 
 def pick_piece(pieces, where, step):
-    for j, piece in enumerate(pieces):
-
-        @pl.when(step == j)
+    if len(pieces) == 1:
+        where[...] = pieces[0][...]
+        return
+    for at, piece in enumerate(pieces):
+
+        @pl.when(step == at)
         def _(piece=piece):
             where[...] = piece[...]
 
 
-def store_part(parts, value, step, rows):
-    if len(parts) == 1:
-        parts[0][pl.ds(pl.multiple_of(step * rows, rows), rows), :] = value
-        return
-    for j, part in enumerate(parts):
-
-        @pl.when(step == j)
-        def _(part=part):
-            part[...] = value
-
-
-def store_halves(send, keep, total, number, order):
+def store_halves(send, keep, total, number, order, columns=slice(None)):
     half, rows = send.shape[0], send.shape[1]
     for at, j in enumerate(order):
         where = send if at < half else keep
         block = total[pl.ds(pl.multiple_of((number ^ j) * rows, rows), rows), :]
-        where[at % half] = block.astype(bf16)
-
-
-def halves_shape(size, rows, columns):
-    return jax.ShapeDtypeStruct((max(size // 2, 1), rows, columns), bf16)
+        where[at % half, :, columns] = block.astype(bf16)
 
 
 def call(kernel, name, grid, prefetch, operands, specs, outs, out_specs, scratch, flops, extra=0):
@@ -207,23 +261,23 @@
     return done[0] if len(done) == 1 else jnp.concatenate(done, axis=1)
 
 
-def project_qkv(ids, info, sent, gain, shift, weight, bias, tables, width):
-    groups, pieces = len(sent), len(weight)
-    rows, model = sent[0].shape
+def project_qkv(ids, info, sent, gain, shift, pack, bias, tables, width):
+    groups, held, pieces = sent.groups, len(sent.arrays), len(pack.arrays)
+    rows, model = sent.rows, sent.model
 
     def kernel(ids, info, *refs):
-        sent_refs, refs = refs[:groups], refs[groups:]
+        sent_refs, refs = refs[:held], refs[held:]
         weight_refs, refs = refs[:pieces], refs[pieces:]
         gain, shift, bias, cos, low, high, q_out, k_out, v_out, whole, block = refs
         step = pl.program_id(0)
 
         @pl.when(step == 0)
         def _():
-            place_pieces(weight_refs, whole, ids[1])
+            pack.place(weight_refs, whole, ids[1], slice(0, 3 * width))
 
         pick_piece(sent_refs, block, step)
         qkv = dot_nn(shift_gain(block[...], gain, shift), whole[...]) + bias[...]
-        first = (ids[0] ^ step) * (rows // SEG)
+        first = (ids[0] ^ ids[2 + step]) * (rows // SEG)
         for at in range(rows // SEG):
             number = first + at
             table = pl.ds(pl.multiple_of(info[number // NB, number % NB, 4] * SEG, SEG), SEG)
@@ -233,7 +287,7 @@
             k_out[own, :] = turn(qkv[own, width : 2 * width], *tabs, 1.0).astype(bf16)
         v_out[...] = qkv[:, 2 * width :].astype(bf16)
 
-    operands = [*sent, *weight, gain, shift, bias, *tables]
+    operands = [*sent.arrays, *pack.arrays, gain, shift, bias, *tables]
     out = shaped(groups * rows, width)
     return call(
         kernel,
@@ -241,7 +295,7 @@
         (groups,),
         [ids, info],
         operands,
-        [resident(x.shape) for x in operands],
+        sent.specs + [resident(x.shape) for x in operands[held:]],
         [out] * 3,
         [own_block(rows, width)] * 3,
         [pltpu.VMEM((model, 3 * width), bf16), pltpu.VMEM((rows, model), bf16)],
@@ -249,31 +303,30 @@
     )
 
 
-def project_grad(ids, grad, weight):
-    groups, pieces = len(grad), len(weight)
-    rows, model = grad[0].shape
-    width = weight[0].shape[1]
+def project_grad(ids, grad, pack, width):
+    groups, held, pieces = grad.groups, len(grad.arrays), len(pack.arrays)
+    rows, model = grad.rows, grad.model
 
     def kernel(ids, *refs):
-        grad_refs, refs = refs[:groups], refs[groups:]
+        grad_refs, refs = refs[:held], refs[held:]
         weight_refs, (out, whole, block) = refs[:pieces], refs[pieces:]
         step = pl.program_id(0)
 
         @pl.when(step == 0)
         def _():
-            place_pieces(weight_refs, whole, ids[1])
+            pack.place(weight_refs, whole, ids[1], slice(3 * width, 4 * width))
 
         pick_piece(grad_refs, block, step)
         out[...] = dot_nn(block[...], whole[...]).astype(bf16)
 
-    operands = [*grad, *weight]
+    operands = [*grad.arrays, *pack.arrays]
     return call(
         kernel,
         "project_grad",
         (groups,),
         [ids],
         operands,
-        [resident(x.shape) for x in operands],
+        grad.specs + [resident(x.shape) for x in operands[held:]],
         [shaped(groups * rows, width)],
         [own_block(rows, width)],
         [pltpu.VMEM((model, width), bf16), pltpu.VMEM((rows, model), bf16)],
@@ -403,82 +456,58 @@
     )
 
 
-def project_context(ids, context, grad, weight, order):
-    groups, pieces = len(grad), len(weight)
-    rows, model = grad[0].shape
-    width = context.shape[1]
-    parts = groups if groups <= 4 else 1
+def project_context(ids, context, pack, groups, model):
+    pieces = len(pack.arrays)
+    rows, width = context.shape[0] // groups, context.shape[1]
 
     def kernel(ids, ctx, *refs):
-        grad_refs, refs = refs[:groups], refs[groups:]
-        weight_refs, refs = refs[:pieces], refs[pieces:]
-        part_refs, refs = refs[:parts], refs[parts:]
-        send, keep, whole, block, total = refs
+        weight_refs, (send, keep, whole) = refs[:pieces], refs[pieces:]
         step = pl.program_id(0)
 
         @pl.when(step == 0)
         def _():
-            place_pieces(weight_refs, whole, ids[1])
-            total[...] = jnp.zeros_like(total)
-
-        pick_piece(grad_refs, block, step)
-        store_part(part_refs, dot_nt(ctx[...], whole[...]).astype(bf16), step, rows)
-        total[...] += dot_tn(block[...], ctx[...])
-
-        @pl.when(step == groups - 1)
-        def _():
-            store_halves(send, keep, total, ids[1], order)
-
-    operands = [context, *grad, *weight]
-    part = shaped(groups * rows // parts, model)
-    halves = halves_shape(pieces, model // pieces, width)
-    outs = [part] * parts + [halves] * 2
-    out = call(
+            pack.place(weight_refs, whole, ids[1], slice(3 * width, 4 * width))
+
+        store_half(send, keep, dot_nt(ctx[...], whole[...]).astype(bf16), step, groups)
+
+    operands = [context, *pack.arrays]
+    half = shaped(groups // 2, rows, model)
+    return call(
         kernel,
         "project_context",
         (groups,),
         [ids],
         operands,
         [own_block(rows, width)] + [resident(x.shape) for x in operands[1:]],
-        outs,
-        [resident(x.shape) for x in outs],
-        [
-            pltpu.VMEM((model, width), bf16),
-            pltpu.VMEM((rows, model), bf16),
-            pltpu.VMEM((model, width), f32),
-        ],
-        4 * groups * rows * model * width,
-    )
-    return split_parts(out[:parts], groups), out[parts], out[parts + 1]
-
-
-def split_parts(parts, groups):
-    if len(parts) == groups:
-        return list(parts)
-    rows = parts[0].shape[0] // groups
-    return [parts[0][j * rows : (j + 1) * rows] for j in range(groups)]
-
-
-def mlp_forward(ids, sent, gain, shift, fc, bias, out):
-    groups, pieces = len(sent), len(fc)
-    rows, model = sent[0].shape
-    units = fc[0].shape[1]
-    parts = groups if groups <= 4 else 1
+        [half] * 2,
+        half_blocks(groups, rows, model),
+        [pltpu.VMEM((model, width), bf16)],
+        2 * groups * rows * model * width,
+    )
+
+
+def mlp_forward(ids, sent, grad, gain, shift, fc, bias, out, out_order):
+    groups, held, pieces = sent.groups, len(sent.arrays), len(fc.arrays)
+    rows, model = sent.rows, sent.model
+    units = fc.arrays[0].shape[1]
 
     def kernel(ids, *refs):
-        sent_refs, refs = refs[:groups], refs[groups:]
+        sent_refs, refs = refs[:held], refs[held:]
+        grad_refs, refs = refs[:held], refs[held:]
         fc_refs, refs = refs[:pieces], refs[pieces:]
         out_refs, refs = refs[:pieces], refs[pieces:]
-        gain, shift, bias, act_ref, slope_ref = refs[:5]
-        part_refs, (fc_whole, out_whole, block) = refs[5 : 5 + parts], refs[5 + parts :]
+        gain, shift, bias, act_ref, slope_ref, send, keep, out_send, out_keep = refs[:9]
+        fc_whole, out_whole, block, grad_block, total = refs[9:]
         step = pl.program_id(0)
 
         @pl.when(step == 0)
         def _():
-            place_pieces(fc_refs, fc_whole, ids[1])
-            place_pieces(out_refs, out_whole, ids[1])
+            fc.place(fc_refs, fc_whole, ids[1], slice(None))
+            out.place(out_refs, out_whole, ids[1], slice(None))
+            total[...] = jnp.zeros_like(total)
 
         pick_piece(sent_refs, block, step)
+        pick_piece(grad_refs, grad_block, step)
         hidden = dot_nn(shift_gain(block[...], gain, shift), fc_whole[...]) + bias[...]
         size = jnp.abs(hidden)
         ratio = 1.0 / (1.0 + TAIL_SLOPE * size)
@@ -491,50 +520,64 @@
         active = (hidden * chance).astype(bf16)
         act_ref[...] = active
         slope_ref[...] = chance + hidden * bell * 0.3989422804014327
-        store_part(part_refs, dot_nt(active, out_whole[...]).astype(bf16), step, rows)
-
-    operands = [*sent, *fc, *out, gain, shift, bias]
-    part = shaped(groups * rows // parts, model)
-    outs = [shaped(groups * rows, units), shaped(groups * rows, units, dtype=f32)] + [part] * parts
-    done = call(
+        store_half(send, keep, dot_nt(active, out_whole[...]).astype(bf16), step, groups)
+        total[...] += dot_tn(grad_block[...], active)
+
+        @pl.when(step == groups - 1)
+        def _():
+            store_halves(out_send, out_keep, total, ids[1], out_order)
+
+    operands = [*sent.arrays, *grad.arrays, *fc.arrays, *out.arrays, gain, shift, bias]
+    count = model // fc.rows
+    outs = [
+        shaped(groups * rows, units),
+        shaped(groups * rows, units, dtype=f32),
+        shaped(groups // 2, rows, model),
+        shaped(groups // 2, rows, model),
+        shaped(count // 2, fc.rows, units),
+        shaped(count // 2, fc.rows, units),
+    ]
+    return call(
         kernel,
         "mlp_forward",
         (groups,),
         [ids],
         operands,
-        [resident(x.shape) for x in operands],
+        sent.specs + grad.specs + [resident(x.shape) for x in operands[2 * held :]],
         outs,
-        [step_block(rows, units)] * 2 + [resident(part.shape)] * parts,
+        [step_block(rows, units)] * 2
+        + half_blocks(groups, rows, model)
+        + [resident(x.shape) for x in outs[4:]],
         [
             pltpu.VMEM((model, units), bf16),
             pltpu.VMEM((model, units), bf16),
             pltpu.VMEM((rows, model), bf16),
+            pltpu.VMEM((rows, model), bf16),
+            pltpu.VMEM((model, units), f32),
         ],
-        4 * groups * rows * model * units,
-    )
-    return done[0], done[1], split_parts(done[2:], groups)
-
-
-def mlp_backward(ids, sent, grad, active, slope, gain, shift, fc, out, fc_order, out_order):
-    groups, pieces = len(sent), len(fc)
-    rows, model = sent[0].shape
-    units = fc[0].shape[1]
-
-    def kernel(ids, act_ref, slope_ref, *refs):
-        sent_refs, refs = refs[:groups], refs[groups:]
-        grad_refs, refs = refs[:groups], refs[groups:]
+        6 * groups * rows * model * units,
+    )
+
+
+def mlp_backward(ids, sent, grad, slope, gain, shift, fc, out, fc_order):
+    groups, held, pieces = sent.groups, len(sent.arrays), len(fc.arrays)
+    rows, model = sent.rows, sent.model
+    units = fc.arrays[0].shape[1]
+
+    def kernel(ids, slope_ref, *refs):
+        sent_refs, refs = refs[:held], refs[held:]
+        grad_refs, refs = refs[:held], refs[held:]
         fc_refs, refs = refs[:pieces], refs[pieces:]
         out_refs, refs = refs[:pieces], refs[pieces:]
-        gain, shift, back_ref, bias_ref, sums_ref, fc_send, fc_keep, out_send, out_keep = refs[:9]
-        fc_whole, out_whole, block, grad_block, fc_total, out_total = refs[9:]
+        gain, shift, back_ref, bias_ref, sums_ref, fc_send, fc_keep = refs[:7]
+        fc_whole, out_whole, block, grad_block, fc_total = refs[7:]
         step = pl.program_id(0)
 
         @pl.when(step == 0)
         def _():
-            place_pieces(fc_refs, fc_whole, ids[1])
-            place_pieces(out_refs, out_whole, ids[1])
+            fc.place(fc_refs, fc_whole, ids[1], slice(None))
+            out.place(out_refs, out_whole, ids[1], slice(None))
             fc_total[...] = jnp.zeros_like(fc_total)
-            out_total[...] = jnp.zeros_like(out_total)
             bias_ref[...] = jnp.zeros_like(bias_ref)
             sums_ref[...] = jnp.zeros_like(sums_ref)
 
@@ -548,27 +591,30 @@
         sums_ref[0:1, :] += jnp.sum(back * token.astype(f32), axis=0, keepdims=True)
         sums_ref[1:2, :] += jnp.sum(back, axis=0, keepdims=True)
         fc_total[...] += dot_tn(shift_gain(token, gain, shift), hidden)
-        out_total[...] += dot_tn(grad_block[...], act_ref[...])
 
         @pl.when(step == groups - 1)
         def _():
             store_halves(fc_send, fc_keep, fc_total, ids[1], fc_order)
-            store_halves(out_send, out_keep, out_total, ids[1], out_order)
-
-    operands = [active, slope, *sent, *grad, *fc, *out, gain, shift]
-    halves = halves_shape(pieces, model // pieces, units)
+
+    operands = [slope, *sent.arrays, *grad.arrays, *fc.arrays, *out.arrays, gain, shift]
+    count = model // fc.rows
     outs = [
         shaped(groups * rows, model, dtype=f32),
         shaped(8, units, dtype=f32),
         shaped(8, model, dtype=f32),
-    ] + [halves] * 4
+        shaped(count // 2, fc.rows, units),
+        shaped(count // 2, fc.rows, units),
+    ]
     return call(
         kernel,
         "mlp_backward",
         (groups,),
         [ids],
         operands,
-        [step_block(rows, units)] * 2 + [resident(x.shape) for x in operands[2:]],
+        [step_block(rows, units)]
+        + sent.specs
+        + grad.specs
+        + [resident(x.shape) for x in operands[1 + 2 * held :]],
         outs,
         [step_block(rows, model)] + [resident(x.shape) for x in outs[1:]],
         [
@@ -577,36 +623,39 @@
             pltpu.VMEM((rows, model), bf16),
             pltpu.VMEM((rows, model), bf16),
             pltpu.VMEM((model, units), f32),
-            pltpu.VMEM((model, units), f32),
         ],
-        8 * groups * rows * model * units,
-    )
-
-
-def qkv_backward(ids, info, tables, dq, dk, dv, sent, back_mlp, gain, shift, gain_mlp, weight, order):
-    groups, pieces = len(sent), len(weight)
-    rows, model = sent[0].shape
+        6 * groups * rows * model * units,
+    )
+
+
+def qkv_backward(
+    ids, info, tables, dq, dk, dv, context, sent, grad, back_mlp, gain, shift, gain_mlp, pack, dp_order
+):
+    groups, held, pieces = sent.groups, len(sent.arrays), len(pack.arrays)
+    rows, model = sent.rows, sent.model
     width = dq.shape[1]
-    parts = groups if groups <= 4 else 1
-
-    def kernel(ids, info, dq_ref, dk_ref, dv_ref, mlp_ref, *refs):
-        sent_refs, refs = refs[:groups], refs[groups:]
+
+    def kernel(ids, info, dq_ref, dk_ref, dv_ref, ctx_ref, mlp_ref, *refs):
+        sent_refs, refs = refs[:held], refs[held:]
+        grad_refs, refs = refs[:held], refs[held:]
         weight_refs, refs = refs[:pieces], refs[pieces:]
         gain, shift, gain_mlp, cos, low, high = refs[:6]
-        part_refs, refs = refs[6 : 6 + parts], refs[6 + parts :]
-        bias_ref, sums_ref, send, keep, whole, block, total, grads = refs
+        part_send, part_keep, bias_ref, sums_ref, send, keep = refs[6:12]
+        whole, block, grad_block, total, dense_total, grads = refs[12:]
         step = pl.program_id(0)
 
         @pl.when(step == 0)
         def _():
-            place_pieces(weight_refs, whole, ids[1])
+            pack.place(weight_refs, whole, ids[1], slice(0, 3 * width))
             total[...] = jnp.zeros_like(total)
+            dense_total[...] = jnp.zeros_like(dense_total)
             bias_ref[...] = jnp.zeros_like(bias_ref)
             sums_ref[...] = jnp.zeros_like(sums_ref)
 
         pick_piece(sent_refs, block, step)
+        pick_piece(grad_refs, grad_block, step)
         grads[:, :width] = dq_ref[...]
-        first = (ids[0] ^ step) * (rows // SEG)
+        first = (ids[0] ^ ids[2 + step]) * (rows // SEG)
         for at in range(rows // SEG):
             number = first + at
             table = pl.ds(pl.multiple_of(info[number // NB, number % NB, 4] * SEG, SEG), SEG)
@@ -620,41 +669,61 @@
         sums_ref[0:1, :] += jnp.sum(back * token.astype(f32), axis=0, keepdims=True)
         sums_ref[1:2, :] += jnp.sum(back, axis=0, keepdims=True)
         part = (back * gain[...] + mlp_ref[...] * gain_mlp[...]).astype(bf16)
-        store_part(part_refs, part, step, rows)
+        store_half(part_send, part_keep, part, step, groups)
         total[...] += dot_tn(shift_gain(token, gain, shift), grads[...])
+        dense_total[...] += dot_tn(grad_block[...], ctx_ref[...])
 
         @pl.when(step == groups - 1)
         def _():
-            store_halves(send, keep, total, ids[1], order)
-
-    operands = [dq, dk, dv, back_mlp, *sent, *weight, gain, shift, gain_mlp, *tables]
-    part = shaped(groups * rows // parts, model)
-    halves = halves_shape(pieces, model // pieces, 3 * width)
-    outs = (
-        [part] * parts
-        + [shaped(8, 3 * width, dtype=f32), shaped(8, model, dtype=f32)]
-        + [halves] * 2
-    )
-    done = call(
+            store_halves(send, keep, total, ids[1], dp_order, slice(0, 3 * width))
+            store_halves(send, keep, dense_total, ids[1], dp_order, slice(3 * width, 4 * width))
+
+    operands = [
+        dq,
+        dk,
+        dv,
+        context,
+        back_mlp,
+        *sent.arrays,
+        *grad.arrays,
+        *pack.arrays,
+        gain,
+        shift,
+        gain_mlp,
+        *tables,
+    ]
+    count = model // pack.rows
+    outs = [
+        shaped(groups // 2, rows, model),
+        shaped(groups // 2, rows, model),
+        shaped(8, 3 * width, dtype=f32),
+        shaped(8, model, dtype=f32),
+        shaped(count // 2, pack.rows, 4 * width),
+        shaped(count // 2, pack.rows, 4 * width),
+    ]
+    return call(
         kernel,
         "qkv_backward",
         (groups,),
         [ids, info],
         operands,
-        [own_block(rows, width)] * 3
+        [own_block(rows, width)] * 4
         + [step_block(rows, model)]
-        + [resident(x.shape) for x in operands[4:]],
+        + sent.specs
+        + grad.specs
+        + [resident(x.shape) for x in operands[5 + 2 * held :]],
         outs,
-        [resident(x.shape) for x in outs],
+        half_blocks(groups, rows, model) + [resident(x.shape) for x in outs[2:]],
         [
             pltpu.VMEM((model, 3 * width), bf16),
             pltpu.VMEM((rows, model), bf16),
+            pltpu.VMEM((rows, model), bf16),
             pltpu.VMEM((model, 3 * width), f32),
+            pltpu.VMEM((model, width), f32),
             pltpu.VMEM((rows, 3 * width), bf16),
         ],
-        4 * groups * rows * model * 3 * width,
-    )
-    return (split_parts(done[:parts], groups), *done[parts:])
+        2 * groups * rows * model * 7 * width,
+    )
 
 
 def tree_table(segment_ids, parent_ids):
@@ -721,33 +790,55 @@
 ):
     tensor_rank = lax.axis_index("tensor")
     data_rank = lax.axis_index("dp")
-    ids = jnp.stack([tensor_rank, data_rank]).astype(jnp.int32)
     rows_local = stream_in.shape[0]
     model = stream_in.shape[1]
     qkv_width = qkv_weight.shape[1]
     heads = qkv_width // (3 * HD)
     width = heads * HD
     units = fc_weight.shape[1]
-    tensor_bits = bits_of(lax.axis_size("tensor"))
+    groups = lax.axis_size("tensor")
+    tensor_bits = bits_of(groups)
     far_first = tensor_bits[:0:-1] + tensor_bits[:1]
+    order = halving_order(tensor_bits)
+    ids = jnp.stack([tensor_rank, data_rank, *order]).astype(jnp.int32)
     data_bits = bits_of(lax.axis_size("dp"))
     rows_first = data_bits[:0:-1] + data_bits[:1]
     columns_first = data_bits[:1] + data_bits[:0:-1]
+    out_bits, fc_bits = columns_first[::-1], rows_first[::-1]
+
+    attn_pack = Pack(
+        jnp.concatenate(
+            [by_kind(qkv_weight.astype(bf16), heads), dense_weight.astype(bf16).T], axis=1
+        ),
+        "dp",
+        rows_first,
+    )
+    fc_pack = Pack(fc_weight.astype(bf16), "dp", rows_first)
+    out_pack = Pack(out_weight.astype(bf16).T, "dp", columns_first)
 
     row_mean = jnp.mean(stream_in, axis=-1, keepdims=True)
     centred = stream_in - row_mean
     row_var = jnp.mean(centred * centred, axis=-1, keepdims=True)
     inv_std = lax.rsqrt(row_var + eps_norm)
     normalized = centred * inv_std
-    sent_norm = normalized.astype(bf16)
-
-    qkv_pieces = gather_pieces(by_kind(qkv_weight.astype(bf16), heads), "dp", rows_first)
-    dense_pieces = gather_pieces(dense_weight.astype(bf16).T, "dp", columns_first)
-    fc_pieces = gather_pieces(fc_weight.astype(bf16), "dp", rows_first)
-    out_pieces = gather_pieces(out_weight.astype(bf16).T, "dp", columns_first)
-    sent = gather_pieces(sent_norm, "tensor", far_first)
-    first_grad = lax.optimization_barrier((out_grad, sent[-1]))[0]
-    grad = gather_pieces(first_grad, "tensor", far_first)
+    sent = gather_far(normalized.astype(bf16), "tensor", tensor_bits)
+
+    attn_pack.double()
+    out_pack.double()
+    tie_packs(attn_pack, out_pack)
+    rounds = len(data_bits)
+    for number in range(1, rounds - 1):
+        attn_pack.double()
+        fc_pack.double()
+    sent = tie_packs(attn_pack, fc_pack, out_pack, beside=sent)
+    out_grad, sent[0] = tie(out_grad, sent[0])
+    grad = gather_far(out_grad, "tensor", tensor_bits)
+    sent = gather_near(sent, "tensor")
+    attn_pack.double()
+    fc_pack.double()
+    while len(out_pack.bits) > 1:
+        out_pack.double()
+    sent = Tokens(tie_packs(attn_pack, fc_pack, out_pack, beside=sent), order)
 
     info = tree_table(segment_ids, parent_ids)
     tables = angle_tables()
@@ -759,53 +850,80 @@
     fc_bias_own = lax.dynamic_slice_in_dim(fc_bias, tensor_rank * units, units)[None, :]
 
     queries, keys, values = project_qkv(
-        ids, info, sent, gain_attn, shift_attn, qkv_pieces, qkv_bias_own, tables, width
-    )
-    active, slope, mlp_parts = mlp_forward(
-        ids, sent, gain_mlp, shift_mlp, fc_pieces, fc_bias_own, out_pieces
-    )
-    mlp_sum = scatter_parts(mlp_parts, "tensor", tensor_bits)
-    grad_context = project_grad(ids, grad, dense_pieces)
-    context, dq, dk, dv = attention(info, tables, queries, keys, values, grad_context)
-    out_bits, fc_bits = columns_first[::-1], rows_first[::-1]
-    attn_parts, dense_send, dense_keep = project_context(
-        ids, context, grad, dense_pieces, halving_order(out_bits)
-    )
-    attn_sum = scatter_parts(attn_parts, "tensor", tensor_bits)
-    back_mlp, fc_bias_sums, mlp_sums, fc_send, fc_keep, out_send, out_keep = mlp_backward(
+        ids, info, sent, gain_attn, shift_attn, attn_pack, qkv_bias_own, tables, width
+    )
+    queries, keys, values, *grad = tie(queries, keys, values, *grad)
+    grad = Tokens(gather_near(grad, "tensor"), order)
+    grad_context = project_grad(ids, grad, attn_pack, width)
+    fc_pack.double()
+    out_pack.double()
+    done = attention(info, tables, queries, keys, values, grad_context)
+    context, dq, dk, dv = tie_packs(fc_pack, out_pack, beside=done)
+    attn_parts = Halving(
+        *project_context(ids, context, attn_pack, groups, model), "tensor", tensor_bits
+    )
+    attn_parts.most()
+    sent.arrays[0], attn_parts.send = tie(sent.arrays[0], attn_parts.send)
+    attn_parts.swap()
+    done = mlp_forward(
         ids,
         sent,
         grad,
-        active,
-        slope,
         gain_mlp,
         shift_mlp,
-        fc_pieces,
-        out_pieces,
-        halving_order(fc_bits),
+        fc_pack,
+        fc_bias_own,
+        out_pack,
         halving_order(out_bits),
     )
-    back_parts, qkv_bias_sums, attn_sums, qkv_send, qkv_keep = qkv_backward(
+    active, slope, mlp_send, mlp_keep, out_send, out_keep = tie_halves(done, attn_parts)
+    attn_parts.add()
+    mlp_parts = Halving(mlp_send, mlp_keep, "tensor", tensor_bits)
+    mlp_parts.most()
+    slope, mlp_parts.send = tie(slope, mlp_parts.send)
+    out_parts = Halving(out_send, out_keep, "dp", out_bits)
+    mlp_parts.swap()
+    out_parts.swap()
+    done = mlp_backward(
+        ids, sent, grad, slope, gain_mlp, shift_mlp, fc_pack, out_pack, halving_order(fc_bits)
+    )
+    back_mlp, fc_bias_sums, mlp_sums, fc_send, fc_keep = tie_halves(done, mlp_parts, out_parts)
+    mlp_parts.add()
+    out_parts.add()
+    back_mlp, out_parts.send = tie(back_mlp, out_parts.send)
+    fc_parts = Halving(fc_send, fc_keep, "dp", fc_bits)
+    out_parts.swap()
+    fc_parts.swap()
+    done = qkv_backward(
         ids,
         info,
         tables,
         dq,
         dk,
         dv,
+        context,
         sent,
+        grad,
         back_mlp,
         gain_attn,
         shift_attn,
         gain_mlp,
-        qkv_pieces,
+        attn_pack,
         halving_order(fc_bits),
     )
-    grad_sent = scatter_parts(back_parts, "tensor", tensor_bits)
-
-    fc_weight_grad = scatter_halves(fc_send, fc_keep, "dp", fc_bits)
-    out_weight_grad = scatter_halves(out_send, out_keep, "dp", out_bits).T
-    dense_weight_grad = scatter_halves(dense_send, dense_keep, "dp", out_bits).T
-    qkv_weight_grad = by_head(scatter_halves(qkv_send, qkv_keep, "dp", fc_bits), heads)
+    done = tie_halves(done, out_parts, fc_parts)
+    back_send, back_keep, qkv_bias_sums, attn_sums, qkv_send, qkv_keep = done
+    out_parts.add()
+    fc_parts.add()
+    attn_sum, mlp_sum = attn_parts.total, mlp_parts.total
+    qkv_parts = Halving(qkv_send, qkv_keep, "dp", fc_bits)
+    grad_sent = Halving(back_send, back_keep, "tensor", tensor_bits).finish()
+
+    fc_weight_grad = fc_parts.finish()
+    out_weight_grad = out_parts.finish().T
+    attn_total = qkv_parts.finish()
+    dense_weight_grad = attn_total[:, 3 * width :].T
+    qkv_weight_grad = by_head(attn_total[:, : 3 * width], heads)
 
     attn_out = attn_sum + dense_bias
     mlp_out = mlp_sum + out_bias
@@ -818,31 +936,34 @@
     )
 
     residual_part = jnp.sum(out_grad.astype(f32), axis=0)
-    squares = jnp.stack([jnp.sum(output * output), jnp.sum(attn_out * attn_out), jnp.sum(mlp_out * mlp_out)])
-    count_all = float(rows_local * lax.axis_size("dp") * lax.axis_size("tensor") * model)
-
+    squares = jnp.stack(
+        [jnp.sum(output * output), jnp.sum(attn_out * attn_out), jnp.sum(mlp_out * mlp_out)]
+    )
+    count_all = float(rows_local * lax.axis_size("dp") * groups * model)
     fc_bias_spread = lax.dynamic_update_slice(
         jnp.zeros(fc_bias.shape, f32), fc_bias_sums[0], (tensor_rank * units,)
     )
-    early = jnp.concatenate(
-        [residual_part, mlp_sums[0], mlp_sums[1], fc_bias_spread, jnp.pad(squares, (0, 125))]
-    )
-    early = sum_everywhere(early, ("tensor", "dp"))
     qkv_bias_spread = lax.dynamic_update_slice(
         jnp.zeros(qkv_bias.shape, f32), by_head(qkv_bias_sums[0], heads), (tensor_rank * qkv_width,)
     )
-    late = jnp.concatenate([attn_sums[0], attn_sums[1], qkv_bias_spread])
-    late = sum_everywhere(late, ("tensor", "dp"))
-
-    residual_grad = early[:model]
-    gain_mlp_grad = early[model : 2 * model]
-    shift_mlp_grad = early[2 * model : 3 * model]
-    fc_bias_grad = early[3 * model : 3 * model + fc_bias.shape[0]]
-    squares = early[3 * model + fc_bias.shape[0] :][:3]
-    gain_attn_grad = late[:model]
-    shift_attn_grad = late[model : 2 * model]
-    qkv_bias_grad = late[2 * model :]
-    root_squares = jnp.sqrt(squares / count_all)
+    sums = [
+        residual_part,
+        mlp_sums[0],
+        mlp_sums[1],
+        attn_sums[0],
+        attn_sums[1],
+        fc_bias_spread,
+        qkv_bias_spread,
+        jnp.pad(squares, (0, 125)),
+    ]
+    packed = sum_everywhere(jnp.concatenate(sums), ("tensor", "dp"))
+    split = []
+    for part in sums:
+        split.append(packed[: part.shape[0]])
+        packed = packed[part.shape[0] :]
+    residual_grad, gain_mlp_grad, shift_mlp_grad, gain_attn_grad, shift_attn_grad = split[:5]
+    fc_bias_grad, qkv_bias_grad, squares = split[5:]
+    root_squares = jnp.sqrt(squares[:3] / count_all)
     return (
         output,
         stream_grad,

time: 476 us -> 391 us (0.82)
  waiting for transfers between devices: 171 us -> 96.7 us
  starting transfers between devices: 72.3 us -> 29 us
  other arithmetic: 29.6 us -> 47.9 us
  local copies, waits for them, and re-layouts: 20.6 us -> 33.3 us
    ppermute x65 -> x35, waiting for transfers between devices: 171 us -> 96.7 us  [swap(): return lax.ppermute(block, axis, [(i, i ^ bit) for i in range(size)])]
    ppermute x65 -> x35, starting transfers between devices: 72.3 us -> 29 us  [swap(): return lax.ppermute(block, axis, [(i, i ^ bit) for i in range(size)])]
    add x9, other arithmetic: 3.9 us -> 16.3 us  [add(): total = sum([x.astype(f32) for x in self.terms] + [self.got.astype(f32)])]
    concatenate x2 -> x8, other arithmetic: 2.02 us -> 10.1 us  [the longest x6 8.08 us: double(): jnp.concatenate(self.arrays, axis=0)]
    unnamed x103 -> x92, local copies, waits for them, and re-layouts: 8.1 us -> 14.8 us
    convert_element_type x5 -> x2, other arithmetic: 7.79 us -> 1.4 us  [the longest x1 1.37 us: local(): sent = gather_far(normalized.astype(bf16), 'tensor', tensor_bits)]
    slice x13 -> x15, local copies, waits for them, and re-layouts: 4.95 us -> 10.8 us  [the longest x9 7.95 us: add(): self.send = total[:half].astype(bf16)]
  transfers between devices with their start and end apart: 65 -> 35, of which waited for: 26 -> 16; matrix products, arithmetic and copies ran while one was open for 9% -> 16% of each run, Pallas kernels for 37% -> 44%
where the time goes in v2:
time: 391 us; the launch traced here: 385 us
  Pallas kernels  176 us (45%)
  waiting for transfers between devices  96.7 us (25%)
  other arithmetic  47.9 us (12%)
  local copies, waits for them, and re-layouts  33.3 us (9%)
  starting transfers between devices  29 us (7%)
    pallas_call x7, Pallas kernels, call(): pl.pallas_call(kernel, grid_spec=pltpu.PrefetchScalarGridSpec(num_scalar_...  176 us
    ppermute x35, waiting for transfers between devices, swap(): return lax.ppermute(block, axis, [(i, i ^ bit) for i in range(size)])  96.7 us
    ppermute x35, starting transfers between devices, swap(): return lax.ppermute(block, axis, [(i, i ^ bit) for i in range(size)])  29 us
    add x9, other arithmetic, add(): total = sum([x.astype(f32) for x in self.terms] + [self.got.astype(f32)])  16.3 us
    unnamed x92, local copies, waits for them, and re-layouts  14.8 us
    concatenate x6, other arithmetic, double(): jnp.concatenate(self.arrays, axis=0)  8.08 us
    slice x9, local copies, waits for them, and re-layouts, add(): self.send = total[:half].astype(bf16)  7.95 us
  transfers between devices with their start and end apart: 35, of which 16 were waited for; matrix products, arithmetic and copies ran while one was open for 16% of the time, Pallas kernels for 44%

profile of v2, /device:TPU:0, one launch (start us, length us, event | category | flops | bytes accessed | tf_op | source)
XLA Modules:
  0.0 384.6 jit_solution(4225835161758260094)
XLA Ops:
  0.7 2.1 reduce_sum.85
  3.6 1.4 fusion.7.refs_3_
  5.0 2.9 collective-permute-start
  8.4 2.7 collective-permute-start.1
  11.1 1.2 copy.110
  12.3 1.6 collective-permute-start.2
  14.4 15.1 %collective-permute-done.1.refs_5_.refs_1_.refs_9_ = bf16[128,1024]{1,0:T(8,128)(2,1)S(1)} collective-permute-done((bf16[128,1024]{1,0:T(8,128)(2,1)S(1)}, bf16[128,1024]{1,0:T(8,128)(2,1)S(1)}, u32[]{:S(2)}, u32[]{:S(2)}) %collective-permute-start.1) | collective-permute-done | bytes 262176 | tf_op jit(solution)/shard_map/ppermute | solution.py:60
  29.5 0.9 pad_maximum_fusion.3
  31.2 3.0 collective-permute-done.4.refs_9_
  34.2 11.0 %collective-permute-done.3.refs_6_.refs_2_.refs_10_ = bf16[256,1024]{1,0:T(8,128)(2,1)S(1)} collective-permute-done((bf16[256,1024]{1,0:T(8,128)(2,1)}, bf16[256,1024]{1,0:T(8,128)(2,1)S(1)}, u32[]{:S(2)}, u32[]{:S(2)}) %collective-permute-start.3) | collective-permute-done | bytes 524320 | tf_op jit(solution)/shard_map/ppermute | solution.py:60
  45.7 1.0 pad_maximum_fusion
  46.8 1.5 collective-permute-start.7
  49.1 1.7 collective-permute-start.9
  54.2 1.0 pad_maximum_fusion.4
  55.3 19.9 %collective-permute-done.9.refs_14_ = bf16[256,1024]{1,0:T(8,128)(2,1)} collective-permute-done((bf16[256,1024]{1,0:T(8,128)(2,1)}, bf16[256,1024]{1,0:T(8,128)(2,1)}, u32[]{:S(2)}, u32[]{:S(2)}) %collective-permute-start.9) | collective-permute-done | bytes 524320 | tf_op jit(solution)/shard_map/ppermute | solution.py:60
  75.2 4.0 %fusion.17 = (f32[1280,128]{1,0:T(8,128)}, f32[1280,128]{1,0:T(8,128)}, f32[1280,128]{1,0:T(8,128)}) fusion(s32[128]{0:T(128)S(1)} %get-tuple-element.326, s32[128]{0:T(128)S(1)} %get-tuple-element.327, pred[128]{0:T(512)(128)(4,1)S(1)} %compare_and_fusion, f32[1280]{0:T(1024)S(1)} %iota_convert_fusion), kind=kLoop, calls=%fused_computation.57 | loop fusion | flops 3932160 | bytes 1972352 | tf_op jit(solution)/shard_map/jit(_where)/select_n | solution.py:757
  79.2 9.0 %collective-permute-done.8.refs_10_ = bf16[256,1024]{1,0:T(8,128)(2,1)S(1)} collective-permute-done((bf16[256,1024]{1,0:T(8,128)(2,1)S(1)}, bf16[256,1024]{1,0:T(8,128)(2,1)S(1)}, u32[]{:S(2)}, u32[]{:S(2)}) %collective-permute-start.8) | collective-permute-done | bytes 524320 | tf_op jit(solution)/shard_map/ppermute | solution.py:60
  89.0 12.1 %project_qkv.1 = (bf16[2560,256]{1,0:T(8,128)(2,1)}, bf16[2560,256]{1,0:T(8,128)(2,1)}, bf16[2560,256]{1,0:T(8,128)(2,1)}) custom-call(s32[6]{0:T(128)} %stack.31.ids, s32[1,20,5]{2,1,0:T(8,128)} %stack.32.info, bf16[640,1024]{1,0:T(8,128)(2,1)} %collective-permute-done.6.refs_0_, bf16[640,1024]{1,0:T(8,128)(2,1)} %collective-permute-done.5.refs_1_, ...), custom_call_target="tpu_custom_call" | custom-call | flops 4026531840 | bytes 13249536 | tf_op jit(solution)/shard_map/project_qkv/pallas_call | solution.py:219
  101.7 2.2 pad_maximum_fusion.2
  104.5 2.2 pad_maximum_fusion.1
  107.1 7.1 %project_grad.1.do_ref = bf16[2560,256]{1,0:T(8,128)(2,1)} custom-call(s32[6]{0:T(128)} %stack.31.ids, bf16[640,1024]{1,0:T(8,128)(2,1)} %collective-permute-done.11.refs_0_.refs_4_, bf16[640,1024]{1,0:T(8,128)(2,1)} %collective-permute-done.12.refs_1_.refs_5_, bf16[640,1024]{1,0:T(8,128)(2,1)} %collective-permute-done.10.refs_2_.refs_6_, ...), custom_call_target="tpu_custom_call" | custom-call | flops 1342177280 | bytes 8650752 | tf_op jit(solution)/shard_map/project_grad/pallas_call | solution.py:219
  114.3 55.4 %attention.1 = (bf16[2560,256]{1,0:T(8,128)(2,1)}, bf16[2560,256]{1,0:T(8,128)(2,1)}, bf16[2560,256]{1,0:T(8,128)(2,1)}, bf16[2560,256]{1,0:T(8,128)(2,1)}) custom-call(s32[1,20,5]{2,1,0:T(8,128)} %stack.32.info, bf16[2560,256]{1,0:T(8,128)(2,1)} %get-tuple-element.139.q_ref, bf16[2560,256]{1,0:T(8,128)(2,1)} %project_grad.1.do_ref, ...), custom_call_target="tpu_custom_call" | custom-call | flops 31406948352 | bytes 12451840 | tf_op jit(solution)/shard_map/attention/pallas_call | solution.py:219
  169.7 7.3 %project_context.1 = (bf16[2,640,1024]{2,1,0:T(8,128)(2,1)}, bf16[2,640,1024]{2,1,0:T(8,128)(2,1)}) custom-call(s32[6]{0:T(128)} %stack.31.ids, bf16[2560,256]{1,0:T(8,128)(2,1)} %get-tuple-element.154.ctx.ctx_ref, bf16[128,1024]{1,0:T(8,128)(2,1)} %copy-done.10, bf16[128,1024]{1,0:T(8,128)(2,1)} %copy-done.13, bf16[256,1024]{1,0:T(8,128)(2,1)} %copy-done.18, ...), custom_call_target="tpu_custom_call" | custom-call | flops 1342177280 | bytes 8650752 | tf_op jit(solution)/shard_map/project_context/pallas_call | solution.py:219
  177.0 1.3 dynamic_slice.7
  178.3 3.8 collective-permute-done.15
  182.1 2.9 convert_add_fusion.2
  185.0 2.3 copy-done.3
  187.3 1.3 slice.263
  189.1 39.9 %mlp_forward.1 = (bf16[2560,1024]{1,0:T(8,128)(2,1)}, f32[2560,1024]{1,0:T(8,128)}, bf16[2,640,1024]{2,1,0:T(8,128)(2,1)}, bf16[2,640,1024]{2,1,0:T(8,128)(2,1)}...) custom-call(s32[6]{0:T(128)} %stack.31.ids, bf16[640,1024]{1,0:T(8,128)(2,1)} %collective-permute-done.6.refs_0_, ...), custom_call_target="tpu_custom_call" | custom-call | flops 16106127360 | bytes 37761024 | tf_op jit(solution)/shard_map/mlp_forward/pallas_call | solution.py:219
  229.2 1.4 collective-permute-start.19
  230.5 3.7 collective-permute-done.17
  234.3 2.9 convert_add_fusion.1
  237.2 2.4 copy-done.4
  239.6 1.3 slice.262
  240.8 1.5 collective-permute-start.18
  242.3 28.9 %mlp_backward.1 = (f32[2560,1024]{1,0:T(8,128)}, f32[8,1024]{1,0:T(8,128)}, f32[8,1024]{1,0:T(8,128)}, bf16[4,128,1024]{2,1,0:T(8,128)(2,1)}, bf16[4,128,1024]{2,1,0:T(8,128)(2,1)}) custom-call(s32[6]{0:T(128)} %stack.31.ids, f32[2560,1024]{1,0:T(8,128)} %get-tuple-element.176.slope_ref, bf16[640,1024]{1,0:T(8,128)(2,1)} %collective-permute-done.6.refs_0_, ...), custom_call_target="tpu_custom_call" | custom-call | flops 16106127360 | bytes 37822464 | tf_op jit(solution)/shard_map/mlp_backward/pallas_call | solution.py:219
  271.9 1.5 collective-permute-start.21
  273.4 1.9 convert_add_fusion.6
  275.3 1.4 copy-done.5
  276.7 0.9 slice.266
  277.6 3.4 collective-permute-start.20
  281.0 25.5 %qkv_backward.1 = (bf16[2,640,1024]{2,1,0:T(8,128)(2,1)}, bf16[2,640,1024]{2,1,0:T(8,128)(2,1)}, f32[8,768]{1,0:T(8,128)}, f32[8,1024]{1,0:T(8,128)}, bf16[4,128...) custom-call(s32[6]{0:T(128)} %stack.31.ids, s32[1,20,5]{2,1,0:T(8,128)} %stack.32.info, ...), custom_call_target="tpu_custom_call" | custom-call | flops 9395240960 | bytes 37687296 | tf_op jit(solution)/shard_map/qkv_backward/pallas_call | solution.py:219
  309.2 2.6 collective-permute-done.22
  311.7 2.9 convert_add_fusion
  314.7 1.3 slice.261
  315.9 1.5 collective-permute-start.23
  317.5 2.2 convert_add_fusion.4
  319.7 1.0 slice.264
  323.6 0.9 fusion.43
  324.5 10.5 %collective-permute-done.32 = bf16[2,128,1024]{2,1,0:T(8,128)(2,1)} collective-permute-done((bf16[2,128,1024]{2,1,0:T(8,128)(2,1)}, bf16[2,128,1024]{2,1,0:T(8,128)(2,1)}, u32[]{:S(2)}, u32[]{:S(2)}) %collective-permute-start.32) | collective-permute-done | bytes 524320 | tf_op jit(solution)/shard_map/ppermute | solution.py:60
  335.0 1.5 slice_add_fusion.4
  337.5 1.6 convert_add_fusion.5
  340.0 7.0 %collective-permute-done.23 = bf16[1,640,1024]{2,1,0:T(8,128)(2,1)S(1)} collective-permute-done((bf16[1,640,1024]{2,1,0:T(8,128)(2,1)}, bf16[1,640,1024]{2,1,0:T(8,128)(2,1)S(1)}, u32[]{:S(2)}, u32[]{:S(2)}) %collective-permute-start.23) | collective-permute-done | bytes 1310752 | tf_op jit(solution)/shard_map/ppermute | solution.py:60
  349.4 7.6 %multiply_reduce_fusion.2 = (f32[]{:T(128)}, f32[640,1024]{1,0:T(8,128)}, f32[]{:T(128)}, f32[]{:T(128)}, f32[640,1024]{1,0:T(8,128)}, /*index=5*/f32[1024]{0:T(1024)S(1)}) fusion(f32[1024]{0:T(1024)S(1)} %copy-done.35, bf16[1,640,1024]{2,1,0:T(8,128)(2,1)S(1)} %copy-done.22, f32[2,640,1024]{2,1,0:T(8,128)} %copy-done.4, f32[640,1024]{1,0:T(8,128)S(1)} %copy-done.1, ...), kind=kLoop, calls=%fused_computation.22 | loop fusion | flops 16382973 | bytes 20994060 | tf_op jit(solution)/shard_map/reduce_sum | solution.py:940
  357.1 2.0 constant_dynamic-update-slice_fusion
  360.4 1.6 collective-permute-start.25
  361.9 1.8 fusion.18
  363.7 2.0 copy.117
  366.3 1.8 fusion.19
  368.1 1.8 collective-permute-done.26
  370.7 4.6 %collective-permute-done.31 = bf16[1,128,1024]{2,1,0:T(8,128)(2,1)S(1)} collective-permute-done((bf16[1,128,1024]{2,1,0:T(8,128)(2,1)}, bf16[1,128,1024]{2,1,0:T(8,128)(2,1)S(1)}, u32[]{:S(2)}, u32[]{:S(2)}) %collective-permute-start.31) | collective-permute-done | bytes 262176 | tf_op jit(solution)/shard_map/ppermute | solution.py:60
  375.3 1.0 collective-permute-done.27
  377.1 0.9 copy.115
  378.8 2.7 collective-permute-done.28
  (189 shorter events, 28.0 us)
Async XLA Ops:
  0.6 2.5 copy-start
  3.6 4.4 %copy-start.30 = (f32[128,768]{1,0:T(8,128)S(1)}, f32[128,768]{1,0:T(8,128)}, u32[]{:S(2)}) copy-start(f32[128,768]{1,0:T(8,128)} %param.23) | copy-start | bytes 1179652
  3.6 4.7 %copy-start.31 = (f32[256,128]{1,0:T(8,128)S(1)}, f32[256,128]{1,0:T(8,128)}, u32[]{:S(2)}) copy-start(f32[256,128]{1,0:T(8,128)} %param.25) | copy-start | bytes 393220
  5.0 8.9 %copy-start.28 = (f32[128,1024]{1,0:T(8,128)S(1)}, f32[128,1024]{1,0:T(8,128)}, u32[]{:S(2)}) copy-start(f32[128,1024]{1,0:T(8,128)} %param.27) | copy-start | bytes 1572868
  5.0 9.3 %copy-start.34 = (s32[2560]{0:T(1024)S(1)}, s32[2560]{0:T(1024)}, u32[]{:S(2)}) copy-start(s32[2560]{0:T(1024)} %param.17) | copy-start | bytes 30724
  5.0 25.5 %copy-start.33 = (s32[2560]{0:T(1024)S(1)}, s32[2560]{0:T(1024)}, u32[]{:S(2)}) copy-start(s32[2560]{0:T(1024)} %param.18) | copy-start | bytes 30724
  5.0 40.3 %collective-permute-start = (bf16[640,1024]{1,0:T(8,128)(2,1)}, bf16[640,1024]{1,0:T(8,128)(2,1)}, u32[]{:S(2)}, u32[]{:S(2)}) collective-permute-start(bf16[640,1024]{1,0:T(8,128)(2,1)} %fusion.7.refs_3_), channel_id=1, source_target_pairs={{0,2},{1,3},{2,0},{3,1},{4,6},{5,7},{6,4},{7,5},{8,10},{9,11},{10,... | collective-permute-start | bytes 3932168 | tf_op jit(solution)/shard_map/ppermute | solution.py:60
  8.4 40.7 %copy-start.10 = (bf16[128,1024]{1,0:T(8,128)(2,1)}, bf16[128,1024]{1,0:T(8,128)(2,1)S(1)}, u32[]{:S(2)}) copy-start(bf16[128,1024]{1,0:T(8,128)(2,1)S(1)} %pad_maximum_fusion.6.refs_4_.refs_0_.refs_8_) | copy-start | bytes 786436
  8.4 21.1 %collective-permute-start.1 = (bf16[128,1024]{1,0:T(8,128)(2,1)S(1)}, bf16[128,1024]{1,0:T(8,128)(2,1)S(1)}, u32[]{:S(2)}, u32[]{:S(2)}) collective-permute-start(bf16[128,1024]{1,0:T(8,128)(2,1)S(1)} %pad_maximum_fusion.6.refs_4_.refs_0_.refs_8_), channel_id=1, source_target_pairs={{0,16},{4,20},{8,24},{12,28},{16,0},{20,4},{24,8},{28,12},{1,17},{... | collective-permute-start | bytes 786440 | tf_op jit(solution)/shard_map/ppermute | solution.py:60
  12.2 41.4 %copy-start.14 = (bf16[1024,128]{0,1:T(8,128)(2,1)}, bf16[1024,128]{0,1:T(8,128)(2,1)S(1)}, u32[]{:S(2)}) copy-start(bf16[1024,128]{0,1:T(8,128)(2,1)S(1)} %copy.110) | copy-start | bytes 786436
  12.3 38.6 %copy-start.8 = (bf16[640,1024]{1,0:T(8,128)(2,1)S(1)}, bf16[640,1024]{1,0:T(8,128)(2,1)}, u32[]{:S(2)}) copy-start(bf16[640,1024]{1,0:T(8,128)(2,1)} %refs_7_.2) | copy-start | bytes 3932164
  12.3 17.3 %collective-permute-start.2 = (bf16[128,1024]{1,0:T(8,128)(2,1)S(1)}, bf16[128,1024]{1,0:T(8,128)(2,1)S(1)}, u32[]{:S(2)}, u32[]{:S(2)}) collective-permute-start(bf16[128,1024]{1,0:T(8,128)(2,1)S(1)} %bitcast.80), channel_id=1, source_target_pairs={{0,4},{4,0},{8,12},{12,8},{16,20},{20,16},{24,28},{28,24},{1,5},{5... | collective-permute-start | bytes 786440 | tf_op jit(solution)/shard_map/ppermute | solution.py:60
  13.9 41.3 %copy-start.16 = (bf16[128,1024]{1,0:T(8,128)(2,1)}, bf16[128,1024]{1,0:T(8,128)(2,1)S(1)}, u32[]{:S(2)}) copy-start(bf16[128,1024]{1,0:T(8,128)(2,1)S(1)} %convert_element_type.136.refs_8_) | copy-start | bytes 786436
  13.9 20.3 %collective-permute-start.4 = (bf16[128,1024]{1,0:T(8,128)(2,1)S(1)}, bf16[128,1024]{1,0:T(8,128)(2,1)}, u32[]{:S(2)}, u32[]{:S(2)}) collective-permute-start(bf16[128,1024]{1,0:T(8,128)(2,1)S(1)} %convert_element_type.136.refs_8_), channel_id=1, source_target_pairs={{0,16},{4,20},{8,24},{12,28},{16,0},{20,4},{24,8},{28,12},{1,17},{... | collective-permute-start | bytes 786440 | tf_op jit(solution)/shard_map/ppermute | solution.py:60
  29.5 25.7 %copy-start.13 = (bf16[128,1024]{1,0:T(8,128)(2,1)}, bf16[128,1024]{1,0:T(8,128)(2,1)S(1)}, u32[]{:S(2)}) copy-start(bf16[128,1024]{1,0:T(8,128)(2,1)S(1)} %collective-permute-done.1.refs_5_.refs_1_.refs_9_) | copy-start | bytes 786436
  29.5 25.7 %copy-start.25 = (bf16[128,1024]{1,0:T(8,128)(2,1)}, bf16[128,1024]{1,0:T(8,128)(2,1)S(1)}, u32[]{:S(2)}) copy-start(bf16[128,1024]{1,0:T(8,128)(2,1)S(1)} %collective-permute-done.2.refs_13_) | copy-start | bytes 786436
  30.4 14.8 %collective-permute-start.3 = (bf16[256,1024]{1,0:T(8,128)(2,1)}, bf16[256,1024]{1,0:T(8,128)(2,1)S(1)}, u32[]{:S(2)}, u32[]{:S(2)}) collective-permute-start(bf16[256,1024]{1,0:T(8,128)(2,1)} %pad_maximum_fusion.3), channel_id=1, source_target_pairs={{0,8},{4,12},{8,0},{12,4},{16,24},{20,28},{24,16},{28,20},{1,9},{5... | collective-permute-start | bytes 1572872 | tf_op jit(solution)/shard_map/ppermute | solution.py:60
  45.2 34.0 %copy-start.18 = (bf16[256,1024]{1,0:T(8,128)(2,1)}, bf16[256,1024]{1,0:T(8,128)(2,1)S(1)}, u32[]{:S(2)}) copy-start(bf16[256,1024]{1,0:T(8,128)(2,1)S(1)} %collective-permute-done.3.refs_6_.refs_2_.refs_10_) | copy-start | bytes 1572868
  45.2 43.0 %collective-permute-start.5 = (bf16[640,1024]{1,0:T(8,128)(2,1)}, bf16[640,1024]{1,0:T(8,128)(2,1)}, u32[]{:S(2)}, u32[]{:S(2)}) collective-permute-start(bf16[640,1024]{1,0:T(8,128)(2,1)} %fusion.7.refs_3_), channel_id=1, source_target_pairs={{0,1},{1,0},{2,3},{3,2},{4,5},{5,4},{6,7},{7,6},{8,9},{9,8},{10,11... | collective-permute-start | bytes 3932168 | tf_op jit(solution)/shard_map/ppermute | solution.py:60
  45.2 43.0 %collective-permute-start.6 = (bf16[640,1024]{1,0:T(8,128)(2,1)}, bf16[640,1024]{1,0:T(8,128)(2,1)}, u32[]{:S(2)}, u32[]{:S(2)}) collective-permute-start(bf16[640,1024]{1,0:T(8,128)(2,1)} %collective-permute-done.refs_2_), channel_id=1, source_target_pairs={{0,1},{1,0},{2,3},{3,2},{4,5},{5,4},{6,7},{7,6},{8,9},{9,8},{10,11... | collective-permute-start | bytes 3932168 | tf_op jit(solution)/shard_map/ppermute | solution.py:60
  46.8 41.4 %collective-permute-start.7 = (bf16[512,1024]{1,0:T(8,128)(2,1)}, bf16[512,1024]{1,0:T(8,128)(2,1)}, u32[]{:S(2)}, u32[]{:S(2)}) collective-permute-start(bf16[512,1024]{1,0:T(8,128)(2,1)} %pad_maximum_fusion), channel_id=1, source_target_pairs={{0,4},{4,0},{8,12},{12,8},{16,20},{20,16},{24,28},{28,24},{1,5},{5... | collective-permute-start | bytes 3145736 | tf_op jit(solution)/shard_map/ppermute | solution.py:60
  49.1 26.1 %collective-permute-start.9 = (bf16[256,1024]{1,0:T(8,128)(2,1)}, bf16[256,1024]{1,0:T(8,128)(2,1)}, u32[]{:S(2)}, u32[]{:S(2)}) collective-permute-start(bf16[256,1024]{1,0:T(8,128)(2,1)} %pad_maximum_fusion.5), channel_id=1, source_target_pairs={{0,16},{4,20},{8,24},{12,28},{16,0},{20,4},{24,8},{28,12},{1,17},{... | collective-permute-start | bytes 1572872 | tf_op jit(solution)/shard_map/ppermute | solution.py:60
  50.8 50.3 %collective-permute-start.10 = (bf16[640,1024]{1,0:T(8,128)(2,1)S(1)}, bf16[640,1024]{1,0:T(8,128)(2,1)}, u32[]{:S(2)}, u32[]{:S(2)}) collective-permute-start(bf16[640,1024]{1,0:T(8,128)(2,1)S(1)} %copy-done.8), channel_id=1, source_target_pairs={{0,2},{1,3},{2,0},{3,1},{4,6},{5,7},{6,4},{7,5},{8,10},{9,11},{10,... | collective-permute-start | bytes 3932168 | tf_op jit(solution)/shard_map/ppermute | solution.py:60
  75.2 13.0 %collective-permute-start.8 = (bf16[256,1024]{1,0:T(8,128)(2,1)S(1)}, bf16[256,1024]{1,0:T(8,128)(2,1)S(1)}, u32[]{:S(2)}, u32[]{:S(2)}) collective-permute-start(bf16[256,1024]{1,0:T(8,128)(2,1)S(1)} %pad_maximum_fusion.4), channel_id=1, source_target_pairs={{0,8},{4,12},{8,0},{12,4},{16,24},{20,28},{24,16},{28,20},{1,9},{5... | collective-permute-start | bytes 1572872 | tf_op jit(solution)/shard_map/ppermute | solution.py:60
  89.0 12.7 %copy-start.15 = (bf16[1024,128]{0,1:T(8,128)(2,1)S(1)}, bf16[1024,128]{0,1:T(8,128)(2,1)}, u32[]{:S(2)}) copy-start(bf16[1024,128]{0,1:T(8,128)(2,1)} %copy-done.14) | copy-start | bytes 786436
  89.0 15.5 %copy-start.17 = (bf16[128,1024]{1,0:T(8,128)(2,1)S(1)}, bf16[128,1024]{1,0:T(8,128)(2,1)}, u32[]{:S(2)}) copy-start(bf16[128,1024]{1,0:T(8,128)(2,1)} %copy-done.16) | copy-start | bytes 786436
  101.1 6.0 %collective-permute-start.11 = (bf16[640,1024]{1,0:T(8,128)(2,1)}, bf16[640,1024]{1,0:T(8,128)(2,1)}, u32[]{:S(2)}, u32[]{:S(2)}) collective-permute-start(bf16[640,1024]{1,0:T(8,128)(2,1)} %collective-permute-done.10.refs_2_.refs_6_), channel_id=1, source_target_pairs={{0,1},{1,0},{2,3},{3,2},{4,5},{5,4},{6,7},{7,6},{8,9},{9,8},{10,11... | collective-permute-start | bytes 3932168 | tf_op jit(solution)/shard_map/ppermute | solution.py:60
  101.2 6.0 %collective-permute-start.12 = (bf16[640,1024]{1,0:T(8,128)(2,1)S(1)}, bf16[640,1024]{1,0:T(8,128)(2,1)}, u32[]{:S(2)}, u32[]{:S(2)}) collective-permute-start(bf16[640,1024]{1,0:T(8,128)(2,1)S(1)} %copy-done.8), channel_id=1, source_target_pairs={{0,1},{1,0},{2,3},{3,2},{4,5},{5,4},{6,7},{7,6},{8,9},{9,8},{10,11... | collective-permute-start | bytes 3932168 | tf_op jit(solution)/shard_map/ppermute | solution.py:60
  103.8 65.8 %collective-permute-start.14 = (bf16[512,1024]{1,0:T(8,128)(2,1)}, bf16[512,1024]{1,0:T(8,128)(2,1)}, u32[]{:S(2)}, u32[]{:S(2)}) collective-permute-start(bf16[512,1024]{1,0:T(8,128)(2,1)} %pad_maximum_fusion.2), channel_id=1, source_target_pairs={{0,8},{4,12},{8,0},{12,4},{16,24},{20,28},{24,16},{28,20},{1,9},{5... | collective-permute-start | bytes 3145736 | tf_op jit(solution)/shard_map/ppermute | solution.py:60
  106.6 63.0 %collective-permute-start.13 = (bf16[512,1024]{1,0:T(8,128)(2,1)}, bf16[512,1024]{1,0:T(8,128)(2,1)}, u32[]{:S(2)}, u32[]{:S(2)}) collective-permute-start(bf16[512,1024]{1,0:T(8,128)(2,1)} %pad_maximum_fusion.1), channel_id=1, source_target_pairs={{0,4},{4,0},{8,12},{12,8},{16,20},{20,16},{24,28},{28,24},{1,5},{5... | collective-permute-start | bytes 3145736 | tf_op jit(solution)/shard_map/ppermute | solution.py:60
  177.0 5.1 %collective-permute-start.15 = (bf16[2,640,1024]{2,1,0:T(8,128)(2,1)}, bf16[2,640,1024]{2,1,0:T(8,128)(2,1)S(1)}, u32[]{:S(2)}, u32[]{:S(2)}) collective-permute-start(bf16[2,640,1024]{2,1,0:T(8,128)(2,1)} %get-tuple-element.156), channel_id=1, source_target_pairs={{0,1},{1,0},{2,3},{3,2},{4,5},{5,4},{6,7},{7,6},{8,9},{9,8},{10,11... | collective-permute-start | bytes 7864328 | tf_op jit(solution)/shard_map/ppermute | solution.py:60
  185.0 2.3 copy-start.3
  188.6 40.5 %collective-permute-start.16 = (bf16[1,640,1024]{2,1,0:T(8,128)(2,1)}, bf16[1,640,1024]{2,1,0:T(8,128)(2,1)S(1)}, u32[]{:S(2)}, u32[]{:S(2)}) collective-permute-start(bf16[1,640,1024]{2,1,0:T(8,128)(2,1)} %slice.263), channel_id=1, source_target_pairs={{0,2},{1,3},{2,0},{3,1},{4,6},{5,7},{6,4},{7,5},{8,10},{9,11},{10,... | collective-permute-start | bytes 3932168 | tf_op jit(solution)/shard_map/ppermute | solution.py:60
  229.1 8.1 %copy-start.19 = (bf16[1,640,1024]{2,1,0:T(8,128)(2,1)}, bf16[1,640,1024]{2,1,0:T(8,128)(2,1)S(1)}, u32[]{:S(2)}) copy-start(bf16[1,640,1024]{2,1,0:T(8,128)(2,1)S(1)} %collective-permute-done.16) | copy-start | bytes 3932164
  229.1 5.2 %collective-permute-start.17 = (bf16[2,640,1024]{2,1,0:T(8,128)(2,1)}, bf16[2,640,1024]{2,1,0:T(8,128)(2,1)S(1)}, u32[]{:S(2)}, u32[]{:S(2)}) collective-permute-start(bf16[2,640,1024]{2,1,0:T(8,128)(2,1)} %get-tuple-element.174), channel_id=1, source_target_pairs={{0,1},{1,0},{2,3},{3,2},{4,5},{5,4},{6,7},{7,6},{8,9},{9,8},{10,11... | collective-permute-start | bytes 7864328 | tf_op jit(solution)/shard_map/ppermute | solution.py:60
  229.2 42.1 %collective-permute-start.19 = (bf16[4,128,1024]{2,1,0:T(8,128)(2,1)}, bf16[4,128,1024]{2,1,0:T(8,128)(2,1)}, u32[]{:S(2)}, u32[]{:S(2)}) collective-permute-start(bf16[4,128,1024]{2,1,0:T(8,128)(2,1)} %get-tuple-element.183), channel_id=1, source_target_pairs={{0,8},{4,12},{8,0},{12,4},{16,24},{20,28},{24,16},{28,20},{1,9},{5... | collective-permute-start | bytes 3145736 | tf_op jit(solution)/shard_map/ppermute | solution.py:60
  237.2 2.4 copy-start.4
  240.8 31.0 %collective-permute-start.18 = (bf16[1,640,1024]{2,1,0:T(8,128)(2,1)}, bf16[1,640,1024]{2,1,0:T(8,128)(2,1)S(1)}, u32[]{:S(2)}, u32[]{:S(2)}) collective-permute-start(bf16[1,640,1024]{2,1,0:T(8,128)(2,1)} %slice.262), channel_id=1, source_target_pairs={{0,2},{1,3},{2,0},{3,1},{4,6},{5,7},{6,4},{7,5},{8,10},{9,11},{10,... | collective-permute-start | bytes 3932168 | tf_op jit(solution)/shard_map/ppermute | solution.py:60
  271.9 5.8 %copy-start.21 = (bf16[1,640,1024]{2,1,0:T(8,128)(2,1)}, bf16[1,640,1024]{2,1,0:T(8,128)(2,1)S(1)}, u32[]{:S(2)}) copy-start(bf16[1,640,1024]{2,1,0:T(8,128)(2,1)S(1)} %collective-permute-done.18) | copy-start | bytes 3932164
  271.9 34.7 %collective-permute-start.21 = (bf16[4,128,1024]{2,1,0:T(8,128)(2,1)}, bf16[4,128,1024]{2,1,0:T(8,128)(2,1)}, u32[]{:S(2)}, u32[]{:S(2)}) collective-permute-start(bf16[4,128,1024]{2,1,0:T(8,128)(2,1)} %get-tuple-element.199), channel_id=1, source_target_pairs={{0,4},{4,0},{8,12},{12,8},{16,20},{20,16},{24,28},{28,24},{1,5},{5... | collective-permute-start | bytes 3145736 | tf_op jit(solution)/shard_map/ppermute | solution.py:60
  277.6 28.9 %collective-permute-start.20 = (bf16[2,128,1024]{2,1,0:T(8,128)(2,1)}, bf16[2,128,1024]{2,1,0:T(8,128)(2,1)S(1)}, u32[]{:S(2)}, u32[]{:S(2)}) collective-permute-start(bf16[2,128,1024]{2,1,0:T(8,128)(2,1)} %slice.266), channel_id=1, source_target_pairs={{0,16},{4,20},{8,24},{12,28},{16,0},{20,4},{24,8},{28,12},{1,17},{... | collective-permute-start | bytes 1572872 | tf_op jit(solution)/shard_map/ppermute | solution.py:60
  306.5 8.1 %copy-start.26 = (bf16[2,128,1024]{2,1,0:T(8,128)(2,1)}, bf16[2,128,1024]{2,1,0:T(8,128)(2,1)S(1)}, u32[]{:S(2)}) copy-start(bf16[2,128,1024]{2,1,0:T(8,128)(2,1)S(1)} %collective-permute-done.20) | copy-start | bytes 1572868
  306.6 5.2 %collective-permute-start.22 = (bf16[2,640,1024]{2,1,0:T(8,128)(2,1)}, bf16[2,640,1024]{2,1,0:T(8,128)(2,1)S(1)}, u32[]{:S(2)}, u32[]{:S(2)}) collective-permute-start(bf16[2,640,1024]{2,1,0:T(8,128)(2,1)} %get-tuple-element.201), channel_id=1, source_target_pairs={{0,1},{1,0},{2,3},{3,2},{4,5},{5,4},{6,7},{7,6},{8,9},{9,8},{10,11... | collective-permute-start | bytes 7864328 | tf_op jit(solution)/shard_map/ppermute | solution.py:60
  308.7 28.9 %collective-permute-start.29 = (bf16[4,128,1024]{2,1,0:T(8,128)(2,1)}, bf16[4,128,1024]{2,1,0:T(8,128)(2,1)}, u32[]{:S(2)}, u32[]{:S(2)}) collective-permute-start(bf16[4,128,1024]{2,1,0:T(8,128)(2,1)} %get-tuple-element.207), channel_id=1, source_target_pairs={{0,4},{4,0},{8,12},{12,8},{16,20},{20,16},{24,28},{28,24},{1,5},{5... | collective-permute-start | bytes 3145736 | tf_op jit(solution)/shard_map/ppermute | solution.py:60
  314.7 5.0 %copy-start.2 = (f32[2,640,1024]{2,1,0:T(8,128)}, f32[2,640,1024]{2,1,0:T(8,128)S(1)}, u32[]{:S(2)}) copy-start(f32[2,640,1024]{2,1,0:T(8,128)S(1)} %convert_add_fusion) | copy-start | bytes 15728644
  314.7 2.8 copy-start.24
  315.9 5.0 %copy-start.6 = (f32[4,128,1024]{2,1,0:T(8,128)S(1)}, f32[4,128,1024]{2,1,0:T(8,128)}, u32[]{:S(2)}) copy-start(f32[4,128,1024]{2,1,0:T(8,128)} %copy-done.5) | copy-start | bytes 6291460
  315.9 5.0 %copy-start.27 = (bf16[2,128,1024]{2,1,0:T(8,128)(2,1)S(1)}, bf16[2,128,1024]{2,1,0:T(8,128)(2,1)}, u32[]{:S(2)}) copy-start(bf16[2,128,1024]{2,1,0:T(8,128)(2,1)} %copy-done.26) | copy-start | bytes 1572868
  315.9 31.0 %collective-permute-start.23 = (bf16[1,640,1024]{2,1,0:T(8,128)(2,1)}, bf16[1,640,1024]{2,1,0:T(8,128)(2,1)S(1)}, u32[]{:S(2)}, u32[]{:S(2)}) collective-permute-start(bf16[1,640,1024]{2,1,0:T(8,128)(2,1)} %slice.261), channel_id=1, source_target_pairs={{0,2},{1,3},{2,0},{3,1},{4,6},{5,7},{6,4},{7,5},{8,10},{9,11},{10,... | collective-permute-start | bytes 3932168 | tf_op jit(solution)/shard_map/ppermute | solution.py:60
  320.7 14.3 %collective-permute-start.32 = (bf16[2,128,1024]{2,1,0:T(8,128)(2,1)}, bf16[2,128,1024]{2,1,0:T(8,128)(2,1)}, u32[]{:S(2)}, u32[]{:S(2)}) collective-permute-start(bf16[2,128,1024]{2,1,0:T(8,128)(2,1)} %slice.264), channel_id=1, source_target_pairs={{0,8},{4,12},{8,0},{12,4},{16,24},{20,28},{24,16},{28,20},{1,9},{5... | collective-permute-start | bytes 1572872 | tf_op jit(solution)/shard_map/ppermute | solution.py:60
  321.0 26.0 %slice-start = ((s8[5242880]{0:T(1024)(128)(4,1)}), s8[1048576]{0:T(1024)(128)(4,1)S(1)}, s32[]{:S(2)}) async-start(s8[5242880]{0:T(1024)(128)(4,1)} %bitcast.78), calls=%async_computation | async-start | bytes 2097152
  321.9 40.0 %collective-permute-start.34 = (bf16[1,128,1024]{2,1,0:T(8,128)(2,1)}, bf16[1,128,1024]{2,1,0:T(8,128)(2,1)}, u32[]{:S(2)}, u32[]{:S(2)}) collective-permute-start(bf16[1,128,1024]{2,1,0:T(8,128)(2,1)} %slice.267), channel_id=1, source_target_pairs={{0,4},{4,0},{8,12},{12,8},{16,20},{20,16},{24,28},{28,24},{1,5},{5... | collective-permute-start | bytes 786440 | tf_op jit(solution)/shard_map/ppermute | solution.py:60
  323.6 13.9 %copy-start.23 = (bf16[4,128,1024]{2,1,0:T(8,128)(2,1)S(1)}, bf16[4,128,1024]{2,1,0:T(8,128)(2,1)}, u32[]{:S(2)}) copy-start(bf16[4,128,1024]{2,1,0:T(8,128)(2,1)} %get-tuple-element.206) | copy-start | bytes 3145732
  324.5 22.5 %slice-start.1 = ((s8[5242880]{0:T(1024)(128)(4,1)}), s8[4194304]{0:T(1024)(128)(4,1)S(1)}, s32[]{:S(2)}) async-start(s8[5242880]{0:T(1024)(128)(4,1)} %bitcast.78), calls=%async_computation.1 | async-start | bytes 8388608
  337.3 29.1 %collective-permute-start.33 = (bf16[1,128,1024]{2,1,0:T(8,128)(2,1)}, bf16[1,128,1024]{2,1,0:T(8,128)(2,1)}, u32[]{:S(2)}, u32[]{:S(2)}) collective-permute-start(bf16[1,128,1024]{2,1,0:T(8,128)(2,1)} %slice.268), channel_id=1, source_target_pairs={{0,16},{4,20},{8,24},{12,28},{16,0},{20,4},{24,8},{28,12},{1,17},{... | collective-permute-start | bytes 786440 | tf_op jit(solution)/shard_map/ppermute | solution.py:60
  339.1 8.2 %copy-start.1 = (f32[640,1024]{1,0:T(8,128)S(1)}, f32[640,1024]{1,0:T(8,128)}, u32[]{:S(2)}) copy-start(f32[640,1024]{1,0:T(8,128)} %param.16) | copy-start | bytes 7864324
  339.2 19.9 %collective-permute-start.30 = (bf16[2,128,1024]{2,1,0:T(8,128)(2,1)S(1)}, bf16[2,128,1024]{2,1,0:T(8,128)(2,1)S(1)}, u32[]{:S(2)}, u32[]{:S(2)}) collective-permute-start(bf16[2,128,1024]{2,1,0:T(8,128)(2,1)S(1)} %slice.265), channel_id=1, source_target_pairs={{0,8},{4,12},{8,0},{12,4},{16,24},{20,28},{24,16},{28,20},{1,9},{5... | collective-permute-start | bytes 1572872 | tf_op jit(solution)/shard_map/ppermute | solution.py:60
  359.1 7.3 %copy-start.12 = (f32[2,128,1024]{2,1,0:T(8,128)S(1)}, f32[2,128,1024]{2,1,0:T(8,128)}, u32[]{:S(2)}) copy-start(f32[2,128,1024]{2,1,0:T(8,128)} %copy-done.11) | copy-start | bytes 3145732
  359.1 1.3 collective-permute-start.24
  360.0 15.3 %collective-permute-start.31 = (bf16[1,128,1024]{2,1,0:T(8,128)(2,1)}, bf16[1,128,1024]{2,1,0:T(8,128)(2,1)S(1)}, u32[]{:S(2)}, u32[]{:S(2)}) collective-permute-start(bf16[1,128,1024]{2,1,0:T(8,128)(2,1)} %slice.269), channel_id=1, source_target_pairs={{0,16},{4,20},{8,24},{12,28},{16,0},{20,4},{24,8},{28,12},{1,17},{... | collective-permute-start | bytes 786440 | tf_op jit(solution)/shard_map/ppermute | solution.py:60
  360.4 5.4 %collective-permute-start.25 = (f32[12416]{0:T(1024)S(1)}, f32[12416]{0:T(1024)S(1)}, u32[]{:S(2)}, u32[]{:S(2)}) collective-permute-start(f32[12416]{0:T(1024)S(1)} %add.220), channel_id=1, source_target_pairs={{0,2},{1,3},{2,0},{3,1},{4,6},{5,7},{6,4},{7,5},{8,10},{9,11},{10,... | collective-permute-start | bytes 149000 | tf_op jit(solution)/shard_map/ppermute | solution.py:60
  365.8 4.2 %collective-permute-start.26 = (f32[12416]{0:T(1024)S(1)}, f32[12416]{0:T(1024)S(1)}, u32[]{:S(2)}, u32[]{:S(2)}) collective-permute-start(f32[12416]{0:T(1024)S(1)} %add.221), channel_id=1, source_target_pairs={{0,4},{4,0},{8,12},{12,8},{16,20},{20,16},{24,28},{28,24},{1,5},{5... | collective-permute-start | bytes 149000 | tf_op jit(solution)/shard_map/ppermute | solution.py:60
  370.0 6.3 %collective-permute-start.27 = (f32[12416]{0:T(1024)S(1)}, f32[12416]{0:T(1024)S(1)}, u32[]{:S(2)}, u32[]{:S(2)}) collective-permute-start(f32[12416]{0:T(1024)S(1)} %add.222), channel_id=1, source_target_pairs={{0,8},{4,12},{8,0},{12,4},{16,24},{20,28},{24,16},{28,20},{1,9},{5... | collective-permute-start | bytes 149000 | tf_op jit(solution)/shard_map/ppermute | solution.py:60
  376.3 5.2 %collective-permute-start.28 = (f32[12416]{0:T(1024)S(1)}, f32[12416]{0:T(1024)S(1)}, u32[]{:S(2)}, u32[]{:S(2)}) collective-permute-start(f32[12416]{0:T(1024)S(1)} %add.223), channel_id=1, source_target_pairs={{0,16},{4,20},{8,24},{12,28},{16,0},{20,4},{24,8},{28,12},{1,17},{... | collective-permute-start | bytes 149000 | tf_op jit(solution)/shard_map/ppermute | solution.py:60
  (10 other events, 16.4 us)

commit v3 on v2

--- a/solution.py
+++ b/solution.py
@@ -118,13 +118,16 @@
         self.got = swap(self.send, self.axis, self.bits.pop(0))
 
     def add(self):
-        total = sum([x.astype(f32) for x in self.terms] + [self.got.astype(f32)])
-        if self.bits:
-            half = total.shape[0] // 2
-            self.send = total[:half].astype(bf16)
-            self.terms = [total[half:]]
+        terms = self.terms + [self.got]
+        if self.got.shape[0] > 1:
+            half = self.got.shape[0] // 2
+            self.send = sum(x[:half].astype(f32) for x in terms).astype(bf16)
+            self.terms = [x[half:] for x in terms]
         else:
-            self.total = total[0]
+            self.terms = [x[0] for x in terms]
+
+    def total(self):
+        return sum(x.astype(f32) for x in self.terms)
 
     def most(self):
         while len(self.bits) > 1:
@@ -135,7 +138,7 @@
         while self.bits:
             self.swap()
             self.add()
-        return self.total
+        return self.total()
 
 
 def tie_halves(values, *halvings):
@@ -143,13 +146,6 @@
     for x, got in zip(halvings, flat[len(values) :]):
         x.got = got
     return flat[: len(values)]
-
-
-def sum_everywhere(value, axes):
-    for axis in axes:
-        for bit in bits_of(lax.axis_size(axis)):
-            value = value + swap(value, axis, bit)
-    return value
 
 
 def resident(shape):
@@ -206,11 +202,11 @@
             where[...] = piece[...]
 
 
-def store_halves(send, keep, total, number, order, columns=slice(None)):
+def store_halves(send, keep, total, number, order, columns=slice(None), source=slice(None)):
     half, rows = send.shape[0], send.shape[1]
     for at, j in enumerate(order):
         where = send if at < half else keep
-        block = total[pl.ds(pl.multiple_of((number ^ j) * rows, rows), rows), :]
+        block = total[pl.ds(pl.multiple_of((number ^ j) * rows, rows), rows), source]
         where[at % half, :, columns] = block.astype(bf16)
 
 
@@ -273,7 +269,7 @@
 
         @pl.when(step == 0)
         def _():
-            pack.place(weight_refs, whole, ids[1], slice(0, 3 * width))
+            pack.place(weight_refs, whole, ids[1], slice(None))
 
         pick_piece(sent_refs, block, step)
         qkv = dot_nn(shift_gain(block[...], gain, shift), whole[...]) + bias[...]
@@ -314,7 +310,7 @@
 
         @pl.when(step == 0)
         def _():
-            pack.place(weight_refs, whole, ids[1], slice(3 * width, 4 * width))
+            pack.place(weight_refs, whole, ids[1], slice(None))
 
         pick_piece(grad_refs, block, step)
         out[...] = dot_nn(block[...], whole[...]).astype(bf16)
@@ -456,33 +452,95 @@
     )
 
 
-def project_context(ids, context, pack, groups, model):
-    pieces = len(pack.arrays)
-    rows, width = context.shape[0] // groups, context.shape[1]
-
-    def kernel(ids, ctx, *refs):
-        weight_refs, (send, keep, whole) = refs[:pieces], refs[pieces:]
+def attention_backward(
+    ids, info, tables, context, dq, dk, dv, sent, grad, gain, shift, qkv_pack, dense_pack, bits
+):
+    groups, held, pieces = sent.groups, len(sent.arrays), len(dense_pack.arrays)
+    rows, model = sent.rows, sent.model
+    width = dq.shape[1]
+    order = halving_order(bits)
+
+    def kernel(ids, info, ctx_ref, dq_ref, dk_ref, dv_ref, *refs):
+        sent_refs, refs = refs[:held], refs[held:]
+        grad_refs, refs = refs[:held], refs[held:]
+        weight_refs, refs = refs[:pieces], refs[pieces:]
+        gain, shift, cos, low, high, part_send, part_keep, grads, bias_ref, send, keep = refs[:11]
+        whole, block, grad_block, total, dense_total = refs[11:]
         step = pl.program_id(0)
 
         @pl.when(step == 0)
         def _():
-            pack.place(weight_refs, whole, ids[1], slice(3 * width, 4 * width))
-
-        store_half(send, keep, dot_nt(ctx[...], whole[...]).astype(bf16), step, groups)
-
-    operands = [context, *pack.arrays]
-    half = shaped(groups // 2, rows, model)
+            dense_pack.place(weight_refs, whole, ids[1], slice(None))
+            total[...] = jnp.zeros_like(total)
+            dense_total[...] = jnp.zeros_like(dense_total)
+            bias_ref[...] = jnp.zeros_like(bias_ref)
+
+        pick_piece(sent_refs, block, step)
+        pick_piece(grad_refs, grad_block, step)
+        store_half(
+            part_send, part_keep, dot_nt(ctx_ref[...], whole[...]).astype(bf16), step, groups
+        )
+        grads[:, :width] = dq_ref[...]
+        first = (ids[0] ^ ids[2 + step]) * (rows // SEG)
+        for at in range(rows // SEG):
+            number = first + at
+            table = pl.ds(pl.multiple_of(info[number // NB, number % NB, 4] * SEG, SEG), SEG)
+            own = slice(at * SEG, (at + 1) * SEG)
+            turned = turn(dk_ref[own, :], cos[table, :], low[table, :], high[table, :], -1.0)
+            grads[own, width : 2 * width] = turned.astype(bf16)
+        grads[:, 2 * width :] = dv_ref[...]
+        bias_ref[0:1, :] += jnp.sum(grads[...].astype(f32), axis=0, keepdims=True)
+        total[...] += dot_tn(shift_gain(block[...], gain, shift), grads[...])
+        dense_total[...] += dot_tn(grad_block[...], ctx_ref[...])
+
+        @pl.when(step == groups - 1)
+        def _():
+            store_halves(send, keep, total, ids[1], order, slice(0, 3 * width))
+            store_halves(send, keep, dense_total, ids[1], order, slice(3 * width, 4 * width))
+
+    operands = [
+        context,
+        dq,
+        dk,
+        dv,
+        *sent.arrays,
+        *grad.arrays,
+        *dense_pack.arrays,
+        gain,
+        shift,
+        *tables,
+    ]
+    count = model // qkv_pack.rows
+    outs = [
+        shaped(groups // 2, rows, model),
+        shaped(groups // 2, rows, model),
+        shaped(groups * rows, 3 * width),
+        shaped(8, 3 * width, dtype=f32),
+        shaped(count // 2, qkv_pack.rows, 4 * width),
+        shaped(count // 2, qkv_pack.rows, 4 * width),
+    ]
     return call(
         kernel,
-        "project_context",
+        "attention_backward",
         (groups,),
-        [ids],
+        [ids, info],
         operands,
-        [own_block(rows, width)] + [resident(x.shape) for x in operands[1:]],
-        [half] * 2,
-        half_blocks(groups, rows, model),
-        [pltpu.VMEM((model, width), bf16)],
-        2 * groups * rows * model * width,
+        [own_block(rows, width)] * 4
+        + sent.specs
+        + grad.specs
+        + [resident(x.shape) for x in operands[4 + 2 * held :]],
+        outs,
+        half_blocks(groups, rows, model)
+        + [step_block(rows, 3 * width)]
+        + [resident(x.shape) for x in outs[3:]],
+        [
+            pltpu.VMEM((model, width), bf16),
+            pltpu.VMEM((rows, model), bf16),
+            pltpu.VMEM((rows, model), bf16),
+            pltpu.VMEM((model, 3 * width), f32),
+            pltpu.VMEM((model, width), f32),
+        ],
+        2 * groups * rows * model * 5 * width,
     )
 
 
@@ -559,7 +617,7 @@
     )
 
 
-def mlp_backward(ids, sent, grad, slope, gain, shift, fc, out, fc_order):
+def hidden_backward(ids, sent, grad, slope, gain, shift, fc, out, orders):
     groups, held, pieces = sent.groups, len(sent.arrays), len(fc.arrays)
     rows, model = sent.rows, sent.model
     units = fc.arrays[0].shape[1]
@@ -567,47 +625,38 @@
     def kernel(ids, slope_ref, *refs):
         sent_refs, refs = refs[:held], refs[held:]
         grad_refs, refs = refs[:held], refs[held:]
-        fc_refs, refs = refs[:pieces], refs[pieces:]
         out_refs, refs = refs[:pieces], refs[pieces:]
-        gain, shift, back_ref, bias_ref, sums_ref, fc_send, fc_keep = refs[:7]
-        fc_whole, out_whole, block, grad_block, fc_total = refs[7:]
+        gain, shift, hidden_ref, bias_ref, *halves = refs[:8]
+        out_whole, block, grad_block, fc_total = refs[8:]
         step = pl.program_id(0)
 
         @pl.when(step == 0)
         def _():
-            fc.place(fc_refs, fc_whole, ids[1], slice(None))
             out.place(out_refs, out_whole, ids[1], slice(None))
             fc_total[...] = jnp.zeros_like(fc_total)
             bias_ref[...] = jnp.zeros_like(bias_ref)
-            sums_ref[...] = jnp.zeros_like(sums_ref)
 
         pick_piece(sent_refs, block, step)
         pick_piece(grad_refs, grad_block, step)
         hidden = (dot_nn(grad_block[...], out_whole[...]) * slope_ref[...]).astype(bf16)
+        hidden_ref[...] = hidden
         bias_ref[0:1, :] += jnp.sum(hidden.astype(f32), axis=0, keepdims=True)
-        back = dot_nt(hidden, fc_whole[...])
-        back_ref[...] = back
-        token = block[...]
-        sums_ref[0:1, :] += jnp.sum(back * token.astype(f32), axis=0, keepdims=True)
-        sums_ref[1:2, :] += jnp.sum(back, axis=0, keepdims=True)
-        fc_total[...] += dot_tn(shift_gain(token, gain, shift), hidden)
+        fc_total[...] += dot_tn(shift_gain(block[...], gain, shift), hidden)
 
         @pl.when(step == groups - 1)
         def _():
-            store_halves(fc_send, fc_keep, fc_total, ids[1], fc_order)
-
-    operands = [slope, *sent.arrays, *grad.arrays, *fc.arrays, *out.arrays, gain, shift]
+            for at, order in enumerate(orders):
+                source = slice(at * units // 2, (at + 1) * units // 2)
+                send, keep = halves[2 * at : 2 * at + 2]
+                store_halves(send, keep, fc_total, ids[1], order, source=source)
+
+    operands = [slope, *sent.arrays, *grad.arrays, *out.arrays, gain, shift]
     count = model // fc.rows
-    outs = [
-        shaped(groups * rows, model, dtype=f32),
-        shaped(8, units, dtype=f32),
-        shaped(8, model, dtype=f32),
-        shaped(count // 2, fc.rows, units),
-        shaped(count // 2, fc.rows, units),
-    ]
+    outs = [shaped(groups * rows, units), shaped(8, units, dtype=f32)]
+    outs += [shaped(count // 2, fc.rows, units // 2)] * 4
     return call(
         kernel,
-        "mlp_backward",
+        "hidden_backward",
         (groups,),
         [ids],
         operands,
@@ -616,114 +665,139 @@
         + grad.specs
         + [resident(x.shape) for x in operands[1 + 2 * held :]],
         outs,
-        [step_block(rows, model)] + [resident(x.shape) for x in outs[1:]],
+        [step_block(rows, units)] + [resident(x.shape) for x in outs[1:]],
         [
-            pltpu.VMEM((model, units), bf16),
             pltpu.VMEM((model, units), bf16),
             pltpu.VMEM((rows, model), bf16),
             pltpu.VMEM((rows, model), bf16),
             pltpu.VMEM((model, units), f32),
         ],
-        6 * groups * rows * model * units,
-    )
-
-
-def qkv_backward(
-    ids, info, tables, dq, dk, dv, context, sent, grad, back_mlp, gain, shift, gain_mlp, pack, dp_order
-):
-    groups, held, pieces = sent.groups, len(sent.arrays), len(pack.arrays)
+        4 * groups * rows * model * units,
+    )
+
+
+def norm_backward(ids, sent, grads, hidden, gain_attn, gain_mlp, qkv_pack, fc):
+    groups, held, pieces = sent.groups, len(sent.arrays), len(fc.arrays)
     rows, model = sent.rows, sent.model
-    width = dq.shape[1]
-
-    def kernel(ids, info, dq_ref, dk_ref, dv_ref, ctx_ref, mlp_ref, *refs):
+    units, columns = hidden.shape[1], grads.shape[1]
+
+    def kernel(ids, grads_ref, hidden_ref, *refs):
         sent_refs, refs = refs[:held], refs[held:]
-        grad_refs, refs = refs[:held], refs[held:]
-        weight_refs, refs = refs[:pieces], refs[pieces:]
-        gain, shift, gain_mlp, cos, low, high = refs[:6]
-        part_send, part_keep, bias_ref, sums_ref, send, keep = refs[6:12]
-        whole, block, grad_block, total, dense_total, grads = refs[12:]
+        qkv_refs, refs = refs[:pieces], refs[pieces:]
+        fc_refs, refs = refs[:pieces], refs[pieces:]
+        gain_attn, gain_mlp, send, keep, sums_ref, qkv_whole, fc_whole, block = refs
         step = pl.program_id(0)
 
         @pl.when(step == 0)
         def _():
-            pack.place(weight_refs, whole, ids[1], slice(0, 3 * width))
-            total[...] = jnp.zeros_like(total)
-            dense_total[...] = jnp.zeros_like(dense_total)
-            bias_ref[...] = jnp.zeros_like(bias_ref)
+            qkv_pack.place(qkv_refs, qkv_whole, ids[1], slice(None))
+            fc.place(fc_refs, fc_whole, ids[1], slice(None))
             sums_ref[...] = jnp.zeros_like(sums_ref)
 
         pick_piece(sent_refs, block, step)
-        pick_piece(grad_refs, grad_block, step)
-        grads[:, :width] = dq_ref[...]
-        first = (ids[0] ^ ids[2 + step]) * (rows // SEG)
-        for at in range(rows // SEG):
-            number = first + at
-            table = pl.ds(pl.multiple_of(info[number // NB, number % NB, 4] * SEG, SEG), SEG)
-            own = slice(at * SEG, (at + 1) * SEG)
-            turned = turn(dk_ref[own, :], cos[table, :], low[table, :], high[table, :], -1.0)
-            grads[own, width : 2 * width] = turned.astype(bf16)
-        grads[:, 2 * width :] = dv_ref[...]
-        bias_ref[0:1, :] += jnp.sum(grads[...].astype(f32), axis=0, keepdims=True)
-        back = dot_nt(grads[...], whole[...])
-        token = block[...]
-        sums_ref[0:1, :] += jnp.sum(back * token.astype(f32), axis=0, keepdims=True)
+        token = block[...].astype(f32)
+        back = dot_nt(grads_ref[...], qkv_whole[...])
+        sums_ref[0:1, :] += jnp.sum(back * token, axis=0, keepdims=True)
         sums_ref[1:2, :] += jnp.sum(back, axis=0, keepdims=True)
-        part = (back * gain[...] + mlp_ref[...] * gain_mlp[...]).astype(bf16)
-        store_half(part_send, part_keep, part, step, groups)
-        total[...] += dot_tn(shift_gain(token, gain, shift), grads[...])
-        dense_total[...] += dot_tn(grad_block[...], ctx_ref[...])
-
-        @pl.when(step == groups - 1)
-        def _():
-            store_halves(send, keep, total, ids[1], dp_order, slice(0, 3 * width))
-            store_halves(send, keep, dense_total, ids[1], dp_order, slice(3 * width, 4 * width))
-
-    operands = [
-        dq,
-        dk,
-        dv,
-        context,
-        back_mlp,
-        *sent.arrays,
-        *grad.arrays,
-        *pack.arrays,
-        gain,
-        shift,
-        gain_mlp,
-        *tables,
-    ]
-    count = model // pack.rows
+        part = back * gain_attn[...]
+        back = dot_nt(hidden_ref[...], fc_whole[...])
+        sums_ref[2:3, :] += jnp.sum(back * token, axis=0, keepdims=True)
+        sums_ref[3:4, :] += jnp.sum(back, axis=0, keepdims=True)
+        part = part + back * gain_mlp[...]
+        store_half(send, keep, part.astype(bf16), step, groups)
+
+    operands = [grads, hidden, *sent.arrays, *qkv_pack.arrays, *fc.arrays, gain_attn, gain_mlp]
     outs = [
         shaped(groups // 2, rows, model),
         shaped(groups // 2, rows, model),
-        shaped(8, 3 * width, dtype=f32),
         shaped(8, model, dtype=f32),
-        shaped(count // 2, pack.rows, 4 * width),
-        shaped(count // 2, pack.rows, 4 * width),
     ]
     return call(
         kernel,
-        "qkv_backward",
+        "norm_backward",
         (groups,),
-        [ids, info],
+        [ids],
         operands,
-        [own_block(rows, width)] * 4
-        + [step_block(rows, model)]
+        [step_block(rows, columns), step_block(rows, units)]
         + sent.specs
-        + grad.specs
-        + [resident(x.shape) for x in operands[5 + 2 * held :]],
+        + [resident(x.shape) for x in operands[2 + held :]],
         outs,
         half_blocks(groups, rows, model) + [resident(x.shape) for x in outs[2:]],
         [
-            pltpu.VMEM((model, 3 * width), bf16),
+            pltpu.VMEM((model, columns), bf16),
+            pltpu.VMEM((model, units), bf16),
             pltpu.VMEM((rows, model), bf16),
-            pltpu.VMEM((rows, model), bf16),
-            pltpu.VMEM((model, 3 * width), f32),
-            pltpu.VMEM((model, width), f32),
-            pltpu.VMEM((rows, 3 * width), bf16),
         ],
-        2 * groups * rows * model * 7 * width,
-    )
+        2 * groups * rows * model * (units + columns),
+    )
+
+
+def finish_output(stream, attn_terms, mlp_terms, dense_bias, out_bias):
+    rows, model = stream.shape
+    block = 128
+    first, second = len(attn_terms), len(mlp_terms)
+
+    def kernel(stream_ref, *refs):
+        attn_refs, refs = refs[:first], refs[first:]
+        mlp_refs, (dense_bias, out_bias, out_ref, sums_ref) = refs[:second], refs[second:]
+
+        @pl.when(pl.program_id(0) == 0)
+        def _():
+            sums_ref[...] = jnp.zeros_like(sums_ref)
+
+        attn = sum(x[...].astype(f32) for x in attn_refs) + dense_bias[...]
+        mlp = sum(x[...].astype(f32) for x in mlp_refs) + out_bias[...]
+        output = stream_ref[...] + attn + mlp
+        out_ref[...] = output
+        for at, value in enumerate((output, attn, mlp)):
+            sums_ref[at : at + 1, :] += jnp.sum(value * value, axis=0, keepdims=True)
+
+    operands = [stream, *attn_terms, *mlp_terms, dense_bias, out_bias]
+    outs = [shaped(rows, model, dtype=f32), shaped(8, model, dtype=f32)]
+    return call(
+        kernel,
+        "finish_output",
+        (rows // block,),
+        [],
+        operands,
+        [step_block(block, model)] * (1 + first + second)
+        + [resident(dense_bias.shape), resident(out_bias.shape)],
+        outs,
+        [step_block(block, model), resident(outs[1].shape)],
+        [],
+        rows * model * 16,
+    )
+
+
+def finish_grad(grad, normalized, inv_std, terms, chunks):
+    rows, model = grad.shape
+    count, block = len(chunks), chunks[0].shape[0]
+    held = len(terms)
+
+    def kernel(grad_ref, norm_ref, std_ref, *refs):
+        term_refs, chunk_refs, (out_ref, last) = refs[:held], refs[held:-2], refs[-2:]
+        pick_piece(chunk_refs, last, pl.program_id(0))
+        sent = sum(x[...].astype(f32) for x in term_refs) + last[...].astype(f32)
+        norm = norm_ref[...]
+        mean = jnp.sum(sent, axis=1, keepdims=True) / model
+        cross = jnp.sum(sent * norm, axis=1, keepdims=True) / model
+        out_ref[...] = grad_ref[...].astype(f32) + std_ref[...] * (sent - mean - norm * cross)
+
+    operands = [grad, normalized, inv_std, *terms, *chunks]
+    return call(
+        kernel,
+        "finish_grad",
+        (count,),
+        [],
+        operands,
+        [step_block(block, model), step_block(block, model), step_block(block, 1)]
+        + [step_block(block, model)] * held
+        + [resident(x.shape) for x in chunks],
+        [shaped(rows, model, dtype=f32)],
+        [step_block(block, model)],
+        [pltpu.VMEM((block, model), bf16)],
+        rows * model * 12,
+    )[0]
 
 
 def tree_table(segment_ids, parent_ids):
@@ -806,13 +880,8 @@
     columns_first = data_bits[:1] + data_bits[:0:-1]
     out_bits, fc_bits = columns_first[::-1], rows_first[::-1]
 
-    attn_pack = Pack(
-        jnp.concatenate(
-            [by_kind(qkv_weight.astype(bf16), heads), dense_weight.astype(bf16).T], axis=1
-        ),
-        "dp",
-        rows_first,
-    )
+    qkv_pack = Pack(by_kind(qkv_weight.astype(bf16), heads), "dp", rows_first)
+    dense_pack = Pack(dense_weight.astype(bf16).T, "dp", columns_first)
     fc_pack = Pack(fc_weight.astype(bf16), "dp", rows_first)
     out_pack = Pack(out_weight.astype(bf16).T, "dp", columns_first)
 
@@ -823,22 +892,23 @@
     normalized = centred * inv_std
     sent = gather_far(normalized.astype(bf16), "tensor", tensor_bits)
 
-    attn_pack.double()
+    qkv_pack.double()
+    dense_pack.double()
     out_pack.double()
-    tie_packs(attn_pack, out_pack)
-    rounds = len(data_bits)
-    for number in range(1, rounds - 1):
-        attn_pack.double()
-        fc_pack.double()
-    sent = tie_packs(attn_pack, fc_pack, out_pack, beside=sent)
+    tie_packs(qkv_pack, dense_pack, fc_pack, out_pack)
+    while len(qkv_pack.bits) > 1:
+        qkv_pack.double()
+        dense_pack.double()
+    fc_pack.double()
+    sent = tie_packs(qkv_pack, dense_pack, fc_pack, out_pack, beside=sent)
     out_grad, sent[0] = tie(out_grad, sent[0])
     grad = gather_far(out_grad, "tensor", tensor_bits)
     sent = gather_near(sent, "tensor")
-    attn_pack.double()
-    fc_pack.double()
+    qkv_pack.double()
+    dense_pack.double()
     while len(out_pack.bits) > 1:
         out_pack.double()
-    sent = Tokens(tie_packs(attn_pack, fc_pack, out_pack, beside=sent), order)
+    sent = Tokens(tie_packs(qkv_pack, dense_pack, out_pack, beside=sent), order)
 
     info = tree_table(segment_ids, parent_ids)
     tables = angle_tables()
@@ -849,22 +919,40 @@
     )[None, :]
     fc_bias_own = lax.dynamic_slice_in_dim(fc_bias, tensor_rank * units, units)[None, :]
 
-    queries, keys, values = project_qkv(
-        ids, info, sent, gain_attn, shift_attn, attn_pack, qkv_bias_own, tables, width
-    )
-    queries, keys, values, *grad = tie(queries, keys, values, *grad)
+    while len(fc_pack.bits) > 1:
+        fc_pack.double()
+    done = project_qkv(
+        ids, info, sent, gain_attn, shift_attn, qkv_pack, qkv_bias_own, tables, width
+    )
+    queries, keys, values, *grad = tie_packs(fc_pack, beside=[*done, *grad])
     grad = Tokens(gather_near(grad, "tensor"), order)
-    grad_context = project_grad(ids, grad, attn_pack, width)
+    grad_context = project_grad(ids, grad, dense_pack, width)
     fc_pack.double()
     out_pack.double()
     done = attention(info, tables, queries, keys, values, grad_context)
     context, dq, dk, dv = tie_packs(fc_pack, out_pack, beside=done)
-    attn_parts = Halving(
-        *project_context(ids, context, attn_pack, groups, model), "tensor", tensor_bits
-    )
+    attn_send, attn_keep, grads, qkv_bias_sums, qkv_send, qkv_keep = attention_backward(
+        ids,
+        info,
+        tables,
+        context,
+        dq,
+        dk,
+        dv,
+        sent,
+        grad,
+        gain_attn,
+        shift_attn,
+        qkv_pack,
+        dense_pack,
+        fc_bits,
+    )
+    attn_parts = Halving(attn_send, attn_keep, "tensor", tensor_bits)
+    qkv_parts = Halving(qkv_send, qkv_keep, "dp", fc_bits)
     attn_parts.most()
     sent.arrays[0], attn_parts.send = tie(sent.arrays[0], attn_parts.send)
     attn_parts.swap()
+    qkv_parts.swap()
     done = mlp_forward(
         ids,
         sent,
@@ -874,96 +962,110 @@
         fc_pack,
         fc_bias_own,
         out_pack,
-        halving_order(out_bits),
-    )
-    active, slope, mlp_send, mlp_keep, out_send, out_keep = tie_halves(done, attn_parts)
+        halving_order(fc_bits),
+    )
+    done = tie_halves(done, attn_parts, qkv_parts)
+    active, slope, mlp_send, mlp_keep, out_send, out_keep = done
     attn_parts.add()
+    qkv_parts.add()
     mlp_parts = Halving(mlp_send, mlp_keep, "tensor", tensor_bits)
     mlp_parts.most()
-    slope, mlp_parts.send = tie(slope, mlp_parts.send)
-    out_parts = Halving(out_send, out_keep, "dp", out_bits)
+    slope, mlp_parts.send, qkv_parts.send = tie(slope, mlp_parts.send, qkv_parts.send)
+    out_parts = Halving(out_send, out_keep, "dp", fc_bits)
     mlp_parts.swap()
     out_parts.swap()
-    done = mlp_backward(
-        ids, sent, grad, slope, gain_mlp, shift_mlp, fc_pack, out_pack, halving_order(fc_bits)
-    )
-    back_mlp, fc_bias_sums, mlp_sums, fc_send, fc_keep = tie_halves(done, mlp_parts, out_parts)
-    mlp_parts.add()
-    out_parts.add()
-    back_mlp, out_parts.send = tie(back_mlp, out_parts.send)
-    fc_parts = Halving(fc_send, fc_keep, "dp", fc_bits)
-    out_parts.swap()
-    fc_parts.swap()
-    done = qkv_backward(
+    qkv_parts.swap()
+    done = hidden_backward(
         ids,
-        info,
-        tables,
-        dq,
-        dk,
-        dv,
-        context,
         sent,
         grad,
-        back_mlp,
-        gain_attn,
-        shift_attn,
+        slope,
         gain_mlp,
-        attn_pack,
-        halving_order(fc_bits),
-    )
-    done = tie_halves(done, out_parts, fc_parts)
-    back_send, back_keep, qkv_bias_sums, attn_sums, qkv_send, qkv_keep = done
-    out_parts.add()
-    fc_parts.add()
-    attn_sum, mlp_sum = attn_parts.total, mlp_parts.total
-    qkv_parts = Halving(qkv_send, qkv_keep, "dp", fc_bits)
-    grad_sent = Halving(back_send, back_keep, "tensor", tensor_bits).finish()
-
-    fc_weight_grad = fc_parts.finish()
+        shift_mlp,
+        fc_pack,
+        out_pack,
+        [halving_order(fc_bits), halving_order(out_bits)],
+    )
+    hidden, fc_bias_sums, *halves = tie_halves(done, qkv_parts)
+    qkv_parts.add()
+    hidden, qkv_parts.send = tie(hidden, qkv_parts.send)
+    low_parts = Halving(*halves[:2], "dp", fc_bits)
+    high_parts = Halving(*halves[2:], "dp", out_bits)
+    low_parts.swap()
+    high_parts.swap()
+    qkv_parts.swap()
+    done = norm_backward(ids, sent, grads, hidden, gain_attn, gain_mlp, qkv_pack, fc_pack)
+    back_send, back_keep, norm_sums = tie_halves(
+        done, mlp_parts, out_parts, qkv_parts, low_parts, high_parts
+    )
+    mlp_parts.add()
+    for parts in (out_parts, qkv_parts, low_parts, high_parts):
+        parts.add()
+
+    back_parts = Halving(back_send, back_keep, "tensor", tensor_bits)
+    while len(back_parts.bits) > 2:
+        back_parts.swap()
+        back_parts.add()
+    back_parts.swap()
+    output, squares = tie_halves(
+        finish_output(
+            stream_in, attn_parts.terms, mlp_parts.terms, dense_bias[None, :], out_bias[None, :]
+        ),
+        back_parts,
+    )
+    back_parts.add()
+    fc_bias_spread = lax.dynamic_update_slice(
+        jnp.zeros(fc_bias.shape, f32), fc_bias_sums[0], (tensor_rank * units,)
+    )
+    qkv_bias_spread = lax.dynamic_update_slice(
+        jnp.zeros(qkv_bias.shape, f32), by_head(qkv_bias_sums[0], heads), (tensor_rank * qkv_width,)
+    )
+    sums = jnp.concatenate(
+        [
+            norm_sums[:4].reshape(-1),
+            squares[:3].reshape(-1),
+            jnp.sum(out_grad.astype(f32), axis=0),
+            fc_bias_spread,
+            qkv_bias_spread,
+        ]
+    )
+    steps = [(axis, bit) for axis in ("tensor", "dp") for bit in bits_of(lax.axis_size(axis))]
+    chunks = jnp.split(back_parts.send, 4, axis=1)
+    sums = sums + swap(sums, *steps[0])
+    for parts in (out_parts, low_parts, high_parts):
+        parts.swap()
+    got = []
+    for at, step in enumerate(steps[1:]):
+        other = swap(sums, *step)
+        if at == 1:
+            (other,) = tie_halves([other], out_parts, low_parts, high_parts)
+        if 1 <= at <= len(chunks):
+            other, got[-1] = tie(other, got[-1])
+        if at < len(chunks):
+            sums, chunk = tie(sums, chunks[at])
+            got.append(swap(chunk, "tensor", back_parts.bits[-1]))
+        sums = sums + other
+    for parts in (out_parts, low_parts, high_parts):
+        parts.add()
+    stream_grad = finish_grad(
+        out_grad, normalized, inv_std, [x[0] for x in back_parts.terms], [x[0] for x in got]
+    )
+
     out_weight_grad = out_parts.finish().T
     attn_total = qkv_parts.finish()
     dense_weight_grad = attn_total[:, 3 * width :].T
     qkv_weight_grad = by_head(attn_total[:, : 3 * width], heads)
-
-    attn_out = attn_sum + dense_bias
-    mlp_out = mlp_sum + out_bias
-    output = stream_in + attn_out + mlp_out
-
-    mean_grad = jnp.mean(grad_sent, axis=-1, keepdims=True)
-    mean_cross = jnp.mean(grad_sent * normalized, axis=-1, keepdims=True)
-    stream_grad = out_grad.astype(f32) + inv_std * (
-        grad_sent - mean_grad - normalized * mean_cross
-    )
-
-    residual_part = jnp.sum(out_grad.astype(f32), axis=0)
-    squares = jnp.stack(
-        [jnp.sum(output * output), jnp.sum(attn_out * attn_out), jnp.sum(mlp_out * mlp_out)]
-    )
+    fc_weight_grad = jnp.concatenate([low_parts.finish(), high_parts.finish()], axis=1)
+
     count_all = float(rows_local * lax.axis_size("dp") * groups * model)
-    fc_bias_spread = lax.dynamic_update_slice(
-        jnp.zeros(fc_bias.shape, f32), fc_bias_sums[0], (tensor_rank * units,)
-    )
-    qkv_bias_spread = lax.dynamic_update_slice(
-        jnp.zeros(qkv_bias.shape, f32), by_head(qkv_bias_sums[0], heads), (tensor_rank * qkv_width,)
-    )
-    sums = [
-        residual_part,
-        mlp_sums[0],
-        mlp_sums[1],
-        attn_sums[0],
-        attn_sums[1],
-        fc_bias_spread,
-        qkv_bias_spread,
-        jnp.pad(squares, (0, 125)),
-    ]
-    packed = sum_everywhere(jnp.concatenate(sums), ("tensor", "dp"))
-    split = []
-    for part in sums:
-        split.append(packed[: part.shape[0]])
-        packed = packed[part.shape[0] :]
-    residual_grad, gain_mlp_grad, shift_mlp_grad, gain_attn_grad, shift_attn_grad = split[:5]
-    fc_bias_grad, qkv_bias_grad, squares = split[5:]
-    root_squares = jnp.sqrt(squares[:3] / count_all)
+    gain_attn_grad, shift_attn_grad, gain_mlp_grad, shift_mlp_grad = sums[: 4 * model].reshape(
+        4, model
+    )
+    squares = jnp.sum(sums[4 * model : 7 * model].reshape(3, model), axis=1)
+    root_squares = jnp.sqrt(squares / count_all)
+    residual_grad = sums[7 * model : 8 * model]
+    fc_bias_grad = sums[8 * model : 8 * model + fc_bias.shape[0]]
+    qkv_bias_grad = sums[8 * model + fc_bias.shape[0] :]
     return (
         output,
         stream_grad,

time: 391 us -> 383 us (0.980)
  waiting for transfers between devices: 96.7 us -> 63.4 us
  Pallas kernels: 176 us -> 190 us
  starting transfers between devices: 29 us -> 42.4 us
    ppermute x35 -> x44, waiting for transfers between devices: 96.7 us -> 63.4 us  [swap(): return lax.ppermute(block, axis, [(i, i ^ bit) for i in range(size)])]
    convert_element_type x0 -> x11, other arithmetic: none -> 18.9 us  [add(): self.send = sum((x[:half].astype(f32) for x in terms)).astype(bf16)]
    squeeze x0 -> x6, local copies, waits for them, and re-layouts: none -> 14.7 us  [the longest x4 9.59 us: add(): self.terms = [x[0] for x in terms]]
    pallas_call x7 -> x9, Pallas kernels: 176 us -> 190 us  [call(): pl.pallas_call(kernel, grid_spec=pltpu.PrefetchScalarGridSpec(num_scalar_...]
    ppermute x35 -> x44, starting transfers between devices: 29 us -> 42.4 us  [swap(): return lax.ppermute(block, axis, [(i, i ^ bit) for i in range(size)])]
    add x14 -> x8, other arithmetic: 16.3 us -> 3.4 us  [the longest x3 3.35 us: total(): return sum((x.astype(f32) for x in self.terms))]
    slice x14 -> x5, local copies, waits for them, and re-layouts: 11.5 us -> 1.88 us  [the longest x2 0.67 us: local(): squares = jnp.sum(sums[4 * model:7 * model].reshape(3, model), axis=1)]
    reduce_sum x3 -> x2, other arithmetic: 8.66 us -> 0.36 us  [the longest x1 0.23 us: local(): jnp.sum(out_grad.astype(f32), axis=0)]
  transfers between devices with their start and end apart: 35 -> 44, of which waited for: 16 -> 12; matrix products, arithmetic and copies ran while one was open for 16% -> 18% of each run, Pallas kernels for 44% -> 43%
where the time goes in v3:
time: 383 us; the launch traced here: 375 us
  Pallas kernels  190 us (50%)
  waiting for transfers between devices  63.4 us (17%)
  other arithmetic  44.2 us (12%)
  starting transfers between devices  42.4 us (11%)
  local copies, waits for them, and re-layouts  33.6 us (9%)
    pallas_call x9, Pallas kernels, call(): pl.pallas_call(kernel, grid_spec=pltpu.PrefetchScalarGridSpec(num_scalar_...  190 us
    ppermute x44, waiting for transfers between devices, swap(): return lax.ppermute(block, axis, [(i, i ^ bit) for i in range(size)])  63.4 us
    ppermute x44, starting transfers between devices, swap(): return lax.ppermute(block, axis, [(i, i ^ bit) for i in range(size)])  42.4 us
    convert_element_type x11, other arithmetic, add(): self.send = sum((x[:half].astype(f32) for x in terms)).astype(bf16)  18.9 us
    squeeze x4, local copies, waits for them, and re-layouts, add(): self.terms = [x[0] for x in terms]  9.59 us
  transfers between devices with their start and end apart: 44, of which 12 were waited for; matrix products, arithmetic and copies ran while one was open for 18% of the time, Pallas kernels for 43%

profile of v3, /device:TPU:0, one launch (start us, length us, event | category | flops | bytes accessed | tf_op | source)
XLA Modules:
  0.0 375.4 jit_solution(6032001808949778537)
XLA Ops:
  0.7 2.1 reduce_sum.49
  3.6 2.3 fusion.28
  5.9 3.0 collective-permute-start
  9.3 2.7 collective-permute-start.1
  11.9 1.0 copy.129
  12.9 1.6 collective-permute-start.2
  16.1 1.9 collective-permute-done.2.refs_5_.refs_9_
  18.0 2.8 collective-permute-done.1.refs_5_
  20.8 1.8 collective-permute-done.3.refs_13_.refs_9_
  22.9 1.6 collective-permute-start.4
  25.8 2.4 collective-permute-start.5
  28.6 1.7 fusion.27
  30.3 13.8 %collective-permute-done.5.refs_6_.refs_10_ = bf16[256,256]{1,0:T(8,128)(2,1)S(1)} collective-permute-done((bf16[256,256]{1,0:T(8,128)(2,1)S(1)}, bf16[256,256]{1,0:T(8,128)(2,1)S(1)}, u32[]{:S(2)}, u32[]{:S(2)}) %collective-permute-start.5) | collective-permute-done | bytes 131104 | tf_op jit(solution)/shard_map/ppermute | solution.py:60
  47.1 1.9 pad_maximum_fusion.2
  49.8 3.0 collective-permute-start.11
  52.8 3.4 collective-permute-done.10.refs_7_.refs_11_
  56.7 3.9 %fusion.8 = (f32[1280,128]{1,0:T(8,128)}, f32[1280,128]{1,0:T(8,128)}, f32[1280,128]{1,0:T(8,128)}) fusion(s32[128]{0:T(128)S(1)} %copy-done.45, s32[128]{0:T(128)S(1)} %copy-done.46, pred[128]{0:T(512)(128)(4,1)S(1)} %compare_and_fusion, f32[1280]{0:T(1024)S(1)} %copy-done.38), kind=kLoop, calls=%fused_computation.34 | loop fusion | flops 3932160 | bytes 1972352 | tf_op jit(solution)/shard_map/jit(_where)/select_n | solution.py:831
  61.4 14.1 %collective-permute-done.11.refs_14_.refs_10_ = bf16[256,1024]{1,0:T(8,128)(2,1)S(1)} collective-permute-done((bf16[256,1024]{1,0:T(8,128)(2,1)S(1)}, bf16[256,1024]{1,0:T(8,128)(2,1)S(1)}, u32[]{:S(2)}, u32[]{:S(2)}) %collective-permute-start.11) | collective-permute-done | bytes 524320 | tf_op jit(solution)/shard_map/ppermute | solution.py:60
  80.0 11.9 %project_qkv.1 = (bf16[2560,256]{1,0:T(8,128)(2,1)}, bf16[2560,256]{1,0:T(8,128)(2,1)}, bf16[2560,256]{1,0:T(8,128)(2,1)}) custom-call(s32[6]{0:T(128)} %stack.19.ids, s32[1,20,5]{2,1,0:T(8,128)} %stack.20.info, bf16[640,1024]{1,0:T(8,128)(2,1)} %collective-permute-done.8.refs_0_, bf16[640,1024]{1,0:T(8,128)(2,1)} %collective-permute-done.7.refs_1_, ...), custom_call_target="tpu_custom_call" | custom-call | flops 4026531840 | bytes 12725248 | tf_op jit(solution)/shard_map/project_qkv/pallas_call | solution.py:215
  92.5 2.2 pad_maximum_fusion
  94.6 1.4 collective-permute-start.16
  96.0 1.0 pad_maximum_fusion.1
  97.1 2.0 collective-permute-start.17
  99.1 6.6 %project_grad.1.do_ref = bf16[2560,256]{1,0:T(8,128)(2,1)} custom-call(s32[6]{0:T(128)} %stack.19.ids, bf16[640,1024]{1,0:T(8,128)(2,1)} %collective-permute-done.14.refs_0_.refs_4_, bf16[640,1024]{1,0:T(8,128)(2,1)} %collective-permute-done.15.refs_1_.refs_5_, bf16[640,1024]{1,0:T(8,128)(2,1)} %collective-permute-done.12.refs_2_.refs_6_, ...), custom_call_target="tpu_custom_call" | custom-call | flops 1342177280 | bytes 7077888 | tf_op jit(solution)/shard_map/project_grad/pallas_call | solution.py:215
  105.7 55.3 %attention.1 = (bf16[2560,256]{1,0:T(8,128)(2,1)}, bf16[2560,256]{1,0:T(8,128)(2,1)}, bf16[2560,256]{1,0:T(8,128)(2,1)}, bf16[2560,256]{1,0:T(8,128)(2,1)}) custom-call(s32[1,20,5]{2,1,0:T(8,128)} %stack.20.info, bf16[2560,256]{1,0:T(8,128)(2,1)} %get-tuple-element.182.q_ref, bf16[2560,256]{1,0:T(8,128)(2,1)} %project_grad.1.do_ref, ...), custom_call_target="tpu_custom_call" | custom-call | flops 31406948352 | bytes 12451840 | tf_op jit(solution)/shard_map/attention/pallas_call | solution.py:215
  161.1 21.6 %attention_backward.1 = (bf16[2,640,1024]{2,1,0:T(8,128)(2,1)}, bf16[2,640,1024]{2,1,0:T(8,128)(2,1)}, bf16[2560,768]{1,0:T(8,128)(2,1)}, f32[8,768]{1,0:T(8,128...) custom-call(s32[6]{0:T(128)} %stack.19.ids, s32[1,20,5]{2,1,0:T(8,128)} %stack.20.info, ...), custom_call_target="tpu_custom_call" | custom-call | flops 6710886400 | bytes 29523968 | tf_op jit(solution)/shard_map/attention_backward/pallas_call | solution.py:215
  182.7 1.3 dynamic_slice.7
  184.7 3.2 collective-permute-done.18
  187.8 3.9 %add_convert_fusion.2 = bf16[1,640,1024]{2,1,0:T(8,128)(2,1)} fusion(bf16[2,640,1024]{2,1,0:T(8,128)(2,1)S(1)} %collective-permute-done.18, bf16[2,640,1024]{2,1,0:T(8,128)(2,1)} %get-tuple-element.205), kind=kLoop, calls=%fused_computation.3 | loop fusion | flops 2621440 | bytes 3932160 | tf_op jit(solution)/shard_map/convert_element_type | solution.py:124
  192.2 39.4 %mlp_forward.1 = (bf16[2560,1024]{1,0:T(8,128)(2,1)}, f32[2560,1024]{1,0:T(8,128)}, bf16[2,640,1024]{2,1,0:T(8,128)(2,1)}, bf16[2,640,1024]{2,1,0:T(8,128)(2,1)}...) custom-call(s32[6]{0:T(128)} %stack.19.ids, bf16[640,1024]{1,0:T(8,128)(2,1)} %collective-permute-done.8.refs_0_, ...), custom_call_target="tpu_custom_call" | custom-call | flops 16106127360 | bytes 37761024 | tf_op jit(solution)/shard_map/mlp_forward/pallas_call | solution.py:215
  234.0 2.6 slice_bitcast_fusion.5.refs_0_
  237.3 1.2 add_convert_fusion.4
  238.6 2.9 add_convert_fusion.1
  242.1 1.5 collective-permute-start.23
  243.7 22.5 %hidden_backward.1 = (bf16[2560,1024]{1,0:T(8,128)(2,1)}, f32[8,1024]{1,0:T(8,128)}, bf16[4,128,512]{2,1,0:T(8,128)(2,1)}, bf16[4,128,512]{2,1,0:T(8,128)(2,1)},...) custom-call(s32[6]{0:T(128)} %stack.19.ids, f32[2560,1024]{1,0:T(8,128)} %get-tuple-element.230.slope_ref, ...), custom_call_target="tpu_custom_call" | custom-call | flops 10737418240 | bytes 30449664 | tf_op jit(solution)/shard_map/hidden_backward/pallas_call | solution.py:215
  266.1 1.9 add_convert_fusion.8
  268.1 2.3 collective-permute-start.25
  271.7 19.2 %norm_backward.1 = (bf16[2,640,1024]{2,1,0:T(8,128)(2,1)}, bf16[2,640,1024]{2,1,0:T(8,128)(2,1)}, f32[8,1024]{1,0:T(8,128)}) custom-call(s32[6]{0:T(128)} %stack.19.ids, bf16[2560,768]{1,0:T(8,128)(2,1)} %get-tuple-element.226.grads_ref, bf16[2560,1024]{1,0:T(8,128)(2,1)} %get-tuple-element.240.hidden_ref, bf16[640,1024]{1,0:T(8,128)(2,1)} %collective-permute-done.8.refs_0_, ...), custom_call_target="tpu_custom_call" | custom-call | flops 9395240960 | bytes 23371776 | tf_op jit(solution)/shard_map/norm_backward/pallas_call | solution.py:215
  291.0 3.3 slice_bitcast_fusion.1.refs_1_
  294.3 1.1 slice_bitcast_fusion.4.refs_3_
  295.4 2.6 slice_bitcast_fusion.refs_4_
  299.0 1.2 add_convert_fusion.3
  300.2 1.3 collective-permute-start.32
  301.5 1.7 add_convert_fusion.7
  304.0 1.0 add_convert_fusion.6
  305.0 2.1 collective-permute-start.34
  307.2 1.3 add_bitcast_fusion.1
  310.5 7.5 %finish_output.1 = (f32[640,1024]{1,0:T(8,128)}, f32[8,1024]{1,0:T(8,128)}) custom-call(f32[640,1024]{1,0:T(8,128)} %stream_ref.1, bf16[640,1024]{1,0:T(8,128)(2,1)} %slice_bitcast_fusion.5.refs_0_, bf16[640,1024]{1,0:T(8,128)(2,1)} %slice_bitcast_fusion.1.refs_1_, bf16[640,1024]{1,0:T(8,128)(2,1)} %bitcast.19.refs_2_, ...), custom_call_target="tpu_custom_call" | custom-call | flops 10485760 | bytes 13148160 | tf_op jit(solution)/shard_map/finish_output/pallas_call | solution.py:215
  318.0 2.6 slice_bitcast_fusion.3.refs_0_
  320.8 1.8 add_convert_fusion
  323.4 3.7 collective-permute-done.30
  327.8 2.5 slice_bitcast_fusion.2.refs_1_
  330.9 1.5 collective-permute-start.37
  332.4 1.0 add_convert_fusion.9
  333.4 1.4 collective-permute-start.42
  336.7 1.2 add_convert_fusion.5
  337.9 2.2 collective-permute-start.43
  340.0 1.0 add_bitcast_fusion.2
  341.1 8.7 %collective-permute-done.41 = bf16[1,128,512]{2,1,0:T(8,128)(2,1)S(1)} collective-permute-done((bf16[1,128,512]{2,1,0:T(8,128)(2,1)S(1)}, bf16[1,128,512]{2,1,0:T(8,128)(2,1)S(1)}, u32[]{:S(2)}, u32[]{:S(2)}) %collective-permute-start.41) | collective-permute-done | bytes 131104 | tf_op jit(solution)/shard_map/ppermute | solution.py:60
  352.3 3.4 collective-permute-done.36
  355.8 1.2 add_bitcast_fusion
  358.5 2.7 collective-permute-done.38
  363.8 3.8 %collective-permute-done.40 = bf16[1,160,1024]{2,1,0:T(8,128)(2,1)S(1)} collective-permute-done((bf16[1,160,1024]{2,1,0:T(8,128)(2,1)S(1)}, bf16[1,160,1024]{2,1,0:T(8,128)(2,1)S(1)}, u32[]{:S(2)}, u32[]{:S(2)}) %collective-permute-start.40) | collective-permute-done | bytes 327712 | tf_op jit(solution)/shard_map/ppermute | solution.py:60
  368.3 6.3 %finish_grad.1 = f32[640,1024]{1,0:T(8,128)} custom-call(bf16[640,1024]{1,0:T(8,128)(2,1)} %grad_ref, f32[640,1024]{1,0:T(8,128)} %get-tuple-element.376.norm_ref, f32[640,1]{1,0:T(8,128)} %rsqrt.7.std_ref, bf16[640,1024]{1,0:T(8,128)(2,1)} %slice_bitcast_fusion.3.refs_0_, bf16[640,1024]{1,0:T(8,128)(2,1)} %slice_bitcast_fusion.2.refs_1_, ...), custom_call_target="tpu_custom_call" | custom-call | flops 7864320 | bytes 10488320 | tf_op jit(solution)/shard_map/finish_grad/pallas_call | solution.py:215
  (227 shorter events, 36.8 us)
Async XLA Ops:
  3.6 10.9 %copy-start.20 = (f32[1024,128]{1,0:T(8,128)S(1)}, f32[1024,128]{1,0:T(8,128)}, u32[]{:S(2)}) copy-start(f32[1024,128]{1,0:T(8,128)} %param.29) | copy-start | bytes 1572868
  5.9 39.0 %collective-permute-start = (bf16[640,1024]{1,0:T(8,128)(2,1)}, bf16[640,1024]{1,0:T(8,128)(2,1)}, u32[]{:S(2)}, u32[]{:S(2)}) collective-permute-start(bf16[640,1024]{1,0:T(8,128)(2,1)} %get-tuple-element.171.refs_3_), channel_id=1, source_target_pairs={{0,2},{1,3},{2,0},{3,1},{4,6},{5,7},{6,4},{7,5},{8,10},{9,11},{10,... | collective-permute-start | bytes 3932168 | tf_op jit(solution)/shard_map/ppermute | solution.py:60
  9.3 11.5 %collective-permute-start.1 = (bf16[128,768]{1,0:T(8,128)(2,1)S(1)}, bf16[128,768]{1,0:T(8,128)(2,1)S(1)}, u32[]{:S(2)}, u32[]{:S(2)}) collective-permute-start(bf16[128,768]{1,0:T(8,128)(2,1)S(1)} %copy.128), channel_id=1, source_target_pairs={{0,16},{4,20},{8,24},{12,28},{16,0},{20,4},{24,8},{28,12},{1,17},{... | collective-permute-start | bytes 589832 | tf_op jit(solution)/shard_map/ppermute | solution.py:60
  12.9 36.1 %copy-start.10 = (bf16[256,128]{0,1:T(8,128)(2,1)}, bf16[256,128]{0,1:T(8,128)(2,1)S(1)}, u32[]{:S(2)}) copy-start(bf16[256,128]{0,1:T(8,128)(2,1)S(1)} %copy.129) | copy-start | bytes 196612
  12.9 5.0 %collective-permute-start.2 = (bf16[128,256]{1,0:T(8,128)(2,1)S(1)}, bf16[128,256]{1,0:T(8,128)(2,1)S(1)}, u32[]{:S(2)}, u32[]{:S(2)}) collective-permute-start(bf16[128,256]{1,0:T(8,128)(2,1)S(1)} %bitcast.80), channel_id=1, source_target_pairs={{0,4},{4,0},{8,12},{12,8},{16,20},{20,16},{24,28},{28,24},{1,5},{5... | collective-permute-start | bytes 196616 | tf_op jit(solution)/shard_map/ppermute | solution.py:60
  14.7 81.3 %copy-start.8 = (bf16[1024,128]{0,1:T(8,128)(2,1)}, bf16[1024,128]{0,1:T(8,128)(2,1)S(1)}, u32[]{:S(2)}) copy-start(bf16[1024,128]{0,1:T(8,128)(2,1)S(1)} %copy.130) | copy-start | bytes 786436
  14.7 8.0 %collective-permute-start.3 = (bf16[128,1024]{1,0:T(8,128)(2,1)S(1)}, bf16[128,1024]{1,0:T(8,128)(2,1)S(1)}, u32[]{:S(2)}, u32[]{:S(2)}) collective-permute-start(bf16[128,1024]{1,0:T(8,128)(2,1)S(1)} %bitcast.72), channel_id=1, source_target_pairs={{0,4},{4,0},{8,12},{12,8},{16,20},{20,16},{24,28},{28,24},{1,5},{5... | collective-permute-start | bytes 786440 | tf_op jit(solution)/shard_map/ppermute | solution.py:60
  16.1 76.4 %copy-start.7 = (bf16[128,1024]{1,0:T(8,128)(2,1)}, bf16[128,1024]{1,0:T(8,128)(2,1)S(1)}, u32[]{:S(2)}) copy-start(bf16[128,1024]{1,0:T(8,128)(2,1)S(1)} %convert_element_type.235.refs_8_) | copy-start | bytes 786436
  18.0 28.2 %copy-start.18 = (bf16[128,256]{1,0:T(8,128)(2,1)}, bf16[128,256]{1,0:T(8,128)(2,1)S(1)}, u32[]{:S(2)}) copy-start(bf16[128,256]{1,0:T(8,128)(2,1)S(1)} %collective-permute-done.2.refs_5_.refs_9_) | copy-start | bytes 196612
  20.8 28.9 %copy-start.17 = (bf16[128,768]{1,0:T(8,128)(2,1)}, bf16[128,768]{1,0:T(8,128)(2,1)S(1)}, u32[]{:S(2)}) copy-start(bf16[128,768]{1,0:T(8,128)(2,1)S(1)} %collective-permute-done.1.refs_5_) | copy-start | bytes 589828
  22.7 27.1 %copy-start.15 = (bf16[128,1024]{1,0:T(8,128)(2,1)}, bf16[128,1024]{1,0:T(8,128)(2,1)S(1)}, u32[]{:S(2)}) copy-start(bf16[128,1024]{1,0:T(8,128)(2,1)S(1)} %collective-permute-done.3.refs_13_.refs_9_) | copy-start | bytes 786436
  22.9 33.3 %copy-start.1 = (bf16[640,1024]{1,0:T(8,128)(2,1)S(1)}, bf16[640,1024]{1,0:T(8,128)(2,1)}, u32[]{:S(2)}) copy-start(bf16[640,1024]{1,0:T(8,128)(2,1)} %grad_ref) | copy-start | bytes 3932164
  22.9 21.3 %collective-permute-start.4 = (bf16[256,768]{1,0:T(8,128)(2,1)S(1)}, bf16[256,768]{1,0:T(8,128)(2,1)S(1)}, u32[]{:S(2)}, u32[]{:S(2)}) collective-permute-start(bf16[256,768]{1,0:T(8,128)(2,1)S(1)} %pad_maximum_fusion.6), channel_id=1, source_target_pairs={{0,8},{4,12},{8,0},{12,4},{16,24},{20,28},{24,16},{28,20},{1,9},{5... | collective-permute-start | bytes 1179656 | tf_op jit(solution)/shard_map/ppermute | solution.py:60
  25.1 19.0 %collective-permute-start.6 = (bf16[128,1024]{1,0:T(8,128)(2,1)S(1)}, bf16[128,1024]{1,0:T(8,128)(2,1)S(1)}, u32[]{:S(2)}, u32[]{:S(2)}) collective-permute-start(bf16[128,1024]{1,0:T(8,128)(2,1)S(1)} %convert_element_type.235.refs_8_), channel_id=1, source_target_pairs={{0,16},{4,20},{8,24},{12,28},{16,0},{20,4},{24,8},{28,12},{1,17},{... | collective-permute-start | bytes 786440 | tf_op jit(solution)/shard_map/ppermute | solution.py:60
  25.8 18.3 %collective-permute-start.5 = (bf16[256,256]{1,0:T(8,128)(2,1)S(1)}, bf16[256,256]{1,0:T(8,128)(2,1)S(1)}, u32[]{:S(2)}, u32[]{:S(2)}) collective-permute-start(bf16[256,256]{1,0:T(8,128)(2,1)S(1)} %pad_maximum_fusion.8), channel_id=1, source_target_pairs={{0,16},{4,20},{8,24},{12,28},{16,0},{20,4},{24,8},{28,12},{1,17},{... | collective-permute-start | bytes 393224 | tf_op jit(solution)/shard_map/ppermute | solution.py:60
  44.1 12.6 %copy-start.38 = (f32[1280]{0:T(1024)S(1)}, f32[1280]{0:T(1024)}, u32[]{:S(2)}) copy-start(f32[1280]{0:T(1024)} %iota_convert_fusion) | copy-start | bytes 15364
  44.1 12.6 %copy-start.45 = (s32[128]{0:T(128)S(1)}, s32[128]{0:T(128)}, u32[]{:S(2)}) copy-start(s32[128]{0:T(128)} %get-tuple-element.398) | copy-start | bytes 1540
  44.1 12.6 %copy-start.46 = (s32[128]{0:T(128)S(1)}, s32[128]{0:T(128)}, u32[]{:S(2)}) copy-start(s32[128]{0:T(128)} %get-tuple-element.399) | copy-start | bytes 1540
  44.1 16.5 %copy-start.14 = (bf16[128,1024]{1,0:T(8,128)(2,1)}, bf16[128,1024]{1,0:T(8,128)(2,1)S(1)}, u32[]{:S(2)}) copy-start(bf16[128,1024]{1,0:T(8,128)(2,1)S(1)} %collective-permute-done.6.refs_9_) | copy-start | bytes 786436
  45.0 34.2 %collective-permute-start.7 = (bf16[640,1024]{1,0:T(8,128)(2,1)}, bf16[640,1024]{1,0:T(8,128)(2,1)}, u32[]{:S(2)}, u32[]{:S(2)}) collective-permute-start(bf16[640,1024]{1,0:T(8,128)(2,1)} %get-tuple-element.171.refs_3_), channel_id=1, source_target_pairs={{0,1},{1,0},{2,3},{3,2},{4,5},{5,4},{6,7},{7,6},{8,9},{9,8},{10,11... | collective-permute-start | bytes 3932168 | tf_op jit(solution)/shard_map/ppermute | solution.py:60
  45.0 34.2 %collective-permute-start.8 = (bf16[640,1024]{1,0:T(8,128)(2,1)}, bf16[640,1024]{1,0:T(8,128)(2,1)}, u32[]{:S(2)}, u32[]{:S(2)}) collective-permute-start(bf16[640,1024]{1,0:T(8,128)(2,1)} %collective-permute-done.refs_2_), channel_id=1, source_target_pairs={{0,1},{1,0},{2,3},{3,2},{4,5},{5,4},{6,7},{7,6},{8,9},{9,8},{10,11... | collective-permute-start | bytes 3932168 | tf_op jit(solution)/shard_map/ppermute | solution.py:60
  46.2 9.9 %collective-permute-start.10 = (bf16[512,256]{1,0:T(8,128)(2,1)}, bf16[512,256]{1,0:T(8,128)(2,1)}, u32[]{:S(2)}, u32[]{:S(2)}) collective-permute-start(bf16[512,256]{1,0:T(8,128)(2,1)} %pad_maximum_fusion.7), channel_id=1, source_target_pairs={{0,8},{4,12},{8,0},{12,4},{16,24},{20,28},{24,16},{28,20},{1,9},{5... | collective-permute-start | bytes 786440 | tf_op jit(solution)/shard_map/ppermute | solution.py:60
  49.1 30.1 %collective-permute-start.9 = (bf16[512,768]{1,0:T(8,128)(2,1)}, bf16[512,768]{1,0:T(8,128)(2,1)}, u32[]{:S(2)}, u32[]{:S(2)}) collective-permute-start(bf16[512,768]{1,0:T(8,128)(2,1)} %pad_maximum_fusion.2), channel_id=1, source_target_pairs={{0,4},{4,0},{8,12},{12,8},{16,20},{20,16},{24,28},{28,24},{1,5},{5... | collective-permute-start | bytes 2359304 | tf_op jit(solution)/shard_map/ppermute | solution.py:60
  49.8 25.8 %collective-permute-start.11 = (bf16[256,1024]{1,0:T(8,128)(2,1)S(1)}, bf16[256,1024]{1,0:T(8,128)(2,1)S(1)}, u32[]{:S(2)}, u32[]{:S(2)}) collective-permute-start(bf16[256,1024]{1,0:T(8,128)(2,1)S(1)} %pad_maximum_fusion.3), channel_id=1, source_target_pairs={{0,16},{4,20},{8,24},{12,28},{16,0},{20,4},{24,8},{28,12},{1,17},{... | collective-permute-start | bytes 1572872 | tf_op jit(solution)/shard_map/ppermute | solution.py:60
  56.1 35.8 %collective-permute-start.12 = (bf16[640,1024]{1,0:T(8,128)(2,1)S(1)}, bf16[640,1024]{1,0:T(8,128)(2,1)}, u32[]{:S(2)}, u32[]{:S(2)}) collective-permute-start(bf16[640,1024]{1,0:T(8,128)(2,1)S(1)} %copy-done.1), channel_id=1, source_target_pairs={{0,2},{1,3},{2,0},{3,1},{4,6},{5,7},{6,4},{7,5},{8,10},{9,11},{10,... | collective-permute-start | bytes 3932168 | tf_op jit(solution)/shard_map/ppermute | solution.py:60
  76.4 15.5 %collective-permute-start.13 = (bf16[256,1024]{1,0:T(8,128)(2,1)}, bf16[256,1024]{1,0:T(8,128)(2,1)}, u32[]{:S(2)}, u32[]{:S(2)}) collective-permute-start(bf16[256,1024]{1,0:T(8,128)(2,1)} %pad_maximum_fusion.4), channel_id=1, source_target_pairs={{0,8},{4,12},{8,0},{12,4},{16,24},{20,28},{24,16},{28,20},{1,9},{5... | collective-permute-start | bytes 1572872 | tf_op jit(solution)/shard_map/ppermute | solution.py:60
  91.9 7.2 %collective-permute-start.14 = (bf16[640,1024]{1,0:T(8,128)(2,1)}, bf16[640,1024]{1,0:T(8,128)(2,1)}, u32[]{:S(2)}, u32[]{:S(2)}) collective-permute-start(bf16[640,1024]{1,0:T(8,128)(2,1)} %collective-permute-done.12.refs_2_.refs_6_), channel_id=1, source_target_pairs={{0,1},{1,0},{2,3},{3,2},{4,5},{5,4},{6,7},{7,6},{8,9},{9,8},{10,11... | collective-permute-start | bytes 3932168 | tf_op jit(solution)/shard_map/ppermute | solution.py:60
  92.0 7.1 %collective-permute-start.15 = (bf16[640,1024]{1,0:T(8,128)(2,1)S(1)}, bf16[640,1024]{1,0:T(8,128)(2,1)}, u32[]{:S(2)}, u32[]{:S(2)}) collective-permute-start(bf16[640,1024]{1,0:T(8,128)(2,1)S(1)} %copy-done.1), channel_id=1, source_target_pairs={{0,1},{1,0},{2,3},{3,2},{4,5},{5,4},{6,7},{7,6},{8,9},{9,8},{10,11... | collective-permute-start | bytes 3932168 | tf_op jit(solution)/shard_map/ppermute | solution.py:60
  94.6 66.4 %collective-permute-start.16 = (bf16[512,1024]{1,0:T(8,128)(2,1)}, bf16[512,1024]{1,0:T(8,128)(2,1)}, u32[]{:S(2)}, u32[]{:S(2)}) collective-permute-start(bf16[512,1024]{1,0:T(8,128)(2,1)} %pad_maximum_fusion), channel_id=1, source_target_pairs={{0,4},{4,0},{8,12},{12,8},{16,20},{20,16},{24,28},{28,24},{1,5},{5... | collective-permute-start | bytes 3145736 | tf_op jit(solution)/shard_map/ppermute | solution.py:60
  97.1 64.0 %collective-permute-start.17 = (bf16[512,1024]{1,0:T(8,128)(2,1)}, bf16[512,1024]{1,0:T(8,128)(2,1)}, u32[]{:S(2)}, u32[]{:S(2)}) collective-permute-start(bf16[512,1024]{1,0:T(8,128)(2,1)} %pad_maximum_fusion.1), channel_id=1, source_target_pairs={{0,8},{4,12},{8,0},{12,4},{16,24},{20,28},{24,16},{28,20},{1,9},{5... | collective-permute-start | bytes 3145736 | tf_op jit(solution)/shard_map/ppermute | solution.py:60
  182.7 5.2 %collective-permute-start.18 = (bf16[2,640,1024]{2,1,0:T(8,128)(2,1)}, bf16[2,640,1024]{2,1,0:T(8,128)(2,1)S(1)}, u32[]{:S(2)}, u32[]{:S(2)}) collective-permute-start(bf16[2,640,1024]{2,1,0:T(8,128)(2,1)} %get-tuple-element.206), channel_id=1, source_target_pairs={{0,1},{1,0},{2,3},{3,2},{4,5},{5,4},{6,7},{7,6},{8,9},{9,8},{10,11... | collective-permute-start | bytes 7864328 | tf_op jit(solution)/shard_map/ppermute | solution.py:60
  184.0 47.6 %collective-permute-start.20 = (bf16[4,128,1024]{2,1,0:T(8,128)(2,1)}, bf16[4,128,1024]{2,1,0:T(8,128)(2,1)}, u32[]{:S(2)}, u32[]{:S(2)}) collective-permute-start(bf16[4,128,1024]{2,1,0:T(8,128)(2,1)} %get-tuple-element.222), channel_id=1, source_target_pairs={{0,4},{4,0},{8,12},{12,8},{16,20},{20,16},{24,28},{28,24},{1,5},{5... | collective-permute-start | bytes 3145736 | tf_op jit(solution)/shard_map/ppermute | solution.py:60
  191.7 40.0 %collective-permute-start.19 = (bf16[1,640,1024]{2,1,0:T(8,128)(2,1)}, bf16[1,640,1024]{2,1,0:T(8,128)(2,1)}, u32[]{:S(2)}, u32[]{:S(2)}) collective-permute-start(bf16[1,640,1024]{2,1,0:T(8,128)(2,1)} %add_convert_fusion.2), channel_id=1, source_target_pairs={{0,2},{1,3},{2,0},{3,1},{4,6},{5,7},{6,4},{7,5},{8,10},{9,11},{10,... | collective-permute-start | bytes 3932168 | tf_op jit(solution)/shard_map/ppermute | solution.py:60
  192.2 39.5 %copy-start.37 = (f32[640]{0:T(1024)S(1)}, f32[640]{0:T(1024)}, u32[]{:S(2)}) copy-start(f32[640]{0:T(1024)} %copy-done.36) | copy-start | bytes 7684
  192.2 40.4 %copy-start.2 = (bf16[640,1024]{1,0:T(8,128)(2,1)S(1)}, bf16[640,1024]{1,0:T(8,128)(2,1)}, u32[]{:S(2)}) copy-start(bf16[640,1024]{1,0:T(8,128)(2,1)} %grad_ref) | copy-start | bytes 3932164
  231.7 6.9 %collective-permute-start.21 = (bf16[2,640,1024]{2,1,0:T(8,128)(2,1)}, bf16[2,640,1024]{2,1,0:T(8,128)(2,1)}, u32[]{:S(2)}, u32[]{:S(2)}) collective-permute-start(bf16[2,640,1024]{2,1,0:T(8,128)(2,1)} %get-tuple-element.225), channel_id=1, source_target_pairs={{0,1},{1,0},{2,3},{3,2},{4,5},{5,4},{6,7},{7,6},{8,9},{9,8},{10,11... | collective-permute-start | bytes 7864328 | tf_op jit(solution)/shard_map/ppermute | solution.py:60
  236.6 54.2 %collective-permute-start.24 = (bf16[4,128,1024]{2,1,0:T(8,128)(2,1)}, bf16[4,128,1024]{2,1,0:T(8,128)(2,1)}, u32[]{:S(2)}, u32[]{:S(2)}) collective-permute-start(bf16[4,128,1024]{2,1,0:T(8,128)(2,1)} %get-tuple-element.245), channel_id=1, source_target_pairs={{0,4},{4,0},{8,12},{12,8},{16,20},{20,16},{24,28},{28,24},{1,5},{5... | collective-permute-start | bytes 3145736 | tf_op jit(solution)/shard_map/ppermute | solution.py:60
  241.5 24.6 %collective-permute-start.22 = (bf16[2,128,1024]{2,1,0:T(8,128)(2,1)S(1)}, bf16[2,128,1024]{2,1,0:T(8,128)(2,1)}, u32[]{:S(2)}, u32[]{:S(2)}) collective-permute-start(bf16[2,128,1024]{2,1,0:T(8,128)(2,1)S(1)} %add_convert_fusion.4), channel_id=1, source_target_pairs={{0,8},{4,12},{8,0},{12,4},{16,24},{20,28},{24,16},{28,20},{1,9},{5... | collective-permute-start | bytes 1572872 | tf_op jit(solution)/shard_map/ppermute | solution.py:60
  242.1 48.8 %collective-permute-start.23 = (bf16[1,640,1024]{2,1,0:T(8,128)(2,1)}, bf16[1,640,1024]{2,1,0:T(8,128)(2,1)S(1)}, u32[]{:S(2)}, u32[]{:S(2)}) collective-permute-start(bf16[1,640,1024]{2,1,0:T(8,128)(2,1)} %add_convert_fusion.1), channel_id=1, source_target_pairs={{0,2},{1,3},{2,0},{3,1},{4,6},{5,7},{6,4},{7,5},{8,10},{9,11},{10,... | collective-permute-start | bytes 3932168 | tf_op jit(solution)/shard_map/ppermute | solution.py:60
  268.1 22.8 %collective-permute-start.25 = (bf16[1,128,1024]{2,1,0:T(8,128)(2,1)}, bf16[1,128,1024]{2,1,0:T(8,128)(2,1)}, u32[]{:S(2)}, u32[]{:S(2)}) collective-permute-start(bf16[1,128,1024]{2,1,0:T(8,128)(2,1)} %add_convert_fusion.8), channel_id=1, source_target_pairs={{0,16},{4,20},{8,24},{12,28},{16,0},{20,4},{24,8},{28,12},{1,17},{... | collective-permute-start | bytes 786440 | tf_op jit(solution)/shard_map/ppermute | solution.py:60
  270.4 20.5 %collective-permute-start.26 = (bf16[4,128,512]{2,1,0:T(8,128)(2,1)}, bf16[4,128,512]{2,1,0:T(8,128)(2,1)S(1)}, u32[]{:S(2)}, u32[]{:S(2)}) collective-permute-start(bf16[4,128,512]{2,1,0:T(8,128)(2,1)} %get-tuple-element.247), channel_id=1, source_target_pairs={{0,4},{4,0},{8,12},{12,8},{16,20},{20,16},{24,28},{28,24},{1,5},{5... | collective-permute-start | bytes 1572872 | tf_op jit(solution)/shard_map/ppermute | solution.py:60
  270.9 20.0 %collective-permute-start.27 = (bf16[4,128,512]{2,1,0:T(8,128)(2,1)}, bf16[4,128,512]{2,1,0:T(8,128)(2,1)}, u32[]{:S(2)}, u32[]{:S(2)}) collective-permute-start(bf16[4,128,512]{2,1,0:T(8,128)(2,1)} %get-tuple-element.248), channel_id=1, source_target_pairs={{0,8},{4,12},{8,0},{12,4},{16,24},{20,28},{24,16},{28,20},{1,9},{5... | collective-permute-start | bytes 1572872 | tf_op jit(solution)/shard_map/ppermute | solution.py:60
  290.9 29.7 %collective-permute-start.28 = (bf16[2,640,1024]{2,1,0:T(8,128)(2,1)}, bf16[2,640,1024]{2,1,0:T(8,128)(2,1)}, u32[]{:S(2)}, u32[]{:S(2)}) collective-permute-start(bf16[2,640,1024]{2,1,0:T(8,128)(2,1)} %get-tuple-element.252), channel_id=1, source_target_pairs={{0,1},{1,0},{2,3},{3,2},{4,5},{5,4},{6,7},{7,6},{8,9},{9,8},{10,11... | collective-permute-start | bytes 7864328 | tf_op jit(solution)/shard_map/ppermute | solution.py:60
  300.2 32.1 %collective-permute-start.32 = (bf16[2,128,1024]{2,1,0:T(8,128)(2,1)S(1)}, bf16[2,128,1024]{2,1,0:T(8,128)(2,1)}, u32[]{:S(2)}, u32[]{:S(2)}) collective-permute-start(bf16[2,128,1024]{2,1,0:T(8,128)(2,1)S(1)} %add_convert_fusion.3), channel_id=1, source_target_pairs={{0,8},{4,12},{8,0},{12,4},{16,24},{20,28},{24,16},{28,20},{1,9},{5... | collective-permute-start | bytes 1572872 | tf_op jit(solution)/shard_map/ppermute | solution.py:60
  303.2 27.6 %collective-permute-start.33 = (bf16[2,128,512]{2,1,0:T(8,128)(2,1)}, bf16[2,128,512]{2,1,0:T(8,128)(2,1)}, u32[]{:S(2)}, u32[]{:S(2)}) collective-permute-start(bf16[2,128,512]{2,1,0:T(8,128)(2,1)} %add_convert_fusion.7), channel_id=1, source_target_pairs={{0,8},{4,12},{8,0},{12,4},{16,24},{20,28},{24,16},{28,20},{1,9},{5... | collective-permute-start | bytes 786440 | tf_op jit(solution)/shard_map/ppermute | solution.py:60
  305.0 27.3 %collective-permute-start.34 = (bf16[2,128,512]{2,1,0:T(8,128)(2,1)S(1)}, bf16[2,128,512]{2,1,0:T(8,128)(2,1)}, u32[]{:S(2)}, u32[]{:S(2)}) collective-permute-start(bf16[2,128,512]{2,1,0:T(8,128)(2,1)S(1)} %add_convert_fusion.6), channel_id=1, source_target_pairs={{0,16},{4,20},{8,24},{12,28},{16,0},{20,4},{24,8},{28,12},{1,17},{... | collective-permute-start | bytes 786440 | tf_op jit(solution)/shard_map/ppermute | solution.py:60
  320.7 1.9 collective-permute-start.29
  322.6 4.5 %collective-permute-start.30 = (f32[15360]{0:T(1024)S(1)}, f32[15360]{0:T(1024)S(1)}, u32[]{:S(2)}, u32[]{:S(2)}) collective-permute-start(f32[15360]{0:T(1024)S(1)} %add.245), channel_id=1, source_target_pairs={{0,2},{1,3},{2,0},{3,1},{4,6},{5,7},{6,4},{7,5},{8,10},{9,11},{10,... | collective-permute-start | bytes 184328 | tf_op jit(solution)/shard_map/ppermute | solution.py:60
  323.3 11.5 %copy-start.23 = (bf16[4,128,512]{2,1,0:T(8,128)(2,1)S(1)}, bf16[4,128,512]{2,1,0:T(8,128)(2,1)}, u32[]{:S(2)}) copy-start(bf16[4,128,512]{2,1,0:T(8,128)(2,1)} %get-tuple-element.263) | copy-start | bytes 1572868
  323.4 11.5 %copy-start.27 = (bf16[4,128,512]{2,1,0:T(8,128)(2,1)S(1)}, bf16[4,128,512]{2,1,0:T(8,128)(2,1)}, u32[]{:S(2)}) copy-start(bf16[4,128,512]{2,1,0:T(8,128)(2,1)} %copy-done.26) | copy-start | bytes 1572868
  323.4 13.3 %copy-start.12 = (bf16[4,128,1024]{2,1,0:T(8,128)(2,1)S(1)}, bf16[4,128,1024]{2,1,0:T(8,128)(2,1)}, u32[]{:S(2)}) copy-start(bf16[4,128,1024]{2,1,0:T(8,128)(2,1)} %get-tuple-element.261) | copy-start | bytes 3145732
  327.1 5.2 %collective-permute-start.31 = (f32[15360]{0:T(1024)S(1)}, f32[15360]{0:T(1024)S(1)}, u32[]{:S(2)}, u32[]{:S(2)}) collective-permute-start(f32[15360]{0:T(1024)S(1)} %add.247), channel_id=1, source_target_pairs={{0,4},{4,0},{8,12},{12,8},{16,20},{20,16},{24,28},{28,24},{1,5},{5... | collective-permute-start | bytes 184328 | tf_op jit(solution)/shard_map/ppermute | solution.py:60
  330.3 20.4 %collective-permute-start.35 = (bf16[1,160,1024]{2,1,0:T(8,128)(2,1)S(1)}, bf16[1,160,1024]{2,1,0:T(8,128)(2,1)S(1)}, u32[]{:S(2)}, u32[]{:S(2)}) collective-permute-start(bf16[1,160,1024]{2,1,0:T(8,128)(2,1)S(1)} %get-tuple-element.268), channel_id=1, source_target_pairs={{0,2},{1,3},{2,0},{3,1},{4,6},{5,7},{6,4},{7,5},{8,10},{9,11},{10,... | collective-permute-start | bytes 983048 | tf_op jit(solution)/shard_map/ppermute | solution.py:60
  330.9 24.8 %collective-permute-start.37 = (bf16[1,160,1024]{2,1,0:T(8,128)(2,1)S(1)}, bf16[1,160,1024]{2,1,0:T(8,128)(2,1)S(1)}, u32[]{:S(2)}, u32[]{:S(2)}) collective-permute-start(bf16[1,160,1024]{2,1,0:T(8,128)(2,1)S(1)} %get-tuple-element.272), channel_id=1, source_target_pairs={{0,2},{1,3},{2,0},{3,1},{4,6},{5,7},{6,4},{7,5},{8,10},{9,11},{10,... | collective-permute-start | bytes 983048 | tf_op jit(solution)/shard_map/ppermute | solution.py:60
  333.4 6.6 %collective-permute-start.42 = (bf16[1,128,512]{2,1,0:T(8,128)(2,1)S(1)}, bf16[1,128,512]{2,1,0:T(8,128)(2,1)S(1)}, u32[]{:S(2)}, u32[]{:S(2)}) collective-permute-start(bf16[1,128,512]{2,1,0:T(8,128)(2,1)S(1)} %add_convert_fusion.9), channel_id=1, source_target_pairs={{0,4},{4,0},{8,12},{12,8},{16,20},{20,16},{24,28},{28,24},{1,5},{5... | collective-permute-start | bytes 393224 | tf_op jit(solution)/shard_map/ppermute | solution.py:60
  335.8 14.0 %collective-permute-start.41 = (bf16[1,128,512]{2,1,0:T(8,128)(2,1)S(1)}, bf16[1,128,512]{2,1,0:T(8,128)(2,1)S(1)}, u32[]{:S(2)}, u32[]{:S(2)}) collective-permute-start(bf16[1,128,512]{2,1,0:T(8,128)(2,1)S(1)} %add_convert_fusion.10), channel_id=1, source_target_pairs={{0,16},{4,20},{8,24},{12,28},{16,0},{20,4},{24,8},{28,12},{1,17},{... | collective-permute-start | bytes 393224 | tf_op jit(solution)/shard_map/ppermute | solution.py:60
  337.9 17.9 %collective-permute-start.43 = (bf16[1,128,1024]{2,1,0:T(8,128)(2,1)S(1)}, bf16[1,128,1024]{2,1,0:T(8,128)(2,1)S(1)}, u32[]{:S(2)}, u32[]{:S(2)}) collective-permute-start(bf16[1,128,1024]{2,1,0:T(8,128)(2,1)S(1)} %add_convert_fusion.5), channel_id=1, source_target_pairs={{0,16},{4,20},{8,24},{12,28},{16,0},{20,4},{24,8},{28,12},{1,17},{... | collective-permute-start | bytes 786440 | tf_op jit(solution)/shard_map/ppermute | solution.py:60
  350.8 10.5 %copy-start.32 = (bf16[1,160,1024]{2,1,0:T(8,128)(2,1)}, bf16[1,160,1024]{2,1,0:T(8,128)(2,1)S(1)}, u32[]{:S(2)}) copy-start(bf16[1,160,1024]{2,1,0:T(8,128)(2,1)S(1)} %collective-permute-done.35) | copy-start | bytes 983044
  350.8 4.9 %collective-permute-start.36 = (f32[15360]{0:T(1024)S(1)}, f32[15360]{0:T(1024)S(1)}, u32[]{:S(2)}, u32[]{:S(2)}) collective-permute-start(f32[15360]{0:T(1024)S(1)} %add.251), channel_id=1, source_target_pairs={{0,8},{4,12},{8,0},{12,4},{16,24},{20,28},{24,16},{28,20},{1,9},{5... | collective-permute-start | bytes 184328 | tf_op jit(solution)/shard_map/ppermute | solution.py:60
  350.9 10.4 %collective-permute-start.39 = (bf16[1,160,1024]{2,1,0:T(8,128)(2,1)S(1)}, bf16[1,160,1024]{2,1,0:T(8,128)(2,1)S(1)}, u32[]{:S(2)}, u32[]{:S(2)}) collective-permute-start(bf16[1,160,1024]{2,1,0:T(8,128)(2,1)S(1)} %get-tuple-element.276), channel_id=1, source_target_pairs={{0,2},{1,3},{2,0},{3,1},{4,6},{5,7},{6,4},{7,5},{8,10},{9,11},{10,... | collective-permute-start | bytes 983048 | tf_op jit(solution)/shard_map/ppermute | solution.py:60
  355.7 12.0 %copy-start.33 = (bf16[1,160,1024]{2,1,0:T(8,128)(2,1)}, bf16[1,160,1024]{2,1,0:T(8,128)(2,1)S(1)}, u32[]{:S(2)}) copy-start(bf16[1,160,1024]{2,1,0:T(8,128)(2,1)S(1)} %collective-permute-done.37) | copy-start | bytes 983044
  355.7 5.5 %collective-permute-start.38 = (f32[15360]{0:T(1024)S(1)}, f32[15360]{0:T(1024)S(1)}, u32[]{:S(2)}, u32[]{:S(2)}) collective-permute-start(f32[15360]{0:T(1024)S(1)} %add.252), channel_id=1, source_target_pairs={{0,16},{4,20},{8,24},{12,28},{16,0},{20,4},{24,8},{28,12},{1,17},{... | collective-permute-start | bytes 184328 | tf_op jit(solution)/shard_map/ppermute | solution.py:60
  358.0 9.6 %collective-permute-start.40 = (bf16[1,160,1024]{2,1,0:T(8,128)(2,1)S(1)}, bf16[1,160,1024]{2,1,0:T(8,128)(2,1)S(1)}, u32[]{:S(2)}, u32[]{:S(2)}) collective-permute-start(bf16[1,160,1024]{2,1,0:T(8,128)(2,1)S(1)} %get-tuple-element.278), channel_id=1, source_target_pairs={{0,2},{1,3},{2,0},{3,1},{4,6},{5,7},{6,4},{7,5},{8,10},{9,11},{10,... | collective-permute-start | bytes 983048 | tf_op jit(solution)/shard_map/ppermute | solution.py:60
  362.5 12.1 %copy-start.39 = (f32[1024]{0:T(1024)}, f32[1024]{0:T(1024)S(1)}, u32[]{:S(2)}) copy-start(f32[1024]{0:T(1024)S(1)} %get-tuple-element.428) | copy-start | bytes 12292
  (27 other events, 134.8 us)

commit v4 on v3

--- a/solution.py
+++ b/solution.py
@@ -19,20 +19,6 @@
 masked_score = -1e30
 VMEM_MOST = 62 << 20
 
-TAIL_SLOPE = 0.3
-TAIL_COEFS = (
-    0.11968663334846497,
-    0.11957288533449173,
-    0.11022695899009705,
-    0.07842729985713959,
-    0.09605274349451065,
-    -0.07923758029937744,
-    0.191569522023201,
-    -0.22805799543857574,
-    0.1123715341091156,
-    -0.02061200700700283,
-)
-
 
 def dot_nn(left, right):
     return lax.dot_general(left, right, (((1,), (0,)), ((), ())), preferred_element_type=f32)
@@ -87,11 +73,21 @@
         self.owners.append([j ^ bit for owners in self.owners for j in owners])
         self.arrays.append(swap(held, self.axis, bit))
 
-    def place(self, refs, where, number, columns):
+    def specs(self):
+        return [pl.BlockSpec(memory_space=pl.ANY)] * len(self.arrays)
+
+    def pieces(self):
+        return sum(len(owners) for owners in self.owners)
+
+    def copies(self, refs, where, number, done):
+        started = []
         for ref, owners in zip(refs, self.owners):
             for at, j in enumerate(owners):
                 rows = pl.ds(pl.multiple_of((number ^ j) * self.rows, self.rows), self.rows)
-                where[rows, :] = ref[at * self.rows : (at + 1) * self.rows, columns]
+                source = ref.at[pl.ds(at * self.rows, self.rows), :]
+                copy = pltpu.make_async_copy(source, where.at[rows, :], done.at[len(started)])
+                started.append(copy)
+        return started
 
 
 def tie_packs(*packs, beside=()):
@@ -112,22 +108,19 @@
 
 class Halving:
     def __init__(self, send, keep, axis, bits):
-        self.send, self.terms, self.axis, self.bits = send, [keep], axis, list(bits)
+        self.send, self.axis, self.bits = send, axis, list(bits)
+        self.terms = [(keep, 0)]
 
     def swap(self):
         self.got = swap(self.send, self.axis, self.bits.pop(0))
 
     def add(self):
-        terms = self.terms + [self.got]
-        if self.got.shape[0] > 1:
-            half = self.got.shape[0] // 2
-            self.send = sum(x[:half].astype(f32) for x in terms).astype(bf16)
-            self.terms = [x[half:] for x in terms]
-        else:
-            self.terms = [x[0] for x in terms]
-
-    def total(self):
-        return sum(x.astype(f32) for x in self.terms)
+        self.terms.append((self.got, 0))
+        half = self.got.shape[0] // 2
+        if half:
+            sends = [x[at : at + half].astype(f32) for x, at in self.terms]
+            self.send = sum(sends).astype(bf16)
+            self.terms = [(x, at + half) for x, at in self.terms]
 
     def most(self):
         while len(self.bits) > 1:
@@ -138,7 +131,7 @@
         while self.bits:
             self.swap()
             self.add()
-        return self.total()
+        return sum(x[at].astype(f32) for x, at in self.terms)
 
 
 def tie_halves(values, *halvings):
@@ -183,18 +176,31 @@
 class Tokens:
     def __init__(self, pieces, order):
         self.groups, (self.rows, self.model) = len(pieces), pieces[0].shape
-        if self.groups <= 4:
-            self.arrays = [pieces[j] for j in order]
-            self.specs = [resident(x.shape) for x in pieces]
-        else:
-            self.arrays = [jnp.concatenate([pieces[j] for j in order], axis=0)]
-            self.specs = [step_block(self.rows, self.model)]
+        self.arrays = [pieces[j] for j in order]
+        self.specs = [pl.BlockSpec(memory_space=pl.ANY)] * self.groups
+
+    def scratch(self):
+        return [
+            pltpu.VMEM((2, self.rows, self.model), bf16),
+            pltpu.SemaphoreType.DMA((2,)),
+        ]
+
+    def fetch(self, refs, held, done, step):
+        def copy(at):
+            return pltpu.make_async_copy(refs[at], held.at[at % 2], done.at[at % 2])
+
+        for at in range(self.groups):
+
+            @pl.when(step == at)
+            def _(at=at):
+                if at == 0:
+                    copy(0).start()
+                if at + 1 < self.groups:
+                    copy(at + 1).start()
+                copy(at).wait()
 
 
 def pick_piece(pieces, where, step):
-    if len(pieces) == 1:
-        where[...] = pieces[0][...]
-        return
     for at, piece in enumerate(pieces):
 
         @pl.when(step == at)
@@ -257,22 +263,36 @@
     return done[0] if len(done) == 1 else jnp.concatenate(done, axis=1)
 
 
+def weight_scratch(pack):
+    model = pack.rows * pack.pieces()
+    columns = pack.arrays[0].shape[1]
+    return [pltpu.VMEM((model, columns), bf16), pltpu.SemaphoreType.DMA((pack.pieces(),))]
+
+
 def project_qkv(ids, info, sent, gain, shift, pack, bias, tables, width):
-    groups, held, pieces = sent.groups, len(sent.arrays), len(pack.arrays)
-    rows, model = sent.rows, sent.model
+    groups, held, rows, model = sent.groups, len(sent.arrays), sent.rows, sent.model
 
     def kernel(ids, info, *refs):
         sent_refs, refs = refs[:held], refs[held:]
-        weight_refs, refs = refs[:pieces], refs[pieces:]
-        gain, shift, bias, cos, low, high, q_out, k_out, v_out, whole, block = refs
+        weight_refs, refs = refs[: len(pack.arrays)], refs[len(pack.arrays) :]
+        gain, shift, bias, cos, low, high, q_out, k_out, v_out = refs[:9]
+        block, arrived, whole, placed = refs[9:]
         step = pl.program_id(0)
 
         @pl.when(step == 0)
         def _():
-            pack.place(weight_refs, whole, ids[1], slice(None))
-
-        pick_piece(sent_refs, block, step)
-        qkv = dot_nn(shift_gain(block[...], gain, shift), whole[...]) + bias[...]
+            for copy in pack.copies(weight_refs, whole, ids[1], placed):
+                copy.start()
+
+        sent.fetch(sent_refs, block, arrived, step)
+
+        @pl.when(step == 0)
+        def _():
+            for copy in pack.copies(weight_refs, whole, ids[1], placed):
+                copy.wait()
+
+        token = block[step % 2]
+        qkv = dot_nn(shift_gain(token, gain, shift), whole[...]) + bias[...]
         first = (ids[0] ^ ids[2 + step]) * (rows // SEG)
         for at in range(rows // SEG):
             number = first + at
@@ -291,29 +311,37 @@
         (groups,),
         [ids, info],
         operands,
-        sent.specs + [resident(x.shape) for x in operands[held:]],
+        sent.specs
+        + pack.specs()
+        + [resident(x.shape) for x in operands[held + len(pack.arrays) :]],
         [out] * 3,
         [own_block(rows, width)] * 3,
-        [pltpu.VMEM((model, 3 * width), bf16), pltpu.VMEM((rows, model), bf16)],
+        sent.scratch() + weight_scratch(pack),
         2 * groups * rows * model * 3 * width,
     )
 
 
 def project_grad(ids, grad, pack, width):
-    groups, held, pieces = grad.groups, len(grad.arrays), len(pack.arrays)
-    rows, model = grad.rows, grad.model
+    groups, held, rows, model = grad.groups, len(grad.arrays), grad.rows, grad.model
 
     def kernel(ids, *refs):
         grad_refs, refs = refs[:held], refs[held:]
-        weight_refs, (out, whole, block) = refs[:pieces], refs[pieces:]
+        weight_refs, (out, block, arrived, whole, placed) = refs[:-5], refs[-5:]
         step = pl.program_id(0)
 
         @pl.when(step == 0)
         def _():
-            pack.place(weight_refs, whole, ids[1], slice(None))
-
-        pick_piece(grad_refs, block, step)
-        out[...] = dot_nn(block[...], whole[...]).astype(bf16)
+            for copy in pack.copies(weight_refs, whole, ids[1], placed):
+                copy.start()
+
+        grad.fetch(grad_refs, block, arrived, step)
+
+        @pl.when(step == 0)
+        def _():
+            for copy in pack.copies(weight_refs, whole, ids[1], placed):
+                copy.wait()
+
+        out[...] = dot_nn(block[step % 2], whole[...]).astype(bf16)
 
     operands = [*grad.arrays, *pack.arrays]
     return call(
@@ -322,10 +350,10 @@
         (groups,),
         [ids],
         operands,
-        grad.specs + [resident(x.shape) for x in operands[held:]],
+        grad.specs + pack.specs(),
         [shaped(groups * rows, width)],
         [own_block(rows, width)],
-        [pltpu.VMEM((model, width), bf16), pltpu.VMEM((rows, model), bf16)],
+        grad.scratch() + weight_scratch(pack),
         2 * groups * rows * model * width,
     )[0]
 
@@ -452,34 +480,174 @@
     )
 
 
-def attention_backward(
-    ids, info, tables, context, dq, dk, dv, sent, grad, gain, shift, qkv_pack, dense_pack, bits
-):
-    groups, held, pieces = sent.groups, len(sent.arrays), len(dense_pack.arrays)
-    rows, model = sent.rows, sent.model
-    width = dq.shape[1]
-    order = halving_order(bits)
-
-    def kernel(ids, info, ctx_ref, dq_ref, dk_ref, dv_ref, *refs):
+def project_context(ids, context, pack, groups, model):
+    rows, width = context.shape[0] // groups, context.shape[1]
+
+    def kernel(ids, ctx, *refs):
+        weight_refs, (send, keep, whole, placed) = refs[:-4], refs[-4:]
+        step = pl.program_id(0)
+
+        @pl.when(step == 0)
+        def _():
+            copies = pack.copies(weight_refs, whole, ids[1], placed)
+            for copy in copies:
+                copy.start()
+            for copy in copies:
+                copy.wait()
+
+        store_half(send, keep, dot_nt(ctx[...], whole[...]).astype(bf16), step, groups)
+
+    operands = [context, *pack.arrays]
+    half = shaped(groups // 2, rows, model)
+    return call(
+        kernel,
+        "project_context",
+        (groups,),
+        [ids],
+        operands,
+        [own_block(rows, width)] + pack.specs(),
+        [half] * 2,
+        half_blocks(groups, rows, model),
+        weight_scratch(pack),
+        2 * groups * rows * model * width,
+    )
+
+
+def mlp(ids, sent, grad, context, gain, shift, fc, bias, out, orders):
+    groups, held, rows, model = sent.groups, len(sent.arrays), sent.rows, sent.model
+    pieces, units, width = len(fc.arrays), fc.arrays[0].shape[1], context.shape[1]
+
+    def kernel(ids, ctx_ref, *refs):
         sent_refs, refs = refs[:held], refs[held:]
         grad_refs, refs = refs[:held], refs[held:]
-        weight_refs, refs = refs[:pieces], refs[pieces:]
-        gain, shift, cos, low, high, part_send, part_keep, grads, bias_ref, send, keep = refs[:11]
-        whole, block, grad_block, total, dense_total = refs[11:]
+        fc_refs, refs = refs[:pieces], refs[pieces:]
+        out_refs, refs = refs[:pieces], refs[pieces:]
+        gain, shift, bias, part_send, part_keep, hidden_ref, bias_ref = refs[:7]
+        stacks, refs = refs[7:11], refs[11:]
+        block, arrived, grad_block, grad_arrived, fc_whole, fc_placed, out_whole, out_placed = refs[:8]
+        act_ref, fc_total, out_total, dense_total = refs[8:]
         step = pl.program_id(0)
+
+        def weights():
+            copies = fc.copies(fc_refs, fc_whole, ids[1], fc_placed)
+            return copies + out.copies(out_refs, out_whole, ids[1], out_placed)
 
         @pl.when(step == 0)
         def _():
-            dense_pack.place(weight_refs, whole, ids[1], slice(None))
-            total[...] = jnp.zeros_like(total)
+            for copy in weights():
+                copy.start()
+            fc_total[...] = jnp.zeros_like(fc_total)
+            out_total[...] = jnp.zeros_like(out_total)
             dense_total[...] = jnp.zeros_like(dense_total)
             bias_ref[...] = jnp.zeros_like(bias_ref)
 
-        pick_piece(sent_refs, block, step)
-        pick_piece(grad_refs, grad_block, step)
+        sent.fetch(sent_refs, block, arrived, step)
+        grad.fetch(grad_refs, grad_block, grad_arrived, step)
+
+        @pl.when(step == 0)
+        def _():
+            for copy in weights():
+                copy.wait()
+
+        token, grads = block[step % 2], grad_block[step % 2]
+        normed = shift_gain(token, gain, shift)
+        count = 2
+        parts = [slice(k * rows // count, (k + 1) * rows // count) for k in range(count)]
+        hidden = [dot_nn(normed[x], fc_whole[...]) + bias[...] for x in parts]
+        back = [dot_nn(grads[x], out_whole[...]) for x in parts]
+        for x, field, slope in zip(parts, hidden, back):
+            chance = 0.5 + 0.5 * lax.erf(field * 0.7071067811865476)
+            bell = jnp.exp(field * field * -0.5) * 0.3989422804014327
+            act_ref[x, :] = (field * chance).astype(bf16)
+            low = (slope * (chance + field * bell)).astype(bf16)
+            hidden_ref[x, :] = low
+            bias_ref[0:1, :] += jnp.sum(low.astype(f32), axis=0, keepdims=True)
         store_half(
-            part_send, part_keep, dot_nt(ctx_ref[...], whole[...]).astype(bf16), step, groups
+            part_send, part_keep, dot_nt(act_ref[...], out_whole[...]).astype(bf16), step, groups
         )
+        out_total[...] += dot_tn(grads, act_ref[...])
+        fc_total[...] += dot_tn(normed, hidden_ref[...])
+        dense_total[...] += dot_tn(grads, ctx_ref[...])
+
+        @pl.when(step == groups - 1)
+        def _():
+            half = units // 2
+            for at, order in enumerate(orders):
+                stack = stacks[2 * at : 2 * at + 2]
+                source = slice(at * half, (at + 1) * half)
+                store_halves(*stack, fc_total, ids[1], order, slice(0, half), source)
+                store_halves(*stack, out_total, ids[1], order, slice(half, units), source)
+            columns = slice(units, units + width)
+            store_halves(*stacks[:2], dense_total, ids[1], orders[0], columns)
+
+    operands = [context, *sent.arrays, *grad.arrays, *fc.arrays, *out.arrays, gain, shift, bias]
+    count = model // fc.rows
+    outs = [
+        shaped(groups // 2, rows, model),
+        shaped(groups // 2, rows, model),
+        shaped(groups * rows, units),
+        shaped(8, units, dtype=f32),
+    ]
+    outs += [shaped(count // 2, fc.rows, units + width)] * 2
+    outs += [shaped(count // 2, fc.rows, units)] * 2
+    return call(
+        kernel,
+        "mlp",
+        (groups,),
+        [ids],
+        operands,
+        [own_block(rows, width)]
+        + sent.specs
+        + grad.specs
+        + fc.specs()
+        + out.specs()
+        + [resident(x.shape) for x in operands[-3:]],
+        outs,
+        half_blocks(groups, rows, model)
+        + [step_block(rows, units)]
+        + [resident(x.shape) for x in outs[3:]],
+        sent.scratch()
+        + grad.scratch()
+        + weight_scratch(fc)
+        + weight_scratch(out)
+        + [
+            pltpu.VMEM((rows, units), bf16),
+            pltpu.VMEM((model, units), f32),
+            pltpu.VMEM((model, units), f32),
+            pltpu.VMEM((model, width), f32),
+        ],
+        10 * groups * rows * model * units,
+    )
+
+
+def norm_backward(
+    ids, info, tables, sent, dq, dk, dv, hidden, gain_attn, shift_attn, gain_mlp, qkv_pack, fc, orders
+):
+    groups, held, rows, model = sent.groups, len(sent.arrays), sent.rows, sent.model
+    pieces, units, width = len(fc.arrays), hidden.shape[1], dq.shape[1]
+
+    def kernel(ids, info, dq_ref, dk_ref, dv_ref, hidden_ref, *refs):
+        sent_refs, refs = refs[:held], refs[held:]
+        qkv_refs, refs = refs[:pieces], refs[pieces:]
+        fc_refs, refs = refs[:pieces], refs[pieces:]
+        gain_attn, shift_attn, gain_mlp, cos, low, high = refs[:6]
+        send, keep, sums_ref, bias_ref, *halves = refs[6:14]
+        block, arrived, qkv_whole, qkv_placed, fc_whole, fc_placed, grads, total = refs[14:]
+        step = pl.program_id(0)
+
+        def weights():
+            copies = qkv_pack.copies(qkv_refs, qkv_whole, ids[1], qkv_placed)
+            return copies + fc.copies(fc_refs, fc_whole, ids[1], fc_placed)
+
+        @pl.when(step == 0)
+        def _():
+            for copy in weights():
+                copy.start()
+            sums_ref[...] = jnp.zeros_like(sums_ref)
+            bias_ref[...] = jnp.zeros_like(bias_ref)
+            total[...] = jnp.zeros_like(total)
+
+        sent.fetch(sent_refs, block, arrived, step)
         grads[:, :width] = dq_ref[...]
         first = (ids[0] ^ ids[2 + step]) * (rows // SEG)
         for at in range(rows // SEG):
@@ -490,246 +658,77 @@
             grads[own, width : 2 * width] = turned.astype(bf16)
         grads[:, 2 * width :] = dv_ref[...]
         bias_ref[0:1, :] += jnp.sum(grads[...].astype(f32), axis=0, keepdims=True)
-        total[...] += dot_tn(shift_gain(block[...], gain, shift), grads[...])
-        dense_total[...] += dot_tn(grad_block[...], ctx_ref[...])
+
+        @pl.when(step == 0)
+        def _():
+            for copy in weights():
+                copy.wait()
+
+        token = block[step % 2]
+        total[...] += dot_tn(shift_gain(token, gain_attn, shift_attn), grads[...])
+        back_attn = dot_nt(grads[...], qkv_whole[...])
+        back_mlp = dot_nt(hidden_ref[...], fc_whole[...])
+        token = token.astype(f32)
+        for at, back in enumerate((back_attn, back_mlp)):
+            sums_ref[2 * at : 2 * at + 1, :] += jnp.sum(back * token, axis=0, keepdims=True)
+            sums_ref[2 * at + 1 : 2 * at + 2, :] += jnp.sum(back, axis=0, keepdims=True)
+        part = back_attn * gain_attn[...] + back_mlp * gain_mlp[...]
+        store_half(send, keep, part.astype(bf16), step, groups)
 
         @pl.when(step == groups - 1)
         def _():
-            store_halves(send, keep, total, ids[1], order, slice(0, 3 * width))
-            store_halves(send, keep, dense_total, ids[1], order, slice(3 * width, 4 * width))
+            for at, order in enumerate(orders):
+                source = slice(at * 3 * width // 2, (at + 1) * 3 * width // 2)
+                store_halves(*halves[2 * at : 2 * at + 2], total, ids[1], order, source=source)
 
     operands = [
-        context,
         dq,
         dk,
         dv,
+        hidden,
         *sent.arrays,
-        *grad.arrays,
-        *dense_pack.arrays,
-        gain,
-        shift,
+        *qkv_pack.arrays,
+        *fc.arrays,
+        gain_attn,
+        shift_attn,
+        gain_mlp,
         *tables,
     ]
-    count = model // qkv_pack.rows
-    outs = [
-        shaped(groups // 2, rows, model),
-        shaped(groups // 2, rows, model),
-        shaped(groups * rows, 3 * width),
-        shaped(8, 3 * width, dtype=f32),
-        shaped(count // 2, qkv_pack.rows, 4 * width),
-        shaped(count // 2, qkv_pack.rows, 4 * width),
-    ]
-    return call(
-        kernel,
-        "attention_backward",
-        (groups,),
-        [ids, info],
-        operands,
-        [own_block(rows, width)] * 4
-        + sent.specs
-        + grad.specs
-        + [resident(x.shape) for x in operands[4 + 2 * held :]],
-        outs,
-        half_blocks(groups, rows, model)
-        + [step_block(rows, 3 * width)]
-        + [resident(x.shape) for x in outs[3:]],
-        [
-            pltpu.VMEM((model, width), bf16),
-            pltpu.VMEM((rows, model), bf16),
-            pltpu.VMEM((rows, model), bf16),
-            pltpu.VMEM((model, 3 * width), f32),
-            pltpu.VMEM((model, width), f32),
-        ],
-        2 * groups * rows * model * 5 * width,
-    )
-
-
-def mlp_forward(ids, sent, grad, gain, shift, fc, bias, out, out_order):
-    groups, held, pieces = sent.groups, len(sent.arrays), len(fc.arrays)
-    rows, model = sent.rows, sent.model
-    units = fc.arrays[0].shape[1]
-
-    def kernel(ids, *refs):
-        sent_refs, refs = refs[:held], refs[held:]
-        grad_refs, refs = refs[:held], refs[held:]
-        fc_refs, refs = refs[:pieces], refs[pieces:]
-        out_refs, refs = refs[:pieces], refs[pieces:]
-        gain, shift, bias, act_ref, slope_ref, send, keep, out_send, out_keep = refs[:9]
-        fc_whole, out_whole, block, grad_block, total = refs[9:]
-        step = pl.program_id(0)
-
-        @pl.when(step == 0)
-        def _():
-            fc.place(fc_refs, fc_whole, ids[1], slice(None))
-            out.place(out_refs, out_whole, ids[1], slice(None))
-            total[...] = jnp.zeros_like(total)
-
-        pick_piece(sent_refs, block, step)
-        pick_piece(grad_refs, grad_block, step)
-        hidden = dot_nn(shift_gain(block[...], gain, shift), fc_whole[...]) + bias[...]
-        size = jnp.abs(hidden)
-        ratio = 1.0 / (1.0 + TAIL_SLOPE * size)
-        tail = jnp.full_like(ratio, TAIL_COEFS[-1])
-        for coef in TAIL_COEFS[-2::-1]:
-            tail = tail * ratio + coef
-        bell = jnp.exp(hidden * hidden * -0.5)
-        tail = tail * ratio * bell
-        chance = jnp.where(hidden < 0, tail, 1.0 - tail)
-        active = (hidden * chance).astype(bf16)
-        act_ref[...] = active
-        slope_ref[...] = chance + hidden * bell * 0.3989422804014327
-        store_half(send, keep, dot_nt(active, out_whole[...]).astype(bf16), step, groups)
-        total[...] += dot_tn(grad_block[...], active)
-
-        @pl.when(step == groups - 1)
-        def _():
-            store_halves(out_send, out_keep, total, ids[1], out_order)
-
-    operands = [*sent.arrays, *grad.arrays, *fc.arrays, *out.arrays, gain, shift, bias]
     count = model // fc.rows
-    outs = [
-        shaped(groups * rows, units),
-        shaped(groups * rows, units, dtype=f32),
-        shaped(groups // 2, rows, model),
-        shaped(groups // 2, rows, model),
-        shaped(count // 2, fc.rows, units),
-        shaped(count // 2, fc.rows, units),
-    ]
-    return call(
-        kernel,
-        "mlp_forward",
-        (groups,),
-        [ids],
-        operands,
-        sent.specs + grad.specs + [resident(x.shape) for x in operands[2 * held :]],
-        outs,
-        [step_block(rows, units)] * 2
-        + half_blocks(groups, rows, model)
-        + [resident(x.shape) for x in outs[4:]],
-        [
-            pltpu.VMEM((model, units), bf16),
-            pltpu.VMEM((model, units), bf16),
-            pltpu.VMEM((rows, model), bf16),
-            pltpu.VMEM((rows, model), bf16),
-            pltpu.VMEM((model, units), f32),
-        ],
-        6 * groups * rows * model * units,
-    )
-
-
-def hidden_backward(ids, sent, grad, slope, gain, shift, fc, out, orders):
-    groups, held, pieces = sent.groups, len(sent.arrays), len(fc.arrays)
-    rows, model = sent.rows, sent.model
-    units = fc.arrays[0].shape[1]
-
-    def kernel(ids, slope_ref, *refs):
-        sent_refs, refs = refs[:held], refs[held:]
-        grad_refs, refs = refs[:held], refs[held:]
-        out_refs, refs = refs[:pieces], refs[pieces:]
-        gain, shift, hidden_ref, bias_ref, *halves = refs[:8]
-        out_whole, block, grad_block, fc_total = refs[8:]
-        step = pl.program_id(0)
-
-        @pl.when(step == 0)
-        def _():
-            out.place(out_refs, out_whole, ids[1], slice(None))
-            fc_total[...] = jnp.zeros_like(fc_total)
-            bias_ref[...] = jnp.zeros_like(bias_ref)
-
-        pick_piece(sent_refs, block, step)
-        pick_piece(grad_refs, grad_block, step)
-        hidden = (dot_nn(grad_block[...], out_whole[...]) * slope_ref[...]).astype(bf16)
-        hidden_ref[...] = hidden
-        bias_ref[0:1, :] += jnp.sum(hidden.astype(f32), axis=0, keepdims=True)
-        fc_total[...] += dot_tn(shift_gain(block[...], gain, shift), hidden)
-
-        @pl.when(step == groups - 1)
-        def _():
-            for at, order in enumerate(orders):
-                source = slice(at * units // 2, (at + 1) * units // 2)
-                send, keep = halves[2 * at : 2 * at + 2]
-                store_halves(send, keep, fc_total, ids[1], order, source=source)
-
-    operands = [slope, *sent.arrays, *grad.arrays, *out.arrays, gain, shift]
-    count = model // fc.rows
-    outs = [shaped(groups * rows, units), shaped(8, units, dtype=f32)]
-    outs += [shaped(count // 2, fc.rows, units // 2)] * 4
-    return call(
-        kernel,
-        "hidden_backward",
-        (groups,),
-        [ids],
-        operands,
-        [step_block(rows, units)]
-        + sent.specs
-        + grad.specs
-        + [resident(x.shape) for x in operands[1 + 2 * held :]],
-        outs,
-        [step_block(rows, units)] + [resident(x.shape) for x in outs[1:]],
-        [
-            pltpu.VMEM((model, units), bf16),
-            pltpu.VMEM((rows, model), bf16),
-            pltpu.VMEM((rows, model), bf16),
-            pltpu.VMEM((model, units), f32),
-        ],
-        4 * groups * rows * model * units,
-    )
-
-
-def norm_backward(ids, sent, grads, hidden, gain_attn, gain_mlp, qkv_pack, fc):
-    groups, held, pieces = sent.groups, len(sent.arrays), len(fc.arrays)
-    rows, model = sent.rows, sent.model
-    units, columns = hidden.shape[1], grads.shape[1]
-
-    def kernel(ids, grads_ref, hidden_ref, *refs):
-        sent_refs, refs = refs[:held], refs[held:]
-        qkv_refs, refs = refs[:pieces], refs[pieces:]
-        fc_refs, refs = refs[:pieces], refs[pieces:]
-        gain_attn, gain_mlp, send, keep, sums_ref, qkv_whole, fc_whole, block = refs
-        step = pl.program_id(0)
-
-        @pl.when(step == 0)
-        def _():
-            qkv_pack.place(qkv_refs, qkv_whole, ids[1], slice(None))
-            fc.place(fc_refs, fc_whole, ids[1], slice(None))
-            sums_ref[...] = jnp.zeros_like(sums_ref)
-
-        pick_piece(sent_refs, block, step)
-        token = block[...].astype(f32)
-        back = dot_nt(grads_ref[...], qkv_whole[...])
-        sums_ref[0:1, :] += jnp.sum(back * token, axis=0, keepdims=True)
-        sums_ref[1:2, :] += jnp.sum(back, axis=0, keepdims=True)
-        part = back * gain_attn[...]
-        back = dot_nt(hidden_ref[...], fc_whole[...])
-        sums_ref[2:3, :] += jnp.sum(back * token, axis=0, keepdims=True)
-        sums_ref[3:4, :] += jnp.sum(back, axis=0, keepdims=True)
-        part = part + back * gain_mlp[...]
-        store_half(send, keep, part.astype(bf16), step, groups)
-
-    operands = [grads, hidden, *sent.arrays, *qkv_pack.arrays, *fc.arrays, gain_attn, gain_mlp]
     outs = [
         shaped(groups // 2, rows, model),
         shaped(groups // 2, rows, model),
         shaped(8, model, dtype=f32),
+        shaped(8, 3 * width, dtype=f32),
     ]
+    outs += [shaped(count // 2, fc.rows, 3 * width // 2)] * 4
     return call(
         kernel,
         "norm_backward",
         (groups,),
-        [ids],
+        [ids, info],
         operands,
-        [step_block(rows, columns), step_block(rows, units)]
+        [own_block(rows, width)] * 3
+        + [step_block(rows, units)]
         + sent.specs
-        + [resident(x.shape) for x in operands[2 + held :]],
+        + qkv_pack.specs()
+        + fc.specs()
+        + [resident(x.shape) for x in operands[-6:]],
         outs,
         half_blocks(groups, rows, model) + [resident(x.shape) for x in outs[2:]],
-        [
-            pltpu.VMEM((model, columns), bf16),
-            pltpu.VMEM((model, units), bf16),
-            pltpu.VMEM((rows, model), bf16),
-        ],
-        2 * groups * rows * model * (units + columns),
-    )
+        sent.scratch()
+        + weight_scratch(qkv_pack)
+        + weight_scratch(fc)
+        + [pltpu.VMEM((rows, 3 * width), bf16), pltpu.VMEM((model, 3 * width), f32)],
+        2 * groups * rows * model * (units + 6 * width),
+    )
+
+
+def taken(terms, block):
+    return [
+        pl.BlockSpec((pl.Squeezed(), block, x.shape[2]), lambda i, *_, at=at: (at, i, 0))
+        for x, at in terms
+    ]
 
 
 def finish_output(stream, attn_terms, mlp_terms, dense_bias, out_bias):
@@ -752,7 +751,8 @@
         for at, value in enumerate((output, attn, mlp)):
             sums_ref[at : at + 1, :] += jnp.sum(value * value, axis=0, keepdims=True)
 
-    operands = [stream, *attn_terms, *mlp_terms, dense_bias, out_bias]
+    terms = [*attn_terms, *mlp_terms]
+    operands = [stream, *[x for x, _ in terms], dense_bias, out_bias]
     outs = [shaped(rows, model, dtype=f32), shaped(8, model, dtype=f32)]
     return call(
         kernel,
@@ -760,7 +760,8 @@
         (rows // block,),
         [],
         operands,
-        [step_block(block, model)] * (1 + first + second)
+        [step_block(block, model)]
+        + taken(terms, block)
         + [resident(dense_bias.shape), resident(out_bias.shape)],
         outs,
         [step_block(block, model), resident(outs[1].shape)],
@@ -783,7 +784,7 @@
         cross = jnp.sum(sent * norm, axis=1, keepdims=True) / model
         out_ref[...] = grad_ref[...].astype(f32) + std_ref[...] * (sent - mean - norm * cross)
 
-    operands = [grad, normalized, inv_std, *terms, *chunks]
+    operands = [grad, normalized, inv_std, *[x for x, _ in terms], *chunks]
     return call(
         kernel,
         "finish_grad",
@@ -791,7 +792,7 @@
         [],
         operands,
         [step_block(block, model), step_block(block, model), step_block(block, 1)]
-        + [step_block(block, model)] * held
+        + taken(terms, block)
         + [resident(x.shape) for x in chunks],
         [shaped(rows, model, dtype=f32)],
         [step_block(block, model)],
@@ -878,7 +879,8 @@
     data_bits = bits_of(lax.axis_size("dp"))
     rows_first = data_bits[:0:-1] + data_bits[:1]
     columns_first = data_bits[:1] + data_bits[:0:-1]
-    out_bits, fc_bits = columns_first[::-1], rows_first[::-1]
+    near_bits = data_bits
+    next_bits = data_bits[1:2] + data_bits[:1] + data_bits[2:]
 
     qkv_pack = Pack(by_kind(qkv_weight.astype(bf16), heads), "dp", rows_first)
     dense_pack = Pack(dense_weight.astype(bf16).T, "dp", columns_first)
@@ -931,75 +933,61 @@
     out_pack.double()
     done = attention(info, tables, queries, keys, values, grad_context)
     context, dq, dk, dv = tie_packs(fc_pack, out_pack, beside=done)
-    attn_send, attn_keep, grads, qkv_bias_sums, qkv_send, qkv_keep = attention_backward(
-        ids,
-        info,
-        tables,
-        context,
-        dq,
-        dk,
-        dv,
-        sent,
-        grad,
-        gain_attn,
-        shift_attn,
-        qkv_pack,
-        dense_pack,
-        fc_bits,
-    )
-    attn_parts = Halving(attn_send, attn_keep, "tensor", tensor_bits)
-    qkv_parts = Halving(qkv_send, qkv_keep, "dp", fc_bits)
+    attn_parts = Halving(
+        *project_context(ids, context, dense_pack, groups, model), "tensor", tensor_bits
+    )
     attn_parts.most()
-    sent.arrays[0], attn_parts.send = tie(sent.arrays[0], attn_parts.send)
+    context, attn_parts.send = tie(context, attn_parts.send)
     attn_parts.swap()
-    qkv_parts.swap()
-    done = mlp_forward(
+    done = mlp(
         ids,
         sent,
         grad,
+        context,
         gain_mlp,
         shift_mlp,
         fc_pack,
         fc_bias_own,
         out_pack,
-        halving_order(fc_bits),
-    )
-    done = tie_halves(done, attn_parts, qkv_parts)
-    active, slope, mlp_send, mlp_keep, out_send, out_keep = done
+        [halving_order(near_bits), halving_order(next_bits)],
+    )
+    done = tie_halves(done, attn_parts)
+    mlp_send, mlp_keep, hidden, fc_bias_sums, *stacks = done
     attn_parts.add()
-    qkv_parts.add()
     mlp_parts = Halving(mlp_send, mlp_keep, "tensor", tensor_bits)
+    mlp_sums = [
+        Halving(*stacks[:2], "dp", near_bits),
+        Halving(*stacks[2:], "dp", next_bits),
+    ]
     mlp_parts.most()
-    slope, mlp_parts.send, qkv_parts.send = tie(slope, mlp_parts.send, qkv_parts.send)
-    out_parts = Halving(out_send, out_keep, "dp", fc_bits)
+    hidden, mlp_parts.send = tie(hidden, mlp_parts.send)
     mlp_parts.swap()
-    out_parts.swap()
-    qkv_parts.swap()
-    done = hidden_backward(
+    for parts in mlp_sums:
+        parts.swap()
+    done = norm_backward(
         ids,
+        info,
+        tables,
         sent,
-        grad,
-        slope,
+        dq,
+        dk,
+        dv,
+        hidden,
+        gain_attn,
+        shift_attn,
         gain_mlp,
-        shift_mlp,
+        qkv_pack,
         fc_pack,
-        out_pack,
-        [halving_order(fc_bits), halving_order(out_bits)],
-    )
-    hidden, fc_bias_sums, *halves = tie_halves(done, qkv_parts)
-    qkv_parts.add()
-    hidden, qkv_parts.send = tie(hidden, qkv_parts.send)
-    low_parts = Halving(*halves[:2], "dp", fc_bits)
-    high_parts = Halving(*halves[2:], "dp", out_bits)
-    low_parts.swap()
-    high_parts.swap()
-    qkv_parts.swap()
-    done = norm_backward(ids, sent, grads, hidden, gain_attn, gain_mlp, qkv_pack, fc_pack)
-    back_send, back_keep, norm_sums = tie_halves(
-        done, mlp_parts, out_parts, qkv_parts, low_parts, high_parts
-    )
+        [halving_order(near_bits), halving_order(next_bits)],
+    )
+    done = tie_halves(done, mlp_parts, *mlp_sums)
+    back_send, back_keep, norm_sums, qkv_bias_sums, *stacks = done
+    qkv_sums = [
+        Halving(*stacks[:2], "dp", near_bits),
+        Halving(*stacks[2:], "dp", next_bits),
+    ]
     mlp_parts.add()
-    for parts in (out_parts, qkv_parts, low_parts, high_parts):
+    for parts in mlp_sums:
         parts.add()
 
     back_parts = Halving(back_send, back_keep, "tensor", tensor_bits)
@@ -1032,30 +1020,30 @@
     steps = [(axis, bit) for axis in ("tensor", "dp") for bit in bits_of(lax.axis_size(axis))]
     chunks = jnp.split(back_parts.send, 4, axis=1)
     sums = sums + swap(sums, *steps[0])
-    for parts in (out_parts, low_parts, high_parts):
+    for parts in mlp_sums + qkv_sums:
         parts.swap()
     got = []
     for at, step in enumerate(steps[1:]):
         other = swap(sums, *step)
-        if at == 1:
-            (other,) = tie_halves([other], out_parts, low_parts, high_parts)
-        if 1 <= at <= len(chunks):
-            other, got[-1] = tie(other, got[-1])
         if at < len(chunks):
-            sums, chunk = tie(sums, chunks[at])
-            got.append(swap(chunk, "tensor", back_parts.bits[-1]))
+            got.append(swap(chunks[at], "tensor", back_parts.bits[-1]))
+            other, got[-1], *chunks[at + 1 :] = tie(other, got[-1], *chunks[at + 1 :])
+        if at == 2:
+            (other,) = tie_halves([other], *mlp_sums, *qkv_sums)
         sums = sums + other
-    for parts in (out_parts, low_parts, high_parts):
+    for parts in mlp_sums + qkv_sums:
         parts.add()
     stream_grad = finish_grad(
-        out_grad, normalized, inv_std, [x[0] for x in back_parts.terms], [x[0] for x in got]
-    )
-
-    out_weight_grad = out_parts.finish().T
-    attn_total = qkv_parts.finish()
-    dense_weight_grad = attn_total[:, 3 * width :].T
-    qkv_weight_grad = by_head(attn_total[:, : 3 * width], heads)
-    fc_weight_grad = jnp.concatenate([low_parts.finish(), high_parts.finish()], axis=1)
+        out_grad, normalized, inv_std, back_parts.terms, [x[0] for x in got]
+    )
+
+    first, second = [parts.finish() for parts in mlp_sums]
+    half = units // 2
+    fc_weight_grad = jnp.concatenate([first[:, :half], second[:, :half]], axis=1)
+    out_weight_grad = jnp.concatenate([first[:, half:units], second[:, half:]], axis=1).T
+    dense_weight_grad = first[:, units:].T
+    total = jnp.concatenate([parts.finish() for parts in qkv_sums], axis=1)
+    qkv_weight_grad = by_head(total, heads)
 
     count_all = float(rows_local * lax.axis_size("dp") * groups * model)
     gain_attn_grad, shift_attn_grad, gain_mlp_grad, shift_mlp_grad = sums[: 4 * model].reshape(

time: 383 us -> 381 us (level)
  waiting for transfers between devices: 63.4 us -> 99.4 us
  Pallas kernels: 190 us -> 166 us
  local copies, waits for them, and re-layouts: 33.6 us -> 20.9 us
  other arithmetic: 44.2 us -> 38.6 us
  starting transfers between devices: 42.4 us -> 46.7 us
    ppermute x44, waiting for transfers between devices: 63.4 us -> 99.4 us  [swap(): return lax.ppermute(block, axis, [(i, i ^ bit) for i in range(size)])]
    pallas_call x9 -> x8, Pallas kernels: 190 us -> 166 us  [call(): pl.pallas_call(kernel, grid_spec=pltpu.PrefetchScalarGridSpec(num_scalar_...]
    squeeze x6 -> x0, local copies, waits for them, and re-layouts: 14.7 us -> none  [the longest x4 9.59 us: add(): self.terms = [x[0] for x in terms]]
    ppermute x44, starting transfers between devices: 42.4 us -> 46.7 us  [swap(): return lax.ppermute(block, axis, [(i, i ^ bit) for i in range(size)])]
    unnamed x106 -> x88, local copies, waits for them, and re-layouts: 7.51 us -> 7.99 us
  transfers between devices with their start and end apart: 44 -> 44, of which waited for: 12 -> 14; matrix products, arithmetic and copies ran while one was open for 18% -> 10% of each run, Pallas kernels for 43% -> 41%
where the time goes in v4:
time: 381 us; the launch traced here: 374 us
  Pallas kernels  166 us (44%)
  waiting for transfers between devices  99.4 us (26%)
  starting transfers between devices  46.7 us (12%)
  other arithmetic  38.6 us (10%)
  local copies, waits for them, and re-layouts  20.9 us (5%)
    pallas_call x8, Pallas kernels, call(): pl.pallas_call(kernel, grid_spec=pltpu.PrefetchScalarGridSpec(num_scalar_...  166 us
    ppermute x44, waiting for transfers between devices, swap(): return lax.ppermute(block, axis, [(i, i ^ bit) for i in range(size)])  99.4 us
    ppermute x44, starting transfers between devices, swap(): return lax.ppermute(block, axis, [(i, i ^ bit) for i in range(size)])  46.7 us
    convert_element_type x11, other arithmetic, add(): self.send = sum(sends).astype(bf16)  15.5 us
    unnamed x88, local copies, waits for them, and re-layouts  7.99 us
    concatenate x8, other arithmetic, double(): jnp.concatenate(self.arrays, axis=0)  7.74 us
  transfers between devices with their start and end apart: 44, of which 14 were waited for; matrix products, arithmetic and copies ran while one was open for 10% of the time, Pallas kernels for 41%

profile of v4, /device:TPU:0, one launch (start us, length us, event | category | flops | bytes accessed | tf_op | source)
XLA Modules:
  0.0 373.9 jit_solution(12378683215607297817)
XLA Ops:
  0.7 2.1 reduce_sum.49
  3.6 2.3 fusion.28
  6.0 3.0 collective-permute-start
  9.3 2.7 collective-permute-start.1
  12.1 1.6 collective-permute-start.3
  14.7 6.4 %collective-permute-done.2.refs_5_.refs_1_ = bf16[128,256]{1,0:T(8,128)(2,1)S(1)} collective-permute-done((bf16[128,256]{1,0:T(8,128)(2,1)S(1)}, bf16[128,256]{1,0:T(8,128)(2,1)S(1)}, u32[]{:S(2)}, u32[]{:S(2)}) %collective-permute-start.2) | collective-permute-done | bytes 65568 | tf_op jit(solution)/shard_map/ppermute | solution.py:46
  21.3 1.6 collective-permute-start.4
  23.5 2.2 collective-permute-start.6
  27.0 1.0 fusion.27
  28.1 15.2 %collective-permute-done.5.refs_6_.refs_2_ = bf16[256,256]{1,0:T(8,128)(2,1)S(1)} collective-permute-done((bf16[256,256]{1,0:T(8,128)(2,1)S(1)}, bf16[256,256]{1,0:T(8,128)(2,1)S(1)}, u32[]{:S(2)}, u32[]{:S(2)}) %collective-permute-start.5) | collective-permute-done | bytes 131104 | tf_op jit(solution)/shard_map/ppermute | solution.py:46
  46.4 1.9 pad_maximum_fusion.2
  48.3 1.5 collective-permute-start.9
  49.8 2.9 collective-permute-start.11
  53.3 4.0 %fusion.8 = (f32[1280,128]{1,0:T(8,128)}, f32[1280,128]{1,0:T(8,128)}, f32[1280,128]{1,0:T(8,128)}) fusion(s32[128]{0:T(128)S(1)} %copy-done.34, s32[128]{0:T(128)S(1)} %copy-done.35, pred[128]{0:T(512)(128)(4,1)S(1)} %compare_and_fusion, f32[1280]{0:T(1024)S(1)} %copy-done.29), kind=kLoop, calls=%fused_computation.30 | loop fusion | flops 3932160 | bytes 1972352 | tf_op jit(solution)/shard_map/jit(_where)/select_n | solution.py:832
  58.1 17.7 %collective-permute-done.11.refs_14_ = bf16[256,1024]{1,0:T(8,128)(2,1)S(1)} collective-permute-done((bf16[256,1024]{1,0:T(8,128)(2,1)S(1)}, bf16[256,1024]{1,0:T(8,128)(2,1)S(1)}, u32[]{:S(2)}, u32[]{:S(2)}) %collective-permute-start.11) | collective-permute-done | bytes 524320 | tf_op jit(solution)/shard_map/ppermute | solution.py:46
  79.5 0.8 copy.134.refs_4_
  80.3 11.4 %project_qkv.1 = (bf16[2560,256]{1,0:T(8,128)(2,1)}, bf16[2560,256]{1,0:T(8,128)(2,1)}, bf16[2560,256]{1,0:T(8,128)(2,1)}) custom-call(s32[6]{0:T(128)} %stack.19.ids, s32[1,20,5]{2,1,0:T(8,128)} %stack.20.info, bf16[640,1024]{1,0:T(8,128)(2,1)} %collective-permute-done.8.refs_0_, bf16[640,1024]{1,0:T(8,128)(2,1)} %collective-permute-done.7.refs_1_, ...), custom_call_target="tpu_custom_call" | custom-call | flops 4026531840 | bytes 12725248 | tf_op jit(solution)/shard_map/project_qkv/pallas_call | solution.py:221
  92.4 2.1 pad_maximum_fusion.1
  94.5 2.0 collective-permute-start.17
  96.5 2.1 pad_maximum_fusion
  99.1 6.2 %project_grad.1.do_ref = bf16[2560,256]{1,0:T(8,128)(2,1)} custom-call(s32[6]{0:T(128)} %stack.19.ids, bf16[640,1024]{1,0:T(8,128)(2,1)} %collective-permute-done.14.refs_0_.refs_4_, bf16[640,1024]{1,0:T(8,128)(2,1)} %collective-permute-done.15.refs_1_.refs_5_, bf16[640,1024]{1,0:T(8,128)(2,1)} %collective-permute-done.12.refs_2_.refs_6_, ...), custom_call_target="tpu_custom_call" | custom-call | flops 1342177280 | bytes 7077888 | tf_op jit(solution)/shard_map/project_grad/pallas_call | solution.py:221
  105.3 55.3 %attention.1 = (bf16[2560,256]{1,0:T(8,128)(2,1)}, bf16[2560,256]{1,0:T(8,128)(2,1)}, bf16[2560,256]{1,0:T(8,128)(2,1)}, bf16[2560,256]{1,0:T(8,128)(2,1)}) custom-call(s32[1,20,5]{2,1,0:T(8,128)} %stack.20.info, bf16[2560,256]{1,0:T(8,128)(2,1)} %get-tuple-element.176.q_ref, bf16[2560,256]{1,0:T(8,128)(2,1)} %project_grad.1.do_ref, ...), custom_call_target="tpu_custom_call" | custom-call | flops 31406948352 | bytes 12451840 | tf_op jit(solution)/shard_map/attention/pallas_call | solution.py:221
  160.7 7.6 %project_context.1 = (bf16[2,640,1024]{2,1,0:T(8,128)(2,1)}, bf16[2,640,1024]{2,1,0:T(8,128)(2,1)}) custom-call(s32[6]{0:T(128)} %stack.19.ids, bf16[2560,256]{1,0:T(8,128)(2,1)} %get-tuple-element.198.ctx.ctx_ref, bf16[128,256]{1,0:T(8,128)(2,1)} %bitcast.68, bf16[128,256]{1,0:T(8,128)(2,1)} %copy-done.14, bf16[256,256]{1,0:T(8,128)(2,1)} %copy-done.15, ...), custom_call_target="tpu_custom_call" | custom-call | flops 1342177280 | bytes 7077888 | tf_op jit(solution)/shard_map/project_context/pallas_call | solution.py:221
  168.4 1.3 dynamic_slice.7
  169.7 3.8 %collective-permute-done.18.refs_1_ = bf16[2,640,1024]{2,1,0:T(8,128)(2,1)S(1)} collective-permute-done((bf16[2,640,1024]{2,1,0:T(8,128)(2,1)}, bf16[2,640,1024]{2,1,0:T(8,128)(2,1)S(1)}, u32[]{:S(2)}, u32[]{:S(2)}) %collective-permute-start.18) | collective-permute-done | bytes 2621472 | tf_op jit(solution)/shard_map/ppermute | solution.py:46
  173.5 3.8 %add_convert_fusion.2 = bf16[1,640,1024]{2,1,0:T(8,128)(2,1)} fusion(bf16[2,640,1024]{2,1,0:T(8,128)(2,1)S(1)} %collective-permute-done.18.refs_1_, bf16[2,640,1024]{2,1,0:T(8,128)(2,1)} %get-tuple-element.196.refs_0_), kind=kLoop, calls=%fused_computation.3 | loop fusion | flops 2621440 | bytes 3932160 | tf_op jit(solution)/shard_map/convert_element_type | solution.py:122
  177.9 44.9 %mlp.1 = (bf16[2,640,1024]{2,1,0:T(8,128)(2,1)}, bf16[2,640,1024]{2,1,0:T(8,128)(2,1)}, bf16[2560,1024]{1,0:T(8,128)(2,1)}, f32[8,1024]{1,0:T(8,128)}, bf16[4,12...) custom-call(s32[6]{0:T(128)} %stack.19.ids, ...), custom_call_target="tpu_custom_call" | custom-call | flops 26843545600 | bytes 31240192 | tf_op jit(solution)/shard_map/mlp/pallas_call | solution.py:221
  222.9 1.6 collective-permute-start.22
  224.5 3.5 collective-permute-done.20.refs_4_
  228.0 3.9 %add_convert_fusion.1 = bf16[1,640,1024]{2,1,0:T(8,128)(2,1)} fusion(bf16[2,640,1024]{2,1,0:T(8,128)(2,1)S(1)} %collective-permute-done.20.refs_4_, bf16[2,640,1024]{2,1,0:T(8,128)(2,1)} %get-tuple-element.217.refs_3_), kind=kLoop, calls=%fused_computation.2 | loop fusion | flops 2621440 | bytes 3932160 | tf_op jit(solution)/shard_map/convert_element_type | solution.py:122
  231.9 1.5 collective-permute-start.21
  233.4 27.3 %norm_backward.1 = (bf16[2,640,1024]{2,1,0:T(8,128)(2,1)}, bf16[2,640,1024]{2,1,0:T(8,128)(2,1)}, f32[8,1024]{1,0:T(8,128)}, f32[8,768]{1,0:T(8,128)}, bf16[4,12...) custom-call(s32[6]{0:T(128)} %stack.19.ids, ...), custom_call_target="tpu_custom_call" | custom-call | flops 13421772800 | bytes 26939392 | tf_op jit(solution)/shard_map/norm_backward/pallas_call | solution.py:221
  260.7 2.3 collective-permute-done.21.refs_5_
  265.4 7.4 %finish_output.1 = (f32[640,1024]{1,0:T(8,128)}, f32[8,1024]{1,0:T(8,128)}) custom-call(f32[640,1024]{1,0:T(8,128)} %stream_ref.1, bf16[2,640,1024]{2,1,0:T(8,128)(2,1)} %get-tuple-element.196.refs_0_, bf16[2,640,1024]{2,1,0:T(8,128)(2,1)} %copy-done.3, bf16[1,640,1024]{2,1,0:T(8,128)(2,1)} %collective-permute-done.19.refs_2_, ...), custom_call_target="tpu_custom_call" | custom-call | flops 10485760 | bytes 18391040 | tf_op jit(solution)/shard_map/finish_output/pallas_call | solution.py:221
  274.2 2.2 add_convert_fusion
  277.2 1.5 collective-permute-start.27
  279.4 1.2 add_convert_fusion.3
  280.7 7.5 %collective-permute-done.26 = f32[15360]{0:T(1024)S(1)} collective-permute-done((f32[15360]{0:T(1024)S(1)}, f32[15360]{0:T(1024)S(1)}, u32[]{:S(2)}, u32[]{:S(2)}) %collective-permute-start.26) | collective-permute-done | bytes 61472 | tf_op jit(solution)/shard_map/ppermute | solution.py:46
  288.9 1.5 collective-permute-start.29
  290.4 1.2 add_convert_fusion.4
  291.7 1.6 collective-permute-start.33
  293.9 1.5 collective-permute-start.34
  295.4 12.6 %collective-permute-done.28 = f32[15360]{0:T(1024)S(1)} collective-permute-done((f32[15360]{0:T(1024)S(1)}, f32[15360]{0:T(1024)S(1)}, u32[]{:S(2)}, u32[]{:S(2)}) %collective-permute-start.28) | collective-permute-done | bytes 61472 | tf_op jit(solution)/shard_map/ppermute | solution.py:46
  308.7 2.1 collective-permute-start.30
  310.8 5.6 %collective-permute-done.30 = f32[15360]{0:T(1024)S(1)} collective-permute-done((f32[15360]{0:T(1024)S(1)}, f32[15360]{0:T(1024)S(1)}, u32[]{:S(2)}, u32[]{:S(2)}) %collective-permute-start.30) | collective-permute-done | bytes 61472 | tf_op jit(solution)/shard_map/ppermute | solution.py:46
  316.9 0.9 rsqrt.7.std_ref
  317.8 5.7 %collective-permute-done.31 = bf16[1,160,1024]{2,1,0:T(8,128)(2,1)S(1)} collective-permute-done((bf16[1,160,1024]{2,1,0:T(8,128)(2,1)S(1)}, bf16[1,160,1024]{2,1,0:T(8,128)(2,1)S(1)}, u32[]{:S(2)}, u32[]{:S(2)}) %collective-permute-start.31) | collective-permute-done | bytes 327712 | tf_op jit(solution)/shard_map/ppermute | solution.py:46
  324.2 1.1 add_convert_fusion.6
  325.3 1.0 collective-permute-start.43
  326.3 1.8 add_convert_fusion.5
  328.1 2.0 collective-permute-start.42
  330.4 1.6 collective-permute-start.40
  332.0 2.7 collective-permute-start.36
  334.7 5.2 %collective-permute-done.38 = bf16[2,128,384]{2,1,0:T(8,128)(2,1)S(1)} collective-permute-done((bf16[2,128,384]{2,1,0:T(8,128)(2,1)S(1)}, bf16[2,128,384]{2,1,0:T(8,128)(2,1)S(1)}, u32[]{:S(2)}, u32[]{:S(2)}) %collective-permute-start.38) | collective-permute-done | bytes 196640 | tf_op jit(solution)/shard_map/ppermute | solution.py:46
  340.3 3.4 collective-permute-start.39
  343.7 1.0 collective-permute-done.43
  344.8 1.1 add_bitcast_fusion.1
  345.9 11.9 %collective-permute-done.39 = bf16[1,128,384]{2,1,0:T(8,128)(2,1)S(1)} collective-permute-done((bf16[1,128,384]{2,1,0:T(8,128)(2,1)S(1)}, bf16[1,128,384]{2,1,0:T(8,128)(2,1)S(1)}, u32[]{:S(2)}, u32[]{:S(2)}) %collective-permute-start.39) | collective-permute-done | bytes 98336 | tf_op jit(solution)/shard_map/ppermute | solution.py:46
  357.9 1.0 collective-permute-done.41
  359.2 0.9 copy.140
  360.1 1.2 add_bitcast_fusion
  363.3 1.0 copy.142
  365.7 0.8 pad_maximum_fusion.5
  366.5 6.3 %finish_grad.1 = f32[640,1024]{1,0:T(8,128)} custom-call(bf16[640,1024]{1,0:T(8,128)(2,1)} %grad_ref, f32[640,1024]{1,0:T(8,128)} %get-tuple-element.364.norm_ref, f32[640,1]{1,0:T(8,128)} %rsqrt.7.std_ref, bf16[2,640,1024]{2,1,0:T(8,128)(2,1)} %get-tuple-element.240.refs_0_, bf16[2,640,1024]{2,1,0:T(8,128)(2,1)} %collective-permute-done.24.refs_1_, ...), custom_call_target="tpu_custom_call" | custom-call | flops 7864320 | bytes 13109760 | tf_op jit(solution)/shard_map/finish_grad/pallas_call | solution.py:221
  (205 shorter events, 27.9 us)
Async XLA Ops:
  5.9 8.6 %copy-start.31 = (s32[2560]{0:T(1024)S(1)}, s32[2560]{0:T(1024)}, u32[]{:S(2)}) copy-start(s32[2560]{0:T(1024)} %param.18) | copy-start | bytes 30724
  6.0 8.7 %copy-start.17 = (f32[128,1024]{1,0:T(8,128)S(1)}, f32[128,1024]{1,0:T(8,128)}, u32[]{:S(2)}) copy-start(f32[128,1024]{1,0:T(8,128)} %param.27) | copy-start | bytes 1572868
  6.0 37.3 %collective-permute-start = (bf16[640,1024]{1,0:T(8,128)(2,1)}, bf16[640,1024]{1,0:T(8,128)(2,1)}, u32[]{:S(2)}, u32[]{:S(2)}) collective-permute-start(bf16[640,1024]{1,0:T(8,128)(2,1)} %get-tuple-element.165.refs_3_), channel_id=1, source_target_pairs={{0,2},{1,3},{2,0},{3,1},{4,6},{5,7},{6,4},{7,5},{8,10},{9,11},{10,... | collective-permute-start | bytes 3932168 | tf_op jit(solution)/shard_map/ppermute | solution.py:46
  9.3 11.8 %collective-permute-start.1 = (bf16[128,768]{1,0:T(8,128)(2,1)S(1)}, bf16[128,768]{1,0:T(8,128)(2,1)S(1)}, u32[]{:S(2)}, u32[]{:S(2)}) collective-permute-start(bf16[128,768]{1,0:T(8,128)(2,1)S(1)} %copy.128), channel_id=1, source_target_pairs={{0,16},{4,20},{8,24},{12,28},{16,0},{20,4},{24,8},{28,12},{1,17},{... | collective-permute-start | bytes 589832 | tf_op jit(solution)/shard_map/ppermute | solution.py:46
  12.1 80.3 %copy-start.6 = (bf16[1024,128]{0,1:T(8,128)(2,1)}, bf16[1024,128]{0,1:T(8,128)(2,1)S(1)}, u32[]{:S(2)}) copy-start(bf16[1024,128]{0,1:T(8,128)(2,1)S(1)} %copy.130) | copy-start | bytes 786436
  12.1 9.0 %collective-permute-start.3 = (bf16[128,1024]{1,0:T(8,128)(2,1)S(1)}, bf16[128,1024]{1,0:T(8,128)(2,1)S(1)}, u32[]{:S(2)}, u32[]{:S(2)}) collective-permute-start(bf16[128,1024]{1,0:T(8,128)(2,1)S(1)} %bitcast.58), channel_id=1, source_target_pairs={{0,4},{4,0},{8,12},{12,8},{16,20},{20,16},{24,28},{28,24},{1,5},{5... | collective-permute-start | bytes 786440 | tf_op jit(solution)/shard_map/ppermute | solution.py:46
  13.8 32.5 %copy-start.8 = (bf16[256,128]{0,1:T(8,128)(2,1)}, bf16[256,128]{0,1:T(8,128)(2,1)S(1)}, u32[]{:S(2)}) copy-start(bf16[256,128]{0,1:T(8,128)(2,1)S(1)} %copy.129) | copy-start | bytes 196612
  13.8 7.3 %collective-permute-start.2 = (bf16[128,256]{1,0:T(8,128)(2,1)S(1)}, bf16[128,256]{1,0:T(8,128)(2,1)S(1)}, u32[]{:S(2)}, u32[]{:S(2)}) collective-permute-start(bf16[128,256]{1,0:T(8,128)(2,1)S(1)} %bitcast.64), channel_id=1, source_target_pairs={{0,4},{4,0},{8,12},{12,8},{16,20},{20,16},{24,28},{28,24},{1,5},{5... | collective-permute-start | bytes 196616 | tf_op jit(solution)/shard_map/ppermute | solution.py:46
  14.7 81.8 %copy-start.5 = (bf16[128,1024]{1,0:T(8,128)(2,1)}, bf16[128,1024]{1,0:T(8,128)(2,1)S(1)}, u32[]{:S(2)}) copy-start(bf16[128,1024]{1,0:T(8,128)(2,1)S(1)} %convert_element_type.235.refs_8_) | copy-start | bytes 786436
  21.1 24.4 %copy-start.14 = (bf16[128,256]{1,0:T(8,128)(2,1)}, bf16[128,256]{1,0:T(8,128)(2,1)S(1)}, u32[]{:S(2)}) copy-start(bf16[128,256]{1,0:T(8,128)(2,1)S(1)} %collective-permute-done.2.refs_5_.refs_1_) | copy-start | bytes 196612
  21.1 27.2 %copy-start.13 = (bf16[128,768]{1,0:T(8,128)(2,1)}, bf16[128,768]{1,0:T(8,128)(2,1)S(1)}, u32[]{:S(2)}) copy-start(bf16[128,768]{1,0:T(8,128)(2,1)S(1)} %collective-permute-done.1.refs_5_) | copy-start | bytes 589828
  21.1 28.7 %copy-start.12 = (bf16[128,1024]{1,0:T(8,128)(2,1)}, bf16[128,1024]{1,0:T(8,128)(2,1)S(1)}, u32[]{:S(2)}) copy-start(bf16[128,1024]{1,0:T(8,128)(2,1)S(1)} %collective-permute-done.3.refs_13_) | copy-start | bytes 786436
  21.3 22.0 %collective-permute-start.4 = (bf16[256,768]{1,0:T(8,128)(2,1)S(1)}, bf16[256,768]{1,0:T(8,128)(2,1)S(1)}, u32[]{:S(2)}, u32[]{:S(2)}) collective-permute-start(bf16[256,768]{1,0:T(8,128)(2,1)S(1)} %pad_maximum_fusion.6), channel_id=1, source_target_pairs={{0,8},{4,12},{8,0},{12,4},{16,24},{20,28},{24,16},{28,20},{1,9},{5... | collective-permute-start | bytes 1179656 | tf_op jit(solution)/shard_map/ppermute | solution.py:46
  23.5 19.7 %collective-permute-start.6 = (bf16[128,1024]{1,0:T(8,128)(2,1)S(1)}, bf16[128,1024]{1,0:T(8,128)(2,1)S(1)}, u32[]{:S(2)}, u32[]{:S(2)}) collective-permute-start(bf16[128,1024]{1,0:T(8,128)(2,1)S(1)} %convert_element_type.235.refs_8_), channel_id=1, source_target_pairs={{0,16},{4,20},{8,24},{12,28},{16,0},{20,4},{24,8},{28,12},{1,17},{... | collective-permute-start | bytes 786440 | tf_op jit(solution)/shard_map/ppermute | solution.py:46
  25.8 17.5 %collective-permute-start.5 = (bf16[256,256]{1,0:T(8,128)(2,1)S(1)}, bf16[256,256]{1,0:T(8,128)(2,1)S(1)}, u32[]{:S(2)}, u32[]{:S(2)}) collective-permute-start(bf16[256,256]{1,0:T(8,128)(2,1)S(1)} %pad_maximum_fusion.9), channel_id=1, source_target_pairs={{0,16},{4,20},{8,24},{12,28},{16,0},{20,4},{24,8},{28,12},{1,17},{... | collective-permute-start | bytes 393224 | tf_op jit(solution)/shard_map/ppermute | solution.py:46
  43.3 14.0 %copy-start.10 = (bf16[128,1024]{1,0:T(8,128)(2,1)}, bf16[128,1024]{1,0:T(8,128)(2,1)S(1)}, u32[]{:S(2)}) copy-start(bf16[128,1024]{1,0:T(8,128)(2,1)S(1)} %collective-permute-done.6.refs_9_) | copy-start | bytes 786436
  44.8 8.5 %copy-start.29 = (f32[1280]{0:T(1024)S(1)}, f32[1280]{0:T(1024)}, u32[]{:S(2)}) copy-start(f32[1280]{0:T(1024)} %iota_convert_fusion) | copy-start | bytes 15364
  44.8 8.5 %copy-start.34 = (s32[128]{0:T(128)S(1)}, s32[128]{0:T(128)}, u32[]{:S(2)}) copy-start(s32[128]{0:T(128)} %get-tuple-element.390) | copy-start | bytes 1540
  44.8 8.5 %copy-start.35 = (s32[128]{0:T(128)S(1)}, s32[128]{0:T(128)}, u32[]{:S(2)}) copy-start(s32[128]{0:T(128)} %get-tuple-element.391) | copy-start | bytes 1540
  44.8 8.0 %collective-permute-start.10 = (bf16[512,256]{1,0:T(8,128)(2,1)}, bf16[512,256]{1,0:T(8,128)(2,1)}, u32[]{:S(2)}, u32[]{:S(2)}) collective-permute-start(bf16[512,256]{1,0:T(8,128)(2,1)} %pad_maximum_fusion.8), channel_id=1, source_target_pairs={{0,8},{4,12},{8,0},{12,4},{16,24},{20,28},{24,16},{28,20},{1,9},{5... | collective-permute-start | bytes 786440 | tf_op jit(solution)/shard_map/ppermute | solution.py:46
  44.9 34.6 %collective-permute-start.7 = (bf16[640,1024]{1,0:T(8,128)(2,1)}, bf16[640,1024]{1,0:T(8,128)(2,1)}, u32[]{:S(2)}, u32[]{:S(2)}) collective-permute-start(bf16[640,1024]{1,0:T(8,128)(2,1)} %get-tuple-element.165.refs_3_), channel_id=1, source_target_pairs={{0,1},{1,0},{2,3},{3,2},{4,5},{5,4},{6,7},{7,6},{8,9},{9,8},{10,11... | collective-permute-start | bytes 3932168 | tf_op jit(solution)/shard_map/ppermute | solution.py:46
  44.9 34.5 %collective-permute-start.8 = (bf16[640,1024]{1,0:T(8,128)(2,1)}, bf16[640,1024]{1,0:T(8,128)(2,1)}, u32[]{:S(2)}, u32[]{:S(2)}) collective-permute-start(bf16[640,1024]{1,0:T(8,128)(2,1)} %collective-permute-done.refs_2_), channel_id=1, source_target_pairs={{0,1},{1,0},{2,3},{3,2},{4,5},{5,4},{6,7},{7,6},{8,9},{9,8},{10,11... | collective-permute-start | bytes 3932168 | tf_op jit(solution)/shard_map/ppermute | solution.py:46
  48.3 31.2 %collective-permute-start.9 = (bf16[512,768]{1,0:T(8,128)(2,1)}, bf16[512,768]{1,0:T(8,128)(2,1)}, u32[]{:S(2)}, u32[]{:S(2)}) collective-permute-start(bf16[512,768]{1,0:T(8,128)(2,1)} %pad_maximum_fusion.2), channel_id=1, source_target_pairs={{0,4},{4,0},{8,12},{12,8},{16,20},{20,16},{24,28},{28,24},{1,5},{5... | collective-permute-start | bytes 2359304 | tf_op jit(solution)/shard_map/ppermute | solution.py:46
  49.8 26.0 %collective-permute-start.11 = (bf16[256,1024]{1,0:T(8,128)(2,1)S(1)}, bf16[256,1024]{1,0:T(8,128)(2,1)S(1)}, u32[]{:S(2)}, u32[]{:S(2)}) collective-permute-start(bf16[256,1024]{1,0:T(8,128)(2,1)S(1)} %pad_maximum_fusion.3), channel_id=1, source_target_pairs={{0,16},{4,20},{8,24},{12,28},{16,0},{20,4},{24,8},{28,12},{1,17},{... | collective-permute-start | bytes 1572872 | tf_op jit(solution)/shard_map/ppermute | solution.py:46
  52.8 39.0 %collective-permute-start.12 = (bf16[640,1024]{1,0:T(8,128)(2,1)S(1)}, bf16[640,1024]{1,0:T(8,128)(2,1)}, u32[]{:S(2)}, u32[]{:S(2)}) collective-permute-start(bf16[640,1024]{1,0:T(8,128)(2,1)S(1)} %copy-done.1), channel_id=1, source_target_pairs={{0,2},{1,3},{2,0},{3,1},{4,6},{5,7},{6,4},{7,5},{8,10},{9,11},{10,... | collective-permute-start | bytes 3932168 | tf_op jit(solution)/shard_map/ppermute | solution.py:46
  76.6 15.2 %collective-permute-start.13 = (bf16[256,1024]{1,0:T(8,128)(2,1)}, bf16[256,1024]{1,0:T(8,128)(2,1)}, u32[]{:S(2)}, u32[]{:S(2)}) collective-permute-start(bf16[256,1024]{1,0:T(8,128)(2,1)} %pad_maximum_fusion.4), channel_id=1, source_target_pairs={{0,8},{4,12},{8,0},{12,4},{16,24},{20,28},{24,16},{28,20},{1,9},{5... | collective-permute-start | bytes 1572872 | tf_op jit(solution)/shard_map/ppermute | solution.py:46
  91.8 7.3 %collective-permute-start.14 = (bf16[640,1024]{1,0:T(8,128)(2,1)}, bf16[640,1024]{1,0:T(8,128)(2,1)}, u32[]{:S(2)}, u32[]{:S(2)}) collective-permute-start(bf16[640,1024]{1,0:T(8,128)(2,1)} %collective-permute-done.12.refs_2_.refs_6_), channel_id=1, source_target_pairs={{0,1},{1,0},{2,3},{3,2},{4,5},{5,4},{6,7},{7,6},{8,9},{9,8},{10,11... | collective-permute-start | bytes 3932168 | tf_op jit(solution)/shard_map/ppermute | solution.py:46
  91.9 7.2 %collective-permute-start.15 = (bf16[640,1024]{1,0:T(8,128)(2,1)S(1)}, bf16[640,1024]{1,0:T(8,128)(2,1)}, u32[]{:S(2)}, u32[]{:S(2)}) collective-permute-start(bf16[640,1024]{1,0:T(8,128)(2,1)S(1)} %copy-done.1), channel_id=1, source_target_pairs={{0,1},{1,0},{2,3},{3,2},{4,5},{5,4},{6,7},{7,6},{8,9},{9,8},{10,11... | collective-permute-start | bytes 3932168 | tf_op jit(solution)/shard_map/ppermute | solution.py:46
  94.5 66.2 %collective-permute-start.17 = (bf16[512,1024]{1,0:T(8,128)(2,1)}, bf16[512,1024]{1,0:T(8,128)(2,1)}, u32[]{:S(2)}, u32[]{:S(2)}) collective-permute-start(bf16[512,1024]{1,0:T(8,128)(2,1)} %pad_maximum_fusion.1), channel_id=1, source_target_pairs={{0,8},{4,12},{8,0},{12,4},{16,24},{20,28},{24,16},{28,20},{1,9},{5... | collective-permute-start | bytes 3145736 | tf_op jit(solution)/shard_map/ppermute | solution.py:46
  98.6 62.1 %collective-permute-start.16 = (bf16[512,1024]{1,0:T(8,128)(2,1)}, bf16[512,1024]{1,0:T(8,128)(2,1)}, u32[]{:S(2)}, u32[]{:S(2)}) collective-permute-start(bf16[512,1024]{1,0:T(8,128)(2,1)} %pad_maximum_fusion), channel_id=1, source_target_pairs={{0,4},{4,0},{8,12},{12,8},{16,20},{20,16},{24,28},{28,24},{1,5},{5... | collective-permute-start | bytes 3145736 | tf_op jit(solution)/shard_map/ppermute | solution.py:46
  168.3 5.2 %collective-permute-start.18 = (bf16[2,640,1024]{2,1,0:T(8,128)(2,1)}, bf16[2,640,1024]{2,1,0:T(8,128)(2,1)S(1)}, u32[]{:S(2)}, u32[]{:S(2)}) collective-permute-start(bf16[2,640,1024]{2,1,0:T(8,128)(2,1)} %get-tuple-element.197), channel_id=1, source_target_pairs={{0,1},{1,0},{2,3},{3,2},{4,5},{5,4},{6,7},{7,6},{8,9},{9,8},{10,11... | collective-permute-start | bytes 7864328 | tf_op jit(solution)/shard_map/ppermute | solution.py:46
  177.4 45.5 %collective-permute-start.19 = (bf16[1,640,1024]{2,1,0:T(8,128)(2,1)}, bf16[1,640,1024]{2,1,0:T(8,128)(2,1)}, u32[]{:S(2)}, u32[]{:S(2)}) collective-permute-start(bf16[1,640,1024]{2,1,0:T(8,128)(2,1)} %add_convert_fusion.2), channel_id=1, source_target_pairs={{0,2},{1,3},{2,0},{3,1},{4,6},{5,7},{6,4},{7,5},{8,10},{9,11},{10,... | collective-permute-start | bytes 3932168 | tf_op jit(solution)/shard_map/ppermute | solution.py:46
  222.8 5.2 %collective-permute-start.20 = (bf16[2,640,1024]{2,1,0:T(8,128)(2,1)}, bf16[2,640,1024]{2,1,0:T(8,128)(2,1)S(1)}, u32[]{:S(2)}, u32[]{:S(2)}) collective-permute-start(bf16[2,640,1024]{2,1,0:T(8,128)(2,1)} %get-tuple-element.218), channel_id=1, source_target_pairs={{0,1},{1,0},{2,3},{3,2},{4,5},{5,4},{6,7},{7,6},{8,9},{9,8},{10,11... | collective-permute-start | bytes 7864328 | tf_op jit(solution)/shard_map/ppermute | solution.py:46
  222.9 37.8 %collective-permute-start.22 = (bf16[4,128,1280]{2,1,0:T(8,128)(2,1)}, bf16[4,128,1280]{2,1,0:T(8,128)(2,1)}, u32[]{:S(2)}, u32[]{:S(2)}) collective-permute-start(bf16[4,128,1280]{2,1,0:T(8,128)(2,1)} %get-tuple-element.233), channel_id=1, source_target_pairs={{0,4},{4,0},{8,12},{12,8},{16,20},{20,16},{24,28},{28,24},{1,5},{5... | collective-permute-start | bytes 3932168 | tf_op jit(solution)/shard_map/ppermute | solution.py:46
  231.9 31.1 %copy-start.2 = (bf16[640,1024]{1,0:T(8,128)(2,1)S(1)}, bf16[640,1024]{1,0:T(8,128)(2,1)}, u32[]{:S(2)}) copy-start(bf16[640,1024]{1,0:T(8,128)(2,1)} %grad_ref) | copy-start | bytes 3932164
  231.9 31.1 %collective-permute-start.21 = (bf16[1,640,1024]{2,1,0:T(8,128)(2,1)}, bf16[1,640,1024]{2,1,0:T(8,128)(2,1)}, u32[]{:S(2)}, u32[]{:S(2)}) collective-permute-start(bf16[1,640,1024]{2,1,0:T(8,128)(2,1)} %add_convert_fusion.1), channel_id=1, source_target_pairs={{0,2},{1,3},{2,0},{3,1},{4,6},{5,7},{6,4},{7,5},{8,10},{9,11},{10,... | collective-permute-start | bytes 3932168 | tf_op jit(solution)/shard_map/ppermute | solution.py:46
  233.4 27.3 %collective-permute-start.23 = (bf16[4,128,1024]{2,1,0:T(8,128)(2,1)}, bf16[4,128,1024]{2,1,0:T(8,128)(2,1)}, u32[]{:S(2)}, u32[]{:S(2)}) collective-permute-start(bf16[4,128,1024]{2,1,0:T(8,128)(2,1)} %get-tuple-element.234), channel_id=1, source_target_pairs={{0,8},{4,12},{8,0},{12,4},{16,24},{20,28},{24,16},{28,20},{1,9},{5... | collective-permute-start | bytes 3145736 | tf_op jit(solution)/shard_map/ppermute | solution.py:46
  263.0 9.8 %collective-permute-start.24 = (bf16[2,640,1024]{2,1,0:T(8,128)(2,1)}, bf16[2,640,1024]{2,1,0:T(8,128)(2,1)}, u32[]{:S(2)}, u32[]{:S(2)}) collective-permute-start(bf16[2,640,1024]{2,1,0:T(8,128)(2,1)} %get-tuple-element.238), channel_id=1, source_target_pairs={{0,1},{1,0},{2,3},{3,2},{4,5},{5,4},{6,7},{7,6},{8,9},{9,8},{10,11... | collective-permute-start | bytes 7864328 | tf_op jit(solution)/shard_map/ppermute | solution.py:46
  273.6 5.1 %collective-permute-start.25 = (f32[15360]{0:T(1024)S(1)}, f32[15360]{0:T(1024)S(1)}, u32[]{:S(2)}, u32[]{:S(2)}) collective-permute-start(f32[15360]{0:T(1024)S(1)} %constant_dynamic-update-slice_fusion), channel_id=1, source_target_pairs={{0,1},{1,0},{2,3},{3,2},{4,5},{5,4},{6,7},{7,6},{8,9},{9,8},{10,11... | collective-permute-start | bytes 184328 | tf_op jit(solution)/shard_map/ppermute | solution.py:46
  277.2 13.2 %copy-start.9 = (bf16[4,128,1024]{2,1,0:T(8,128)(2,1)S(1)}, bf16[4,128,1024]{2,1,0:T(8,128)(2,1)}, u32[]{:S(2)}) copy-start(bf16[4,128,1024]{2,1,0:T(8,128)(2,1)} %get-tuple-element.259) | copy-start | bytes 3145732
  277.2 11.0 %collective-permute-start.27 = (bf16[1,160,1024]{2,1,0:T(8,128)(2,1)S(1)}, bf16[1,160,1024]{2,1,0:T(8,128)(2,1)S(1)}, u32[]{:S(2)}, u32[]{:S(2)}) collective-permute-start(bf16[1,160,1024]{2,1,0:T(8,128)(2,1)S(1)} %get-tuple-element.370), channel_id=1, source_target_pairs={{0,2},{1,3},{2,0},{3,1},{4,6},{5,7},{6,4},{7,5},{8,10},{9,11},{10,... | collective-permute-start | bytes 983048 | tf_op jit(solution)/shard_map/ppermute | solution.py:46
  278.7 15.2 %copy-start.37 = (bf16[4,128,384]{2,1,0:T(8,128)(2,1)S(1)}, bf16[4,128,384]{2,1,0:T(8,128)(2,1)}, u32[]{:S(2)}) copy-start(bf16[4,128,384]{2,1,0:T(8,128)(2,1)} %get-tuple-element.261) | copy-start | bytes 1179652
  278.7 29.2 %copy-start.36 = (bf16[4,128,384]{2,1,0:T(8,128)(2,1)S(1)}, bf16[4,128,384]{2,1,0:T(8,128)(2,1)}, u32[]{:S(2)}) copy-start(bf16[4,128,384]{2,1,0:T(8,128)(2,1)} %get-tuple-element.262) | copy-start | bytes 1179652
  278.7 38.2 %copy-start.28 = (f32[640]{0:T(1024)S(1)}, f32[640]{0:T(1024)}, u32[]{:S(2)}) copy-start(f32[640]{0:T(1024)} %copy-done.27) | copy-start | bytes 7684
  278.7 9.4 %collective-permute-start.26 = (f32[15360]{0:T(1024)S(1)}, f32[15360]{0:T(1024)S(1)}, u32[]{:S(2)}, u32[]{:S(2)}) collective-permute-start(f32[15360]{0:T(1024)S(1)} %add.242), channel_id=1, source_target_pairs={{0,2},{1,3},{2,0},{3,1},{4,6},{5,7},{6,4},{7,5},{8,10},{9,11},{10,... | collective-permute-start | bytes 184328 | tf_op jit(solution)/shard_map/ppermute | solution.py:46
  280.6 43.6 %collective-permute-start.32 = (bf16[2,128,1280]{2,1,0:T(8,128)(2,1)S(1)}, bf16[2,128,1280]{2,1,0:T(8,128)(2,1)S(1)}, u32[]{:S(2)}, u32[]{:S(2)}) collective-permute-start(bf16[2,128,1280]{2,1,0:T(8,128)(2,1)S(1)} %add_convert_fusion.3), channel_id=1, source_target_pairs={{0,8},{4,12},{8,0},{12,4},{16,24},{20,28},{24,16},{28,20},{1,9},{5... | collective-permute-start | bytes 1966088 | tf_op jit(solution)/shard_map/ppermute | solution.py:46
  288.9 19.0 %collective-permute-start.29 = (bf16[1,160,1024]{2,1,0:T(8,128)(2,1)S(1)}, bf16[1,160,1024]{2,1,0:T(8,128)(2,1)S(1)}, u32[]{:S(2)}, u32[]{:S(2)}) collective-permute-start(bf16[1,160,1024]{2,1,0:T(8,128)(2,1)S(1)} %get-tuple-element.248), channel_id=1, source_target_pairs={{0,2},{1,3},{2,0},{3,1},{4,6},{5,7},{6,4},{7,5},{8,10},{9,11},{10,... | collective-permute-start | bytes 983048 | tf_op jit(solution)/shard_map/ppermute | solution.py:46
  291.7 38.4 %copy-start.21 = (bf16[4,128,384]{2,1,0:T(8,128)(2,1)S(1)}, bf16[4,128,384]{2,1,0:T(8,128)(2,1)}, u32[]{:S(2)}) copy-start(bf16[4,128,384]{2,1,0:T(8,128)(2,1)} %get-tuple-element.267) | copy-start | bytes 1179652
  291.7 31.8 %collective-permute-start.33 = (bf16[2,128,1024]{2,1,0:T(8,128)(2,1)S(1)}, bf16[2,128,1024]{2,1,0:T(8,128)(2,1)S(1)}, u32[]{:S(2)}, u32[]{:S(2)}) collective-permute-start(bf16[2,128,1024]{2,1,0:T(8,128)(2,1)S(1)} %add_convert_fusion.4), channel_id=1, source_target_pairs={{0,4},{4,0},{8,12},{12,8},{16,20},{20,16},{24,28},{28,24},{1,5},{5... | collective-permute-start | bytes 1572872 | tf_op jit(solution)/shard_map/ppermute | solution.py:46
  293.3 14.7 %collective-permute-start.28 = (f32[15360]{0:T(1024)S(1)}, f32[15360]{0:T(1024)S(1)}, u32[]{:S(2)}, u32[]{:S(2)}) collective-permute-start(f32[15360]{0:T(1024)S(1)} %add.244), channel_id=1, source_target_pairs={{0,4},{4,0},{8,12},{12,8},{16,20},{20,16},{24,28},{28,24},{1,5},{5... | collective-permute-start | bytes 184328 | tf_op jit(solution)/shard_map/ppermute | solution.py:46
  293.9 29.6 %collective-permute-start.34 = (bf16[4,128,384]{2,1,0:T(8,128)(2,1)S(1)}, bf16[4,128,384]{2,1,0:T(8,128)(2,1)S(1)}, u32[]{:S(2)}, u32[]{:S(2)}) collective-permute-start(bf16[4,128,384]{2,1,0:T(8,128)(2,1)S(1)} %copy-done.37), channel_id=1, source_target_pairs={{0,4},{4,0},{8,12},{12,8},{16,20},{20,16},{24,28},{28,24},{1,5},{5... | collective-permute-start | bytes 1179656 | tf_op jit(solution)/shard_map/ppermute | solution.py:46
  307.9 15.5 %collective-permute-start.35 = (bf16[4,128,384]{2,1,0:T(8,128)(2,1)S(1)}, bf16[4,128,384]{2,1,0:T(8,128)(2,1)S(1)}, u32[]{:S(2)}, u32[]{:S(2)}) collective-permute-start(bf16[4,128,384]{2,1,0:T(8,128)(2,1)S(1)} %copy-done.36), channel_id=1, source_target_pairs={{0,8},{4,12},{8,0},{12,4},{16,24},{20,28},{24,16},{28,20},{1,9},{5... | collective-permute-start | bytes 1179656 | tf_op jit(solution)/shard_map/ppermute | solution.py:46
  308.7 21.6 %copy-start.20 = (bf16[4,128,384]{2,1,0:T(8,128)(2,1)S(1)}, bf16[4,128,384]{2,1,0:T(8,128)(2,1)}, u32[]{:S(2)}) copy-start(bf16[4,128,384]{2,1,0:T(8,128)(2,1)} %get-tuple-element.269) | copy-start | bytes 1179652
  308.7 7.7 %collective-permute-start.30 = (f32[15360]{0:T(1024)S(1)}, f32[15360]{0:T(1024)S(1)}, u32[]{:S(2)}, u32[]{:S(2)}) collective-permute-start(f32[15360]{0:T(1024)S(1)} %add.245), channel_id=1, source_target_pairs={{0,8},{4,12},{8,0},{12,4},{16,24},{20,28},{24,16},{28,20},{1,9},{5... | collective-permute-start | bytes 184328 | tf_op jit(solution)/shard_map/ppermute | solution.py:46
  316.4 7.1 %collective-permute-start.31 = (bf16[1,160,1024]{2,1,0:T(8,128)(2,1)S(1)}, bf16[1,160,1024]{2,1,0:T(8,128)(2,1)S(1)}, u32[]{:S(2)}, u32[]{:S(2)}) collective-permute-start(bf16[1,160,1024]{2,1,0:T(8,128)(2,1)S(1)} %get-tuple-element.253), channel_id=1, source_target_pairs={{0,2},{1,3},{2,0},{3,1},{4,6},{5,7},{6,4},{7,5},{8,10},{9,11},{10,... | collective-permute-start | bytes 983048 | tf_op jit(solution)/shard_map/ppermute | solution.py:46
  325.3 19.5 %collective-permute-start.43 = (bf16[1,128,1024]{2,1,0:T(8,128)(2,1)S(1)}, bf16[1,128,1024]{2,1,0:T(8,128)(2,1)S(1)}, u32[]{:S(2)}, u32[]{:S(2)}) collective-permute-start(bf16[1,128,1024]{2,1,0:T(8,128)(2,1)S(1)} %add_convert_fusion.6), channel_id=1, source_target_pairs={{0,16},{4,20},{8,24},{12,28},{16,0},{20,4},{24,8},{28,12},{1,17},{... | collective-permute-start | bytes 786440 | tf_op jit(solution)/shard_map/ppermute | solution.py:46
  328.1 32.0 %collective-permute-start.42 = (bf16[1,128,1280]{2,1,0:T(8,128)(2,1)}, bf16[1,128,1280]{2,1,0:T(8,128)(2,1)}, u32[]{:S(2)}, u32[]{:S(2)}) collective-permute-start(bf16[1,128,1280]{2,1,0:T(8,128)(2,1)} %add_convert_fusion.5), channel_id=1, source_target_pairs={{0,16},{4,20},{8,24},{12,28},{16,0},{20,4},{24,8},{28,12},{1,17},{... | collective-permute-start | bytes 983048 | tf_op jit(solution)/shard_map/ppermute | solution.py:46
  330.1 9.7 %collective-permute-start.38 = (bf16[2,128,384]{2,1,0:T(8,128)(2,1)S(1)}, bf16[2,128,384]{2,1,0:T(8,128)(2,1)S(1)}, u32[]{:S(2)}, u32[]{:S(2)}) collective-permute-start(bf16[2,128,384]{2,1,0:T(8,128)(2,1)S(1)} %add_convert_fusion.8), channel_id=1, source_target_pairs={{0,8},{4,12},{8,0},{12,4},{16,24},{20,28},{24,16},{28,20},{1,9},{5... | collective-permute-start | bytes 589832 | tf_op jit(solution)/shard_map/ppermute | solution.py:46
  330.4 9.9 %collective-permute-start.40 = (bf16[2,128,384]{2,1,0:T(8,128)(2,1)S(1)}, bf16[2,128,384]{2,1,0:T(8,128)(2,1)S(1)}, u32[]{:S(2)}, u32[]{:S(2)}) collective-permute-start(bf16[2,128,384]{2,1,0:T(8,128)(2,1)S(1)} %add_convert_fusion.7), channel_id=1, source_target_pairs={{0,4},{4,0},{8,12},{12,8},{16,20},{20,16},{24,28},{28,24},{1,5},{5... | collective-permute-start | bytes 589832 | tf_op jit(solution)/shard_map/ppermute | solution.py:46
  332.0 29.4 %collective-permute-start.36 = (f32[15360]{0:T(1024)S(1)}, f32[15360]{0:T(1024)S(1)}, u32[]{:S(2)}, u32[]{:S(2)}) collective-permute-start(f32[15360]{0:T(1024)S(1)} %add.248), channel_id=1, source_target_pairs={{0,16},{4,20},{8,24},{12,28},{16,0},{20,4},{24,8},{28,12},{1,17},{... | collective-permute-start | bytes 184328 | tf_op jit(solution)/shard_map/ppermute | solution.py:46
  339.9 21.6 %collective-permute-start.37 = (bf16[1,160,1024]{2,1,0:T(8,128)(2,1)}, bf16[1,160,1024]{2,1,0:T(8,128)(2,1)}, u32[]{:S(2)}, u32[]{:S(2)}) collective-permute-start(bf16[1,160,1024]{2,1,0:T(8,128)(2,1)} %get-tuple-element.264), channel_id=1, source_target_pairs={{0,2},{1,3},{2,0},{3,1},{4,6},{5,7},{6,4},{7,5},{8,10},{9,11},{10,... | collective-permute-start | bytes 983048 | tf_op jit(solution)/shard_map/ppermute | solution.py:46
  340.3 17.5 %collective-permute-start.39 = (bf16[1,128,384]{2,1,0:T(8,128)(2,1)S(1)}, bf16[1,128,384]{2,1,0:T(8,128)(2,1)S(1)}, u32[]{:S(2)}, u32[]{:S(2)}) collective-permute-start(bf16[1,128,384]{2,1,0:T(8,128)(2,1)S(1)} %add_convert_fusion.10), channel_id=1, source_target_pairs={{0,16},{4,20},{8,24},{12,28},{16,0},{20,4},{24,8},{28,12},{1,17},{... | collective-permute-start | bytes 294920 | tf_op jit(solution)/shard_map/ppermute | solution.py:46
  344.8 14.1 %collective-permute-start.41 = (bf16[1,128,384]{2,1,0:T(8,128)(2,1)S(1)}, bf16[1,128,384]{2,1,0:T(8,128)(2,1)S(1)}, u32[]{:S(2)}, u32[]{:S(2)}) collective-permute-start(bf16[1,128,384]{2,1,0:T(8,128)(2,1)S(1)} %add_convert_fusion.9), channel_id=1, source_target_pairs={{0,16},{4,20},{8,24},{12,28},{16,0},{20,4},{24,8},{28,12},{1,17},{... | collective-permute-start | bytes 294920 | tf_op jit(solution)/shard_map/ppermute | solution.py:46
  362.6 10.2 %copy-start.30 = (f32[1024]{0:T(1024)}, f32[1024]{0:T(1024)S(1)}, u32[]{:S(2)}) copy-start(f32[1024]{0:T(1024)S(1)} %get-tuple-element.420) | copy-start | bytes 12292
  (18 other events, 69.4 us)

commit v5 on v4

--- a/solution.py
+++ b/solution.py
@@ -118,8 +118,7 @@
         self.terms.append((self.got, 0))
         half = self.got.shape[0] // 2
         if half:
-            sends = [x[at : at + half].astype(f32) for x, at in self.terms]
-            self.send = sum(sends).astype(bf16)
+            self.send = add_terms(self.terms, half)
             self.terms = [(x, at + half) for x, at in self.terms]
 
     def most(self):
@@ -198,14 +197,6 @@
                 if at + 1 < self.groups:
                     copy(at + 1).start()
                 copy(at).wait()
-
-
-def pick_piece(pieces, where, step):
-    for at, piece in enumerate(pieces):
-
-        @pl.when(step == at)
-        def _(piece=piece):
-            where[...] = piece[...]
 
 
 def store_halves(send, keep, total, number, order, columns=slice(None), source=slice(None)):
@@ -513,11 +504,73 @@
     )
 
 
-def mlp(ids, sent, grad, context, gain, shift, fc, bias, out, orders):
+def attention_weights(ids, info, tables, context, dq, dk, dv, sent, grad, gain, shift, orders):
     groups, held, rows, model = sent.groups, len(sent.arrays), sent.rows, sent.model
-    pieces, units, width = len(fc.arrays), fc.arrays[0].shape[1], context.shape[1]
-
-    def kernel(ids, ctx_ref, *refs):
+    width, count = dq.shape[1], len(orders[0])
+
+    def kernel(ids, info, ctx_ref, dq_ref, dk_ref, dv_ref, *refs):
+        sent_refs, refs = refs[:held], refs[held:]
+        grad_refs, refs = refs[:held], refs[held:]
+        gain, shift, cos, low, high, grads, bias_ref, *stacks = refs[:11]
+        block, arrived, grad_block, grad_arrived, total, dense_total = refs[11:]
+        step = pl.program_id(0)
+
+        @pl.when(step == 0)
+        def _():
+            total[...] = jnp.zeros_like(total)
+            dense_total[...] = jnp.zeros_like(dense_total)
+            bias_ref[...] = jnp.zeros_like(bias_ref)
+
+        sent.fetch(sent_refs, block, arrived, step)
+        grad.fetch(grad_refs, grad_block, grad_arrived, step)
+        grads[:, :width] = dq_ref[...]
+        first = (ids[0] ^ ids[2 + step]) * (rows // SEG)
+        for at in range(rows // SEG):
+            number = first + at
+            table = pl.ds(pl.multiple_of(info[number // NB, number % NB, 4] * SEG, SEG), SEG)
+            own = slice(at * SEG, (at + 1) * SEG)
+            turned = turn(dk_ref[own, :], cos[table, :], low[table, :], high[table, :], -1.0)
+            grads[own, width : 2 * width] = turned.astype(bf16)
+        grads[:, 2 * width :] = dv_ref[...]
+        bias_ref[0:1, :] += jnp.sum(grads[...].astype(f32), axis=0, keepdims=True)
+        total[...] += dot_tn(shift_gain(block[step % 2], gain, shift), grads[...])
+        dense_total[...] += dot_tn(grad_block[step % 2], ctx_ref[...])
+
+        @pl.when(step == groups - 1)
+        def _():
+            store_halves(*stacks[:2], total, ids[1], orders[0], source=slice(0, 2 * width))
+            source = slice(2 * width, 3 * width)
+            store_halves(*stacks[2:], total, ids[1], orders[1], slice(0, width), source)
+            columns = slice(width, 2 * width)
+            store_halves(*stacks[2:], dense_total, ids[1], orders[1], columns)
+
+    operands = [context, dq, dk, dv, *sent.arrays, *grad.arrays, gain, shift, *tables]
+    outs = [shaped(groups * rows, 3 * width), shaped(8, 3 * width, dtype=f32)]
+    outs += [shaped(count // 2, model // count, 2 * width)] * 4
+    return call(
+        kernel,
+        "attention_weights",
+        (groups,),
+        [ids, info],
+        operands,
+        [own_block(rows, width)] * 4
+        + sent.specs
+        + grad.specs
+        + [resident(x.shape) for x in operands[-5:]],
+        outs,
+        [step_block(rows, 3 * width)] + [resident(x.shape) for x in outs[1:]],
+        sent.scratch()
+        + grad.scratch()
+        + [pltpu.VMEM((model, 3 * width), f32), pltpu.VMEM((model, width), f32)],
+        2 * groups * rows * model * 4 * width,
+    )
+
+
+def mlp(ids, sent, grad, gain, shift, fc, bias, out, orders):
+    groups, held, rows, model = sent.groups, len(sent.arrays), sent.rows, sent.model
+    pieces, units = len(fc.arrays), fc.arrays[0].shape[1]
+
+    def kernel(ids, *refs):
         sent_refs, refs = refs[:held], refs[held:]
         grad_refs, refs = refs[:held], refs[held:]
         fc_refs, refs = refs[:pieces], refs[pieces:]
@@ -525,7 +578,7 @@
         gain, shift, bias, part_send, part_keep, hidden_ref, bias_ref = refs[:7]
         stacks, refs = refs[7:11], refs[11:]
         block, arrived, grad_block, grad_arrived, fc_whole, fc_placed, out_whole, out_placed = refs[:8]
-        act_ref, fc_total, out_total, dense_total = refs[8:]
+        act_ref, fc_total, out_total = refs[8:]
         step = pl.program_id(0)
 
         def weights():
@@ -538,7 +591,6 @@
                 copy.start()
             fc_total[...] = jnp.zeros_like(fc_total)
             out_total[...] = jnp.zeros_like(out_total)
-            dense_total[...] = jnp.zeros_like(dense_total)
             bias_ref[...] = jnp.zeros_like(bias_ref)
 
         sent.fetch(sent_refs, block, arrived, step)
@@ -567,7 +619,6 @@
         )
         out_total[...] += dot_tn(grads, act_ref[...])
         fc_total[...] += dot_tn(normed, hidden_ref[...])
-        dense_total[...] += dot_tn(grads, ctx_ref[...])
 
         @pl.when(step == groups - 1)
         def _():
@@ -577,10 +628,8 @@
                 source = slice(at * half, (at + 1) * half)
                 store_halves(*stack, fc_total, ids[1], order, slice(0, half), source)
                 store_halves(*stack, out_total, ids[1], order, slice(half, units), source)
-            columns = slice(units, units + width)
-            store_halves(*stacks[:2], dense_total, ids[1], orders[0], columns)
-
-    operands = [context, *sent.arrays, *grad.arrays, *fc.arrays, *out.arrays, gain, shift, bias]
+
+    operands = [*sent.arrays, *grad.arrays, *fc.arrays, *out.arrays, gain, shift, bias]
     count = model // fc.rows
     outs = [
         shaped(groups // 2, rows, model),
@@ -588,16 +637,14 @@
         shaped(groups * rows, units),
         shaped(8, units, dtype=f32),
     ]
-    outs += [shaped(count // 2, fc.rows, units + width)] * 2
-    outs += [shaped(count // 2, fc.rows, units)] * 2
+    outs += [shaped(count // 2, fc.rows, units)] * 4
     return call(
         kernel,
         "mlp",
         (groups,),
         [ids],
         operands,
-        [own_block(rows, width)]
-        + sent.specs
+        sent.specs
         + grad.specs
         + fc.specs()
         + out.specs()
@@ -614,25 +661,21 @@
             pltpu.VMEM((rows, units), bf16),
             pltpu.VMEM((model, units), f32),
             pltpu.VMEM((model, units), f32),
-            pltpu.VMEM((model, width), f32),
         ],
         10 * groups * rows * model * units,
     )
 
 
-def norm_backward(
-    ids, info, tables, sent, dq, dk, dv, hidden, gain_attn, shift_attn, gain_mlp, qkv_pack, fc, orders
-):
+def norm_backward(ids, sent, grads, hidden, gain_attn, gain_mlp, qkv_pack, fc):
     groups, held, rows, model = sent.groups, len(sent.arrays), sent.rows, sent.model
-    pieces, units, width = len(fc.arrays), hidden.shape[1], dq.shape[1]
-
-    def kernel(ids, info, dq_ref, dk_ref, dv_ref, hidden_ref, *refs):
+    pieces, units, columns = len(fc.arrays), hidden.shape[1], grads.shape[1]
+
+    def kernel(ids, grads_ref, hidden_ref, *refs):
         sent_refs, refs = refs[:held], refs[held:]
         qkv_refs, refs = refs[:pieces], refs[pieces:]
         fc_refs, refs = refs[:pieces], refs[pieces:]
-        gain_attn, shift_attn, gain_mlp, cos, low, high = refs[:6]
-        send, keep, sums_ref, bias_ref, *halves = refs[6:14]
-        block, arrived, qkv_whole, qkv_placed, fc_whole, fc_placed, grads, total = refs[14:]
+        gain_attn, gain_mlp, send, keep, sums_ref = refs[:5]
+        block, arrived, qkv_whole, qkv_placed, fc_whole, fc_placed = refs[5:]
         step = pl.program_id(0)
 
         def weights():
@@ -644,83 +687,44 @@
             for copy in weights():
                 copy.start()
             sums_ref[...] = jnp.zeros_like(sums_ref)
-            bias_ref[...] = jnp.zeros_like(bias_ref)
-            total[...] = jnp.zeros_like(total)
 
         sent.fetch(sent_refs, block, arrived, step)
-        grads[:, :width] = dq_ref[...]
-        first = (ids[0] ^ ids[2 + step]) * (rows // SEG)
-        for at in range(rows // SEG):
-            number = first + at
-            table = pl.ds(pl.multiple_of(info[number // NB, number % NB, 4] * SEG, SEG), SEG)
-            own = slice(at * SEG, (at + 1) * SEG)
-            turned = turn(dk_ref[own, :], cos[table, :], low[table, :], high[table, :], -1.0)
-            grads[own, width : 2 * width] = turned.astype(bf16)
-        grads[:, 2 * width :] = dv_ref[...]
-        bias_ref[0:1, :] += jnp.sum(grads[...].astype(f32), axis=0, keepdims=True)
 
         @pl.when(step == 0)
         def _():
             for copy in weights():
                 copy.wait()
 
-        token = block[step % 2]
-        total[...] += dot_tn(shift_gain(token, gain_attn, shift_attn), grads[...])
-        back_attn = dot_nt(grads[...], qkv_whole[...])
+        back_attn = dot_nt(grads_ref[...], qkv_whole[...])
         back_mlp = dot_nt(hidden_ref[...], fc_whole[...])
-        token = token.astype(f32)
+        token = block[step % 2].astype(f32)
         for at, back in enumerate((back_attn, back_mlp)):
             sums_ref[2 * at : 2 * at + 1, :] += jnp.sum(back * token, axis=0, keepdims=True)
             sums_ref[2 * at + 1 : 2 * at + 2, :] += jnp.sum(back, axis=0, keepdims=True)
         part = back_attn * gain_attn[...] + back_mlp * gain_mlp[...]
         store_half(send, keep, part.astype(bf16), step, groups)
 
-        @pl.when(step == groups - 1)
-        def _():
-            for at, order in enumerate(orders):
-                source = slice(at * 3 * width // 2, (at + 1) * 3 * width // 2)
-                store_halves(*halves[2 * at : 2 * at + 2], total, ids[1], order, source=source)
-
-    operands = [
-        dq,
-        dk,
-        dv,
-        hidden,
-        *sent.arrays,
-        *qkv_pack.arrays,
-        *fc.arrays,
-        gain_attn,
-        shift_attn,
-        gain_mlp,
-        *tables,
-    ]
-    count = model // fc.rows
+    operands = [grads, hidden, *sent.arrays, *qkv_pack.arrays, *fc.arrays, gain_attn, gain_mlp]
     outs = [
         shaped(groups // 2, rows, model),
         shaped(groups // 2, rows, model),
         shaped(8, model, dtype=f32),
-        shaped(8, 3 * width, dtype=f32),
     ]
-    outs += [shaped(count // 2, fc.rows, 3 * width // 2)] * 4
     return call(
         kernel,
         "norm_backward",
         (groups,),
-        [ids, info],
+        [ids],
         operands,
-        [own_block(rows, width)] * 3
-        + [step_block(rows, units)]
+        [step_block(rows, columns), step_block(rows, units)]
         + sent.specs
         + qkv_pack.specs()
         + fc.specs()
-        + [resident(x.shape) for x in operands[-6:]],
+        + [resident(x.shape) for x in operands[-2:]],
         outs,
         half_blocks(groups, rows, model) + [resident(x.shape) for x in outs[2:]],
-        sent.scratch()
-        + weight_scratch(qkv_pack)
-        + weight_scratch(fc)
-        + [pltpu.VMEM((rows, 3 * width), bf16), pltpu.VMEM((model, 3 * width), f32)],
-        2 * groups * rows * model * (units + 6 * width),
+        sent.scratch() + weight_scratch(qkv_pack) + weight_scratch(fc),
+        2 * groups * rows * model * (units + columns),
     )
 
 
@@ -729,6 +733,31 @@
         pl.BlockSpec((pl.Squeezed(), block, x.shape[2]), lambda i, *_, at=at: (at, i, 0))
         for x, at in terms
     ]
+
+
+def add_terms(terms, half, start=0, rows=None):
+    columns = terms[0][0].shape[2]
+    rows = terms[0][0].shape[1] if rows is None else rows
+    block = max(x for x in (320, 160, 128, 64) if rows % x == 0 and start % x == 0)
+    skip = start // block
+
+    def kernel(*refs):
+        refs[-1][...] = sum(x[...].astype(f32) for x in refs[:-1]).astype(bf16)
+
+    shape = (pl.Squeezed(), block, columns)
+    out = shaped(half, rows, columns)
+    return call(
+        kernel,
+        "add_terms",
+        (half, rows // block),
+        [],
+        [x for x, _ in terms],
+        [pl.BlockSpec(shape, lambda k, i, *_, at=at: (at + k, i + skip, 0)) for _, at in terms],
+        [out],
+        [pl.BlockSpec(shape, lambda k, i, *_: (k, i, 0))],
+        [],
+        half * rows * columns * len(terms),
+    )[0]
 
 
 def finish_output(stream, attn_terms, mlp_terms, dense_bias, out_bias):
@@ -770,33 +799,36 @@
     )
 
 
-def finish_grad(grad, normalized, inv_std, terms, chunks):
+def finish_grad(grad, normalized, inv_std, terms, first, rest):
     rows, model = grad.shape
-    count, block = len(chunks), chunks[0].shape[0]
-    held = len(terms)
+    block = first.shape[1]
 
     def kernel(grad_ref, norm_ref, std_ref, *refs):
-        term_refs, chunk_refs, (out_ref, last) = refs[:held], refs[held:-2], refs[-2:]
-        pick_piece(chunk_refs, last, pl.program_id(0))
-        sent = sum(x[...].astype(f32) for x in term_refs) + last[...].astype(f32)
+        term_refs, (first_ref, rest_ref, out_ref) = refs[:-3], refs[-3:]
+        last = jnp.where(pl.program_id(0) == 0, first_ref[...].astype(f32), rest_ref[...].astype(f32))
+        sent = sum(x[...].astype(f32) for x in term_refs) + last
         norm = norm_ref[...]
         mean = jnp.sum(sent, axis=1, keepdims=True) / model
         cross = jnp.sum(sent * norm, axis=1, keepdims=True) / model
         out_ref[...] = grad_ref[...].astype(f32) + std_ref[...] * (sent - mean - norm * cross)
 
-    operands = [grad, normalized, inv_std, *[x for x, _ in terms], *chunks]
+    operands = [grad, normalized, inv_std, *[x for x, _ in terms], first, rest]
+    piece = (pl.Squeezed(), block, model)
     return call(
         kernel,
         "finish_grad",
-        (count,),
+        (rows // block,),
         [],
         operands,
         [step_block(block, model), step_block(block, model), step_block(block, 1)]
         + taken(terms, block)
-        + [resident(x.shape) for x in chunks],
+        + [
+            pl.BlockSpec(piece, lambda i, *_: (0, 0, 0)),
+            pl.BlockSpec(piece, lambda i, *_: (0, jnp.maximum(i - 1, 0), 0)),
+        ],
         [shaped(rows, model, dtype=f32)],
         [step_block(block, model)],
-        [pltpu.VMEM((block, model), bf16)],
+        [],
         rows * model * 12,
     )[0]
 
@@ -879,13 +911,14 @@
     data_bits = bits_of(lax.axis_size("dp"))
     rows_first = data_bits[:0:-1] + data_bits[:1]
     columns_first = data_bits[:1] + data_bits[:0:-1]
+    between = data_bits[:1:-1] + data_bits[:2]
     near_bits = data_bits
     next_bits = data_bits[1:2] + data_bits[:1] + data_bits[2:]
 
     qkv_pack = Pack(by_kind(qkv_weight.astype(bf16), heads), "dp", rows_first)
     dense_pack = Pack(dense_weight.astype(bf16).T, "dp", columns_first)
     fc_pack = Pack(fc_weight.astype(bf16), "dp", rows_first)
-    out_pack = Pack(out_weight.astype(bf16).T, "dp", columns_first)
+    out_pack = Pack(out_weight.astype(bf16).T, "dp", between)
 
     row_mean = jnp.mean(stream_in, axis=-1, keepdims=True)
     centred = stream_in - row_mean
@@ -896,21 +929,19 @@
 
     qkv_pack.double()
     dense_pack.double()
+    tie_packs(qkv_pack, dense_pack, fc_pack, out_pack)
+    fc_pack.double()
     out_pack.double()
-    tie_packs(qkv_pack, dense_pack, fc_pack, out_pack)
     while len(qkv_pack.bits) > 1:
         qkv_pack.double()
         dense_pack.double()
-    fc_pack.double()
-    sent = tie_packs(qkv_pack, dense_pack, fc_pack, out_pack, beside=sent)
-    out_grad, sent[0] = tie(out_grad, sent[0])
+    out_grad, *sent = tie_packs(qkv_pack, dense_pack, beside=[out_grad, *sent])
     grad = gather_far(out_grad, "tensor", tensor_bits)
     sent = gather_near(sent, "tensor")
     qkv_pack.double()
     dense_pack.double()
-    while len(out_pack.bits) > 1:
-        out_pack.double()
-    sent = Tokens(tie_packs(qkv_pack, dense_pack, out_pack, beside=sent), order)
+    sent = tie_packs(qkv_pack, dense_pack, fc_pack, out_pack, beside=sent)
+    sent = Tokens(sent, order)
 
     info = tree_table(segment_ids, parent_ids)
     tables = angle_tables()
@@ -923,85 +954,86 @@
 
     while len(fc_pack.bits) > 1:
         fc_pack.double()
+        out_pack.double()
     done = project_qkv(
         ids, info, sent, gain_attn, shift_attn, qkv_pack, qkv_bias_own, tables, width
     )
-    queries, keys, values, *grad = tie_packs(fc_pack, beside=[*done, *grad])
+    queries, keys, values, *grad = tie_packs(fc_pack, out_pack, beside=[*done, *grad])
     grad = Tokens(gather_near(grad, "tensor"), order)
     grad_context = project_grad(ids, grad, dense_pack, width)
     fc_pack.double()
     out_pack.double()
     done = attention(info, tables, queries, keys, values, grad_context)
     context, dq, dk, dv = tie_packs(fc_pack, out_pack, beside=done)
+    dp_orders = [halving_order(near_bits), halving_order(next_bits)]
     attn_parts = Halving(
         *project_context(ids, context, dense_pack, groups, model), "tensor", tensor_bits
     )
-    attn_parts.most()
-    context, attn_parts.send = tie(context, attn_parts.send)
+    while len(attn_parts.bits) > 2:
+        attn_parts.swap()
+        attn_parts.add()
+    attn_parts.send, context = tie(attn_parts.send, context)
     attn_parts.swap()
+    done = attention_weights(
+        ids, info, tables, context, dq, dk, dv, sent, grad, gain_attn, shift_attn, dp_orders
+    )
+    grads, qkv_bias_sums, *stacks = tie_halves(done, attn_parts)
+    attn_parts.add()
+    qkv_sums = [Halving(*stacks[:2], "dp", near_bits), Halving(*stacks[2:], "dp", next_bits)]
+    sent.arrays[0], attn_parts.send = tie(sent.arrays[0], attn_parts.send)
+    attn_parts.swap()
+    for parts in qkv_sums:
+        parts.swap()
     done = mlp(
-        ids,
-        sent,
-        grad,
-        context,
-        gain_mlp,
-        shift_mlp,
-        fc_pack,
-        fc_bias_own,
-        out_pack,
-        [halving_order(near_bits), halving_order(next_bits)],
-    )
-    done = tie_halves(done, attn_parts)
+        ids, sent, grad, gain_mlp, shift_mlp, fc_pack, fc_bias_own, out_pack, dp_orders
+    )
+    done = tie_halves(done, attn_parts, *qkv_sums)
     mlp_send, mlp_keep, hidden, fc_bias_sums, *stacks = done
     attn_parts.add()
     mlp_parts = Halving(mlp_send, mlp_keep, "tensor", tensor_bits)
-    mlp_sums = [
-        Halving(*stacks[:2], "dp", near_bits),
-        Halving(*stacks[2:], "dp", next_bits),
-    ]
-    mlp_parts.most()
+    mlp_sums = [Halving(*stacks[:2], "dp", near_bits), Halving(*stacks[2:], "dp", next_bits)]
+    while len(mlp_parts.bits) > 2:
+        mlp_parts.swap()
+        mlp_parts.add()
+    mlp_parts.swap()
+    for parts in qkv_sums:
+        parts.add()
+    mlp_parts.got, *sends = tie(mlp_parts.got, *[parts.send for parts in qkv_sums])
+    for parts, send in zip(qkv_sums, sends):
+        parts.send = send
+    mlp_parts.add()
     hidden, mlp_parts.send = tie(hidden, mlp_parts.send)
     mlp_parts.swap()
-    for parts in mlp_sums:
+    for parts in qkv_sums + mlp_sums:
         parts.swap()
-    done = norm_backward(
-        ids,
-        info,
-        tables,
-        sent,
-        dq,
-        dk,
-        dv,
-        hidden,
-        gain_attn,
-        shift_attn,
-        gain_mlp,
-        qkv_pack,
-        fc_pack,
-        [halving_order(near_bits), halving_order(next_bits)],
-    )
-    done = tie_halves(done, mlp_parts, *mlp_sums)
-    back_send, back_keep, norm_sums, qkv_bias_sums, *stacks = done
-    qkv_sums = [
-        Halving(*stacks[:2], "dp", near_bits),
-        Halving(*stacks[2:], "dp", next_bits),
-    ]
+    done = norm_backward(ids, sent, grads, hidden, gain_attn, gain_mlp, qkv_pack, fc_pack)
+    done = tie_halves(done, mlp_parts, *qkv_sums, *mlp_sums)
+    back_send, back_keep, norm_sums = done
     mlp_parts.add()
-    for parts in mlp_sums:
-        parts.add()
 
     back_parts = Halving(back_send, back_keep, "tensor", tensor_bits)
     while len(back_parts.bits) > 2:
         back_parts.swap()
         back_parts.add()
     back_parts.swap()
-    output, squares = tie_halves(
-        finish_output(
-            stream_in, attn_parts.terms, mlp_parts.terms, dense_bias[None, :], out_bias[None, :]
-        ),
-        back_parts,
-    )
-    back_parts.add()
+    for parts in qkv_sums + mlp_sums:
+        parts.add()
+    back_parts.got, *sends = tie(back_parts.got, *[parts.send for parts in qkv_sums + mlp_sums])
+    for parts, send in zip(qkv_sums + mlp_sums, sends):
+        parts.send = send
+    back_parts.terms.append((back_parts.got, 0))
+    quarter, last = rows_local // 4, back_parts.bits[-1]
+    first = add_terms(back_parts.terms, 1, 0, quarter)
+    rest = add_terms(back_parts.terms, 1, quarter, rows_local - quarter)
+    back_parts.terms = [(x, at + 1) for x, at in back_parts.terms]
+    stream_in, first, rest = tie(stream_in, first, rest)
+    first, rest = swap(first, "tensor", last), swap(rest, "tensor", last)
+    for parts in qkv_sums + mlp_sums:
+        parts.swap()
+    output, squares = finish_output(
+        stream_in, attn_parts.terms, mlp_parts.terms, dense_bias[None, :], out_bias[None, :]
+    )
+    output, squares, first = tie(output, squares, first)
     fc_bias_spread = lax.dynamic_update_slice(
         jnp.zeros(fc_bias.shape, f32), fc_bias_sums[0], (tensor_rank * units,)
     )
@@ -1017,33 +1049,28 @@
             qkv_bias_spread,
         ]
     )
-    steps = [(axis, bit) for axis in ("tensor", "dp") for bit in bits_of(lax.axis_size(axis))]
-    chunks = jnp.split(back_parts.send, 4, axis=1)
-    sums = sums + swap(sums, *steps[0])
-    for parts in mlp_sums + qkv_sums:
-        parts.swap()
-    got = []
-    for at, step in enumerate(steps[1:]):
-        other = swap(sums, *step)
-        if at < len(chunks):
-            got.append(swap(chunks[at], "tensor", back_parts.bits[-1]))
-            other, got[-1], *chunks[at + 1 :] = tie(other, got[-1], *chunks[at + 1 :])
-        if at == 2:
-            (other,) = tie_halves([other], *mlp_sums, *qkv_sums)
-        sums = sums + other
-    for parts in mlp_sums + qkv_sums:
+    sums = sums + swap(sums, "tensor", 1)
+    (sums,) = tie_halves([sums], *qkv_sums, *mlp_sums)
+    for bit in data_bits[1:]:
+        sums = sums + swap(sums, "dp", bit)
+    for parts in qkv_sums + mlp_sums:
         parts.add()
-    stream_grad = finish_grad(
-        out_grad, normalized, inv_std, back_parts.terms, [x[0] for x in got]
-    )
+    sums, *sends = tie(sums, *[parts.send for parts in mlp_sums])
+    for parts, send in zip(mlp_sums, sends):
+        parts.send = send
+    sums = sums + swap(sums, "dp", data_bits[0])
+    sums, rest = tie(sums, rest)
+    for bit in tensor_bits[1:]:
+        sums = sums + swap(sums, "tensor", bit)
+    stream_grad = finish_grad(out_grad, normalized, inv_std, back_parts.terms, first, rest)
 
     first, second = [parts.finish() for parts in mlp_sums]
     half = units // 2
     fc_weight_grad = jnp.concatenate([first[:, :half], second[:, :half]], axis=1)
-    out_weight_grad = jnp.concatenate([first[:, half:units], second[:, half:]], axis=1).T
-    dense_weight_grad = first[:, units:].T
-    total = jnp.concatenate([parts.finish() for parts in qkv_sums], axis=1)
-    qkv_weight_grad = by_head(total, heads)
+    out_weight_grad = jnp.concatenate([first[:, half:], second[:, half:]], axis=1).T
+    first, second = [parts.finish() for parts in qkv_sums]
+    dense_weight_grad = second[:, width:].T
+    qkv_weight_grad = by_head(jnp.concatenate([first, second[:, :width]], axis=1), heads)
 
     count_all = float(rows_local * lax.axis_size("dp") * groups * model)
     gain_attn_grad, shift_attn_grad, gain_mlp_grad, shift_mlp_grad = sums[: 4 * model].reshape(

time: 381 us -> 371 us (0.974); the launches traced: 374 us -> 369 us
  waiting for transfers between devices: 99.4 us -> 67.8 us
  Pallas kernels: 166 us -> 197 us
  other arithmetic: 38.6 us -> 26 us
  local copies, waits for them, and re-layouts: 20.9 us -> 26.7 us
    ppermute x44 -> x42, waiting for transfers between devices: 99.4 us -> 67.8 us  [swap(): return lax.ppermute(block, axis, [(i, i ^ bit) for i in range(size)])]
    pallas_call x8 -> x21, Pallas kernels: 166 us -> 197 us  [call(): pl.pallas_call(kernel, grid_spec=pltpu.PrefetchScalarGridSpec(num_scalar_...]
    convert_element_type x11 -> x0, other arithmetic: 15.5 us -> none  [add(): self.send = sum(sends).astype(bf16)]
    ppermute x44 -> x42, starting transfers between devices: 46.7 us -> 50 us  [swap(): return lax.ppermute(block, axis, [(i, i ^ bit) for i in range(size)])]
    unnamed x88 -> x82, local copies, waits for them, and re-layouts: 7.99 us -> 9.64 us
  transfers between devices with their start and end apart: 44 -> 42, of which waited for: 14 -> 15; matrix products, arithmetic and copies ran while one was open for 10% -> 12% of each run, Pallas kernels for 41% -> 48%
where the time goes in v5:
time: 371 us; the launch traced here: 369 us
  Pallas kernels  197 us (53%)
  waiting for transfers between devices  67.8 us (18%)
  starting transfers between devices  50 us (13%)
  local copies, waits for them, and re-layouts  26.7 us (7%)
  other arithmetic  26 us (7%)
    pallas_call x21, Pallas kernels, call(): pl.pallas_call(kernel, grid_spec=pltpu.PrefetchScalarGridSpec(num_scalar_...  197 us
    ppermute x42, waiting for transfers between devices, swap(): return lax.ppermute(block, axis, [(i, i ^ bit) for i in range(size)])  67.8 us
    ppermute x42, starting transfers between devices, swap(): return lax.ppermute(block, axis, [(i, i ^ bit) for i in range(size)])  50 us
    unnamed x82, local copies, waits for them, and re-layouts  9.64 us
    concatenate x8, other arithmetic, double(): jnp.concatenate(self.arrays, axis=0)  7.94 us
  transfers between devices with their start and end apart: 42, of which 15 were waited for; matrix products, arithmetic and copies ran while one was open for 12% of the time, Pallas kernels for 48%

profile of v5, /device:TPU:0, one launch (start us, length us, event | category | flops | bytes accessed | tf_op | source)
XLA Modules:
  0.0 368.7 jit_solution(2967614195613491462)
XLA Ops:
  0.7 2.1 reduce_sum.49
  3.6 2.3 fusion.28
  5.9 2.9 collective-permute-start
  9.2 2.7 collective-permute-start.1
  12.9 1.6 collective-permute-start.2
  14.7 2.5 collective-permute-done.2.refs_5_.refs_1_
  17.2 3.5 collective-permute-done.1.refs_5_
  21.7 3.4 collective-permute-start.4
  25.1 7.9 %collective-permute-done.4.refs_6_.refs_2_ = bf16[256,256]{1,0:T(8,128)(2,1)S(1)} collective-permute-done((bf16[256,256]{1,0:T(8,128)(2,1)S(1)}, bf16[256,256]{1,0:T(8,128)(2,1)S(1)}, u32[]{:S(2)}, u32[]{:S(2)}) %collective-permute-start.4) | collective-permute-done | bytes 131104 | tf_op jit(solution)/shard_map/ppermute | solution.py:46
  33.8 4.2 %collective-permute-done.refs_2_ = bf16[640,1024]{1,0:T(8,128)(2,1)} collective-permute-done((bf16[640,1024]{1,0:T(8,128)(2,1)}, bf16[640,1024]{1,0:T(8,128)(2,1)}, u32[]{:S(2)}, u32[]{:S(2)}) %collective-permute-start) | collective-permute-done | bytes 1310752 | tf_op jit(solution)/shard_map/ppermute | solution.py:46
  38.4 2.8 collective-permute-start.10
  41.5 1.9 pad_maximum_fusion.2
  43.5 1.8 collective-permute-start.7
  45.2 4.0 %fusion.8 = (f32[1280,128]{1,0:T(8,128)}, f32[1280,128]{1,0:T(8,128)}, f32[1280,128]{1,0:T(8,128)}) fusion(s32[128]{0:T(128)S(1)} %get-tuple-element.406, s32[128]{0:T(128)S(1)} %get-tuple-element.407, pred[128]{0:T(512)(128)(4,1)S(1)} %compare_and_fusion, f32[1280]{0:T(1024)S(1)} %iota_convert_fusion), kind=kLoop, calls=%fused_computation.23 | loop fusion | flops 3932160 | bytes 1972352 | tf_op jit(solution)/shard_map/jit(_where)/select_n | solution.py:864
  49.3 10.4 %collective-permute-done.10.refs_13_ = bf16[128,1024]{1,0:T(8,128)(2,1)S(1)} collective-permute-done((bf16[128,1024]{1,0:T(8,128)(2,1)S(1)}, bf16[128,1024]{1,0:T(8,128)(2,1)S(1)}, u32[]{:S(2)}, u32[]{:S(2)}) %collective-permute-start.10) | collective-permute-done | bytes 262176 | tf_op jit(solution)/shard_map/ppermute | solution.py:46
  59.7 1.8 collective-permute-start.11
  61.5 3.1 collective-permute-done.9.refs_9_
  66.1 6.1 %collective-permute-done.8.refs_7_.refs_3_ = bf16[512,256]{1,0:T(8,128)(2,1)S(1)} collective-permute-done((bf16[512,256]{1,0:T(8,128)(2,1)S(1)}, bf16[512,256]{1,0:T(8,128)(2,1)S(1)}, u32[]{:S(2)}, u32[]{:S(2)}) %collective-permute-start.8) | collective-permute-done | bytes 262176 | tf_op jit(solution)/shard_map/ppermute | solution.py:46
  73.1 1.3 collective-permute-start.13
  75.3 1.5 collective-permute-start.12
  80.5 11.5 %project_qkv.1 = (bf16[2560,256]{1,0:T(8,128)(2,1)}, bf16[2560,256]{1,0:T(8,128)(2,1)}, bf16[2560,256]{1,0:T(8,128)(2,1)}) custom-call(s32[6]{0:T(128)} %stack.19.ids, s32[1,20,5]{2,1,0:T(8,128)} %stack.20.info, bf16[640,1024]{1,0:T(8,128)(2,1)} %collective-permute-done.6.refs_0_, bf16[640,1024]{1,0:T(8,128)(2,1)} %collective-permute-done.5.refs_1_, ...), custom_call_target="tpu_custom_call" | custom-call | flops 4026531840 | bytes 12725248 | tf_op jit(solution)/shard_map/project_qkv/pallas_call | solution.py:212
  92.6 2.2 pad_maximum_fusion.1
  95.2 2.1 pad_maximum_fusion
  98.0 6.2 %project_grad.1.do_ref = bf16[2560,256]{1,0:T(8,128)(2,1)} custom-call(s32[6]{0:T(128)} %stack.19.ids, bf16[640,1024]{1,0:T(8,128)(2,1)} %collective-permute-done.14.refs_0_.refs_4_, bf16[640,1024]{1,0:T(8,128)(2,1)} %collective-permute-done.15.refs_1_.refs_5_, bf16[640,1024]{1,0:T(8,128)(2,1)} %collective-permute-done.11.refs_2_.refs_6_, ...), custom_call_target="tpu_custom_call" | custom-call | flops 1342177280 | bytes 7077888 | tf_op jit(solution)/shard_map/project_grad/pallas_call | solution.py:212
  104.3 55.2 %attention.1 = (bf16[2560,256]{1,0:T(8,128)(2,1)}, bf16[2560,256]{1,0:T(8,128)(2,1)}, bf16[2560,256]{1,0:T(8,128)(2,1)}, bf16[2560,256]{1,0:T(8,128)(2,1)}) custom-call(s32[1,20,5]{2,1,0:T(8,128)} %stack.20.info, bf16[2560,256]{1,0:T(8,128)(2,1)} %get-tuple-element.183.q_ref, bf16[2560,256]{1,0:T(8,128)(2,1)} %project_grad.1.do_ref, ...), custom_call_target="tpu_custom_call" | custom-call | flops 31406948352 | bytes 12451840 | tf_op jit(solution)/shard_map/attention/pallas_call | solution.py:212
  159.5 7.6 %project_context.1 = (bf16[2,640,1024]{2,1,0:T(8,128)(2,1)}, bf16[2,640,1024]{2,1,0:T(8,128)(2,1)}) custom-call(s32[6]{0:T(128)} %stack.19.ids, bf16[2560,256]{1,0:T(8,128)(2,1)} %get-tuple-element.204.ctx.ctx_ref, bf16[128,256]{1,0:T(8,128)(2,1)} %bitcast.64, bf16[128,256]{1,0:T(8,128)(2,1)} %copy-done.16, bf16[256,256]{1,0:T(8,128)(2,1)} %copy-done.21, ...), custom_call_target="tpu_custom_call" | custom-call | flops 1342177280 | bytes 7077888 | tf_op jit(solution)/shard_map/project_context/pallas_call | solution.py:212
  168.5 16.6 %attention_weights.1 = (bf16[2560,768]{1,0:T(8,128)(2,1)}, f32[8,768]{1,0:T(8,128)}, bf16[4,128,512]{2,1,0:T(8,128)(2,1)}, bf16[4,128,512]{2,1,0:T(8,128)(2,1)},...) custom-call(s32[6]{0:T(128)} %stack.19.ids, s32[1,20,5]{2,1,0:T(8,128)} %stack.20.info, ...), custom_call_target="tpu_custom_call" | custom-call | flops 5368709120 | bytes 23756800 | tf_op jit(solution)/shard_map/attention_weights/pallas_call | solution.py:212
  185.1 2.8 add_terms.12
  189.2 1.5 collective-permute-start.20
  190.7 1.5 collective-permute-start.21
  192.3 41.9 %mlp.1 = (bf16[2,640,1024]{2,1,0:T(8,128)(2,1)}, bf16[2,640,1024]{2,1,0:T(8,128)(2,1)}, bf16[2560,1024]{1,0:T(8,128)(2,1)}, f32[8,1024]{1,0:T(8,128)}, bf16[4,12...) custom-call(s32[6]{0:T(128)} %stack.19.ids, ...), custom_call_target="tpu_custom_call" | custom-call | flops 26843545600 | bytes 29405184 | tf_op jit(solution)/shard_map/mlp/pallas_call | solution.py:212
  235.1 1.8 add_terms.14
  236.8 1.8 add_terms.13
  239.6 2.7 add_terms.15
  244.0 1.4 collective-permute-start.24
  245.4 1.5 collective-permute-start.25
  246.9 18.7 %norm_backward.1 = (bf16[2,640,1024]{2,1,0:T(8,128)(2,1)}, bf16[2,640,1024]{2,1,0:T(8,128)(2,1)}, f32[8,1024]{1,0:T(8,128)}) custom-call(s32[6]{0:T(128)} %stack.19.ids, bf16[2560,768]{1,0:T(8,128)(2,1)} %get-tuple-element.215.grads_ref, bf16[2560,1024]{1,0:T(8,128)(2,1)} %get-tuple-element.246.hidden_ref, bf16[640,1024]{1,0:T(8,128)(2,1)} %collective-permute-done.6.refs_0_, ...), custom_call_target="tpu_custom_call" | custom-call | flops 9395240960 | bytes 23371776 | tf_op jit(solution)/shard_map/norm_backward/pallas_call | solution.py:212
  265.6 3.6 collective-permute-done.26.refs_1_
  269.8 4.1 %collective-permute-done.24.refs_2_ = bf16[2,128,512]{2,1,0:T(8,128)(2,1)S(1)} collective-permute-done((bf16[2,128,512]{2,1,0:T(8,128)(2,1)}, bf16[2,128,512]{2,1,0:T(8,128)(2,1)S(1)}, u32[]{:S(2)}, u32[]{:S(2)}) %collective-permute-start.24) | collective-permute-done | bytes 262176 | tf_op jit(solution)/shard_map/ppermute | solution.py:46
  276.3 1.4 dynamic_update_slice.7
  279.1 1.4 dynamic_update_slice.6
  280.5 1.7 add_terms.17
  282.2 1.7 add_terms.16
  284.0 2.0 add_terms.19
  285.9 1.9 add_terms.18
  287.9 3.3 add_terms.21
  291.2 1.9 add_terms.20
  293.1 1.5 collective-permute-start.29
  295.0 1.5 collective-permute-start.34
  297.1 3.2 collective-permute-start.31
  300.4 7.4 %finish_output.1 = (f32[640,1024]{1,0:T(8,128)}, f32[8,1024]{1,0:T(8,128)}) custom-call(f32[640,1024]{1,0:T(8,128)} %stream_ref, bf16[2,640,1024]{2,1,0:T(8,128)(2,1)} %get-tuple-element.216.refs_0_, bf16[2,640,1024]{2,1,0:T(8,128)(2,1)} %collective-permute-done.18.refs_1_, bf16[1,640,1024]{2,1,0:T(8,128)(2,1)} %collective-permute-done.19.refs_2_, ...), custom_call_target="tpu_custom_call" | custom-call | flops 10485760 | bytes 18391040 | tf_op jit(solution)/shard_map/finish_output/pallas_call | solution.py:212
  310.4 1.3 constant_dynamic-update-slice_fusion.1
  311.8 1.3 constant_dynamic-update-slice_fusion
  313.1 1.6 rsqrt.7.std_ref
  316.1 1.8 collective-permute-start.35
  319.0 1.4 collective-permute-done.35
  320.4 3.0 collective-permute-start.36
  324.4 1.9 add_terms.23
  326.3 1.9 add_terms.22
  332.3 2.3 collective-permute-start.41
  334.6 15.6 %collective-permute-done.40 = bf16[1,128,1024]{2,1,0:T(8,128)(2,1)S(1)} collective-permute-done((bf16[1,128,1024]{2,1,0:T(8,128)(2,1)}, bf16[1,128,1024]{2,1,0:T(8,128)(2,1)S(1)}, u32[]{:S(2)}, u32[]{:S(2)}) %collective-permute-start.40) | collective-permute-done | bytes 262176 | tf_op jit(solution)/shard_map/ppermute | solution.py:46
  351.5 3.0 collective-permute-done.41
  355.8 1.5 collective-permute-start.39
  359.2 6.4 %finish_grad.1 = f32[640,1024]{1,0:T(8,128)} custom-call(bf16[640,1024]{1,0:T(8,128)(2,1)} %grad_ref, f32[640,1024]{1,0:T(8,128)} %get-tuple-element.382.norm_ref, f32[640,1]{1,0:T(8,128)} %rsqrt.7.std_ref, bf16[2,640,1024]{2,1,0:T(8,128)(2,1)} %get-tuple-element.255.refs_0_, bf16[2,640,1024]{2,1,0:T(8,128)(2,1)} %collective-permute-done.28.refs_1_, ...), custom_call_target="tpu_custom_call" | custom-call | flops 7864320 | bytes 13109760 | tf_op jit(solution)/shard_map/finish_grad/pallas_call | solution.py:212
  (196 shorter events, 42.8 us)
Async XLA Ops:
  3.6 10.8 %copy-start.22 = (f32[1024,128]{1,0:T(8,128)S(1)}, f32[1024,128]{1,0:T(8,128)}, u32[]{:S(2)}) copy-start(f32[1024,128]{1,0:T(8,128)} %param.29) | copy-start | bytes 1572868
  5.9 8.7 %copy-start.23 = (f32[128,1024]{1,0:T(8,128)S(1)}, f32[128,1024]{1,0:T(8,128)}, u32[]{:S(2)}) copy-start(f32[128,1024]{1,0:T(8,128)} %param.27) | copy-start | bytes 1572868
  5.9 32.0 %collective-permute-start = (bf16[640,1024]{1,0:T(8,128)(2,1)}, bf16[640,1024]{1,0:T(8,128)(2,1)}, u32[]{:S(2)}, u32[]{:S(2)}) collective-permute-start(bf16[640,1024]{1,0:T(8,128)(2,1)} %get-tuple-element.170.refs_3_), channel_id=1, source_target_pairs={{0,2},{1,3},{2,0},{3,1},{4,6},{5,7},{6,4},{7,5},{8,10},{9,11},{10,... | collective-permute-start | bytes 3932168 | tf_op jit(solution)/shard_map/ppermute | solution.py:46
  9.2 11.5 %collective-permute-start.1 = (bf16[128,768]{1,0:T(8,128)(2,1)S(1)}, bf16[128,768]{1,0:T(8,128)(2,1)S(1)}, u32[]{:S(2)}, u32[]{:S(2)}) collective-permute-start(bf16[128,768]{1,0:T(8,128)(2,1)S(1)} %copy.128), channel_id=1, source_target_pairs={{0,16},{4,20},{8,24},{12,28},{16,0},{20,4},{24,8},{28,12},{1,17},{... | collective-permute-start | bytes 589832 | tf_op jit(solution)/shard_map/ppermute | solution.py:46
  12.8 48.7 %copy-start.11 = (bf16[256,128]{0,1:T(8,128)(2,1)}, bf16[256,128]{0,1:T(8,128)(2,1)S(1)}, u32[]{:S(2)}) copy-start(bf16[256,128]{0,1:T(8,128)(2,1)S(1)} %copy.129) | copy-start | bytes 196612
  12.9 4.3 %collective-permute-start.2 = (bf16[128,256]{1,0:T(8,128)(2,1)S(1)}, bf16[128,256]{1,0:T(8,128)(2,1)S(1)}, u32[]{:S(2)}, u32[]{:S(2)}) collective-permute-start(bf16[128,256]{1,0:T(8,128)(2,1)S(1)} %bitcast.60), channel_id=1, source_target_pairs={{0,4},{4,0},{8,12},{12,8},{16,20},{20,16},{24,28},{28,24},{1,5},{5... | collective-permute-start | bytes 196616 | tf_op jit(solution)/shard_map/ppermute | solution.py:46
  14.6 78.0 %copy-start.6 = (bf16[1024,128]{0,1:T(8,128)(2,1)}, bf16[1024,128]{0,1:T(8,128)(2,1)S(1)}, u32[]{:S(2)}) copy-start(bf16[1024,128]{0,1:T(8,128)(2,1)S(1)} %copy.130) | copy-start | bytes 786436
  14.6 80.6 %copy-start.5 = (bf16[128,1024]{1,0:T(8,128)(2,1)}, bf16[128,1024]{1,0:T(8,128)(2,1)S(1)}, u32[]{:S(2)}) copy-start(bf16[128,1024]{1,0:T(8,128)(2,1)S(1)} %convert_element_type.124.refs_8_) | copy-start | bytes 786436
  17.2 44.3 %copy-start.16 = (bf16[128,256]{1,0:T(8,128)(2,1)}, bf16[128,256]{1,0:T(8,128)(2,1)S(1)}, u32[]{:S(2)}) copy-start(bf16[128,256]{1,0:T(8,128)(2,1)S(1)} %collective-permute-done.2.refs_5_.refs_1_) | copy-start | bytes 196612
  20.7 28.5 %copy-start.15 = (bf16[128,768]{1,0:T(8,128)(2,1)}, bf16[128,768]{1,0:T(8,128)(2,1)S(1)}, u32[]{:S(2)}) copy-start(bf16[128,768]{1,0:T(8,128)(2,1)S(1)} %collective-permute-done.1.refs_5_) | copy-start | bytes 589828
  20.9 28.3 %copy-start.32 = (s32[2560]{0:T(1024)S(1)}, s32[2560]{0:T(1024)}, u32[]{:S(2)}) copy-start(s32[2560]{0:T(1024)} %param.17) | copy-start | bytes 30724
  20.9 38.8 %copy-start.1 = (bf16[640,1024]{1,0:T(8,128)(2,1)S(1)}, bf16[640,1024]{1,0:T(8,128)(2,1)}, u32[]{:S(2)}) copy-start(bf16[640,1024]{1,0:T(8,128)(2,1)} %grad_ref) | copy-start | bytes 3932164
  20.9 12.8 %collective-permute-start.3 = (bf16[256,768]{1,0:T(8,128)(2,1)S(1)}, bf16[256,768]{1,0:T(8,128)(2,1)S(1)}, u32[]{:S(2)}, u32[]{:S(2)}) collective-permute-start(bf16[256,768]{1,0:T(8,128)(2,1)S(1)} %pad_maximum_fusion.6), channel_id=1, source_target_pairs={{0,8},{4,12},{8,0},{12,4},{16,24},{20,28},{24,16},{28,20},{1,9},{5... | collective-permute-start | bytes 1179656 | tf_op jit(solution)/shard_map/ppermute | solution.py:46
  21.7 11.4 %collective-permute-start.4 = (bf16[256,256]{1,0:T(8,128)(2,1)S(1)}, bf16[256,256]{1,0:T(8,128)(2,1)S(1)}, u32[]{:S(2)}, u32[]{:S(2)}) collective-permute-start(bf16[256,256]{1,0:T(8,128)(2,1)S(1)} %pad_maximum_fusion.9), channel_id=1, source_target_pairs={{0,16},{4,20},{8,24},{12,28},{16,0},{20,4},{24,8},{28,12},{1,17},{... | collective-permute-start | bytes 393224 | tf_op jit(solution)/shard_map/ppermute | solution.py:46
  33.0 28.5 %copy-start.21 = (bf16[256,256]{1,0:T(8,128)(2,1)}, bf16[256,256]{1,0:T(8,128)(2,1)S(1)}, u32[]{:S(2)}) copy-start(bf16[256,256]{1,0:T(8,128)(2,1)S(1)} %collective-permute-done.4.refs_6_.refs_2_) | copy-start | bytes 393220
  37.9 34.3 %collective-permute-start.5 = (bf16[640,1024]{1,0:T(8,128)(2,1)}, bf16[640,1024]{1,0:T(8,128)(2,1)}, u32[]{:S(2)}, u32[]{:S(2)}) collective-permute-start(bf16[640,1024]{1,0:T(8,128)(2,1)} %get-tuple-element.170.refs_3_), channel_id=1, source_target_pairs={{0,1},{1,0},{2,3},{3,2},{4,5},{5,4},{6,7},{7,6},{8,9},{9,8},{10,11... | collective-permute-start | bytes 3932168 | tf_op jit(solution)/shard_map/ppermute | solution.py:46
  37.9 34.3 %collective-permute-start.6 = (bf16[640,1024]{1,0:T(8,128)(2,1)}, bf16[640,1024]{1,0:T(8,128)(2,1)}, u32[]{:S(2)}, u32[]{:S(2)}) collective-permute-start(bf16[640,1024]{1,0:T(8,128)(2,1)} %collective-permute-done.refs_2_), channel_id=1, source_target_pairs={{0,1},{1,0},{2,3},{3,2},{4,5},{5,4},{6,7},{7,6},{8,9},{9,8},{10,11... | collective-permute-start | bytes 3932168 | tf_op jit(solution)/shard_map/ppermute | solution.py:46
  38.4 21.3 %collective-permute-start.10 = (bf16[128,1024]{1,0:T(8,128)(2,1)S(1)}, bf16[128,1024]{1,0:T(8,128)(2,1)S(1)}, u32[]{:S(2)}, u32[]{:S(2)}) collective-permute-start(bf16[128,1024]{1,0:T(8,128)(2,1)S(1)} %bitcast.54), channel_id=1, source_target_pairs={{0,16},{4,20},{8,24},{12,28},{16,0},{20,4},{24,8},{28,12},{1,17},{... | collective-permute-start | bytes 786440 | tf_op jit(solution)/shard_map/ppermute | solution.py:46
  41.3 23.3 %collective-permute-start.9 = (bf16[128,1024]{1,0:T(8,128)(2,1)S(1)}, bf16[128,1024]{1,0:T(8,128)(2,1)S(1)}, u32[]{:S(2)}, u32[]{:S(2)}) collective-permute-start(bf16[128,1024]{1,0:T(8,128)(2,1)S(1)} %convert_element_type.124.refs_8_), channel_id=1, source_target_pairs={{0,16},{4,20},{8,24},{12,28},{16,0},{20,4},{24,8},{28,12},{1,17},{... | collective-permute-start | bytes 786440 | tf_op jit(solution)/shard_map/ppermute | solution.py:46
  41.5 23.8 %copy-start.31 = (s32[2560]{0:T(1024)S(1)}, s32[2560]{0:T(1024)}, u32[]{:S(2)}) copy-start(s32[2560]{0:T(1024)} %param.18) | copy-start | bytes 30724
  43.5 28.7 %collective-permute-start.7 = (bf16[512,768]{1,0:T(8,128)(2,1)}, bf16[512,768]{1,0:T(8,128)(2,1)}, u32[]{:S(2)}, u32[]{:S(2)}) collective-permute-start(bf16[512,768]{1,0:T(8,128)(2,1)} %pad_maximum_fusion.2), channel_id=1, source_target_pairs={{0,4},{4,0},{8,12},{12,8},{16,20},{20,16},{24,28},{28,24},{1,5},{5... | collective-permute-start | bytes 2359304 | tf_op jit(solution)/shard_map/ppermute | solution.py:46
  59.7 20.8 %copy-start.14 = (bf16[128,1024]{1,0:T(8,128)(2,1)}, bf16[128,1024]{1,0:T(8,128)(2,1)S(1)}, u32[]{:S(2)}) copy-start(bf16[128,1024]{1,0:T(8,128)(2,1)S(1)} %collective-permute-done.10.refs_13_) | copy-start | bytes 786436
  59.7 32.2 %collective-permute-start.11 = (bf16[640,1024]{1,0:T(8,128)(2,1)S(1)}, bf16[640,1024]{1,0:T(8,128)(2,1)}, u32[]{:S(2)}, u32[]{:S(2)}) collective-permute-start(bf16[640,1024]{1,0:T(8,128)(2,1)S(1)} %copy-done.1), channel_id=1, source_target_pairs={{0,2},{1,3},{2,0},{3,1},{4,6},{5,7},{6,4},{7,5},{8,10},{9,11},{10,... | collective-permute-start | bytes 3932168 | tf_op jit(solution)/shard_map/ppermute | solution.py:46
  64.6 15.9 %copy-start.12 = (bf16[128,1024]{1,0:T(8,128)(2,1)}, bf16[128,1024]{1,0:T(8,128)(2,1)S(1)}, u32[]{:S(2)}) copy-start(bf16[128,1024]{1,0:T(8,128)(2,1)S(1)} %collective-permute-done.9.refs_9_) | copy-start | bytes 786436
  64.6 7.6 %collective-permute-start.8 = (bf16[512,256]{1,0:T(8,128)(2,1)S(1)}, bf16[512,256]{1,0:T(8,128)(2,1)S(1)}, u32[]{:S(2)}, u32[]{:S(2)}) collective-permute-start(bf16[512,256]{1,0:T(8,128)(2,1)S(1)} %pad_maximum_fusion.8), channel_id=1, source_target_pairs={{0,8},{4,12},{8,0},{12,4},{16,24},{20,28},{24,16},{28,20},{1,9},{5... | collective-permute-start | bytes 786440 | tf_op jit(solution)/shard_map/ppermute | solution.py:46
  73.1 18.9 %collective-permute-start.13 = (bf16[256,1024]{1,0:T(8,128)(2,1)}, bf16[256,1024]{1,0:T(8,128)(2,1)}, u32[]{:S(2)}, u32[]{:S(2)}) collective-permute-start(bf16[256,1024]{1,0:T(8,128)(2,1)} %pad_maximum_fusion.4), channel_id=1, source_target_pairs={{0,4},{4,0},{8,12},{12,8},{16,20},{20,16},{24,28},{28,24},{1,5},{5... | collective-permute-start | bytes 1572872 | tf_op jit(solution)/shard_map/ppermute | solution.py:46
  75.3 16.7 %collective-permute-start.12 = (bf16[256,1024]{1,0:T(8,128)(2,1)}, bf16[256,1024]{1,0:T(8,128)(2,1)}, u32[]{:S(2)}, u32[]{:S(2)}) collective-permute-start(bf16[256,1024]{1,0:T(8,128)(2,1)} %pad_maximum_fusion.3), channel_id=1, source_target_pairs={{0,8},{4,12},{8,0},{12,4},{16,24},{20,28},{24,16},{28,20},{1,9},{5... | collective-permute-start | bytes 1572872 | tf_op jit(solution)/shard_map/ppermute | solution.py:46
  92.0 6.0 %collective-permute-start.14 = (bf16[640,1024]{1,0:T(8,128)(2,1)}, bf16[640,1024]{1,0:T(8,128)(2,1)}, u32[]{:S(2)}, u32[]{:S(2)}) collective-permute-start(bf16[640,1024]{1,0:T(8,128)(2,1)} %collective-permute-done.11.refs_2_.refs_6_), channel_id=1, source_target_pairs={{0,1},{1,0},{2,3},{3,2},{4,5},{5,4},{6,7},{7,6},{8,9},{9,8},{10,11... | collective-permute-start | bytes 3932168 | tf_op jit(solution)/shard_map/ppermute | solution.py:46
  92.1 5.9 %collective-permute-start.15 = (bf16[640,1024]{1,0:T(8,128)(2,1)S(1)}, bf16[640,1024]{1,0:T(8,128)(2,1)}, u32[]{:S(2)}, u32[]{:S(2)}) collective-permute-start(bf16[640,1024]{1,0:T(8,128)(2,1)S(1)} %copy-done.1), channel_id=1, source_target_pairs={{0,1},{1,0},{2,3},{3,2},{4,5},{5,4},{6,7},{7,6},{8,9},{9,8},{10,11... | collective-permute-start | bytes 3932168 | tf_op jit(solution)/shard_map/ppermute | solution.py:46
  94.8 64.7 %collective-permute-start.17 = (bf16[512,1024]{1,0:T(8,128)(2,1)}, bf16[512,1024]{1,0:T(8,128)(2,1)}, u32[]{:S(2)}, u32[]{:S(2)}) collective-permute-start(bf16[512,1024]{1,0:T(8,128)(2,1)} %pad_maximum_fusion.1), channel_id=1, source_target_pairs={{0,8},{4,12},{8,0},{12,4},{16,24},{20,28},{24,16},{28,20},{1,9},{5... | collective-permute-start | bytes 3145736 | tf_op jit(solution)/shard_map/ppermute | solution.py:46
  97.3 62.2 %collective-permute-start.16 = (bf16[512,1024]{1,0:T(8,128)(2,1)}, bf16[512,1024]{1,0:T(8,128)(2,1)}, u32[]{:S(2)}, u32[]{:S(2)}) collective-permute-start(bf16[512,1024]{1,0:T(8,128)(2,1)} %pad_maximum_fusion), channel_id=1, source_target_pairs={{0,4},{4,0},{8,12},{12,8},{16,20},{20,16},{24,28},{28,24},{1,5},{5... | collective-permute-start | bytes 3145736 | tf_op jit(solution)/shard_map/ppermute | solution.py:46
  167.2 17.9 %collective-permute-start.18 = (bf16[2,640,1024]{2,1,0:T(8,128)(2,1)}, bf16[2,640,1024]{2,1,0:T(8,128)(2,1)}, u32[]{:S(2)}, u32[]{:S(2)}) collective-permute-start(bf16[2,640,1024]{2,1,0:T(8,128)(2,1)} %get-tuple-element.214), channel_id=1, source_target_pairs={{0,1},{1,0},{2,3},{3,2},{4,5},{5,4},{6,7},{7,6},{8,9},{9,8},{10,11... | collective-permute-start | bytes 7864328 | tf_op jit(solution)/shard_map/ppermute | solution.py:46
  187.9 46.3 %collective-permute-start.19 = (bf16[1,640,1024]{2,1,0:T(8,128)(2,1)}, bf16[1,640,1024]{2,1,0:T(8,128)(2,1)}, u32[]{:S(2)}, u32[]{:S(2)}) collective-permute-start(bf16[1,640,1024]{2,1,0:T(8,128)(2,1)} %add_terms.12), channel_id=1, source_target_pairs={{0,2},{1,3},{2,0},{3,1},{4,6},{5,7},{6,4},{7,5},{8,10},{9,11},{10,... | collective-permute-start | bytes 3932168 | tf_op jit(solution)/shard_map/ppermute | solution.py:46
  189.2 45.0 %collective-permute-start.20 = (bf16[4,128,512]{2,1,0:T(8,128)(2,1)}, bf16[4,128,512]{2,1,0:T(8,128)(2,1)S(1)}, u32[]{:S(2)}, u32[]{:S(2)}) collective-permute-start(bf16[4,128,512]{2,1,0:T(8,128)(2,1)} %get-tuple-element.236), channel_id=1, source_target_pairs={{0,4},{4,0},{8,12},{12,8},{16,20},{20,16},{24,28},{28,24},{1,5},{5... | collective-permute-start | bytes 1572872 | tf_op jit(solution)/shard_map/ppermute | solution.py:46
  190.7 43.5 %collective-permute-start.21 = (bf16[4,128,512]{2,1,0:T(8,128)(2,1)S(1)}, bf16[4,128,512]{2,1,0:T(8,128)(2,1)S(1)}, u32[]{:S(2)}, u32[]{:S(2)}) collective-permute-start(bf16[4,128,512]{2,1,0:T(8,128)(2,1)S(1)} %copy-done.34), channel_id=1, source_target_pairs={{0,8},{4,12},{8,0},{12,4},{16,24},{20,28},{24,16},{28,20},{1,9},{5... | collective-permute-start | bytes 1572872 | tf_op jit(solution)/shard_map/ppermute | solution.py:46
  234.3 5.3 %collective-permute-start.22 = (bf16[2,640,1024]{2,1,0:T(8,128)(2,1)}, bf16[2,640,1024]{2,1,0:T(8,128)(2,1)}, u32[]{:S(2)}, u32[]{:S(2)}) collective-permute-start(bf16[2,640,1024]{2,1,0:T(8,128)(2,1)} %get-tuple-element.240), channel_id=1, source_target_pairs={{0,1},{1,0},{2,3},{3,2},{4,5},{5,4},{6,7},{7,6},{8,9},{9,8},{10,11... | collective-permute-start | bytes 7864328 | tf_op jit(solution)/shard_map/ppermute | solution.py:46
  242.3 31.6 %copy-start.2 = (bf16[640,1024]{1,0:T(8,128)(2,1)S(1)}, bf16[640,1024]{1,0:T(8,128)(2,1)}, u32[]{:S(2)}) copy-start(bf16[640,1024]{1,0:T(8,128)(2,1)} %grad_ref) | copy-start | bytes 3932164
  242.3 31.6 %collective-permute-start.23 = (bf16[1,640,1024]{2,1,0:T(8,128)(2,1)}, bf16[1,640,1024]{2,1,0:T(8,128)(2,1)}, u32[]{:S(2)}, u32[]{:S(2)}) collective-permute-start(bf16[1,640,1024]{2,1,0:T(8,128)(2,1)} %add_terms.15), channel_id=1, source_target_pairs={{0,2},{1,3},{2,0},{3,1},{4,6},{5,7},{6,4},{7,5},{8,10},{9,11},{10,... | collective-permute-start | bytes 3932168 | tf_op jit(solution)/shard_map/ppermute | solution.py:46
  242.8 26.4 %collective-permute-start.26 = (bf16[4,128,1024]{2,1,0:T(8,128)(2,1)}, bf16[4,128,1024]{2,1,0:T(8,128)(2,1)}, u32[]{:S(2)}, u32[]{:S(2)}) collective-permute-start(bf16[4,128,1024]{2,1,0:T(8,128)(2,1)} %get-tuple-element.253), channel_id=1, source_target_pairs={{0,4},{4,0},{8,12},{12,8},{16,20},{20,16},{24,28},{28,24},{1,5},{5... | collective-permute-start | bytes 3145736 | tf_op jit(solution)/shard_map/ppermute | solution.py:46
  243.4 26.4 %collective-permute-start.27 = (bf16[4,128,1024]{2,1,0:T(8,128)(2,1)}, bf16[4,128,1024]{2,1,0:T(8,128)(2,1)}, u32[]{:S(2)}, u32[]{:S(2)}) collective-permute-start(bf16[4,128,1024]{2,1,0:T(8,128)(2,1)} %get-tuple-element.254), channel_id=1, source_target_pairs={{0,8},{4,12},{8,0},{12,4},{16,24},{20,28},{24,16},{28,20},{1,9},{5... | collective-permute-start | bytes 3145736 | tf_op jit(solution)/shard_map/ppermute | solution.py:46
  244.0 29.8 %collective-permute-start.24 = (bf16[2,128,512]{2,1,0:T(8,128)(2,1)}, bf16[2,128,512]{2,1,0:T(8,128)(2,1)S(1)}, u32[]{:S(2)}, u32[]{:S(2)}) collective-permute-start(bf16[2,128,512]{2,1,0:T(8,128)(2,1)} %add_terms.13), channel_id=1, source_target_pairs={{0,8},{4,12},{8,0},{12,4},{16,24},{20,28},{24,16},{28,20},{1,9},{5... | collective-permute-start | bytes 786440 | tf_op jit(solution)/shard_map/ppermute | solution.py:46
  245.4 28.4 %collective-permute-start.25 = (bf16[2,128,512]{2,1,0:T(8,128)(2,1)}, bf16[2,128,512]{2,1,0:T(8,128)(2,1)S(1)}, u32[]{:S(2)}, u32[]{:S(2)}) collective-permute-start(bf16[2,128,512]{2,1,0:T(8,128)(2,1)} %add_terms.14), channel_id=1, source_target_pairs={{0,4},{4,0},{8,12},{12,8},{16,20},{20,16},{24,28},{28,24},{1,5},{5... | collective-permute-start | bytes 786440 | tf_op jit(solution)/shard_map/ppermute | solution.py:46
  273.8 8.4 %copy-start.19 = (bf16[2,128,512]{2,1,0:T(8,128)(2,1)}, bf16[2,128,512]{2,1,0:T(8,128)(2,1)S(1)}, u32[]{:S(2)}) copy-start(bf16[2,128,512]{2,1,0:T(8,128)(2,1)S(1)} %collective-permute-done.24.refs_2_) | copy-start | bytes 786436
  273.8 14.0 %collective-permute-start.28 = (bf16[2,640,1024]{2,1,0:T(8,128)(2,1)}, bf16[2,640,1024]{2,1,0:T(8,128)(2,1)}, u32[]{:S(2)}, u32[]{:S(2)}) collective-permute-start(bf16[2,640,1024]{2,1,0:T(8,128)(2,1)} %get-tuple-element.256), channel_id=1, source_target_pairs={{0,1},{1,0},{2,3},{3,2},{4,5},{5,4},{6,7},{7,6},{8,9},{9,8},{10,11... | collective-permute-start | bytes 7864328 | tf_op jit(solution)/shard_map/ppermute | solution.py:46
  293.1 14.7 %collective-permute-start.29 = (bf16[1,160,1024]{2,1,0:T(8,128)(2,1)}, bf16[1,160,1024]{2,1,0:T(8,128)(2,1)S(1)}, u32[]{:S(2)}, u32[]{:S(2)}) collective-permute-start(bf16[1,160,1024]{2,1,0:T(8,128)(2,1)} %add_terms.20), channel_id=1, source_target_pairs={{0,2},{1,3},{2,0},{3,1},{4,6},{5,7},{6,4},{7,5},{8,10},{9,11},{10,... | collective-permute-start | bytes 983048 | tf_op jit(solution)/shard_map/ppermute | solution.py:46
  294.5 21.5 %collective-permute-start.33 = (bf16[2,128,1024]{2,1,0:T(8,128)(2,1)}, bf16[2,128,1024]{2,1,0:T(8,128)(2,1)S(1)}, u32[]{:S(2)}, u32[]{:S(2)}) collective-permute-start(bf16[2,128,1024]{2,1,0:T(8,128)(2,1)} %add_terms.18), channel_id=1, source_target_pairs={{0,8},{4,12},{8,0},{12,4},{16,24},{20,28},{24,16},{28,20},{1,9},{5... | collective-permute-start | bytes 1572872 | tf_op jit(solution)/shard_map/ppermute | solution.py:46
  295.0 21.0 %collective-permute-start.34 = (bf16[2,128,1024]{2,1,0:T(8,128)(2,1)}, bf16[2,128,1024]{2,1,0:T(8,128)(2,1)S(1)}, u32[]{:S(2)}, u32[]{:S(2)}) collective-permute-start(bf16[2,128,1024]{2,1,0:T(8,128)(2,1)} %add_terms.19), channel_id=1, source_target_pairs={{0,4},{4,0},{8,12},{12,8},{16,20},{20,16},{24,28},{28,24},{1,5},{5... | collective-permute-start | bytes 1572872 | tf_op jit(solution)/shard_map/ppermute | solution.py:46
  297.1 18.9 %collective-permute-start.31 = (bf16[1,128,512]{2,1,0:T(8,128)(2,1)}, bf16[1,128,512]{2,1,0:T(8,128)(2,1)}, u32[]{:S(2)}, u32[]{:S(2)}) collective-permute-start(bf16[1,128,512]{2,1,0:T(8,128)(2,1)} %add_terms.16), channel_id=1, source_target_pairs={{0,16},{4,20},{8,24},{12,28},{16,0},{20,4},{24,8},{28,12},{1,17},{... | collective-permute-start | bytes 393224 | tf_op jit(solution)/shard_map/ppermute | solution.py:46
  300.3 15.7 %collective-permute-start.32 = (bf16[1,128,512]{2,1,0:T(8,128)(2,1)}, bf16[1,128,512]{2,1,0:T(8,128)(2,1)S(1)}, u32[]{:S(2)}, u32[]{:S(2)}) collective-permute-start(bf16[1,128,512]{2,1,0:T(8,128)(2,1)} %add_terms.17), channel_id=1, source_target_pairs={{0,16},{4,20},{8,24},{12,28},{16,0},{20,4},{24,8},{28,12},{1,17},{... | collective-permute-start | bytes 393224 | tf_op jit(solution)/shard_map/ppermute | solution.py:46
  300.4 17.5 %copy-start.20 = (bf16[2,128,512]{2,1,0:T(8,128)(2,1)S(1)}, bf16[2,128,512]{2,1,0:T(8,128)(2,1)}, u32[]{:S(2)}) copy-start(bf16[2,128,512]{2,1,0:T(8,128)(2,1)} %copy-done.19) | copy-start | bytes 786436
  300.4 23.0 %copy-start.18 = (bf16[2,128,512]{2,1,0:T(8,128)(2,1)S(1)}, bf16[2,128,512]{2,1,0:T(8,128)(2,1)}, u32[]{:S(2)}) copy-start(bf16[2,128,512]{2,1,0:T(8,128)(2,1)} %copy-done.17) | copy-start | bytes 786436
  307.7 8.3 %copy-start.26 = (bf16[1,160,1024]{2,1,0:T(8,128)(2,1)}, bf16[1,160,1024]{2,1,0:T(8,128)(2,1)S(1)}, u32[]{:S(2)}) copy-start(bf16[1,160,1024]{2,1,0:T(8,128)(2,1)S(1)} %collective-permute-done.29.refs_2_) | copy-start | bytes 983044
  313.1 1.6 collective-permute-start.30
  314.6 41.2 %collective-permute-start.38 = (bf16[1,480,1024]{2,1,0:T(8,128)(2,1)}, bf16[1,480,1024]{2,1,0:T(8,128)(2,1)}, u32[]{:S(2)}, u32[]{:S(2)}) collective-permute-start(bf16[1,480,1024]{2,1,0:T(8,128)(2,1)} %add_terms.21), channel_id=1, source_target_pairs={{0,2},{1,3},{2,0},{3,1},{4,6},{5,7},{6,4},{7,5},{8,10},{9,11},{10,... | collective-permute-start | bytes 2949128 | tf_op jit(solution)/shard_map/ppermute | solution.py:46
  316.0 10.3 %copy-start.9 = (bf16[2,128,1024]{2,1,0:T(8,128)(2,1)}, bf16[2,128,1024]{2,1,0:T(8,128)(2,1)S(1)}, u32[]{:S(2)}) copy-start(bf16[2,128,1024]{2,1,0:T(8,128)(2,1)S(1)} %collective-permute-done.33.refs_2_) | copy-start | bytes 1572868
  316.1 8.3 %copy-start.7 = (bf16[2,128,1024]{2,1,0:T(8,128)(2,1)}, bf16[2,128,1024]{2,1,0:T(8,128)(2,1)S(1)}, u32[]{:S(2)}) copy-start(bf16[2,128,1024]{2,1,0:T(8,128)(2,1)S(1)} %collective-permute-done.34.refs_2_) | copy-start | bytes 1572868
  316.1 4.3 %collective-permute-start.35 = (f32[15360]{0:T(1024)S(1)}, f32[15360]{0:T(1024)S(1)}, u32[]{:S(2)}, u32[]{:S(2)}) collective-permute-start(f32[15360]{0:T(1024)S(1)} %add.195), channel_id=1, source_target_pairs={{0,8},{4,12},{8,0},{12,4},{16,24},{20,28},{24,16},{28,20},{1,9},{5... | collective-permute-start | bytes 184328 | tf_op jit(solution)/shard_map/ppermute | solution.py:46
  320.4 7.8 %collective-permute-start.36 = (f32[15360]{0:T(1024)S(1)}, f32[15360]{0:T(1024)}, u32[]{:S(2)}, u32[]{:S(2)}) collective-permute-start(f32[15360]{0:T(1024)S(1)} %add.196), channel_id=1, source_target_pairs={{0,16},{4,20},{8,24},{12,28},{16,0},{20,4},{24,8},{28,12},{1,17},{... | collective-permute-start | bytes 184328 | tf_op jit(solution)/shard_map/ppermute | solution.py:46
  329.1 21.2 %copy-start.10 = (bf16[2,128,1024]{2,1,0:T(8,128)(2,1)S(1)}, bf16[2,128,1024]{2,1,0:T(8,128)(2,1)}, u32[]{:S(2)}) copy-start(bf16[2,128,1024]{2,1,0:T(8,128)(2,1)} %copy-done.9) | copy-start | bytes 1572868
  329.1 21.2 %collective-permute-start.40 = (bf16[1,128,1024]{2,1,0:T(8,128)(2,1)}, bf16[1,128,1024]{2,1,0:T(8,128)(2,1)S(1)}, u32[]{:S(2)}, u32[]{:S(2)}) collective-permute-start(bf16[1,128,1024]{2,1,0:T(8,128)(2,1)} %add_terms.22), channel_id=1, source_target_pairs={{0,16},{4,20},{8,24},{12,28},{16,0},{20,4},{24,8},{28,12},{1,17},{... | collective-permute-start | bytes 786440 | tf_op jit(solution)/shard_map/ppermute | solution.py:46
  329.5 5.1 %collective-permute-start.37 = (f32[15360]{0:T(1024)S(1)}, f32[15360]{0:T(1024)S(1)}, u32[]{:S(2)}, u32[]{:S(2)}) collective-permute-start(f32[15360]{0:T(1024)S(1)} %add.197), channel_id=1, source_target_pairs={{0,4},{4,0},{8,12},{12,8},{16,20},{20,16},{24,28},{28,24},{1,5},{5... | collective-permute-start | bytes 184328 | tf_op jit(solution)/shard_map/ppermute | solution.py:46
  330.6 23.9 %copy-start.8 = (bf16[2,128,1024]{2,1,0:T(8,128)(2,1)S(1)}, bf16[2,128,1024]{2,1,0:T(8,128)(2,1)}, u32[]{:S(2)}) copy-start(bf16[2,128,1024]{2,1,0:T(8,128)(2,1)} %copy-done.7) | copy-start | bytes 1572868
  332.3 22.3 %collective-permute-start.41 = (bf16[1,128,1024]{2,1,0:T(8,128)(2,1)S(1)}, bf16[1,128,1024]{2,1,0:T(8,128)(2,1)S(1)}, u32[]{:S(2)}, u32[]{:S(2)}) collective-permute-start(bf16[1,128,1024]{2,1,0:T(8,128)(2,1)S(1)} %copy-done.28), channel_id=1, source_target_pairs={{0,16},{4,20},{8,24},{12,28},{16,0},{20,4},{24,8},{28,12},{1,17},{... | collective-permute-start | bytes 786440 | tf_op jit(solution)/shard_map/ppermute | solution.py:46
  355.8 9.8 %collective-permute-start.39 = (f32[15360]{0:T(1024)S(1)}, f32[15360]{0:T(1024)S(1)}, u32[]{:S(2)}, u32[]{:S(2)}) collective-permute-start(f32[15360]{0:T(1024)S(1)} %add.198), channel_id=1, source_target_pairs={{0,2},{1,3},{2,0},{3,1},{4,6},{5,7},{6,4},{7,5},{8,10},{9,11},{10,... | collective-permute-start | bytes 184328 | tf_op jit(solution)/shard_map/ppermute | solution.py:46
  (13 other events, 54.2 us)

commit v6 on v5

--- a/solution.py
+++ b/solution.py
@@ -17,7 +17,6 @@
 bf16 = jnp.bfloat16
 eps_norm = 1e-05
 masked_score = -1e30
-VMEM_MOST = 62 << 20
 
 
 def dot_nn(left, right):
@@ -54,11 +53,6 @@
     pieces = [block]
     for bit in bits[1:]:
         pieces = pieces + [swap(piece, axis, bit) for piece in pieces]
-    return pieces
-
-
-def gather_near(pieces, axis):
-    pieces = [x for piece in pieces for x in (piece, swap(piece, axis, 1))]
     return pieces
 
 
@@ -130,7 +124,7 @@
         while self.bits:
             self.swap()
             self.add()
-        return sum(x[at].astype(f32) for x, at in self.terms)
+        return self.terms
 
 
 def tie_halves(values, *halvings):
@@ -173,30 +167,39 @@
 
 
 class Tokens:
-    def __init__(self, pieces, order):
-        self.groups, (self.rows, self.model) = len(pieces), pieces[0].shape
-        self.arrays = [pieces[j] for j in order]
-        self.specs = [pl.BlockSpec(memory_space=pl.ANY)] * self.groups
+    def __init__(self, blocks, order):
+        blocks = [blocks[j] for j in order]
+        self.groups, self.counts = len(blocks), [len(block) for block in blocks]
+        self.rows, self.model = sum(x.shape[0] for x in blocks[0]), blocks[0][0].shape[1]
+        self.arrays = [x for block in blocks for x in block]
+        self.specs = [pl.BlockSpec(memory_space=pl.ANY)] * len(self.arrays)
 
     def scratch(self):
         return [
             pltpu.VMEM((2, self.rows, self.model), bf16),
-            pltpu.SemaphoreType.DMA((2,)),
+            pltpu.SemaphoreType.DMA((2, max(self.counts))),
         ]
 
     def fetch(self, refs, held, done, step):
-        def copy(at):
-            return pltpu.make_async_copy(refs[at], held.at[at % 2], done.at[at % 2])
+        def copies(at):
+            first, start, found = sum(self.counts[:at]), 0, []
+            for k, ref in enumerate(refs[first : first + self.counts[at]]):
+                where = held.at[at % 2, pl.ds(start, ref.shape[0]), :]
+                found.append(pltpu.make_async_copy(ref, where, done.at[at % 2, k]))
+                start += ref.shape[0]
+            return found
 
         for at in range(self.groups):
 
             @pl.when(step == at)
             def _(at=at):
-                if at == 0:
-                    copy(0).start()
+                ahead = copies(at) if at == 0 else []
                 if at + 1 < self.groups:
-                    copy(at + 1).start()
-                copy(at).wait()
+                    ahead = ahead + copies(at + 1)
+                for copy in ahead:
+                    copy.start()
+                for copy in copies(at):
+                    copy.wait()
 
 
 def store_halves(send, keep, total, number, order, columns=slice(None), source=slice(None)):
@@ -207,7 +210,9 @@
         where[at % half, :, columns] = block.astype(bf16)
 
 
-def call(kernel, name, grid, prefetch, operands, specs, outs, out_specs, scratch, flops, extra=0):
+def call(
+    kernel, name, grid, prefetch, operands, specs, outs, out_specs, scratch, flops, extra=0, room=12
+):
     size = sum(x.size * x.dtype.itemsize for x in list(operands) + list(outs))
     return pl.pallas_call(
         kernel,
@@ -220,7 +225,7 @@
         ),
         out_shape=outs,
         compiler_params=pltpu.CompilerParams(
-            dimension_semantics=("arbitrary",) * len(grid), vmem_limit_bytes=VMEM_MOST
+            dimension_semantics=("arbitrary",) * len(grid), vmem_limit_bytes=room << 20
         ),
         cost_estimate=pl.CostEstimate(
             flops=int(flops), bytes_accessed=int(size), transcendentals=int(extra)
@@ -309,6 +314,7 @@
         [own_block(rows, width)] * 3,
         sent.scratch() + weight_scratch(pack),
         2 * groups * rows * model * 3 * width,
+        room=14,
     )
 
 
@@ -468,6 +474,7 @@
         [pltpu.VMEM((NB, width, SEG), f32), pltpu.VMEM((NB, width, SEG), f32)],
         scores * width * 2 * 6 * 1.3,
         scores,
+        room=22,
     )
 
 
@@ -510,7 +517,7 @@
 
     def kernel(ids, info, ctx_ref, dq_ref, dk_ref, dv_ref, *refs):
         sent_refs, refs = refs[:held], refs[held:]
-        grad_refs, refs = refs[:held], refs[held:]
+        grad_refs, refs = refs[: len(grad.arrays)], refs[len(grad.arrays) :]
         gain, shift, cos, low, high, grads, bias_ref, *stacks = refs[:11]
         block, arrived, grad_block, grad_arrived, total, dense_total = refs[11:]
         step = pl.program_id(0)
@@ -563,6 +570,7 @@
         + grad.scratch()
         + [pltpu.VMEM((model, 3 * width), f32), pltpu.VMEM((model, width), f32)],
         2 * groups * rows * model * 4 * width,
+        room=24,
     )
 
 
@@ -572,7 +580,7 @@
 
     def kernel(ids, *refs):
         sent_refs, refs = refs[:held], refs[held:]
-        grad_refs, refs = refs[:held], refs[held:]
+        grad_refs, refs = refs[: len(grad.arrays)], refs[len(grad.arrays) :]
         fc_refs, refs = refs[:pieces], refs[pieces:]
         out_refs, refs = refs[:pieces], refs[pieces:]
         gain, shift, bias, part_send, part_keep, hidden_ref, bias_ref = refs[:7]
@@ -663,6 +671,7 @@
             pltpu.VMEM((model, units), f32),
         ],
         10 * groups * rows * model * units,
+        room=42,
     )
 
 
@@ -725,6 +734,7 @@
         half_blocks(groups, rows, model) + [resident(x.shape) for x in outs[2:]],
         sent.scratch() + weight_scratch(qkv_pack) + weight_scratch(fc),
         2 * groups * rows * model * (units + columns),
+        room=26,
     )
 
 
@@ -735,11 +745,9 @@
     ]
 
 
-def add_terms(terms, half, start=0, rows=None):
-    columns = terms[0][0].shape[2]
-    rows = terms[0][0].shape[1] if rows is None else rows
-    block = max(x for x in (320, 160, 128, 64) if rows % x == 0 and start % x == 0)
-    skip = start // block
+def add_terms(terms, half):
+    _, rows, columns = terms[0][0].shape
+    block = max(x for x in (320, 128, 64) if rows % x == 0)
 
     def kernel(*refs):
         refs[-1][...] = sum(x[...].astype(f32) for x in refs[:-1]).astype(bf16)
@@ -752,7 +760,7 @@
         (half, rows // block),
         [],
         [x for x, _ in terms],
-        [pl.BlockSpec(shape, lambda k, i, *_, at=at: (at + k, i + skip, 0)) for _, at in terms],
+        [pl.BlockSpec(shape, lambda k, i, *_, at=at: (at + k, i, 0)) for _, at in terms],
         [out],
         [pl.BlockSpec(shape, lambda k, i, *_: (k, i, 0))],
         [],
@@ -760,42 +768,186 @@
     )[0]
 
 
-def finish_output(stream, attn_terms, mlp_terms, dense_bias, out_bias):
+def add_split(terms, count):
+    _, rows, columns = terms[0][0].shape
+    block = rows // count
+
+    def kernel(*refs):
+        total = sum(x[...].astype(f32) for x in refs[:-2]).astype(bf16)
+
+        @pl.when(pl.program_id(0) == 0)
+        def _():
+            refs[-2][...] = total
+
+        @pl.when(pl.program_id(0) > 0)
+        def _():
+            refs[-1][...] = total
+
+    shape = (pl.Squeezed(), block, columns)
+    return call(
+        kernel,
+        "add_split",
+        (count,),
+        [],
+        [x for x, _ in terms],
+        [pl.BlockSpec(shape, lambda i, *_, at=at: (at, i, 0)) for _, at in terms],
+        [shaped(1, block, columns), shaped(1, rows - block, columns)],
+        [
+            pl.BlockSpec(shape, lambda i, *_: (0, 0, 0)),
+            pl.BlockSpec(shape, lambda i, *_: (0, jnp.maximum(i - 1, 0), 0)),
+        ],
+        [],
+        rows * columns * len(terms),
+    )
+
+
+def whole_terms(terms, count):
+    return [
+        pl.BlockSpec((count, *x.shape[1:]), lambda *_, at=at: (at // count, 0, 0)) for x, at in terms
+    ]
+
+
+def add_stacks(stacks):
+    counts = []
+    for parts in stacks:
+        parts.terms.append((parts.got, 0))
+        counts.append(parts.got.shape[0] // 2)
+    held = [len(parts.terms) for parts in stacks]
+    operands = [x for parts in stacks for x, _ in parts.terms]
+
+    def kernel(*refs):
+        for at, half in enumerate(counts):
+            first = sum(held[:at])
+            total = sum(x[...].astype(f32) for x in refs[first : first + held[at]])
+            refs[len(operands) + at][...] = total.astype(bf16)
+
+    outs = [shaped(n, *parts.got.shape[1:]) for n, parts in zip(counts, stacks)]
+    sends = call(
+        kernel,
+        "add_stacks",
+        (1,),
+        [],
+        operands,
+        [x for n, parts in zip(counts, stacks) for x in whole_terms(parts.terms, n)],
+        outs,
+        [resident(x.shape) for x in outs],
+        [],
+        sum(x.size for x in operands) // 2,
+        room=16,
+    )
+    for n, parts, send in zip(counts, stacks, sends):
+        parts.send = send
+        parts.terms = [(x, at + n) for x, at in parts.terms]
+
+
+def finish_mlp_weights(first, second):
+    held, (_, rows, units) = len(first), first[0][0].shape
+    half = units // 2
+
+    def kernel(*refs):
+        low = sum(x[0].astype(f32) for x in refs[:held])
+        high = sum(x[0].astype(f32) for x in refs[held:-2])
+        refs[-2][:, :half] = low[:, :half]
+        refs[-2][:, half:] = high[:, :half]
+        refs[-1][:half, :] = low[:, half:].T
+        refs[-1][half:, :] = high[:, half:].T
+
+    operands = [x for x, _ in [*first, *second]]
+    outs = [shaped(rows, units, dtype=f32), shaped(units, rows, dtype=f32)]
+    return call(
+        kernel,
+        "finish_mlp_weights",
+        (1,),
+        [],
+        operands,
+        whole_terms([*first, *second], 1),
+        outs,
+        [resident(x.shape) for x in outs],
+        [],
+        len(operands) * rows * units,
+    )
+
+
+def finish_attention_weights(first, second):
+    held, (_, rows, columns) = len(first), first[0][0].shape
+    width = columns // 2
+
+    def kernel(*refs):
+        low = sum(x[0].astype(f32) for x in refs[:held])
+        high = sum(x[0].astype(f32) for x in refs[held:-2])
+        for head in range(width // HD):
+            for kind, (source, start) in enumerate(((low, 0), (low, width), (high, 0))):
+                at = (3 * head + kind) * HD
+                own = start + head * HD
+                refs[-2][:, at : at + HD] = source[:, own : own + HD]
+        refs[-1][...] = high[:, width:].T
+
+    operands = [x for x, _ in [*first, *second]]
+    outs = [shaped(rows, 3 * width, dtype=f32), shaped(width, rows, dtype=f32)]
+    return call(
+        kernel,
+        "finish_attention_weights",
+        (1,),
+        [],
+        operands,
+        whole_terms([*first, *second], 1),
+        outs,
+        [resident(x.shape) for x in outs],
+        [],
+        len(operands) * rows * columns,
+    )
+
+
+def sum_rows(groups):
+    return (12 + groups + 7) // 8 * 8
+
+
+def finish_output(ids, stream, grad, attn_terms, mlp_terms, dense_bias, out_bias, norm_sums, fc_sums, qkv_sums, groups):
     rows, model = stream.shape
-    block = 128
+    block = 160
     first, second = len(attn_terms), len(mlp_terms)
-
-    def kernel(stream_ref, *refs):
+    units, columns = fc_sums.shape[1], qkv_sums.shape[1]
+    across = model // units
+
+    def kernel(ids, stream_ref, grad_ref, *refs):
         attn_refs, refs = refs[:first], refs[first:]
-        mlp_refs, (dense_bias, out_bias, out_ref, sums_ref) = refs[:second], refs[second:]
+        mlp_refs, refs = refs[:second], refs[second:]
+        dense_bias, out_bias, norm_ref, fc_ref, qkv_ref, out_ref, sums_ref = refs
 
         @pl.when(pl.program_id(0) == 0)
         def _():
             sums_ref[...] = jnp.zeros_like(sums_ref)
+            sums_ref[0:4, :] = norm_ref[0:4, :]
+            own = jnp.concatenate([fc_ref[0:1, :]] * across, axis=1) if across > 1 else fc_ref[0:1, :]
+            lane = lax.broadcasted_iota(jnp.int32, (1, model), 1) // units
+            sums_ref[pl.ds(8 + ids[0] // across, 1), :] = jnp.where(lane == ids[0] % across, own, 0.0)
+            sums_ref[pl.ds(12 + ids[0], 1), :columns] = qkv_ref[0:1, :]
 
         attn = sum(x[...].astype(f32) for x in attn_refs) + dense_bias[...]
         mlp = sum(x[...].astype(f32) for x in mlp_refs) + out_bias[...]
         output = stream_ref[...] + attn + mlp
         out_ref[...] = output
         for at, value in enumerate((output, attn, mlp)):
-            sums_ref[at : at + 1, :] += jnp.sum(value * value, axis=0, keepdims=True)
+            sums_ref[4 + at : 5 + at, :] += jnp.sum(value * value, axis=0, keepdims=True)
+        sums_ref[7:8, :] += jnp.sum(grad_ref[...].astype(f32), axis=0, keepdims=True)
 
     terms = [*attn_terms, *mlp_terms]
-    operands = [stream, *[x for x, _ in terms], dense_bias, out_bias]
-    outs = [shaped(rows, model, dtype=f32), shaped(8, model, dtype=f32)]
+    operands = [stream, grad, *[x for x, _ in terms], dense_bias, out_bias, norm_sums, fc_sums, qkv_sums]
+    outs = [shaped(rows, model, dtype=f32), shaped(sum_rows(groups), model, dtype=f32)]
     return call(
         kernel,
         "finish_output",
         (rows // block,),
-        [],
+        [ids],
         operands,
-        [step_block(block, model)]
+        [step_block(block, model), step_block(block, model)]
         + taken(terms, block)
-        + [resident(dense_bias.shape), resident(out_bias.shape)],
+        + [resident(x.shape) for x in operands[-5:]],
         outs,
         [step_block(block, model), resident(outs[1].shape)],
         [],
         rows * model * 16,
+        room=16,
     )
 
 
@@ -911,14 +1063,13 @@
     data_bits = bits_of(lax.axis_size("dp"))
     rows_first = data_bits[:0:-1] + data_bits[:1]
     columns_first = data_bits[:1] + data_bits[:0:-1]
-    between = data_bits[:1:-1] + data_bits[:2]
     near_bits = data_bits
     next_bits = data_bits[1:2] + data_bits[:1] + data_bits[2:]
 
     qkv_pack = Pack(by_kind(qkv_weight.astype(bf16), heads), "dp", rows_first)
     dense_pack = Pack(dense_weight.astype(bf16).T, "dp", columns_first)
     fc_pack = Pack(fc_weight.astype(bf16), "dp", rows_first)
-    out_pack = Pack(out_weight.astype(bf16).T, "dp", between)
+    out_pack = Pack(out_weight.astype(bf16).T, "dp", rows_first)
 
     row_mean = jnp.mean(stream_in, axis=-1, keepdims=True)
     centred = stream_in - row_mean
@@ -927,21 +1078,35 @@
     normalized = centred * inv_std
     sent = gather_far(normalized.astype(bf16), "tensor", tensor_bits)
 
+    sent_near, near = swap(sent[0], "tensor", 1), swap(out_grad, "tensor", 1)
     qkv_pack.double()
     dense_pack.double()
-    tie_packs(qkv_pack, dense_pack, fc_pack, out_pack)
-    fc_pack.double()
-    out_pack.double()
+    (near,) = tie_packs(qkv_pack, dense_pack, fc_pack, beside=[near])
     while len(qkv_pack.bits) > 1:
         qkv_pack.double()
         dense_pack.double()
-    out_grad, *sent = tie_packs(qkv_pack, dense_pack, beside=[out_grad, *sent])
-    grad = gather_far(out_grad, "tensor", tensor_bits)
-    sent = gather_near(sent, "tensor")
+    fc_pack.double()
+    cut = rows_local * 3 // 5
+    early, late = out_grad[:cut], out_grad[cut:]
+    early, late, sent_near, *sent = tie_packs(
+        qkv_pack, dense_pack, fc_pack, out_pack, beside=[early, late, sent_near, *sent]
+    )
+    early_far = gather_far(early, "tensor", tensor_bits)[1:]
+    sent_near = [sent_near] + [swap(x, "tensor", 1) for x in sent[1:]]
+    sent = [x for pair in zip(sent, sent_near) for x in pair]
     qkv_pack.double()
     dense_pack.double()
-    sent = tie_packs(qkv_pack, dense_pack, fc_pack, out_pack, beside=sent)
-    sent = Tokens(sent, order)
+    while len(fc_pack.bits) > 1:
+        fc_pack.double()
+    out_pack.double()
+    late, *done = tie_packs(
+        qkv_pack, dense_pack, fc_pack, out_pack, beside=[late, *sent, *early_far]
+    )
+    sent, early_far = Tokens([(x,) for x in done[:groups]], order), done[groups:]
+    late_far = gather_far(late, "tensor", tensor_bits)[1:]
+    early_near = [swap(x, "tensor", 1) for x in early_far]
+    while len(out_pack.bits) > 1:
+        out_pack.double()
 
     info = tree_table(segment_ids, parent_ids)
     tables = angle_tables()
@@ -952,14 +1117,15 @@
     )[None, :]
     fc_bias_own = lax.dynamic_slice_in_dim(fc_bias, tensor_rank * units, units)[None, :]
 
-    while len(fc_pack.bits) > 1:
-        fc_pack.double()
-        out_pack.double()
     done = project_qkv(
         ids, info, sent, gain_attn, shift_attn, qkv_pack, qkv_bias_own, tables, width
     )
-    queries, keys, values, *grad = tie_packs(fc_pack, out_pack, beside=[*done, *grad])
-    grad = Tokens(gather_near(grad, "tensor"), order)
+    done = tie_packs(out_pack, beside=[*done, *early_near, *late_far])
+    (queries, keys, values), done = done[:3], done[3:]
+    early_near, late_far = done[: groups // 2 - 1], done[groups // 2 - 1 :]
+    late_near = [swap(x, "tensor", 1) for x in late_far]
+    far = zip(zip(early_far, late_far), zip(early_near, late_near))
+    grad = Tokens([(out_grad,), (near,), *[x for pair in far for x in pair]], order)
     grad_context = project_grad(ids, grad, dense_pack, width)
     fc_pack.double()
     out_pack.double()
@@ -996,11 +1162,7 @@
         mlp_parts.swap()
         mlp_parts.add()
     mlp_parts.swap()
-    for parts in qkv_sums:
-        parts.add()
-    mlp_parts.got, *sends = tie(mlp_parts.got, *[parts.send for parts in qkv_sums])
-    for parts, send in zip(qkv_sums, sends):
-        parts.send = send
+    add_stacks(qkv_sums)
     mlp_parts.add()
     hidden, mlp_parts.send = tie(hidden, mlp_parts.send)
     mlp_parts.swap()
@@ -1016,45 +1178,38 @@
         back_parts.swap()
         back_parts.add()
     back_parts.swap()
-    for parts in qkv_sums + mlp_sums:
-        parts.add()
-    back_parts.got, *sends = tie(back_parts.got, *[parts.send for parts in qkv_sums + mlp_sums])
-    for parts, send in zip(qkv_sums + mlp_sums, sends):
-        parts.send = send
+    add_stacks(qkv_sums + mlp_sums)
+
     back_parts.terms.append((back_parts.got, 0))
-    quarter, last = rows_local // 4, back_parts.bits[-1]
-    first = add_terms(back_parts.terms, 1, 0, quarter)
-    rest = add_terms(back_parts.terms, 1, quarter, rows_local - quarter)
+    last = back_parts.bits[-1]
+    first, rest = add_split(back_parts.terms, 4)
     back_parts.terms = [(x, at + 1) for x, at in back_parts.terms]
     stream_in, first, rest = tie(stream_in, first, rest)
     first, rest = swap(first, "tensor", last), swap(rest, "tensor", last)
     for parts in qkv_sums + mlp_sums:
         parts.swap()
-    output, squares = finish_output(
-        stream_in, attn_parts.terms, mlp_parts.terms, dense_bias[None, :], out_bias[None, :]
-    )
-    output, squares, first = tie(output, squares, first)
-    fc_bias_spread = lax.dynamic_update_slice(
-        jnp.zeros(fc_bias.shape, f32), fc_bias_sums[0], (tensor_rank * units,)
-    )
-    qkv_bias_spread = lax.dynamic_update_slice(
-        jnp.zeros(qkv_bias.shape, f32), by_head(qkv_bias_sums[0], heads), (tensor_rank * qkv_width,)
-    )
-    sums = jnp.concatenate(
-        [
-            norm_sums[:4].reshape(-1),
-            squares[:3].reshape(-1),
-            jnp.sum(out_grad.astype(f32), axis=0),
-            fc_bias_spread,
-            qkv_bias_spread,
-        ]
-    )
+    output, sums = finish_output(
+        ids,
+        stream_in,
+        out_grad,
+        attn_parts.terms,
+        mlp_parts.terms,
+        dense_bias[None, :],
+        out_bias[None, :],
+        norm_sums,
+        fc_bias_sums,
+        qkv_bias_sums,
+        groups,
+    )
+    output, sums, first = tie(output, sums, first)
+
     sums = sums + swap(sums, "tensor", 1)
     (sums,) = tie_halves([sums], *qkv_sums, *mlp_sums)
     for bit in data_bits[1:]:
         sums = sums + swap(sums, "dp", bit)
-    for parts in qkv_sums + mlp_sums:
+    for parts in qkv_sums:
         parts.add()
+    add_stacks(mlp_sums)
     sums, *sends = tie(sums, *[parts.send for parts in mlp_sums])
     for parts, send in zip(mlp_sums, sends):
         parts.send = send
@@ -1064,23 +1219,15 @@
         sums = sums + swap(sums, "tensor", bit)
     stream_grad = finish_grad(out_grad, normalized, inv_std, back_parts.terms, first, rest)
 
-    first, second = [parts.finish() for parts in mlp_sums]
-    half = units // 2
-    fc_weight_grad = jnp.concatenate([first[:, :half], second[:, :half]], axis=1)
-    out_weight_grad = jnp.concatenate([first[:, half:], second[:, half:]], axis=1).T
-    first, second = [parts.finish() for parts in qkv_sums]
-    dense_weight_grad = second[:, width:].T
-    qkv_weight_grad = by_head(jnp.concatenate([first, second[:, :width]], axis=1), heads)
+    fc_weight_grad, out_weight_grad = finish_mlp_weights(*[x.finish() for x in mlp_sums])
+    qkv_weight_grad, dense_weight_grad = finish_attention_weights(*[x.finish() for x in qkv_sums])
 
     count_all = float(rows_local * lax.axis_size("dp") * groups * model)
-    gain_attn_grad, shift_attn_grad, gain_mlp_grad, shift_mlp_grad = sums[: 4 * model].reshape(
-        4, model
-    )
-    squares = jnp.sum(sums[4 * model : 7 * model].reshape(3, model), axis=1)
-    root_squares = jnp.sqrt(squares / count_all)
-    residual_grad = sums[7 * model : 8 * model]
-    fc_bias_grad = sums[8 * model : 8 * model + fc_bias.shape[0]]
-    qkv_bias_grad = sums[8 * model + fc_bias.shape[0] :]
+    gain_attn_grad, shift_attn_grad, gain_mlp_grad, shift_mlp_grad = (sums[x] for x in range(4))
+    root_squares = jnp.sqrt(jnp.sum(sums[4:7], axis=1) / count_all)
+    residual_grad = sums[7]
+    fc_bias_grad = sums[8:12].reshape(-1)
+    qkv_bias_grad = by_head(sums[12 : 12 + groups, :qkv_width], heads).reshape(-1)
     return (
         output,
         stream_grad,

time: 371 us -> 382 us (1.030)
  Pallas kernels: 197 us -> 154 us
  waiting for transfers between devices: 67.8 us -> 110 us
  local copies, waits for them, and re-layouts: 26.7 us -> 48.2 us
  starting transfers between devices: 50 us -> 41.3 us
    pallas_call x21 -> x17, Pallas kernels: 197 us -> 154 us  [call(): pl.pallas_call(kernel, grid_spec=pltpu.PrefetchScalarGridSpec(num_scalar_...]
    ppermute x42 -> x44, waiting for transfers between devices: 67.8 us -> 110 us  [swap(): return lax.ppermute(block, axis, [(i, i ^ bit) for i in range(size)])]
    unnamed x82 -> x152, local copies, waits for them, and re-layouts: 9.64 us -> 32.3 us
    ppermute x42 -> x44, starting transfers between devices: 50 us -> 41.3 us  [swap(): return lax.ppermute(block, axis, [(i, i ^ bit) for i in range(size)])]
    add x4 -> x0, other arithmetic: 4.5 us -> none  [finish(): return sum((x[at].astype(f32) for x, at in self.terms))]
  transfers between devices with their start and end apart: 42 -> 44, of which waited for: 15 -> 18; matrix products, arithmetic and copies ran while one was open for 12% -> 11% of each run, Pallas kernels for 48% -> 37%
where the time goes in v6:
time: 382 us; the launch traced here: 381 us
  Pallas kernels  154 us (40%)
  waiting for transfers between devices  110 us (29%)
  local copies, waits for them, and re-layouts  48.2 us (13%)
  starting transfers between devices  41.3 us (11%)
  other arithmetic  25.1 us (7%)
    pallas_call x17, Pallas kernels, call(): pl.pallas_call(kernel, grid_spec=pltpu.PrefetchScalarGridSpec(num_scalar_...  154 us
    ppermute x44, waiting for transfers between devices, swap(): return lax.ppermute(block, axis, [(i, i ^ bit) for i in range(size)])  110 us
    ppermute x44, starting transfers between devices, swap(): return lax.ppermute(block, axis, [(i, i ^ bit) for i in range(size)])  41.3 us
    unnamed x152, local copies, waits for them, and re-layouts  32.3 us
    concatenate x8, other arithmetic, double(): jnp.concatenate(self.arrays, axis=0)  10.3 us
  transfers between devices with their start and end apart: 44, of which 18 were waited for; matrix products, arithmetic and copies ran while one was open for 11% of the time, Pallas kernels for 37%

profile of v6, /device:TPU:0, one launch (start us, length us, event | category | flops | bytes accessed | tf_op | source)
XLA Modules:
  0.0 380.6 jit_solution(14469586723039189919)
XLA Ops:
  1.2 2.2 reduce_sum.40
  3.8 2.3 fusion.28
  6.4 2.5 collective-permute-start.1
  9.9 2.6 collective-permute-start.3
  12.6 1.6 collective-permute-start.4
  15.3 1.7 collective-permute-done.4.refs_7_.refs_1_
  17.0 5.3 %collective-permute-done.3.refs_5_ = bf16[128,768]{1,0:T(8,128)(2,1)S(1)} collective-permute-done((bf16[128,768]{1,0:T(8,128)(2,1)}, bf16[128,768]{1,0:T(8,128)(2,1)S(1)}, u32[]{:S(2)}, u32[]{:S(2)}) %collective-permute-start.3) | collective-permute-done | bytes 196640 | tf_op jit(solution)/shard_map/ppermute | solution.py:45
  23.1 1.7 pad_maximum_fusion.5
  25.6 3.3 collective-permute-start.7
  30.1 2.1 slice.42
  32.2 1.9 slice.43
  35.3 3.4 collective-permute-done.1.refs_2_
  38.6 7.9 %collective-permute-done.6.refs_8_.refs_2_ = bf16[256,256]{1,0:T(8,128)(2,1)} collective-permute-done((bf16[256,256]{1,0:T(8,128)(2,1)}, bf16[256,256]{1,0:T(8,128)(2,1)}, u32[]{:S(2)}, u32[]{:S(2)}) %collective-permute-start.6) | collective-permute-done | bytes 131104 | tf_op jit(solution)/shard_map/ppermute | solution.py:45
  47.2 1.7 copy.109
  49.0 2.1 pad_maximum_fusion.2
  51.0 1.5 collective-permute-start.10
  54.8 1.6 collective-permute-start.12
  56.4 4.6 %fusion.8 = (f32[1280,128]{1,0:T(8,128)}, f32[1280,128]{1,0:T(8,128)}, f32[1280,128]{1,0:T(8,128)}) fusion(s32[128]{0:T(128)S(1)} %get-tuple-element.330, s32[128]{0:T(128)S(1)} %get-tuple-element.331, pred[128]{0:T(512)(128)(4,1)} %compare_and_fusion, f32[1280]{0:T(1024)S(1)} %iota_convert_fusion), kind=kLoop, calls=%fused_computation.22 | loop fusion | flops 3932160 | bytes 1972352 | tf_op jit(solution)/shard_map/jit(_where)/select_n | solution.py:1016
  61.1 1.6 collective-permute-done.11.refs_9_.refs_3_
  66.8 9.6 %collective-permute-done.13.refs_15_ = bf16[128,1024]{1,0:T(8,128)(2,1)} collective-permute-done((bf16[128,1024]{1,0:T(8,128)(2,1)S(1)}, bf16[128,1024]{1,0:T(8,128)(2,1)}, u32[]{:S(2)}, u32[]{:S(2)}) %collective-permute-start.13) | collective-permute-done | bytes 262176 | tf_op jit(solution)/shard_map/ppermute | solution.py:45
  76.5 2.1 collective-permute-done.12.refs_12_.refs_10_
  78.7 1.6 collective-permute-start.15
  80.2 1.8 pad_maximum_fusion.4
  85.3 1.4 broadcast_in_dim_reshape.3.refs_10_
  88.2 1.7 copy.111.refs_4_
  97.1 9.1 %project_qkv.1 = (bf16[2560,256]{1,0:T(8,128)(2,1)S(1)}, bf16[2560,256]{1,0:T(8,128)(2,1)S(1)}, bf16[2560,256]{1,0:T(8,128)(2,1)S(1)}) custom-call(s32[6]{0:T(128)S(1)} %stack.19.ids, s32[1,20,5]{2,1,0:T(8,128)S(1)} %stack.20.info, bf16[640,1024]{1,0:T(8,128)(2,1)} %collective-permute-done.8.refs_0_, bf16[640,1024]{1,0:T(8,128)(2,1)} %collective-permute-done.refs_1_, ...), custom_call_target="tpu_custom_call" | custom-call | flops 4026531840 | bytes 12725248 | tf_op jit(solution)/shard_map/project_qkv/pallas_call | solution.py:217
  109.3 1.6 collective-permute-start.19
  110.9 5.2 %project_grad.1.do_ref = bf16[2560,256]{1,0:T(8,128)(2,1)S(1)} custom-call(s32[6]{0:T(128)S(1)} %stack.19.ids, bf16[384,1024]{1,0:T(8,128)(2,1)} %collective-permute-done.14.refs_0_.refs_4_, bf16[256,1024]{1,0:T(8,128)(2,1)S(1)} %collective-permute-done.17.refs_1_.refs_5_, bf16[640,1024]{1,0:T(8,128)(2,1)} %collective-permute-done.2.refs_2_.refs_6_, ...), custom_call_target="tpu_custom_call" | custom-call | flops 1342177280 | bytes 7077888 | tf_op jit(solution)/shard_map/project_grad/pallas_call | solution.py:217
  116.9 50.0 %attention.1 = (bf16[2560,256]{1,0:T(8,128)(2,1)S(1)}, bf16[2560,256]{1,0:T(8,128)(2,1)S(1)}, bf16[2560,256]{1,0:T(8,128)(2,1)S(1)}, bf16[2560,256]{1,0:T(8,128)(2,1)S(1)}) custom-call(s32[1,20,5]{2,1,0:T(8,128)S(1)} %stack.20.info, bf16[2560,256]{1,0:T(8,128)(2,1)S(1)} %get-tuple-element.198.q_ref, bf16[2560,256]{1,0:T(8,128)(2,1)S(1)} %project_grad.1.do_ref, ...), custom_call_target="tpu_custom_call" | custom-call | flops 31406948352 | bytes 12451840 | tf_op jit(solution)/shard_map/attention/pallas_call | solution.py:217
  169.1 6.0 %project_context.1 = (bf16[2,640,1024]{2,1,0:T(8,128)(2,1)}, bf16[2,640,1024]{2,1,0:T(8,128)(2,1)S(1)}) custom-call(s32[6]{0:T(128)S(1)} %stack.19.ids, bf16[2560,256]{1,0:T(8,128)(2,1)S(1)} %get-tuple-element.220.ctx.ctx_ref, bf16[128,256]{1,0:T(8,128)(2,1)S(1)} %bitcast.47, bf16[128,256]{1,0:T(8,128)(2,1)S(1)} %collective-permute-done.4.refs_7_.refs_1_, ...), custom_call_target="tpu_custom_call" | custom-call | flops 1342177280 | bytes 7077888 | tf_op jit(solution)/shard_map/project_context/pallas_call | solution.py:217
  175.2 1.5 copy-done.5
  177.3 1.3 copy-done.2
  181.8 1.3 copy-done.57
  183.2 1.3 copy-done.59
  184.5 1.3 copy-done.61
  185.8 1.3 copy-done.63
  187.1 12.3 %attention_weights.1 = (bf16[2560,768]{1,0:T(8,128)(2,1)S(1)}, f32[8,768]{1,0:T(8,128)S(1)}, bf16[4,128,512]{2,1,0:T(8,128)(2,1)S(1)}, bf16[4,128,512]{2,1,0:T(8...) custom-call(s32[6]{0:T(128)S(1)} %stack.19.ids, s32[1,20,5]{2,1,0:T(8,128)S(1)} %stack.20.info, ...), custom_call_target="tpu_custom_call" | custom-call | flops 5368709120 | bytes 23756800 | tf_op jit(solution)/shard_map/attention_weights/pallas_call | solution.py:217
  199.5 3.7 add_terms.2
  205.1 39.7 %mlp.1 = (bf16[2,640,1024]{2,1,0:T(8,128)(2,1)}, bf16[2,640,1024]{2,1,0:T(8,128)(2,1)}, bf16[2560,1024]{1,0:T(8,128)(2,1)}, f32[8,1024]{1,0:T(8,128)S(1)}, bf16[...) custom-call(s32[6]{0:T(128)S(1)} %stack.19.ids, ...), custom_call_target="tpu_custom_call" | custom-call | flops 26843545600 | bytes 29405184 | tf_op jit(solution)/shard_map/mlp/pallas_call | solution.py:217
  245.0 5.1 %collective-permute-done.24.refs_1_.refs_4_ = bf16[2,640,1024]{2,1,0:T(8,128)(2,1)S(1)} collective-permute-done((bf16[2,640,1024]{2,1,0:T(8,128)(2,1)}, bf16[2,640,1024]{2,1,0:T(8,128)(2,1)S(1)}, u32[]{:S(2)}, u32[]{:S(2)}) %collective-permute-start.24) | collective-permute-done | bytes 2621472 | tf_op jit(solution)/shard_map/ppermute | solution.py:45
  250.1 1.7 copy-done.7
  253.0 1.5 collective-permute-start.25
  254.5 1.5 collective-permute-start.28
  256.1 1.2 collective-permute-start.29
  258.8 2.1 copy-done.55
  260.9 2.5 copy-done.64
  263.4 15.4 %norm_backward.1 = (bf16[2,640,1024]{2,1,0:T(8,128)(2,1)S(1)}, bf16[2,640,1024]{2,1,0:T(8,128)(2,1)S(1)}, f32[8,1024]{1,0:T(8,128)S(1)}) custom-call(s32[6]{0:T(128)S(1)} %stack.19.ids, bf16[2560,768]{1,0:T(8,128)(2,1)S(1)} %copy-done.55, bf16[2560,1024]{1,0:T(8,128)(2,1)S(1)} %copy-done.64, bf16[640,1024]{1,0:T(8,128)(2,1)} %collective-permute-done.8.refs_0_, ...), custom_call_target="tpu_custom_call" | custom-call | flops 9395240960 | bytes 23371776 | tf_op jit(solution)/shard_map/norm_backward/pallas_call | solution.py:217
  278.8 7.7 %collective-permute-done.26.refs_2_ = bf16[2,128,512]{2,1,0:T(8,128)(2,1)S(1)} collective-permute-done((bf16[2,128,512]{2,1,0:T(8,128)(2,1)S(1)}, bf16[2,128,512]{2,1,0:T(8,128)(2,1)S(1)}, u32[]{:S(2)}, u32[]{:S(2)}) %collective-permute-start.26) | collective-permute-done | bytes 262176 | tf_op jit(solution)/shard_map/ppermute | solution.py:45
  287.6 4.9 %collective-permute-done.30.refs_1_ = bf16[2,640,1024]{2,1,0:T(8,128)(2,1)S(1)} collective-permute-done((bf16[2,640,1024]{2,1,0:T(8,128)(2,1)S(1)}, bf16[2,640,1024]{2,1,0:T(8,128)(2,1)S(1)}, u32[]{:S(2)}, u32[]{:S(2)}) %collective-permute-start.30) | collective-permute-done | bytes 2621472 | tf_op jit(solution)/shard_map/ppermute | solution.py:45
  293.9 1.5 collective-permute-start.31
  295.7 1.3 collective-permute-start.35
  297.5 5.1 %finish_output.1 = (f32[640,1024]{1,0:T(8,128)}, f32[16,1024]{1,0:T(8,128)S(1)}) custom-call(s32[6]{0:T(128)S(1)} %stack.19.ids, f32[640,1024]{1,0:T(8,128)S(1)} %copy-done, bf16[640,1024]{1,0:T(8,128)(2,1)S(1)} %copy-done.3, bf16[2,640,1024]{2,1,0:T(8,128)(2,1)S(1)} %copy-done.6, bf16[2,640,1024]{2,1,0:T(8,128)(2,1)} %collective-permute-done.20.refs_1_, ...), custom_call_target="tpu_custom_call" | custom-call | flops 10485760 | bytes 19824640 | tf_op jit(solution)/shard_map/finish_output/pallas_call | solution.py:217
  302.6 21.5 %collective-permute-done.31.refs_2_ = bf16[1,160,1024]{2,1,0:T(8,128)(2,1)S(1)} collective-permute-done((bf16[1,160,1024]{2,1,0:T(8,128)(2,1)S(1)}, bf16[1,160,1024]{2,1,0:T(8,128)(2,1)S(1)}, u32[]{:S(2)}, u32[]{:S(2)}) %collective-permute-start.31) | collective-permute-done | bytes 327712 | tf_op jit(solution)/shard_map/ppermute | solution.py:45
  324.2 1.4 collective-permute-start.33
  325.5 1.5 collective-permute-start.34
  327.1 9.9 %collective-permute-done.33.refs_3_ = bf16[1,128,512]{2,1,0:T(8,128)(2,1)S(1)} collective-permute-done((bf16[1,128,512]{2,1,0:T(8,128)(2,1)S(1)}, bf16[1,128,512]{2,1,0:T(8,128)(2,1)S(1)}, u32[]{:S(2)}, u32[]{:S(2)}) %collective-permute-start.33) | collective-permute-done | bytes 131104 | tf_op jit(solution)/shard_map/ppermute | solution.py:45
  337.0 2.4 collective-permute-done.34.refs_7_
  339.4 4.3 %collective-permute-done.37 = f32[16,1024]{1,0:T(8,128)S(1)} collective-permute-done((f32[16,1024]{1,0:T(8,128)S(1)}, f32[16,1024]{1,0:T(8,128)S(1)}, u32[]{:S(2)}, u32[]{:S(2)}) %collective-permute-start.37) | collective-permute-done | bytes 65568 | tf_op jit(solution)/shard_map/ppermute | solution.py:45
  344.8 4.2 %collective-permute-done.38 = f32[16,1024]{1,0:T(8,128)S(1)} collective-permute-done((f32[16,1024]{1,0:T(8,128)S(1)}, f32[16,1024]{1,0:T(8,128)S(1)}, u32[]{:S(2)}, u32[]{:S(2)}) %collective-permute-start.38) | collective-permute-done | bytes 65568 | tf_op jit(solution)/shard_map/ppermute | solution.py:45
  349.9 2.1 collective-permute-start.43
  352.6 3.8 collective-permute-done.39
  358.1 9.5 %collective-permute-done.42.refs_3_ = bf16[1,128,1024]{2,1,0:T(8,128)(2,1)S(1)} collective-permute-done((bf16[1,128,1024]{2,1,0:T(8,128)(2,1)S(1)}, bf16[1,128,1024]{2,1,0:T(8,128)(2,1)S(1)}, u32[]{:S(2)}, u32[]{:S(2)}) %collective-permute-start.42) | collective-permute-done | bytes 262176 | tf_op jit(solution)/shard_map/ppermute | solution.py:45
  367.5 5.5 %collective-permute-done.43.refs_7_ = bf16[1,128,1024]{2,1,0:T(8,128)(2,1)S(1)} collective-permute-done((bf16[1,128,1024]{2,1,0:T(8,128)(2,1)S(1)}, bf16[1,128,1024]{2,1,0:T(8,128)(2,1)S(1)}, u32[]{:S(2)}, u32[]{:S(2)}) %collective-permute-start.43) | collective-permute-done | bytes 262176 | tf_op jit(solution)/shard_map/ppermute | solution.py:45
  374.3 3.0 finish_grad.1
  (244 shorter events, 53.2 us)
Async XLA Ops:
  0.7 21.6 %collective-permute-start.2 = (bf16[640,1024]{1,0:T(8,128)(2,1)}, bf16[640,1024]{1,0:T(8,128)(2,1)}, u32[]{:S(2)}, u32[]{:S(2)}) collective-permute-start(bf16[640,1024]{1,0:T(8,128)(2,1)} %grad_ref.3), channel_id=1, source_target_pairs={{0,1},{1,0},{2,3},{3,2},{4,5},{5,4},{6,7},{7,6},{8,9},{9,8},{10,11... | collective-permute-start | bytes 3932168 | tf_op jit(solution)/shard_map/ppermute | solution.py:45
  3.8 8.7 %copy-start.67 = (f32[256,128]{1,0:T(8,128)S(1)}, f32[256,128]{1,0:T(8,128)}, u32[]{:S(2)}) copy-start(f32[256,128]{1,0:T(8,128)} %param.25) | copy-start | bytes 393220
  6.1 29.1 %collective-permute-start = (bf16[640,1024]{1,0:T(8,128)(2,1)}, bf16[640,1024]{1,0:T(8,128)(2,1)}, u32[]{:S(2)}, u32[]{:S(2)}) collective-permute-start(bf16[640,1024]{1,0:T(8,128)(2,1)} %get-tuple-element.186.refs_3_), channel_id=1, source_target_pairs={{0,1},{1,0},{2,3},{3,2},{4,5},{5,4},{6,7},{7,6},{8,9},{9,8},{10,11... | collective-permute-start | bytes 3932168 | tf_op jit(solution)/shard_map/ppermute | solution.py:45
  6.4 32.3 %collective-permute-start.1 = (bf16[640,1024]{1,0:T(8,128)(2,1)}, bf16[640,1024]{1,0:T(8,128)(2,1)}, u32[]{:S(2)}, u32[]{:S(2)}) collective-permute-start(bf16[640,1024]{1,0:T(8,128)(2,1)} %get-tuple-element.186.refs_3_), channel_id=1, source_target_pairs={{0,2},{1,3},{2,0},{3,1},{4,6},{5,7},{6,4},{7,5},{8,10},{9,11},{10,... | collective-permute-start | bytes 3932168 | tf_op jit(solution)/shard_map/ppermute | solution.py:45
  9.1 16.5 %copy-start.65 = (bf16[128,3,4,64]{0,3,2,1:T(8,128)(2,1)}, bf16[128,3,4,64]{0,3,2,1:T(8,128)(2,1)S(1)}, u32[]{:S(2)}) copy-start(bf16[128,3,4,64]{0,3,2,1:T(8,128)(2,1)S(1)} %copy.104) | copy-start | bytes 589828
  9.9 12.3 %collective-permute-start.3 = (bf16[128,768]{1,0:T(8,128)(2,1)}, bf16[128,768]{1,0:T(8,128)(2,1)S(1)}, u32[]{:S(2)}, u32[]{:S(2)}) collective-permute-start(bf16[128,768]{1,0:T(8,128)(2,1)} %copy.105), channel_id=1, source_target_pairs={{0,16},{4,20},{8,24},{12,28},{16,0},{20,4},{24,8},{28,12},{1,17},{... | collective-permute-start | bytes 589832 | tf_op jit(solution)/shard_map/ppermute | solution.py:45
  12.6 4.3 %collective-permute-start.4 = (bf16[128,256]{1,0:T(8,128)(2,1)S(1)}, bf16[128,256]{1,0:T(8,128)(2,1)S(1)}, u32[]{:S(2)}, u32[]{:S(2)}) collective-permute-start(bf16[128,256]{1,0:T(8,128)(2,1)S(1)} %bitcast.43), channel_id=1, source_target_pairs={{0,4},{4,0},{8,12},{12,8},{16,20},{20,16},{24,28},{28,24},{1,5},{5... | collective-permute-start | bytes 196616 | tf_op jit(solution)/shard_map/ppermute | solution.py:45
  15.3 91.0 %copy-start.13 = (bf16[128,1024]{1,0:T(8,128)(2,1)}, bf16[128,1024]{1,0:T(8,128)(2,1)S(1)}, u32[]{:S(2)}) copy-start(bf16[128,1024]{1,0:T(8,128)(2,1)S(1)} %convert_element_type.57.refs_10_.refs_8_) | copy-start | bytes 786436
  24.8 21.8 %collective-permute-start.5 = (bf16[256,768]{1,0:T(8,128)(2,1)}, bf16[256,768]{1,0:T(8,128)(2,1)}, u32[]{:S(2)}, u32[]{:S(2)}) collective-permute-start(bf16[256,768]{1,0:T(8,128)(2,1)} %pad_maximum_fusion.5), channel_id=1, source_target_pairs={{0,8},{4,12},{8,0},{12,4},{16,24},{20,28},{24,16},{28,20},{1,9},{5... | collective-permute-start | bytes 1179656 | tf_op jit(solution)/shard_map/ppermute | solution.py:45
  25.6 21.0 %collective-permute-start.7 = (bf16[128,1024]{1,0:T(8,128)(2,1)S(1)}, bf16[128,1024]{1,0:T(8,128)(2,1)S(1)}, u32[]{:S(2)}, u32[]{:S(2)}) collective-permute-start(bf16[128,1024]{1,0:T(8,128)(2,1)S(1)} %convert_element_type.57.refs_10_.refs_8_), channel_id=1, source_target_pairs={{0,16},{4,20},{8,24},{12,28},{16,0},{20,4},{24,8},{28,12},{1,17},{... | collective-permute-start | bytes 786440 | tf_op jit(solution)/shard_map/ppermute | solution.py:45
  29.6 16.9 %collective-permute-start.6 = (bf16[256,256]{1,0:T(8,128)(2,1)}, bf16[256,256]{1,0:T(8,128)(2,1)}, u32[]{:S(2)}, u32[]{:S(2)}) collective-permute-start(bf16[256,256]{1,0:T(8,128)(2,1)} %pad_maximum_fusion.7), channel_id=1, source_target_pairs={{0,16},{4,20},{8,24},{12,28},{16,0},{20,4},{24,8},{28,12},{1,17},{... | collective-permute-start | bytes 393224 | tf_op jit(solution)/shard_map/ppermute | solution.py:45
  35.2 72.9 %copy-start.15 = (bf16[1024,128]{0,1:T(8,128)(2,1)}, bf16[1024,128]{0,1:T(8,128)(2,1)S(1)}, u32[]{:S(2)}) copy-start(bf16[1024,128]{0,1:T(8,128)(2,1)S(1)} %copy.108) | copy-start | bytes 786436
  46.5 59.8 %copy-start.21 = (bf16[128,1024]{1,0:T(8,128)(2,1)}, bf16[128,1024]{1,0:T(8,128)(2,1)S(1)}, u32[]{:S(2)}) copy-start(bf16[128,1024]{1,0:T(8,128)(2,1)S(1)} %collective-permute-done.7.refs_11_.refs_9_) | copy-start | bytes 786436
  46.5 32.1 %collective-permute-start.8 = (bf16[640,1024]{1,0:T(8,128)(2,1)}, bf16[640,1024]{1,0:T(8,128)(2,1)}, u32[]{:S(2)}, u32[]{:S(2)}) collective-permute-start(bf16[640,1024]{1,0:T(8,128)(2,1)} %collective-permute-done.1.refs_2_), channel_id=1, source_target_pairs={{0,1},{1,0},{2,3},{3,2},{4,5},{5,4},{6,7},{7,6},{8,9},{9,8},{10,11... | collective-permute-start | bytes 3932168 | tf_op jit(solution)/shard_map/ppermute | solution.py:45
  46.6 32.0 %collective-permute-start.9 = (bf16[384,1024]{1,0:T(8,128)(2,1)}, bf16[384,1024]{1,0:T(8,128)(2,1)}, u32[]{:S(2)}, u32[]{:S(2)}) collective-permute-start(bf16[384,1024]{1,0:T(8,128)(2,1)} %slice.42), channel_id=1, source_target_pairs={{0,2},{1,3},{2,0},{3,1},{4,6},{5,7},{6,4},{7,5},{8,10},{9,11},{10,... | collective-permute-start | bytes 2359304 | tf_op jit(solution)/shard_map/ppermute | solution.py:45
  51.0 10.0 %copy-start.72 = (s32[2560]{0:T(1024)S(1)}, s32[2560]{0:T(1024)}, u32[]{:S(2)}) copy-start(s32[2560]{0:T(1024)} %param.17) | copy-start | bytes 30724
  51.0 13.3 %copy-start.71 = (s32[2560]{0:T(1024)S(1)}, s32[2560]{0:T(1024)}, u32[]{:S(2)}) copy-start(s32[2560]{0:T(1024)} %param.18) | copy-start | bytes 30724
  51.0 27.6 %collective-permute-start.10 = (bf16[512,768]{1,0:T(8,128)(2,1)}, bf16[512,768]{1,0:T(8,128)(2,1)}, u32[]{:S(2)}, u32[]{:S(2)}) collective-permute-start(bf16[512,768]{1,0:T(8,128)(2,1)} %pad_maximum_fusion.2), channel_id=1, source_target_pairs={{0,4},{4,0},{8,12},{12,8},{16,20},{20,16},{24,28},{28,24},{1,5},{5... | collective-permute-start | bytes 2359304 | tf_op jit(solution)/shard_map/ppermute | solution.py:45
  53.5 9.3 %collective-permute-start.11 = (bf16[512,256]{1,0:T(8,128)(2,1)S(1)}, bf16[512,256]{1,0:T(8,128)(2,1)S(1)}, u32[]{:S(2)}, u32[]{:S(2)}) collective-permute-start(bf16[512,256]{1,0:T(8,128)(2,1)S(1)} %pad_maximum_fusion.6), channel_id=1, source_target_pairs={{0,8},{4,12},{8,0},{12,4},{16,24},{20,28},{24,16},{28,20},{1,9},{5... | collective-permute-start | bytes 786440 | tf_op jit(solution)/shard_map/ppermute | solution.py:45
  54.8 23.8 %collective-permute-start.12 = (bf16[256,1024]{1,0:T(8,128)(2,1)}, bf16[256,1024]{1,0:T(8,128)(2,1)}, u32[]{:S(2)}, u32[]{:S(2)}) collective-permute-start(bf16[256,1024]{1,0:T(8,128)(2,1)} %pad_maximum_fusion.3), channel_id=1, source_target_pairs={{0,8},{4,12},{8,0},{12,4},{16,24},{20,28},{24,16},{28,20},{1,9},{5... | collective-permute-start | bytes 1572872 | tf_op jit(solution)/shard_map/ppermute | solution.py:45
  63.4 13.0 %collective-permute-start.13 = (bf16[128,1024]{1,0:T(8,128)(2,1)S(1)}, bf16[128,1024]{1,0:T(8,128)(2,1)}, u32[]{:S(2)}, u32[]{:S(2)}) collective-permute-start(bf16[128,1024]{1,0:T(8,128)(2,1)S(1)} %bitcast.39), channel_id=1, source_target_pairs={{0,16},{4,20},{8,24},{12,28},{16,0},{20,4},{24,8},{28,12},{1,17},{... | collective-permute-start | bytes 786440 | tf_op jit(solution)/shard_map/ppermute | solution.py:45
  78.6 27.6 %collective-permute-start.14 = (bf16[384,1024]{1,0:T(8,128)(2,1)}, bf16[384,1024]{1,0:T(8,128)(2,1)}, u32[]{:S(2)}, u32[]{:S(2)}) collective-permute-start(bf16[384,1024]{1,0:T(8,128)(2,1)} %collective-permute-done.9.refs_3_.refs_7_), channel_id=1, source_target_pairs={{0,1},{1,0},{2,3},{3,2},{4,5},{5,4},{6,7},{7,6},{8,9},{9,8},{10,11... | collective-permute-start | bytes 2359304 | tf_op jit(solution)/shard_map/ppermute | solution.py:45
  78.7 27.5 %collective-permute-start.15 = (bf16[256,1024]{1,0:T(8,128)(2,1)}, bf16[256,1024]{1,0:T(8,128)(2,1)}, u32[]{:S(2)}, u32[]{:S(2)}) collective-permute-start(bf16[256,1024]{1,0:T(8,128)(2,1)} %slice.43), channel_id=1, source_target_pairs={{0,2},{1,3},{2,0},{3,1},{4,6},{5,7},{6,4},{7,5},{8,10},{9,11},{10,... | collective-permute-start | bytes 1572872 | tf_op jit(solution)/shard_map/ppermute | solution.py:45
  82.0 24.2 %collective-permute-start.16 = (bf16[256,1024]{1,0:T(8,128)(2,1)}, bf16[256,1024]{1,0:T(8,128)(2,1)}, u32[]{:S(2)}, u32[]{:S(2)}) collective-permute-start(bf16[256,1024]{1,0:T(8,128)(2,1)} %pad_maximum_fusion.4), channel_id=1, source_target_pairs={{0,8},{4,12},{8,0},{12,4},{16,24},{20,28},{24,16},{28,20},{1,9},{5... | collective-permute-start | bytes 1572872 | tf_op jit(solution)/shard_map/ppermute | solution.py:45
  106.2 4.7 %collective-permute-start.17 = (bf16[256,1024]{1,0:T(8,128)(2,1)}, bf16[256,1024]{1,0:T(8,128)(2,1)S(1)}, u32[]{:S(2)}, u32[]{:S(2)}) collective-permute-start(bf16[256,1024]{1,0:T(8,128)(2,1)} %collective-permute-done.15.refs_4_.refs_8_), channel_id=1, source_target_pairs={{0,1},{1,0},{2,3},{3,2},{4,5},{5,4},{6,7},{7,6},{8,9},{9,8},{10,11... | collective-permute-start | bytes 1572872 | tf_op jit(solution)/shard_map/ppermute | solution.py:45
  107.5 61.5 %collective-permute-start.18 = (bf16[512,1024]{1,0:T(8,128)(2,1)S(1)}, bf16[512,1024]{1,0:T(8,128)(2,1)S(1)}, u32[]{:S(2)}, u32[]{:S(2)}) collective-permute-start(bf16[512,1024]{1,0:T(8,128)(2,1)S(1)} %pad_maximum_fusion), channel_id=1, source_target_pairs={{0,4},{4,0},{8,12},{12,8},{16,20},{20,16},{24,28},{28,24},{1,5},{5... | collective-permute-start | bytes 3145736 | tf_op jit(solution)/shard_map/ppermute | solution.py:45
  109.3 7.6 %copy-start.27 = (f32[1280,128]{1,0:T(8,128)S(1)}, f32[1280,128]{1,0:T(8,128)}, u32[]{:S(2)}) copy-start(f32[1280,128]{1,0:T(8,128)} %get-tuple-element.323.refs_13_.high.refs_14_) | copy-start | bytes 1966084
  109.3 7.6 %copy-start.29 = (f32[1280,128]{1,0:T(8,128)S(1)}, f32[1280,128]{1,0:T(8,128)}, u32[]{:S(2)}) copy-start(f32[1280,128]{1,0:T(8,128)} %get-tuple-element.324.refs_11_.cos.refs_12_) | copy-start | bytes 1966084
  109.3 7.6 %copy-start.32 = (f32[1280,128]{1,0:T(8,128)S(1)}, f32[1280,128]{1,0:T(8,128)}, u32[]{:S(2)}) copy-start(f32[1280,128]{1,0:T(8,128)} %get-tuple-element.325.refs_12_.low.refs_13_) | copy-start | bytes 1966084
  109.3 59.7 %collective-permute-start.19 = (bf16[512,1024]{1,0:T(8,128)(2,1)S(1)}, bf16[512,1024]{1,0:T(8,128)(2,1)S(1)}, u32[]{:S(2)}, u32[]{:S(2)}) collective-permute-start(bf16[512,1024]{1,0:T(8,128)(2,1)S(1)} %pad_maximum_fusion.1), channel_id=1, source_target_pairs={{0,4},{4,0},{8,12},{12,8},{16,20},{20,16},{24,28},{28,24},{1,5},{5... | collective-permute-start | bytes 3145736 | tf_op jit(solution)/shard_map/ppermute | solution.py:45
  169.1 8.2 %copy-start.49 = (f32[1024]{0:T(1024)S(1)}, f32[1024]{0:T(1024)}, u32[]{:S(2)}) copy-start(f32[1024]{0:T(1024)} %param.20) | copy-start | bytes 12292
  169.1 8.2 %copy-start.52 = (f32[1024]{0:T(1024)S(1)}, f32[1024]{0:T(1024)}, u32[]{:S(2)}) copy-start(f32[1024]{0:T(1024)} %param.19) | copy-start | bytes 12292
  176.6 22.8 %collective-permute-start.20 = (bf16[2,640,1024]{2,1,0:T(8,128)(2,1)}, bf16[2,640,1024]{2,1,0:T(8,128)(2,1)}, u32[]{:S(2)}, u32[]{:S(2)}) collective-permute-start(bf16[2,640,1024]{2,1,0:T(8,128)(2,1)} %get-tuple-element.230), channel_id=1, source_target_pairs={{0,1},{1,0},{2,3},{3,2},{4,5},{5,4},{6,7},{7,6},{8,9},{9,8},{10,11... | collective-permute-start | bytes 7864328 | tf_op jit(solution)/shard_map/ppermute | solution.py:45
  187.1 12.3 %copy-start.6 = (bf16[2,640,1024]{2,1,0:T(8,128)(2,1)S(1)}, bf16[2,640,1024]{2,1,0:T(8,128)(2,1)}, u32[]{:S(2)}) copy-start(bf16[2,640,1024]{2,1,0:T(8,128)(2,1)} %copy-done.5) | copy-start | bytes 7864324
  203.2 41.7 %collective-permute-start.21 = (bf16[1,640,1024]{2,1,0:T(8,128)(2,1)}, bf16[1,640,1024]{2,1,0:T(8,128)(2,1)S(1)}, u32[]{:S(2)}, u32[]{:S(2)}) collective-permute-start(bf16[1,640,1024]{2,1,0:T(8,128)(2,1)} %add_terms.2), channel_id=1, source_target_pairs={{0,2},{1,3},{2,0},{3,1},{4,6},{5,7},{6,4},{7,5},{8,10},{9,11},{10,... | collective-permute-start | bytes 3932168 | tf_op jit(solution)/shard_map/ppermute | solution.py:45
  203.7 41.1 %collective-permute-start.22 = (bf16[4,128,512]{2,1,0:T(8,128)(2,1)S(1)}, bf16[4,128,512]{2,1,0:T(8,128)(2,1)S(1)}, u32[]{:S(2)}, u32[]{:S(2)}) collective-permute-start(bf16[4,128,512]{2,1,0:T(8,128)(2,1)S(1)} %get-tuple-element.252), channel_id=1, source_target_pairs={{0,4},{4,0},{8,12},{12,8},{16,20},{20,16},{24,28},{28,24},{1,5},{5... | collective-permute-start | bytes 1572872 | tf_op jit(solution)/shard_map/ppermute | solution.py:45
  204.2 40.6 %collective-permute-start.23 = (bf16[4,128,512]{2,1,0:T(8,128)(2,1)S(1)}, bf16[4,128,512]{2,1,0:T(8,128)(2,1)S(1)}, u32[]{:S(2)}, u32[]{:S(2)}) collective-permute-start(bf16[4,128,512]{2,1,0:T(8,128)(2,1)S(1)} %get-tuple-element.253), channel_id=1, source_target_pairs={{0,8},{4,12},{8,0},{12,4},{16,24},{20,28},{24,16},{28,20},{1,9},{5... | collective-permute-start | bytes 1572872 | tf_op jit(solution)/shard_map/ppermute | solution.py:45
  244.8 12.4 %copy-start.9 = (bf16[4,128,512]{2,1,0:T(8,128)(2,1)}, bf16[4,128,512]{2,1,0:T(8,128)(2,1)S(1)}, u32[]{:S(2)}) copy-start(bf16[4,128,512]{2,1,0:T(8,128)(2,1)S(1)} %collective-permute-done.22.refs_1_) | copy-start | bytes 1572868
  244.9 12.4 %copy-start.11 = (bf16[4,128,512]{2,1,0:T(8,128)(2,1)}, bf16[4,128,512]{2,1,0:T(8,128)(2,1)S(1)}, u32[]{:S(2)}) copy-start(bf16[4,128,512]{2,1,0:T(8,128)(2,1)S(1)} %collective-permute-done.23.refs_3_.refs_4_.refs_5_) | copy-start | bytes 1572868
  244.9 8.1 %copy-start.17 = (bf16[1,640,1024]{2,1,0:T(8,128)(2,1)}, bf16[1,640,1024]{2,1,0:T(8,128)(2,1)S(1)}, u32[]{:S(2)}) copy-start(bf16[1,640,1024]{2,1,0:T(8,128)(2,1)S(1)} %collective-permute-done.21.refs_2_) | copy-start | bytes 3932164
  244.9 5.2 %collective-permute-start.24 = (bf16[2,640,1024]{2,1,0:T(8,128)(2,1)}, bf16[2,640,1024]{2,1,0:T(8,128)(2,1)S(1)}, u32[]{:S(2)}, u32[]{:S(2)}) collective-permute-start(bf16[2,640,1024]{2,1,0:T(8,128)(2,1)} %get-tuple-element.256), channel_id=1, source_target_pairs={{0,1},{1,0},{2,3},{3,2},{4,5},{5,4},{6,7},{7,6},{8,9},{9,8},{10,11... | collective-permute-start | bytes 7864328 | tf_op jit(solution)/shard_map/ppermute | solution.py:45
  253.0 33.5 %collective-permute-start.25 = (bf16[1,640,1024]{2,1,0:T(8,128)(2,1)}, bf16[1,640,1024]{2,1,0:T(8,128)(2,1)S(1)}, u32[]{:S(2)}, u32[]{:S(2)}) collective-permute-start(bf16[1,640,1024]{2,1,0:T(8,128)(2,1)} %add_terms.3), channel_id=1, source_target_pairs={{0,2},{1,3},{2,0},{3,1},{4,6},{5,7},{6,4},{7,5},{8,10},{9,11},{10,... | collective-permute-start | bytes 3932168 | tf_op jit(solution)/shard_map/ppermute | solution.py:45
  254.5 32.0 %collective-permute-start.28 = (bf16[4,128,1024]{2,1,0:T(8,128)(2,1)}, bf16[4,128,1024]{2,1,0:T(8,128)(2,1)S(1)}, u32[]{:S(2)}, u32[]{:S(2)}) collective-permute-start(bf16[4,128,1024]{2,1,0:T(8,128)(2,1)} %get-tuple-element.268), channel_id=1, source_target_pairs={{0,4},{4,0},{8,12},{12,8},{16,20},{20,16},{24,28},{28,24},{1,5},{5... | collective-permute-start | bytes 3145736 | tf_op jit(solution)/shard_map/ppermute | solution.py:45
  256.1 30.5 %collective-permute-start.29 = (bf16[4,128,1024]{2,1,0:T(8,128)(2,1)}, bf16[4,128,1024]{2,1,0:T(8,128)(2,1)S(1)}, u32[]{:S(2)}, u32[]{:S(2)}) collective-permute-start(bf16[4,128,1024]{2,1,0:T(8,128)(2,1)} %get-tuple-element.269), channel_id=1, source_target_pairs={{0,8},{4,12},{8,0},{12,4},{16,24},{20,28},{24,16},{28,20},{1,9},{5... | collective-permute-start | bytes 3145736 | tf_op jit(solution)/shard_map/ppermute | solution.py:45
  257.4 29.1 %collective-permute-start.26 = (bf16[2,128,512]{2,1,0:T(8,128)(2,1)S(1)}, bf16[2,128,512]{2,1,0:T(8,128)(2,1)S(1)}, u32[]{:S(2)}, u32[]{:S(2)}) collective-permute-start(bf16[2,128,512]{2,1,0:T(8,128)(2,1)S(1)} %get-tuple-element.266), channel_id=1, source_target_pairs={{0,8},{4,12},{8,0},{12,4},{16,24},{20,28},{24,16},{28,20},{1,9},{5... | collective-permute-start | bytes 786440 | tf_op jit(solution)/shard_map/ppermute | solution.py:45
  258.3 28.2 %collective-permute-start.27 = (bf16[2,128,512]{2,1,0:T(8,128)(2,1)S(1)}, bf16[2,128,512]{2,1,0:T(8,128)(2,1)S(1)}, u32[]{:S(2)}, u32[]{:S(2)}) collective-permute-start(bf16[2,128,512]{2,1,0:T(8,128)(2,1)S(1)} %get-tuple-element.267), channel_id=1, source_target_pairs={{0,4},{4,0},{8,12},{12,8},{16,20},{20,16},{24,28},{28,24},{1,5},{5... | collective-permute-start | bytes 786440 | tf_op jit(solution)/shard_map/ppermute | solution.py:45
  287.6 7.8 %copy-start.10 = (bf16[4,128,512]{2,1,0:T(8,128)(2,1)S(1)}, bf16[4,128,512]{2,1,0:T(8,128)(2,1)}, u32[]{:S(2)}) copy-start(bf16[4,128,512]{2,1,0:T(8,128)(2,1)} %copy-done.9) | copy-start | bytes 1572868
  287.6 7.8 %copy-start.12 = (bf16[4,128,512]{2,1,0:T(8,128)(2,1)S(1)}, bf16[4,128,512]{2,1,0:T(8,128)(2,1)}, u32[]{:S(2)}) copy-start(bf16[4,128,512]{2,1,0:T(8,128)(2,1)} %copy-done.11) | copy-start | bytes 1572868
  287.6 4.9 %collective-permute-start.30 = (bf16[2,640,1024]{2,1,0:T(8,128)(2,1)S(1)}, bf16[2,640,1024]{2,1,0:T(8,128)(2,1)S(1)}, u32[]{:S(2)}, u32[]{:S(2)}) collective-permute-start(bf16[2,640,1024]{2,1,0:T(8,128)(2,1)S(1)} %get-tuple-element.271), channel_id=1, source_target_pairs={{0,1},{1,0},{2,3},{3,2},{4,5},{5,4},{6,7},{7,6},{8,9},{9,8},{10,11... | collective-permute-start | bytes 7864328 | tf_op jit(solution)/shard_map/ppermute | solution.py:45
  293.3 63.1 %collective-permute-start.40 = (bf16[1,480,1024]{2,1,0:T(8,128)(2,1)S(1)}, bf16[1,480,1024]{2,1,0:T(8,128)(2,1)S(1)}, u32[]{:S(2)}, u32[]{:S(2)}) collective-permute-start(bf16[1,480,1024]{2,1,0:T(8,128)(2,1)S(1)} %get-tuple-element.302), channel_id=1, source_target_pairs={{0,2},{1,3},{2,0},{3,1},{4,6},{5,7},{6,4},{7,5},{8,10},{9,11},{10,... | collective-permute-start | bytes 2949128 | tf_op jit(solution)/shard_map/ppermute | solution.py:45
  293.9 30.3 %collective-permute-start.31 = (bf16[1,160,1024]{2,1,0:T(8,128)(2,1)S(1)}, bf16[1,160,1024]{2,1,0:T(8,128)(2,1)S(1)}, u32[]{:S(2)}, u32[]{:S(2)}) collective-permute-start(bf16[1,160,1024]{2,1,0:T(8,128)(2,1)S(1)} %get-tuple-element.282), channel_id=1, source_target_pairs={{0,2},{1,3},{2,0},{3,1},{4,6},{5,7},{6,4},{7,5},{8,10},{9,11},{10,... | collective-permute-start | bytes 983048 | tf_op jit(solution)/shard_map/ppermute | solution.py:45
  295.7 43.7 %collective-permute-start.35 = (bf16[2,128,1024]{2,1,0:T(8,128)(2,1)S(1)}, bf16[2,128,1024]{2,1,0:T(8,128)(2,1)S(1)}, u32[]{:S(2)}, u32[]{:S(2)}) collective-permute-start(bf16[2,128,1024]{2,1,0:T(8,128)(2,1)S(1)} %get-tuple-element.294), channel_id=1, source_target_pairs={{0,8},{4,12},{8,0},{12,4},{16,24},{20,28},{24,16},{28,20},{1,9},{5... | collective-permute-start | bytes 1572872 | tf_op jit(solution)/shard_map/ppermute | solution.py:45
  297.0 42.4 %collective-permute-start.36 = (bf16[2,128,1024]{2,1,0:T(8,128)(2,1)S(1)}, bf16[2,128,1024]{2,1,0:T(8,128)(2,1)S(1)}, u32[]{:S(2)}, u32[]{:S(2)}) collective-permute-start(bf16[2,128,1024]{2,1,0:T(8,128)(2,1)S(1)} %get-tuple-element.295), channel_id=1, source_target_pairs={{0,4},{4,0},{8,12},{12,8},{16,20},{20,16},{24,28},{28,24},{1,5},{5... | collective-permute-start | bytes 1572872 | tf_op jit(solution)/shard_map/ppermute | solution.py:45
  324.1 1.4 collective-permute-start.32
  324.2 12.8 %collective-permute-start.33 = (bf16[1,128,512]{2,1,0:T(8,128)(2,1)S(1)}, bf16[1,128,512]{2,1,0:T(8,128)(2,1)S(1)}, u32[]{:S(2)}, u32[]{:S(2)}) collective-permute-start(bf16[1,128,512]{2,1,0:T(8,128)(2,1)S(1)} %get-tuple-element.292), channel_id=1, source_target_pairs={{0,16},{4,20},{8,24},{12,28},{16,0},{20,4},{24,8},{28,12},{1,17},{... | collective-permute-start | bytes 393224 | tf_op jit(solution)/shard_map/ppermute | solution.py:45
  325.5 13.9 %collective-permute-start.34 = (bf16[1,128,512]{2,1,0:T(8,128)(2,1)S(1)}, bf16[1,128,512]{2,1,0:T(8,128)(2,1)S(1)}, u32[]{:S(2)}, u32[]{:S(2)}) collective-permute-start(bf16[1,128,512]{2,1,0:T(8,128)(2,1)S(1)} %get-tuple-element.293), channel_id=1, source_target_pairs={{0,16},{4,20},{8,24},{12,28},{16,0},{20,4},{24,8},{28,12},{1,17},{... | collective-permute-start | bytes 393224 | tf_op jit(solution)/shard_map/ppermute | solution.py:45
  339.4 4.3 %collective-permute-start.37 = (f32[16,1024]{1,0:T(8,128)S(1)}, f32[16,1024]{1,0:T(8,128)S(1)}, u32[]{:S(2)}, u32[]{:S(2)}) collective-permute-start(f32[16,1024]{1,0:T(8,128)S(1)} %add.137), channel_id=1, source_target_pairs={{0,8},{4,12},{8,0},{12,4},{16,24},{20,28},{24,16},{28,20},{1,9},{5... | collective-permute-start | bytes 196616 | tf_op jit(solution)/shard_map/ppermute | solution.py:45
  343.7 13.3 %copy-start.69 = (f32[640]{0:T(1024)S(1)}, f32[640]{0:T(1024)}, u32[]{:S(2)}) copy-start(f32[640]{0:T(1024)} %copy-done.68) | copy-start | bytes 7684
  343.7 5.4 %collective-permute-start.38 = (f32[16,1024]{1,0:T(8,128)S(1)}, f32[16,1024]{1,0:T(8,128)S(1)}, u32[]{:S(2)}, u32[]{:S(2)}) collective-permute-start(f32[16,1024]{1,0:T(8,128)S(1)} %add.138), channel_id=1, source_target_pairs={{0,16},{4,20},{8,24},{12,28},{16,0},{20,4},{24,8},{28,12},{1,17},{... | collective-permute-start | bytes 196616 | tf_op jit(solution)/shard_map/ppermute | solution.py:45
  349.1 18.5 %collective-permute-start.42 = (bf16[1,128,1024]{2,1,0:T(8,128)(2,1)S(1)}, bf16[1,128,1024]{2,1,0:T(8,128)(2,1)S(1)}, u32[]{:S(2)}, u32[]{:S(2)}) collective-permute-start(bf16[1,128,1024]{2,1,0:T(8,128)(2,1)S(1)} %get-tuple-element.309), channel_id=1, source_target_pairs={{0,16},{4,20},{8,24},{12,28},{16,0},{20,4},{24,8},{28,12},{1,17},{... | collective-permute-start | bytes 786440 | tf_op jit(solution)/shard_map/ppermute | solution.py:45
  349.9 23.2 %collective-permute-start.43 = (bf16[1,128,1024]{2,1,0:T(8,128)(2,1)S(1)}, bf16[1,128,1024]{2,1,0:T(8,128)(2,1)S(1)}, u32[]{:S(2)}, u32[]{:S(2)}) collective-permute-start(bf16[1,128,1024]{2,1,0:T(8,128)(2,1)S(1)} %get-tuple-element.310), channel_id=1, source_target_pairs={{0,16},{4,20},{8,24},{12,28},{16,0},{20,4},{24,8},{28,12},{1,17},{... | collective-permute-start | bytes 786440 | tf_op jit(solution)/shard_map/ppermute | solution.py:45
  352.1 4.3 %collective-permute-start.39 = (f32[16,1024]{1,0:T(8,128)S(1)}, f32[16,1024]{1,0:T(8,128)S(1)}, u32[]{:S(2)}, u32[]{:S(2)}) collective-permute-start(f32[16,1024]{1,0:T(8,128)S(1)} %add.139), channel_id=1, source_target_pairs={{0,4},{4,0},{8,12},{12,8},{16,20},{20,16},{24,28},{28,24},{1,5},{5... | collective-permute-start | bytes 196616 | tf_op jit(solution)/shard_map/ppermute | solution.py:45
  356.4 21.0 %collective-permute-start.41 = (f32[16,1024]{1,0:T(8,128)S(1)}, f32[16,1024]{1,0:T(8,128)S(1)}, u32[]{:S(2)}, u32[]{:S(2)}) collective-permute-start(f32[16,1024]{1,0:T(8,128)S(1)} %add.140), channel_id=1, source_target_pairs={{0,2},{1,3},{2,0},{3,1},{4,6},{5,7},{6,4},{7,5},{8,10},{9,11},{10,... | collective-permute-start | bytes 196616 | tf_op jit(solution)/shard_map/ppermute | solution.py:45
  358.1 16.2 %copy-start.4 = (f32[640,1024]{1,0:T(8,128)S(1)}, f32[640,1024]{1,0:T(8,128)}, u32[]{:S(2)}) copy-start(f32[640,1024]{1,0:T(8,128)} %get-tuple-element.314.norm_ref) | copy-start | bytes 7864324
  (53 other events, 165.2 us)

commit v7 on v6

--- a/solution.py
+++ b/solution.py
@@ -68,7 +68,7 @@
         self.arrays.append(swap(held, self.axis, bit))
 
     def specs(self):
-        return [pl.BlockSpec(memory_space=pl.ANY)] * len(self.arrays)
+        return [pl.BlockSpec(memory_space=pltpu.HBM)] * len(self.arrays)
 
     def pieces(self):
         return sum(len(owners) for owners in self.owners)
@@ -172,7 +172,7 @@
         self.groups, self.counts = len(blocks), [len(block) for block in blocks]
         self.rows, self.model = sum(x.shape[0] for x in blocks[0]), blocks[0][0].shape[1]
         self.arrays = [x for block in blocks for x in block]
-        self.specs = [pl.BlockSpec(memory_space=pl.ANY)] * len(self.arrays)
+        self.specs = [pl.BlockSpec(memory_space=pltpu.HBM)] * len(self.arrays)
 
     def scratch(self):
         return [
@@ -508,6 +508,7 @@
         half_blocks(groups, rows, model),
         weight_scratch(pack),
         2 * groups * rows * model * width,
+        room=14,
     )
 
 
@@ -768,39 +769,6 @@
     )[0]
 
 
-def add_split(terms, count):
-    _, rows, columns = terms[0][0].shape
-    block = rows // count
-
-    def kernel(*refs):
-        total = sum(x[...].astype(f32) for x in refs[:-2]).astype(bf16)
-
-        @pl.when(pl.program_id(0) == 0)
-        def _():
-            refs[-2][...] = total
-
-        @pl.when(pl.program_id(0) > 0)
-        def _():
-            refs[-1][...] = total
-
-    shape = (pl.Squeezed(), block, columns)
-    return call(
-        kernel,
-        "add_split",
-        (count,),
-        [],
-        [x for x, _ in terms],
-        [pl.BlockSpec(shape, lambda i, *_, at=at: (at, i, 0)) for _, at in terms],
-        [shaped(1, block, columns), shaped(1, rows - block, columns)],
-        [
-            pl.BlockSpec(shape, lambda i, *_: (0, 0, 0)),
-            pl.BlockSpec(shape, lambda i, *_: (0, jnp.maximum(i - 1, 0), 0)),
-        ],
-        [],
-        rows * columns * len(terms),
-    )
-
-
 def whole_terms(terms, count):
     return [
         pl.BlockSpec((count, *x.shape[1:]), lambda *_, at=at: (at // count, 0, 0)) for x, at in terms
@@ -951,21 +919,19 @@
     )
 
 
-def finish_grad(grad, normalized, inv_std, terms, first, rest):
+def finish_grad(grad, normalized, inv_std, terms):
     rows, model = grad.shape
-    block = first.shape[1]
+    block = 160
 
     def kernel(grad_ref, norm_ref, std_ref, *refs):
-        term_refs, (first_ref, rest_ref, out_ref) = refs[:-3], refs[-3:]
-        last = jnp.where(pl.program_id(0) == 0, first_ref[...].astype(f32), rest_ref[...].astype(f32))
-        sent = sum(x[...].astype(f32) for x in term_refs) + last
+        term_refs, out_ref = refs[:-1], refs[-1]
+        sent = sum(x[...].astype(f32) for x in term_refs)
         norm = norm_ref[...]
         mean = jnp.sum(sent, axis=1, keepdims=True) / model
         cross = jnp.sum(sent * norm, axis=1, keepdims=True) / model
         out_ref[...] = grad_ref[...].astype(f32) + std_ref[...] * (sent - mean - norm * cross)
 
-    operands = [grad, normalized, inv_std, *[x for x, _ in terms], first, rest]
-    piece = (pl.Squeezed(), block, model)
+    operands = [grad, normalized, inv_std, *[x for x, _ in terms]]
     return call(
         kernel,
         "finish_grad",
@@ -973,11 +939,7 @@
         [],
         operands,
         [step_block(block, model), step_block(block, model), step_block(block, 1)]
-        + taken(terms, block)
-        + [
-            pl.BlockSpec(piece, lambda i, *_: (0, 0, 0)),
-            pl.BlockSpec(piece, lambda i, *_: (0, jnp.maximum(i - 1, 0), 0)),
-        ],
+        + taken(terms, block),
         [shaped(rows, model, dtype=f32)],
         [step_block(block, model)],
         [],
@@ -1078,36 +1040,6 @@
     normalized = centred * inv_std
     sent = gather_far(normalized.astype(bf16), "tensor", tensor_bits)
 
-    sent_near, near = swap(sent[0], "tensor", 1), swap(out_grad, "tensor", 1)
-    qkv_pack.double()
-    dense_pack.double()
-    (near,) = tie_packs(qkv_pack, dense_pack, fc_pack, beside=[near])
-    while len(qkv_pack.bits) > 1:
-        qkv_pack.double()
-        dense_pack.double()
-    fc_pack.double()
-    cut = rows_local * 3 // 5
-    early, late = out_grad[:cut], out_grad[cut:]
-    early, late, sent_near, *sent = tie_packs(
-        qkv_pack, dense_pack, fc_pack, out_pack, beside=[early, late, sent_near, *sent]
-    )
-    early_far = gather_far(early, "tensor", tensor_bits)[1:]
-    sent_near = [sent_near] + [swap(x, "tensor", 1) for x in sent[1:]]
-    sent = [x for pair in zip(sent, sent_near) for x in pair]
-    qkv_pack.double()
-    dense_pack.double()
-    while len(fc_pack.bits) > 1:
-        fc_pack.double()
-    out_pack.double()
-    late, *done = tie_packs(
-        qkv_pack, dense_pack, fc_pack, out_pack, beside=[late, *sent, *early_far]
-    )
-    sent, early_far = Tokens([(x,) for x in done[:groups]], order), done[groups:]
-    late_far = gather_far(late, "tensor", tensor_bits)[1:]
-    early_near = [swap(x, "tensor", 1) for x in early_far]
-    while len(out_pack.bits) > 1:
-        out_pack.double()
-
     info = tree_table(segment_ids, parent_ids)
     tables = angle_tables()
     gain_attn, shift_attn = norm_gain_attn[None, :], norm_shift_attn[None, :]
@@ -1117,10 +1049,43 @@
     )[None, :]
     fc_bias_own = lax.dynamic_slice_in_dim(fc_bias, tensor_rank * units, units)[None, :]
 
+    sent_near, near = swap(sent[0], "tensor", 1), swap(out_grad, "tensor", 1)
+    cut = rows_local * 3 // 5
+    early, late = out_grad[:cut], out_grad[cut:]
+    qkv_pack.double()
+    dense_pack.double()
+    near, early, late = tie_packs(qkv_pack, dense_pack, fc_pack, beside=[near, early, late])
+    while len(qkv_pack.bits) > 1:
+        qkv_pack.double()
+        dense_pack.double()
+    fc_pack.double()
+    done = tie_packs(
+        qkv_pack,
+        dense_pack,
+        out_pack,
+        beside=[early, late, info, *tables, qkv_bias_own, fc_bias_own, sent_near, *sent],
+    )
+    early, late, info, *done = done
+    tables, (qkv_bias_own, fc_bias_own, sent_near), sent = done[:3], done[3:6], done[6:]
+    early_far = gather_far(early, "tensor", tensor_bits)[1:]
+    sent_near = [sent_near] + [swap(x, "tensor", 1) for x in sent[1:]]
+    sent = [x for pair in zip(sent, sent_near) for x in pair]
+    qkv_pack.double()
+    dense_pack.double()
+    late, *done = tie_packs(
+        qkv_pack, dense_pack, fc_pack, out_pack, beside=[late, *sent, *early_far]
+    )
+    sent, early_far = Tokens([(x,) for x in done[:groups]], order), done[groups:]
+    late_far = gather_far(late, "tensor", tensor_bits)[1:]
+    early_near = [swap(x, "tensor", 1) for x in early_far]
+    out_pack.double()
+    while len(fc_pack.bits) > 1:
+        fc_pack.double()
+
     done = project_qkv(
         ids, info, sent, gain_attn, shift_attn, qkv_pack, qkv_bias_own, tables, width
     )
-    done = tie_packs(out_pack, beside=[*done, *early_near, *late_far])
+    done = tie_packs(fc_pack, out_pack, beside=[*done, *early_near, *late_far])
     (queries, keys, values), done = done[:3], done[3:]
     early_near, late_far = done[: groups // 2 - 1], done[groups // 2 - 1 :]
     late_near = [swap(x, "tensor", 1) for x in late_far]
@@ -1128,7 +1093,8 @@
     grad = Tokens([(out_grad,), (near,), *[x for pair in far for x in pair]], order)
     grad_context = project_grad(ids, grad, dense_pack, width)
     fc_pack.double()
-    out_pack.double()
+    while len(out_pack.bits) > 1:
+        out_pack.double()
     done = attention(info, tables, queries, keys, values, grad_context)
     context, dq, dk, dv = tie_packs(fc_pack, out_pack, beside=done)
     dp_orders = [halving_order(near_bits), halving_order(next_bits)]
@@ -1140,10 +1106,11 @@
         attn_parts.add()
     attn_parts.send, context = tie(attn_parts.send, context)
     attn_parts.swap()
+    out_pack.double()
     done = attention_weights(
         ids, info, tables, context, dq, dk, dv, sent, grad, gain_attn, shift_attn, dp_orders
     )
-    grads, qkv_bias_sums, *stacks = tie_halves(done, attn_parts)
+    grads, qkv_bias_sums, *stacks = tie_halves(tie_packs(out_pack, beside=done), attn_parts)
     attn_parts.add()
     qkv_sums = [Halving(*stacks[:2], "dp", near_bits), Halving(*stacks[2:], "dp", next_bits)]
     sent.arrays[0], attn_parts.send = tie(sent.arrays[0], attn_parts.send)
@@ -1180,12 +1147,9 @@
     back_parts.swap()
     add_stacks(qkv_sums + mlp_sums)
 
-    back_parts.terms.append((back_parts.got, 0))
-    last = back_parts.bits[-1]
-    first, rest = add_split(back_parts.terms, 4)
-    back_parts.terms = [(x, at + 1) for x, at in back_parts.terms]
-    stream_in, first, rest = tie(stream_in, first, rest)
-    first, rest = swap(first, "tensor", last), swap(rest, "tensor", last)
+    back_parts.add()
+    stream_in, back_parts.send = tie(stream_in, back_parts.send)
+    back_parts.swap()
     for parts in qkv_sums + mlp_sums:
         parts.swap()
     output, sums = finish_output(
@@ -1201,7 +1165,6 @@
         qkv_bias_sums,
         groups,
     )
-    output, sums, first = tie(output, sums, first)
 
     sums = sums + swap(sums, "tensor", 1)
     (sums,) = tie_halves([sums], *qkv_sums, *mlp_sums)
@@ -1214,10 +1177,11 @@
     for parts, send in zip(mlp_sums, sends):
         parts.send = send
     sums = sums + swap(sums, "dp", data_bits[0])
-    sums, rest = tie(sums, rest)
+    sums, back_parts.got = tie(sums, back_parts.got)
+    back_parts.add()
     for bit in tensor_bits[1:]:
         sums = sums + swap(sums, "tensor", bit)
-    stream_grad = finish_grad(out_grad, normalized, inv_std, back_parts.terms, first, rest)
+    stream_grad = finish_grad(out_grad, normalized, inv_std, back_parts.terms)
 
     fc_weight_grad, out_weight_grad = finish_mlp_weights(*[x.finish() for x in mlp_sums])
     qkv_weight_grad, dense_weight_grad = finish_attention_weights(*[x.finish() for x in qkv_sums])

time: 382 us -> 340 us (0.89)
  waiting for transfers between devices: 110 us -> 83.8 us
  local copies, waits for them, and re-layouts: 48.2 us -> 33.8 us
  other arithmetic: 25.1 us -> 16.7 us
  starting transfers between devices: 41.3 us -> 45.4 us
    ppermute x44 -> x43, waiting for transfers between devices: 110 us -> 83.8 us  [swap(): return lax.ppermute(block, axis, [(i, i ^ bit) for i in range(size)])]
    unnamed x152 -> x118, local copies, waits for them, and re-layouts: 32.3 us -> 20.6 us
    ppermute x44 -> x43, starting transfers between devices: 41.3 us -> 45.4 us  [swap(): return lax.ppermute(block, axis, [(i, i ^ bit) for i in range(size)])]
    concatenate x8, other arithmetic: 10.3 us -> 6.42 us  [double(): jnp.concatenate(self.arrays, axis=0)]
  transfers between devices with their start and end apart: 44 -> 43, of which waited for: 18 -> 17; matrix products, arithmetic and copies ran while one was open for 11% -> 7% of each run, Pallas kernels for 37% -> 44%
where the time goes in v7:
time: 340 us; the launch traced here: 338 us
  Pallas kernels  157 us (46%)
  waiting for transfers between devices  83.8 us (25%)
  starting transfers between devices  45.4 us (13%)
  local copies, waits for them, and re-layouts  33.8 us (10%)
  other arithmetic  16.7 us (5%)
    pallas_call x17, Pallas kernels, call(): pl.pallas_call(kernel, grid_spec=pltpu.PrefetchScalarGridSpec(num_scalar_...  157 us
    ppermute x43, waiting for transfers between devices, swap(): return lax.ppermute(block, axis, [(i, i ^ bit) for i in range(size)])  83.8 us
    ppermute x43, starting transfers between devices, swap(): return lax.ppermute(block, axis, [(i, i ^ bit) for i in range(size)])  45.4 us
    unnamed x118, local copies, waits for them, and re-layouts  20.6 us
  transfers between devices with their start and end apart: 43, of which 17 were waited for; matrix products, arithmetic and copies ran while one was open for 7% of the time, Pallas kernels for 44%

profile of v7, /device:TPU:0, one launch (start us, length us, event | category | flops | bytes accessed | tf_op | source)
XLA Modules:
  0.0 338.4 jit_solution(7511930576103009892)
XLA Ops:
  0.7 2.1 reduce_sum.40
  3.6 2.3 fusion.28
  6.4 2.5 collective-permute-start.4
  10.1 2.6 collective-permute-start.1
  12.8 1.6 collective-permute-start.2
  14.4 2.1 slice.39
  16.5 1.9 slice.40
  19.6 4.0 %fusion.8 = (f32[1280,128]{1,0:T(8,128)}, f32[1280,128]{1,0:T(8,128)}, f32[1280,128]{1,0:T(8,128)}) fusion(s32[128]{0:T(128)S(1)} %get-tuple-element.346, s32[128]{0:T(128)S(1)} %get-tuple-element.347, pred[128]{0:T(512)(128)(4,1)S(1)} %compare_and_fusion, f32[1280]{0:T(1024)S(1)} %iota_convert_fusion), kind=kLoop, calls=%fused_computation.22 | loop fusion | flops 3932160 | bytes 1972352 | tf_op jit(solution)/shard_map/jit(_where)/select_n | solution.py:978
  24.5 1.7 pad_maximum_fusion.5
  26.2 1.6 collective-permute-start.5
  28.5 1.4 collective-permute-start.6
  30.9 1.2 copy.114
  32.9 5.7 %collective-permute-done.4.refs_2_ = bf16[640,1024]{1,0:T(8,128)(2,1)} collective-permute-done((bf16[640,1024]{1,0:T(8,128)(2,1)}, bf16[640,1024]{1,0:T(8,128)(2,1)}, u32[]{:S(2)}, u32[]{:S(2)}) %collective-permute-start.4) | collective-permute-done | bytes 1310752 | tf_op jit(solution)/shard_map/ppermute | solution.py:45
  40.6 1.7 copy.115
  43.4 1.4 collective-permute-start.9
  44.9 2.6 collective-permute-start.11
  48.4 1.6 collective-permute-start.10
  50.0 9.6 %collective-permute-done.11.refs_11_.refs_9_ = bf16[128,1024]{1,0:T(8,128)(2,1)S(1)} collective-permute-done((bf16[128,1024]{1,0:T(8,128)(2,1)S(1)}, bf16[128,1024]{1,0:T(8,128)(2,1)S(1)}, u32[]{:S(2)}, u32[]{:S(2)}) %collective-permute-start.11) | collective-permute-done | bytes 262176 | tf_op jit(solution)/shard_map/ppermute | solution.py:45
  61.3 1.9 collective-permute-done.9.refs_7_
  64.1 1.5 collective-permute-start.13
  66.4 1.5 collective-permute-start.14
  68.1 1.7 copy.117.refs_4_
  69.8 1.7 collective-permute-start.15
  76.9 9.7 %project_qkv.1 = (bf16[2560,256]{1,0:T(8,128)(2,1)S(1)}, bf16[2560,256]{1,0:T(8,128)(2,1)S(1)}, bf16[2560,256]{1,0:T(8,128)(2,1)S(1)}) custom-call(s32[6]{0:T(128)S(1)} %stack.19.ids, s32[1,20,5]{2,1,0:T(8,128)S(1)} %copy.119.info, bf16[640,1024]{1,0:T(8,128)(2,1)} %collective-permute-done.7.refs_0_, bf16[640,1024]{1,0:T(8,128)(2,1)} %collective-permute-done.3.refs_1_, ...), custom_call_target="tpu_custom_call" | custom-call | flops 4026531840 | bytes 12725248 | tf_op jit(solution)/shard_map/project_qkv/pallas_call | solution.py:217
  87.9 1.6 collective-permute-start.17
  90.7 5.3 %project_grad.1.do_ref = bf16[2560,256]{1,0:T(8,128)(2,1)S(1)} custom-call(s32[6]{0:T(128)S(1)} %stack.19.ids, bf16[384,1024]{1,0:T(8,128)(2,1)} %collective-permute-done.12.refs_0_.refs_4_, bf16[256,1024]{1,0:T(8,128)(2,1)S(1)} %collective-permute-done.16.refs_1_.refs_5_, bf16[640,1024]{1,0:T(8,128)(2,1)} %collective-permute-done.refs_2_.refs_6_, ...), custom_call_target="tpu_custom_call" | custom-call | flops 1342177280 | bytes 7077888 | tf_op jit(solution)/shard_map/project_grad/pallas_call | solution.py:217
  96.1 50.5 %attention.1 = (bf16[2560,256]{1,0:T(8,128)(2,1)S(1)}, bf16[2560,256]{1,0:T(8,128)(2,1)S(1)}, bf16[2560,256]{1,0:T(8,128)(2,1)S(1)}, bf16[2560,256]{1,0:T(8,128)(2,1)S(1)}) custom-call(s32[1,20,5]{2,1,0:T(8,128)S(1)} %copy.119.info, bf16[2560,256]{1,0:T(8,128)(2,1)S(1)} %get-tuple-element.213.q_ref, bf16[2560,256]{1,0:T(8,128)(2,1)S(1)} %project_grad.1.do_ref, ...), custom_call_target="tpu_custom_call" | custom-call | flops 31406948352 | bytes 12451840 | tf_op jit(solution)/shard_map/attention/pallas_call | solution.py:217
  146.6 4.4 %project_context.1 = (bf16[2,640,1024]{2,1,0:T(8,128)(2,1)S(1)}, bf16[2,640,1024]{2,1,0:T(8,128)(2,1)S(1)}) custom-call(s32[6]{0:T(128)S(1)} %stack.19.ids, bf16[2560,256]{1,0:T(8,128)(2,1)S(1)} %get-tuple-element.234.ctx.ctx_ref, bf16[128,256]{1,0:T(8,128)(2,1)S(1)} %bitcast.47, bf16[128,256]{1,0:T(8,128)(2,1)S(1)} %collective-permute-done.2.refs_7_.refs_1_, ...), custom_call_target="tpu_custom_call" | custom-call | flops 1342177280 | bytes 7077888 | tf_op jit(solution)/shard_map/project_context/pallas_call | solution.py:217
  151.2 1.5 collective-permute-start.19
  152.8 13.2 %attention_weights.1 = (bf16[2560,768]{1,0:T(8,128)(2,1)S(1)}, f32[8,768]{1,0:T(8,128)S(1)}, bf16[4,128,512]{2,1,0:T(8,128)(2,1)}, bf16[4,128,512]{2,1,0:T(8,128...) custom-call(s32[6]{0:T(128)S(1)} %stack.19.ids, s32[1,20,5]{2,1,0:T(8,128)S(1)} %copy.119.info, ...), custom_call_target="tpu_custom_call" | custom-call | flops 5368709120 | bytes 23756800 | tf_op jit(solution)/shard_map/attention_weights/pallas_call | solution.py:217
  166.0 1.9 copy-done.44
  167.9 8.9 %collective-permute-done.19.refs_17_ = bf16[512,1024]{1,0:T(8,128)(2,1)S(1)} collective-permute-done((bf16[512,1024]{1,0:T(8,128)(2,1)S(1)}, bf16[512,1024]{1,0:T(8,128)(2,1)S(1)}, u32[]{:S(2)}, u32[]{:S(2)}) %collective-permute-start.19) | collective-permute-done | bytes 1048608 | tf_op jit(solution)/shard_map/ppermute | solution.py:45
  176.9 1.2 add_terms.3
  178.2 1.4 collective-permute-start.21
  180.9 1.2 copy-done.36
  182.2 39.4 %mlp.1 = (bf16[2,640,1024]{2,1,0:T(8,128)(2,1)}, bf16[2,640,1024]{2,1,0:T(8,128)(2,1)}, bf16[2560,1024]{1,0:T(8,128)(2,1)}, f32[8,1024]{1,0:T(8,128)S(1)}, bf16[...) custom-call(s32[6]{0:T(128)S(1)} %stack.19.ids, ...), custom_call_target="tpu_custom_call" | custom-call | flops 26843545600 | bytes 29405184 | tf_op jit(solution)/shard_map/mlp/pallas_call | solution.py:217
  222.6 5.1 %collective-permute-done.24.refs_1_.refs_4_ = bf16[2,640,1024]{2,1,0:T(8,128)(2,1)S(1)} collective-permute-done((bf16[2,640,1024]{2,1,0:T(8,128)(2,1)}, bf16[2,640,1024]{2,1,0:T(8,128)(2,1)S(1)}, u32[]{:S(2)}, u32[]{:S(2)}) %collective-permute-start.24) | collective-permute-done | bytes 2621472 | tf_op jit(solution)/shard_map/ppermute | solution.py:45
  227.7 1.7 copy-done.2
  229.5 1.2 add_terms.4
  231.6 1.4 collective-permute-start.28
  234.1 1.7 add_stacks.3
  237.4 2.5 copy-done.46
  239.9 15.8 %norm_backward.1 = (bf16[2,640,1024]{2,1,0:T(8,128)(2,1)S(1)}, bf16[2,640,1024]{2,1,0:T(8,128)(2,1)S(1)}, f32[8,1024]{1,0:T(8,128)S(1)}) custom-call(s32[6]{0:T(128)S(1)} %stack.19.ids, bf16[2560,768]{1,0:T(8,128)(2,1)S(1)} %copy-done.45, bf16[2560,1024]{1,0:T(8,128)(2,1)S(1)} %copy-done.46, bf16[640,1024]{1,0:T(8,128)(2,1)} %collective-permute-done.7.refs_0_, ...), custom_call_target="tpu_custom_call" | custom-call | flops 9395240960 | bytes 23371776 | tf_op jit(solution)/shard_map/norm_backward/pallas_call | solution.py:217
  255.7 7.8 %collective-permute-done.26.refs_2_ = bf16[2,128,512]{2,1,0:T(8,128)(2,1)S(1)} collective-permute-done((bf16[2,128,512]{2,1,0:T(8,128)(2,1)}, bf16[2,128,512]{2,1,0:T(8,128)(2,1)S(1)}, u32[]{:S(2)}, u32[]{:S(2)}) %collective-permute-start.26) | collective-permute-done | bytes 262176 | tf_op jit(solution)/shard_map/ppermute | solution.py:45
  265.6 4.9 %collective-permute-done.30.refs_1_ = bf16[2,640,1024]{2,1,0:T(8,128)(2,1)S(1)} collective-permute-done((bf16[2,640,1024]{2,1,0:T(8,128)(2,1)S(1)}, bf16[2,640,1024]{2,1,0:T(8,128)(2,1)S(1)}, u32[]{:S(2)}, u32[]{:S(2)}) %collective-permute-start.30) | collective-permute-done | bytes 2621472 | tf_op jit(solution)/shard_map/ppermute | solution.py:45
  270.9 1.3 collective-permute-start.39
  272.1 1.3 add_stacks.4
  273.4 1.3 collective-permute-start.34
  275.5 5.6 %finish_output.1 = (f32[640,1024]{1,0:T(8,128)}, f32[16,1024]{1,0:T(8,128)S(1)}) custom-call(s32[6]{0:T(128)S(1)} %stack.19.ids, f32[640,1024]{1,0:T(8,128)S(1)} %copy-done, bf16[640,1024]{1,0:T(8,128)(2,1)} %grad_ref.3, bf16[2,640,1024]{2,1,0:T(8,128)(2,1)S(1)} %get-tuple-element.255.refs_0_, bf16[2,640,1024]{2,1,0:T(8,128)(2,1)S(1)} %collective-permute-done.20.refs_1_, ...), custom_call_target="tpu_custom_call" | custom-call | flops 10485760 | bytes 19824640 | tf_op jit(solution)/shard_map/finish_output/pallas_call | solution.py:217
  281.1 1.3 collective-permute-start.32
  282.4 1.6 collective-permute-start.33
  284.0 9.9 %collective-permute-done.32.refs_3_ = bf16[1,128,512]{2,1,0:T(8,128)(2,1)S(1)} collective-permute-done((bf16[1,128,512]{2,1,0:T(8,128)(2,1)S(1)}, bf16[1,128,512]{2,1,0:T(8,128)(2,1)S(1)}, u32[]{:S(2)}, u32[]{:S(2)}) %collective-permute-start.32) | collective-permute-done | bytes 131104 | tf_op jit(solution)/shard_map/ppermute | solution.py:45
  294.0 2.4 collective-permute-done.33.refs_7_
  296.4 4.3 %collective-permute-done.36 = f32[16,1024]{1,0:T(8,128)S(1)} collective-permute-done((f32[16,1024]{1,0:T(8,128)S(1)}, f32[16,1024]{1,0:T(8,128)S(1)}, u32[]{:S(2)}, u32[]{:S(2)}) %collective-permute-start.36) | collective-permute-done | bytes 65568 | tf_op jit(solution)/shard_map/ppermute | solution.py:45
  300.9 5.1 %collective-permute-done.37 = f32[16,1024]{1,0:T(8,128)S(1)} collective-permute-done((f32[16,1024]{1,0:T(8,128)S(1)}, f32[16,1024]{1,0:T(8,128)S(1)}, u32[]{:S(2)}, u32[]{:S(2)}) %collective-permute-start.37) | collective-permute-done | bytes 65568 | tf_op jit(solution)/shard_map/ppermute | solution.py:45
  306.1 2.9 collective-permute-start.42
  309.0 1.2 collective-permute-start.38
  310.3 3.0 collective-permute-done.38
  313.3 1.4 collective-permute-start.40
  314.9 1.8 finish_attention_weights.1
  316.7 7.2 %collective-permute-done.41.refs_3_ = bf16[1,128,1024]{2,1,0:T(8,128)(2,1)S(1)} collective-permute-done((bf16[1,128,1024]{2,1,0:T(8,128)(2,1)S(1)}, bf16[1,128,1024]{2,1,0:T(8,128)(2,1)S(1)}, u32[]{:S(2)}, u32[]{:S(2)}) %collective-permute-start.41) | collective-permute-done | bytes 262176 | tf_op jit(solution)/shard_map/ppermute | solution.py:45
  323.9 5.5 %collective-permute-done.42.refs_7_ = bf16[1,128,1024]{2,1,0:T(8,128)(2,1)S(1)} collective-permute-done((bf16[1,128,1024]{2,1,0:T(8,128)(2,1)S(1)}, bf16[1,128,1024]{2,1,0:T(8,128)(2,1)S(1)}, u32[]{:S(2)}, u32[]{:S(2)}) %collective-permute-start.42) | collective-permute-done | bytes 262176 | tf_op jit(solution)/shard_map/ppermute | solution.py:45
  329.4 1.2 finish_mlp_weights.1
  330.6 4.5 %finish_grad.1 = f32[640,1024]{1,0:T(8,128)} custom-call(bf16[640,1024]{1,0:T(8,128)(2,1)} %grad_ref.3, f32[640,1024]{1,0:T(8,128)S(1)} %copy-done.1, f32[640,1]{1,0:T(8,128)S(1)} %rsqrt.7.std_ref, bf16[2,640,1024]{2,1,0:T(8,128)(2,1)S(1)} %get-tuple-element.294.refs_0_, bf16[2,640,1024]{2,1,0:T(8,128)(2,1)S(1)} %collective-permute-done.30.refs_1_, ...), custom_call_target="tpu_custom_call" | custom-call | flops 7864320 | bytes 13109760 | tf_op jit(solution)/shard_map/finish_grad/pallas_call | solution.py:217
  (215 shorter events, 35.8 us)
Async XLA Ops:
  3.6 9.1 %copy-start.50 = (f32[256,128]{1,0:T(8,128)S(1)}, f32[256,128]{1,0:T(8,128)}, u32[]{:S(2)}) copy-start(f32[256,128]{1,0:T(8,128)} %param.25) | copy-start | bytes 393220
  5.9 27.0 %collective-permute-start.3 = (bf16[640,1024]{1,0:T(8,128)(2,1)}, bf16[640,1024]{1,0:T(8,128)(2,1)}, u32[]{:S(2)}, u32[]{:S(2)}) collective-permute-start(bf16[640,1024]{1,0:T(8,128)(2,1)} %get-tuple-element.196.refs_3_), channel_id=1, source_target_pairs={{0,1},{1,0},{2,3},{3,2},{4,5},{5,4},{6,7},{7,6},{8,9},{9,8},{10,11... | collective-permute-start | bytes 3932168 | tf_op jit(solution)/shard_map/ppermute | solution.py:45
  6.4 32.3 %collective-permute-start.4 = (bf16[640,1024]{1,0:T(8,128)(2,1)}, bf16[640,1024]{1,0:T(8,128)(2,1)}, u32[]{:S(2)}, u32[]{:S(2)}) collective-permute-start(bf16[640,1024]{1,0:T(8,128)(2,1)} %get-tuple-element.196.refs_3_), channel_id=1, source_target_pairs={{0,2},{1,3},{2,0},{3,1},{4,6},{5,7},{6,4},{7,5},{8,10},{9,11},{10,... | collective-permute-start | bytes 3932168 | tf_op jit(solution)/shard_map/ppermute | solution.py:45
  8.8 14.8 %collective-permute-start = (bf16[640,1024]{1,0:T(8,128)(2,1)}, bf16[640,1024]{1,0:T(8,128)(2,1)}, u32[]{:S(2)}, u32[]{:S(2)}) collective-permute-start(bf16[640,1024]{1,0:T(8,128)(2,1)} %grad_ref.3), channel_id=1, source_target_pairs={{0,1},{1,0},{2,3},{3,2},{4,5},{5,4},{6,7},{7,6},{8,9},{9,8},{10,11... | collective-permute-start | bytes 3932168 | tf_op jit(solution)/shard_map/ppermute | solution.py:45
  9.3 21.7 %copy-start.47 = (bf16[128,3,4,64]{0,3,2,1:T(8,128)(2,1)}, bf16[128,3,4,64]{0,3,2,1:T(8,128)(2,1)S(1)}, u32[]{:S(2)}) copy-start(bf16[128,3,4,64]{0,3,2,1:T(8,128)(2,1)S(1)} %copy.103) | copy-start | bytes 589828
  9.3 9.1 %copy-start.53 = (s32[2560]{0:T(1024)S(1)}, s32[2560]{0:T(1024)}, u32[]{:S(2)}) copy-start(s32[2560]{0:T(1024)} %param.17) | copy-start | bytes 30724
  9.3 9.2 %copy-start.52 = (s32[2560]{0:T(1024)S(1)}, s32[2560]{0:T(1024)}, u32[]{:S(2)}) copy-start(s32[2560]{0:T(1024)} %param.18) | copy-start | bytes 30724
  10.1 13.5 %collective-permute-start.1 = (bf16[128,768]{1,0:T(8,128)(2,1)}, bf16[128,768]{1,0:T(8,128)(2,1)S(1)}, u32[]{:S(2)}, u32[]{:S(2)}) collective-permute-start(bf16[128,768]{1,0:T(8,128)(2,1)} %copy.104), channel_id=1, source_target_pairs={{0,16},{4,20},{8,24},{12,28},{16,0},{20,4},{24,8},{28,12},{1,17},{... | collective-permute-start | bytes 589832 | tf_op jit(solution)/shard_map/ppermute | solution.py:45
  12.8 10.8 %collective-permute-start.2 = (bf16[128,256]{1,0:T(8,128)(2,1)S(1)}, bf16[128,256]{1,0:T(8,128)(2,1)S(1)}, u32[]{:S(2)}, u32[]{:S(2)}) collective-permute-start(bf16[128,256]{1,0:T(8,128)(2,1)S(1)} %bitcast.43), channel_id=1, source_target_pairs={{0,4},{4,0},{8,12},{12,8},{16,20},{20,16},{24,28},{28,24},{1,5},{5... | collective-permute-start | bytes 196616 | tf_op jit(solution)/shard_map/ppermute | solution.py:45
  23.6 47.9 %copy-start.14 = (bf16[128,768]{1,0:T(8,128)(2,1)}, bf16[128,768]{1,0:T(8,128)(2,1)S(1)}, u32[]{:S(2)}) copy-start(bf16[128,768]{1,0:T(8,128)(2,1)S(1)} %collective-permute-done.1.refs_5_) | copy-start | bytes 589828
  26.2 13.9 %collective-permute-start.5 = (bf16[256,768]{1,0:T(8,128)(2,1)}, bf16[256,768]{1,0:T(8,128)(2,1)}, u32[]{:S(2)}, u32[]{:S(2)}) collective-permute-start(bf16[256,768]{1,0:T(8,128)(2,1)} %pad_maximum_fusion.5), channel_id=1, source_target_pairs={{0,8},{4,12},{8,0},{12,4},{16,24},{20,28},{24,16},{28,20},{1,9},{5... | collective-permute-start | bytes 1179656 | tf_op jit(solution)/shard_map/ppermute | solution.py:45
  28.5 10.6 %collective-permute-start.6 = (bf16[256,256]{1,0:T(8,128)(2,1)}, bf16[256,256]{1,0:T(8,128)(2,1)}, u32[]{:S(2)}, u32[]{:S(2)}) collective-permute-start(bf16[256,256]{1,0:T(8,128)(2,1)} %pad_maximum_fusion.7), channel_id=1, source_target_pairs={{0,16},{4,20},{8,24},{12,28},{16,0},{20,4},{24,8},{28,12},{1,17},{... | collective-permute-start | bytes 393224 | tf_op jit(solution)/shard_map/ppermute | solution.py:45
  32.1 119.0 %copy-start.10 = (bf16[1024,128]{0,1:T(8,128)(2,1)}, bf16[1024,128]{0,1:T(8,128)(2,1)S(1)}, u32[]{:S(2)}) copy-start(bf16[1024,128]{0,1:T(8,128)(2,1)S(1)} %copy.114) | copy-start | bytes 786436
  32.1 39.5 %copy-start.40 = (f32[1024]{0:T(1024)S(1)}, f32[1024]{0:T(1024)}, u32[]{:S(2)}) copy-start(f32[1024]{0:T(1024)} %param.20) | copy-start | bytes 12292
  32.1 39.5 %copy-start.42 = (f32[1024]{0:T(1024)S(1)}, f32[1024]{0:T(1024)}, u32[]{:S(2)}) copy-start(f32[1024]{0:T(1024)} %param.19) | copy-start | bytes 12292
  40.0 24.0 %collective-permute-start.7 = (bf16[640,1024]{1,0:T(8,128)(2,1)}, bf16[640,1024]{1,0:T(8,128)(2,1)}, u32[]{:S(2)}, u32[]{:S(2)}) collective-permute-start(bf16[640,1024]{1,0:T(8,128)(2,1)} %collective-permute-done.4.refs_2_), channel_id=1, source_target_pairs={{0,1},{1,0},{2,3},{3,2},{4,5},{5,4},{6,7},{7,6},{8,9},{9,8},{10,11... | collective-permute-start | bytes 3932168 | tf_op jit(solution)/shard_map/ppermute | solution.py:45
  40.1 21.2 %collective-permute-start.8 = (bf16[384,1024]{1,0:T(8,128)(2,1)}, bf16[384,1024]{1,0:T(8,128)(2,1)}, u32[]{:S(2)}, u32[]{:S(2)}) collective-permute-start(bf16[384,1024]{1,0:T(8,128)(2,1)} %slice.39), channel_id=1, source_target_pairs={{0,2},{1,3},{2,0},{3,1},{4,6},{5,7},{6,4},{7,5},{8,10},{9,11},{10,... | collective-permute-start | bytes 2359304 | tf_op jit(solution)/shard_map/ppermute | solution.py:45
  43.4 19.7 %collective-permute-start.9 = (bf16[512,768]{1,0:T(8,128)(2,1)S(1)}, bf16[512,768]{1,0:T(8,128)(2,1)S(1)}, u32[]{:S(2)}, u32[]{:S(2)}) collective-permute-start(bf16[512,768]{1,0:T(8,128)(2,1)S(1)} %pad_maximum_fusion.2), channel_id=1, source_target_pairs={{0,4},{4,0},{8,12},{12,8},{16,20},{20,16},{24,28},{28,24},{1,5},{5... | collective-permute-start | bytes 2359304 | tf_op jit(solution)/shard_map/ppermute | solution.py:45
  44.9 14.7 %collective-permute-start.11 = (bf16[128,1024]{1,0:T(8,128)(2,1)S(1)}, bf16[128,1024]{1,0:T(8,128)(2,1)S(1)}, u32[]{:S(2)}, u32[]{:S(2)}) collective-permute-start(bf16[128,1024]{1,0:T(8,128)(2,1)S(1)} %convert_element_type.32.refs_10_.refs_8_), channel_id=1, source_target_pairs={{0,16},{4,20},{8,24},{12,28},{16,0},{20,4},{24,8},{28,12},{1,17},{... | collective-permute-start | bytes 786440 | tf_op jit(solution)/shard_map/ppermute | solution.py:45
  48.4 12.2 %collective-permute-start.10 = (bf16[512,256]{1,0:T(8,128)(2,1)S(1)}, bf16[512,256]{1,0:T(8,128)(2,1)S(1)}, u32[]{:S(2)}, u32[]{:S(2)}) collective-permute-start(bf16[512,256]{1,0:T(8,128)(2,1)S(1)} %pad_maximum_fusion.6), channel_id=1, source_target_pairs={{0,8},{4,12},{8,0},{12,4},{16,24},{20,28},{24,16},{28,20},{1,9},{5... | collective-permute-start | bytes 786440 | tf_op jit(solution)/shard_map/ppermute | solution.py:45
  64.1 22.6 %collective-permute-start.12 = (bf16[384,1024]{1,0:T(8,128)(2,1)}, bf16[384,1024]{1,0:T(8,128)(2,1)}, u32[]{:S(2)}, u32[]{:S(2)}) collective-permute-start(bf16[384,1024]{1,0:T(8,128)(2,1)} %collective-permute-done.8.refs_3_.refs_7_), channel_id=1, source_target_pairs={{0,1},{1,0},{2,3},{3,2},{4,5},{5,4},{6,7},{7,6},{8,9},{9,8},{10,11... | collective-permute-start | bytes 2359304 | tf_op jit(solution)/shard_map/ppermute | solution.py:45
  64.1 22.6 %collective-permute-start.13 = (bf16[256,1024]{1,0:T(8,128)(2,1)}, bf16[256,1024]{1,0:T(8,128)(2,1)}, u32[]{:S(2)}, u32[]{:S(2)}) collective-permute-start(bf16[256,1024]{1,0:T(8,128)(2,1)} %slice.40), channel_id=1, source_target_pairs={{0,2},{1,3},{2,0},{3,1},{4,6},{5,7},{6,4},{7,5},{8,10},{9,11},{10,... | collective-permute-start | bytes 1572872 | tf_op jit(solution)/shard_map/ppermute | solution.py:45
  66.4 20.3 %collective-permute-start.14 = (bf16[256,1024]{1,0:T(8,128)(2,1)}, bf16[256,1024]{1,0:T(8,128)(2,1)}, u32[]{:S(2)}, u32[]{:S(2)}) collective-permute-start(bf16[256,1024]{1,0:T(8,128)(2,1)} %pad_maximum_fusion.3), channel_id=1, source_target_pairs={{0,8},{4,12},{8,0},{12,4},{16,24},{20,28},{24,16},{28,20},{1,9},{5... | collective-permute-start | bytes 1572872 | tf_op jit(solution)/shard_map/ppermute | solution.py:45
  69.8 16.8 %collective-permute-start.15 = (bf16[128,1024]{1,0:T(8,128)(2,1)S(1)}, bf16[128,1024]{1,0:T(8,128)(2,1)S(1)}, u32[]{:S(2)}, u32[]{:S(2)}) collective-permute-start(bf16[128,1024]{1,0:T(8,128)(2,1)S(1)} %bitcast.39), channel_id=1, source_target_pairs={{0,16},{4,20},{8,24},{12,28},{16,0},{20,4},{24,8},{28,12},{1,17},{... | collective-permute-start | bytes 786440 | tf_op jit(solution)/shard_map/ppermute | solution.py:45
  76.9 9.9 %copy-start.13 = (bf16[128,1024]{1,0:T(8,128)(2,1)S(1)}, bf16[128,1024]{1,0:T(8,128)(2,1)}, u32[]{:S(2)}) copy-start(bf16[128,1024]{1,0:T(8,128)(2,1)} %copy-done.12) | copy-start | bytes 786436
  86.7 4.0 %collective-permute-start.16 = (bf16[256,1024]{1,0:T(8,128)(2,1)}, bf16[256,1024]{1,0:T(8,128)(2,1)S(1)}, u32[]{:S(2)}, u32[]{:S(2)}) collective-permute-start(bf16[256,1024]{1,0:T(8,128)(2,1)} %collective-permute-done.13.refs_4_.refs_8_), channel_id=1, source_target_pairs={{0,1},{1,0},{2,3},{3,2},{4,5},{5,4},{6,7},{7,6},{8,9},{9,8},{10,11... | collective-permute-start | bytes 1572872 | tf_op jit(solution)/shard_map/ppermute | solution.py:45
  87.9 58.7 %collective-permute-start.17 = (bf16[512,1024]{1,0:T(8,128)(2,1)S(1)}, bf16[512,1024]{1,0:T(8,128)(2,1)S(1)}, u32[]{:S(2)}, u32[]{:S(2)}) collective-permute-start(bf16[512,1024]{1,0:T(8,128)(2,1)S(1)} %pad_maximum_fusion), channel_id=1, source_target_pairs={{0,4},{4,0},{8,12},{12,8},{16,20},{20,16},{24,28},{28,24},{1,5},{5... | collective-permute-start | bytes 3145736 | tf_op jit(solution)/shard_map/ppermute | solution.py:45
  89.5 6.5 %copy-start.17 = (f32[1280,128]{1,0:T(8,128)S(1)}, f32[1280,128]{1,0:T(8,128)}, u32[]{:S(2)}) copy-start(f32[1280,128]{1,0:T(8,128)} %get-tuple-element.204.refs_13_.high.refs_14_) | copy-start | bytes 1966084
  89.5 6.5 %copy-start.19 = (f32[1280,128]{1,0:T(8,128)S(1)}, f32[1280,128]{1,0:T(8,128)}, u32[]{:S(2)}) copy-start(f32[1280,128]{1,0:T(8,128)} %get-tuple-element.202.refs_11_.cos.refs_12_) | copy-start | bytes 1966084
  89.5 57.0 %collective-permute-start.18 = (bf16[256,1024]{1,0:T(8,128)(2,1)S(1)}, bf16[256,1024]{1,0:T(8,128)(2,1)S(1)}, u32[]{:S(2)}, u32[]{:S(2)}) collective-permute-start(bf16[256,1024]{1,0:T(8,128)(2,1)S(1)} %pad_maximum_fusion.4), channel_id=1, source_target_pairs={{0,8},{4,12},{8,0},{12,4},{16,24},{20,28},{24,16},{28,20},{1,9},{5... | collective-permute-start | bytes 1572872 | tf_op jit(solution)/shard_map/ppermute | solution.py:45
  90.7 62.0 %copy-start.22 = (bf16[256,1024]{1,0:T(8,128)(2,1)}, bf16[256,1024]{1,0:T(8,128)(2,1)S(1)}, u32[]{:S(2)}) copy-start(bf16[256,1024]{1,0:T(8,128)(2,1)S(1)} %collective-permute-done.16.refs_1_.refs_5_) | copy-start | bytes 1572868
  151.0 25.8 %collective-permute-start.20 = (bf16[2,640,1024]{2,1,0:T(8,128)(2,1)S(1)}, bf16[2,640,1024]{2,1,0:T(8,128)(2,1)S(1)}, u32[]{:S(2)}, u32[]{:S(2)}) collective-permute-start(bf16[2,640,1024]{2,1,0:T(8,128)(2,1)S(1)} %get-tuple-element.253), channel_id=1, source_target_pairs={{0,1},{1,0},{2,3},{3,2},{4,5},{5,4},{6,7},{7,6},{8,9},{9,8},{10,11... | collective-permute-start | bytes 7864328 | tf_op jit(solution)/shard_map/ppermute | solution.py:45
  151.2 25.6 %collective-permute-start.19 = (bf16[512,1024]{1,0:T(8,128)(2,1)S(1)}, bf16[512,1024]{1,0:T(8,128)(2,1)S(1)}, u32[]{:S(2)}, u32[]{:S(2)}) collective-permute-start(bf16[512,1024]{1,0:T(8,128)(2,1)S(1)} %pad_maximum_fusion.1), channel_id=1, source_target_pairs={{0,4},{4,0},{8,12},{12,8},{16,20},{20,16},{24,28},{28,24},{1,5},{5... | collective-permute-start | bytes 3145736 | tf_op jit(solution)/shard_map/ppermute | solution.py:45
  178.2 44.3 %collective-permute-start.21 = (bf16[1,640,1024]{2,1,0:T(8,128)(2,1)}, bf16[1,640,1024]{2,1,0:T(8,128)(2,1)}, u32[]{:S(2)}, u32[]{:S(2)}) collective-permute-start(bf16[1,640,1024]{2,1,0:T(8,128)(2,1)} %add_terms.3), channel_id=1, source_target_pairs={{0,2},{1,3},{2,0},{3,1},{4,6},{5,7},{6,4},{7,5},{8,10},{9,11},{10,... | collective-permute-start | bytes 3932168 | tf_op jit(solution)/shard_map/ppermute | solution.py:45
  179.6 42.9 %collective-permute-start.22 = (bf16[4,128,512]{2,1,0:T(8,128)(2,1)}, bf16[4,128,512]{2,1,0:T(8,128)(2,1)S(1)}, u32[]{:S(2)}, u32[]{:S(2)}) collective-permute-start(bf16[4,128,512]{2,1,0:T(8,128)(2,1)} %get-tuple-element.276), channel_id=1, source_target_pairs={{0,4},{4,0},{8,12},{12,8},{16,20},{20,16},{24,28},{28,24},{1,5},{5... | collective-permute-start | bytes 1572872 | tf_op jit(solution)/shard_map/ppermute | solution.py:45
  180.2 42.3 %collective-permute-start.23 = (bf16[4,128,512]{2,1,0:T(8,128)(2,1)}, bf16[4,128,512]{2,1,0:T(8,128)(2,1)}, u32[]{:S(2)}, u32[]{:S(2)}) collective-permute-start(bf16[4,128,512]{2,1,0:T(8,128)(2,1)} %get-tuple-element.277), channel_id=1, source_target_pairs={{0,8},{4,12},{8,0},{12,4},{16,24},{20,28},{24,16},{28,20},{1,9},{5... | collective-permute-start | bytes 1572872 | tf_op jit(solution)/shard_map/ppermute | solution.py:45
  222.6 5.2 %collective-permute-start.24 = (bf16[2,640,1024]{2,1,0:T(8,128)(2,1)}, bf16[2,640,1024]{2,1,0:T(8,128)(2,1)S(1)}, u32[]{:S(2)}, u32[]{:S(2)}) collective-permute-start(bf16[2,640,1024]{2,1,0:T(8,128)(2,1)} %get-tuple-element.280), channel_id=1, source_target_pairs={{0,1},{1,0},{2,3},{3,2},{4,5},{5,4},{6,7},{7,6},{8,9},{9,8},{10,11... | collective-permute-start | bytes 7864328 | tf_op jit(solution)/shard_map/ppermute | solution.py:45
  229.5 7.9 %copy-start.39 = (bf16[512,768]{1,0:T(8,128)(2,1)S(1)}, bf16[512,768]{1,0:T(8,128)(2,1)}, u32[]{:S(2)}) copy-start(bf16[512,768]{1,0:T(8,128)(2,1)} %copy-done.37) | copy-start | bytes 2359300
  229.5 7.9 %copy-start.45 = (bf16[2560,768]{1,0:T(8,128)(2,1)S(1)}, bf16[2560,768]{1,0:T(8,128)(2,1)}, u32[]{:S(2)}) copy-start(bf16[2560,768]{1,0:T(8,128)(2,1)} %copy-done.44) | copy-start | bytes 11796484
  230.7 6.7 %copy-start.15 = (bf16[128,768]{1,0:T(8,128)(2,1)S(1)}, bf16[128,768]{1,0:T(8,128)(2,1)}, u32[]{:S(2)}) copy-start(bf16[128,768]{1,0:T(8,128)(2,1)} %copy-done.14) | copy-start | bytes 589828
  230.7 6.7 %copy-start.29 = (bf16[128,768]{1,0:T(8,128)(2,1)S(1)}, bf16[128,768]{1,0:T(8,128)(2,1)}, u32[]{:S(2)}) copy-start(bf16[128,768]{1,0:T(8,128)(2,1)} %copy.117.refs_4_) | copy-start | bytes 589828
  230.7 6.7 %copy-start.34 = (bf16[512,1024]{1,0:T(8,128)(2,1)S(1)}, bf16[512,1024]{1,0:T(8,128)(2,1)}, u32[]{:S(2)}) copy-start(bf16[512,1024]{1,0:T(8,128)(2,1)} %copy-done.32) | copy-start | bytes 3145732
  230.7 34.8 %collective-permute-start.25 = (bf16[1,640,1024]{2,1,0:T(8,128)(2,1)}, bf16[1,640,1024]{2,1,0:T(8,128)(2,1)}, u32[]{:S(2)}, u32[]{:S(2)}) collective-permute-start(bf16[1,640,1024]{2,1,0:T(8,128)(2,1)} %add_terms.4), channel_id=1, source_target_pairs={{0,2},{1,3},{2,0},{3,1},{4,6},{5,7},{6,4},{7,5},{8,10},{9,11},{10,... | collective-permute-start | bytes 3932168 | tf_op jit(solution)/shard_map/ppermute | solution.py:45
  231.6 31.9 %collective-permute-start.28 = (bf16[4,128,1024]{2,1,0:T(8,128)(2,1)}, bf16[4,128,1024]{2,1,0:T(8,128)(2,1)S(1)}, u32[]{:S(2)}, u32[]{:S(2)}) collective-permute-start(bf16[4,128,1024]{2,1,0:T(8,128)(2,1)} %get-tuple-element.292), channel_id=1, source_target_pairs={{0,4},{4,0},{8,12},{12,8},{16,20},{20,16},{24,28},{28,24},{1,5},{5... | collective-permute-start | bytes 3145736 | tf_op jit(solution)/shard_map/ppermute | solution.py:45
  233.0 31.5 %collective-permute-start.29 = (bf16[4,128,1024]{2,1,0:T(8,128)(2,1)}, bf16[4,128,1024]{2,1,0:T(8,128)(2,1)S(1)}, u32[]{:S(2)}, u32[]{:S(2)}) collective-permute-start(bf16[4,128,1024]{2,1,0:T(8,128)(2,1)} %get-tuple-element.293), channel_id=1, source_target_pairs={{0,8},{4,12},{8,0},{12,4},{16,24},{20,28},{24,16},{28,20},{1,9},{5... | collective-permute-start | bytes 3145736 | tf_op jit(solution)/shard_map/ppermute | solution.py:45
  235.9 27.6 %collective-permute-start.26 = (bf16[2,128,512]{2,1,0:T(8,128)(2,1)}, bf16[2,128,512]{2,1,0:T(8,128)(2,1)S(1)}, u32[]{:S(2)}, u32[]{:S(2)}) collective-permute-start(bf16[2,128,512]{2,1,0:T(8,128)(2,1)} %get-tuple-element.290), channel_id=1, source_target_pairs={{0,8},{4,12},{8,0},{12,4},{16,24},{20,28},{24,16},{28,20},{1,9},{5... | collective-permute-start | bytes 786440 | tf_op jit(solution)/shard_map/ppermute | solution.py:45
  236.8 26.7 %collective-permute-start.27 = (bf16[2,128,512]{2,1,0:T(8,128)(2,1)S(1)}, bf16[2,128,512]{2,1,0:T(8,128)(2,1)S(1)}, u32[]{:S(2)}, u32[]{:S(2)}) collective-permute-start(bf16[2,128,512]{2,1,0:T(8,128)(2,1)S(1)} %get-tuple-element.291), channel_id=1, source_target_pairs={{0,4},{4,0},{8,12},{12,8},{16,20},{20,16},{24,28},{28,24},{1,5},{5... | collective-permute-start | bytes 786440 | tf_op jit(solution)/shard_map/ppermute | solution.py:45
  265.5 6.6 %copy-start.5 = (bf16[4,128,1024]{2,1,0:T(8,128)(2,1)S(1)}, bf16[4,128,1024]{2,1,0:T(8,128)(2,1)}, u32[]{:S(2)}) copy-start(bf16[4,128,1024]{2,1,0:T(8,128)(2,1)} %copy-done.4) | copy-start | bytes 3145732
  265.5 6.6 %copy-start.7 = (bf16[4,128,1024]{2,1,0:T(8,128)(2,1)S(1)}, bf16[4,128,1024]{2,1,0:T(8,128)(2,1)}, u32[]{:S(2)}) copy-start(bf16[4,128,1024]{2,1,0:T(8,128)(2,1)} %copy-done.6) | copy-start | bytes 3145732
  265.5 6.6 %copy-start.9 = (bf16[4,128,1024]{2,1,0:T(8,128)(2,1)S(1)}, bf16[4,128,1024]{2,1,0:T(8,128)(2,1)}, u32[]{:S(2)}) copy-start(bf16[4,128,1024]{2,1,0:T(8,128)(2,1)} %copy-done.8) | copy-start | bytes 3145732
  265.5 5.0 %collective-permute-start.30 = (bf16[2,640,1024]{2,1,0:T(8,128)(2,1)S(1)}, bf16[2,640,1024]{2,1,0:T(8,128)(2,1)S(1)}, u32[]{:S(2)}, u32[]{:S(2)}) collective-permute-start(bf16[2,640,1024]{2,1,0:T(8,128)(2,1)S(1)} %get-tuple-element.295), channel_id=1, source_target_pairs={{0,1},{1,0},{2,3},{3,2},{4,5},{5,4},{6,7},{7,6},{8,9},{9,8},{10,11... | collective-permute-start | bytes 7864328 | tf_op jit(solution)/shard_map/ppermute | solution.py:45
  270.9 42.5 %collective-permute-start.39 = (bf16[1,640,1024]{2,1,0:T(8,128)(2,1)S(1)}, bf16[1,640,1024]{2,1,0:T(8,128)(2,1)S(1)}, u32[]{:S(2)}, u32[]{:S(2)}) collective-permute-start(bf16[1,640,1024]{2,1,0:T(8,128)(2,1)S(1)} %add_terms.5), channel_id=1, source_target_pairs={{0,2},{1,3},{2,0},{3,1},{4,6},{5,7},{6,4},{7,5},{8,10},{9,11},{10,... | collective-permute-start | bytes 3932168 | tf_op jit(solution)/shard_map/ppermute | solution.py:45
  273.4 23.0 %collective-permute-start.34 = (bf16[2,128,1024]{2,1,0:T(8,128)(2,1)S(1)}, bf16[2,128,1024]{2,1,0:T(8,128)(2,1)S(1)}, u32[]{:S(2)}, u32[]{:S(2)}) collective-permute-start(bf16[2,128,1024]{2,1,0:T(8,128)(2,1)S(1)} %get-tuple-element.312), channel_id=1, source_target_pairs={{0,8},{4,12},{8,0},{12,4},{16,24},{20,28},{24,16},{28,20},{1,9},{5... | collective-permute-start | bytes 1572872 | tf_op jit(solution)/shard_map/ppermute | solution.py:45
  274.7 21.6 %collective-permute-start.35 = (bf16[2,128,1024]{2,1,0:T(8,128)(2,1)S(1)}, bf16[2,128,1024]{2,1,0:T(8,128)(2,1)S(1)}, u32[]{:S(2)}, u32[]{:S(2)}) collective-permute-start(bf16[2,128,1024]{2,1,0:T(8,128)(2,1)S(1)} %get-tuple-element.313), channel_id=1, source_target_pairs={{0,4},{4,0},{8,12},{12,8},{16,20},{20,16},{24,28},{28,24},{1,5},{5... | collective-permute-start | bytes 1572872 | tf_op jit(solution)/shard_map/ppermute | solution.py:45
  281.1 1.3 collective-permute-start.31
  281.1 12.9 %collective-permute-start.32 = (bf16[1,128,512]{2,1,0:T(8,128)(2,1)S(1)}, bf16[1,128,512]{2,1,0:T(8,128)(2,1)S(1)}, u32[]{:S(2)}, u32[]{:S(2)}) collective-permute-start(bf16[1,128,512]{2,1,0:T(8,128)(2,1)S(1)} %get-tuple-element.310), channel_id=1, source_target_pairs={{0,16},{4,20},{8,24},{12,28},{16,0},{20,4},{24,8},{28,12},{1,17},{... | collective-permute-start | bytes 393224 | tf_op jit(solution)/shard_map/ppermute | solution.py:45
  282.4 14.0 %collective-permute-start.33 = (bf16[1,128,512]{2,1,0:T(8,128)(2,1)S(1)}, bf16[1,128,512]{2,1,0:T(8,128)(2,1)S(1)}, u32[]{:S(2)}, u32[]{:S(2)}) collective-permute-start(bf16[1,128,512]{2,1,0:T(8,128)(2,1)S(1)} %get-tuple-element.311), channel_id=1, source_target_pairs={{0,16},{4,20},{8,24},{12,28},{16,0},{20,4},{24,8},{28,12},{1,17},{... | collective-permute-start | bytes 393224 | tf_op jit(solution)/shard_map/ppermute | solution.py:45
  296.4 4.3 %collective-permute-start.36 = (f32[16,1024]{1,0:T(8,128)S(1)}, f32[16,1024]{1,0:T(8,128)S(1)}, u32[]{:S(2)}, u32[]{:S(2)}) collective-permute-start(f32[16,1024]{1,0:T(8,128)S(1)} %add.113), channel_id=1, source_target_pairs={{0,8},{4,12},{8,0},{12,4},{16,24},{20,28},{24,16},{28,20},{1,9},{5... | collective-permute-start | bytes 196616 | tf_op jit(solution)/shard_map/ppermute | solution.py:45
  300.7 5.4 %collective-permute-start.37 = (f32[16,1024]{1,0:T(8,128)S(1)}, f32[16,1024]{1,0:T(8,128)S(1)}, u32[]{:S(2)}, u32[]{:S(2)}) collective-permute-start(f32[16,1024]{1,0:T(8,128)S(1)} %add.114), channel_id=1, source_target_pairs={{0,16},{4,20},{8,24},{12,28},{16,0},{20,4},{24,8},{28,12},{1,17},{... | collective-permute-start | bytes 196616 | tf_op jit(solution)/shard_map/ppermute | solution.py:45
  306.1 17.8 %collective-permute-start.41 = (bf16[1,128,1024]{2,1,0:T(8,128)(2,1)S(1)}, bf16[1,128,1024]{2,1,0:T(8,128)(2,1)S(1)}, u32[]{:S(2)}, u32[]{:S(2)}) collective-permute-start(bf16[1,128,1024]{2,1,0:T(8,128)(2,1)S(1)} %get-tuple-element.327), channel_id=1, source_target_pairs={{0,16},{4,20},{8,24},{12,28},{16,0},{20,4},{24,8},{28,12},{1,17},{... | collective-permute-start | bytes 786440 | tf_op jit(solution)/shard_map/ppermute | solution.py:45
  306.1 23.3 %collective-permute-start.42 = (bf16[1,128,1024]{2,1,0:T(8,128)(2,1)S(1)}, bf16[1,128,1024]{2,1,0:T(8,128)(2,1)S(1)}, u32[]{:S(2)}, u32[]{:S(2)}) collective-permute-start(bf16[1,128,1024]{2,1,0:T(8,128)(2,1)S(1)} %get-tuple-element.328), channel_id=1, source_target_pairs={{0,16},{4,20},{8,24},{12,28},{16,0},{20,4},{24,8},{28,12},{1,17},{... | collective-permute-start | bytes 786440 | tf_op jit(solution)/shard_map/ppermute | solution.py:45
  309.0 4.3 %collective-permute-start.38 = (f32[16,1024]{1,0:T(8,128)S(1)}, f32[16,1024]{1,0:T(8,128)S(1)}, u32[]{:S(2)}, u32[]{:S(2)}) collective-permute-start(f32[16,1024]{1,0:T(8,128)S(1)} %add.115), channel_id=1, source_target_pairs={{0,4},{4,0},{8,12},{12,8},{16,20},{20,16},{24,28},{28,24},{1,5},{5... | collective-permute-start | bytes 196616 | tf_op jit(solution)/shard_map/ppermute | solution.py:45
  313.3 21.8 %collective-permute-start.40 = (f32[16,1024]{1,0:T(8,128)S(1)}, f32[16,1024]{1,0:T(8,128)S(1)}, u32[]{:S(2)}, u32[]{:S(2)}) collective-permute-start(f32[16,1024]{1,0:T(8,128)S(1)} %add.116), channel_id=1, source_target_pairs={{0,2},{1,3},{2,0},{3,1},{4,6},{5,7},{6,4},{7,5},{8,10},{9,11},{10,... | collective-permute-start | bytes 196616 | tf_op jit(solution)/shard_map/ppermute | solution.py:45
  316.7 13.9 %copy-start.1 = (f32[640,1024]{1,0:T(8,128)S(1)}, f32[640,1024]{1,0:T(8,128)}, u32[]{:S(2)}) copy-start(f32[640,1024]{1,0:T(8,128)} %get-tuple-element.332.norm_ref) | copy-start | bytes 7864324
  (33 other events, 98.8 us)

commit v8 on v7

--- a/solution.py
+++ b/solution.py
@@ -242,9 +242,10 @@
     return (block.astype(f32) * gain[...] + shift[...]).astype(bf16)
 
 
-def turn(block, cosine, low_sine, high_sine, sign):
+def turn(block, cosine, sine, sign):
     width = block.shape[1]
     step = min(width, 128)
+    lane = lax.broadcasted_iota(jnp.int32, (block.shape[0], step), 1) % HD
     done = []
     for start in range(0, width, step):
         part = block[:, start : start + step]
@@ -254,7 +255,7 @@
         else:
             left = jnp.concatenate([part[:, ROT // 2 :], part[:, : ROT // 2]], axis=1)
             right = jnp.concatenate([part[:, -ROT // 2 :], part[:, : -ROT // 2]], axis=1)
-        moved = left * low_sine[:, :step] + right * high_sine[:, :step]
+        moved = jnp.where(lane < ROT // 2, -left, right) * sine[:, :step]
         done.append(part * cosine[:, :step] + moved * sign)
     return done[0] if len(done) == 1 else jnp.concatenate(done, axis=1)
 
@@ -265,14 +266,71 @@
     return [pltpu.VMEM((model, columns), bf16), pltpu.SemaphoreType.DMA((pack.pieces(),))]
 
 
+def prepare_weights(qkv, dense, fc, out):
+    rows, columns = qkv.shape
+    width = columns // 3
+
+    def kernel(qkv_ref, dense_ref, fc_ref, out_ref, qkv_to, dense_to, fc_to, out_to):
+        for head in range(width // HD):
+            for kind in range(3):
+                at, own = (3 * head + kind) * HD, kind * width + head * HD
+                qkv_to[:, own : own + HD] = qkv_ref[:, at : at + HD].astype(bf16)
+        dense_to[...] = dense_ref[...].T.astype(bf16)
+        fc_to[...] = fc_ref[...].astype(bf16)
+        out_to[...] = out_ref[...].T.astype(bf16)
+
+    operands = [qkv, dense, fc, out]
+    outs = [shaped(*qkv.shape), shaped(*dense.shape[::-1]), shaped(*fc.shape), shaped(*out.shape[::-1])]
+    return call(
+        kernel,
+        "prepare_weights",
+        (1,),
+        [],
+        operands,
+        [resident(x.shape) for x in operands],
+        outs,
+        [resident(x.shape) for x in outs],
+        [],
+        rows * columns,
+    )
+
+
+def normalize(stream):
+    rows, model = stream.shape
+    block = 160
+
+    def kernel(stream_ref, sent_ref, norm_ref, std_ref):
+        field = stream_ref[...]
+        centred = field - jnp.sum(field, axis=1, keepdims=True) / model
+        variance = jnp.sum(centred * centred, axis=1, keepdims=True) / model
+        scale = lax.rsqrt(variance + eps_norm)
+        norm = centred * scale
+        norm_ref[...] = norm
+        sent_ref[...] = norm.astype(bf16)
+        std_ref[...] = scale
+
+    return call(
+        kernel,
+        "normalize",
+        (rows // block,),
+        [],
+        [stream],
+        [step_block(block, model)],
+        [shaped(rows, model), shaped(rows, model, dtype=f32), shaped(rows, 1, dtype=f32)],
+        [step_block(block, model), step_block(block, model), step_block(block, 1)],
+        [],
+        rows * model * 8,
+    )
+
+
 def project_qkv(ids, info, sent, gain, shift, pack, bias, tables, width):
     groups, held, rows, model = sent.groups, len(sent.arrays), sent.rows, sent.model
 
     def kernel(ids, info, *refs):
         sent_refs, refs = refs[:held], refs[held:]
         weight_refs, refs = refs[: len(pack.arrays)], refs[len(pack.arrays) :]
-        gain, shift, bias, cos, low, high, q_out, k_out, v_out = refs[:9]
-        block, arrived, whole, placed = refs[9:]
+        gain, shift, bias, cos, sine, q_out, k_out, v_out = refs[:8]
+        block, arrived, whole, placed = refs[8:]
         step = pl.program_id(0)
 
         @pl.when(step == 0)
@@ -293,7 +351,7 @@
         for at in range(rows // SEG):
             number = first + at
             table = pl.ds(pl.multiple_of(info[number // NB, number % NB, 4] * SEG, SEG), SEG)
-            tabs = (cos[table, :], low[table, :], high[table, :])
+            tabs = (cos[table, :], sine[table, :])
             own = slice(at * SEG, (at + 1) * SEG)
             q_out[own, :] = (turn(qkv[own, :width], *tabs, 1.0) * HD**-0.5).astype(bf16)
             k_out[own, :] = turn(qkv[own, width : 2 * width], *tabs, 1.0).astype(bf16)
@@ -356,7 +414,7 @@
 
 
 def attention_kernel(
-    info, q_ref, do_ref, k_ref, v_ref, cos, low, high, ctx_ref, dq_ref, dk_ref, dv_ref, dk_sum, dv_sum
+    info, q_ref, do_ref, k_ref, v_ref, cos, sine, ctx_ref, dq_ref, dk_ref, dv_ref, dk_sum, dv_sum
 ):
     tree, step = pl.program_id(0), pl.program_id(1)
     width = q_ref.shape[1]
@@ -416,7 +474,7 @@
             ctx_own = jnp.where(lane_head == h, context[h * SEG : (h + 1) * SEG], ctx_own)
             dq_own = jnp.where(lane_head == h, dq[h * SEG : (h + 1) * SEG], dq_own)
         ctx_ref[...] = ctx_own.astype(bf16)
-        dq_ref[...] = turn(dq_own * HD**-0.5, cos, low, high, -1.0).astype(bf16)
+        dq_ref[...] = turn(dq_own * HD**-0.5, cos, sine, -1.0).astype(bf16)
         for h in range(heads):
             own = slice(h * SEG, (h + 1) * SEG)
             part = slice(h * HD, (h + 1) * HD)
@@ -468,7 +526,7 @@
         (trees, NB),
         [info],
         [queries, grads, keys, values, *tables],
-        [block, block, whole, whole, table, table, table],
+        [block, block, whole, whole, table, table],
         [shaped(total, width)] * 4,
         [block, block, whole, whole],
         [pltpu.VMEM((NB, width, SEG), f32), pltpu.VMEM((NB, width, SEG), f32)],
@@ -519,8 +577,8 @@
     def kernel(ids, info, ctx_ref, dq_ref, dk_ref, dv_ref, *refs):
         sent_refs, refs = refs[:held], refs[held:]
         grad_refs, refs = refs[: len(grad.arrays)], refs[len(grad.arrays) :]
-        gain, shift, cos, low, high, grads, bias_ref, *stacks = refs[:11]
-        block, arrived, grad_block, grad_arrived, total, dense_total = refs[11:]
+        gain, shift, cos, sine, grads, bias_ref, *stacks = refs[:10]
+        block, arrived, grad_block, grad_arrived, total, dense_total = refs[10:]
         step = pl.program_id(0)
 
         @pl.when(step == 0)
@@ -537,7 +595,7 @@
             number = first + at
             table = pl.ds(pl.multiple_of(info[number // NB, number % NB, 4] * SEG, SEG), SEG)
             own = slice(at * SEG, (at + 1) * SEG)
-            turned = turn(dk_ref[own, :], cos[table, :], low[table, :], high[table, :], -1.0)
+            turned = turn(dk_ref[own, :], cos[table, :], sine[table, :], -1.0)
             grads[own, width : 2 * width] = turned.astype(bf16)
         grads[:, 2 * width :] = dv_ref[...]
         bias_ref[0:1, :] += jnp.sum(grads[...].astype(f32), axis=0, keepdims=True)
@@ -564,7 +622,7 @@
         [own_block(rows, width)] * 4
         + sent.specs
         + grad.specs
-        + [resident(x.shape) for x in operands[-5:]],
+        + [resident(x.shape) for x in operands[-4:]],
         outs,
         [step_block(rows, 3 * width)] + [resident(x.shape) for x in outs[1:]],
         sent.scratch()
@@ -973,10 +1031,8 @@
     frequency = 10000.0 ** (-((lane % half).astype(f32) * 2.0 / ROT))
     angle = place * frequency
     cosine = jnp.where(lane < ROT, jnp.cos(angle), 1.0)
-    sine = jnp.sin(angle)
-    low = jnp.where(lane < half, -sine, 0.0)
-    high = jnp.where((lane >= half) & (lane < ROT), sine, 0.0)
-    return cosine, low, high
+    sine = jnp.where(lane < ROT, jnp.sin(angle), 0.0)
+    return cosine, sine
 
 
 def by_kind(array, heads):
@@ -1028,17 +1084,14 @@
     near_bits = data_bits
     next_bits = data_bits[1:2] + data_bits[:1] + data_bits[2:]
 
-    qkv_pack = Pack(by_kind(qkv_weight.astype(bf16), heads), "dp", rows_first)
-    dense_pack = Pack(dense_weight.astype(bf16).T, "dp", columns_first)
-    fc_pack = Pack(fc_weight.astype(bf16), "dp", rows_first)
-    out_pack = Pack(out_weight.astype(bf16).T, "dp", rows_first)
-
-    row_mean = jnp.mean(stream_in, axis=-1, keepdims=True)
-    centred = stream_in - row_mean
-    row_var = jnp.mean(centred * centred, axis=-1, keepdims=True)
-    inv_std = lax.rsqrt(row_var + eps_norm)
-    normalized = centred * inv_std
-    sent = gather_far(normalized.astype(bf16), "tensor", tensor_bits)
+    blocks = prepare_weights(qkv_weight, dense_weight, fc_weight, out_weight)
+    qkv_pack = Pack(blocks[0], "dp", rows_first)
+    dense_pack = Pack(blocks[1], "dp", columns_first)
+    fc_pack = Pack(blocks[2], "dp", rows_first)
+    out_pack = Pack(blocks[3], "dp", rows_first)
+
+    sent_norm, normalized, inv_std = normalize(stream_in)
+    sent = gather_far(sent_norm, "tensor", tensor_bits)
 
     info = tree_table(segment_ids, parent_ids)
     tables = angle_tables()
@@ -1066,7 +1119,7 @@
         beside=[early, late, info, *tables, qkv_bias_own, fc_bias_own, sent_near, *sent],
     )
     early, late, info, *done = done
-    tables, (qkv_bias_own, fc_bias_own, sent_near), sent = done[:3], done[3:6], done[6:]
+    tables, (qkv_bias_own, fc_bias_own, sent_near), sent = done[:2], done[2:5], done[5:]
     early_far = gather_far(early, "tensor", tensor_bits)[1:]
     sent_near = [sent_near] + [swap(x, "tensor", 1) for x in sent[1:]]
     sent = [x for pair in zip(sent, sent_near) for x in pair]
@@ -1091,10 +1144,11 @@
     late_near = [swap(x, "tensor", 1) for x in late_far]
     far = zip(zip(early_far, late_far), zip(early_near, late_near))
     grad = Tokens([(out_grad,), (near,), *[x for pair in far for x in pair]], order)
-    grad_context = project_grad(ids, grad, dense_pack, width)
-    fc_pack.double()
     while len(out_pack.bits) > 1:
         out_pack.double()
+    (grad_context,) = tie_packs(out_pack, beside=[project_grad(ids, grad, dense_pack, width)])
+    fc_pack.double()
+    out_pack.double()
     done = attention(info, tables, queries, keys, values, grad_context)
     context, dq, dk, dv = tie_packs(fc_pack, out_pack, beside=done)
     dp_orders = [halving_order(near_bits), halving_order(next_bits)]
@@ -1106,11 +1160,10 @@
         attn_parts.add()
     attn_parts.send, context = tie(attn_parts.send, context)
     attn_parts.swap()
-    out_pack.double()
     done = attention_weights(
         ids, info, tables, context, dq, dk, dv, sent, grad, gain_attn, shift_attn, dp_orders
     )
-    grads, qkv_bias_sums, *stacks = tie_halves(tie_packs(out_pack, beside=done), attn_parts)
+    grads, qkv_bias_sums, *stacks = tie_halves(done, attn_parts)
     attn_parts.add()
     qkv_sums = [Halving(*stacks[:2], "dp", near_bits), Halving(*stacks[2:], "dp", next_bits)]
     sent.arrays[0], attn_parts.send = tie(sent.arrays[0], attn_parts.send)
@@ -1166,17 +1219,18 @@
         groups,
     )
 
-    sums = sums + swap(sums, "tensor", 1)
-    (sums,) = tie_halves([sums], *qkv_sums, *mlp_sums)
-    for bit in data_bits[1:]:
-        sums = sums + swap(sums, "dp", bit)
+    output, sums = tie_halves([output, sums], *qkv_sums)
     for parts in qkv_sums:
         parts.add()
+
+    sums = sums + swap(sums, "tensor", 1)
+    (sums,) = tie_halves([sums], *mlp_sums)
     add_stacks(mlp_sums)
     sums, *sends = tie(sums, *[parts.send for parts in mlp_sums])
     for parts, send in zip(mlp_sums, sends):
         parts.send = send
-    sums = sums + swap(sums, "dp", data_bits[0])
+    for bit in data_bits[::-1]:
+        sums = sums + swap(sums, "dp", bit)
     sums, back_parts.got = tie(sums, back_parts.got)
     back_parts.add()
     for bit in tensor_bits[1:]:

time: 340 us -> 344 us (1.012)
  local copies, waits for them, and re-layouts: 33.8 us -> 46.2 us
  Pallas kernels: 157 us -> 149 us
    unnamed x118 -> x175, local copies, waits for them, and re-layouts: 20.6 us -> 30.8 us
    pallas_call x17 -> x19, Pallas kernels: 157 us -> 149 us  [call(): pl.pallas_call(kernel, grid_spec=pltpu.PrefetchScalarGridSpec(num_scalar_...]
    optimization_barrier x4 -> x1, local copies, waits for them, and re-layouts: 4.4 us -> 0.77 us  [tie(): return lax.optimization_barrier(values)]
  transfers between devices with their start and end apart: 43 -> 43, of which waited for: 17 -> 17; matrix products, arithmetic and copies ran while one was open for 7% -> 9% of each run, Pallas kernels for 44% -> 41%
where the time goes in v8:
time: 344 us; the launch traced here: 343 us
  Pallas kernels  149 us (43%)
  waiting for transfers between devices  85.7 us (25%)
  local copies, waits for them, and re-layouts  46.2 us (13%)
  starting transfers between devices  43.3 us (13%)
  other arithmetic  16.3 us (5%)
    pallas_call x19, Pallas kernels, call(): pl.pallas_call(kernel, grid_spec=pltpu.PrefetchScalarGridSpec(num_scalar_...  149 us
    ppermute x43, waiting for transfers between devices, swap(): return lax.ppermute(block, axis, [(i, i ^ bit) for i in range(size)])  85.7 us
    ppermute x43, starting transfers between devices, swap(): return lax.ppermute(block, axis, [(i, i ^ bit) for i in range(size)])  43.3 us
    unnamed x175, local copies, waits for them, and re-layouts  30.8 us
  transfers between devices with their start and end apart: 43, of which 17 were waited for; matrix products, arithmetic and copies ran while one was open for 9% of the time, Pallas kernels for 41%

profile of v8, /device:TPU:0, one launch (start us, length us, event | category | flops | bytes accessed | tf_op | source)
XLA Modules:
  0.0 342.5 jit_solution(900833098878160613)
XLA Ops:
  0.7 1.8 copy-done.4
  2.5 2.3 normalize.1
  4.8 1.6 copy-done.14
  6.9 2.5 collective-permute-start.4
  11.5 2.7 collective-permute-start.1
  14.1 1.5 collective-permute-start.2
  19.5 1.3 fusion.13
  23.0 1.3 copy.60
  24.3 1.3 copy.61
  26.2 4.5 %fusion = (f32[1280,128]{1,0:T(8,128)}, f32[1280,128]{1,0:T(8,128)}) fusion(s32[128]{0:T(128)S(1)} %copy-done.82, s32[128]{0:T(128)} %get-tuple-element.350, pred[128]{0:T(512)(128)(4,1)} %compare_and_fusion, f32[1280]{0:T(1024)} %iota_convert_fusion), kind=kLoop, calls=%fused_computation.9 | loop fusion | flops 3112960 | bytes 1316992 | tf_op jit(solution)/shard_map/jit(_where)/select_n | solution.py:1034
  32.8 1.6 collective-permute-start.5
  35.2 1.5 pad_maximum_fusion.7
  37.1 1.3 copy.64
  38.4 1.4 dynamic_slice.6
  42.6 1.2 constant_dynamic-update-slice_fusion
  43.7 2.1 collective-permute-done.6.refs_8_.refs_2_
  48.9 2.5 collective-permute-start.11
  52.4 11.1 %collective-permute-done.11.refs_11_.refs_9_ = bf16[128,1024]{1,0:T(8,128)(2,1)S(1)} collective-permute-done((bf16[128,1024]{1,0:T(8,128)(2,1)S(1)}, bf16[128,1024]{1,0:T(8,128)(2,1)S(1)}, u32[]{:S(2)}, u32[]{:S(2)}) %collective-permute-start.11) | collective-permute-done | bytes 262176 | tf_op jit(solution)/shard_map/ppermute | solution.py:45
  63.5 2.3 collective-permute-done.10.refs_9_.refs_3_
  67.0 1.1 collective-permute-done.9.refs_7_
  68.9 1.1 copy-done.57
  70.0 1.5 collective-permute-start.13
  73.6 2.1 collective-permute-start.15
  77.5 1.1 copy-done.39
  78.6 1.1 copy-done.41
  79.7 1.3 copy-done.58
  81.0 1.1 copy-done.69
  82.2 8.5 %project_qkv.1 = (bf16[2560,256]{1,0:T(8,128)(2,1)S(1)}, bf16[2560,256]{1,0:T(8,128)(2,1)S(1)}, bf16[2560,256]{1,0:T(8,128)(2,1)S(1)}) custom-call(s32[6]{0:T(128)S(1)} %stack.19.ids, s32[1,20,5]{2,1,0:T(8,128)S(1)} %copy.68.info, bf16[640,1024]{1,0:T(8,128)(2,1)S(1)} %copy-done.58, bf16[640,1024]{1,0:T(8,128)(2,1)} %collective-permute-done.3.refs_1_, ...), custom_call_target="tpu_custom_call" | custom-call | flops 4026531840 | bytes 12069888 | tf_op jit(solution)/shard_map/project_qkv/pallas_call | solution.py:217
  90.7 1.7 collective-permute-done.14.refs_12_.refs_10_
  92.4 2.5 collective-permute-start.17
  94.9 1.1 pad_maximum_fusion
  96.6 5.0 %project_grad.1.do_ref = bf16[2560,256]{1,0:T(8,128)(2,1)S(1)} custom-call(s32[6]{0:T(128)S(1)} %stack.19.ids, bf16[384,1024]{1,0:T(8,128)(2,1)} %collective-permute-done.12.refs_0_.refs_4_, bf16[256,1024]{1,0:T(8,128)(2,1)S(1)} %collective-permute-done.16.refs_1_.refs_5_, bf16[640,1024]{1,0:T(8,128)(2,1)S(1)} %collective-permute-done.refs_2_.refs_6_, ...), custom_call_target="tpu_custom_call" | custom-call | flops 1342177280 | bytes 7077888 | tf_op jit(solution)/shard_map/project_grad/pallas_call | solution.py:217
  101.7 5.8 %collective-permute-done.17.refs_16_ = bf16[256,1024]{1,0:T(8,128)(2,1)S(1)} collective-permute-done((bf16[256,1024]{1,0:T(8,128)(2,1)S(1)}, bf16[256,1024]{1,0:T(8,128)(2,1)S(1)}, u32[]{:S(2)}, u32[]{:S(2)}) %collective-permute-start.17) | collective-permute-done | bytes 524320 | tf_op jit(solution)/shard_map/ppermute | solution.py:45
  108.8 50.1 %attention.1 = (bf16[2560,256]{1,0:T(8,128)(2,1)S(1)}, bf16[2560,256]{1,0:T(8,128)(2,1)S(1)}, bf16[2560,256]{1,0:T(8,128)(2,1)S(1)}, bf16[2560,256]{1,0:T(8,128)(2,1)S(1)}) custom-call(s32[1,20,5]{2,1,0:T(8,128)S(1)} %copy.68.info, bf16[2560,256]{1,0:T(8,128)(2,1)S(1)} %get-tuple-element.220.q_ref, bf16[2560,256]{1,0:T(8,128)(2,1)S(1)} %project_grad.1.do_ref, ...), custom_call_target="tpu_custom_call" | custom-call | flops 31406948352 | bytes 11796480 | tf_op jit(solution)/shard_map/attention/pallas_call | solution.py:217
  159.9 4.3 %project_context.1 = (bf16[2,640,1024]{2,1,0:T(8,128)(2,1)S(1)}, bf16[2,640,1024]{2,1,0:T(8,128)(2,1)S(1)}) custom-call(s32[6]{0:T(128)S(1)} %stack.19.ids, bf16[2560,256]{1,0:T(8,128)(2,1)S(1)} %get-tuple-element.245.ctx.ctx_ref, bf16[128,256]{1,0:T(8,128)(2,1)} %get-tuple-element.224.refs_6_.refs_0_, ...), custom_call_target="tpu_custom_call" | custom-call | flops 1342177280 | bytes 7077888 | tf_op jit(solution)/shard_map/project_context/pallas_call | solution.py:217
  164.3 12.5 %attention_weights.1 = (bf16[2560,768]{1,0:T(8,128)(2,1)S(1)}, f32[8,768]{1,0:T(8,128)S(1)}, bf16[4,128,512]{2,1,0:T(8,128)(2,1)}, bf16[4,128,512]{2,1,0:T(8,128...) custom-call(s32[6]{0:T(128)S(1)} %stack.19.ids, s32[1,20,5]{2,1,0:T(8,128)S(1)} %copy.68.info, ...), custom_call_target="tpu_custom_call" | custom-call | flops 5368709120 | bytes 23101440 | tf_op jit(solution)/shard_map/attention_weights/pallas_call | solution.py:217
  176.8 2.0 copy-done.75
  179.9 1.5 collective-permute-start.22
  181.4 1.7 collective-permute-start.23
  183.2 38.8 %mlp.1 = (bf16[2,640,1024]{2,1,0:T(8,128)(2,1)}, bf16[2,640,1024]{2,1,0:T(8,128)(2,1)}, bf16[2560,1024]{1,0:T(8,128)(2,1)}, f32[8,1024]{1,0:T(8,128)S(1)}, bf16[...) custom-call(s32[6]{0:T(128)S(1)} %stack.19.ids, ...), custom_call_target="tpu_custom_call" | custom-call | flops 26843545600 | bytes 29405184 | tf_op jit(solution)/shard_map/mlp/pallas_call | solution.py:217
  222.0 1.1 copy-done.16
  223.1 5.1 %collective-permute-done.24.refs_1_.refs_4_ = bf16[2,640,1024]{2,1,0:T(8,128)(2,1)S(1)} collective-permute-done((bf16[2,640,1024]{2,1,0:T(8,128)(2,1)}, bf16[2,640,1024]{2,1,0:T(8,128)(2,1)S(1)}, u32[]{:S(2)}, u32[]{:S(2)}) %collective-permute-start.24) | collective-permute-done | bytes 2621472 | tf_op jit(solution)/shard_map/ppermute | solution.py:45
  228.3 1.7 copy-done.2
  230.0 1.2 add_terms.4
  231.2 1.6 collective-permute-start.25
  234.4 1.7 collective-permute-start.26
  236.2 1.5 collective-permute-start.27
  237.8 2.5 copy-done.77
  240.2 15.3 %norm_backward.1 = (bf16[2,640,1024]{2,1,0:T(8,128)(2,1)S(1)}, bf16[2,640,1024]{2,1,0:T(8,128)(2,1)S(1)}, f32[8,1024]{1,0:T(8,128)S(1)}) custom-call(s32[6]{0:T(128)S(1)} %stack.19.ids, bf16[2560,768]{1,0:T(8,128)(2,1)S(1)} %copy-done.76, bf16[2560,1024]{1,0:T(8,128)(2,1)S(1)} %copy-done.77, bf16[640,1024]{1,0:T(8,128)(2,1)S(1)} %copy-done.61, ...), custom_call_target="tpu_custom_call" | custom-call | flops 9395240960 | bytes 23371776 | tf_op jit(solution)/shard_map/norm_backward/pallas_call | solution.py:217
  255.5 8.2 %collective-permute-done.26.refs_2_ = bf16[2,128,512]{2,1,0:T(8,128)(2,1)S(1)} collective-permute-done((bf16[2,128,512]{2,1,0:T(8,128)(2,1)}, bf16[2,128,512]{2,1,0:T(8,128)(2,1)S(1)}, u32[]{:S(2)}, u32[]{:S(2)}) %collective-permute-start.26) | collective-permute-done | bytes 262176 | tf_op jit(solution)/shard_map/ppermute | solution.py:45
  268.3 4.9 %collective-permute-done.30.refs_1_ = bf16[2,640,1024]{2,1,0:T(8,128)(2,1)S(1)} collective-permute-done((bf16[2,640,1024]{2,1,0:T(8,128)(2,1)S(1)}, bf16[2,640,1024]{2,1,0:T(8,128)(2,1)S(1)}, u32[]{:S(2)}, u32[]{:S(2)}) %collective-permute-start.30) | collective-permute-done | bytes 2621472 | tf_op jit(solution)/shard_map/ppermute | solution.py:45
  274.6 1.2 collective-permute-start.34
  277.0 2.4 collective-permute-start.32
  279.5 3.7 %finish_output.1 = (f32[640,1024]{1,0:T(8,128)}, f32[16,1024]{1,0:T(8,128)S(1)}) custom-call(s32[6]{0:T(128)S(1)} %stack.19.ids, f32[640,1024]{1,0:T(8,128)S(1)} %copy-done.5, bf16[640,1024]{1,0:T(8,128)(2,1)S(1)} %copy-done.1, bf16[2,640,1024]{2,1,0:T(8,128)(2,1)S(1)} %get-tuple-element.257.refs_0_, ...), custom_call_target="tpu_custom_call" | custom-call | flops 10485760 | bytes 19824640 | tf_op jit(solution)/shard_map/finish_output/pallas_call | solution.py:217
  283.2 7.8 %collective-permute-done.31.refs_3_ = bf16[1,128,512]{2,1,0:T(8,128)(2,1)S(1)} collective-permute-done((bf16[1,128,512]{2,1,0:T(8,128)(2,1)S(1)}, bf16[1,128,512]{2,1,0:T(8,128)(2,1)S(1)}, u32[]{:S(2)}, u32[]{:S(2)}) %collective-permute-start.31) | collective-permute-done | bytes 131104 | tf_op jit(solution)/shard_map/ppermute | solution.py:45
  291.0 1.7 collective-permute-done.32.refs_7_
  292.7 1.3 collective-permute-done.33
  294.2 3.4 collective-permute-start.41
  297.7 2.8 collective-permute-start.36
  300.5 23.4 %collective-permute-done.36 = f32[16,1024]{1,0:T(8,128)S(1)} collective-permute-done((f32[16,1024]{1,0:T(8,128)S(1)}, f32[16,1024]{1,0:T(8,128)S(1)}, u32[]{:S(2)}, u32[]{:S(2)}) %collective-permute-start.36) | collective-permute-done | bytes 65568 | tf_op jit(solution)/shard_map/ppermute | solution.py:45
  324.0 4.3 %collective-permute-done.37 = f32[16,1024]{1,0:T(8,128)S(1)} collective-permute-done((f32[16,1024]{1,0:T(8,128)S(1)}, f32[16,1024]{1,0:T(8,128)S(1)}, u32[]{:S(2)}, u32[]{:S(2)}) %collective-permute-start.37) | collective-permute-done | bytes 65568 | tf_op jit(solution)/shard_map/ppermute | solution.py:45
  329.0 3.6 %collective-permute-done.38 = f32[16,1024]{1,0:T(8,128)S(1)} collective-permute-done((f32[16,1024]{1,0:T(8,128)S(1)}, f32[16,1024]{1,0:T(8,128)S(1)}, u32[]{:S(2)}, u32[]{:S(2)}) %collective-permute-start.38) | collective-permute-done | bytes 65568 | tf_op jit(solution)/shard_map/ppermute | solution.py:45
  334.2 1.2 finish_mlp_weights.1
  336.3 2.9 finish_grad.1
  (262 shorter events, 45.1 us)
Async XLA Ops:
  0.6 8.7 %copy-start = (bf16[640,1024]{1,0:T(8,128)(2,1)S(1)}, bf16[640,1024]{1,0:T(8,128)(2,1)}, u32[]{:S(2)}) copy-start(bf16[640,1024]{1,0:T(8,128)(2,1)} %grad_ref.3) | copy-start | bytes 3932164
  2.5 7.1 %copy-start.54 = (f32[256,128]{1,0:T(8,128)S(1)}, f32[256,128]{1,0:T(8,128)}, u32[]{:S(2)}) copy-start(f32[256,128]{1,0:T(8,128)} %dense_ref.1) | copy-start | bytes 393220
  2.5 13.7 %copy-start.80 = (s32[2560]{0:T(1024)S(1)}, s32[2560]{0:T(1024)}, u32[]{:S(2)}) copy-start(s32[2560]{0:T(1024)} %param.17) | copy-start | bytes 30724
  2.5 13.8 %copy-start.79 = (s32[2560]{0:T(1024)S(1)}, s32[2560]{0:T(1024)}, u32[]{:S(2)}) copy-start(s32[2560]{0:T(1024)} %param.18) | copy-start | bytes 30724
  6.4 37.3 %collective-permute-start.3 = (bf16[640,1024]{1,0:T(8,128)(2,1)}, bf16[640,1024]{1,0:T(8,128)(2,1)}, u32[]{:S(2)}, u32[]{:S(2)}) collective-permute-start(bf16[640,1024]{1,0:T(8,128)(2,1)} %get-tuple-element.204.refs_3_), channel_id=1, source_target_pairs={{0,1},{1,0},{2,3},{3,2},{4,5},{5,4},{6,7},{7,6},{8,9},{9,8},{10,11... | collective-permute-start | bytes 3932168 | tf_op jit(solution)/shard_map/ppermute | solution.py:45
  6.9 36.9 %collective-permute-start.4 = (bf16[640,1024]{1,0:T(8,128)(2,1)}, bf16[640,1024]{1,0:T(8,128)(2,1)}, u32[]{:S(2)}, u32[]{:S(2)}) collective-permute-start(bf16[640,1024]{1,0:T(8,128)(2,1)} %get-tuple-element.204.refs_3_), channel_id=1, source_target_pairs={{0,2},{1,3},{2,0},{3,1},{4,6},{5,7},{6,4},{7,5},{8,10},{9,11},{10,... | collective-permute-start | bytes 3932168 | tf_op jit(solution)/shard_map/ppermute | solution.py:45
  9.4 22.7 %collective-permute-start = (bf16[640,1024]{1,0:T(8,128)(2,1)S(1)}, bf16[640,1024]{1,0:T(8,128)(2,1)S(1)}, u32[]{:S(2)}, u32[]{:S(2)}) collective-permute-start(bf16[640,1024]{1,0:T(8,128)(2,1)S(1)} %copy-done), channel_id=1, source_target_pairs={{0,1},{1,0},{2,3},{3,2},{4,5},{5,4},{6,7},{7,6},{8,9},{9,8},{10,11... | collective-permute-start | bytes 3932168 | tf_op jit(solution)/shard_map/ppermute | solution.py:45
  11.4 35.8 %copy-start.33 = (bf16[128,768]{1,0:T(8,128)(2,1)}, bf16[128,768]{1,0:T(8,128)(2,1)S(1)}, u32[]{:S(2)}) copy-start(bf16[128,768]{1,0:T(8,128)(2,1)S(1)} %get-tuple-element.205.refs_4_) | copy-start | bytes 589828
  11.4 83.5 %copy-start.21 = (bf16[128,1024]{1,0:T(8,128)(2,1)}, bf16[128,1024]{1,0:T(8,128)(2,1)S(1)}, u32[]{:S(2)}) copy-start(bf16[128,1024]{1,0:T(8,128)(2,1)S(1)} %get-tuple-element.260.refs_10_.refs_8_) | copy-start | bytes 786436
  11.4 96.0 %copy-start.24 = (bf16[128,1024]{1,0:T(8,128)(2,1)}, bf16[128,1024]{1,0:T(8,128)(2,1)S(1)}, u32[]{:S(2)}) copy-start(bf16[128,1024]{1,0:T(8,128)(2,1)S(1)} %get-tuple-element.264.refs_14_) | copy-start | bytes 786436
  11.5 20.6 %collective-permute-start.1 = (bf16[128,768]{1,0:T(8,128)(2,1)S(1)}, bf16[128,768]{1,0:T(8,128)(2,1)S(1)}, u32[]{:S(2)}, u32[]{:S(2)}) collective-permute-start(bf16[128,768]{1,0:T(8,128)(2,1)S(1)} %get-tuple-element.205.refs_4_), channel_id=1, source_target_pairs={{0,16},{4,20},{8,24},{12,28},{16,0},{20,4},{24,8},{28,12},{1,17},{... | collective-permute-start | bytes 589832 | tf_op jit(solution)/shard_map/ppermute | solution.py:45
  14.1 17.9 %collective-permute-start.2 = (bf16[128,256]{1,0:T(8,128)(2,1)}, bf16[128,256]{1,0:T(8,128)(2,1)}, u32[]{:S(2)}, u32[]{:S(2)}) collective-permute-start(bf16[128,256]{1,0:T(8,128)(2,1)} %get-tuple-element.224.refs_6_.refs_0_), channel_id=1, source_target_pairs={{0,4},{4,0},{8,12},{12,8},{16,20},{20,16},{24,28},{28,24},{1,5},{5... | collective-permute-start | bytes 196616 | tf_op jit(solution)/shard_map/ppermute | solution.py:45
  26.2 8.2 %copy-start.83 = (s32[1,20,1]{1,0,2:T(1,128)S(1)}, s32[1,20,1]{1,0,2:T(1,128)}, u32[]{:S(2)}) copy-start(s32[1,20,1]{1,0,2:T(1,128)} %copy.62) | copy-start | bytes 244
  32.0 16.3 %copy-start.36 = (bf16[128,768]{1,0:T(8,128)(2,1)}, bf16[128,768]{1,0:T(8,128)(2,1)S(1)}, u32[]{:S(2)}) copy-start(bf16[128,768]{1,0:T(8,128)(2,1)S(1)} %collective-permute-done.1.refs_5_) | copy-start | bytes 589828
  32.0 132.3 %copy-start.20 = (bf16[640,1024]{1,0:T(8,128)(2,1)}, bf16[640,1024]{1,0:T(8,128)(2,1)S(1)}, u32[]{:S(2)}) copy-start(bf16[640,1024]{1,0:T(8,128)(2,1)S(1)} %collective-permute-done.refs_2_.refs_6_) | copy-start | bytes 3932164
  32.0 43.6 %copy-start.71 = (f32[1024]{0:T(1024)S(1)}, f32[1024]{0:T(1024)}, u32[]{:S(2)}) copy-start(f32[1024]{0:T(1024)} %param.20) | copy-start | bytes 12292
  32.1 43.6 %copy-start.73 = (f32[1024]{0:T(1024)S(1)}, f32[1024]{0:T(1024)}, u32[]{:S(2)}) copy-start(f32[1024]{0:T(1024)} %param.19) | copy-start | bytes 12292
  32.8 13.9 %collective-permute-start.5 = (bf16[256,768]{1,0:T(8,128)(2,1)}, bf16[256,768]{1,0:T(8,128)(2,1)}, u32[]{:S(2)}, u32[]{:S(2)}) collective-permute-start(bf16[256,768]{1,0:T(8,128)(2,1)} %pad_maximum_fusion.5), channel_id=1, source_target_pairs={{0,8},{4,12},{8,0},{12,4},{16,24},{20,28},{24,16},{28,20},{1,9},{5... | collective-permute-start | bytes 1179656 | tf_op jit(solution)/shard_map/ppermute | solution.py:45
  36.7 9.1 %collective-permute-start.6 = (bf16[256,256]{1,0:T(8,128)(2,1)}, bf16[256,256]{1,0:T(8,128)(2,1)}, u32[]{:S(2)}, u32[]{:S(2)}) collective-permute-start(bf16[256,256]{1,0:T(8,128)(2,1)} %pad_maximum_fusion.7), channel_id=1, source_target_pairs={{0,16},{4,20},{8,24},{12,28},{16,0},{20,4},{24,8},{28,12},{1,17},{... | collective-permute-start | bytes 393224 | tf_op jit(solution)/shard_map/ppermute | solution.py:45
  46.7 22.2 %collective-permute-start.7 = (bf16[640,1024]{1,0:T(8,128)(2,1)}, bf16[640,1024]{1,0:T(8,128)(2,1)S(1)}, u32[]{:S(2)}, u32[]{:S(2)}) collective-permute-start(bf16[640,1024]{1,0:T(8,128)(2,1)} %collective-permute-done.4.refs_2_), channel_id=1, source_target_pairs={{0,1},{1,0},{2,3},{3,2},{4,5},{5,4},{6,7},{7,6},{8,9},{9,8},{10,11... | collective-permute-start | bytes 3932168 | tf_op jit(solution)/shard_map/ppermute | solution.py:45
  46.7 20.3 %collective-permute-start.8 = (bf16[384,1024]{1,0:T(8,128)(2,1)}, bf16[384,1024]{1,0:T(8,128)(2,1)}, u32[]{:S(2)}, u32[]{:S(2)}) collective-permute-start(bf16[384,1024]{1,0:T(8,128)(2,1)} %slice.39), channel_id=1, source_target_pairs={{0,2},{1,3},{2,0},{3,1},{4,6},{5,7},{6,4},{7,5},{8,10},{9,11},{10,... | collective-permute-start | bytes 2359304 | tf_op jit(solution)/shard_map/ppermute | solution.py:45
  48.3 19.7 %collective-permute-start.9 = (bf16[512,768]{1,0:T(8,128)(2,1)S(1)}, bf16[512,768]{1,0:T(8,128)(2,1)S(1)}, u32[]{:S(2)}, u32[]{:S(2)}) collective-permute-start(bf16[512,768]{1,0:T(8,128)(2,1)S(1)} %pad_maximum_fusion.2), channel_id=1, source_target_pairs={{0,4},{4,0},{8,12},{12,8},{16,20},{20,16},{24,28},{28,24},{1,5},{5... | collective-permute-start | bytes 2359304 | tf_op jit(solution)/shard_map/ppermute | solution.py:45
  48.9 14.6 %collective-permute-start.11 = (bf16[128,1024]{1,0:T(8,128)(2,1)S(1)}, bf16[128,1024]{1,0:T(8,128)(2,1)S(1)}, u32[]{:S(2)}, u32[]{:S(2)}) collective-permute-start(bf16[128,1024]{1,0:T(8,128)(2,1)S(1)} %get-tuple-element.260.refs_10_.refs_8_), channel_id=1, source_target_pairs={{0,16},{4,20},{8,24},{12,28},{16,0},{20,4},{24,8},{28,12},{1,17},{... | collective-permute-start | bytes 786440 | tf_op jit(solution)/shard_map/ppermute | solution.py:45
  52.3 13.5 %collective-permute-start.10 = (bf16[512,256]{1,0:T(8,128)(2,1)S(1)}, bf16[512,256]{1,0:T(8,128)(2,1)S(1)}, u32[]{:S(2)}, u32[]{:S(2)}) collective-permute-start(bf16[512,256]{1,0:T(8,128)(2,1)S(1)} %pad_maximum_fusion.6), channel_id=1, source_target_pairs={{0,8},{4,12},{8,0},{12,4},{16,24},{20,28},{24,16},{28,20},{1,9},{5... | collective-permute-start | bytes 786440 | tf_op jit(solution)/shard_map/ppermute | solution.py:45
  63.5 31.4 %copy-start.26 = (bf16[128,1024]{1,0:T(8,128)(2,1)}, bf16[128,1024]{1,0:T(8,128)(2,1)S(1)}, u32[]{:S(2)}) copy-start(bf16[128,1024]{1,0:T(8,128)(2,1)S(1)} %collective-permute-done.11.refs_11_.refs_9_) | copy-start | bytes 786436
  70.0 22.3 %collective-permute-start.12 = (bf16[384,1024]{1,0:T(8,128)(2,1)}, bf16[384,1024]{1,0:T(8,128)(2,1)}, u32[]{:S(2)}, u32[]{:S(2)}) collective-permute-start(bf16[384,1024]{1,0:T(8,128)(2,1)} %collective-permute-done.8.refs_3_.refs_7_), channel_id=1, source_target_pairs={{0,1},{1,0},{2,3},{3,2},{4,5},{5,4},{6,7},{7,6},{8,9},{9,8},{10,11... | collective-permute-start | bytes 2359304 | tf_op jit(solution)/shard_map/ppermute | solution.py:45
  70.0 20.6 %collective-permute-start.13 = (bf16[256,1024]{1,0:T(8,128)(2,1)}, bf16[256,1024]{1,0:T(8,128)(2,1)}, u32[]{:S(2)}, u32[]{:S(2)}) collective-permute-start(bf16[256,1024]{1,0:T(8,128)(2,1)} %slice.40), channel_id=1, source_target_pairs={{0,2},{1,3},{2,0},{3,1},{4,6},{5,7},{6,4},{7,5},{8,10},{9,11},{10,... | collective-permute-start | bytes 1572872 | tf_op jit(solution)/shard_map/ppermute | solution.py:45
  72.3 20.0 %collective-permute-start.14 = (bf16[256,1024]{1,0:T(8,128)(2,1)}, bf16[256,1024]{1,0:T(8,128)(2,1)}, u32[]{:S(2)}, u32[]{:S(2)}) collective-permute-start(bf16[256,1024]{1,0:T(8,128)(2,1)} %pad_maximum_fusion.3), channel_id=1, source_target_pairs={{0,8},{4,12},{8,0},{12,4},{16,24},{20,28},{24,16},{28,20},{1,9},{5... | collective-permute-start | bytes 1572872 | tf_op jit(solution)/shard_map/ppermute | solution.py:45
  73.6 17.1 %collective-permute-start.15 = (bf16[128,1024]{1,0:T(8,128)(2,1)S(1)}, bf16[128,1024]{1,0:T(8,128)(2,1)S(1)}, u32[]{:S(2)}, u32[]{:S(2)}) collective-permute-start(bf16[128,1024]{1,0:T(8,128)(2,1)S(1)} %get-tuple-element.264.refs_14_), channel_id=1, source_target_pairs={{0,16},{4,20},{8,24},{12,28},{16,0},{20,4},{24,8},{28,12},{1,17},{... | collective-permute-start | bytes 786440 | tf_op jit(solution)/shard_map/ppermute | solution.py:45
  92.3 4.3 %collective-permute-start.16 = (bf16[256,1024]{1,0:T(8,128)(2,1)}, bf16[256,1024]{1,0:T(8,128)(2,1)S(1)}, u32[]{:S(2)}, u32[]{:S(2)}) collective-permute-start(bf16[256,1024]{1,0:T(8,128)(2,1)} %collective-permute-done.13.refs_4_.refs_8_), channel_id=1, source_target_pairs={{0,1},{1,0},{2,3},{3,2},{4,5},{5,4},{6,7},{7,6},{8,9},{9,8},{10,11... | collective-permute-start | bytes 1572872 | tf_op jit(solution)/shard_map/ppermute | solution.py:45
  92.4 15.1 %collective-permute-start.17 = (bf16[256,1024]{1,0:T(8,128)(2,1)S(1)}, bf16[256,1024]{1,0:T(8,128)(2,1)S(1)}, u32[]{:S(2)}, u32[]{:S(2)}) collective-permute-start(bf16[256,1024]{1,0:T(8,128)(2,1)S(1)} %pad_maximum_fusion.4), channel_id=1, source_target_pairs={{0,8},{4,12},{8,0},{12,4},{16,24},{20,28},{24,16},{28,20},{1,9},{5... | collective-permute-start | bytes 1572872 | tf_op jit(solution)/shard_map/ppermute | solution.py:45
  96.0 62.9 %collective-permute-start.18 = (bf16[512,1024]{1,0:T(8,128)(2,1)S(1)}, bf16[512,1024]{1,0:T(8,128)(2,1)S(1)}, u32[]{:S(2)}, u32[]{:S(2)}) collective-permute-start(bf16[512,1024]{1,0:T(8,128)(2,1)S(1)} %pad_maximum_fusion), channel_id=1, source_target_pairs={{0,4},{4,0},{8,12},{12,8},{16,20},{20,16},{24,28},{28,24},{1,5},{5... | collective-permute-start | bytes 3145736 | tf_op jit(solution)/shard_map/ppermute | solution.py:45
  96.6 67.7 %copy-start.43 = (bf16[256,1024]{1,0:T(8,128)(2,1)}, bf16[256,1024]{1,0:T(8,128)(2,1)S(1)}, u32[]{:S(2)}) copy-start(bf16[256,1024]{1,0:T(8,128)(2,1)S(1)} %collective-permute-done.16.refs_1_.refs_5_) | copy-start | bytes 1572868
  101.6 7.2 %copy-start.40 = (f32[1280,128]{1,0:T(8,128)S(1)}, f32[1280,128]{1,0:T(8,128)}, u32[]{:S(2)}) copy-start(f32[1280,128]{1,0:T(8,128)} %get-tuple-element.211.refs_12_.sine.refs_13_) | copy-start | bytes 1966084
  101.6 7.1 %copy-start.42 = (f32[1280,128]{1,0:T(8,128)S(1)}, f32[1280,128]{1,0:T(8,128)}, u32[]{:S(2)}) copy-start(f32[1280,128]{1,0:T(8,128)} %get-tuple-element.210.refs_11_.cos.refs_12_) | copy-start | bytes 1966084
  108.3 50.6 %collective-permute-start.19 = (bf16[512,1024]{1,0:T(8,128)(2,1)S(1)}, bf16[512,1024]{1,0:T(8,128)(2,1)S(1)}, u32[]{:S(2)}, u32[]{:S(2)}) collective-permute-start(bf16[512,1024]{1,0:T(8,128)(2,1)S(1)} %pad_maximum_fusion.1), channel_id=1, source_target_pairs={{0,4},{4,0},{8,12},{12,8},{16,20},{20,16},{24,28},{28,24},{1,5},{5... | collective-permute-start | bytes 3145736 | tf_op jit(solution)/shard_map/ppermute | solution.py:45
  164.2 14.6 %collective-permute-start.20 = (bf16[2,640,1024]{2,1,0:T(8,128)(2,1)S(1)}, bf16[2,640,1024]{2,1,0:T(8,128)(2,1)S(1)}, u32[]{:S(2)}, u32[]{:S(2)}) collective-permute-start(bf16[2,640,1024]{2,1,0:T(8,128)(2,1)S(1)} %get-tuple-element.255), channel_id=1, source_target_pairs={{0,1},{1,0},{2,3},{3,2},{4,5},{5,4},{6,7},{7,6},{8,9},{9,8},{10,11... | collective-permute-start | bytes 7864328 | tf_op jit(solution)/shard_map/ppermute | solution.py:45
  179.3 42.8 %collective-permute-start.21 = (bf16[1,640,1024]{2,1,0:T(8,128)(2,1)S(1)}, bf16[1,640,1024]{2,1,0:T(8,128)(2,1)S(1)}, u32[]{:S(2)}, u32[]{:S(2)}) collective-permute-start(bf16[1,640,1024]{2,1,0:T(8,128)(2,1)S(1)} %add_terms.3), channel_id=1, source_target_pairs={{0,2},{1,3},{2,0},{3,1},{4,6},{5,7},{6,4},{7,5},{8,10},{9,11},{10,... | collective-permute-start | bytes 3932168 | tf_op jit(solution)/shard_map/ppermute | solution.py:45
  179.9 42.1 %collective-permute-start.22 = (bf16[4,128,512]{2,1,0:T(8,128)(2,1)}, bf16[4,128,512]{2,1,0:T(8,128)(2,1)S(1)}, u32[]{:S(2)}, u32[]{:S(2)}) collective-permute-start(bf16[4,128,512]{2,1,0:T(8,128)(2,1)} %get-tuple-element.278), channel_id=1, source_target_pairs={{0,4},{4,0},{8,12},{12,8},{16,20},{20,16},{24,28},{28,24},{1,5},{5... | collective-permute-start | bytes 1572872 | tf_op jit(solution)/shard_map/ppermute | solution.py:45
  181.4 40.6 %collective-permute-start.23 = (bf16[4,128,512]{2,1,0:T(8,128)(2,1)}, bf16[4,128,512]{2,1,0:T(8,128)(2,1)S(1)}, u32[]{:S(2)}, u32[]{:S(2)}) collective-permute-start(bf16[4,128,512]{2,1,0:T(8,128)(2,1)} %get-tuple-element.279), channel_id=1, source_target_pairs={{0,8},{4,12},{8,0},{12,4},{16,24},{20,28},{24,16},{28,20},{1,9},{5... | collective-permute-start | bytes 1572872 | tf_op jit(solution)/shard_map/ppermute | solution.py:45
  222.0 11.6 %copy-start.10 = (bf16[4,128,512]{2,1,0:T(8,128)(2,1)}, bf16[4,128,512]{2,1,0:T(8,128)(2,1)S(1)}, u32[]{:S(2)}) copy-start(bf16[4,128,512]{2,1,0:T(8,128)(2,1)S(1)} %collective-permute-done.22.refs_1_) | copy-start | bytes 1572868
  222.0 11.6 %copy-start.12 = (bf16[4,128,512]{2,1,0:T(8,128)(2,1)}, bf16[4,128,512]{2,1,0:T(8,128)(2,1)S(1)}, u32[]{:S(2)}) copy-start(bf16[4,128,512]{2,1,0:T(8,128)(2,1)S(1)} %collective-permute-done.23.refs_3_.refs_4_.refs_5_) | copy-start | bytes 1572868
  223.1 5.1 %collective-permute-start.24 = (bf16[2,640,1024]{2,1,0:T(8,128)(2,1)}, bf16[2,640,1024]{2,1,0:T(8,128)(2,1)S(1)}, u32[]{:S(2)}, u32[]{:S(2)}) collective-permute-start(bf16[2,640,1024]{2,1,0:T(8,128)(2,1)} %get-tuple-element.282), channel_id=1, source_target_pairs={{0,1},{1,0},{2,3},{3,2},{4,5},{5,4},{6,7},{7,6},{8,9},{9,8},{10,11... | collective-permute-start | bytes 7864328 | tf_op jit(solution)/shard_map/ppermute | solution.py:45
  230.0 7.7 %copy-start.61 = (bf16[640,1024]{1,0:T(8,128)(2,1)S(1)}, bf16[640,1024]{1,0:T(8,128)(2,1)}, u32[]{:S(2)}) copy-start(bf16[640,1024]{1,0:T(8,128)(2,1)} %copy-done.57) | copy-start | bytes 3932164
  230.0 7.7 %copy-start.70 = (bf16[512,768]{1,0:T(8,128)(2,1)S(1)}, bf16[512,768]{1,0:T(8,128)(2,1)}, u32[]{:S(2)}) copy-start(bf16[512,768]{1,0:T(8,128)(2,1)} %copy-done.68) | copy-start | bytes 2359300
  230.0 7.7 %copy-start.76 = (bf16[2560,768]{1,0:T(8,128)(2,1)S(1)}, bf16[2560,768]{1,0:T(8,128)(2,1)}, u32[]{:S(2)}) copy-start(bf16[2560,768]{1,0:T(8,128)(2,1)} %copy-done.75) | copy-start | bytes 11796484
  231.2 35.9 %collective-permute-start.25 = (bf16[1,640,1024]{2,1,0:T(8,128)(2,1)}, bf16[1,640,1024]{2,1,0:T(8,128)(2,1)S(1)}, u32[]{:S(2)}, u32[]{:S(2)}) collective-permute-start(bf16[1,640,1024]{2,1,0:T(8,128)(2,1)} %add_terms.4), channel_id=1, source_target_pairs={{0,2},{1,3},{2,0},{3,1},{4,6},{5,7},{6,4},{7,5},{8,10},{9,11},{10,... | collective-permute-start | bytes 3932168 | tf_op jit(solution)/shard_map/ppermute | solution.py:45
  232.8 32.4 %collective-permute-start.28 = (bf16[4,128,1024]{2,1,0:T(8,128)(2,1)}, bf16[4,128,1024]{2,1,0:T(8,128)(2,1)S(1)}, u32[]{:S(2)}, u32[]{:S(2)}) collective-permute-start(bf16[4,128,1024]{2,1,0:T(8,128)(2,1)} %get-tuple-element.294), channel_id=1, source_target_pairs={{0,4},{4,0},{8,12},{12,8},{16,20},{20,16},{24,28},{28,24},{1,5},{5... | collective-permute-start | bytes 3145736 | tf_op jit(solution)/shard_map/ppermute | solution.py:45
  233.3 32.9 %collective-permute-start.29 = (bf16[4,128,1024]{2,1,0:T(8,128)(2,1)}, bf16[4,128,1024]{2,1,0:T(8,128)(2,1)S(1)}, u32[]{:S(2)}, u32[]{:S(2)}) collective-permute-start(bf16[4,128,1024]{2,1,0:T(8,128)(2,1)} %copy-done.65), channel_id=1, source_target_pairs={{0,8},{4,12},{8,0},{12,4},{16,24},{20,28},{24,16},{28,20},{1,9},{5... | collective-permute-start | bytes 3145736 | tf_op jit(solution)/shard_map/ppermute | solution.py:45
  234.4 29.3 %collective-permute-start.26 = (bf16[2,128,512]{2,1,0:T(8,128)(2,1)}, bf16[2,128,512]{2,1,0:T(8,128)(2,1)S(1)}, u32[]{:S(2)}, u32[]{:S(2)}) collective-permute-start(bf16[2,128,512]{2,1,0:T(8,128)(2,1)} %get-tuple-element.292), channel_id=1, source_target_pairs={{0,8},{4,12},{8,0},{12,4},{16,24},{20,28},{24,16},{28,20},{1,9},{5... | collective-permute-start | bytes 786440 | tf_op jit(solution)/shard_map/ppermute | solution.py:45
  236.2 28.3 %collective-permute-start.27 = (bf16[2,128,512]{2,1,0:T(8,128)(2,1)}, bf16[2,128,512]{2,1,0:T(8,128)(2,1)S(1)}, u32[]{:S(2)}, u32[]{:S(2)}) collective-permute-start(bf16[2,128,512]{2,1,0:T(8,128)(2,1)} %get-tuple-element.293), channel_id=1, source_target_pairs={{0,4},{4,0},{8,12},{12,8},{16,20},{20,16},{24,28},{28,24},{1,5},{5... | collective-permute-start | bytes 786440 | tf_op jit(solution)/shard_map/ppermute | solution.py:45
  268.3 5.0 %collective-permute-start.30 = (bf16[2,640,1024]{2,1,0:T(8,128)(2,1)S(1)}, bf16[2,640,1024]{2,1,0:T(8,128)(2,1)S(1)}, u32[]{:S(2)}, u32[]{:S(2)}) collective-permute-start(bf16[2,640,1024]{2,1,0:T(8,128)(2,1)S(1)} %get-tuple-element.297), channel_id=1, source_target_pairs={{0,1},{1,0},{2,3},{3,2},{4,5},{5,4},{6,7},{7,6},{8,9},{9,8},{10,11... | collective-permute-start | bytes 7864328 | tf_op jit(solution)/shard_map/ppermute | solution.py:45
  273.6 59.0 %collective-permute-start.39 = (bf16[1,640,1024]{2,1,0:T(8,128)(2,1)S(1)}, bf16[1,640,1024]{2,1,0:T(8,128)(2,1)S(1)}, u32[]{:S(2)}, u32[]{:S(2)}) collective-permute-start(bf16[1,640,1024]{2,1,0:T(8,128)(2,1)S(1)} %add_terms.5), channel_id=1, source_target_pairs={{0,2},{1,3},{2,0},{3,1},{4,6},{5,7},{6,4},{7,5},{8,10},{9,11},{10,... | collective-permute-start | bytes 3932168 | tf_op jit(solution)/shard_map/ppermute | solution.py:45
  274.6 19.4 %collective-permute-start.34 = (bf16[2,128,1024]{2,1,0:T(8,128)(2,1)S(1)}, bf16[2,128,1024]{2,1,0:T(8,128)(2,1)S(1)}, u32[]{:S(2)}, u32[]{:S(2)}) collective-permute-start(bf16[2,128,1024]{2,1,0:T(8,128)(2,1)S(1)} %get-tuple-element.318), channel_id=1, source_target_pairs={{0,8},{4,12},{8,0},{12,4},{16,24},{20,28},{24,16},{28,20},{1,9},{5... | collective-permute-start | bytes 1572872 | tf_op jit(solution)/shard_map/ppermute | solution.py:45
  275.8 18.1 %collective-permute-start.35 = (bf16[2,128,1024]{2,1,0:T(8,128)(2,1)S(1)}, bf16[2,128,1024]{2,1,0:T(8,128)(2,1)S(1)}, u32[]{:S(2)}, u32[]{:S(2)}) collective-permute-start(bf16[2,128,1024]{2,1,0:T(8,128)(2,1)S(1)} %get-tuple-element.319), channel_id=1, source_target_pairs={{0,4},{4,0},{8,12},{12,8},{16,20},{20,16},{24,28},{28,24},{1,5},{5... | collective-permute-start | bytes 1572872 | tf_op jit(solution)/shard_map/ppermute | solution.py:45
  276.5 14.5 %collective-permute-start.31 = (bf16[1,128,512]{2,1,0:T(8,128)(2,1)S(1)}, bf16[1,128,512]{2,1,0:T(8,128)(2,1)S(1)}, u32[]{:S(2)}, u32[]{:S(2)}) collective-permute-start(bf16[1,128,512]{2,1,0:T(8,128)(2,1)S(1)} %get-tuple-element.312), channel_id=1, source_target_pairs={{0,16},{4,20},{8,24},{12,28},{16,0},{20,4},{24,8},{28,12},{1,17},{... | collective-permute-start | bytes 393224 | tf_op jit(solution)/shard_map/ppermute | solution.py:45
  277.0 15.7 %collective-permute-start.32 = (bf16[1,128,512]{2,1,0:T(8,128)(2,1)S(1)}, bf16[1,128,512]{2,1,0:T(8,128)(2,1)S(1)}, u32[]{:S(2)}, u32[]{:S(2)}) collective-permute-start(bf16[1,128,512]{2,1,0:T(8,128)(2,1)S(1)} %get-tuple-element.313), channel_id=1, source_target_pairs={{0,16},{4,20},{8,24},{12,28},{16,0},{20,4},{24,8},{28,12},{1,17},{... | collective-permute-start | bytes 393224 | tf_op jit(solution)/shard_map/ppermute | solution.py:45
  292.7 1.3 collective-permute-start.33
  294.2 40.0 %collective-permute-start.41 = (bf16[1,128,1024]{2,1,0:T(8,128)(2,1)S(1)}, bf16[1,128,1024]{2,1,0:T(8,128)(2,1)S(1)}, u32[]{:S(2)}, u32[]{:S(2)}) collective-permute-start(bf16[1,128,1024]{2,1,0:T(8,128)(2,1)S(1)} %get-tuple-element.333), channel_id=1, source_target_pairs={{0,16},{4,20},{8,24},{12,28},{16,0},{20,4},{24,8},{28,12},{1,17},{... | collective-permute-start | bytes 786440 | tf_op jit(solution)/shard_map/ppermute | solution.py:45
  297.6 36.6 %collective-permute-start.42 = (bf16[1,128,1024]{2,1,0:T(8,128)(2,1)S(1)}, bf16[1,128,1024]{2,1,0:T(8,128)(2,1)S(1)}, u32[]{:S(2)}, u32[]{:S(2)}) collective-permute-start(bf16[1,128,1024]{2,1,0:T(8,128)(2,1)S(1)} %get-tuple-element.334), channel_id=1, source_target_pairs={{0,16},{4,20},{8,24},{12,28},{16,0},{20,4},{24,8},{28,12},{1,17},{... | collective-permute-start | bytes 786440 | tf_op jit(solution)/shard_map/ppermute | solution.py:45
  297.7 26.2 %collective-permute-start.36 = (f32[16,1024]{1,0:T(8,128)S(1)}, f32[16,1024]{1,0:T(8,128)S(1)}, u32[]{:S(2)}, u32[]{:S(2)}) collective-permute-start(f32[16,1024]{1,0:T(8,128)S(1)} %add.91), channel_id=1, source_target_pairs={{0,16},{4,20},{8,24},{12,28},{16,0},{20,4},{24,8},{28,12},{1,17},{... | collective-permute-start | bytes 196616 | tf_op jit(solution)/shard_map/ppermute | solution.py:45
  323.9 4.3 %collective-permute-start.37 = (f32[16,1024]{1,0:T(8,128)S(1)}, f32[16,1024]{1,0:T(8,128)S(1)}, u32[]{:S(2)}, u32[]{:S(2)}) collective-permute-start(f32[16,1024]{1,0:T(8,128)S(1)} %add.92), channel_id=1, source_target_pairs={{0,8},{4,12},{8,0},{12,4},{16,24},{20,28},{24,16},{28,20},{1,9},{5... | collective-permute-start | bytes 196616 | tf_op jit(solution)/shard_map/ppermute | solution.py:45
  328.2 4.3 %collective-permute-start.38 = (f32[16,1024]{1,0:T(8,128)S(1)}, f32[16,1024]{1,0:T(8,128)S(1)}, u32[]{:S(2)}, u32[]{:S(2)}) collective-permute-start(f32[16,1024]{1,0:T(8,128)S(1)} %add.93), channel_id=1, source_target_pairs={{0,4},{4,0},{8,12},{12,8},{16,20},{20,16},{24,28},{28,24},{1,5},{5... | collective-permute-start | bytes 196616 | tf_op jit(solution)/shard_map/ppermute | solution.py:45
  332.6 6.7 %collective-permute-start.40 = (f32[16,1024]{1,0:T(8,128)S(1)}, f32[16,1024]{1,0:T(8,128)S(1)}, u32[]{:S(2)}, u32[]{:S(2)}) collective-permute-start(f32[16,1024]{1,0:T(8,128)S(1)} %add.94), channel_id=1, source_target_pairs={{0,2},{1,3},{2,0},{3,1},{4,6},{5,7},{6,4},{7,5},{8,10},{9,11},{10,... | collective-permute-start | bytes 196616 | tf_op jit(solution)/shard_map/ppermute | solution.py:45
  (63 other events, 235.2 us)

commit v9 on v8

--- a/solution.py
+++ b/solution.py
@@ -330,7 +330,7 @@
         sent_refs, refs = refs[:held], refs[held:]
         weight_refs, refs = refs[: len(pack.arrays)], refs[len(pack.arrays) :]
         gain, shift, bias, cos, sine, q_out, k_out, v_out = refs[:8]
-        block, arrived, whole, placed = refs[8:]
+        block, arrived, whole, placed, added = refs[8:]
         step = pl.program_id(0)
 
         @pl.when(step == 0)
@@ -344,9 +344,14 @@
         def _():
             for copy in pack.copies(weight_refs, whole, ids[1], placed):
                 copy.wait()
+            own = bias[pl.ds(ids[0], 1), :]
+            for head in range(width // HD):
+                for kind in range(3):
+                    at, to = (3 * head + kind) * HD, kind * width + head * HD
+                    added[:, to : to + HD] = own[:, at : at + HD]
 
         token = block[step % 2]
-        qkv = dot_nn(shift_gain(token, gain, shift), whole[...]) + bias[...]
+        qkv = dot_nn(shift_gain(token, gain, shift), whole[...]) + added[...]
         first = (ids[0] ^ ids[2 + step]) * (rows // SEG)
         for at in range(rows // SEG):
             number = first + at
@@ -370,9 +375,9 @@
         + [resident(x.shape) for x in operands[held + len(pack.arrays) :]],
         [out] * 3,
         [own_block(rows, width)] * 3,
-        sent.scratch() + weight_scratch(pack),
+        sent.scratch() + weight_scratch(pack) + [pltpu.VMEM((1, 3 * width), f32)],
         2 * groups * rows * model * 3 * width,
-        room=14,
+        room=62,
     )
 
 
@@ -672,7 +677,8 @@
         normed = shift_gain(token, gain, shift)
         count = 2
         parts = [slice(k * rows // count, (k + 1) * rows // count) for k in range(count)]
-        hidden = [dot_nn(normed[x], fc_whole[...]) + bias[...] for x in parts]
+        added = bias[pl.ds(ids[0], 1), :]
+        hidden = [dot_nn(normed[x], fc_whole[...]) + added for x in parts]
         back = [dot_nn(grads[x], out_whole[...]) for x in parts]
         for x, field, slope in zip(parts, hidden, back):
             chance = 0.5 + 0.5 * lax.erf(field * 0.7071067811865476)
@@ -1007,29 +1013,48 @@
 
 def tree_table(segment_ids, parent_ids):
     trees = segment_ids.shape[0] // TREE
-    segment = segment_ids.reshape(trees, NB, SEG)[:, :, 0]
-    parent = parent_ids.reshape(trees, NB, SEG)[:, :, 0]
-    block = lax.broadcasted_iota(jnp.int32, (trees, NB), 1)
-    trunk = block < NT
-    leaf = (parent != segment[:, :1]) & ~trunk
-    at = lax.broadcasted_iota(jnp.int32, (trees, NB, NB), 2)
-    owner = jnp.sum(jnp.where(segment[:, None, :] == parent[:, :, None], at, 0), axis=2)
-    odd = block % 2 == 1
-    first = jnp.where(trunk, block // 2 * 2, block)
-    second = jnp.where(trunk, block // 2 * 2 + 1, jnp.where(leaf, owner, block))
-    first_most = jnp.where(trunk & odd, SEG, 0)
-    second_most = jnp.where(trunk, jnp.where(odd, 0, -SEG), jnp.where(leaf, SEG, -SEG))
-    table = jnp.where(trunk, block, jnp.where(leaf, NT + 1, NT))
-    return jnp.stack([first, second, first_most, second_most, table], axis=2).astype(jnp.int32)
-
-
-def angle_tables():
+
+    def kernel(segment, parent, table):
+        for tree in range(trees):
+            for block in range(NT):
+                odd = block % 2
+                row = (block - odd, block - odd + 1, SEG * odd, -SEG * (1 - odd), block)
+                for at, value in enumerate(row):
+                    table[tree, block, at] = value
+
+            def place(block, carry):
+                first = tree * TREE
+                owner = parent[first + block * SEG]
+                leaf = (owner != segment[first]).astype(jnp.int32)
+                at = block
+                for other in range(NT, NB):
+                    at = jnp.where(segment[first + other * SEG] == owner, other, at)
+                table[tree, block, 0] = block
+                table[tree, block, 1] = at
+                table[tree, block, 2] = 0
+                table[tree, block, 3] = SEG * (2 * leaf - 1)
+                table[tree, block, 4] = NT + leaf
+                return carry
+
+            lax.fori_loop(NT, NB, place, 0)
+
+    smem = pl.BlockSpec(memory_space=pltpu.SMEM)
+    return pl.pallas_call(
+        kernel,
+        in_specs=[smem, smem],
+        out_specs=smem,
+        out_shape=jax.ShapeDtypeStruct((trees, NB, 5), jnp.int32),
+        name="tree_table",
+    )(segment_ids, parent_ids)
+
+
+def angle_tables(zero):
     places = TRUNK + 2 * SEG
     place = lax.broadcasted_iota(jnp.int32, (places, 2 * HD), 0).astype(f32)
     lane = lax.broadcasted_iota(jnp.int32, (places, 2 * HD), 1) % HD
     half = ROT // 2
     frequency = 10000.0 ** (-((lane % half).astype(f32) * 2.0 / ROT))
-    angle = place * frequency
+    angle = (place + zero) * frequency
     cosine = jnp.where(lane < ROT, jnp.cos(angle), 1.0)
     sine = jnp.where(lane < ROT, jnp.sin(angle), 0.0)
     return cosine, sine
@@ -1083,6 +1108,7 @@
     columns_first = data_bits[:1] + data_bits[:0:-1]
     near_bits = data_bits
     next_bits = data_bits[1:2] + data_bits[:1] + data_bits[2:]
+    qkv_bits = [data_bits[:1] + data_bits[:0:-1], data_bits[1:2] + data_bits[2:] + data_bits[:1]]
 
     blocks = prepare_weights(qkv_weight, dense_weight, fc_weight, out_weight)
     qkv_pack = Pack(blocks[0], "dp", rows_first)
@@ -1094,20 +1120,19 @@
     sent = gather_far(sent_norm, "tensor", tensor_bits)
 
     info = tree_table(segment_ids, parent_ids)
-    tables = angle_tables()
     gain_attn, shift_attn = norm_gain_attn[None, :], norm_shift_attn[None, :]
     gain_mlp, shift_mlp = norm_gain_mlp[None, :], norm_shift_mlp[None, :]
-    qkv_bias_own = by_kind(
-        lax.dynamic_slice_in_dim(qkv_bias, tensor_rank * qkv_width, qkv_width), heads
-    )[None, :]
-    fc_bias_own = lax.dynamic_slice_in_dim(fc_bias, tensor_rank * units, units)[None, :]
-
     sent_near, near = swap(sent[0], "tensor", 1), swap(out_grad, "tensor", 1)
     cut = rows_local * 3 // 5
     early, late = out_grad[:cut], out_grad[cut:]
     qkv_pack.double()
     dense_pack.double()
-    near, early, late = tie_packs(qkv_pack, dense_pack, fc_pack, beside=[near, early, late])
+    zero = jnp.zeros((), f32)
+    near, early, late, zero, qkv_bias, fc_bias, info = tie_packs(
+        qkv_pack, dense_pack, fc_pack, beside=[near, early, late, zero, qkv_bias, fc_bias, info]
+    )
+    tables = angle_tables(zero)
+    qkv_rows, fc_rows = qkv_bias.reshape(groups, qkv_width), fc_bias.reshape(groups, units)
     while len(qkv_pack.bits) > 1:
         qkv_pack.double()
         dense_pack.double()
@@ -1116,10 +1141,10 @@
         qkv_pack,
         dense_pack,
         out_pack,
-        beside=[early, late, info, *tables, qkv_bias_own, fc_bias_own, sent_near, *sent],
-    )
-    early, late, info, *done = done
-    tables, (qkv_bias_own, fc_bias_own, sent_near), sent = done[:2], done[2:5], done[5:]
+        beside=[early, late, *tables, qkv_rows, fc_rows, sent_near, *sent],
+    )
+    early, late, *done = done
+    tables, (qkv_rows, fc_rows, sent_near), sent = done[:2], done[2:5], done[5:]
     early_far = gather_far(early, "tensor", tensor_bits)[1:]
     sent_near = [sent_near] + [swap(x, "tensor", 1) for x in sent[1:]]
     sent = [x for pair in zip(sent, sent_near) for x in pair]
@@ -1136,7 +1161,7 @@
         fc_pack.double()
 
     done = project_qkv(
-        ids, info, sent, gain_attn, shift_attn, qkv_pack, qkv_bias_own, tables, width
+        ids, info, sent, gain_attn, shift_attn, qkv_pack, qkv_rows, tables, width
     )
     done = tie_packs(fc_pack, out_pack, beside=[*done, *early_near, *late_far])
     (queries, keys, values), done = done[:3], done[3:]
@@ -1152,6 +1177,7 @@
     done = attention(info, tables, queries, keys, values, grad_context)
     context, dq, dk, dv = tie_packs(fc_pack, out_pack, beside=done)
     dp_orders = [halving_order(near_bits), halving_order(next_bits)]
+    qkv_orders = [halving_order(bits) for bits in qkv_bits]
     attn_parts = Halving(
         *project_context(ids, context, dense_pack, groups, model), "tensor", tensor_bits
     )
@@ -1161,17 +1187,17 @@
     attn_parts.send, context = tie(attn_parts.send, context)
     attn_parts.swap()
     done = attention_weights(
-        ids, info, tables, context, dq, dk, dv, sent, grad, gain_attn, shift_attn, dp_orders
+        ids, info, tables, context, dq, dk, dv, sent, grad, gain_attn, shift_attn, qkv_orders
     )
     grads, qkv_bias_sums, *stacks = tie_halves(done, attn_parts)
     attn_parts.add()
-    qkv_sums = [Halving(*stacks[:2], "dp", near_bits), Halving(*stacks[2:], "dp", next_bits)]
+    qkv_sums = [Halving(*stacks[:2], "dp", qkv_bits[0]), Halving(*stacks[2:], "dp", qkv_bits[1])]
     sent.arrays[0], attn_parts.send = tie(sent.arrays[0], attn_parts.send)
     attn_parts.swap()
     for parts in qkv_sums:
         parts.swap()
     done = mlp(
-        ids, sent, grad, gain_mlp, shift_mlp, fc_pack, fc_bias_own, out_pack, dp_orders
+        ids, sent, grad, gain_mlp, shift_mlp, fc_pack, fc_rows, out_pack, dp_orders
     )
     done = tie_halves(done, attn_parts, *qkv_sums)
     mlp_send, mlp_keep, hidden, fc_bias_sums, *stacks = done
@@ -1226,10 +1252,12 @@
     sums = sums + swap(sums, "tensor", 1)
     (sums,) = tie_halves([sums], *mlp_sums)
     add_stacks(mlp_sums)
+    for bit in data_bits[2:]:
+        sums = sums + swap(sums, "dp", bit)
     sums, *sends = tie(sums, *[parts.send for parts in mlp_sums])
     for parts, send in zip(mlp_sums, sends):
         parts.send = send
-    for bit in data_bits[::-1]:
+    for bit in data_bits[:2]:
         sums = sums + swap(sums, "dp", bit)
     sums, back_parts.got = tie(sums, back_parts.got)
     back_parts.add()

time: 344 us -> 331 us (0.962)
  local copies, waits for them, and re-layouts: 46.2 us -> 25.2 us
  starting transfers between devices: 43.3 us -> 50 us
  Pallas kernels: 149 us -> 154 us
    unnamed x175 -> x153, local copies, waits for them, and re-layouts: 30.8 us -> 18.8 us
    ppermute x43, starting transfers between devices: 43.3 us -> 50 us  [swap(): return lax.ppermute(block, axis, [(i, i ^ bit) for i in range(size)])]
    select_n x5 -> x0, local copies, waits for them, and re-layouts: 5.26 us -> none  [the longest x1 1.29 us: tree_table(): table = jnp.where(trunk, block, jnp.where(leaf, NT + 1, NT))]
  transfers between devices with their start and end apart: 43 -> 43, of which waited for: 17 -> 21; matrix products, arithmetic and copies ran while one was open for 9% -> 5% of each run, Pallas kernels for 41% -> 45%
where the time goes in v9:
time: 331 us; the launch traced here: 330 us
  Pallas kernels  154 us (47%)
  waiting for transfers between devices  85.6 us (26%)
  starting transfers between devices  50 us (15%)
  local copies, waits for them, and re-layouts  25.2 us (8%)
  other arithmetic  13.2 us (4%)
    pallas_call x19, Pallas kernels, call(): pl.pallas_call(kernel, grid_spec=pltpu.PrefetchScalarGridSpec(num_scalar_...  152 us
    ppermute x43, waiting for transfers between devices, swap(): return lax.ppermute(block, axis, [(i, i ^ bit) for i in range(size)])  85.6 us
    ppermute x43, starting transfers between devices, swap(): return lax.ppermute(block, axis, [(i, i ^ bit) for i in range(size)])  50 us
    unnamed x153, local copies, waits for them, and re-layouts  18.8 us
    concatenate x8, other arithmetic, double(): jnp.concatenate(self.arrays, axis=0)  8.75 us
  transfers between devices with their start and end apart: 43, of which 21 were waited for; matrix products, arithmetic and copies ran while one was open for 5% of the time, Pallas kernels for 45%

profile of v9, /device:TPU:0, one launch (start us, length us, event | category | flops | bytes accessed | tf_op | source)
XLA Modules:
  0.0 329.9 jit_solution(8440772668835886151)
XLA Ops:
  1.2 1.7 copy-done.4
  2.9 2.2 normalize.1
  5.2 1.5 copy-done.14
  6.8 2.9 collective-permute-start.4
  11.5 2.7 collective-permute-start.1
  14.1 1.5 collective-permute-start.2
  17.4 2.0 tree_table.1.info
  19.4 3.9 %collective-permute-done.1.refs_5_ = bf16[128,768]{1,0:T(8,128)(2,1)S(1)} collective-permute-done((bf16[128,768]{1,0:T(8,128)(2,1)S(1)}, bf16[128,768]{1,0:T(8,128)(2,1)S(1)}, u32[]{:S(2)}, u32[]{:S(2)}) %collective-permute-start.1) | collective-permute-done | bytes 196640 | tf_op jit(solution)/shard_map/ppermute | solution.py:45
  24.8 1.5 pad_maximum_fusion.7
  26.4 3.4 %collective-permute-start.6 = (bf16[256,256]{1,0:T(8,128)(2,1)}, bf16[256,256]{1,0:T(8,128)(2,1)}, u32[]{:S(2)}, u32[]{:S(2)}) collective-permute-start(bf16[256,256]{1,0:T(8,128)(2,1)} %pad_maximum_fusion.7), channel_id=1, source_target_pairs={{0,16},{4,20},{8,24},{12,28},{16,0},{20,4},{24,8},{28,12},{1,17},{... | collective-permute-start | bytes 393224 | tf_op jit(solution)/shard_map/ppermute | solution.py:45
  29.8 3.8 %fusion = (f32[1280,128]{1,0:T(8,128)}, f32[1280,128]{1,0:T(8,128)}) fusion(s32[128]{0:T(128)S(1)} %get-tuple-element.350, s32[128]{0:T(128)S(1)} %get-tuple-element.351, pred[128]{0:T(512)(128)(4,1)S(1)} %compare_and_fusion, f32[1280]{0:T(1024)S(1)} %convert_add_fusion), kind=kLoop, calls=%fused_computation.9 | loop fusion | flops 3112960 | bytes 1316992 | tf_op jit(solution)/shard_map/jit(_where)/select_n | solution.py:1059
  33.5 1.3 reshape.42.refs_10_
  34.8 1.3 reshape.43.refs_20_
  36.2 2.8 collective-permute-done.4.refs_2_
  39.0 1.8 collective-permute-start.8
  41.9 1.6 collective-permute-start.9
  43.5 2.6 collective-permute-start.11
  47.0 1.6 collective-permute-start.10
  48.7 9.5 %collective-permute-done.11.refs_11_.refs_9_ = bf16[128,1024]{1,0:T(8,128)(2,1)S(1)} collective-permute-done((bf16[128,1024]{1,0:T(8,128)(2,1)S(1)}, bf16[128,1024]{1,0:T(8,128)(2,1)S(1)}, u32[]{:S(2)}, u32[]{:S(2)}) %collective-permute-start.11) | collective-permute-done | bytes 262176 | tf_op jit(solution)/shard_map/ppermute | solution.py:45
  58.2 1.2 collective-permute-done.10.refs_9_.refs_3_
  60.1 1.4 collective-permute-done.9.refs_7_
  63.0 1.6 collective-permute-start.14
  65.2 2.6 collective-permute-start.15
  67.8 11.3 %project_qkv.1 = (bf16[2560,256]{1,0:T(8,128)(2,1)}, bf16[2560,256]{1,0:T(8,128)(2,1)}, bf16[2560,256]{1,0:T(8,128)(2,1)}) custom-call(s32[6]{0:T(128)} %stack.11.ids, s32[1,20,5]{2,1,0:T(8,128)} %tree_table.1.info, bf16[640,1024]{1,0:T(8,128)(2,1)} %copy-done.52, bf16[640,1024]{1,0:T(8,128)(2,1)} %collective-permute-done.3.refs_1_, ...), custom_call_target="tpu_custom_call" | custom-call | flops 4026531840 | bytes 12079104 | tf_op jit(solution)/shard_map/project_qkv/pallas_call | solution.py:217
  79.1 2.8 collective-permute-done.15.refs_15_
  83.8 2.9 collective-permute-start.17
  87.9 1.6 collective-permute-start.18
  89.6 5.6 %project_grad.1.do_ref = bf16[2560,256]{1,0:T(8,128)(2,1)S(1)} custom-call(s32[6]{0:T(128)S(1)} %copy-done.49, bf16[384,1024]{1,0:T(8,128)(2,1)} %collective-permute-done.12.refs_0_.refs_4_, bf16[256,1024]{1,0:T(8,128)(2,1)S(1)} %collective-permute-done.16.refs_1_.refs_5_, bf16[640,1024]{1,0:T(8,128)(2,1)S(1)} %copy-done.21, ...), custom_call_target="tpu_custom_call" | custom-call | flops 1342177280 | bytes 7077888 | tf_op jit(solution)/shard_map/project_grad/pallas_call | solution.py:217
  95.1 4.2 %collective-permute-done.17.refs_16_ = bf16[256,1024]{1,0:T(8,128)(2,1)S(1)} collective-permute-done((bf16[256,1024]{1,0:T(8,128)(2,1)S(1)}, bf16[256,1024]{1,0:T(8,128)(2,1)S(1)}, u32[]{:S(2)}, u32[]{:S(2)}) %collective-permute-start.17) | collective-permute-done | bytes 524320 | tf_op jit(solution)/shard_map/ppermute | solution.py:45
  100.5 1.6 collective-permute-start.19
  102.1 49.9 %attention.1 = (bf16[2560,256]{1,0:T(8,128)(2,1)S(1)}, bf16[2560,256]{1,0:T(8,128)(2,1)S(1)}, bf16[2560,256]{1,0:T(8,128)(2,1)S(1)}, bf16[2560,256]{1,0:T(8,128)(2,1)S(1)}) custom-call(s32[1,20,5]{2,1,0:T(8,128)S(1)} %copy-done.48, bf16[2560,256]{1,0:T(8,128)(2,1)S(1)} %copy-done.70, bf16[2560,256]{1,0:T(8,128)(2,1)S(1)} %project_grad.1.do_ref, ...), custom_call_target="tpu_custom_call" | custom-call | flops 31406948352 | bytes 11796480 | tf_op jit(solution)/shard_map/attention/pallas_call | solution.py:217
  152.1 4.8 %project_context.1 = (bf16[2,640,1024]{2,1,0:T(8,128)(2,1)S(1)}, bf16[2,640,1024]{2,1,0:T(8,128)(2,1)S(1)}) custom-call(s32[6]{0:T(128)S(1)} %copy-done.49, bf16[2560,256]{1,0:T(8,128)(2,1)S(1)} %get-tuple-element.251.ctx.ctx_ref, bf16[128,256]{1,0:T(8,128)(2,1)} %get-tuple-element.230.refs_6_.refs_0_, ...), custom_call_target="tpu_custom_call" | custom-call | flops 1342177280 | bytes 7077888 | tf_op jit(solution)/shard_map/project_context/pallas_call | solution.py:217
  157.1 12.3 %attention_weights.1 = (bf16[2560,768]{1,0:T(8,128)(2,1)S(1)}, f32[8,768]{1,0:T(8,128)S(1)}, bf16[4,128,512]{2,1,0:T(8,128)(2,1)}, bf16[4,128,512]{2,1,0:T(8,128...) custom-call(s32[6]{0:T(128)S(1)} %copy-done.49, s32[1,20,5]{2,1,0:T(8,128)S(1)} %copy-done.48, ...), custom_call_target="tpu_custom_call" | custom-call | flops 5368709120 | bytes 23101440 | tf_op jit(solution)/shard_map/attention_weights/pallas_call | solution.py:217
  169.4 1.9 copy-done.68
  171.8 1.6 collective-permute-start.21
  173.8 1.7 collective-permute-start.23
  175.7 38.8 %mlp.1 = (bf16[2,640,1024]{2,1,0:T(8,128)(2,1)}, bf16[2,640,1024]{2,1,0:T(8,128)(2,1)}, bf16[2560,1024]{1,0:T(8,128)(2,1)}, f32[8,1024]{1,0:T(8,128)S(1)}, bf16[...) custom-call(s32[6]{0:T(128)S(1)} %copy-done.49, ...), custom_call_target="tpu_custom_call" | custom-call | flops 26843545600 | bytes 29417472 | tf_op jit(solution)/shard_map/mlp/pallas_call | solution.py:217
  215.7 5.1 %collective-permute-done.24.refs_1_.refs_4_ = bf16[2,640,1024]{2,1,0:T(8,128)(2,1)S(1)} collective-permute-done((bf16[2,640,1024]{2,1,0:T(8,128)(2,1)}, bf16[2,640,1024]{2,1,0:T(8,128)(2,1)S(1)}, u32[]{:S(2)}, u32[]{:S(2)}) %collective-permute-start.24) | collective-permute-done | bytes 2621472 | tf_op jit(solution)/shard_map/ppermute | solution.py:45
  220.8 1.7 copy-done.2
  222.6 1.2 add_terms.4
  224.4 1.5 collective-permute-start.28
  226.3 1.7 collective-permute-start.26
  228.0 1.3 collective-permute-start.27
  229.4 2.1 copy-done.69
  231.5 2.5 copy-done.73
  233.9 15.4 %norm_backward.1 = (bf16[2,640,1024]{2,1,0:T(8,128)(2,1)S(1)}, bf16[2,640,1024]{2,1,0:T(8,128)(2,1)S(1)}, f32[8,1024]{1,0:T(8,128)S(1)}) custom-call(s32[6]{0:T(128)S(1)} %copy-done.49, bf16[2560,768]{1,0:T(8,128)(2,1)S(1)} %copy-done.69, bf16[2560,1024]{1,0:T(8,128)(2,1)S(1)} %copy-done.73, bf16[640,1024]{1,0:T(8,128)(2,1)S(1)} %copy-done.55, ...), custom_call_target="tpu_custom_call" | custom-call | flops 9395240960 | bytes 23371776 | tf_op jit(solution)/shard_map/norm_backward/pallas_call | solution.py:217
  249.3 6.3 %collective-permute-done.26.refs_2_ = bf16[2,128,512]{2,1,0:T(8,128)(2,1)S(1)} collective-permute-done((bf16[2,128,512]{2,1,0:T(8,128)(2,1)S(1)}, bf16[2,128,512]{2,1,0:T(8,128)(2,1)S(1)}, u32[]{:S(2)}, u32[]{:S(2)}) %collective-permute-start.26) | collective-permute-done | bytes 262176 | tf_op jit(solution)/shard_map/ppermute | solution.py:45
  255.6 4.2 %collective-permute-done.27.refs_5_.refs_6_ = bf16[2,128,512]{2,1,0:T(8,128)(2,1)S(1)} collective-permute-done((bf16[2,128,512]{2,1,0:T(8,128)(2,1)S(1)}, bf16[2,128,512]{2,1,0:T(8,128)(2,1)S(1)}, u32[]{:S(2)}, u32[]{:S(2)}) %collective-permute-start.27) | collective-permute-done | bytes 262176 | tf_op jit(solution)/shard_map/ppermute | solution.py:45
  264.1 4.9 %collective-permute-done.30.refs_1_ = bf16[2,640,1024]{2,1,0:T(8,128)(2,1)S(1)} collective-permute-done((bf16[2,640,1024]{2,1,0:T(8,128)(2,1)S(1)}, bf16[2,640,1024]{2,1,0:T(8,128)(2,1)S(1)}, u32[]{:S(2)}, u32[]{:S(2)}) %collective-permute-start.30) | collective-permute-done | bytes 2621472 | tf_op jit(solution)/shard_map/ppermute | solution.py:45
  269.4 1.6 collective-permute-start.39
  271.3 2.6 collective-permute-start.34
  274.5 1.5 collective-permute-start.32
  276.0 3.7 %finish_output.1 = (f32[640,1024]{1,0:T(8,128)}, f32[16,1024]{1,0:T(8,128)S(1)}) custom-call(s32[6]{0:T(128)S(1)} %copy-done.49, f32[640,1024]{1,0:T(8,128)S(1)} %copy-done.5, bf16[640,1024]{1,0:T(8,128)(2,1)S(1)} %copy-done.1, bf16[2,640,1024]{2,1,0:T(8,128)(2,1)S(1)} %get-tuple-element.263.refs_0_, ...), custom_call_target="tpu_custom_call" | custom-call | flops 10485760 | bytes 19824640 | tf_op jit(solution)/shard_map/finish_output/pallas_call | solution.py:217
  279.7 8.9 %collective-permute-done.31.refs_3_ = bf16[1,128,512]{2,1,0:T(8,128)(2,1)S(1)} collective-permute-done((bf16[1,128,512]{2,1,0:T(8,128)(2,1)S(1)}, bf16[1,128,512]{2,1,0:T(8,128)(2,1)S(1)}, u32[]{:S(2)}, u32[]{:S(2)}) %collective-permute-start.31) | collective-permute-done | bytes 131104 | tf_op jit(solution)/shard_map/ppermute | solution.py:45
  288.7 1.5 collective-permute-done.32.refs_7_
  290.1 1.3 collective-permute-done.33
  291.7 6.0 %collective-permute-done.36 = f32[16,1024]{1,0:T(8,128)S(1)} collective-permute-done((f32[16,1024]{1,0:T(8,128)S(1)}, f32[16,1024]{1,0:T(8,128)S(1)}, u32[]{:S(2)}, u32[]{:S(2)}) %collective-permute-start.36) | collective-permute-done | bytes 65568 | tf_op jit(solution)/shard_map/ppermute | solution.py:45
  297.8 2.9 collective-permute-start.42
  301.2 3.8 %collective-permute-done.37 = f32[16,1024]{1,0:T(8,128)S(1)} collective-permute-done((f32[16,1024]{1,0:T(8,128)S(1)}, f32[16,1024]{1,0:T(8,128)S(1)}, u32[]{:S(2)}, u32[]{:S(2)}) %collective-permute-start.37) | collective-permute-done | bytes 65568 | tf_op jit(solution)/shard_map/ppermute | solution.py:45
  305.1 5.8 %collective-permute-done.38 = f32[16,1024]{1,0:T(8,128)S(1)} collective-permute-done((f32[16,1024]{1,0:T(8,128)S(1)}, f32[16,1024]{1,0:T(8,128)S(1)}, u32[]{:S(2)}, u32[]{:S(2)}) %collective-permute-start.38) | collective-permute-done | bytes 65568 | tf_op jit(solution)/shard_map/ppermute | solution.py:45
  312.4 4.5 %collective-permute-done.41.refs_3_ = bf16[1,128,1024]{2,1,0:T(8,128)(2,1)S(1)} collective-permute-done((bf16[1,128,1024]{2,1,0:T(8,128)(2,1)S(1)}, bf16[1,128,1024]{2,1,0:T(8,128)(2,1)S(1)}, u32[]{:S(2)}, u32[]{:S(2)}) %collective-permute-start.41) | collective-permute-done | bytes 262176 | tf_op jit(solution)/shard_map/ppermute | solution.py:45
  316.9 5.5 %collective-permute-done.42.refs_7_ = bf16[1,128,1024]{2,1,0:T(8,128)(2,1)S(1)} collective-permute-done((bf16[1,128,1024]{2,1,0:T(8,128)(2,1)S(1)}, bf16[1,128,1024]{2,1,0:T(8,128)(2,1)S(1)}, u32[]{:S(2)}, u32[]{:S(2)}) %collective-permute-start.42) | collective-permute-done | bytes 262176 | tf_op jit(solution)/shard_map/ppermute | solution.py:45
  322.5 1.2 finish_mlp_weights.1
  323.7 2.9 finish_grad.1
  (224 shorter events, 29.6 us)
Async XLA Ops:
  0.6 15.0 %copy-start = (bf16[640,1024]{1,0:T(8,128)(2,1)S(1)}, bf16[640,1024]{1,0:T(8,128)(2,1)}, u32[]{:S(2)}) copy-start(bf16[640,1024]{1,0:T(8,128)(2,1)} %grad_ref.3) | copy-start | bytes 3932164
  0.7 22.7 %collective-permute-start = (bf16[640,1024]{1,0:T(8,128)(2,1)}, bf16[640,1024]{1,0:T(8,128)(2,1)S(1)}, u32[]{:S(2)}, u32[]{:S(2)}) collective-permute-start(bf16[640,1024]{1,0:T(8,128)(2,1)} %grad_ref.3), channel_id=1, source_target_pairs={{0,1},{1,0},{2,3},{3,2},{4,5},{5,4},{6,7},{7,6},{8,9},{9,8},{10,11... | collective-permute-start | bytes 3932168 | tf_op jit(solution)/shard_map/ppermute | solution.py:45
  6.6 29.5 %collective-permute-start.3 = (bf16[640,1024]{1,0:T(8,128)(2,1)}, bf16[640,1024]{1,0:T(8,128)(2,1)}, u32[]{:S(2)}, u32[]{:S(2)}) collective-permute-start(bf16[640,1024]{1,0:T(8,128)(2,1)} %get-tuple-element.210.refs_3_), channel_id=1, source_target_pairs={{0,1},{1,0},{2,3},{3,2},{4,5},{5,4},{6,7},{7,6},{8,9},{9,8},{10,11... | collective-permute-start | bytes 3932168 | tf_op jit(solution)/shard_map/ppermute | solution.py:45
  6.8 32.2 %collective-permute-start.4 = (bf16[640,1024]{1,0:T(8,128)(2,1)}, bf16[640,1024]{1,0:T(8,128)(2,1)}, u32[]{:S(2)}, u32[]{:S(2)}) collective-permute-start(bf16[640,1024]{1,0:T(8,128)(2,1)} %get-tuple-element.210.refs_3_), channel_id=1, source_target_pairs={{0,2},{1,3},{2,0},{3,1},{4,6},{5,7},{6,4},{7,5},{8,10},{9,11},{10,... | collective-permute-start | bytes 3932168 | tf_op jit(solution)/shard_map/ppermute | solution.py:45
  11.5 29.3 %copy-start.29 = (bf16[128,768]{1,0:T(8,128)(2,1)}, bf16[128,768]{1,0:T(8,128)(2,1)S(1)}, u32[]{:S(2)}) copy-start(bf16[128,768]{1,0:T(8,128)(2,1)S(1)} %get-tuple-element.211.refs_4_) | copy-start | bytes 589828
  11.5 75.2 %copy-start.22 = (bf16[128,1024]{1,0:T(8,128)(2,1)}, bf16[128,1024]{1,0:T(8,128)(2,1)S(1)}, u32[]{:S(2)}) copy-start(bf16[128,1024]{1,0:T(8,128)(2,1)S(1)} %get-tuple-element.266.refs_10_.refs_8_) | copy-start | bytes 786436
  11.5 87.8 %copy-start.25 = (bf16[128,1024]{1,0:T(8,128)(2,1)}, bf16[128,1024]{1,0:T(8,128)(2,1)S(1)}, u32[]{:S(2)}) copy-start(bf16[128,1024]{1,0:T(8,128)(2,1)S(1)} %get-tuple-element.270.refs_14_) | copy-start | bytes 786436
  11.5 11.8 %collective-permute-start.1 = (bf16[128,768]{1,0:T(8,128)(2,1)S(1)}, bf16[128,768]{1,0:T(8,128)(2,1)S(1)}, u32[]{:S(2)}, u32[]{:S(2)}) collective-permute-start(bf16[128,768]{1,0:T(8,128)(2,1)S(1)} %get-tuple-element.211.refs_4_), channel_id=1, source_target_pairs={{0,16},{4,20},{8,24},{12,28},{16,0},{20,4},{24,8},{28,12},{1,17},{... | collective-permute-start | bytes 589832 | tf_op jit(solution)/shard_map/ppermute | solution.py:45
  14.1 5.3 %collective-permute-start.2 = (bf16[128,256]{1,0:T(8,128)(2,1)}, bf16[128,256]{1,0:T(8,128)(2,1)}, u32[]{:S(2)}, u32[]{:S(2)}) collective-permute-start(bf16[128,256]{1,0:T(8,128)(2,1)} %get-tuple-element.230.refs_6_.refs_0_), channel_id=1, source_target_pairs={{0,4},{4,0},{8,12},{12,8},{16,20},{20,16},{24,28},{28,24},{1,5},{5... | collective-permute-start | bytes 196616 | tf_op jit(solution)/shard_map/ppermute | solution.py:45
  23.3 23.7 %copy-start.31 = (bf16[128,768]{1,0:T(8,128)(2,1)}, bf16[128,768]{1,0:T(8,128)(2,1)S(1)}, u32[]{:S(2)}) copy-start(bf16[128,768]{1,0:T(8,128)(2,1)S(1)} %collective-permute-done.1.refs_5_) | copy-start | bytes 589828
  23.3 23.7 %copy-start.20 = (bf16[640,1024]{1,0:T(8,128)(2,1)}, bf16[640,1024]{1,0:T(8,128)(2,1)S(1)}, u32[]{:S(2)}) copy-start(bf16[640,1024]{1,0:T(8,128)(2,1)S(1)} %collective-permute-done.refs_2_.refs_6_) | copy-start | bytes 3932164
  24.2 14.8 %collective-permute-start.5 = (bf16[256,768]{1,0:T(8,128)(2,1)}, bf16[256,768]{1,0:T(8,128)(2,1)}, u32[]{:S(2)}, u32[]{:S(2)}) collective-permute-start(bf16[256,768]{1,0:T(8,128)(2,1)} %pad_maximum_fusion.5), channel_id=1, source_target_pairs={{0,8},{4,12},{8,0},{12,4},{16,24},{20,28},{24,16},{28,20},{1,9},{5... | collective-permute-start | bytes 1179656 | tf_op jit(solution)/shard_map/ppermute | solution.py:45
  26.4 12.6 %collective-permute-start.6 = (bf16[256,256]{1,0:T(8,128)(2,1)}, bf16[256,256]{1,0:T(8,128)(2,1)}, u32[]{:S(2)}, u32[]{:S(2)}) collective-permute-start(bf16[256,256]{1,0:T(8,128)(2,1)} %pad_maximum_fusion.7), channel_id=1, source_target_pairs={{0,16},{4,20},{8,24},{12,28},{16,0},{20,4},{24,8},{28,12},{1,17},{... | collective-permute-start | bytes 393224 | tf_op jit(solution)/shard_map/ppermute | solution.py:45
  39.0 22.5 %collective-permute-start.7 = (bf16[640,1024]{1,0:T(8,128)(2,1)}, bf16[640,1024]{1,0:T(8,128)(2,1)S(1)}, u32[]{:S(2)}, u32[]{:S(2)}) collective-permute-start(bf16[640,1024]{1,0:T(8,128)(2,1)} %collective-permute-done.4.refs_2_), channel_id=1, source_target_pairs={{0,1},{1,0},{2,3},{3,2},{4,5},{5,4},{6,7},{7,6},{8,9},{9,8},{10,11... | collective-permute-start | bytes 3932168 | tf_op jit(solution)/shard_map/ppermute | solution.py:45
  39.0 21.1 %collective-permute-start.8 = (bf16[384,1024]{1,0:T(8,128)(2,1)}, bf16[384,1024]{1,0:T(8,128)(2,1)}, u32[]{:S(2)}, u32[]{:S(2)}) collective-permute-start(bf16[384,1024]{1,0:T(8,128)(2,1)} %slice.30), channel_id=1, source_target_pairs={{0,2},{1,3},{2,0},{3,1},{4,6},{5,7},{6,4},{7,5},{8,10},{9,11},{10,... | collective-permute-start | bytes 2359304 | tf_op jit(solution)/shard_map/ppermute | solution.py:45
  41.9 19.7 %collective-permute-start.9 = (bf16[512,768]{1,0:T(8,128)(2,1)S(1)}, bf16[512,768]{1,0:T(8,128)(2,1)S(1)}, u32[]{:S(2)}, u32[]{:S(2)}) collective-permute-start(bf16[512,768]{1,0:T(8,128)(2,1)S(1)} %pad_maximum_fusion.2), channel_id=1, source_target_pairs={{0,4},{4,0},{8,12},{12,8},{16,20},{20,16},{24,28},{28,24},{1,5},{5... | collective-permute-start | bytes 2359304 | tf_op jit(solution)/shard_map/ppermute | solution.py:45
  43.5 14.7 %collective-permute-start.11 = (bf16[128,1024]{1,0:T(8,128)(2,1)S(1)}, bf16[128,1024]{1,0:T(8,128)(2,1)S(1)}, u32[]{:S(2)}, u32[]{:S(2)}) collective-permute-start(bf16[128,1024]{1,0:T(8,128)(2,1)S(1)} %get-tuple-element.266.refs_10_.refs_8_), channel_id=1, source_target_pairs={{0,16},{4,20},{8,24},{12,28},{16,0},{20,4},{24,8},{28,12},{1,17},{... | collective-permute-start | bytes 786440 | tf_op jit(solution)/shard_map/ppermute | solution.py:45
  47.0 12.4 %collective-permute-start.10 = (bf16[512,256]{1,0:T(8,128)(2,1)S(1)}, bf16[512,256]{1,0:T(8,128)(2,1)S(1)}, u32[]{:S(2)}, u32[]{:S(2)}) collective-permute-start(bf16[512,256]{1,0:T(8,128)(2,1)S(1)} %pad_maximum_fusion.6), channel_id=1, source_target_pairs={{0,8},{4,12},{8,0},{12,4},{16,24},{20,28},{24,16},{28,20},{1,9},{5... | collective-permute-start | bytes 786440 | tf_op jit(solution)/shard_map/ppermute | solution.py:45
  61.5 21.3 %collective-permute-start.12 = (bf16[384,1024]{1,0:T(8,128)(2,1)}, bf16[384,1024]{1,0:T(8,128)(2,1)}, u32[]{:S(2)}, u32[]{:S(2)}) collective-permute-start(bf16[384,1024]{1,0:T(8,128)(2,1)} %collective-permute-done.8.refs_3_.refs_7_), channel_id=1, source_target_pairs={{0,1},{1,0},{2,3},{3,2},{4,5},{5,4},{6,7},{7,6},{8,9},{9,8},{10,11... | collective-permute-start | bytes 2359304 | tf_op jit(solution)/shard_map/ppermute | solution.py:45
  61.6 20.4 %collective-permute-start.13 = (bf16[256,1024]{1,0:T(8,128)(2,1)}, bf16[256,1024]{1,0:T(8,128)(2,1)}, u32[]{:S(2)}, u32[]{:S(2)}) collective-permute-start(bf16[256,1024]{1,0:T(8,128)(2,1)} %slice.31), channel_id=1, source_target_pairs={{0,2},{1,3},{2,0},{3,1},{4,6},{5,7},{6,4},{7,5},{8,10},{9,11},{10,... | collective-permute-start | bytes 1572872 | tf_op jit(solution)/shard_map/ppermute | solution.py:45
  63.0 19.8 %collective-permute-start.14 = (bf16[256,1024]{1,0:T(8,128)(2,1)}, bf16[256,1024]{1,0:T(8,128)(2,1)}, u32[]{:S(2)}, u32[]{:S(2)}) collective-permute-start(bf16[256,1024]{1,0:T(8,128)(2,1)} %pad_maximum_fusion.3), channel_id=1, source_target_pairs={{0,8},{4,12},{8,0},{12,4},{16,24},{20,28},{24,16},{28,20},{1,9},{5... | collective-permute-start | bytes 1572872 | tf_op jit(solution)/shard_map/ppermute | solution.py:45
  65.2 16.7 %collective-permute-start.15 = (bf16[128,1024]{1,0:T(8,128)(2,1)S(1)}, bf16[128,1024]{1,0:T(8,128)(2,1)}, u32[]{:S(2)}, u32[]{:S(2)}) collective-permute-start(bf16[128,1024]{1,0:T(8,128)(2,1)S(1)} %get-tuple-element.270.refs_14_), channel_id=1, source_target_pairs={{0,16},{4,20},{8,24},{12,28},{16,0},{20,4},{24,8},{28,12},{1,17},{... | collective-permute-start | bytes 786440 | tf_op jit(solution)/shard_map/ppermute | solution.py:45
  79.1 10.4 %copy-start.21 = (bf16[640,1024]{1,0:T(8,128)(2,1)S(1)}, bf16[640,1024]{1,0:T(8,128)(2,1)}, u32[]{:S(2)}) copy-start(bf16[640,1024]{1,0:T(8,128)(2,1)} %copy-done.20) | copy-start | bytes 3932164
  79.1 10.4 %copy-start.45 = (bf16[512,256]{1,0:T(8,128)(2,1)S(1)}, bf16[512,256]{1,0:T(8,128)(2,1)}, u32[]{:S(2)}) copy-start(bf16[512,256]{1,0:T(8,128)(2,1)} %copy-done.44) | copy-start | bytes 786436
  79.1 10.4 %copy-start.49 = (s32[6]{0:T(128)S(1)}, s32[6]{0:T(128)}, u32[]{:S(2)}) copy-start(s32[6]{0:T(128)} %stack.11.ids) | copy-start | bytes 76
  82.8 6.7 %collective-permute-start.16 = (bf16[256,1024]{1,0:T(8,128)(2,1)}, bf16[256,1024]{1,0:T(8,128)(2,1)S(1)}, u32[]{:S(2)}, u32[]{:S(2)}) collective-permute-start(bf16[256,1024]{1,0:T(8,128)(2,1)} %collective-permute-done.13.refs_4_.refs_8_), channel_id=1, source_target_pairs={{0,1},{1,0},{2,3},{3,2},{4,5},{5,4},{6,7},{7,6},{8,9},{9,8},{10,11... | collective-permute-start | bytes 1572872 | tf_op jit(solution)/shard_map/ppermute | solution.py:45
  83.8 15.5 %collective-permute-start.17 = (bf16[256,1024]{1,0:T(8,128)(2,1)S(1)}, bf16[256,1024]{1,0:T(8,128)(2,1)S(1)}, u32[]{:S(2)}, u32[]{:S(2)}) collective-permute-start(bf16[256,1024]{1,0:T(8,128)(2,1)S(1)} %pad_maximum_fusion.4), channel_id=1, source_target_pairs={{0,8},{4,12},{8,0},{12,4},{16,24},{20,28},{24,16},{28,20},{1,9},{5... | collective-permute-start | bytes 1572872 | tf_op jit(solution)/shard_map/ppermute | solution.py:45
  87.9 64.1 %collective-permute-start.18 = (bf16[512,1024]{1,0:T(8,128)(2,1)S(1)}, bf16[512,1024]{1,0:T(8,128)(2,1)S(1)}, u32[]{:S(2)}, u32[]{:S(2)}) collective-permute-start(bf16[512,1024]{1,0:T(8,128)(2,1)S(1)} %pad_maximum_fusion), channel_id=1, source_target_pairs={{0,4},{4,0},{8,12},{12,8},{16,20},{20,16},{24,28},{28,24},{1,5},{5... | collective-permute-start | bytes 3145736 | tf_op jit(solution)/shard_map/ppermute | solution.py:45
  89.5 67.5 %copy-start.35 = (bf16[256,1024]{1,0:T(8,128)(2,1)}, bf16[256,1024]{1,0:T(8,128)(2,1)S(1)}, u32[]{:S(2)}) copy-start(bf16[256,1024]{1,0:T(8,128)(2,1)S(1)} %collective-permute-done.16.refs_1_.refs_5_) | copy-start | bytes 1572868
  89.5 12.6 %copy-start.70 = (bf16[2560,256]{1,0:T(8,128)(2,1)S(1)}, bf16[2560,256]{1,0:T(8,128)(2,1)}, u32[]{:S(2)}) copy-start(bf16[2560,256]{1,0:T(8,128)(2,1)} %get-tuple-element.226.q_ref) | copy-start | bytes 3932164
  89.5 12.6 %copy-start.71 = (bf16[2560,256]{1,0:T(8,128)(2,1)S(1)}, bf16[2560,256]{1,0:T(8,128)(2,1)}, u32[]{:S(2)}) copy-start(bf16[2560,256]{1,0:T(8,128)(2,1)} %get-tuple-element.237.k_ref) | copy-start | bytes 3932164
  89.5 12.6 %copy-start.72 = (bf16[2560,256]{1,0:T(8,128)(2,1)S(1)}, bf16[2560,256]{1,0:T(8,128)(2,1)}, u32[]{:S(2)}) copy-start(bf16[2560,256]{1,0:T(8,128)(2,1)} %get-tuple-element.238.v_ref) | copy-start | bytes 3932164
  95.1 7.0 %copy-start.33 = (f32[1280,128]{1,0:T(8,128)S(1)}, f32[1280,128]{1,0:T(8,128)}, u32[]{:S(2)}) copy-start(f32[1280,128]{1,0:T(8,128)} %get-tuple-element.217.refs_12_.sine.refs_13_) | copy-start | bytes 1966084
  95.1 7.0 %copy-start.34 = (f32[1280,128]{1,0:T(8,128)S(1)}, f32[1280,128]{1,0:T(8,128)}, u32[]{:S(2)}) copy-start(f32[1280,128]{1,0:T(8,128)} %get-tuple-element.216.refs_11_.cos.refs_12_) | copy-start | bytes 1966084
  100.5 51.5 %collective-permute-start.19 = (bf16[512,1024]{1,0:T(8,128)(2,1)S(1)}, bf16[512,1024]{1,0:T(8,128)(2,1)S(1)}, u32[]{:S(2)}, u32[]{:S(2)}) collective-permute-start(bf16[512,1024]{1,0:T(8,128)(2,1)S(1)} %pad_maximum_fusion.1), channel_id=1, source_target_pairs={{0,4},{4,0},{8,12},{12,8},{16,20},{20,16},{24,28},{28,24},{1,5},{5... | collective-permute-start | bytes 3145736 | tf_op jit(solution)/shard_map/ppermute | solution.py:45
  157.0 14.3 %collective-permute-start.20 = (bf16[2,640,1024]{2,1,0:T(8,128)(2,1)S(1)}, bf16[2,640,1024]{2,1,0:T(8,128)(2,1)S(1)}, u32[]{:S(2)}, u32[]{:S(2)}) collective-permute-start(bf16[2,640,1024]{2,1,0:T(8,128)(2,1)S(1)} %get-tuple-element.261), channel_id=1, source_target_pairs={{0,1},{1,0},{2,3},{3,2},{4,5},{5,4},{6,7},{7,6},{8,9},{9,8},{10,11... | collective-permute-start | bytes 7864328 | tf_op jit(solution)/shard_map/ppermute | solution.py:45
  171.8 42.7 %collective-permute-start.21 = (bf16[1,640,1024]{2,1,0:T(8,128)(2,1)S(1)}, bf16[1,640,1024]{2,1,0:T(8,128)(2,1)S(1)}, u32[]{:S(2)}, u32[]{:S(2)}) collective-permute-start(bf16[1,640,1024]{2,1,0:T(8,128)(2,1)S(1)} %add_terms.3), channel_id=1, source_target_pairs={{0,2},{1,3},{2,0},{3,1},{4,6},{5,7},{6,4},{7,5},{8,10},{9,11},{10,... | collective-permute-start | bytes 3932168 | tf_op jit(solution)/shard_map/ppermute | solution.py:45
  173.3 41.1 %collective-permute-start.22 = (bf16[4,128,512]{2,1,0:T(8,128)(2,1)}, bf16[4,128,512]{2,1,0:T(8,128)(2,1)S(1)}, u32[]{:S(2)}, u32[]{:S(2)}) collective-permute-start(bf16[4,128,512]{2,1,0:T(8,128)(2,1)} %get-tuple-element.284), channel_id=1, source_target_pairs={{0,4},{4,0},{8,12},{12,8},{16,20},{20,16},{24,28},{28,24},{1,5},{5... | collective-permute-start | bytes 1572872 | tf_op jit(solution)/shard_map/ppermute | solution.py:45
  173.8 40.6 %collective-permute-start.23 = (bf16[4,128,512]{2,1,0:T(8,128)(2,1)}, bf16[4,128,512]{2,1,0:T(8,128)(2,1)S(1)}, u32[]{:S(2)}, u32[]{:S(2)}) collective-permute-start(bf16[4,128,512]{2,1,0:T(8,128)(2,1)} %get-tuple-element.285), channel_id=1, source_target_pairs={{0,8},{4,12},{8,0},{12,4},{16,24},{20,28},{24,16},{28,20},{1,9},{5... | collective-permute-start | bytes 1572872 | tf_op jit(solution)/shard_map/ppermute | solution.py:45
  214.5 11.7 %copy-start.10 = (bf16[4,128,512]{2,1,0:T(8,128)(2,1)}, bf16[4,128,512]{2,1,0:T(8,128)(2,1)S(1)}, u32[]{:S(2)}) copy-start(bf16[4,128,512]{2,1,0:T(8,128)(2,1)S(1)} %collective-permute-done.22.refs_1_) | copy-start | bytes 1572868
  214.5 11.7 %copy-start.12 = (bf16[4,128,512]{2,1,0:T(8,128)(2,1)}, bf16[4,128,512]{2,1,0:T(8,128)(2,1)S(1)}, u32[]{:S(2)}) copy-start(bf16[4,128,512]{2,1,0:T(8,128)(2,1)S(1)} %collective-permute-done.23.refs_3_.refs_4_.refs_5_) | copy-start | bytes 1572868
  215.7 5.1 %collective-permute-start.24 = (bf16[2,640,1024]{2,1,0:T(8,128)(2,1)}, bf16[2,640,1024]{2,1,0:T(8,128)(2,1)S(1)}, u32[]{:S(2)}, u32[]{:S(2)}) collective-permute-start(bf16[2,640,1024]{2,1,0:T(8,128)(2,1)} %get-tuple-element.288), channel_id=1, source_target_pairs={{0,1},{1,0},{2,3},{3,2},{4,5},{5,4},{6,7},{7,6},{8,9},{9,8},{10,11... | collective-permute-start | bytes 7864328 | tf_op jit(solution)/shard_map/ppermute | solution.py:45
  223.8 39.2 %collective-permute-start.25 = (bf16[1,640,1024]{2,1,0:T(8,128)(2,1)}, bf16[1,640,1024]{2,1,0:T(8,128)(2,1)S(1)}, u32[]{:S(2)}, u32[]{:S(2)}) collective-permute-start(bf16[1,640,1024]{2,1,0:T(8,128)(2,1)} %add_terms.4), channel_id=1, source_target_pairs={{0,2},{1,3},{2,0},{3,1},{4,6},{5,7},{6,4},{7,5},{8,10},{9,11},{10,... | collective-permute-start | bytes 3932168 | tf_op jit(solution)/shard_map/ppermute | solution.py:45
  224.4 35.4 %collective-permute-start.28 = (bf16[4,128,1024]{2,1,0:T(8,128)(2,1)}, bf16[4,128,1024]{2,1,0:T(8,128)(2,1)S(1)}, u32[]{:S(2)}, u32[]{:S(2)}) collective-permute-start(bf16[4,128,1024]{2,1,0:T(8,128)(2,1)} %copy-done.59), channel_id=1, source_target_pairs={{0,4},{4,0},{8,12},{12,8},{16,20},{20,16},{24,28},{28,24},{1,5},{5... | collective-permute-start | bytes 3145736 | tf_op jit(solution)/shard_map/ppermute | solution.py:45
  225.9 36.1 %collective-permute-start.29 = (bf16[4,128,1024]{2,1,0:T(8,128)(2,1)}, bf16[4,128,1024]{2,1,0:T(8,128)(2,1)S(1)}, u32[]{:S(2)}, u32[]{:S(2)}) collective-permute-start(bf16[4,128,1024]{2,1,0:T(8,128)(2,1)} %get-tuple-element.301), channel_id=1, source_target_pairs={{0,8},{4,12},{8,0},{12,4},{16,24},{20,28},{24,16},{28,20},{1,9},{5... | collective-permute-start | bytes 3145736 | tf_op jit(solution)/shard_map/ppermute | solution.py:45
  226.3 29.3 %collective-permute-start.26 = (bf16[2,128,512]{2,1,0:T(8,128)(2,1)S(1)}, bf16[2,128,512]{2,1,0:T(8,128)(2,1)S(1)}, u32[]{:S(2)}, u32[]{:S(2)}) collective-permute-start(bf16[2,128,512]{2,1,0:T(8,128)(2,1)S(1)} %get-tuple-element.298), channel_id=1, source_target_pairs={{0,16},{4,20},{8,24},{12,28},{16,0},{20,4},{24,8},{28,12},{1,17},{... | collective-permute-start | bytes 786440 | tf_op jit(solution)/shard_map/ppermute | solution.py:45
  228.0 31.8 %collective-permute-start.27 = (bf16[2,128,512]{2,1,0:T(8,128)(2,1)S(1)}, bf16[2,128,512]{2,1,0:T(8,128)(2,1)S(1)}, u32[]{:S(2)}, u32[]{:S(2)}) collective-permute-start(bf16[2,128,512]{2,1,0:T(8,128)(2,1)S(1)} %get-tuple-element.299), channel_id=1, source_target_pairs={{0,16},{4,20},{8,24},{12,28},{16,0},{20,4},{24,8},{28,12},{1,17},{... | collective-permute-start | bytes 786440 | tf_op jit(solution)/shard_map/ppermute | solution.py:45
  264.0 5.0 %collective-permute-start.30 = (bf16[2,640,1024]{2,1,0:T(8,128)(2,1)S(1)}, bf16[2,640,1024]{2,1,0:T(8,128)(2,1)S(1)}, u32[]{:S(2)}, u32[]{:S(2)}) collective-permute-start(bf16[2,640,1024]{2,1,0:T(8,128)(2,1)S(1)} %get-tuple-element.303), channel_id=1, source_target_pairs={{0,1},{1,0},{2,3},{3,2},{4,5},{5,4},{6,7},{7,6},{8,9},{9,8},{10,11... | collective-permute-start | bytes 7864328 | tf_op jit(solution)/shard_map/ppermute | solution.py:45
  269.0 7.0 %copy-start.17 = (bf16[1,640,1024]{2,1,0:T(8,128)(2,1)S(1)}, bf16[1,640,1024]{2,1,0:T(8,128)(2,1)}, u32[]{:S(2)}) copy-start(bf16[1,640,1024]{2,1,0:T(8,128)(2,1)} %copy-done.16) | copy-start | bytes 3932164
  269.0 7.0 %copy-start.19 = (bf16[1,640,1024]{2,1,0:T(8,128)(2,1)S(1)}, bf16[1,640,1024]{2,1,0:T(8,128)(2,1)}, u32[]{:S(2)}) copy-start(bf16[1,640,1024]{2,1,0:T(8,128)(2,1)} %copy-done.18) | copy-start | bytes 3932164
  269.4 41.5 %collective-permute-start.39 = (bf16[1,640,1024]{2,1,0:T(8,128)(2,1)S(1)}, bf16[1,640,1024]{2,1,0:T(8,128)(2,1)S(1)}, u32[]{:S(2)}, u32[]{:S(2)}) collective-permute-start(bf16[1,640,1024]{2,1,0:T(8,128)(2,1)S(1)} %add_terms.5), channel_id=1, source_target_pairs={{0,2},{1,3},{2,0},{3,1},{4,6},{5,7},{6,4},{7,5},{8,10},{9,11},{10,... | collective-permute-start | bytes 3932168 | tf_op jit(solution)/shard_map/ppermute | solution.py:45
  271.3 20.0 %collective-permute-start.34 = (bf16[2,128,1024]{2,1,0:T(8,128)(2,1)S(1)}, bf16[2,128,1024]{2,1,0:T(8,128)(2,1)S(1)}, u32[]{:S(2)}, u32[]{:S(2)}) collective-permute-start(bf16[2,128,1024]{2,1,0:T(8,128)(2,1)S(1)} %get-tuple-element.324), channel_id=1, source_target_pairs={{0,8},{4,12},{8,0},{12,4},{16,24},{20,28},{24,16},{28,20},{1,9},{5... | collective-permute-start | bytes 1572872 | tf_op jit(solution)/shard_map/ppermute | solution.py:45
  273.9 17.5 %collective-permute-start.35 = (bf16[2,128,1024]{2,1,0:T(8,128)(2,1)S(1)}, bf16[2,128,1024]{2,1,0:T(8,128)(2,1)S(1)}, u32[]{:S(2)}, u32[]{:S(2)}) collective-permute-start(bf16[2,128,1024]{2,1,0:T(8,128)(2,1)S(1)} %get-tuple-element.325), channel_id=1, source_target_pairs={{0,4},{4,0},{8,12},{12,8},{16,20},{20,16},{24,28},{28,24},{1,5},{5... | collective-permute-start | bytes 1572872 | tf_op jit(solution)/shard_map/ppermute | solution.py:45
  274.4 14.2 %collective-permute-start.31 = (bf16[1,128,512]{2,1,0:T(8,128)(2,1)S(1)}, bf16[1,128,512]{2,1,0:T(8,128)(2,1)S(1)}, u32[]{:S(2)}, u32[]{:S(2)}) collective-permute-start(bf16[1,128,512]{2,1,0:T(8,128)(2,1)S(1)} %get-tuple-element.318), channel_id=1, source_target_pairs={{0,8},{4,12},{8,0},{12,4},{16,24},{20,28},{24,16},{28,20},{1,9},{5... | collective-permute-start | bytes 393224 | tf_op jit(solution)/shard_map/ppermute | solution.py:45
  274.5 15.6 %collective-permute-start.32 = (bf16[1,128,512]{2,1,0:T(8,128)(2,1)S(1)}, bf16[1,128,512]{2,1,0:T(8,128)(2,1)S(1)}, u32[]{:S(2)}, u32[]{:S(2)}) collective-permute-start(bf16[1,128,512]{2,1,0:T(8,128)(2,1)S(1)} %get-tuple-element.319), channel_id=1, source_target_pairs={{0,4},{4,0},{8,12},{12,8},{16,20},{20,16},{24,28},{28,24},{1,5},{5... | collective-permute-start | bytes 393224 | tf_op jit(solution)/shard_map/ppermute | solution.py:45
  290.1 1.3 collective-permute-start.33
  291.4 6.3 %collective-permute-start.36 = (f32[16,1024]{1,0:T(8,128)S(1)}, f32[16,1024]{1,0:T(8,128)S(1)}, u32[]{:S(2)}, u32[]{:S(2)}) collective-permute-start(f32[16,1024]{1,0:T(8,128)S(1)} %add.41), channel_id=1, source_target_pairs={{0,16},{4,20},{8,24},{12,28},{16,0},{20,4},{24,8},{28,12},{1,17},{... | collective-permute-start | bytes 196616 | tf_op jit(solution)/shard_map/ppermute | solution.py:45
  297.7 19.2 %collective-permute-start.41 = (bf16[1,128,1024]{2,1,0:T(8,128)(2,1)S(1)}, bf16[1,128,1024]{2,1,0:T(8,128)(2,1)S(1)}, u32[]{:S(2)}, u32[]{:S(2)}) collective-permute-start(bf16[1,128,1024]{2,1,0:T(8,128)(2,1)S(1)} %get-tuple-element.339), channel_id=1, source_target_pairs={{0,16},{4,20},{8,24},{12,28},{16,0},{20,4},{24,8},{28,12},{1,17},{... | collective-permute-start | bytes 786440 | tf_op jit(solution)/shard_map/ppermute | solution.py:45
  297.8 24.7 %collective-permute-start.42 = (bf16[1,128,1024]{2,1,0:T(8,128)(2,1)S(1)}, bf16[1,128,1024]{2,1,0:T(8,128)(2,1)S(1)}, u32[]{:S(2)}, u32[]{:S(2)}) collective-permute-start(bf16[1,128,1024]{2,1,0:T(8,128)(2,1)S(1)} %get-tuple-element.340), channel_id=1, source_target_pairs={{0,16},{4,20},{8,24},{12,28},{16,0},{20,4},{24,8},{28,12},{1,17},{... | collective-permute-start | bytes 786440 | tf_op jit(solution)/shard_map/ppermute | solution.py:45
  300.7 4.3 %collective-permute-start.37 = (f32[16,1024]{1,0:T(8,128)S(1)}, f32[16,1024]{1,0:T(8,128)S(1)}, u32[]{:S(2)}, u32[]{:S(2)}) collective-permute-start(f32[16,1024]{1,0:T(8,128)S(1)} %add.42), channel_id=1, source_target_pairs={{0,4},{4,0},{8,12},{12,8},{16,20},{20,16},{24,28},{28,24},{1,5},{5... | collective-permute-start | bytes 196616 | tf_op jit(solution)/shard_map/ppermute | solution.py:45
  305.0 5.9 %collective-permute-start.38 = (f32[16,1024]{1,0:T(8,128)S(1)}, f32[16,1024]{1,0:T(8,128)S(1)}, u32[]{:S(2)}, u32[]{:S(2)}) collective-permute-start(f32[16,1024]{1,0:T(8,128)S(1)} %add.43), channel_id=1, source_target_pairs={{0,8},{4,12},{8,0},{12,4},{16,24},{20,28},{24,16},{28,20},{1,9},{5... | collective-permute-start | bytes 196616 | tf_op jit(solution)/shard_map/ppermute | solution.py:45
  310.9 15.7 %collective-permute-start.40 = (f32[16,1024]{1,0:T(8,128)S(1)}, f32[16,1024]{1,0:T(8,128)S(1)}, u32[]{:S(2)}, u32[]{:S(2)}) collective-permute-start(f32[16,1024]{1,0:T(8,128)S(1)} %add.44), channel_id=1, source_target_pairs={{0,2},{1,3},{2,0},{3,1},{4,6},{5,7},{6,4},{7,5},{8,10},{9,11},{10,... | collective-permute-start | bytes 196616 | tf_op jit(solution)/shard_map/ppermute | solution.py:45
  312.4 11.3 %copy-start.15 = (f32[640,1024]{1,0:T(8,128)S(1)}, f32[640,1024]{1,0:T(8,128)}, u32[]{:S(2)}) copy-start(f32[640,1024]{1,0:T(8,128)} %copy-done.14) | copy-start | bytes 7864324
  312.4 11.3 %copy-start.43 = (f32[640,1]{1,0:T(8,128)S(1)}, f32[640,1]{1,0:T(8,128)}, u32[]{:S(2)}) copy-start(f32[640,1]{1,0:T(8,128)} %copy-done.42) | copy-start | bytes 7684
  (54 other events, 236.5 us)

commit v10 on v9

--- a/solution.py
+++ b/solution.py
@@ -1245,15 +1245,13 @@
         groups,
     )
 
-    output, sums = tie_halves([output, sums], *qkv_sums)
-    for parts in qkv_sums:
-        parts.add()
 
     sums = sums + swap(sums, "tensor", 1)
-    (sums,) = tie_halves([sums], *mlp_sums)
+    for bit in data_bits[3:]:
+        sums = sums + swap(sums, "dp", bit)
+    other, *_ = tie_halves([swap(sums, "dp", data_bits[2])], *mlp_sums)
+    sums = sums + other
     add_stacks(mlp_sums)
-    for bit in data_bits[2:]:
-        sums = sums + swap(sums, "dp", bit)
     sums, *sends = tie(sums, *[parts.send for parts in mlp_sums])
     for parts, send in zip(mlp_sums, sends):
         parts.send = send
@@ -1266,6 +1264,8 @@
     stream_grad = finish_grad(out_grad, normalized, inv_std, back_parts.terms)
 
     fc_weight_grad, out_weight_grad = finish_mlp_weights(*[x.finish() for x in mlp_sums])
+    for parts in qkv_sums:
+        parts.add()
     qkv_weight_grad, dense_weight_grad = finish_attention_weights(*[x.finish() for x in qkv_sums])
 
     count_all = float(rows_local * lax.axis_size("dp") * groups * model)

time: 331 us -> 322 us (0.973)
  waiting for transfers between devices: 85.6 us -> 73.8 us
    ppermute x43, waiting for transfers between devices: 85.6 us -> 73.8 us  [swap(): return lax.ppermute(block, axis, [(i, i ^ bit) for i in range(size)])]
    unnamed x153 -> x151, local copies, waits for them, and re-layouts: 18.8 us -> 19 us
  transfers between devices with their start and end apart: 43 -> 43, of which waited for: 21 -> 20; matrix products, arithmetic and copies ran while one was open for 5% -> 5% of each run, Pallas kernels for 45% -> 46%
where the time goes in v10:
time: 322 us; the launch traced here: 321 us
  Pallas kernels  155 us (48%)
  waiting for transfers between devices  73.8 us (23%)
  starting transfers between devices  52.4 us (16%)
  local copies, waits for them, and re-layouts  25.4 us (8%)
  other arithmetic  13.2 us (4%)
    pallas_call x19, Pallas kernels, call(): pl.pallas_call(kernel, grid_spec=pltpu.PrefetchScalarGridSpec(num_scalar_...  153 us
    ppermute x43, waiting for transfers between devices, swap(): return lax.ppermute(block, axis, [(i, i ^ bit) for i in range(size)])  73.8 us
    ppermute x43, starting transfers between devices, swap(): return lax.ppermute(block, axis, [(i, i ^ bit) for i in range(size)])  52.4 us
    unnamed x151, local copies, waits for them, and re-layouts  19 us
    concatenate x8, other arithmetic, double(): jnp.concatenate(self.arrays, axis=0)  8.71 us
  transfers between devices with their start and end apart: 43, of which 20 were waited for; matrix products, arithmetic and copies ran while one was open for 5% of the time, Pallas kernels for 46%

profile of v10, /device:TPU:0, one launch (start us, length us, event | category | flops | bytes accessed | tf_op | source)
XLA Modules:
  0.0 320.9 jit_solution(17116276271886222351)
XLA Ops:
  1.2 1.7 copy-done.4
  2.9 2.2 normalize.1
  5.2 1.6 copy-done.14
  6.9 2.9 collective-permute-start.4
  11.6 2.7 collective-permute-start.1
  14.3 1.5 collective-permute-start.2
  17.6 2.0 tree_table.1.info
  19.6 3.9 %collective-permute-done.1.refs_5_ = bf16[128,768]{1,0:T(8,128)(2,1)S(1)} collective-permute-done((bf16[128,768]{1,0:T(8,128)(2,1)S(1)}, bf16[128,768]{1,0:T(8,128)(2,1)S(1)}, u32[]{:S(2)}, u32[]{:S(2)}) %collective-permute-start.1) | collective-permute-done | bytes 196640 | tf_op jit(solution)/shard_map/ppermute | solution.py:45
  24.9 1.5 pad_maximum_fusion.7
  26.5 3.4 %collective-permute-start.6 = (bf16[256,256]{1,0:T(8,128)(2,1)}, bf16[256,256]{1,0:T(8,128)(2,1)}, u32[]{:S(2)}, u32[]{:S(2)}) collective-permute-start(bf16[256,256]{1,0:T(8,128)(2,1)} %pad_maximum_fusion.7), channel_id=1, source_target_pairs={{0,16},{4,20},{8,24},{12,28},{16,0},{20,4},{24,8},{28,12},{1,17},{... | collective-permute-start | bytes 393224 | tf_op jit(solution)/shard_map/ppermute | solution.py:45
  29.8 3.8 %fusion = (f32[1280,128]{1,0:T(8,128)}, f32[1280,128]{1,0:T(8,128)}) fusion(s32[128]{0:T(128)S(1)} %get-tuple-element.342, s32[128]{0:T(128)S(1)} %get-tuple-element.343, pred[128]{0:T(512)(128)(4,1)S(1)} %compare_and_fusion, f32[1280]{0:T(1024)S(1)} %convert_add_fusion), kind=kLoop, calls=%fused_computation.9 | loop fusion | flops 3112960 | bytes 1316992 | tf_op jit(solution)/shard_map/jit(_where)/select_n | solution.py:1059
  33.6 1.3 reshape.42.refs_10_
  35.0 1.3 reshape.43.refs_20_
  36.3 2.8 collective-permute-done.4.refs_2_
  39.1 1.8 collective-permute-start.8
  42.0 1.6 collective-permute-start.9
  43.6 2.6 collective-permute-start.11
  47.2 1.6 collective-permute-start.10
  48.8 9.5 %collective-permute-done.11.refs_11_.refs_9_ = bf16[128,1024]{1,0:T(8,128)(2,1)S(1)} collective-permute-done((bf16[128,1024]{1,0:T(8,128)(2,1)S(1)}, bf16[128,1024]{1,0:T(8,128)(2,1)S(1)}, u32[]{:S(2)}, u32[]{:S(2)}) %collective-permute-start.11) | collective-permute-done | bytes 262176 | tf_op jit(solution)/shard_map/ppermute | solution.py:45
  58.3 1.2 collective-permute-done.10.refs_9_.refs_3_
  60.2 1.4 collective-permute-done.9.refs_7_
  63.2 1.7 collective-permute-start.14
  65.4 2.6 collective-permute-start.15
  68.0 11.3 %project_qkv.1 = (bf16[2560,256]{1,0:T(8,128)(2,1)}, bf16[2560,256]{1,0:T(8,128)(2,1)}, bf16[2560,256]{1,0:T(8,128)(2,1)}) custom-call(s32[6]{0:T(128)} %stack.11.ids, s32[1,20,5]{2,1,0:T(8,128)} %tree_table.1.info, bf16[640,1024]{1,0:T(8,128)(2,1)} %copy-done.52, bf16[640,1024]{1,0:T(8,128)(2,1)} %collective-permute-done.3.refs_1_, ...), custom_call_target="tpu_custom_call" | custom-call | flops 4026531840 | bytes 12079104 | tf_op jit(solution)/shard_map/project_qkv/pallas_call | solution.py:217
  79.3 2.8 collective-permute-done.15.refs_15_
  83.9 2.9 collective-permute-start.17
  88.0 1.6 collective-permute-start.18
  89.7 5.6 %project_grad.1.do_ref = bf16[2560,256]{1,0:T(8,128)(2,1)S(1)} custom-call(s32[6]{0:T(128)S(1)} %copy-done.49, bf16[384,1024]{1,0:T(8,128)(2,1)} %collective-permute-done.12.refs_0_.refs_4_, bf16[256,1024]{1,0:T(8,128)(2,1)S(1)} %collective-permute-done.16.refs_1_.refs_5_, bf16[640,1024]{1,0:T(8,128)(2,1)S(1)} %copy-done.21, ...), custom_call_target="tpu_custom_call" | custom-call | flops 1342177280 | bytes 7077888 | tf_op jit(solution)/shard_map/project_grad/pallas_call | solution.py:217
  95.3 4.2 %collective-permute-done.17.refs_16_ = bf16[256,1024]{1,0:T(8,128)(2,1)S(1)} collective-permute-done((bf16[256,1024]{1,0:T(8,128)(2,1)S(1)}, bf16[256,1024]{1,0:T(8,128)(2,1)S(1)}, u32[]{:S(2)}, u32[]{:S(2)}) %collective-permute-start.17) | collective-permute-done | bytes 524320 | tf_op jit(solution)/shard_map/ppermute | solution.py:45
  99.4 1.2 pad_maximum_fusion.1
  100.6 1.6 collective-permute-start.19
  102.3 49.9 %attention.1 = (bf16[2560,256]{1,0:T(8,128)(2,1)S(1)}, bf16[2560,256]{1,0:T(8,128)(2,1)S(1)}, bf16[2560,256]{1,0:T(8,128)(2,1)S(1)}, bf16[2560,256]{1,0:T(8,128)(2,1)S(1)}) custom-call(s32[1,20,5]{2,1,0:T(8,128)S(1)} %copy-done.48, bf16[2560,256]{1,0:T(8,128)(2,1)S(1)} %copy-done.69, bf16[2560,256]{1,0:T(8,128)(2,1)S(1)} %project_grad.1.do_ref, ...), custom_call_target="tpu_custom_call" | custom-call | flops 31406948352 | bytes 11796480 | tf_op jit(solution)/shard_map/attention/pallas_call | solution.py:217
  152.2 4.8 %project_context.1 = (bf16[2,640,1024]{2,1,0:T(8,128)(2,1)S(1)}, bf16[2,640,1024]{2,1,0:T(8,128)(2,1)S(1)}) custom-call(s32[6]{0:T(128)S(1)} %copy-done.49, bf16[2560,256]{1,0:T(8,128)(2,1)S(1)} %get-tuple-element.247.ctx.ctx_ref, bf16[128,256]{1,0:T(8,128)(2,1)} %get-tuple-element.226.refs_6_.refs_0_, ...), custom_call_target="tpu_custom_call" | custom-call | flops 1342177280 | bytes 7077888 | tf_op jit(solution)/shard_map/project_context/pallas_call | solution.py:217
  157.2 12.3 %attention_weights.1 = (bf16[2560,768]{1,0:T(8,128)(2,1)S(1)}, f32[8,768]{1,0:T(8,128)S(1)}, bf16[4,128,512]{2,1,0:T(8,128)(2,1)}, bf16[4,128,512]{2,1,0:T(8,128...) custom-call(s32[6]{0:T(128)S(1)} %copy-done.49, s32[1,20,5]{2,1,0:T(8,128)S(1)} %copy-done.48, ...), custom_call_target="tpu_custom_call" | custom-call | flops 5368709120 | bytes 23101440 | tf_op jit(solution)/shard_map/attention_weights/pallas_call | solution.py:217
  169.6 2.0 copy-done.67
  172.0 1.6 collective-permute-start.21
  174.1 1.7 collective-permute-start.23
  175.9 39.1 %mlp.1 = (bf16[2,640,1024]{2,1,0:T(8,128)(2,1)}, bf16[2,640,1024]{2,1,0:T(8,128)(2,1)}, bf16[2560,1024]{1,0:T(8,128)(2,1)}, f32[8,1024]{1,0:T(8,128)S(1)}, bf16[...) custom-call(s32[6]{0:T(128)S(1)} %copy-done.49, ...), custom_call_target="tpu_custom_call" | custom-call | flops 26843545600 | bytes 29417472 | tf_op jit(solution)/shard_map/mlp/pallas_call | solution.py:217
  216.2 5.1 %collective-permute-done.24.refs_1_.refs_4_ = bf16[2,640,1024]{2,1,0:T(8,128)(2,1)S(1)} collective-permute-done((bf16[2,640,1024]{2,1,0:T(8,128)(2,1)}, bf16[2,640,1024]{2,1,0:T(8,128)(2,1)S(1)}, u32[]{:S(2)}, u32[]{:S(2)}) %collective-permute-start.24) | collective-permute-done | bytes 2621472 | tf_op jit(solution)/shard_map/ppermute | solution.py:45
  221.3 1.7 copy-done.2
  223.1 1.2 add_terms.4
  224.9 1.5 collective-permute-start.28
  226.8 1.7 collective-permute-start.26
  228.5 1.3 collective-permute-start.27
  229.9 2.1 copy-done.68
  232.0 2.5 copy-done.72
  234.5 15.4 %norm_backward.1 = (bf16[2,640,1024]{2,1,0:T(8,128)(2,1)S(1)}, bf16[2,640,1024]{2,1,0:T(8,128)(2,1)S(1)}, f32[8,1024]{1,0:T(8,128)S(1)}) custom-call(s32[6]{0:T(128)S(1)} %copy-done.49, bf16[2560,768]{1,0:T(8,128)(2,1)S(1)} %copy-done.68, bf16[2560,1024]{1,0:T(8,128)(2,1)S(1)} %copy-done.72, bf16[640,1024]{1,0:T(8,128)(2,1)S(1)} %copy-done.55, ...), custom_call_target="tpu_custom_call" | custom-call | flops 9395240960 | bytes 23371776 | tf_op jit(solution)/shard_map/norm_backward/pallas_call | solution.py:217
  249.8 6.3 %collective-permute-done.26.refs_2_ = bf16[2,128,512]{2,1,0:T(8,128)(2,1)S(1)} collective-permute-done((bf16[2,128,512]{2,1,0:T(8,128)(2,1)S(1)}, bf16[2,128,512]{2,1,0:T(8,128)(2,1)S(1)}, u32[]{:S(2)}, u32[]{:S(2)}) %collective-permute-start.26) | collective-permute-done | bytes 262176 | tf_op jit(solution)/shard_map/ppermute | solution.py:45
  256.1 4.2 %collective-permute-done.27.refs_5_.refs_6_ = bf16[2,128,512]{2,1,0:T(8,128)(2,1)S(1)} collective-permute-done((bf16[2,128,512]{2,1,0:T(8,128)(2,1)S(1)}, bf16[2,128,512]{2,1,0:T(8,128)(2,1)S(1)}, u32[]{:S(2)}, u32[]{:S(2)}) %collective-permute-start.27) | collective-permute-done | bytes 262176 | tf_op jit(solution)/shard_map/ppermute | solution.py:45
  261.3 1.2 collective-permute-done.29.refs_9_.refs_4_.refs_5_
  264.6 4.9 %collective-permute-done.30.refs_1_ = bf16[2,640,1024]{2,1,0:T(8,128)(2,1)S(1)} collective-permute-done((bf16[2,640,1024]{2,1,0:T(8,128)(2,1)S(1)}, bf16[2,640,1024]{2,1,0:T(8,128)(2,1)S(1)}, u32[]{:S(2)}, u32[]{:S(2)}) %collective-permute-start.30) | collective-permute-done | bytes 2621472 | tf_op jit(solution)/shard_map/ppermute | solution.py:45
  269.9 1.6 collective-permute-start.37
  271.8 2.5 collective-permute-start.33
  274.9 3.7 %finish_output.1 = (f32[640,1024]{1,0:T(8,128)}, f32[16,1024]{1,0:T(8,128)S(1)}) custom-call(s32[6]{0:T(128)S(1)} %copy-done.49, f32[640,1024]{1,0:T(8,128)S(1)} %copy-done.5, bf16[640,1024]{1,0:T(8,128)(2,1)S(1)} %copy-done.1, bf16[2,640,1024]{2,1,0:T(8,128)(2,1)S(1)} %get-tuple-element.259.refs_0_, ...), custom_call_target="tpu_custom_call" | custom-call | flops 10485760 | bytes 19824640 | tf_op jit(solution)/shard_map/finish_output/pallas_call | solution.py:217
  278.6 1.3 collective-permute-done.31
  280.5 7.2 %collective-permute-done.33.refs_2_ = bf16[2,128,1024]{2,1,0:T(8,128)(2,1)S(1)} collective-permute-done((bf16[2,128,1024]{2,1,0:T(8,128)(2,1)S(1)}, bf16[2,128,1024]{2,1,0:T(8,128)(2,1)S(1)}, u32[]{:S(2)}, u32[]{:S(2)}) %collective-permute-start.33) | collective-permute-done | bytes 524320 | tf_op jit(solution)/shard_map/ppermute | solution.py:45
  288.6 2.6 collective-permute-start.41
  292.3 1.4 collective-permute-start.36
  294.4 9.3 %collective-permute-done.36 = f32[16,1024]{1,0:T(8,128)S(1)} collective-permute-done((f32[16,1024]{1,0:T(8,128)S(1)}, f32[16,1024]{1,0:T(8,128)S(1)}, u32[]{:S(2)}, u32[]{:S(2)}) %collective-permute-start.36) | collective-permute-done | bytes 65568 | tf_op jit(solution)/shard_map/ppermute | solution.py:45
  303.8 1.5 collective-permute-start.40
  305.9 2.8 collective-permute-done.40.refs_7_
  309.6 3.9 %collective-permute-done.42.refs_7_ = bf16[1,128,1024]{2,1,0:T(8,128)(2,1)S(1)} collective-permute-done((bf16[1,128,1024]{2,1,0:T(8,128)(2,1)S(1)}, bf16[1,128,1024]{2,1,0:T(8,128)(2,1)S(1)}, u32[]{:S(2)}, u32[]{:S(2)}) %collective-permute-start.42) | collective-permute-done | bytes 262176 | tf_op jit(solution)/shard_map/ppermute | solution.py:45
  313.5 1.2 finish_mlp_weights.1
  314.7 2.9 finish_grad.1
  (222 shorter events, 29.3 us)
Async XLA Ops:
  0.6 15.2 %copy-start = (bf16[640,1024]{1,0:T(8,128)(2,1)S(1)}, bf16[640,1024]{1,0:T(8,128)(2,1)}, u32[]{:S(2)}) copy-start(bf16[640,1024]{1,0:T(8,128)(2,1)} %grad_ref.3) | copy-start | bytes 3932164
  0.7 22.8 %collective-permute-start = (bf16[640,1024]{1,0:T(8,128)(2,1)}, bf16[640,1024]{1,0:T(8,128)(2,1)S(1)}, u32[]{:S(2)}, u32[]{:S(2)}) collective-permute-start(bf16[640,1024]{1,0:T(8,128)(2,1)} %grad_ref.3), channel_id=1, source_target_pairs={{0,1},{1,0},{2,3},{3,2},{4,5},{5,4},{6,7},{7,6},{8,9},{9,8},{10,11... | collective-permute-start | bytes 3932168 | tf_op jit(solution)/shard_map/ppermute | solution.py:45
  6.8 29.5 %collective-permute-start.3 = (bf16[640,1024]{1,0:T(8,128)(2,1)}, bf16[640,1024]{1,0:T(8,128)(2,1)}, u32[]{:S(2)}, u32[]{:S(2)}) collective-permute-start(bf16[640,1024]{1,0:T(8,128)(2,1)} %get-tuple-element.206.refs_3_), channel_id=1, source_target_pairs={{0,1},{1,0},{2,3},{3,2},{4,5},{5,4},{6,7},{7,6},{8,9},{9,8},{10,11... | collective-permute-start | bytes 3932168 | tf_op jit(solution)/shard_map/ppermute | solution.py:45
  6.9 32.2 %collective-permute-start.4 = (bf16[640,1024]{1,0:T(8,128)(2,1)}, bf16[640,1024]{1,0:T(8,128)(2,1)}, u32[]{:S(2)}, u32[]{:S(2)}) collective-permute-start(bf16[640,1024]{1,0:T(8,128)(2,1)} %get-tuple-element.206.refs_3_), channel_id=1, source_target_pairs={{0,2},{1,3},{2,0},{3,1},{4,6},{5,7},{6,4},{7,5},{8,10},{9,11},{10,... | collective-permute-start | bytes 3932168 | tf_op jit(solution)/shard_map/ppermute | solution.py:45
  11.6 29.3 %copy-start.29 = (bf16[128,768]{1,0:T(8,128)(2,1)}, bf16[128,768]{1,0:T(8,128)(2,1)S(1)}, u32[]{:S(2)}) copy-start(bf16[128,768]{1,0:T(8,128)(2,1)S(1)} %get-tuple-element.207.refs_4_) | copy-start | bytes 589828
  11.6 75.2 %copy-start.22 = (bf16[128,1024]{1,0:T(8,128)(2,1)}, bf16[128,1024]{1,0:T(8,128)(2,1)S(1)}, u32[]{:S(2)}) copy-start(bf16[128,1024]{1,0:T(8,128)(2,1)S(1)} %get-tuple-element.262.refs_10_.refs_8_) | copy-start | bytes 786436
  11.6 87.8 %copy-start.25 = (bf16[128,1024]{1,0:T(8,128)(2,1)}, bf16[128,1024]{1,0:T(8,128)(2,1)S(1)}, u32[]{:S(2)}) copy-start(bf16[128,1024]{1,0:T(8,128)(2,1)S(1)} %get-tuple-element.266.refs_14_) | copy-start | bytes 786436
  11.6 11.8 %collective-permute-start.1 = (bf16[128,768]{1,0:T(8,128)(2,1)S(1)}, bf16[128,768]{1,0:T(8,128)(2,1)S(1)}, u32[]{:S(2)}, u32[]{:S(2)}) collective-permute-start(bf16[128,768]{1,0:T(8,128)(2,1)S(1)} %get-tuple-element.207.refs_4_), channel_id=1, source_target_pairs={{0,16},{4,20},{8,24},{12,28},{16,0},{20,4},{24,8},{28,12},{1,17},{... | collective-permute-start | bytes 589832 | tf_op jit(solution)/shard_map/ppermute | solution.py:45
  14.3 5.3 %collective-permute-start.2 = (bf16[128,256]{1,0:T(8,128)(2,1)}, bf16[128,256]{1,0:T(8,128)(2,1)}, u32[]{:S(2)}, u32[]{:S(2)}) collective-permute-start(bf16[128,256]{1,0:T(8,128)(2,1)} %get-tuple-element.226.refs_6_.refs_0_), channel_id=1, source_target_pairs={{0,4},{4,0},{8,12},{12,8},{16,20},{20,16},{24,28},{28,24},{1,5},{5... | collective-permute-start | bytes 196616 | tf_op jit(solution)/shard_map/ppermute | solution.py:45
  23.4 23.7 %copy-start.31 = (bf16[128,768]{1,0:T(8,128)(2,1)}, bf16[128,768]{1,0:T(8,128)(2,1)S(1)}, u32[]{:S(2)}) copy-start(bf16[128,768]{1,0:T(8,128)(2,1)S(1)} %collective-permute-done.1.refs_5_) | copy-start | bytes 589828
  23.4 23.7 %copy-start.20 = (bf16[640,1024]{1,0:T(8,128)(2,1)}, bf16[640,1024]{1,0:T(8,128)(2,1)S(1)}, u32[]{:S(2)}) copy-start(bf16[640,1024]{1,0:T(8,128)(2,1)S(1)} %collective-permute-done.refs_2_.refs_6_) | copy-start | bytes 3932164
  24.3 14.9 %collective-permute-start.5 = (bf16[256,768]{1,0:T(8,128)(2,1)}, bf16[256,768]{1,0:T(8,128)(2,1)}, u32[]{:S(2)}, u32[]{:S(2)}) collective-permute-start(bf16[256,768]{1,0:T(8,128)(2,1)} %pad_maximum_fusion.5), channel_id=1, source_target_pairs={{0,8},{4,12},{8,0},{12,4},{16,24},{20,28},{24,16},{28,20},{1,9},{5... | collective-permute-start | bytes 1179656 | tf_op jit(solution)/shard_map/ppermute | solution.py:45
  26.5 12.7 %collective-permute-start.6 = (bf16[256,256]{1,0:T(8,128)(2,1)}, bf16[256,256]{1,0:T(8,128)(2,1)}, u32[]{:S(2)}, u32[]{:S(2)}) collective-permute-start(bf16[256,256]{1,0:T(8,128)(2,1)} %pad_maximum_fusion.7), channel_id=1, source_target_pairs={{0,16},{4,20},{8,24},{12,28},{16,0},{20,4},{24,8},{28,12},{1,17},{... | collective-permute-start | bytes 393224 | tf_op jit(solution)/shard_map/ppermute | solution.py:45
  39.1 22.5 %collective-permute-start.7 = (bf16[640,1024]{1,0:T(8,128)(2,1)}, bf16[640,1024]{1,0:T(8,128)(2,1)S(1)}, u32[]{:S(2)}, u32[]{:S(2)}) collective-permute-start(bf16[640,1024]{1,0:T(8,128)(2,1)} %collective-permute-done.4.refs_2_), channel_id=1, source_target_pairs={{0,1},{1,0},{2,3},{3,2},{4,5},{5,4},{6,7},{7,6},{8,9},{9,8},{10,11... | collective-permute-start | bytes 3932168 | tf_op jit(solution)/shard_map/ppermute | solution.py:45
  39.1 21.1 %collective-permute-start.8 = (bf16[384,1024]{1,0:T(8,128)(2,1)}, bf16[384,1024]{1,0:T(8,128)(2,1)}, u32[]{:S(2)}, u32[]{:S(2)}) collective-permute-start(bf16[384,1024]{1,0:T(8,128)(2,1)} %slice.30), channel_id=1, source_target_pairs={{0,2},{1,3},{2,0},{3,1},{4,6},{5,7},{6,4},{7,5},{8,10},{9,11},{10,... | collective-permute-start | bytes 2359304 | tf_op jit(solution)/shard_map/ppermute | solution.py:45
  42.0 19.7 %collective-permute-start.9 = (bf16[512,768]{1,0:T(8,128)(2,1)S(1)}, bf16[512,768]{1,0:T(8,128)(2,1)S(1)}, u32[]{:S(2)}, u32[]{:S(2)}) collective-permute-start(bf16[512,768]{1,0:T(8,128)(2,1)S(1)} %pad_maximum_fusion.2), channel_id=1, source_target_pairs={{0,4},{4,0},{8,12},{12,8},{16,20},{20,16},{24,28},{28,24},{1,5},{5... | collective-permute-start | bytes 2359304 | tf_op jit(solution)/shard_map/ppermute | solution.py:45
  43.6 14.7 %collective-permute-start.11 = (bf16[128,1024]{1,0:T(8,128)(2,1)S(1)}, bf16[128,1024]{1,0:T(8,128)(2,1)S(1)}, u32[]{:S(2)}, u32[]{:S(2)}) collective-permute-start(bf16[128,1024]{1,0:T(8,128)(2,1)S(1)} %get-tuple-element.262.refs_10_.refs_8_), channel_id=1, source_target_pairs={{0,16},{4,20},{8,24},{12,28},{16,0},{20,4},{24,8},{28,12},{1,17},{... | collective-permute-start | bytes 786440 | tf_op jit(solution)/shard_map/ppermute | solution.py:45
  47.2 12.4 %collective-permute-start.10 = (bf16[512,256]{1,0:T(8,128)(2,1)S(1)}, bf16[512,256]{1,0:T(8,128)(2,1)S(1)}, u32[]{:S(2)}, u32[]{:S(2)}) collective-permute-start(bf16[512,256]{1,0:T(8,128)(2,1)S(1)} %pad_maximum_fusion.6), channel_id=1, source_target_pairs={{0,8},{4,12},{8,0},{12,4},{16,24},{20,28},{24,16},{28,20},{1,9},{5... | collective-permute-start | bytes 786440 | tf_op jit(solution)/shard_map/ppermute | solution.py:45
  61.7 21.3 %collective-permute-start.12 = (bf16[384,1024]{1,0:T(8,128)(2,1)}, bf16[384,1024]{1,0:T(8,128)(2,1)}, u32[]{:S(2)}, u32[]{:S(2)}) collective-permute-start(bf16[384,1024]{1,0:T(8,128)(2,1)} %collective-permute-done.8.refs_3_.refs_7_), channel_id=1, source_target_pairs={{0,1},{1,0},{2,3},{3,2},{4,5},{5,4},{6,7},{7,6},{8,9},{9,8},{10,11... | collective-permute-start | bytes 2359304 | tf_op jit(solution)/shard_map/ppermute | solution.py:45
  61.8 20.4 %collective-permute-start.13 = (bf16[256,1024]{1,0:T(8,128)(2,1)}, bf16[256,1024]{1,0:T(8,128)(2,1)}, u32[]{:S(2)}, u32[]{:S(2)}) collective-permute-start(bf16[256,1024]{1,0:T(8,128)(2,1)} %slice.31), channel_id=1, source_target_pairs={{0,2},{1,3},{2,0},{3,1},{4,6},{5,7},{6,4},{7,5},{8,10},{9,11},{10,... | collective-permute-start | bytes 1572872 | tf_op jit(solution)/shard_map/ppermute | solution.py:45
  63.2 19.8 %collective-permute-start.14 = (bf16[256,1024]{1,0:T(8,128)(2,1)}, bf16[256,1024]{1,0:T(8,128)(2,1)}, u32[]{:S(2)}, u32[]{:S(2)}) collective-permute-start(bf16[256,1024]{1,0:T(8,128)(2,1)} %pad_maximum_fusion.3), channel_id=1, source_target_pairs={{0,8},{4,12},{8,0},{12,4},{16,24},{20,28},{24,16},{28,20},{1,9},{5... | collective-permute-start | bytes 1572872 | tf_op jit(solution)/shard_map/ppermute | solution.py:45
  65.4 16.7 %collective-permute-start.15 = (bf16[128,1024]{1,0:T(8,128)(2,1)S(1)}, bf16[128,1024]{1,0:T(8,128)(2,1)}, u32[]{:S(2)}, u32[]{:S(2)}) collective-permute-start(bf16[128,1024]{1,0:T(8,128)(2,1)S(1)} %get-tuple-element.266.refs_14_), channel_id=1, source_target_pairs={{0,16},{4,20},{8,24},{12,28},{16,0},{20,4},{24,8},{28,12},{1,17},{... | collective-permute-start | bytes 786440 | tf_op jit(solution)/shard_map/ppermute | solution.py:45
  79.3 10.4 %copy-start.21 = (bf16[640,1024]{1,0:T(8,128)(2,1)S(1)}, bf16[640,1024]{1,0:T(8,128)(2,1)}, u32[]{:S(2)}) copy-start(bf16[640,1024]{1,0:T(8,128)(2,1)} %copy-done.20) | copy-start | bytes 3932164
  79.3 10.3 %copy-start.45 = (bf16[512,256]{1,0:T(8,128)(2,1)S(1)}, bf16[512,256]{1,0:T(8,128)(2,1)}, u32[]{:S(2)}) copy-start(bf16[512,256]{1,0:T(8,128)(2,1)} %copy-done.44) | copy-start | bytes 786436
  79.3 10.3 %copy-start.49 = (s32[6]{0:T(128)S(1)}, s32[6]{0:T(128)}, u32[]{:S(2)}) copy-start(s32[6]{0:T(128)} %stack.11.ids) | copy-start | bytes 76
  83.0 6.7 %collective-permute-start.16 = (bf16[256,1024]{1,0:T(8,128)(2,1)}, bf16[256,1024]{1,0:T(8,128)(2,1)S(1)}, u32[]{:S(2)}, u32[]{:S(2)}) collective-permute-start(bf16[256,1024]{1,0:T(8,128)(2,1)} %collective-permute-done.13.refs_4_.refs_8_), channel_id=1, source_target_pairs={{0,1},{1,0},{2,3},{3,2},{4,5},{5,4},{6,7},{7,6},{8,9},{9,8},{10,11... | collective-permute-start | bytes 1572872 | tf_op jit(solution)/shard_map/ppermute | solution.py:45
  83.9 15.5 %collective-permute-start.17 = (bf16[256,1024]{1,0:T(8,128)(2,1)S(1)}, bf16[256,1024]{1,0:T(8,128)(2,1)S(1)}, u32[]{:S(2)}, u32[]{:S(2)}) collective-permute-start(bf16[256,1024]{1,0:T(8,128)(2,1)S(1)} %pad_maximum_fusion.4), channel_id=1, source_target_pairs={{0,8},{4,12},{8,0},{12,4},{16,24},{20,28},{24,16},{28,20},{1,9},{5... | collective-permute-start | bytes 1572872 | tf_op jit(solution)/shard_map/ppermute | solution.py:45
  88.0 64.1 %collective-permute-start.18 = (bf16[512,1024]{1,0:T(8,128)(2,1)S(1)}, bf16[512,1024]{1,0:T(8,128)(2,1)S(1)}, u32[]{:S(2)}, u32[]{:S(2)}) collective-permute-start(bf16[512,1024]{1,0:T(8,128)(2,1)S(1)} %pad_maximum_fusion), channel_id=1, source_target_pairs={{0,4},{4,0},{8,12},{12,8},{16,20},{20,16},{24,28},{28,24},{1,5},{5... | collective-permute-start | bytes 3145736 | tf_op jit(solution)/shard_map/ppermute | solution.py:45
  89.6 67.6 %copy-start.35 = (bf16[256,1024]{1,0:T(8,128)(2,1)}, bf16[256,1024]{1,0:T(8,128)(2,1)S(1)}, u32[]{:S(2)}) copy-start(bf16[256,1024]{1,0:T(8,128)(2,1)S(1)} %collective-permute-done.16.refs_1_.refs_5_) | copy-start | bytes 1572868
  89.7 12.6 %copy-start.69 = (bf16[2560,256]{1,0:T(8,128)(2,1)S(1)}, bf16[2560,256]{1,0:T(8,128)(2,1)}, u32[]{:S(2)}) copy-start(bf16[2560,256]{1,0:T(8,128)(2,1)} %get-tuple-element.222.q_ref) | copy-start | bytes 3932164
  89.7 12.6 %copy-start.70 = (bf16[2560,256]{1,0:T(8,128)(2,1)S(1)}, bf16[2560,256]{1,0:T(8,128)(2,1)}, u32[]{:S(2)}) copy-start(bf16[2560,256]{1,0:T(8,128)(2,1)} %get-tuple-element.233.k_ref) | copy-start | bytes 3932164
  89.7 12.6 %copy-start.71 = (bf16[2560,256]{1,0:T(8,128)(2,1)S(1)}, bf16[2560,256]{1,0:T(8,128)(2,1)}, u32[]{:S(2)}) copy-start(bf16[2560,256]{1,0:T(8,128)(2,1)} %get-tuple-element.234.v_ref) | copy-start | bytes 3932164
  95.3 7.0 %copy-start.33 = (f32[1280,128]{1,0:T(8,128)S(1)}, f32[1280,128]{1,0:T(8,128)}, u32[]{:S(2)}) copy-start(f32[1280,128]{1,0:T(8,128)} %get-tuple-element.213.refs_12_.sine.refs_13_) | copy-start | bytes 1966084
  95.3 7.0 %copy-start.34 = (f32[1280,128]{1,0:T(8,128)S(1)}, f32[1280,128]{1,0:T(8,128)}, u32[]{:S(2)}) copy-start(f32[1280,128]{1,0:T(8,128)} %get-tuple-element.212.refs_11_.cos.refs_12_) | copy-start | bytes 1966084
  95.3 7.0 %copy-start.48 = (s32[1,20,5]{2,1,0:T(8,128)S(1)}, s32[1,20,5]{2,1,0:T(8,128)}, u32[]{:S(2)}) copy-start(s32[1,20,5]{2,1,0:T(8,128)} %tree_table.1.info) | copy-start | bytes 1204
  100.6 51.6 %collective-permute-start.19 = (bf16[512,1024]{1,0:T(8,128)(2,1)S(1)}, bf16[512,1024]{1,0:T(8,128)(2,1)S(1)}, u32[]{:S(2)}, u32[]{:S(2)}) collective-permute-start(bf16[512,1024]{1,0:T(8,128)(2,1)S(1)} %pad_maximum_fusion.1), channel_id=1, source_target_pairs={{0,4},{4,0},{8,12},{12,8},{16,20},{20,16},{24,28},{28,24},{1,5},{5... | collective-permute-start | bytes 3145736 | tf_op jit(solution)/shard_map/ppermute | solution.py:45
  157.1 14.4 %collective-permute-start.20 = (bf16[2,640,1024]{2,1,0:T(8,128)(2,1)S(1)}, bf16[2,640,1024]{2,1,0:T(8,128)(2,1)S(1)}, u32[]{:S(2)}, u32[]{:S(2)}) collective-permute-start(bf16[2,640,1024]{2,1,0:T(8,128)(2,1)S(1)} %get-tuple-element.257), channel_id=1, source_target_pairs={{0,1},{1,0},{2,3},{3,2},{4,5},{5,4},{6,7},{7,6},{8,9},{9,8},{10,11... | collective-permute-start | bytes 7864328 | tf_op jit(solution)/shard_map/ppermute | solution.py:45
  172.0 43.0 %collective-permute-start.21 = (bf16[1,640,1024]{2,1,0:T(8,128)(2,1)S(1)}, bf16[1,640,1024]{2,1,0:T(8,128)(2,1)S(1)}, u32[]{:S(2)}, u32[]{:S(2)}) collective-permute-start(bf16[1,640,1024]{2,1,0:T(8,128)(2,1)S(1)} %add_terms.3), channel_id=1, source_target_pairs={{0,2},{1,3},{2,0},{3,1},{4,6},{5,7},{6,4},{7,5},{8,10},{9,11},{10,... | collective-permute-start | bytes 3932168 | tf_op jit(solution)/shard_map/ppermute | solution.py:45
  173.6 41.4 %collective-permute-start.22 = (bf16[4,128,512]{2,1,0:T(8,128)(2,1)}, bf16[4,128,512]{2,1,0:T(8,128)(2,1)S(1)}, u32[]{:S(2)}, u32[]{:S(2)}) collective-permute-start(bf16[4,128,512]{2,1,0:T(8,128)(2,1)} %get-tuple-element.280), channel_id=1, source_target_pairs={{0,4},{4,0},{8,12},{12,8},{16,20},{20,16},{24,28},{28,24},{1,5},{5... | collective-permute-start | bytes 1572872 | tf_op jit(solution)/shard_map/ppermute | solution.py:45
  174.1 41.0 %collective-permute-start.23 = (bf16[4,128,512]{2,1,0:T(8,128)(2,1)}, bf16[4,128,512]{2,1,0:T(8,128)(2,1)S(1)}, u32[]{:S(2)}, u32[]{:S(2)}) collective-permute-start(bf16[4,128,512]{2,1,0:T(8,128)(2,1)} %get-tuple-element.281), channel_id=1, source_target_pairs={{0,8},{4,12},{8,0},{12,4},{16,24},{20,28},{24,16},{28,20},{1,9},{5... | collective-permute-start | bytes 1572872 | tf_op jit(solution)/shard_map/ppermute | solution.py:45
  215.0 11.7 %copy-start.10 = (bf16[4,128,512]{2,1,0:T(8,128)(2,1)}, bf16[4,128,512]{2,1,0:T(8,128)(2,1)S(1)}, u32[]{:S(2)}) copy-start(bf16[4,128,512]{2,1,0:T(8,128)(2,1)S(1)} %collective-permute-done.22.refs_1_) | copy-start | bytes 1572868
  215.0 11.6 %copy-start.12 = (bf16[4,128,512]{2,1,0:T(8,128)(2,1)}, bf16[4,128,512]{2,1,0:T(8,128)(2,1)S(1)}, u32[]{:S(2)}) copy-start(bf16[4,128,512]{2,1,0:T(8,128)(2,1)S(1)} %collective-permute-done.23.refs_3_.refs_4_.refs_5_) | copy-start | bytes 1572868
  216.2 5.1 %collective-permute-start.24 = (bf16[2,640,1024]{2,1,0:T(8,128)(2,1)}, bf16[2,640,1024]{2,1,0:T(8,128)(2,1)S(1)}, u32[]{:S(2)}, u32[]{:S(2)}) collective-permute-start(bf16[2,640,1024]{2,1,0:T(8,128)(2,1)} %get-tuple-element.284), channel_id=1, source_target_pairs={{0,1},{1,0},{2,3},{3,2},{4,5},{5,4},{6,7},{7,6},{8,9},{9,8},{10,11... | collective-permute-start | bytes 7864328 | tf_op jit(solution)/shard_map/ppermute | solution.py:45
  224.3 39.2 %collective-permute-start.25 = (bf16[1,640,1024]{2,1,0:T(8,128)(2,1)}, bf16[1,640,1024]{2,1,0:T(8,128)(2,1)S(1)}, u32[]{:S(2)}, u32[]{:S(2)}) collective-permute-start(bf16[1,640,1024]{2,1,0:T(8,128)(2,1)} %add_terms.4), channel_id=1, source_target_pairs={{0,2},{1,3},{2,0},{3,1},{4,6},{5,7},{6,4},{7,5},{8,10},{9,11},{10,... | collective-permute-start | bytes 3932168 | tf_op jit(solution)/shard_map/ppermute | solution.py:45
  224.9 35.4 %collective-permute-start.28 = (bf16[4,128,1024]{2,1,0:T(8,128)(2,1)}, bf16[4,128,1024]{2,1,0:T(8,128)(2,1)S(1)}, u32[]{:S(2)}, u32[]{:S(2)}) collective-permute-start(bf16[4,128,1024]{2,1,0:T(8,128)(2,1)} %get-tuple-element.296), channel_id=1, source_target_pairs={{0,4},{4,0},{8,12},{12,8},{16,20},{20,16},{24,28},{28,24},{1,5},{5... | collective-permute-start | bytes 3145736 | tf_op jit(solution)/shard_map/ppermute | solution.py:45
  226.4 36.1 %collective-permute-start.29 = (bf16[4,128,1024]{2,1,0:T(8,128)(2,1)}, bf16[4,128,1024]{2,1,0:T(8,128)(2,1)S(1)}, u32[]{:S(2)}, u32[]{:S(2)}) collective-permute-start(bf16[4,128,1024]{2,1,0:T(8,128)(2,1)} %get-tuple-element.297), channel_id=1, source_target_pairs={{0,8},{4,12},{8,0},{12,4},{16,24},{20,28},{24,16},{28,20},{1,9},{5... | collective-permute-start | bytes 3145736 | tf_op jit(solution)/shard_map/ppermute | solution.py:45
  226.8 29.3 %collective-permute-start.26 = (bf16[2,128,512]{2,1,0:T(8,128)(2,1)S(1)}, bf16[2,128,512]{2,1,0:T(8,128)(2,1)S(1)}, u32[]{:S(2)}, u32[]{:S(2)}) collective-permute-start(bf16[2,128,512]{2,1,0:T(8,128)(2,1)S(1)} %get-tuple-element.294), channel_id=1, source_target_pairs={{0,16},{4,20},{8,24},{12,28},{16,0},{20,4},{24,8},{28,12},{1,17},{... | collective-permute-start | bytes 786440 | tf_op jit(solution)/shard_map/ppermute | solution.py:45
  228.5 31.8 %collective-permute-start.27 = (bf16[2,128,512]{2,1,0:T(8,128)(2,1)S(1)}, bf16[2,128,512]{2,1,0:T(8,128)(2,1)S(1)}, u32[]{:S(2)}, u32[]{:S(2)}) collective-permute-start(bf16[2,128,512]{2,1,0:T(8,128)(2,1)S(1)} %get-tuple-element.295), channel_id=1, source_target_pairs={{0,16},{4,20},{8,24},{12,28},{16,0},{20,4},{24,8},{28,12},{1,17},{... | collective-permute-start | bytes 786440 | tf_op jit(solution)/shard_map/ppermute | solution.py:45
  264.5 6.9 %copy-start.9 = (bf16[4,128,1024]{2,1,0:T(8,128)(2,1)S(1)}, bf16[4,128,1024]{2,1,0:T(8,128)(2,1)}, u32[]{:S(2)}) copy-start(bf16[4,128,1024]{2,1,0:T(8,128)(2,1)} %copy-done.8) | copy-start | bytes 3145732
  264.5 6.9 %copy-start.11 = (bf16[4,128,512]{2,1,0:T(8,128)(2,1)S(1)}, bf16[4,128,512]{2,1,0:T(8,128)(2,1)}, u32[]{:S(2)}) copy-start(bf16[4,128,512]{2,1,0:T(8,128)(2,1)} %copy-done.10) | copy-start | bytes 1572868
  264.5 6.9 %copy-start.13 = (bf16[4,128,512]{2,1,0:T(8,128)(2,1)S(1)}, bf16[4,128,512]{2,1,0:T(8,128)(2,1)}, u32[]{:S(2)}) copy-start(bf16[4,128,512]{2,1,0:T(8,128)(2,1)} %copy-done.12) | copy-start | bytes 1572868
  264.5 5.0 %collective-permute-start.30 = (bf16[2,640,1024]{2,1,0:T(8,128)(2,1)S(1)}, bf16[2,640,1024]{2,1,0:T(8,128)(2,1)S(1)}, u32[]{:S(2)}, u32[]{:S(2)}) collective-permute-start(bf16[2,640,1024]{2,1,0:T(8,128)(2,1)S(1)} %get-tuple-element.299), channel_id=1, source_target_pairs={{0,1},{1,0},{2,3},{3,2},{4,5},{5,4},{6,7},{7,6},{8,9},{9,8},{10,11... | collective-permute-start | bytes 7864328 | tf_op jit(solution)/shard_map/ppermute | solution.py:45
  269.9 35.4 %collective-permute-start.37 = (bf16[1,640,1024]{2,1,0:T(8,128)(2,1)S(1)}, bf16[1,640,1024]{2,1,0:T(8,128)(2,1)S(1)}, u32[]{:S(2)}, u32[]{:S(2)}) collective-permute-start(bf16[1,640,1024]{2,1,0:T(8,128)(2,1)S(1)} %add_terms.5), channel_id=1, source_target_pairs={{0,2},{1,3},{2,0},{3,1},{4,6},{5,7},{6,4},{7,5},{8,10},{9,11},{10,... | collective-permute-start | bytes 3932168 | tf_op jit(solution)/shard_map/ppermute | solution.py:45
  271.8 15.9 %collective-permute-start.33 = (bf16[2,128,1024]{2,1,0:T(8,128)(2,1)S(1)}, bf16[2,128,1024]{2,1,0:T(8,128)(2,1)S(1)}, u32[]{:S(2)}, u32[]{:S(2)}) collective-permute-start(bf16[2,128,1024]{2,1,0:T(8,128)(2,1)S(1)} %get-tuple-element.316), channel_id=1, source_target_pairs={{0,8},{4,12},{8,0},{12,4},{16,24},{20,28},{24,16},{28,20},{1,9},{5... | collective-permute-start | bytes 1572872 | tf_op jit(solution)/shard_map/ppermute | solution.py:45
  274.4 13.4 %collective-permute-start.34 = (bf16[2,128,1024]{2,1,0:T(8,128)(2,1)S(1)}, bf16[2,128,1024]{2,1,0:T(8,128)(2,1)S(1)}, u32[]{:S(2)}, u32[]{:S(2)}) collective-permute-start(bf16[2,128,1024]{2,1,0:T(8,128)(2,1)S(1)} %get-tuple-element.317), channel_id=1, source_target_pairs={{0,4},{4,0},{8,12},{12,8},{16,20},{20,16},{24,28},{28,24},{1,5},{5... | collective-permute-start | bytes 1572872 | tf_op jit(solution)/shard_map/ppermute | solution.py:45
  278.6 1.3 collective-permute-start.31
  279.9 7.9 %collective-permute-start.32 = (f32[16,1024]{1,0:T(8,128)S(1)}, f32[16,1024]{1,0:T(8,128)S(1)}, u32[]{:S(2)}, u32[]{:S(2)}) collective-permute-start(f32[16,1024]{1,0:T(8,128)S(1)} %add.41), channel_id=1, source_target_pairs={{0,16},{4,20},{8,24},{12,28},{16,0},{20,4},{24,8},{28,12},{1,17},{... | collective-permute-start | bytes 196616 | tf_op jit(solution)/shard_map/ppermute | solution.py:45
  288.0 4.3 %collective-permute-start.35 = (f32[16,1024]{1,0:T(8,128)S(1)}, f32[16,1024]{1,0:T(8,128)S(1)}, u32[]{:S(2)}, u32[]{:S(2)}) collective-permute-start(f32[16,1024]{1,0:T(8,128)S(1)} %add.42), channel_id=1, source_target_pairs={{0,4},{4,0},{8,12},{12,8},{16,20},{20,16},{24,28},{28,24},{1,5},{5... | collective-permute-start | bytes 196616 | tf_op jit(solution)/shard_map/ppermute | solution.py:45
  288.6 21.1 %collective-permute-start.41 = (bf16[1,128,1024]{2,1,0:T(8,128)(2,1)S(1)}, bf16[1,128,1024]{2,1,0:T(8,128)(2,1)S(1)}, u32[]{:S(2)}, u32[]{:S(2)}) collective-permute-start(bf16[1,128,1024]{2,1,0:T(8,128)(2,1)S(1)} %get-tuple-element.331), channel_id=1, source_target_pairs={{0,16},{4,20},{8,24},{12,28},{16,0},{20,4},{24,8},{28,12},{1,17},{... | collective-permute-start | bytes 786440 | tf_op jit(solution)/shard_map/ppermute | solution.py:45
  291.1 22.4 %collective-permute-start.42 = (bf16[1,128,1024]{2,1,0:T(8,128)(2,1)S(1)}, bf16[1,128,1024]{2,1,0:T(8,128)(2,1)S(1)}, u32[]{:S(2)}, u32[]{:S(2)}) collective-permute-start(bf16[1,128,1024]{2,1,0:T(8,128)(2,1)S(1)} %get-tuple-element.332), channel_id=1, source_target_pairs={{0,16},{4,20},{8,24},{12,28},{16,0},{20,4},{24,8},{28,12},{1,17},{... | collective-permute-start | bytes 786440 | tf_op jit(solution)/shard_map/ppermute | solution.py:45
  292.3 11.4 %collective-permute-start.36 = (f32[16,1024]{1,0:T(8,128)S(1)}, f32[16,1024]{1,0:T(8,128)S(1)}, u32[]{:S(2)}, u32[]{:S(2)}) collective-permute-start(f32[16,1024]{1,0:T(8,128)S(1)} %add.43), channel_id=1, source_target_pairs={{0,8},{4,12},{8,0},{12,4},{16,24},{20,28},{24,16},{28,20},{1,9},{5... | collective-permute-start | bytes 196616 | tf_op jit(solution)/shard_map/ppermute | solution.py:45
  293.8 12.1 %collective-permute-start.39 = (bf16[1,128,512]{2,1,0:T(8,128)(2,1)S(1)}, bf16[1,128,512]{2,1,0:T(8,128)(2,1)S(1)}, u32[]{:S(2)}, u32[]{:S(2)}) collective-permute-start(bf16[1,128,512]{2,1,0:T(8,128)(2,1)S(1)} %get-tuple-element.327), channel_id=1, source_target_pairs={{0,8},{4,12},{8,0},{12,4},{16,24},{20,28},{24,16},{28,20},{1,9},{5... | collective-permute-start | bytes 393224 | tf_op jit(solution)/shard_map/ppermute | solution.py:45
  303.8 5.0 %collective-permute-start.40 = (bf16[1,128,512]{2,1,0:T(8,128)(2,1)S(1)}, bf16[1,128,512]{2,1,0:T(8,128)(2,1)S(1)}, u32[]{:S(2)}, u32[]{:S(2)}) collective-permute-start(bf16[1,128,512]{2,1,0:T(8,128)(2,1)S(1)} %get-tuple-element.328), channel_id=1, source_target_pairs={{0,4},{4,0},{8,12},{12,8},{16,20},{20,16},{24,28},{28,24},{1,5},{5... | collective-permute-start | bytes 393224 | tf_op jit(solution)/shard_map/ppermute | solution.py:45
  305.3 12.3 %collective-permute-start.38 = (f32[16,1024]{1,0:T(8,128)S(1)}, f32[16,1024]{1,0:T(8,128)S(1)}, u32[]{:S(2)}, u32[]{:S(2)}) collective-permute-start(f32[16,1024]{1,0:T(8,128)S(1)} %add.44), channel_id=1, source_target_pairs={{0,2},{1,3},{2,0},{3,1},{4,6},{5,7},{6,4},{7,5},{8,10},{9,11},{10,... | collective-permute-start | bytes 196616 | tf_op jit(solution)/shard_map/ppermute | solution.py:45
  (53 other events, 215.5 us)

commit v11 on v10

--- a/solution.py
+++ b/solution.py
@@ -1108,7 +1108,7 @@
     columns_first = data_bits[:1] + data_bits[:0:-1]
     near_bits = data_bits
     next_bits = data_bits[1:2] + data_bits[:1] + data_bits[2:]
-    qkv_bits = [data_bits[:1] + data_bits[:0:-1], data_bits[1:2] + data_bits[2:] + data_bits[:1]]
+    qkv_bits = [data_bits[:1] + data_bits[:0:-1], next_bits]
 
     blocks = prepare_weights(qkv_weight, dense_weight, fc_weight, out_weight)
     qkv_pack = Pack(blocks[0], "dp", rows_first)
@@ -1249,7 +1249,7 @@
     sums = sums + swap(sums, "tensor", 1)
     for bit in data_bits[3:]:
         sums = sums + swap(sums, "dp", bit)
-    other, *_ = tie_halves([swap(sums, "dp", data_bits[2])], *mlp_sums)
+    other, *_ = tie_halves([swap(sums, "dp", data_bits[2])], *mlp_sums, qkv_sums[1])
     sums = sums + other
     add_stacks(mlp_sums)
     sums, *sends = tie(sums, *[parts.send for parts in mlp_sums])

time: 322 us -> 318 us (0.988)
  waiting for transfers between devices: 73.8 us -> 69.2 us
    ppermute x43, waiting for transfers between devices: 73.8 us -> 69.2 us  [swap(): return lax.ppermute(block, axis, [(i, i ^ bit) for i in range(size)])]
    unnamed x151 -> x153, local copies, waits for them, and re-layouts: 19 us -> 18.8 us
  transfers between devices with their start and end apart: 43 -> 43, of which waited for: 20 -> 20; matrix products, arithmetic and copies ran while one was open for 5% -> 6% of each run, Pallas kernels for 46% -> 47%
where the time goes in v11:
time: 318 us; the launch traced here: 317 us
  Pallas kernels  154 us (48%)
  waiting for transfers between devices  69.2 us (22%)
  starting transfers between devices  53.9 us (17%)
  local copies, waits for them, and re-layouts  25.2 us (8%)
  other arithmetic  13.2 us (4%)
    pallas_call x19, Pallas kernels, call(): pl.pallas_call(kernel, grid_spec=pltpu.PrefetchScalarGridSpec(num_scalar_...  152 us
    ppermute x43, waiting for transfers between devices, swap(): return lax.ppermute(block, axis, [(i, i ^ bit) for i in range(size)])  69.2 us
    ppermute x43, starting transfers between devices, swap(): return lax.ppermute(block, axis, [(i, i ^ bit) for i in range(size)])  53.9 us
    unnamed x153, local copies, waits for them, and re-layouts  18.8 us
    concatenate x8, other arithmetic, double(): jnp.concatenate(self.arrays, axis=0)  8.75 us
  transfers between devices with their start and end apart: 43, of which 20 were waited for; matrix products, arithmetic and copies ran while one was open for 6% of the time, Pallas kernels for 47%

profile of v11, /device:TPU:0, one launch (start us, length us, event | category | flops | bytes accessed | tf_op | source)
XLA Modules:
  0.0 317.4 jit_solution(5594614468952515311)
XLA Ops:
  1.2 1.7 copy-done.4
  2.9 2.2 normalize.1
  5.2 1.5 copy-done.14
  6.8 2.9 collective-permute-start.4
  11.5 2.7 collective-permute-start.1
  14.1 1.5 collective-permute-start.2
  17.4 2.0 tree_table.1.info
  19.4 3.9 %collective-permute-done.1.refs_5_ = bf16[128,768]{1,0:T(8,128)(2,1)S(1)} collective-permute-done((bf16[128,768]{1,0:T(8,128)(2,1)S(1)}, bf16[128,768]{1,0:T(8,128)(2,1)S(1)}, u32[]{:S(2)}, u32[]{:S(2)}) %collective-permute-start.1) | collective-permute-done | bytes 196640 | tf_op jit(solution)/shard_map/ppermute | solution.py:45
  24.8 1.5 pad_maximum_fusion.7
  26.4 3.4 %collective-permute-start.6 = (bf16[256,256]{1,0:T(8,128)(2,1)}, bf16[256,256]{1,0:T(8,128)(2,1)}, u32[]{:S(2)}, u32[]{:S(2)}) collective-permute-start(bf16[256,256]{1,0:T(8,128)(2,1)} %pad_maximum_fusion.7), channel_id=1, source_target_pairs={{0,16},{4,20},{8,24},{12,28},{16,0},{20,4},{24,8},{28,12},{1,17},{... | collective-permute-start | bytes 393224 | tf_op jit(solution)/shard_map/ppermute | solution.py:45
  29.8 3.8 %fusion = (f32[1280,128]{1,0:T(8,128)}, f32[1280,128]{1,0:T(8,128)}) fusion(s32[128]{0:T(128)S(1)} %get-tuple-element.344, s32[128]{0:T(128)S(1)} %get-tuple-element.345, pred[128]{0:T(512)(128)(4,1)S(1)} %compare_and_fusion, f32[1280]{0:T(1024)S(1)} %convert_add_fusion), kind=kLoop, calls=%fused_computation.9 | loop fusion | flops 3112960 | bytes 1316992 | tf_op jit(solution)/shard_map/jit(_where)/select_n | solution.py:1059
  33.5 1.3 reshape.42.refs_10_
  34.8 1.3 reshape.43.refs_20_
  36.2 2.8 collective-permute-done.4.refs_2_
  39.0 1.8 collective-permute-start.8
  41.9 1.6 collective-permute-start.9
  43.5 2.6 collective-permute-start.11
  47.0 1.6 collective-permute-start.10
  48.7 9.5 %collective-permute-done.11.refs_11_.refs_9_ = bf16[128,1024]{1,0:T(8,128)(2,1)S(1)} collective-permute-done((bf16[128,1024]{1,0:T(8,128)(2,1)S(1)}, bf16[128,1024]{1,0:T(8,128)(2,1)S(1)}, u32[]{:S(2)}, u32[]{:S(2)}) %collective-permute-start.11) | collective-permute-done | bytes 262176 | tf_op jit(solution)/shard_map/ppermute | solution.py:45
  58.2 1.2 collective-permute-done.10.refs_9_.refs_3_
  60.1 1.4 collective-permute-done.9.refs_7_
  63.0 1.6 collective-permute-start.14
  65.2 2.6 collective-permute-start.15
  67.8 11.3 %project_qkv.1 = (bf16[2560,256]{1,0:T(8,128)(2,1)}, bf16[2560,256]{1,0:T(8,128)(2,1)}, bf16[2560,256]{1,0:T(8,128)(2,1)}) custom-call(s32[6]{0:T(128)} %stack.11.ids, s32[1,20,5]{2,1,0:T(8,128)} %tree_table.1.info, bf16[640,1024]{1,0:T(8,128)(2,1)} %copy-done.52, bf16[640,1024]{1,0:T(8,128)(2,1)} %collective-permute-done.3.refs_1_, ...), custom_call_target="tpu_custom_call" | custom-call | flops 4026531840 | bytes 12079104 | tf_op jit(solution)/shard_map/project_qkv/pallas_call | solution.py:217
  79.1 2.8 collective-permute-done.15.refs_15_
  83.8 2.9 collective-permute-start.17
  87.9 1.6 collective-permute-start.18
  89.6 5.6 %project_grad.1.do_ref = bf16[2560,256]{1,0:T(8,128)(2,1)S(1)} custom-call(s32[6]{0:T(128)S(1)} %copy-done.49, bf16[384,1024]{1,0:T(8,128)(2,1)} %collective-permute-done.12.refs_0_.refs_4_, bf16[256,1024]{1,0:T(8,128)(2,1)S(1)} %collective-permute-done.16.refs_1_.refs_5_, bf16[640,1024]{1,0:T(8,128)(2,1)S(1)} %copy-done.21, ...), custom_call_target="tpu_custom_call" | custom-call | flops 1342177280 | bytes 7077888 | tf_op jit(solution)/shard_map/project_grad/pallas_call | solution.py:217
  95.1 4.2 %collective-permute-done.17.refs_16_ = bf16[256,1024]{1,0:T(8,128)(2,1)S(1)} collective-permute-done((bf16[256,1024]{1,0:T(8,128)(2,1)S(1)}, bf16[256,1024]{1,0:T(8,128)(2,1)S(1)}, u32[]{:S(2)}, u32[]{:S(2)}) %collective-permute-start.17) | collective-permute-done | bytes 524320 | tf_op jit(solution)/shard_map/ppermute | solution.py:45
  100.5 1.6 collective-permute-start.19
  102.1 49.9 %attention.1 = (bf16[2560,256]{1,0:T(8,128)(2,1)S(1)}, bf16[2560,256]{1,0:T(8,128)(2,1)S(1)}, bf16[2560,256]{1,0:T(8,128)(2,1)S(1)}, bf16[2560,256]{1,0:T(8,128)(2,1)S(1)}) custom-call(s32[1,20,5]{2,1,0:T(8,128)S(1)} %copy-done.48, bf16[2560,256]{1,0:T(8,128)(2,1)S(1)} %copy-done.70, bf16[2560,256]{1,0:T(8,128)(2,1)S(1)} %project_grad.1.do_ref, ...), custom_call_target="tpu_custom_call" | custom-call | flops 31406948352 | bytes 11796480 | tf_op jit(solution)/shard_map/attention/pallas_call | solution.py:217
  152.1 4.8 %project_context.1 = (bf16[2,640,1024]{2,1,0:T(8,128)(2,1)S(1)}, bf16[2,640,1024]{2,1,0:T(8,128)(2,1)S(1)}) custom-call(s32[6]{0:T(128)S(1)} %copy-done.49, bf16[2560,256]{1,0:T(8,128)(2,1)S(1)} %get-tuple-element.248.ctx.ctx_ref, bf16[128,256]{1,0:T(8,128)(2,1)} %get-tuple-element.227.refs_6_.refs_0_, ...), custom_call_target="tpu_custom_call" | custom-call | flops 1342177280 | bytes 7077888 | tf_op jit(solution)/shard_map/project_context/pallas_call | solution.py:217
  157.1 12.3 %attention_weights.1 = (bf16[2560,768]{1,0:T(8,128)(2,1)S(1)}, f32[8,768]{1,0:T(8,128)S(1)}, bf16[4,128,512]{2,1,0:T(8,128)(2,1)}, bf16[4,128,512]{2,1,0:T(8,128...) custom-call(s32[6]{0:T(128)S(1)} %copy-done.49, s32[1,20,5]{2,1,0:T(8,128)S(1)} %copy-done.48, ...), custom_call_target="tpu_custom_call" | custom-call | flops 5368709120 | bytes 23101440 | tf_op jit(solution)/shard_map/attention_weights/pallas_call | solution.py:217
  169.4 1.9 copy-done.68
  171.8 1.6 collective-permute-start.21
  173.8 1.7 collective-permute-start.23
  175.6 38.8 %mlp.1 = (bf16[2,640,1024]{2,1,0:T(8,128)(2,1)}, bf16[2,640,1024]{2,1,0:T(8,128)(2,1)}, bf16[2560,1024]{1,0:T(8,128)(2,1)}, f32[8,1024]{1,0:T(8,128)S(1)}, bf16[...) custom-call(s32[6]{0:T(128)S(1)} %copy-done.49, ...), custom_call_target="tpu_custom_call" | custom-call | flops 26843545600 | bytes 29417472 | tf_op jit(solution)/shard_map/mlp/pallas_call | solution.py:217
  214.5 1.2 copy-done.16
  215.7 5.1 %collective-permute-done.24.refs_1_.refs_4_ = bf16[2,640,1024]{2,1,0:T(8,128)(2,1)S(1)} collective-permute-done((bf16[2,640,1024]{2,1,0:T(8,128)(2,1)}, bf16[2,640,1024]{2,1,0:T(8,128)(2,1)S(1)}, u32[]{:S(2)}, u32[]{:S(2)}) %collective-permute-start.24) | collective-permute-done | bytes 2621472 | tf_op jit(solution)/shard_map/ppermute | solution.py:45
  220.8 1.7 copy-done.2
  222.6 1.2 add_terms.4
  224.4 1.5 collective-permute-start.28
  226.3 1.7 collective-permute-start.26
  229.1 2.1 copy-done.69
  231.2 2.5 copy-done.73
  233.7 15.4 %norm_backward.1 = (bf16[2,640,1024]{2,1,0:T(8,128)(2,1)S(1)}, bf16[2,640,1024]{2,1,0:T(8,128)(2,1)S(1)}, f32[8,1024]{1,0:T(8,128)S(1)}) custom-call(s32[6]{0:T(128)S(1)} %copy-done.49, bf16[2560,768]{1,0:T(8,128)(2,1)S(1)} %copy-done.69, bf16[2560,1024]{1,0:T(8,128)(2,1)S(1)} %copy-done.73, bf16[640,1024]{1,0:T(8,128)(2,1)S(1)} %copy-done.55, ...), custom_call_target="tpu_custom_call" | custom-call | flops 9395240960 | bytes 23371776 | tf_op jit(solution)/shard_map/norm_backward/pallas_call | solution.py:217
  249.1 5.1 %collective-permute-done.26.refs_2_ = bf16[2,128,512]{2,1,0:T(8,128)(2,1)S(1)} collective-permute-done((bf16[2,128,512]{2,1,0:T(8,128)(2,1)S(1)}, bf16[2,128,512]{2,1,0:T(8,128)(2,1)S(1)}, u32[]{:S(2)}, u32[]{:S(2)}) %collective-permute-start.26) | collective-permute-done | bytes 262176 | tf_op jit(solution)/shard_map/ppermute | solution.py:45
  258.5 4.9 %collective-permute-done.30.refs_1_ = bf16[2,640,1024]{2,1,0:T(8,128)(2,1)S(1)} collective-permute-done((bf16[2,640,1024]{2,1,0:T(8,128)(2,1)S(1)}, bf16[2,640,1024]{2,1,0:T(8,128)(2,1)S(1)}, u32[]{:S(2)}, u32[]{:S(2)}) %collective-permute-start.30) | collective-permute-done | bytes 2621472 | tf_op jit(solution)/shard_map/ppermute | solution.py:45
  263.8 1.6 collective-permute-start.38
  265.7 2.6 collective-permute-start.33
  269.0 3.7 %finish_output.1 = (f32[640,1024]{1,0:T(8,128)}, f32[16,1024]{1,0:T(8,128)S(1)}) custom-call(s32[6]{0:T(128)S(1)} %copy-done.49, f32[640,1024]{1,0:T(8,128)S(1)} %copy-done.5, bf16[640,1024]{1,0:T(8,128)(2,1)S(1)} %copy-done.1, bf16[2,640,1024]{2,1,0:T(8,128)(2,1)S(1)} %get-tuple-element.260.refs_0_, ...), custom_call_target="tpu_custom_call" | custom-call | flops 10485760 | bytes 19824640 | tf_op jit(solution)/shard_map/finish_output/pallas_call | solution.py:217
  272.7 1.3 collective-permute-done.31
  274.0 2.8 collective-permute-start.32
  276.8 6.2 %collective-permute-done.35.refs_7_ = bf16[1,128,512]{2,1,0:T(8,128)(2,1)S(1)} collective-permute-done((bf16[1,128,512]{2,1,0:T(8,128)(2,1)S(1)}, bf16[1,128,512]{2,1,0:T(8,128)(2,1)S(1)}, u32[]{:S(2)}, u32[]{:S(2)}) %collective-permute-start.35) | collective-permute-done | bytes 131104 | tf_op jit(solution)/shard_map/ppermute | solution.py:45
  283.0 1.4 collective-permute-done.33.refs_2_
  284.7 2.7 collective-permute-start.41
  288.2 1.5 collective-permute-start.40
  289.7 2.3 collective-permute-done.36
  291.9 1.5 collective-permute-start.37
  293.4 8.5 %collective-permute-done.37 = f32[16,1024]{1,0:T(8,128)S(1)} collective-permute-done((f32[16,1024]{1,0:T(8,128)S(1)}, f32[16,1024]{1,0:T(8,128)S(1)}, u32[]{:S(2)}, u32[]{:S(2)}) %collective-permute-start.37) | collective-permute-done | bytes 65568 | tf_op jit(solution)/shard_map/ppermute | solution.py:45
  303.5 1.6 collective-permute-done.41.refs_3_
  305.1 4.9 %collective-permute-done.42.refs_7_ = bf16[1,128,1024]{2,1,0:T(8,128)(2,1)S(1)} collective-permute-done((bf16[1,128,1024]{2,1,0:T(8,128)(2,1)S(1)}, bf16[1,128,1024]{2,1,0:T(8,128)(2,1)S(1)}, u32[]{:S(2)}, u32[]{:S(2)}) %collective-permute-start.42) | collective-permute-done | bytes 262176 | tf_op jit(solution)/shard_map/ppermute | solution.py:45
  310.0 1.2 finish_mlp_weights.1
  311.2 2.9 finish_grad.1
  (224 shorter events, 29.6 us)
Async XLA Ops:
  0.6 15.0 %copy-start = (bf16[640,1024]{1,0:T(8,128)(2,1)S(1)}, bf16[640,1024]{1,0:T(8,128)(2,1)}, u32[]{:S(2)}) copy-start(bf16[640,1024]{1,0:T(8,128)(2,1)} %grad_ref.3) | copy-start | bytes 3932164
  0.7 22.7 %collective-permute-start = (bf16[640,1024]{1,0:T(8,128)(2,1)}, bf16[640,1024]{1,0:T(8,128)(2,1)S(1)}, u32[]{:S(2)}, u32[]{:S(2)}) collective-permute-start(bf16[640,1024]{1,0:T(8,128)(2,1)} %grad_ref.3), channel_id=1, source_target_pairs={{0,1},{1,0},{2,3},{3,2},{4,5},{5,4},{6,7},{7,6},{8,9},{9,8},{10,11... | collective-permute-start | bytes 3932168 | tf_op jit(solution)/shard_map/ppermute | solution.py:45
  6.6 29.5 %collective-permute-start.3 = (bf16[640,1024]{1,0:T(8,128)(2,1)}, bf16[640,1024]{1,0:T(8,128)(2,1)}, u32[]{:S(2)}, u32[]{:S(2)}) collective-permute-start(bf16[640,1024]{1,0:T(8,128)(2,1)} %get-tuple-element.207.refs_3_), channel_id=1, source_target_pairs={{0,1},{1,0},{2,3},{3,2},{4,5},{5,4},{6,7},{7,6},{8,9},{9,8},{10,11... | collective-permute-start | bytes 3932168 | tf_op jit(solution)/shard_map/ppermute | solution.py:45
  6.8 32.2 %collective-permute-start.4 = (bf16[640,1024]{1,0:T(8,128)(2,1)}, bf16[640,1024]{1,0:T(8,128)(2,1)}, u32[]{:S(2)}, u32[]{:S(2)}) collective-permute-start(bf16[640,1024]{1,0:T(8,128)(2,1)} %get-tuple-element.207.refs_3_), channel_id=1, source_target_pairs={{0,2},{1,3},{2,0},{3,1},{4,6},{5,7},{6,4},{7,5},{8,10},{9,11},{10,... | collective-permute-start | bytes 3932168 | tf_op jit(solution)/shard_map/ppermute | solution.py:45
  11.5 29.3 %copy-start.29 = (bf16[128,768]{1,0:T(8,128)(2,1)}, bf16[128,768]{1,0:T(8,128)(2,1)S(1)}, u32[]{:S(2)}) copy-start(bf16[128,768]{1,0:T(8,128)(2,1)S(1)} %get-tuple-element.208.refs_4_) | copy-start | bytes 589828
  11.5 75.2 %copy-start.22 = (bf16[128,1024]{1,0:T(8,128)(2,1)}, bf16[128,1024]{1,0:T(8,128)(2,1)S(1)}, u32[]{:S(2)}) copy-start(bf16[128,1024]{1,0:T(8,128)(2,1)S(1)} %get-tuple-element.263.refs_10_.refs_8_) | copy-start | bytes 786436
  11.5 87.8 %copy-start.25 = (bf16[128,1024]{1,0:T(8,128)(2,1)}, bf16[128,1024]{1,0:T(8,128)(2,1)S(1)}, u32[]{:S(2)}) copy-start(bf16[128,1024]{1,0:T(8,128)(2,1)S(1)} %get-tuple-element.267.refs_14_) | copy-start | bytes 786436
  11.5 11.8 %collective-permute-start.1 = (bf16[128,768]{1,0:T(8,128)(2,1)S(1)}, bf16[128,768]{1,0:T(8,128)(2,1)S(1)}, u32[]{:S(2)}, u32[]{:S(2)}) collective-permute-start(bf16[128,768]{1,0:T(8,128)(2,1)S(1)} %get-tuple-element.208.refs_4_), channel_id=1, source_target_pairs={{0,16},{4,20},{8,24},{12,28},{16,0},{20,4},{24,8},{28,12},{1,17},{... | collective-permute-start | bytes 589832 | tf_op jit(solution)/shard_map/ppermute | solution.py:45
  14.1 5.3 %collective-permute-start.2 = (bf16[128,256]{1,0:T(8,128)(2,1)}, bf16[128,256]{1,0:T(8,128)(2,1)}, u32[]{:S(2)}, u32[]{:S(2)}) collective-permute-start(bf16[128,256]{1,0:T(8,128)(2,1)} %get-tuple-element.227.refs_6_.refs_0_), channel_id=1, source_target_pairs={{0,4},{4,0},{8,12},{12,8},{16,20},{20,16},{24,28},{28,24},{1,5},{5... | collective-permute-start | bytes 196616 | tf_op jit(solution)/shard_map/ppermute | solution.py:45
  23.3 23.7 %copy-start.31 = (bf16[128,768]{1,0:T(8,128)(2,1)}, bf16[128,768]{1,0:T(8,128)(2,1)S(1)}, u32[]{:S(2)}) copy-start(bf16[128,768]{1,0:T(8,128)(2,1)S(1)} %collective-permute-done.1.refs_5_) | copy-start | bytes 589828
  23.3 23.7 %copy-start.20 = (bf16[640,1024]{1,0:T(8,128)(2,1)}, bf16[640,1024]{1,0:T(8,128)(2,1)S(1)}, u32[]{:S(2)}) copy-start(bf16[640,1024]{1,0:T(8,128)(2,1)S(1)} %collective-permute-done.refs_2_.refs_6_) | copy-start | bytes 3932164
  24.2 14.8 %collective-permute-start.5 = (bf16[256,768]{1,0:T(8,128)(2,1)}, bf16[256,768]{1,0:T(8,128)(2,1)}, u32[]{:S(2)}, u32[]{:S(2)}) collective-permute-start(bf16[256,768]{1,0:T(8,128)(2,1)} %pad_maximum_fusion.5), channel_id=1, source_target_pairs={{0,8},{4,12},{8,0},{12,4},{16,24},{20,28},{24,16},{28,20},{1,9},{5... | collective-permute-start | bytes 1179656 | tf_op jit(solution)/shard_map/ppermute | solution.py:45
  26.4 12.6 %collective-permute-start.6 = (bf16[256,256]{1,0:T(8,128)(2,1)}, bf16[256,256]{1,0:T(8,128)(2,1)}, u32[]{:S(2)}, u32[]{:S(2)}) collective-permute-start(bf16[256,256]{1,0:T(8,128)(2,1)} %pad_maximum_fusion.7), channel_id=1, source_target_pairs={{0,16},{4,20},{8,24},{12,28},{16,0},{20,4},{24,8},{28,12},{1,17},{... | collective-permute-start | bytes 393224 | tf_op jit(solution)/shard_map/ppermute | solution.py:45
  39.0 22.5 %collective-permute-start.7 = (bf16[640,1024]{1,0:T(8,128)(2,1)}, bf16[640,1024]{1,0:T(8,128)(2,1)S(1)}, u32[]{:S(2)}, u32[]{:S(2)}) collective-permute-start(bf16[640,1024]{1,0:T(8,128)(2,1)} %collective-permute-done.4.refs_2_), channel_id=1, source_target_pairs={{0,1},{1,0},{2,3},{3,2},{4,5},{5,4},{6,7},{7,6},{8,9},{9,8},{10,11... | collective-permute-start | bytes 3932168 | tf_op jit(solution)/shard_map/ppermute | solution.py:45
  39.0 21.1 %collective-permute-start.8 = (bf16[384,1024]{1,0:T(8,128)(2,1)}, bf16[384,1024]{1,0:T(8,128)(2,1)}, u32[]{:S(2)}, u32[]{:S(2)}) collective-permute-start(bf16[384,1024]{1,0:T(8,128)(2,1)} %slice.30), channel_id=1, source_target_pairs={{0,2},{1,3},{2,0},{3,1},{4,6},{5,7},{6,4},{7,5},{8,10},{9,11},{10,... | collective-permute-start | bytes 2359304 | tf_op jit(solution)/shard_map/ppermute | solution.py:45
  41.9 19.7 %collective-permute-start.9 = (bf16[512,768]{1,0:T(8,128)(2,1)S(1)}, bf16[512,768]{1,0:T(8,128)(2,1)S(1)}, u32[]{:S(2)}, u32[]{:S(2)}) collective-permute-start(bf16[512,768]{1,0:T(8,128)(2,1)S(1)} %pad_maximum_fusion.2), channel_id=1, source_target_pairs={{0,4},{4,0},{8,12},{12,8},{16,20},{20,16},{24,28},{28,24},{1,5},{5... | collective-permute-start | bytes 2359304 | tf_op jit(solution)/shard_map/ppermute | solution.py:45
  43.5 14.7 %collective-permute-start.11 = (bf16[128,1024]{1,0:T(8,128)(2,1)S(1)}, bf16[128,1024]{1,0:T(8,128)(2,1)S(1)}, u32[]{:S(2)}, u32[]{:S(2)}) collective-permute-start(bf16[128,1024]{1,0:T(8,128)(2,1)S(1)} %get-tuple-element.263.refs_10_.refs_8_), channel_id=1, source_target_pairs={{0,16},{4,20},{8,24},{12,28},{16,0},{20,4},{24,8},{28,12},{1,17},{... | collective-permute-start | bytes 786440 | tf_op jit(solution)/shard_map/ppermute | solution.py:45
  47.0 12.4 %collective-permute-start.10 = (bf16[512,256]{1,0:T(8,128)(2,1)S(1)}, bf16[512,256]{1,0:T(8,128)(2,1)S(1)}, u32[]{:S(2)}, u32[]{:S(2)}) collective-permute-start(bf16[512,256]{1,0:T(8,128)(2,1)S(1)} %pad_maximum_fusion.6), channel_id=1, source_target_pairs={{0,8},{4,12},{8,0},{12,4},{16,24},{20,28},{24,16},{28,20},{1,9},{5... | collective-permute-start | bytes 786440 | tf_op jit(solution)/shard_map/ppermute | solution.py:45
  61.5 21.3 %collective-permute-start.12 = (bf16[384,1024]{1,0:T(8,128)(2,1)}, bf16[384,1024]{1,0:T(8,128)(2,1)}, u32[]{:S(2)}, u32[]{:S(2)}) collective-permute-start(bf16[384,1024]{1,0:T(8,128)(2,1)} %collective-permute-done.8.refs_3_.refs_7_), channel_id=1, source_target_pairs={{0,1},{1,0},{2,3},{3,2},{4,5},{5,4},{6,7},{7,6},{8,9},{9,8},{10,11... | collective-permute-start | bytes 2359304 | tf_op jit(solution)/shard_map/ppermute | solution.py:45
  61.6 20.4 %collective-permute-start.13 = (bf16[256,1024]{1,0:T(8,128)(2,1)}, bf16[256,1024]{1,0:T(8,128)(2,1)}, u32[]{:S(2)}, u32[]{:S(2)}) collective-permute-start(bf16[256,1024]{1,0:T(8,128)(2,1)} %slice.31), channel_id=1, source_target_pairs={{0,2},{1,3},{2,0},{3,1},{4,6},{5,7},{6,4},{7,5},{8,10},{9,11},{10,... | collective-permute-start | bytes 1572872 | tf_op jit(solution)/shard_map/ppermute | solution.py:45
  63.0 19.8 %collective-permute-start.14 = (bf16[256,1024]{1,0:T(8,128)(2,1)}, bf16[256,1024]{1,0:T(8,128)(2,1)}, u32[]{:S(2)}, u32[]{:S(2)}) collective-permute-start(bf16[256,1024]{1,0:T(8,128)(2,1)} %pad_maximum_fusion.3), channel_id=1, source_target_pairs={{0,8},{4,12},{8,0},{12,4},{16,24},{20,28},{24,16},{28,20},{1,9},{5... | collective-permute-start | bytes 1572872 | tf_op jit(solution)/shard_map/ppermute | solution.py:45
  65.2 16.7 %collective-permute-start.15 = (bf16[128,1024]{1,0:T(8,128)(2,1)S(1)}, bf16[128,1024]{1,0:T(8,128)(2,1)}, u32[]{:S(2)}, u32[]{:S(2)}) collective-permute-start(bf16[128,1024]{1,0:T(8,128)(2,1)S(1)} %get-tuple-element.267.refs_14_), channel_id=1, source_target_pairs={{0,16},{4,20},{8,24},{12,28},{16,0},{20,4},{24,8},{28,12},{1,17},{... | collective-permute-start | bytes 786440 | tf_op jit(solution)/shard_map/ppermute | solution.py:45
  79.1 10.4 %copy-start.21 = (bf16[640,1024]{1,0:T(8,128)(2,1)S(1)}, bf16[640,1024]{1,0:T(8,128)(2,1)}, u32[]{:S(2)}) copy-start(bf16[640,1024]{1,0:T(8,128)(2,1)} %copy-done.20) | copy-start | bytes 3932164
  79.1 10.4 %copy-start.45 = (bf16[512,256]{1,0:T(8,128)(2,1)S(1)}, bf16[512,256]{1,0:T(8,128)(2,1)}, u32[]{:S(2)}) copy-start(bf16[512,256]{1,0:T(8,128)(2,1)} %copy-done.44) | copy-start | bytes 786436
  79.1 10.4 %copy-start.49 = (s32[6]{0:T(128)S(1)}, s32[6]{0:T(128)}, u32[]{:S(2)}) copy-start(s32[6]{0:T(128)} %stack.11.ids) | copy-start | bytes 76
  82.8 6.7 %collective-permute-start.16 = (bf16[256,1024]{1,0:T(8,128)(2,1)}, bf16[256,1024]{1,0:T(8,128)(2,1)S(1)}, u32[]{:S(2)}, u32[]{:S(2)}) collective-permute-start(bf16[256,1024]{1,0:T(8,128)(2,1)} %collective-permute-done.13.refs_4_.refs_8_), channel_id=1, source_target_pairs={{0,1},{1,0},{2,3},{3,2},{4,5},{5,4},{6,7},{7,6},{8,9},{9,8},{10,11... | collective-permute-start | bytes 1572872 | tf_op jit(solution)/shard_map/ppermute | solution.py:45
  83.8 15.5 %collective-permute-start.17 = (bf16[256,1024]{1,0:T(8,128)(2,1)S(1)}, bf16[256,1024]{1,0:T(8,128)(2,1)S(1)}, u32[]{:S(2)}, u32[]{:S(2)}) collective-permute-start(bf16[256,1024]{1,0:T(8,128)(2,1)S(1)} %pad_maximum_fusion.4), channel_id=1, source_target_pairs={{0,8},{4,12},{8,0},{12,4},{16,24},{20,28},{24,16},{28,20},{1,9},{5... | collective-permute-start | bytes 1572872 | tf_op jit(solution)/shard_map/ppermute | solution.py:45
  87.9 64.1 %collective-permute-start.18 = (bf16[512,1024]{1,0:T(8,128)(2,1)S(1)}, bf16[512,1024]{1,0:T(8,128)(2,1)S(1)}, u32[]{:S(2)}, u32[]{:S(2)}) collective-permute-start(bf16[512,1024]{1,0:T(8,128)(2,1)S(1)} %pad_maximum_fusion), channel_id=1, source_target_pairs={{0,4},{4,0},{8,12},{12,8},{16,20},{20,16},{24,28},{28,24},{1,5},{5... | collective-permute-start | bytes 3145736 | tf_op jit(solution)/shard_map/ppermute | solution.py:45
  89.5 67.5 %copy-start.35 = (bf16[256,1024]{1,0:T(8,128)(2,1)}, bf16[256,1024]{1,0:T(8,128)(2,1)S(1)}, u32[]{:S(2)}) copy-start(bf16[256,1024]{1,0:T(8,128)(2,1)S(1)} %collective-permute-done.16.refs_1_.refs_5_) | copy-start | bytes 1572868
  89.5 12.6 %copy-start.70 = (bf16[2560,256]{1,0:T(8,128)(2,1)S(1)}, bf16[2560,256]{1,0:T(8,128)(2,1)}, u32[]{:S(2)}) copy-start(bf16[2560,256]{1,0:T(8,128)(2,1)} %get-tuple-element.223.q_ref) | copy-start | bytes 3932164
  89.5 12.6 %copy-start.71 = (bf16[2560,256]{1,0:T(8,128)(2,1)S(1)}, bf16[2560,256]{1,0:T(8,128)(2,1)}, u32[]{:S(2)}) copy-start(bf16[2560,256]{1,0:T(8,128)(2,1)} %get-tuple-element.234.k_ref) | copy-start | bytes 3932164
  89.5 12.6 %copy-start.72 = (bf16[2560,256]{1,0:T(8,128)(2,1)S(1)}, bf16[2560,256]{1,0:T(8,128)(2,1)}, u32[]{:S(2)}) copy-start(bf16[2560,256]{1,0:T(8,128)(2,1)} %get-tuple-element.235.v_ref) | copy-start | bytes 3932164
  95.1 7.0 %copy-start.33 = (f32[1280,128]{1,0:T(8,128)S(1)}, f32[1280,128]{1,0:T(8,128)}, u32[]{:S(2)}) copy-start(f32[1280,128]{1,0:T(8,128)} %get-tuple-element.214.refs_12_.sine.refs_13_) | copy-start | bytes 1966084
  95.1 7.0 %copy-start.34 = (f32[1280,128]{1,0:T(8,128)S(1)}, f32[1280,128]{1,0:T(8,128)}, u32[]{:S(2)}) copy-start(f32[1280,128]{1,0:T(8,128)} %get-tuple-element.213.refs_11_.cos.refs_12_) | copy-start | bytes 1966084
  95.1 7.0 %copy-start.48 = (s32[1,20,5]{2,1,0:T(8,128)S(1)}, s32[1,20,5]{2,1,0:T(8,128)}, u32[]{:S(2)}) copy-start(s32[1,20,5]{2,1,0:T(8,128)} %tree_table.1.info) | copy-start | bytes 1204
  100.5 51.5 %collective-permute-start.19 = (bf16[512,1024]{1,0:T(8,128)(2,1)S(1)}, bf16[512,1024]{1,0:T(8,128)(2,1)S(1)}, u32[]{:S(2)}, u32[]{:S(2)}) collective-permute-start(bf16[512,1024]{1,0:T(8,128)(2,1)S(1)} %pad_maximum_fusion.1), channel_id=1, source_target_pairs={{0,4},{4,0},{8,12},{12,8},{16,20},{20,16},{24,28},{28,24},{1,5},{5... | collective-permute-start | bytes 3145736 | tf_op jit(solution)/shard_map/ppermute | solution.py:45
  157.0 14.3 %collective-permute-start.20 = (bf16[2,640,1024]{2,1,0:T(8,128)(2,1)S(1)}, bf16[2,640,1024]{2,1,0:T(8,128)(2,1)S(1)}, u32[]{:S(2)}, u32[]{:S(2)}) collective-permute-start(bf16[2,640,1024]{2,1,0:T(8,128)(2,1)S(1)} %get-tuple-element.258), channel_id=1, source_target_pairs={{0,1},{1,0},{2,3},{3,2},{4,5},{5,4},{6,7},{7,6},{8,9},{9,8},{10,11... | collective-permute-start | bytes 7864328 | tf_op jit(solution)/shard_map/ppermute | solution.py:45
  171.8 42.7 %collective-permute-start.21 = (bf16[1,640,1024]{2,1,0:T(8,128)(2,1)S(1)}, bf16[1,640,1024]{2,1,0:T(8,128)(2,1)S(1)}, u32[]{:S(2)}, u32[]{:S(2)}) collective-permute-start(bf16[1,640,1024]{2,1,0:T(8,128)(2,1)S(1)} %add_terms.3), channel_id=1, source_target_pairs={{0,2},{1,3},{2,0},{3,1},{4,6},{5,7},{6,4},{7,5},{8,10},{9,11},{10,... | collective-permute-start | bytes 3932168 | tf_op jit(solution)/shard_map/ppermute | solution.py:45
  173.3 41.1 %collective-permute-start.22 = (bf16[4,128,512]{2,1,0:T(8,128)(2,1)}, bf16[4,128,512]{2,1,0:T(8,128)(2,1)S(1)}, u32[]{:S(2)}, u32[]{:S(2)}) collective-permute-start(bf16[4,128,512]{2,1,0:T(8,128)(2,1)} %get-tuple-element.281), channel_id=1, source_target_pairs={{0,4},{4,0},{8,12},{12,8},{16,20},{20,16},{24,28},{28,24},{1,5},{5... | collective-permute-start | bytes 1572872 | tf_op jit(solution)/shard_map/ppermute | solution.py:45
  173.8 40.6 %collective-permute-start.23 = (bf16[4,128,512]{2,1,0:T(8,128)(2,1)}, bf16[4,128,512]{2,1,0:T(8,128)(2,1)S(1)}, u32[]{:S(2)}, u32[]{:S(2)}) collective-permute-start(bf16[4,128,512]{2,1,0:T(8,128)(2,1)} %get-tuple-element.282), channel_id=1, source_target_pairs={{0,8},{4,12},{8,0},{12,4},{16,24},{20,28},{24,16},{28,20},{1,9},{5... | collective-permute-start | bytes 1572872 | tf_op jit(solution)/shard_map/ppermute | solution.py:45
  214.4 11.7 %copy-start.10 = (bf16[4,128,512]{2,1,0:T(8,128)(2,1)}, bf16[4,128,512]{2,1,0:T(8,128)(2,1)S(1)}, u32[]{:S(2)}) copy-start(bf16[4,128,512]{2,1,0:T(8,128)(2,1)S(1)} %collective-permute-done.22.refs_1_) | copy-start | bytes 1572868
  214.5 11.7 %copy-start.12 = (bf16[4,128,512]{2,1,0:T(8,128)(2,1)}, bf16[4,128,512]{2,1,0:T(8,128)(2,1)S(1)}, u32[]{:S(2)}) copy-start(bf16[4,128,512]{2,1,0:T(8,128)(2,1)S(1)} %collective-permute-done.23.refs_3_.refs_4_.refs_5_) | copy-start | bytes 1572868
  215.7 5.1 %collective-permute-start.24 = (bf16[2,640,1024]{2,1,0:T(8,128)(2,1)}, bf16[2,640,1024]{2,1,0:T(8,128)(2,1)S(1)}, u32[]{:S(2)}, u32[]{:S(2)}) collective-permute-start(bf16[2,640,1024]{2,1,0:T(8,128)(2,1)} %get-tuple-element.285), channel_id=1, source_target_pairs={{0,1},{1,0},{2,3},{3,2},{4,5},{5,4},{6,7},{7,6},{8,9},{9,8},{10,11... | collective-permute-start | bytes 7864328 | tf_op jit(solution)/shard_map/ppermute | solution.py:45
  223.8 33.6 %collective-permute-start.25 = (bf16[1,640,1024]{2,1,0:T(8,128)(2,1)}, bf16[1,640,1024]{2,1,0:T(8,128)(2,1)S(1)}, u32[]{:S(2)}, u32[]{:S(2)}) collective-permute-start(bf16[1,640,1024]{2,1,0:T(8,128)(2,1)} %add_terms.4), channel_id=1, source_target_pairs={{0,2},{1,3},{2,0},{3,1},{4,6},{5,7},{6,4},{7,5},{8,10},{9,11},{10,... | collective-permute-start | bytes 3932168 | tf_op jit(solution)/shard_map/ppermute | solution.py:45
  224.4 30.8 %collective-permute-start.28 = (bf16[4,128,1024]{2,1,0:T(8,128)(2,1)}, bf16[4,128,1024]{2,1,0:T(8,128)(2,1)S(1)}, u32[]{:S(2)}, u32[]{:S(2)}) collective-permute-start(bf16[4,128,1024]{2,1,0:T(8,128)(2,1)} %copy-done.59), channel_id=1, source_target_pairs={{0,4},{4,0},{8,12},{12,8},{16,20},{20,16},{24,28},{28,24},{1,5},{5... | collective-permute-start | bytes 3145736 | tf_op jit(solution)/shard_map/ppermute | solution.py:45
  225.9 30.5 %collective-permute-start.29 = (bf16[4,128,1024]{2,1,0:T(8,128)(2,1)}, bf16[4,128,1024]{2,1,0:T(8,128)(2,1)S(1)}, u32[]{:S(2)}, u32[]{:S(2)}) collective-permute-start(bf16[4,128,1024]{2,1,0:T(8,128)(2,1)} %get-tuple-element.298), channel_id=1, source_target_pairs={{0,8},{4,12},{8,0},{12,4},{16,24},{20,28},{24,16},{28,20},{1,9},{5... | collective-permute-start | bytes 3145736 | tf_op jit(solution)/shard_map/ppermute | solution.py:45
  226.3 27.8 %collective-permute-start.26 = (bf16[2,128,512]{2,1,0:T(8,128)(2,1)S(1)}, bf16[2,128,512]{2,1,0:T(8,128)(2,1)S(1)}, u32[]{:S(2)}, u32[]{:S(2)}) collective-permute-start(bf16[2,128,512]{2,1,0:T(8,128)(2,1)S(1)} %get-tuple-element.295), channel_id=1, source_target_pairs={{0,16},{4,20},{8,24},{12,28},{16,0},{20,4},{24,8},{28,12},{1,17},{... | collective-permute-start | bytes 786440 | tf_op jit(solution)/shard_map/ppermute | solution.py:45
  228.0 27.1 %collective-permute-start.27 = (bf16[2,128,512]{2,1,0:T(8,128)(2,1)S(1)}, bf16[2,128,512]{2,1,0:T(8,128)(2,1)S(1)}, u32[]{:S(2)}, u32[]{:S(2)}) collective-permute-start(bf16[2,128,512]{2,1,0:T(8,128)(2,1)S(1)} %get-tuple-element.296), channel_id=1, source_target_pairs={{0,4},{4,0},{8,12},{12,8},{16,20},{20,16},{24,28},{28,24},{1,5},{5... | collective-permute-start | bytes 786440 | tf_op jit(solution)/shard_map/ppermute | solution.py:45
  258.4 7.0 %copy-start.13 = (bf16[4,128,512]{2,1,0:T(8,128)(2,1)S(1)}, bf16[4,128,512]{2,1,0:T(8,128)(2,1)}, u32[]{:S(2)}) copy-start(bf16[4,128,512]{2,1,0:T(8,128)(2,1)} %copy-done.12) | copy-start | bytes 1572868
  258.4 5.0 %collective-permute-start.30 = (bf16[2,640,1024]{2,1,0:T(8,128)(2,1)S(1)}, bf16[2,640,1024]{2,1,0:T(8,128)(2,1)S(1)}, u32[]{:S(2)}, u32[]{:S(2)}) collective-permute-start(bf16[2,640,1024]{2,1,0:T(8,128)(2,1)S(1)} %get-tuple-element.300), channel_id=1, source_target_pairs={{0,1},{1,0},{2,3},{3,2},{4,5},{5,4},{6,7},{7,6},{8,9},{9,8},{10,11... | collective-permute-start | bytes 7864328 | tf_op jit(solution)/shard_map/ppermute | solution.py:45
  263.8 38.2 %collective-permute-start.38 = (bf16[1,640,1024]{2,1,0:T(8,128)(2,1)S(1)}, bf16[1,640,1024]{2,1,0:T(8,128)(2,1)S(1)}, u32[]{:S(2)}, u32[]{:S(2)}) collective-permute-start(bf16[1,640,1024]{2,1,0:T(8,128)(2,1)S(1)} %add_terms.5), channel_id=1, source_target_pairs={{0,2},{1,3},{2,0},{3,1},{4,6},{5,7},{6,4},{7,5},{8,10},{9,11},{10,... | collective-permute-start | bytes 3932168 | tf_op jit(solution)/shard_map/ppermute | solution.py:45
  265.7 18.7 %collective-permute-start.33 = (bf16[2,128,1024]{2,1,0:T(8,128)(2,1)S(1)}, bf16[2,128,1024]{2,1,0:T(8,128)(2,1)S(1)}, u32[]{:S(2)}, u32[]{:S(2)}) collective-permute-start(bf16[2,128,1024]{2,1,0:T(8,128)(2,1)S(1)} %get-tuple-element.317), channel_id=1, source_target_pairs={{0,8},{4,12},{8,0},{12,4},{16,24},{20,28},{24,16},{28,20},{1,9},{5... | collective-permute-start | bytes 1572872 | tf_op jit(solution)/shard_map/ppermute | solution.py:45
  268.3 16.2 %collective-permute-start.34 = (bf16[2,128,1024]{2,1,0:T(8,128)(2,1)S(1)}, bf16[2,128,1024]{2,1,0:T(8,128)(2,1)S(1)}, u32[]{:S(2)}, u32[]{:S(2)}) collective-permute-start(bf16[2,128,1024]{2,1,0:T(8,128)(2,1)S(1)} %get-tuple-element.318), channel_id=1, source_target_pairs={{0,4},{4,0},{8,12},{12,8},{16,20},{20,16},{24,28},{28,24},{1,5},{5... | collective-permute-start | bytes 1572872 | tf_op jit(solution)/shard_map/ppermute | solution.py:45
  268.8 14.2 %collective-permute-start.35 = (bf16[1,128,512]{2,1,0:T(8,128)(2,1)S(1)}, bf16[1,128,512]{2,1,0:T(8,128)(2,1)S(1)}, u32[]{:S(2)}, u32[]{:S(2)}) collective-permute-start(bf16[1,128,512]{2,1,0:T(8,128)(2,1)S(1)} %get-tuple-element.319), channel_id=1, source_target_pairs={{0,16},{4,20},{8,24},{12,28},{16,0},{20,4},{24,8},{28,12},{1,17},{... | collective-permute-start | bytes 393224 | tf_op jit(solution)/shard_map/ppermute | solution.py:45
  272.7 1.3 collective-permute-start.31
  274.0 10.5 %collective-permute-start.32 = (f32[16,1024]{1,0:T(8,128)S(1)}, f32[16,1024]{1,0:T(8,128)S(1)}, u32[]{:S(2)}, u32[]{:S(2)}) collective-permute-start(f32[16,1024]{1,0:T(8,128)S(1)} %add.41), channel_id=1, source_target_pairs={{0,16},{4,20},{8,24},{12,28},{16,0},{20,4},{24,8},{28,12},{1,17},{... | collective-permute-start | bytes 196616 | tf_op jit(solution)/shard_map/ppermute | solution.py:45
  284.7 20.4 %collective-permute-start.41 = (bf16[1,128,1024]{2,1,0:T(8,128)(2,1)S(1)}, bf16[1,128,1024]{2,1,0:T(8,128)(2,1)S(1)}, u32[]{:S(2)}, u32[]{:S(2)}) collective-permute-start(bf16[1,128,1024]{2,1,0:T(8,128)(2,1)S(1)} %get-tuple-element.333), channel_id=1, source_target_pairs={{0,16},{4,20},{8,24},{12,28},{16,0},{20,4},{24,8},{28,12},{1,17},{... | collective-permute-start | bytes 786440 | tf_op jit(solution)/shard_map/ppermute | solution.py:45
  287.4 22.6 %collective-permute-start.42 = (bf16[1,128,1024]{2,1,0:T(8,128)(2,1)S(1)}, bf16[1,128,1024]{2,1,0:T(8,128)(2,1)S(1)}, u32[]{:S(2)}, u32[]{:S(2)}) collective-permute-start(bf16[1,128,1024]{2,1,0:T(8,128)(2,1)S(1)} %get-tuple-element.334), channel_id=1, source_target_pairs={{0,16},{4,20},{8,24},{12,28},{16,0},{20,4},{24,8},{28,12},{1,17},{... | collective-permute-start | bytes 786440 | tf_op jit(solution)/shard_map/ppermute | solution.py:45
  287.7 4.3 %collective-permute-start.36 = (f32[16,1024]{1,0:T(8,128)S(1)}, f32[16,1024]{1,0:T(8,128)S(1)}, u32[]{:S(2)}, u32[]{:S(2)}) collective-permute-start(f32[16,1024]{1,0:T(8,128)S(1)} %add.42), channel_id=1, source_target_pairs={{0,4},{4,0},{8,12},{12,8},{16,20},{20,16},{24,28},{28,24},{1,5},{5... | collective-permute-start | bytes 196616 | tf_op jit(solution)/shard_map/ppermute | solution.py:45
  288.2 14.4 %collective-permute-start.40 = (bf16[1,128,512]{2,1,0:T(8,128)(2,1)S(1)}, bf16[1,128,512]{2,1,0:T(8,128)(2,1)S(1)}, u32[]{:S(2)}, u32[]{:S(2)}) collective-permute-start(bf16[1,128,512]{2,1,0:T(8,128)(2,1)S(1)} %get-tuple-element.329), channel_id=1, source_target_pairs={{0,8},{4,12},{8,0},{12,4},{16,24},{20,28},{24,16},{28,20},{1,9},{5... | collective-permute-start | bytes 393224 | tf_op jit(solution)/shard_map/ppermute | solution.py:45
  291.9 10.0 %collective-permute-start.37 = (f32[16,1024]{1,0:T(8,128)S(1)}, f32[16,1024]{1,0:T(8,128)S(1)}, u32[]{:S(2)}, u32[]{:S(2)}) collective-permute-start(f32[16,1024]{1,0:T(8,128)S(1)} %add.43), channel_id=1, source_target_pairs={{0,8},{4,12},{8,0},{12,4},{16,24},{20,28},{24,16},{28,20},{1,9},{5... | collective-permute-start | bytes 196616 | tf_op jit(solution)/shard_map/ppermute | solution.py:45
  302.0 12.1 %collective-permute-start.39 = (f32[16,1024]{1,0:T(8,128)S(1)}, f32[16,1024]{1,0:T(8,128)S(1)}, u32[]{:S(2)}, u32[]{:S(2)}) collective-permute-start(f32[16,1024]{1,0:T(8,128)S(1)} %add.44), channel_id=1, source_target_pairs={{0,2},{1,3},{2,0},{3,1},{4,6},{5,7},{6,4},{7,5},{8,10},{9,11},{10,... | collective-permute-start | bytes 196616 | tf_op jit(solution)/shard_map/ppermute | solution.py:45
  303.5 7.7 %copy-start.15 = (f32[640,1024]{1,0:T(8,128)S(1)}, f32[640,1024]{1,0:T(8,128)}, u32[]{:S(2)}) copy-start(f32[640,1024]{1,0:T(8,128)} %copy-done.14) | copy-start | bytes 7864324
  303.5 7.7 %copy-start.43 = (f32[640,1]{1,0:T(8,128)S(1)}, f32[640,1]{1,0:T(8,128)}, u32[]{:S(2)}) copy-start(f32[640,1]{1,0:T(8,128)} %copy-done.42) | copy-start | bytes 7684
  (54 other events, 225.2 us)

commit v12 on v11

--- a/solution.py
+++ b/solution.py
@@ -211,9 +211,9 @@
 
 
 def call(
-    kernel, name, grid, prefetch, operands, specs, outs, out_specs, scratch, flops, extra=0, room=12
+    kernel, name, grid, prefetch, operands, specs, outs, out_specs, scratch, flops, extra=0, room=12, light=False
 ):
-    size = sum(x.size * x.dtype.itemsize for x in list(operands) + list(outs))
+    size = 0 if light else sum(x.size * x.dtype.itemsize for x in [*operands, *outs])
     return pl.pallas_call(
         kernel,
         grid_spec=pltpu.PrefetchScalarGridSpec(
@@ -320,6 +320,7 @@
         [step_block(block, model), step_block(block, model), step_block(block, 1)],
         [],
         rows * model * 8,
+        room=62,
     )
 
 
@@ -1007,7 +1008,8 @@
         [shaped(rows, model, dtype=f32)],
         [step_block(block, model)],
         [],
-        rows * model * 12,
+        0,
+        light=True,
     )[0]
 
 
@@ -1259,9 +1261,10 @@
         sums = sums + swap(sums, "dp", bit)
     sums, back_parts.got = tie(sums, back_parts.got)
     back_parts.add()
+    stream_grad = finish_grad(out_grad, normalized, inv_std, back_parts.terms)
+    sums, stream_grad = tie(sums, stream_grad)
     for bit in tensor_bits[1:]:
         sums = sums + swap(sums, "tensor", bit)
-    stream_grad = finish_grad(out_grad, normalized, inv_std, back_parts.terms)
 
     fc_weight_grad, out_weight_grad = finish_mlp_weights(*[x.finish() for x in mlp_sums])
     for parts in qkv_sums:

time: 318 us -> 314 us (0.987)
  other arithmetic: 13.2 us -> 8.77 us
  Pallas kernels: 154 us -> 158 us
    concatenate x8, other arithmetic: 8.75 us -> 4.3 us  [double(): jnp.concatenate(self.arrays, axis=0)]
    pallas_call x19, Pallas kernels: 152 us -> 156 us  [call(): pl.pallas_call(kernel, grid_spec=pltpu.PrefetchScalarGridSpec(num_scalar_...]
    unnamed x153 -> x161, local copies, waits for them, and re-layouts: 18.8 us -> 18.3 us
  transfers between devices with their start and end apart: 43 -> 43, of which waited for: 20 -> 20; matrix products, arithmetic and copies ran while one was open for 6% -> 4% of each run, Pallas kernels for 47% -> 48%
where the time goes in v12:
time: 314 us; the launch traced here: 313 us
  Pallas kernels  158 us (50%)
  waiting for transfers between devices  69.8 us (22%)
  starting transfers between devices  51.9 us (17%)
  local copies, waits for them, and re-layouts  23.3 us (7%)
  other arithmetic  8.77 us (3%)
    pallas_call x19, Pallas kernels, call(): pl.pallas_call(kernel, grid_spec=pltpu.PrefetchScalarGridSpec(num_scalar_...  156 us
    ppermute x43, waiting for transfers between devices, swap(): return lax.ppermute(block, axis, [(i, i ^ bit) for i in range(size)])  69.8 us
    ppermute x43, starting transfers between devices, swap(): return lax.ppermute(block, axis, [(i, i ^ bit) for i in range(size)])  51.9 us
    unnamed x161, local copies, waits for them, and re-layouts  18.3 us
  transfers between devices with their start and end apart: 43, of which 20 were waited for; matrix products, arithmetic and copies ran while one was open for 4% of the time, Pallas kernels for 48%

profile of v12, /device:TPU:0, one launch (start us, length us, event | category | flops | bytes accessed | tf_op | source)
XLA Modules:
  0.0 312.9 jit_solution(12073953567414204801)
XLA Ops:
  1.2 4.7 %normalize.1 = (bf16[640,1024]{1,0:T(8,128)(2,1)}, f32[640,1024]{1,0:T(8,128)}, f32[640,1]{1,0:T(8,128)}) custom-call(f32[640,1024]{1,0:T(8,128)} %stream_ref.2), custom_call_target="tpu_custom_call" | custom-call | flops 5242880 | bytes 6556160 | tf_op jit(solution)/shard_map/normalize/pallas_call | solution.py:217
  6.0 2.9 collective-permute-start.4
  8.9 1.0 copy-done.36
  9.9 1.0 copy-done.37
  13.1 2.7 collective-permute-start.1
  15.8 1.5 collective-permute-start.2
  19.1 2.0 tree_table.1.info
  21.1 3.9 %collective-permute-done.1.refs_5_ = bf16[128,768]{1,0:T(8,128)(2,1)S(1)} collective-permute-done((bf16[128,768]{1,0:T(8,128)(2,1)S(1)}, bf16[128,768]{1,0:T(8,128)(2,1)S(1)}, u32[]{:S(2)}, u32[]{:S(2)}) %collective-permute-start.1) | collective-permute-done | bytes 196640 | tf_op jit(solution)/shard_map/ppermute | solution.py:45
  25.7 3.4 %collective-permute-start.6 = (bf16[256,256]{1,0:T(8,128)(2,1)S(1)}, bf16[256,256]{1,0:T(8,128)(2,1)S(1)}, u32[]{:S(2)}, u32[]{:S(2)}) collective-permute-start(bf16[256,256]{1,0:T(8,128)(2,1)S(1)} %pad_maximum_fusion.7), channel_id=1, source_target_pairs={{0,16},{4,20},{8,24},{12,28},{16,0},{20,4},{24,8},{28,12},{1,17},{... | collective-permute-start | bytes 393224 | tf_op jit(solution)/shard_map/ppermute | solution.py:45
  29.2 3.8 %fusion = (f32[1280,128]{1,0:T(8,128)}, f32[1280,128]{1,0:T(8,128)}) fusion(s32[128]{0:T(128)S(1)} %get-tuple-element.348, s32[128]{0:T(128)S(1)} %get-tuple-element.349, pred[128]{0:T(512)(128)(4,1)S(1)} %compare_and_fusion, f32[1280]{0:T(1024)S(1)} %convert_add_fusion), kind=kLoop, calls=%fused_computation.9 | loop fusion | flops 3112960 | bytes 1316992 | tf_op jit(solution)/shard_map/jit(_where)/select_n | solution.py:1061
  34.2 4.0 %collective-permute-done.4.refs_2_ = bf16[640,1024]{1,0:T(8,128)(2,1)} collective-permute-done((bf16[640,1024]{1,0:T(8,128)(2,1)}, bf16[640,1024]{1,0:T(8,128)(2,1)}, u32[]{:S(2)}, u32[]{:S(2)}) %collective-permute-start.4) | collective-permute-done | bytes 1310752 | tf_op jit(solution)/shard_map/ppermute | solution.py:45
  38.3 1.8 collective-permute-start.8
  40.2 1.6 collective-permute-start.9
  41.8 2.6 collective-permute-start.11
  44.4 1.6 collective-permute-start.10
  46.0 10.4 %collective-permute-done.11.refs_11_.refs_9_ = bf16[128,1024]{1,0:T(8,128)(2,1)S(1)} collective-permute-done((bf16[128,1024]{1,0:T(8,128)(2,1)S(1)}, bf16[128,1024]{1,0:T(8,128)(2,1)S(1)}, u32[]{:S(2)}, u32[]{:S(2)}) %collective-permute-start.11) | collective-permute-done | bytes 262176 | tf_op jit(solution)/shard_map/ppermute | solution.py:45
  56.6 2.0 collective-permute-done.8.refs_3_.refs_7_
  58.6 1.3 collective-permute-done.9.refs_7_
  61.4 2.7 collective-permute-start.14
  64.7 1.7 collective-permute-start.15
  66.4 11.3 %project_qkv.1 = (bf16[2560,256]{1,0:T(8,128)(2,1)}, bf16[2560,256]{1,0:T(8,128)(2,1)}, bf16[2560,256]{1,0:T(8,128)(2,1)}) custom-call(s32[6]{0:T(128)} %stack.11.ids, s32[1,20,5]{2,1,0:T(8,128)} %tree_table.1.info, bf16[640,1024]{1,0:T(8,128)(2,1)} %copy-done.54, bf16[640,1024]{1,0:T(8,128)(2,1)} %collective-permute-done.3.refs_1_, ...), custom_call_target="tpu_custom_call" | custom-call | flops 4026531840 | bytes 12079104 | tf_op jit(solution)/shard_map/project_qkv/pallas_call | solution.py:217
  77.7 3.7 %collective-permute-done.15.refs_15_ = bf16[128,1024]{1,0:T(8,128)(2,1)} collective-permute-done((bf16[128,1024]{1,0:T(8,128)(2,1)S(1)}, bf16[128,1024]{1,0:T(8,128)(2,1)}, u32[]{:S(2)}, u32[]{:S(2)}) %collective-permute-start.15) | collective-permute-done | bytes 262176 | tf_op jit(solution)/shard_map/ppermute | solution.py:45
  83.3 1.8 collective-permute-start.17
  85.1 1.2 pad_maximum_fusion
  86.3 1.6 collective-permute-start.18
  87.9 5.4 %project_grad.1.do_ref = bf16[2560,256]{1,0:T(8,128)(2,1)S(1)} custom-call(s32[6]{0:T(128)S(1)} %copy-done.49, bf16[384,1024]{1,0:T(8,128)(2,1)} %collective-permute-done.12.refs_0_.refs_4_, bf16[256,1024]{1,0:T(8,128)(2,1)S(1)} %collective-permute-done.16.refs_1_.refs_5_, bf16[640,1024]{1,0:T(8,128)(2,1)} %collective-permute-done.refs_2_.refs_6_, ...), custom_call_target="tpu_custom_call" | custom-call | flops 1342177280 | bytes 7077888 | tf_op jit(solution)/shard_map/project_grad/pallas_call | solution.py:217
  93.4 4.3 %collective-permute-done.17.refs_16_ = bf16[256,1024]{1,0:T(8,128)(2,1)S(1)} collective-permute-done((bf16[256,1024]{1,0:T(8,128)(2,1)S(1)}, bf16[256,1024]{1,0:T(8,128)(2,1)S(1)}, u32[]{:S(2)}, u32[]{:S(2)}) %collective-permute-start.17) | collective-permute-done | bytes 524320 | tf_op jit(solution)/shard_map/ppermute | solution.py:45
  97.7 1.2 pad_maximum_fusion.1
  98.9 1.6 collective-permute-start.19
  100.5 49.9 %attention.1 = (bf16[2560,256]{1,0:T(8,128)(2,1)S(1)}, bf16[2560,256]{1,0:T(8,128)(2,1)S(1)}, bf16[2560,256]{1,0:T(8,128)(2,1)S(1)}, bf16[2560,256]{1,0:T(8,128)(2,1)S(1)}) custom-call(s32[1,20,5]{2,1,0:T(8,128)S(1)} %copy-done.48, bf16[2560,256]{1,0:T(8,128)(2,1)S(1)} %copy-done.72, bf16[2560,256]{1,0:T(8,128)(2,1)S(1)} %project_grad.1.do_ref, ...), custom_call_target="tpu_custom_call" | custom-call | flops 31406948352 | bytes 11796480 | tf_op jit(solution)/shard_map/attention/pallas_call | solution.py:217
  151.5 4.0 %project_context.1 = (bf16[2,640,1024]{2,1,0:T(8,128)(2,1)S(1)}, bf16[2,640,1024]{2,1,0:T(8,128)(2,1)S(1)}) custom-call(s32[6]{0:T(128)S(1)} %copy-done.49, bf16[2560,256]{1,0:T(8,128)(2,1)S(1)} %get-tuple-element.250.ctx.ctx_ref, bf16[128,256]{1,0:T(8,128)(2,1)S(1)} %copy-done.29, bf16[128,256]{1,0:T(8,128)(2,1)S(1)} %copy-done.31, ...), custom_call_target="tpu_custom_call" | custom-call | flops 1342177280 | bytes 7077888 | tf_op jit(solution)/shard_map/project_context/pallas_call | solution.py:217
  155.6 12.4 %attention_weights.1 = (bf16[2560,768]{1,0:T(8,128)(2,1)S(1)}, f32[8,768]{1,0:T(8,128)S(1)}, bf16[4,128,512]{2,1,0:T(8,128)(2,1)}, bf16[4,128,512]{2,1,0:T(8,128...) custom-call(s32[6]{0:T(128)S(1)} %copy-done.49, s32[1,20,5]{2,1,0:T(8,128)S(1)} %copy-done.48, ...), custom_call_target="tpu_custom_call" | custom-call | flops 5368709120 | bytes 23101440 | tf_op jit(solution)/shard_map/attention_weights/pallas_call | solution.py:217
  168.1 1.9 copy-done.70
  170.1 1.2 add_terms.3
  171.3 1.4 collective-permute-start.21
  173.2 1.7 collective-permute-start.23
  175.1 38.8 %mlp.1 = (bf16[2,640,1024]{2,1,0:T(8,128)(2,1)}, bf16[2,640,1024]{2,1,0:T(8,128)(2,1)}, bf16[2560,1024]{1,0:T(8,128)(2,1)}, f32[8,1024]{1,0:T(8,128)S(1)}, bf16[...) custom-call(s32[6]{0:T(128)S(1)} %copy-done.49, ...), custom_call_target="tpu_custom_call" | custom-call | flops 26843545600 | bytes 29417472 | tf_op jit(solution)/shard_map/mlp/pallas_call | solution.py:217
  216.4 5.1 %collective-permute-done.24.refs_1_.refs_4_ = bf16[2,640,1024]{2,1,0:T(8,128)(2,1)S(1)} collective-permute-done((bf16[2,640,1024]{2,1,0:T(8,128)(2,1)}, bf16[2,640,1024]{2,1,0:T(8,128)(2,1)S(1)}, u32[]{:S(2)}, u32[]{:S(2)}) %collective-permute-start.24) | collective-permute-done | bytes 2621472 | tf_op jit(solution)/shard_map/ppermute | solution.py:45
  221.6 1.7 copy-done.2
  223.3 1.2 add_terms.4
  225.2 1.5 collective-permute-start.28
  227.9 2.7 collective-permute-start.26
  231.2 2.1 copy-done.71
  233.3 2.5 copy-done.75
  235.8 15.9 %norm_backward.1 = (bf16[2,640,1024]{2,1,0:T(8,128)(2,1)S(1)}, bf16[2,640,1024]{2,1,0:T(8,128)(2,1)S(1)}, f32[8,1024]{1,0:T(8,128)S(1)}) custom-call(s32[6]{0:T(128)S(1)} %copy-done.49, bf16[2560,768]{1,0:T(8,128)(2,1)S(1)} %copy-done.71, bf16[2560,1024]{1,0:T(8,128)(2,1)S(1)} %copy-done.75, bf16[640,1024]{1,0:T(8,128)(2,1)S(1)} %copy-done.57, ...), custom_call_target="tpu_custom_call" | custom-call | flops 9395240960 | bytes 23371776 | tf_op jit(solution)/shard_map/norm_backward/pallas_call | solution.py:217
  251.7 3.2 %collective-permute-done.26.refs_2_ = bf16[2,128,512]{2,1,0:T(8,128)(2,1)S(1)} collective-permute-done((bf16[2,128,512]{2,1,0:T(8,128)(2,1)}, bf16[2,128,512]{2,1,0:T(8,128)(2,1)S(1)}, u32[]{:S(2)}, u32[]{:S(2)}) %collective-permute-start.26) | collective-permute-done | bytes 262176 | tf_op jit(solution)/shard_map/ppermute | solution.py:45
  254.9 1.0 collective-permute-done.27.refs_5_.refs_6_
  256.0 1.0 collective-permute-done.29.refs_9_.refs_4_.refs_5_
  257.0 1.1 copy-done.14
  258.1 4.9 %collective-permute-done.30.refs_1_ = bf16[2,640,1024]{2,1,0:T(8,128)(2,1)S(1)} collective-permute-done((bf16[2,640,1024]{2,1,0:T(8,128)(2,1)S(1)}, bf16[2,640,1024]{2,1,0:T(8,128)(2,1)S(1)}, u32[]{:S(2)}, u32[]{:S(2)}) %collective-permute-start.30) | collective-permute-done | bytes 2621472 | tf_op jit(solution)/shard_map/ppermute | solution.py:45
  263.4 1.5 collective-permute-start.38
  265.2 1.6 collective-permute-start.33
  267.9 3.7 %finish_output.1 = (f32[640,1024]{1,0:T(8,128)}, f32[16,1024]{1,0:T(8,128)S(1)}) custom-call(s32[6]{0:T(128)S(1)} %copy-done.49, f32[640,1024]{1,0:T(8,128)S(1)} %copy-done.4, bf16[640,1024]{1,0:T(8,128)(2,1)S(1)} %copy-done.1, bf16[2,640,1024]{2,1,0:T(8,128)(2,1)S(1)} %get-tuple-element.262.refs_0_, ...), custom_call_target="tpu_custom_call" | custom-call | flops 10485760 | bytes 19824640 | tf_op jit(solution)/shard_map/finish_output/pallas_call | solution.py:217
  271.6 1.3 collective-permute-done.31
  272.9 2.4 collective-permute-start.32
  275.3 6.2 %collective-permute-done.35.refs_7_ = bf16[1,128,512]{2,1,0:T(8,128)(2,1)S(1)} collective-permute-done((bf16[1,128,512]{2,1,0:T(8,128)(2,1)S(1)}, bf16[1,128,512]{2,1,0:T(8,128)(2,1)S(1)}, u32[]{:S(2)}, u32[]{:S(2)}) %collective-permute-start.35) | collective-permute-done | bytes 131104 | tf_op jit(solution)/shard_map/ppermute | solution.py:45
  281.5 1.7 collective-permute-done.33.refs_2_
  283.4 2.5 collective-permute-start.41
  286.9 3.7 %collective-permute-done.36 = f32[16,1024]{1,0:T(8,128)S(1)} collective-permute-done((f32[16,1024]{1,0:T(8,128)S(1)}, f32[16,1024]{1,0:T(8,128)S(1)}, u32[]{:S(2)}, u32[]{:S(2)}) %collective-permute-start.36) | collective-permute-done | bytes 65568 | tf_op jit(solution)/shard_map/ppermute | solution.py:45
  290.7 1.3 collective-permute-start.37
  292.8 6.3 %collective-permute-done.37 = f32[16,1024]{1,0:T(8,128)S(1)} collective-permute-done((f32[16,1024]{1,0:T(8,128)S(1)}, f32[16,1024]{1,0:T(8,128)S(1)}, u32[]{:S(2)}, u32[]{:S(2)}) %collective-permute-start.37) | collective-permute-done | bytes 65568 | tf_op jit(solution)/shard_map/ppermute | solution.py:45
  299.1 2.9 finish_grad.1
  303.7 4.7 %collective-permute-done.42.refs_7_ = bf16[1,128,1024]{2,1,0:T(8,128)(2,1)S(1)} collective-permute-done((bf16[1,128,1024]{2,1,0:T(8,128)(2,1)S(1)}, bf16[1,128,1024]{2,1,0:T(8,128)(2,1)S(1)}, u32[]{:S(2)}, u32[]{:S(2)}) %collective-permute-start.42) | collective-permute-done | bytes 262176 | tf_op jit(solution)/shard_map/ppermute | solution.py:45
  308.4 1.2 finish_mlp_weights.1
  (232 shorter events, 26.2 us)
Async XLA Ops:
  0.6 16.7 %copy-start = (bf16[640,1024]{1,0:T(8,128)(2,1)S(1)}, bf16[640,1024]{1,0:T(8,128)(2,1)}, u32[]{:S(2)}) copy-start(bf16[640,1024]{1,0:T(8,128)(2,1)} %grad_ref.3) | copy-start | bytes 3932164
  0.7 24.3 %collective-permute-start = (bf16[640,1024]{1,0:T(8,128)(2,1)}, bf16[640,1024]{1,0:T(8,128)(2,1)}, u32[]{:S(2)}, u32[]{:S(2)}) collective-permute-start(bf16[640,1024]{1,0:T(8,128)(2,1)} %grad_ref.3), channel_id=1, source_target_pairs={{0,1},{1,0},{2,3},{3,2},{4,5},{5,4},{6,7},{7,6},{8,9},{9,8},{10,11... | collective-permute-start | bytes 3932168 | tf_op jit(solution)/shard_map/ppermute | solution.py:45
  5.9 28.3 %collective-permute-start.3 = (bf16[640,1024]{1,0:T(8,128)(2,1)}, bf16[640,1024]{1,0:T(8,128)(2,1)}, u32[]{:S(2)}, u32[]{:S(2)}) collective-permute-start(bf16[640,1024]{1,0:T(8,128)(2,1)} %get-tuple-element.209.refs_3_), channel_id=1, source_target_pairs={{0,1},{1,0},{2,3},{3,2},{4,5},{5,4},{6,7},{7,6},{8,9},{9,8},{10,11... | collective-permute-start | bytes 3932168 | tf_op jit(solution)/shard_map/ppermute | solution.py:45
  6.0 32.2 %collective-permute-start.4 = (bf16[640,1024]{1,0:T(8,128)(2,1)}, bf16[640,1024]{1,0:T(8,128)(2,1)}, u32[]{:S(2)}, u32[]{:S(2)}) collective-permute-start(bf16[640,1024]{1,0:T(8,128)(2,1)} %get-tuple-element.209.refs_3_), channel_id=1, source_target_pairs={{0,2},{1,3},{2,0},{3,1},{4,6},{5,7},{6,4},{7,5},{8,10},{9,11},{10,... | collective-permute-start | bytes 3932168 | tf_op jit(solution)/shard_map/ppermute | solution.py:45
  13.1 27.0 %copy-start.22 = (bf16[128,768]{1,0:T(8,128)(2,1)}, bf16[128,768]{1,0:T(8,128)(2,1)S(1)}, u32[]{:S(2)}) copy-start(bf16[128,768]{1,0:T(8,128)(2,1)S(1)} %get-tuple-element.210.refs_4_) | copy-start | bytes 589828
  13.1 31.3 %copy-start.28 = (bf16[128,256]{1,0:T(8,128)(2,1)}, bf16[128,256]{1,0:T(8,128)(2,1)S(1)}, u32[]{:S(2)}) copy-start(bf16[128,256]{1,0:T(8,128)(2,1)S(1)} %get-tuple-element.229.refs_6_.refs_0_) | copy-start | bytes 196612
  13.1 72.0 %copy-start.16 = (bf16[128,1024]{1,0:T(8,128)(2,1)}, bf16[128,1024]{1,0:T(8,128)(2,1)S(1)}, u32[]{:S(2)}) copy-start(bf16[128,1024]{1,0:T(8,128)(2,1)S(1)} %get-tuple-element.265.refs_10_.refs_8_) | copy-start | bytes 786436
  13.1 84.6 %copy-start.18 = (bf16[128,1024]{1,0:T(8,128)(2,1)}, bf16[128,1024]{1,0:T(8,128)(2,1)S(1)}, u32[]{:S(2)}) copy-start(bf16[128,1024]{1,0:T(8,128)(2,1)S(1)} %get-tuple-element.269.refs_14_) | copy-start | bytes 786436
  13.1 11.8 %collective-permute-start.1 = (bf16[128,768]{1,0:T(8,128)(2,1)S(1)}, bf16[128,768]{1,0:T(8,128)(2,1)S(1)}, u32[]{:S(2)}, u32[]{:S(2)}) collective-permute-start(bf16[128,768]{1,0:T(8,128)(2,1)S(1)} %get-tuple-element.210.refs_4_), channel_id=1, source_target_pairs={{0,16},{4,20},{8,24},{12,28},{16,0},{20,4},{24,8},{28,12},{1,17},{... | collective-permute-start | bytes 589832 | tf_op jit(solution)/shard_map/ppermute | solution.py:45
  15.8 5.3 %collective-permute-start.2 = (bf16[128,256]{1,0:T(8,128)(2,1)S(1)}, bf16[128,256]{1,0:T(8,128)(2,1)S(1)}, u32[]{:S(2)}, u32[]{:S(2)}) collective-permute-start(bf16[128,256]{1,0:T(8,128)(2,1)S(1)} %get-tuple-element.229.refs_6_.refs_0_), channel_id=1, source_target_pairs={{0,4},{4,0},{8,12},{12,8},{16,20},{20,16},{24,28},{28,24},{1,5},{5... | collective-permute-start | bytes 196616 | tf_op jit(solution)/shard_map/ppermute | solution.py:45
  18.2 14.7 %copy-start.78 = (f32[3072]{0:T(1024)S(1)}, f32[3072]{0:T(1024)}, u32[]{:S(2)}) copy-start(f32[3072]{0:T(1024)} %param.24) | copy-start | bytes 36868
  18.2 15.3 %copy-start.77 = (f32[4096]{0:T(1024)S(1)}, f32[4096]{0:T(1024)}, u32[]{:S(2)}) copy-start(f32[4096]{0:T(1024)} %param.28) | copy-start | bytes 49156
  21.1 23.3 %copy-start.30 = (bf16[128,256]{1,0:T(8,128)(2,1)}, bf16[128,256]{1,0:T(8,128)(2,1)S(1)}, u32[]{:S(2)}) copy-start(bf16[128,256]{1,0:T(8,128)(2,1)S(1)} %collective-permute-done.2.refs_7_.refs_1_) | copy-start | bytes 196612
  24.9 19.4 %copy-start.24 = (bf16[128,768]{1,0:T(8,128)(2,1)}, bf16[128,768]{1,0:T(8,128)(2,1)S(1)}, u32[]{:S(2)}) copy-start(bf16[128,768]{1,0:T(8,128)(2,1)S(1)} %collective-permute-done.1.refs_5_) | copy-start | bytes 589828
  25.0 13.2 %collective-permute-start.5 = (bf16[256,768]{1,0:T(8,128)(2,1)S(1)}, bf16[256,768]{1,0:T(8,128)(2,1)S(1)}, u32[]{:S(2)}, u32[]{:S(2)}) collective-permute-start(bf16[256,768]{1,0:T(8,128)(2,1)S(1)} %pad_maximum_fusion.5), channel_id=1, source_target_pairs={{0,8},{4,12},{8,0},{12,4},{16,24},{20,28},{24,16},{28,20},{1,9},{5... | collective-permute-start | bytes 1179656 | tf_op jit(solution)/shard_map/ppermute | solution.py:45
  25.7 12.5 %collective-permute-start.6 = (bf16[256,256]{1,0:T(8,128)(2,1)S(1)}, bf16[256,256]{1,0:T(8,128)(2,1)S(1)}, u32[]{:S(2)}, u32[]{:S(2)}) collective-permute-start(bf16[256,256]{1,0:T(8,128)(2,1)S(1)} %pad_maximum_fusion.7), channel_id=1, source_target_pairs={{0,16},{4,20},{8,24},{12,28},{16,0},{20,4},{24,8},{28,12},{1,17},{... | collective-permute-start | bytes 393224 | tf_op jit(solution)/shard_map/ppermute | solution.py:45
  38.2 25.9 %copy-start.32 = (bf16[256,256]{1,0:T(8,128)(2,1)}, bf16[256,256]{1,0:T(8,128)(2,1)S(1)}, u32[]{:S(2)}) copy-start(bf16[256,256]{1,0:T(8,128)(2,1)S(1)} %collective-permute-done.6.refs_8_.refs_2_) | copy-start | bytes 393220
  38.2 26.5 %copy-start.41 = (bf16[256,768]{1,0:T(8,128)(2,1)}, bf16[256,768]{1,0:T(8,128)(2,1)S(1)}, u32[]{:S(2)}) copy-start(bf16[256,768]{1,0:T(8,128)(2,1)S(1)} %collective-permute-done.5.refs_6_) | copy-start | bytes 1179652
  38.2 21.6 %collective-permute-start.7 = (bf16[640,1024]{1,0:T(8,128)(2,1)}, bf16[640,1024]{1,0:T(8,128)(2,1)S(1)}, u32[]{:S(2)}, u32[]{:S(2)}) collective-permute-start(bf16[640,1024]{1,0:T(8,128)(2,1)} %collective-permute-done.4.refs_2_), channel_id=1, source_target_pairs={{0,1},{1,0},{2,3},{3,2},{4,5},{5,4},{6,7},{7,6},{8,9},{9,8},{10,11... | collective-permute-start | bytes 3932168 | tf_op jit(solution)/shard_map/ppermute | solution.py:45
  38.3 20.3 %collective-permute-start.8 = (bf16[384,1024]{1,0:T(8,128)(2,1)}, bf16[384,1024]{1,0:T(8,128)(2,1)}, u32[]{:S(2)}, u32[]{:S(2)}) collective-permute-start(bf16[384,1024]{1,0:T(8,128)(2,1)} %slice.30), channel_id=1, source_target_pairs={{0,2},{1,3},{2,0},{3,1},{4,6},{5,7},{6,4},{7,5},{8,10},{9,11},{10,... | collective-permute-start | bytes 2359304 | tf_op jit(solution)/shard_map/ppermute | solution.py:45
  40.2 19.7 %collective-permute-start.9 = (bf16[512,768]{1,0:T(8,128)(2,1)S(1)}, bf16[512,768]{1,0:T(8,128)(2,1)S(1)}, u32[]{:S(2)}, u32[]{:S(2)}) collective-permute-start(bf16[512,768]{1,0:T(8,128)(2,1)S(1)} %pad_maximum_fusion.2), channel_id=1, source_target_pairs={{0,4},{4,0},{8,12},{12,8},{16,20},{20,16},{24,28},{28,24},{1,5},{5... | collective-permute-start | bytes 2359304 | tf_op jit(solution)/shard_map/ppermute | solution.py:45
  41.8 14.7 %collective-permute-start.11 = (bf16[128,1024]{1,0:T(8,128)(2,1)S(1)}, bf16[128,1024]{1,0:T(8,128)(2,1)S(1)}, u32[]{:S(2)}, u32[]{:S(2)}) collective-permute-start(bf16[128,1024]{1,0:T(8,128)(2,1)S(1)} %get-tuple-element.265.refs_10_.refs_8_), channel_id=1, source_target_pairs={{0,16},{4,20},{8,24},{12,28},{16,0},{20,4},{24,8},{28,12},{1,17},{... | collective-permute-start | bytes 786440 | tf_op jit(solution)/shard_map/ppermute | solution.py:45
  44.4 12.2 %collective-permute-start.10 = (bf16[512,256]{1,0:T(8,128)(2,1)S(1)}, bf16[512,256]{1,0:T(8,128)(2,1)S(1)}, u32[]{:S(2)}, u32[]{:S(2)}) collective-permute-start(bf16[512,256]{1,0:T(8,128)(2,1)S(1)} %pad_maximum_fusion.6), channel_id=1, source_target_pairs={{0,8},{4,12},{8,0},{12,4},{16,24},{20,28},{24,16},{28,20},{1,9},{5... | collective-permute-start | bytes 786440 | tf_op jit(solution)/shard_map/ppermute | solution.py:45
  59.9 22.4 %collective-permute-start.12 = (bf16[384,1024]{1,0:T(8,128)(2,1)}, bf16[384,1024]{1,0:T(8,128)(2,1)}, u32[]{:S(2)}, u32[]{:S(2)}) collective-permute-start(bf16[384,1024]{1,0:T(8,128)(2,1)} %collective-permute-done.8.refs_3_.refs_7_), channel_id=1, source_target_pairs={{0,1},{1,0},{2,3},{3,2},{4,5},{5,4},{6,7},{7,6},{8,9},{9,8},{10,11... | collective-permute-start | bytes 2359304 | tf_op jit(solution)/shard_map/ppermute | solution.py:45
  60.0 21.5 %collective-permute-start.13 = (bf16[256,1024]{1,0:T(8,128)(2,1)}, bf16[256,1024]{1,0:T(8,128)(2,1)}, u32[]{:S(2)}, u32[]{:S(2)}) collective-permute-start(bf16[256,1024]{1,0:T(8,128)(2,1)} %slice.31), channel_id=1, source_target_pairs={{0,2},{1,3},{2,0},{3,1},{4,6},{5,7},{6,4},{7,5},{8,10},{9,11},{10,... | collective-permute-start | bytes 1572872 | tf_op jit(solution)/shard_map/ppermute | solution.py:45
  61.4 20.9 %collective-permute-start.14 = (bf16[256,1024]{1,0:T(8,128)(2,1)}, bf16[256,1024]{1,0:T(8,128)(2,1)}, u32[]{:S(2)}, u32[]{:S(2)}) collective-permute-start(bf16[256,1024]{1,0:T(8,128)(2,1)} %pad_maximum_fusion.3), channel_id=1, source_target_pairs={{0,8},{4,12},{8,0},{12,4},{16,24},{20,28},{24,16},{28,20},{1,9},{5... | collective-permute-start | bytes 1572872 | tf_op jit(solution)/shard_map/ppermute | solution.py:45
  64.7 16.7 %collective-permute-start.15 = (bf16[128,1024]{1,0:T(8,128)(2,1)S(1)}, bf16[128,1024]{1,0:T(8,128)(2,1)}, u32[]{:S(2)}, u32[]{:S(2)}) collective-permute-start(bf16[128,1024]{1,0:T(8,128)(2,1)S(1)} %get-tuple-element.269.refs_14_), channel_id=1, source_target_pairs={{0,16},{4,20},{8,24},{12,28},{16,0},{20,4},{24,8},{28,12},{1,17},{... | collective-permute-start | bytes 786440 | tf_op jit(solution)/shard_map/ppermute | solution.py:45
  77.6 10.2 %copy-start.29 = (bf16[128,256]{1,0:T(8,128)(2,1)S(1)}, bf16[128,256]{1,0:T(8,128)(2,1)}, u32[]{:S(2)}) copy-start(bf16[128,256]{1,0:T(8,128)(2,1)} %copy-done.28) | copy-start | bytes 196612
  77.6 10.2 %copy-start.31 = (bf16[128,256]{1,0:T(8,128)(2,1)S(1)}, bf16[128,256]{1,0:T(8,128)(2,1)}, u32[]{:S(2)}) copy-start(bf16[128,256]{1,0:T(8,128)(2,1)} %copy-done.30) | copy-start | bytes 196612
  77.7 10.2 %copy-start.33 = (bf16[256,256]{1,0:T(8,128)(2,1)S(1)}, bf16[256,256]{1,0:T(8,128)(2,1)}, u32[]{:S(2)}) copy-start(bf16[256,256]{1,0:T(8,128)(2,1)} %copy-done.32) | copy-start | bytes 393220
  77.7 10.2 %copy-start.45 = (bf16[512,256]{1,0:T(8,128)(2,1)S(1)}, bf16[512,256]{1,0:T(8,128)(2,1)}, u32[]{:S(2)}) copy-start(bf16[512,256]{1,0:T(8,128)(2,1)} %copy-done.44) | copy-start | bytes 786436
  82.3 5.6 %collective-permute-start.16 = (bf16[256,1024]{1,0:T(8,128)(2,1)}, bf16[256,1024]{1,0:T(8,128)(2,1)S(1)}, u32[]{:S(2)}, u32[]{:S(2)}) collective-permute-start(bf16[256,1024]{1,0:T(8,128)(2,1)} %collective-permute-done.13.refs_4_.refs_8_), channel_id=1, source_target_pairs={{0,1},{1,0},{2,3},{3,2},{4,5},{5,4},{6,7},{7,6},{8,9},{9,8},{10,11... | collective-permute-start | bytes 1572872 | tf_op jit(solution)/shard_map/ppermute | solution.py:45
  83.3 14.4 %collective-permute-start.17 = (bf16[256,1024]{1,0:T(8,128)(2,1)S(1)}, bf16[256,1024]{1,0:T(8,128)(2,1)S(1)}, u32[]{:S(2)}, u32[]{:S(2)}) collective-permute-start(bf16[256,1024]{1,0:T(8,128)(2,1)S(1)} %pad_maximum_fusion.4), channel_id=1, source_target_pairs={{0,8},{4,12},{8,0},{12,4},{16,24},{20,28},{24,16},{28,20},{1,9},{5... | collective-permute-start | bytes 1572872 | tf_op jit(solution)/shard_map/ppermute | solution.py:45
  86.3 64.2 %collective-permute-start.18 = (bf16[512,1024]{1,0:T(8,128)(2,1)S(1)}, bf16[512,1024]{1,0:T(8,128)(2,1)S(1)}, u32[]{:S(2)}, u32[]{:S(2)}) collective-permute-start(bf16[512,1024]{1,0:T(8,128)(2,1)S(1)} %pad_maximum_fusion), channel_id=1, source_target_pairs={{0,4},{4,0},{8,12},{12,8},{16,20},{20,16},{24,28},{28,24},{1,5},{5... | collective-permute-start | bytes 3145736 | tf_op jit(solution)/shard_map/ppermute | solution.py:45
  87.9 67.7 %copy-start.34 = (bf16[256,1024]{1,0:T(8,128)(2,1)}, bf16[256,1024]{1,0:T(8,128)(2,1)S(1)}, u32[]{:S(2)}) copy-start(bf16[256,1024]{1,0:T(8,128)(2,1)S(1)} %collective-permute-done.16.refs_1_.refs_5_) | copy-start | bytes 1572868
  87.9 12.6 %copy-start.72 = (bf16[2560,256]{1,0:T(8,128)(2,1)S(1)}, bf16[2560,256]{1,0:T(8,128)(2,1)}, u32[]{:S(2)}) copy-start(bf16[2560,256]{1,0:T(8,128)(2,1)} %get-tuple-element.225.q_ref) | copy-start | bytes 3932164
  87.9 12.6 %copy-start.73 = (bf16[2560,256]{1,0:T(8,128)(2,1)S(1)}, bf16[2560,256]{1,0:T(8,128)(2,1)}, u32[]{:S(2)}) copy-start(bf16[2560,256]{1,0:T(8,128)(2,1)} %get-tuple-element.236.k_ref) | copy-start | bytes 3932164
  87.9 12.5 %copy-start.74 = (bf16[2560,256]{1,0:T(8,128)(2,1)S(1)}, bf16[2560,256]{1,0:T(8,128)(2,1)}, u32[]{:S(2)}) copy-start(bf16[2560,256]{1,0:T(8,128)(2,1)} %get-tuple-element.237.v_ref) | copy-start | bytes 3932164
  98.9 52.5 %collective-permute-start.19 = (bf16[512,1024]{1,0:T(8,128)(2,1)S(1)}, bf16[512,1024]{1,0:T(8,128)(2,1)S(1)}, u32[]{:S(2)}, u32[]{:S(2)}) collective-permute-start(bf16[512,1024]{1,0:T(8,128)(2,1)S(1)} %pad_maximum_fusion.1), channel_id=1, source_target_pairs={{0,4},{4,0},{8,12},{12,8},{16,20},{20,16},{24,28},{28,24},{1,5},{5... | collective-permute-start | bytes 3145736 | tf_op jit(solution)/shard_map/ppermute | solution.py:45
  155.5 14.5 %collective-permute-start.20 = (bf16[2,640,1024]{2,1,0:T(8,128)(2,1)S(1)}, bf16[2,640,1024]{2,1,0:T(8,128)(2,1)S(1)}, u32[]{:S(2)}, u32[]{:S(2)}) collective-permute-start(bf16[2,640,1024]{2,1,0:T(8,128)(2,1)S(1)} %get-tuple-element.260), channel_id=1, source_target_pairs={{0,1},{1,0},{2,3},{3,2},{4,5},{5,4},{6,7},{7,6},{8,9},{9,8},{10,11... | collective-permute-start | bytes 7864328 | tf_op jit(solution)/shard_map/ppermute | solution.py:45
  171.3 45.1 %collective-permute-start.21 = (bf16[1,640,1024]{2,1,0:T(8,128)(2,1)}, bf16[1,640,1024]{2,1,0:T(8,128)(2,1)S(1)}, u32[]{:S(2)}, u32[]{:S(2)}) collective-permute-start(bf16[1,640,1024]{2,1,0:T(8,128)(2,1)} %add_terms.3), channel_id=1, source_target_pairs={{0,2},{1,3},{2,0},{3,1},{4,6},{5,7},{6,4},{7,5},{8,10},{9,11},{10,... | collective-permute-start | bytes 3932168 | tf_op jit(solution)/shard_map/ppermute | solution.py:45
  172.7 42.1 %collective-permute-start.22 = (bf16[4,128,512]{2,1,0:T(8,128)(2,1)}, bf16[4,128,512]{2,1,0:T(8,128)(2,1)S(1)}, u32[]{:S(2)}, u32[]{:S(2)}) collective-permute-start(bf16[4,128,512]{2,1,0:T(8,128)(2,1)} %get-tuple-element.283), channel_id=1, source_target_pairs={{0,4},{4,0},{8,12},{12,8},{16,20},{20,16},{24,28},{28,24},{1,5},{5... | collective-permute-start | bytes 1572872 | tf_op jit(solution)/shard_map/ppermute | solution.py:45
  173.2 42.4 %collective-permute-start.23 = (bf16[4,128,512]{2,1,0:T(8,128)(2,1)}, bf16[4,128,512]{2,1,0:T(8,128)(2,1)S(1)}, u32[]{:S(2)}, u32[]{:S(2)}) collective-permute-start(bf16[4,128,512]{2,1,0:T(8,128)(2,1)} %get-tuple-element.284), channel_id=1, source_target_pairs={{0,8},{4,12},{8,0},{12,4},{16,24},{20,28},{24,16},{28,20},{1,9},{5... | collective-permute-start | bytes 1572872 | tf_op jit(solution)/shard_map/ppermute | solution.py:45
  216.4 5.1 %collective-permute-start.24 = (bf16[2,640,1024]{2,1,0:T(8,128)(2,1)}, bf16[2,640,1024]{2,1,0:T(8,128)(2,1)S(1)}, u32[]{:S(2)}, u32[]{:S(2)}) collective-permute-start(bf16[2,640,1024]{2,1,0:T(8,128)(2,1)} %get-tuple-element.287), channel_id=1, source_target_pairs={{0,1},{1,0},{2,3},{3,2},{4,5},{5,4},{6,7},{7,6},{8,9},{9,8},{10,11... | collective-permute-start | bytes 7864328 | tf_op jit(solution)/shard_map/ppermute | solution.py:45
  224.6 32.4 %collective-permute-start.25 = (bf16[1,640,1024]{2,1,0:T(8,128)(2,1)}, bf16[1,640,1024]{2,1,0:T(8,128)(2,1)S(1)}, u32[]{:S(2)}, u32[]{:S(2)}) collective-permute-start(bf16[1,640,1024]{2,1,0:T(8,128)(2,1)} %add_terms.4), channel_id=1, source_target_pairs={{0,2},{1,3},{2,0},{3,1},{4,6},{5,7},{6,4},{7,5},{8,10},{9,11},{10,... | collective-permute-start | bytes 3932168 | tf_op jit(solution)/shard_map/ppermute | solution.py:45
  225.2 30.8 %collective-permute-start.28 = (bf16[4,128,1024]{2,1,0:T(8,128)(2,1)}, bf16[4,128,1024]{2,1,0:T(8,128)(2,1)S(1)}, u32[]{:S(2)}, u32[]{:S(2)}) collective-permute-start(bf16[4,128,1024]{2,1,0:T(8,128)(2,1)} %get-tuple-element.299), channel_id=1, source_target_pairs={{0,4},{4,0},{8,12},{12,8},{16,20},{20,16},{24,28},{28,24},{1,5},{5... | collective-permute-start | bytes 3145736 | tf_op jit(solution)/shard_map/ppermute | solution.py:45
  226.7 30.3 %collective-permute-start.29 = (bf16[4,128,1024]{2,1,0:T(8,128)(2,1)S(1)}, bf16[4,128,1024]{2,1,0:T(8,128)(2,1)S(1)}, u32[]{:S(2)}, u32[]{:S(2)}) collective-permute-start(bf16[4,128,1024]{2,1,0:T(8,128)(2,1)S(1)} %copy-done.61), channel_id=1, source_target_pairs={{0,8},{4,12},{8,0},{12,4},{16,24},{20,28},{24,16},{28,20},{1,9},{5... | collective-permute-start | bytes 3145736 | tf_op jit(solution)/shard_map/ppermute | solution.py:45
  227.9 27.0 %collective-permute-start.26 = (bf16[2,128,512]{2,1,0:T(8,128)(2,1)}, bf16[2,128,512]{2,1,0:T(8,128)(2,1)S(1)}, u32[]{:S(2)}, u32[]{:S(2)}) collective-permute-start(bf16[2,128,512]{2,1,0:T(8,128)(2,1)} %get-tuple-element.297), channel_id=1, source_target_pairs={{0,16},{4,20},{8,24},{12,28},{16,0},{20,4},{24,8},{28,12},{1,17},{... | collective-permute-start | bytes 786440 | tf_op jit(solution)/shard_map/ppermute | solution.py:45
  230.6 25.3 %collective-permute-start.27 = (bf16[2,128,512]{2,1,0:T(8,128)(2,1)}, bf16[2,128,512]{2,1,0:T(8,128)(2,1)S(1)}, u32[]{:S(2)}, u32[]{:S(2)}) collective-permute-start(bf16[2,128,512]{2,1,0:T(8,128)(2,1)} %get-tuple-element.298), channel_id=1, source_target_pairs={{0,4},{4,0},{8,12},{12,8},{16,20},{20,16},{24,28},{28,24},{1,5},{5... | collective-permute-start | bytes 786440 | tf_op jit(solution)/shard_map/ppermute | solution.py:45
  258.1 4.9 %collective-permute-start.30 = (bf16[2,640,1024]{2,1,0:T(8,128)(2,1)S(1)}, bf16[2,640,1024]{2,1,0:T(8,128)(2,1)S(1)}, u32[]{:S(2)}, u32[]{:S(2)}) collective-permute-start(bf16[2,640,1024]{2,1,0:T(8,128)(2,1)S(1)} %get-tuple-element.302), channel_id=1, source_target_pairs={{0,1},{1,0},{2,3},{3,2},{4,5},{5,4},{6,7},{7,6},{8,9},{9,8},{10,11... | collective-permute-start | bytes 7864328 | tf_op jit(solution)/shard_map/ppermute | solution.py:45
  263.4 35.7 %collective-permute-start.38 = (bf16[1,640,1024]{2,1,0:T(8,128)(2,1)S(1)}, bf16[1,640,1024]{2,1,0:T(8,128)(2,1)S(1)}, u32[]{:S(2)}, u32[]{:S(2)}) collective-permute-start(bf16[1,640,1024]{2,1,0:T(8,128)(2,1)S(1)} %add_terms.5), channel_id=1, source_target_pairs={{0,2},{1,3},{2,0},{3,1},{4,6},{5,7},{6,4},{7,5},{8,10},{9,11},{10,... | collective-permute-start | bytes 3932168 | tf_op jit(solution)/shard_map/ppermute | solution.py:45
  265.2 18.0 %collective-permute-start.33 = (bf16[2,128,1024]{2,1,0:T(8,128)(2,1)S(1)}, bf16[2,128,1024]{2,1,0:T(8,128)(2,1)S(1)}, u32[]{:S(2)}, u32[]{:S(2)}) collective-permute-start(bf16[2,128,1024]{2,1,0:T(8,128)(2,1)S(1)} %get-tuple-element.317), channel_id=1, source_target_pairs={{0,8},{4,12},{8,0},{12,4},{16,24},{20,28},{24,16},{28,20},{1,9},{5... | collective-permute-start | bytes 1572872 | tf_op jit(solution)/shard_map/ppermute | solution.py:45
  266.8 16.4 %collective-permute-start.34 = (bf16[2,128,1024]{2,1,0:T(8,128)(2,1)S(1)}, bf16[2,128,1024]{2,1,0:T(8,128)(2,1)S(1)}, u32[]{:S(2)}, u32[]{:S(2)}) collective-permute-start(bf16[2,128,1024]{2,1,0:T(8,128)(2,1)S(1)} %get-tuple-element.318), channel_id=1, source_target_pairs={{0,4},{4,0},{8,12},{12,8},{16,20},{20,16},{24,28},{28,24},{1,5},{5... | collective-permute-start | bytes 1572872 | tf_op jit(solution)/shard_map/ppermute | solution.py:45
  267.3 14.2 %collective-permute-start.35 = (bf16[1,128,512]{2,1,0:T(8,128)(2,1)S(1)}, bf16[1,128,512]{2,1,0:T(8,128)(2,1)S(1)}, u32[]{:S(2)}, u32[]{:S(2)}) collective-permute-start(bf16[1,128,512]{2,1,0:T(8,128)(2,1)S(1)} %get-tuple-element.319), channel_id=1, source_target_pairs={{0,16},{4,20},{8,24},{12,28},{16,0},{20,4},{24,8},{28,12},{1,17},{... | collective-permute-start | bytes 393224 | tf_op jit(solution)/shard_map/ppermute | solution.py:45
  271.6 1.3 collective-permute-start.31
  272.9 10.3 %collective-permute-start.32 = (f32[16,1024]{1,0:T(8,128)S(1)}, f32[16,1024]{1,0:T(8,128)S(1)}, u32[]{:S(2)}, u32[]{:S(2)}) collective-permute-start(f32[16,1024]{1,0:T(8,128)S(1)} %add.41), channel_id=1, source_target_pairs={{0,16},{4,20},{8,24},{12,28},{16,0},{20,4},{24,8},{28,12},{1,17},{... | collective-permute-start | bytes 196616 | tf_op jit(solution)/shard_map/ppermute | solution.py:45
  283.2 15.9 %copy-start.11 = (f32[640,1024]{1,0:T(8,128)S(1)}, f32[640,1024]{1,0:T(8,128)}, u32[]{:S(2)}) copy-start(f32[640,1024]{1,0:T(8,128)} %get-tuple-element.328.norm_ref) | copy-start | bytes 7864324
  283.2 15.9 %copy-start.43 = (f32[640,1]{1,0:T(8,128)S(1)}, f32[640,1]{1,0:T(8,128)}, u32[]{:S(2)}) copy-start(f32[640,1]{1,0:T(8,128)} %get-tuple-element.329.std_ref) | copy-start | bytes 7684
  283.4 20.3 %collective-permute-start.41 = (bf16[1,128,1024]{2,1,0:T(8,128)(2,1)S(1)}, bf16[1,128,1024]{2,1,0:T(8,128)(2,1)S(1)}, u32[]{:S(2)}, u32[]{:S(2)}) collective-permute-start(bf16[1,128,1024]{2,1,0:T(8,128)(2,1)S(1)} %get-tuple-element.337), channel_id=1, source_target_pairs={{0,16},{4,20},{8,24},{12,28},{16,0},{20,4},{24,8},{28,12},{1,17},{... | collective-permute-start | bytes 786440 | tf_op jit(solution)/shard_map/ppermute | solution.py:45
  285.9 22.5 %collective-permute-start.42 = (bf16[1,128,1024]{2,1,0:T(8,128)(2,1)S(1)}, bf16[1,128,1024]{2,1,0:T(8,128)(2,1)S(1)}, u32[]{:S(2)}, u32[]{:S(2)}) collective-permute-start(bf16[1,128,1024]{2,1,0:T(8,128)(2,1)S(1)} %get-tuple-element.338), channel_id=1, source_target_pairs={{0,16},{4,20},{8,24},{12,28},{16,0},{20,4},{24,8},{28,12},{1,17},{... | collective-permute-start | bytes 786440 | tf_op jit(solution)/shard_map/ppermute | solution.py:45
  286.4 4.3 %collective-permute-start.36 = (f32[16,1024]{1,0:T(8,128)S(1)}, f32[16,1024]{1,0:T(8,128)S(1)}, u32[]{:S(2)}, u32[]{:S(2)}) collective-permute-start(f32[16,1024]{1,0:T(8,128)S(1)} %add.42), channel_id=1, source_target_pairs={{0,4},{4,0},{8,12},{12,8},{16,20},{20,16},{24,28},{28,24},{1,5},{5... | collective-permute-start | bytes 196616 | tf_op jit(solution)/shard_map/ppermute | solution.py:45
  290.7 8.4 %collective-permute-start.37 = (f32[16,1024]{1,0:T(8,128)S(1)}, f32[16,1024]{1,0:T(8,128)S(1)}, u32[]{:S(2)}, u32[]{:S(2)}) collective-permute-start(f32[16,1024]{1,0:T(8,128)S(1)} %add.43), channel_id=1, source_target_pairs={{0,8},{4,12},{8,0},{12,4},{16,24},{20,28},{24,16},{28,20},{1,9},{5... | collective-permute-start | bytes 196616 | tf_op jit(solution)/shard_map/ppermute | solution.py:45
  292.0 10.8 %collective-permute-start.40 = (bf16[1,128,512]{2,1,0:T(8,128)(2,1)S(1)}, bf16[1,128,512]{2,1,0:T(8,128)(2,1)S(1)}, u32[]{:S(2)}, u32[]{:S(2)}) collective-permute-start(bf16[1,128,512]{2,1,0:T(8,128)(2,1)S(1)} %get-tuple-element.333), channel_id=1, source_target_pairs={{0,8},{4,12},{8,0},{12,4},{16,24},{20,28},{24,16},{28,20},{1,9},{5... | collective-permute-start | bytes 393224 | tf_op jit(solution)/shard_map/ppermute | solution.py:45
  302.0 7.6 %collective-permute-start.39 = (f32[16,1024]{1,0:T(8,128)S(1)}, f32[16,1024]{1,0:T(8,128)S(1)}, u32[]{:S(2)}, u32[]{:S(2)}) collective-permute-start(f32[16,1024]{1,0:T(8,128)S(1)} %add.44), channel_id=1, source_target_pairs={{0,2},{1,3},{2,0},{3,1},{4,6},{5,7},{6,4},{7,5},{8,10},{9,11},{10,... | collective-permute-start | bytes 196616 | tf_op jit(solution)/shard_map/ppermute | solution.py:45
  (58 other events, 254.9 us)

commit v13 on v12

--- a/solution.py
+++ b/solution.py
@@ -127,6 +127,24 @@
         return self.terms
 
 
+class Parts(Halving):
+    def __init__(self, first, second, keep, axis, bits):
+        super().__init__(first, keep, axis, bits)
+        self.second = second
+
+    def begin(self):
+        bit = self.bits.pop(0)
+        self.got, self.other = swap(self.send, self.axis, bit), swap(self.second, self.axis, bit)
+
+    def middle(self):
+        half = self.got.shape[0]
+        self.send = add_terms([*self.terms, (self.got, 0)], half)
+        self.terms = [(self.terms[0][0], half), (self.other, 0)]
+        while len(self.bits) > 1:
+            self.swap()
+            self.add()
+
+
 def tie_halves(values, *halvings):
     flat = tie(*values, *[x.got for x in halvings])
     for x, got in zip(halvings, flat[len(values) :]):
@@ -147,23 +165,29 @@
     return pl.BlockSpec((rows, columns), lambda i, *_: (i, 0))
 
 
-def half_blocks(groups, rows, columns):
-    half = groups // 2
+def part_shapes(groups, rows, columns):
+    quarter = max(groups // 4, 1)
+    return [shaped(n, rows, columns) for n in (quarter, quarter, groups - 2 * quarter)]
+
+
+def part_blocks(groups, rows, columns):
+    quarter = max(groups // 4, 1)
     shape = (pl.Squeezed(), rows, columns)
     return [
-        pl.BlockSpec(shape, lambda i, *_: (jnp.minimum(i, half - 1), 0, 0)),
-        pl.BlockSpec(shape, lambda i, *_: (jnp.maximum(i - half, 0), 0, 0)),
+        pl.BlockSpec(shape, lambda i, *_: (jnp.minimum(i, quarter - 1), 0, 0)),
+        pl.BlockSpec(shape, lambda i, *_: (jnp.clip(i - quarter, 0, quarter - 1), 0, 0)),
+        pl.BlockSpec(shape, lambda i, *_: (jnp.maximum(i - 2 * quarter, 0), 0, 0)),
     ]
 
 
-def store_half(send, keep, value, step, groups):
-    @pl.when(step < groups // 2)
-    def _():
-        send[...] = value
-
-    @pl.when(step >= groups // 2)
-    def _():
-        keep[...] = value
+def store_part(stacks, value, step, groups):
+    quarter = max(groups // 4, 1)
+    turn_of = jnp.minimum(step // quarter, 2)
+    for at, stack in enumerate(stacks):
+
+        @pl.when(turn_of == at)
+        def _(stack=stack):
+            stack[...] = value
 
 
 class Tokens:
@@ -352,16 +376,21 @@
                     added[:, to : to + HD] = own[:, at : at + HD]
 
         token = block[step % 2]
-        qkv = dot_nn(shift_gain(token, gain, shift), whole[...]) + added[...]
-        first = (ids[0] ^ ids[2 + step]) * (rows // SEG)
-        for at in range(rows // SEG):
+        normed = shift_gain(token, gain, shift)
+        blocks = rows // SEG
+        cut = (blocks + 1) // 2
+        both = [dot_nn(normed[x], whole[...]) + added[...] for x in (slice(0, cut * SEG), slice(cut * SEG, rows))]
+        first = (ids[0] ^ ids[2 + step]) * blocks
+        for at in range(blocks):
             number = first + at
             table = pl.ds(pl.multiple_of(info[number // NB, number % NB, 4] * SEG, SEG), SEG)
             tabs = (cos[table, :], sine[table, :])
             own = slice(at * SEG, (at + 1) * SEG)
-            q_out[own, :] = (turn(qkv[own, :width], *tabs, 1.0) * HD**-0.5).astype(bf16)
-            k_out[own, :] = turn(qkv[own, width : 2 * width], *tabs, 1.0).astype(bf16)
-        v_out[...] = qkv[:, 2 * width :].astype(bf16)
+            here = at * SEG if at < cut else (at - cut) * SEG
+            qkv = both[at >= cut][here : here + SEG]
+            q_out[own, :] = (turn(qkv[:, :width], *tabs, 1.0) * HD**-0.5).astype(bf16)
+            k_out[own, :] = turn(qkv[:, width : 2 * width], *tabs, 1.0).astype(bf16)
+            v_out[own, :] = qkv[:, 2 * width :].astype(bf16)
 
     operands = [*sent.arrays, *pack.arrays, gain, shift, bias, *tables]
     out = shaped(groups * rows, width)
@@ -546,7 +575,7 @@
     rows, width = context.shape[0] // groups, context.shape[1]
 
     def kernel(ids, ctx, *refs):
-        weight_refs, (send, keep, whole, placed) = refs[:-4], refs[-4:]
+        weight_refs, stacks, (whole, placed) = refs[:-5], refs[-5:-2], refs[-2:]
         step = pl.program_id(0)
 
         @pl.when(step == 0)
@@ -557,10 +586,9 @@
             for copy in copies:
                 copy.wait()
 
-        store_half(send, keep, dot_nt(ctx[...], whole[...]).astype(bf16), step, groups)
+        store_part(stacks, dot_nt(ctx[...], whole[...]).astype(bf16), step, groups)
 
     operands = [context, *pack.arrays]
-    half = shaped(groups // 2, rows, model)
     return call(
         kernel,
         "project_context",
@@ -568,8 +596,8 @@
         [ids],
         operands,
         [own_block(rows, width)] + pack.specs(),
-        [half] * 2,
-        half_blocks(groups, rows, model),
+        part_shapes(groups, rows, model),
+        part_blocks(groups, rows, model),
         weight_scratch(pack),
         2 * groups * rows * model * width,
         room=14,
@@ -648,8 +676,9 @@
         grad_refs, refs = refs[: len(grad.arrays)], refs[len(grad.arrays) :]
         fc_refs, refs = refs[:pieces], refs[pieces:]
         out_refs, refs = refs[:pieces], refs[pieces:]
-        gain, shift, bias, part_send, part_keep, hidden_ref, bias_ref = refs[:7]
-        stacks, refs = refs[7:11], refs[11:]
+        gain, shift, bias, *parts_out = refs[:6]
+        hidden_ref, bias_ref = refs[6:8]
+        stacks, refs = refs[8:12], refs[12:]
         block, arrived, grad_block, grad_arrived, fc_whole, fc_placed, out_whole, out_placed = refs[:8]
         act_ref, fc_total, out_total = refs[8:]
         step = pl.program_id(0)
@@ -688,9 +717,7 @@
             low = (slope * (chance + field * bell)).astype(bf16)
             hidden_ref[x, :] = low
             bias_ref[0:1, :] += jnp.sum(low.astype(f32), axis=0, keepdims=True)
-        store_half(
-            part_send, part_keep, dot_nt(act_ref[...], out_whole[...]).astype(bf16), step, groups
-        )
+        store_part(parts_out, dot_nt(act_ref[...], out_whole[...]).astype(bf16), step, groups)
         out_total[...] += dot_tn(grads, act_ref[...])
         fc_total[...] += dot_tn(normed, hidden_ref[...])
 
@@ -705,12 +732,8 @@
 
     operands = [*sent.arrays, *grad.arrays, *fc.arrays, *out.arrays, gain, shift, bias]
     count = model // fc.rows
-    outs = [
-        shaped(groups // 2, rows, model),
-        shaped(groups // 2, rows, model),
-        shaped(groups * rows, units),
-        shaped(8, units, dtype=f32),
-    ]
+    outs = part_shapes(groups, rows, model)
+    outs += [shaped(groups * rows, units), shaped(8, units, dtype=f32)]
     outs += [shaped(count // 2, fc.rows, units)] * 4
     return call(
         kernel,
@@ -724,9 +747,9 @@
         + out.specs()
         + [resident(x.shape) for x in operands[-3:]],
         outs,
-        half_blocks(groups, rows, model)
+        part_blocks(groups, rows, model)
         + [step_block(rows, units)]
-        + [resident(x.shape) for x in outs[3:]],
+        + [resident(x.shape) for x in outs[4:]],
         sent.scratch()
         + grad.scratch()
         + weight_scratch(fc)
@@ -749,8 +772,8 @@
         sent_refs, refs = refs[:held], refs[held:]
         qkv_refs, refs = refs[:pieces], refs[pieces:]
         fc_refs, refs = refs[:pieces], refs[pieces:]
-        gain_attn, gain_mlp, send, keep, sums_ref = refs[:5]
-        block, arrived, qkv_whole, qkv_placed, fc_whole, fc_placed = refs[5:]
+        gain_attn, gain_mlp, *stacks = refs[:5]
+        sums_ref, block, arrived, qkv_whole, qkv_placed, fc_whole, fc_placed = refs[5:]
         step = pl.program_id(0)
 
         def weights():
@@ -777,14 +800,10 @@
             sums_ref[2 * at : 2 * at + 1, :] += jnp.sum(back * token, axis=0, keepdims=True)
             sums_ref[2 * at + 1 : 2 * at + 2, :] += jnp.sum(back, axis=0, keepdims=True)
         part = back_attn * gain_attn[...] + back_mlp * gain_mlp[...]
-        store_half(send, keep, part.astype(bf16), step, groups)
+        store_part(stacks, part.astype(bf16), step, groups)
 
     operands = [grads, hidden, *sent.arrays, *qkv_pack.arrays, *fc.arrays, gain_attn, gain_mlp]
-    outs = [
-        shaped(groups // 2, rows, model),
-        shaped(groups // 2, rows, model),
-        shaped(8, model, dtype=f32),
-    ]
+    outs = part_shapes(groups, rows, model) + [shaped(8, model, dtype=f32)]
     return call(
         kernel,
         "norm_backward",
@@ -797,7 +816,7 @@
         + fc.specs()
         + [resident(x.shape) for x in operands[-2:]],
         outs,
-        half_blocks(groups, rows, model) + [resident(x.shape) for x in outs[2:]],
+        part_blocks(groups, rows, model) + [resident(x.shape) for x in outs[3:]],
         sent.scratch() + weight_scratch(qkv_pack) + weight_scratch(fc),
         2 * groups * rows * model * (units + columns),
         room=26,
@@ -1180,19 +1199,16 @@
     context, dq, dk, dv = tie_packs(fc_pack, out_pack, beside=done)
     dp_orders = [halving_order(near_bits), halving_order(next_bits)]
     qkv_orders = [halving_order(bits) for bits in qkv_bits]
-    attn_parts = Halving(
+    attn_parts = Parts(
         *project_context(ids, context, dense_pack, groups, model), "tensor", tensor_bits
     )
-    while len(attn_parts.bits) > 2:
-        attn_parts.swap()
-        attn_parts.add()
-    attn_parts.send, context = tie(attn_parts.send, context)
-    attn_parts.swap()
+    attn_parts.begin()
     done = attention_weights(
         ids, info, tables, context, dq, dk, dv, sent, grad, gain_attn, shift_attn, qkv_orders
     )
-    grads, qkv_bias_sums, *stacks = tie_halves(done, attn_parts)
-    attn_parts.add()
+    *done, attn_parts.other = tie_halves([*done, attn_parts.other], attn_parts)
+    grads, qkv_bias_sums, *stacks = done
+    attn_parts.middle()
     qkv_sums = [Halving(*stacks[:2], "dp", qkv_bits[0]), Halving(*stacks[2:], "dp", qkv_bits[1])]
     sent.arrays[0], attn_parts.send = tie(sent.arrays[0], attn_parts.send)
     attn_parts.swap()
@@ -1202,34 +1218,33 @@
         ids, sent, grad, gain_mlp, shift_mlp, fc_pack, fc_rows, out_pack, dp_orders
     )
     done = tie_halves(done, attn_parts, *qkv_sums)
-    mlp_send, mlp_keep, hidden, fc_bias_sums, *stacks = done
+    *mlp_stacks, hidden, fc_bias_sums = done[:5]
+    stacks = done[5:]
     attn_parts.add()
-    mlp_parts = Halving(mlp_send, mlp_keep, "tensor", tensor_bits)
+    mlp_parts = Parts(*mlp_stacks, "tensor", tensor_bits)
     mlp_sums = [Halving(*stacks[:2], "dp", near_bits), Halving(*stacks[2:], "dp", next_bits)]
-    while len(mlp_parts.bits) > 2:
-        mlp_parts.swap()
-        mlp_parts.add()
-    mlp_parts.swap()
+    mlp_parts.begin()
     add_stacks(qkv_sums)
-    mlp_parts.add()
+    mlp_parts.middle()
     hidden, mlp_parts.send = tie(hidden, mlp_parts.send)
+    hidden, other = tie(hidden, mlp_parts.terms[1][0])
+    mlp_parts.terms[1] = (other, 0)
     mlp_parts.swap()
     for parts in qkv_sums + mlp_sums:
         parts.swap()
     done = norm_backward(ids, sent, grads, hidden, gain_attn, gain_mlp, qkv_pack, fc_pack)
     done = tie_halves(done, mlp_parts, *qkv_sums, *mlp_sums)
-    back_send, back_keep, norm_sums = done
+    *back_stacks, norm_sums = done
     mlp_parts.add()
 
-    back_parts = Halving(back_send, back_keep, "tensor", tensor_bits)
-    while len(back_parts.bits) > 2:
-        back_parts.swap()
-        back_parts.add()
-    back_parts.swap()
+    back_parts = Parts(*back_stacks, "tensor", tensor_bits)
+    back_parts.begin()
     add_stacks(qkv_sums + mlp_sums)
-
-    back_parts.add()
+    back_parts.middle()
+
     stream_in, back_parts.send = tie(stream_in, back_parts.send)
+    stream_in, other = tie(stream_in, back_parts.terms[1][0])
+    back_parts.terms[1] = (other, 0)
     back_parts.swap()
     for parts in qkv_sums + mlp_sums:
         parts.swap()

time: 314 us -> 309 us (0.984)
    ppermute x43 -> x46, starting transfers between devices: 51.9 us -> 49.3 us  [swap(): return lax.ppermute(block, axis, [(i, i ^ bit) for i in range(size)])]
    ppermute x43 -> x46, waiting for transfers between devices: 69.8 us -> 69 us  [swap(): return lax.ppermute(block, axis, [(i, i ^ bit) for i in range(size)])]
    unnamed x161 -> x135, local copies, waits for them, and re-layouts: 18.3 us -> 17.6 us
  transfers between devices with their start and end apart: 43 -> 46, of which waited for: 20 -> 21; matrix products, arithmetic and copies ran while one was open for 4% -> 4% of each run, Pallas kernels for 48% -> 50%
where the time goes in v13:
time: 309 us; the launch traced here: 308 us
  Pallas kernels  157 us (51%)
  waiting for transfers between devices  69 us (22%)
  starting transfers between devices  49.3 us (16%)
  local copies, waits for them, and re-layouts  22.6 us (7%)
  other arithmetic  8.91 us (3%)
    pallas_call x19, Pallas kernels, call(): pl.pallas_call(kernel, grid_spec=pltpu.PrefetchScalarGridSpec(num_scalar_...  154 us
    ppermute x46, waiting for transfers between devices, swap(): return lax.ppermute(block, axis, [(i, i ^ bit) for i in range(size)])  69 us
    ppermute x46, starting transfers between devices, swap(): return lax.ppermute(block, axis, [(i, i ^ bit) for i in range(size)])  49.3 us
    unnamed x135, local copies, waits for them, and re-layouts  17.6 us
  transfers between devices with their start and end apart: 46, of which 21 were waited for; matrix products, arithmetic and copies ran while one was open for 4% of the time, Pallas kernels for 50%

profile of v13, /device:TPU:0, one launch (start us, length us, event | category | flops | bytes accessed | tf_op | source)
XLA Modules:
  0.0 307.8 jit_solution(3857276889731454908)
XLA Ops:
  1.2 4.7 %normalize.1 = (bf16[640,1024]{1,0:T(8,128)(2,1)}, f32[640,1024]{1,0:T(8,128)}, f32[640,1]{1,0:T(8,128)}) custom-call(f32[640,1024]{1,0:T(8,128)} %stream_ref.2), custom_call_target="tpu_custom_call" | custom-call | flops 5242880 | bytes 6556160 | tf_op jit(solution)/shard_map/normalize/pallas_call | solution.py:241
  5.8 2.5 collective-permute-start.4
  8.6 1.0 copy-done.24
  9.6 1.0 copy-done.25
  10.7 1.0 copy-done.28
  12.8 1.6 collective-permute-start.2
  14.4 2.6 collective-permute-start.1
  18.8 2.1 tree_table.1.info
  20.9 5.4 %collective-permute-done.1.refs_5_ = bf16[128,768]{1,0:T(8,128)(2,1)S(1)} collective-permute-done((bf16[128,768]{1,0:T(8,128)(2,1)S(1)}, bf16[128,768]{1,0:T(8,128)(2,1)S(1)}, u32[]{:S(2)}, u32[]{:S(2)}) %collective-permute-start.1) | collective-permute-done | bytes 196640 | tf_op jit(solution)/shard_map/ppermute | solution.py:45
  26.5 4.1 %collective-permute-start.5 = (bf16[256,768]{1,0:T(8,128)(2,1)S(1)}, bf16[256,768]{1,0:T(8,128)(2,1)S(1)}, u32[]{:S(2)}, u32[]{:S(2)}) collective-permute-start(bf16[256,768]{1,0:T(8,128)(2,1)S(1)} %pad_maximum_fusion.5), channel_id=1, source_target_pairs={{0,8},{4,12},{8,0},{12,4},{16,24},{20,28},{24,16},{28,20},{1,9},{5... | collective-permute-start | bytes 1179656 | tf_op jit(solution)/shard_map/ppermute | solution.py:45
  30.6 3.8 %fusion = (f32[1280,128]{1,0:T(8,128)}, f32[1280,128]{1,0:T(8,128)}) fusion(s32[128]{0:T(128)S(1)} %get-tuple-element.364, s32[128]{0:T(128)S(1)} %get-tuple-element.365, pred[128]{0:T(512)(128)(4,1)S(1)} %compare_and_fusion, f32[1280]{0:T(1024)S(1)} %convert_add_fusion), kind=kLoop, calls=%fused_computation.9 | loop fusion | flops 3112960 | bytes 1316992 | tf_op jit(solution)/shard_map/jit(_where)/select_n | solution.py:1080
  35.6 2.5 collective-permute-done.4.refs_2_
  38.1 2.9 collective-permute-done.5.refs_6_
  42.2 2.0 collective-permute-start.11
  44.2 1.6 collective-permute-start.10
  45.9 11.1 %collective-permute-done.11.refs_11_.refs_9_ = bf16[128,1024]{1,0:T(8,128)(2,1)S(1)} collective-permute-done((bf16[128,1024]{1,0:T(8,128)(2,1)S(1)}, bf16[128,1024]{1,0:T(8,128)(2,1)S(1)}, u32[]{:S(2)}, u32[]{:S(2)}) %collective-permute-start.11) | collective-permute-done | bytes 262176 | tf_op jit(solution)/shard_map/ppermute | solution.py:45
  57.2 3.9 %collective-permute-done.9.refs_7_ = bf16[512,768]{1,0:T(8,128)(2,1)S(1)} collective-permute-done((bf16[512,768]{1,0:T(8,128)(2,1)S(1)}, bf16[512,768]{1,0:T(8,128)(2,1)S(1)}, u32[]{:S(2)}, u32[]{:S(2)}) %collective-permute-start.9) | collective-permute-done | bytes 786464 | tf_op jit(solution)/shard_map/ppermute | solution.py:45
  62.8 1.2 collective-permute-start.13
  64.6 2.6 collective-permute-start.15
  67.2 11.1 %project_qkv.1 = (bf16[2560,256]{1,0:T(8,128)(2,1)}, bf16[2560,256]{1,0:T(8,128)(2,1)}, bf16[2560,256]{1,0:T(8,128)(2,1)}) custom-call(s32[6]{0:T(128)} %stack.11.ids, s32[1,20,5]{2,1,0:T(8,128)} %tree_table.1.info, bf16[640,1024]{1,0:T(8,128)(2,1)} %copy-done.42, bf16[640,1024]{1,0:T(8,128)(2,1)} %collective-permute-done.3.refs_1_, ...), custom_call_target="tpu_custom_call" | custom-call | flops 4026531840 | bytes 12079104 | tf_op jit(solution)/shard_map/project_qkv/pallas_call | solution.py:241
  78.3 2.0 collective-permute-done.15.refs_15_
  80.3 2.2 collective-permute-done.14.refs_12_.refs_10_
  82.6 1.0 pad_maximum_fusion.4
  83.6 1.9 collective-permute-start.17
  85.5 1.2 pad_maximum_fusion
  86.6 1.6 collective-permute-start.18
  88.3 5.4 %project_grad.1.do_ref = bf16[2560,256]{1,0:T(8,128)(2,1)S(1)} custom-call(s32[6]{0:T(128)S(1)} %copy-done.37, bf16[384,1024]{1,0:T(8,128)(2,1)} %collective-permute-done.12.refs_0_.refs_4_, bf16[256,1024]{1,0:T(8,128)(2,1)S(1)} %collective-permute-done.16.refs_1_.refs_5_, bf16[640,1024]{1,0:T(8,128)(2,1)} %collective-permute-done.refs_2_.refs_6_, ...), custom_call_target="tpu_custom_call" | custom-call | flops 1342177280 | bytes 7077888 | tf_op jit(solution)/shard_map/project_grad/pallas_call | solution.py:241
  93.8 4.3 %collective-permute-done.17.refs_16_ = bf16[256,1024]{1,0:T(8,128)(2,1)S(1)} collective-permute-done((bf16[256,1024]{1,0:T(8,128)(2,1)S(1)}, bf16[256,1024]{1,0:T(8,128)(2,1)S(1)}, u32[]{:S(2)}, u32[]{:S(2)}) %collective-permute-start.17) | collective-permute-done | bytes 524320 | tf_op jit(solution)/shard_map/ppermute | solution.py:45
  98.1 1.2 pad_maximum_fusion.1
  99.2 1.6 collective-permute-start.19
  100.9 49.9 %attention.1 = (bf16[2560,256]{1,0:T(8,128)(2,1)S(1)}, bf16[2560,256]{1,0:T(8,128)(2,1)S(1)}, bf16[2560,256]{1,0:T(8,128)(2,1)S(1)}, bf16[2560,256]{1,0:T(8,128)(2,1)S(1)}) custom-call(s32[1,20,5]{2,1,0:T(8,128)S(1)} %copy-done.36, bf16[2560,256]{1,0:T(8,128)(2,1)S(1)} %copy-done.58, bf16[2560,256]{1,0:T(8,128)(2,1)S(1)} %project_grad.1.do_ref, ...), custom_call_target="tpu_custom_call" | custom-call | flops 31406948352 | bytes 11796480 | tf_op jit(solution)/shard_map/attention/pallas_call | solution.py:241
  150.8 1.0 copy-done.45
  152.8 4.1 %project_context.1 = (bf16[1,640,1024]{2,1,0:T(8,128)(2,1)S(1)}, bf16[1,640,1024]{2,1,0:T(8,128)(2,1)S(1)}, bf16[2,640,1024]{2,1,0:T(8,128)(2,1)S(1)}) custom-call(s32[6]{0:T(128)S(1)} %copy-done.37, bf16[2560,256]{1,0:T(8,128)(2,1)S(1)} %get-tuple-element.256.ctx_ref.ctx, bf16[128,256]{1,0:T(8,128)(2,1)S(1)} %copy-done.17, bf16[128,256]{1,0:T(8,128)(2,1)S(1)} %copy-done.19, ...), custom_call_target="tpu_custom_call" | custom-call | flops 1342177280 | bytes 7077888 | tf_op jit(solution)/shard_map/project_context/pallas_call | solution.py:241
  157.4 12.5 %attention_weights.1 = (bf16[2560,768]{1,0:T(8,128)(2,1)S(1)}, f32[8,768]{1,0:T(8,128)S(1)}, bf16[4,128,512]{2,1,0:T(8,128)(2,1)}, bf16[4,128,512]{2,1,0:T(8,128...) custom-call(s32[6]{0:T(128)S(1)} %copy-done.37, s32[1,20,5]{2,1,0:T(8,128)S(1)} %copy-done.36, ...), custom_call_target="tpu_custom_call" | custom-call | flops 5368709120 | bytes 23101440 | tf_op jit(solution)/shard_map/attention_weights/pallas_call | solution.py:241
  169.9 2.0 copy-done.56
  172.4 1.7 collective-permute-start.24
  176.1 39.4 %mlp.1 = (bf16[1,640,1024]{2,1,0:T(8,128)(2,1)S(1)}, bf16[1,640,1024]{2,1,0:T(8,128)(2,1)}, bf16[2,640,1024]{2,1,0:T(8,128)(2,1)}, bf16[2560,1024]{1,0:T(8,128)(...) custom-call(s32[6]{0:T(128)S(1)} %copy-done.37, ...), custom_call_target="tpu_custom_call" | custom-call | flops 26843545600 | bytes 29417472 | tf_op jit(solution)/shard_map/mlp/pallas_call | solution.py:241
  216.2 3.6 %collective-permute-done.25.refs_1_ = bf16[1,640,1024]{2,1,0:T(8,128)(2,1)S(1)} collective-permute-done((bf16[1,640,1024]{2,1,0:T(8,128)(2,1)S(1)}, bf16[1,640,1024]{2,1,0:T(8,128)(2,1)S(1)}, u32[]{:S(2)}, u32[]{:S(2)}) %collective-permute-start.25) | collective-permute-done | bytes 1310752 | tf_op jit(solution)/shard_map/ppermute | solution.py:45
  219.8 1.7 copy-done.3
  223.0 1.3 collective-permute-start.30
  225.5 1.7 collective-permute-start.28
  227.9 2.1 copy-done.57
  230.0 2.5 copy-done.61
  232.5 15.7 %norm_backward.1 = (bf16[1,640,1024]{2,1,0:T(8,128)(2,1)S(1)}, bf16[1,640,1024]{2,1,0:T(8,128)(2,1)S(1)}, bf16[2,640,1024]{2,1,0:T(8,128)(2,1)S(1)}, f32[8,1024]{1,0:T(8,128)S(1)}) custom-call(s32[6]{0:T(128)S(1)} %copy-done.37, bf16[2560,768]{1,0:T(8,128)(2,1)S(1)} %copy-done.57, bf16[2560,1024]{1,0:T(8,128)(2,1)S(1)} %copy-done.61, ...), custom_call_target="tpu_custom_call" | custom-call | flops 9395240960 | bytes 23371776 | tf_op jit(solution)/shard_map/norm_backward/pallas_call | solution.py:241
  248.2 4.5 %collective-permute-done.28.refs_2_ = bf16[2,128,512]{2,1,0:T(8,128)(2,1)S(1)} collective-permute-done((bf16[2,128,512]{2,1,0:T(8,128)(2,1)}, bf16[2,128,512]{2,1,0:T(8,128)(2,1)S(1)}, u32[]{:S(2)}, u32[]{:S(2)}) %collective-permute-start.28) | collective-permute-done | bytes 262176 | tf_op jit(solution)/shard_map/ppermute | solution.py:45
  252.8 1.0 collective-permute-done.29.refs_5_.refs_6_
  253.8 1.0 collective-permute-done.31.refs_9_.refs_4_.refs_5_
  255.4 2.5 collective-permute-done.32.refs_1_
  258.3 1.5 collective-permute-start.41
  260.1 1.8 collective-permute-start.36
  262.6 1.3 copy-done.7
  263.9 3.7 %finish_output.1 = (f32[640,1024]{1,0:T(8,128)}, f32[16,1024]{1,0:T(8,128)S(1)}) custom-call(s32[6]{0:T(128)S(1)} %copy-done.37, f32[640,1024]{1,0:T(8,128)S(1)} %copy-done.2, bf16[640,1024]{1,0:T(8,128)(2,1)S(1)} %copy-done.1, bf16[2,640,1024]{2,1,0:T(8,128)(2,1)S(1)} %get-tuple-element.269.refs_0_, ...), custom_call_target="tpu_custom_call" | custom-call | flops 10485760 | bytes 17203200 | tf_op jit(solution)/shard_map/finish_output/pallas_call | solution.py:241
  267.6 1.3 collective-permute-done.34
  268.9 2.8 collective-permute-start.35
  271.7 4.9 %collective-permute-done.38.refs_7_ = bf16[1,128,512]{2,1,0:T(8,128)(2,1)S(1)} collective-permute-done((bf16[1,128,512]{2,1,0:T(8,128)(2,1)S(1)}, bf16[1,128,512]{2,1,0:T(8,128)(2,1)S(1)}, u32[]{:S(2)}, u32[]{:S(2)}) %collective-permute-start.38) | collective-permute-done | bytes 131104 | tf_op jit(solution)/shard_map/ppermute | solution.py:45
  276.6 1.4 collective-permute-done.36.refs_2_
  278.3 2.7 collective-permute-start.44
  281.3 1.7 collective-permute-start.39
  283.0 2.5 collective-permute-done.39
  285.6 1.3 collective-permute-start.40
  287.7 6.5 %collective-permute-done.40 = f32[16,1024]{1,0:T(8,128)S(1)} collective-permute-done((f32[16,1024]{1,0:T(8,128)S(1)}, f32[16,1024]{1,0:T(8,128)S(1)}, u32[]{:S(2)}, u32[]{:S(2)}) %collective-permute-start.40) | collective-permute-done | bytes 65568 | tf_op jit(solution)/shard_map/ppermute | solution.py:45
  294.2 2.9 finish_grad.1
  298.7 4.7 %collective-permute-done.45.refs_7_ = bf16[1,128,1024]{2,1,0:T(8,128)(2,1)S(1)} collective-permute-done((bf16[1,128,1024]{2,1,0:T(8,128)(2,1)S(1)}, bf16[1,128,1024]{2,1,0:T(8,128)(2,1)S(1)}, u32[]{:S(2)}, u32[]{:S(2)}) %collective-permute-start.45) | collective-permute-done | bytes 262176 | tf_op jit(solution)/shard_map/ppermute | solution.py:45
  303.3 1.2 finish_mlp_weights.1
  (212 shorter events, 24.7 us)
Async XLA Ops:
  0.6 25.7 %collective-permute-start = (bf16[640,1024]{1,0:T(8,128)(2,1)}, bf16[640,1024]{1,0:T(8,128)(2,1)}, u32[]{:S(2)}, u32[]{:S(2)}) collective-permute-start(bf16[640,1024]{1,0:T(8,128)(2,1)} %grad_ref.3), channel_id=1, source_target_pairs={{0,1},{1,0},{2,3},{3,2},{4,5},{5,4},{6,7},{7,6},{8,9},{9,8},{10,11... | collective-permute-start | bytes 3932168 | tf_op jit(solution)/shard_map/ppermute | solution.py:45
  5.8 11.2 %copy-start = (bf16[640,1024]{1,0:T(8,128)(2,1)S(1)}, bf16[640,1024]{1,0:T(8,128)(2,1)}, u32[]{:S(2)}) copy-start(bf16[640,1024]{1,0:T(8,128)(2,1)} %grad_ref.3) | copy-start | bytes 3932164
  5.8 32.3 %collective-permute-start.4 = (bf16[640,1024]{1,0:T(8,128)(2,1)}, bf16[640,1024]{1,0:T(8,128)(2,1)}, u32[]{:S(2)}, u32[]{:S(2)}) collective-permute-start(bf16[640,1024]{1,0:T(8,128)(2,1)} %get-tuple-element.217.refs_3_), channel_id=1, source_target_pairs={{0,2},{1,3},{2,0},{3,1},{4,6},{5,7},{6,4},{7,5},{8,10},{9,11},{10,... | collective-permute-start | bytes 3932168 | tf_op jit(solution)/shard_map/ppermute | solution.py:45
  8.4 29.7 %collective-permute-start.3 = (bf16[640,1024]{1,0:T(8,128)(2,1)}, bf16[640,1024]{1,0:T(8,128)(2,1)}, u32[]{:S(2)}, u32[]{:S(2)}) collective-permute-start(bf16[640,1024]{1,0:T(8,128)(2,1)} %get-tuple-element.217.refs_3_), channel_id=1, source_target_pairs={{0,1},{1,0},{2,3},{3,2},{4,5},{5,4},{6,7},{7,6},{8,9},{9,8},{10,11... | collective-permute-start | bytes 3932168 | tf_op jit(solution)/shard_map/ppermute | solution.py:45
  12.8 28.2 %copy-start.10 = (bf16[128,768]{1,0:T(8,128)(2,1)}, bf16[128,768]{1,0:T(8,128)(2,1)S(1)}, u32[]{:S(2)}) copy-start(bf16[128,768]{1,0:T(8,128)(2,1)S(1)} %get-tuple-element.218.refs_4_) | copy-start | bytes 589828
  12.8 31.4 %copy-start.16 = (bf16[128,256]{1,0:T(8,128)(2,1)}, bf16[128,256]{1,0:T(8,128)(2,1)S(1)}, u32[]{:S(2)}) copy-start(bf16[128,256]{1,0:T(8,128)(2,1)S(1)} %get-tuple-element.237.refs_6_.refs_0_) | copy-start | bytes 196612
  12.8 8.1 %collective-permute-start.2 = (bf16[128,256]{1,0:T(8,128)(2,1)S(1)}, bf16[128,256]{1,0:T(8,128)(2,1)S(1)}, u32[]{:S(2)}, u32[]{:S(2)}) collective-permute-start(bf16[128,256]{1,0:T(8,128)(2,1)S(1)} %get-tuple-element.237.refs_6_.refs_0_), channel_id=1, source_target_pairs={{0,4},{4,0},{8,12},{12,8},{16,20},{20,16},{24,28},{28,24},{1,5},{5... | collective-permute-start | bytes 196616 | tf_op jit(solution)/shard_map/ppermute | solution.py:45
  14.4 12.0 %collective-permute-start.1 = (bf16[128,768]{1,0:T(8,128)(2,1)S(1)}, bf16[128,768]{1,0:T(8,128)(2,1)S(1)}, u32[]{:S(2)}, u32[]{:S(2)}) collective-permute-start(bf16[128,768]{1,0:T(8,128)(2,1)S(1)} %get-tuple-element.218.refs_4_), channel_id=1, source_target_pairs={{0,16},{4,20},{8,24},{12,28},{16,0},{20,4},{24,8},{28,12},{1,17},{... | collective-permute-start | bytes 589832 | tf_op jit(solution)/shard_map/ppermute | solution.py:45
  18.8 15.6 %copy-start.65 = (f32[3072]{0:T(1024)S(1)}, f32[3072]{0:T(1024)}, u32[]{:S(2)}) copy-start(f32[3072]{0:T(1024)} %param.24) | copy-start | bytes 36868
  18.8 16.3 %copy-start.64 = (f32[4096]{0:T(1024)S(1)}, f32[4096]{0:T(1024)}, u32[]{:S(2)}) copy-start(f32[4096]{0:T(1024)} %param.28) | copy-start | bytes 49156
  20.9 23.3 %copy-start.18 = (bf16[128,256]{1,0:T(8,128)(2,1)}, bf16[128,256]{1,0:T(8,128)(2,1)S(1)}, u32[]{:S(2)}) copy-start(bf16[128,256]{1,0:T(8,128)(2,1)S(1)} %collective-permute-done.2.refs_7_.refs_1_) | copy-start | bytes 196612
  26.4 14.7 %copy-start.12 = (bf16[128,768]{1,0:T(8,128)(2,1)}, bf16[128,768]{1,0:T(8,128)(2,1)S(1)}, u32[]{:S(2)}) copy-start(bf16[128,768]{1,0:T(8,128)(2,1)S(1)} %collective-permute-done.1.refs_5_) | copy-start | bytes 589828
  26.4 11.7 %collective-permute-start.6 = (bf16[256,256]{1,0:T(8,128)(2,1)S(1)}, bf16[256,256]{1,0:T(8,128)(2,1)S(1)}, u32[]{:S(2)}, u32[]{:S(2)}) collective-permute-start(bf16[256,256]{1,0:T(8,128)(2,1)S(1)} %pad_maximum_fusion.7), channel_id=1, source_target_pairs={{0,16},{4,20},{8,24},{12,28},{16,0},{20,4},{24,8},{28,12},{1,17},{... | collective-permute-start | bytes 393224 | tf_op jit(solution)/shard_map/ppermute | solution.py:45
  26.5 14.5 %collective-permute-start.5 = (bf16[256,768]{1,0:T(8,128)(2,1)S(1)}, bf16[256,768]{1,0:T(8,128)(2,1)S(1)}, u32[]{:S(2)}, u32[]{:S(2)}) collective-permute-start(bf16[256,768]{1,0:T(8,128)(2,1)S(1)} %pad_maximum_fusion.5), channel_id=1, source_target_pairs={{0,8},{4,12},{8,0},{12,4},{16,24},{20,28},{24,16},{28,20},{1,9},{5... | collective-permute-start | bytes 1179656 | tf_op jit(solution)/shard_map/ppermute | solution.py:45
  38.1 24.3 %copy-start.20 = (bf16[256,256]{1,0:T(8,128)(2,1)}, bf16[256,256]{1,0:T(8,128)(2,1)S(1)}, u32[]{:S(2)}) copy-start(bf16[256,256]{1,0:T(8,128)(2,1)S(1)} %collective-permute-done.6.refs_8_.refs_2_) | copy-start | bytes 393220
  41.0 21.4 %copy-start.29 = (bf16[256,768]{1,0:T(8,128)(2,1)}, bf16[256,768]{1,0:T(8,128)(2,1)S(1)}, u32[]{:S(2)}) copy-start(bf16[256,768]{1,0:T(8,128)(2,1)S(1)} %collective-permute-done.5.refs_6_) | copy-start | bytes 1179652
  41.0 20.4 %collective-permute-start.7 = (bf16[640,1024]{1,0:T(8,128)(2,1)}, bf16[640,1024]{1,0:T(8,128)(2,1)S(1)}, u32[]{:S(2)}, u32[]{:S(2)}) collective-permute-start(bf16[640,1024]{1,0:T(8,128)(2,1)} %collective-permute-done.4.refs_2_), channel_id=1, source_target_pairs={{0,1},{1,0},{2,3},{3,2},{4,5},{5,4},{6,7},{7,6},{8,9},{9,8},{10,11... | collective-permute-start | bytes 3932168 | tf_op jit(solution)/shard_map/ppermute | solution.py:45
  41.1 20.0 %collective-permute-start.9 = (bf16[512,768]{1,0:T(8,128)(2,1)S(1)}, bf16[512,768]{1,0:T(8,128)(2,1)S(1)}, u32[]{:S(2)}, u32[]{:S(2)}) collective-permute-start(bf16[512,768]{1,0:T(8,128)(2,1)S(1)} %pad_maximum_fusion.2), channel_id=1, source_target_pairs={{0,4},{4,0},{8,12},{12,8},{16,20},{20,16},{24,28},{28,24},{1,5},{5... | collective-permute-start | bytes 2359304 | tf_op jit(solution)/shard_map/ppermute | solution.py:45
  41.7 19.8 %collective-permute-start.8 = (bf16[384,1024]{1,0:T(8,128)(2,1)S(1)}, bf16[384,1024]{1,0:T(8,128)(2,1)}, u32[]{:S(2)}, u32[]{:S(2)}) collective-permute-start(bf16[384,1024]{1,0:T(8,128)(2,1)S(1)} %copy-done.62), channel_id=1, source_target_pairs={{0,2},{1,3},{2,0},{3,1},{4,6},{5,7},{6,4},{7,5},{8,10},{9,11},{10,... | collective-permute-start | bytes 2359304 | tf_op jit(solution)/shard_map/ppermute | solution.py:45
  42.2 14.8 %collective-permute-start.11 = (bf16[128,1024]{1,0:T(8,128)(2,1)S(1)}, bf16[128,1024]{1,0:T(8,128)(2,1)S(1)}, u32[]{:S(2)}, u32[]{:S(2)}) collective-permute-start(bf16[128,1024]{1,0:T(8,128)(2,1)S(1)} %get-tuple-element.272.refs_10_.refs_8_), channel_id=1, source_target_pairs={{0,16},{4,20},{8,24},{12,28},{16,0},{20,4},{24,8},{28,12},{1,17},{... | collective-permute-start | bytes 786440 | tf_op jit(solution)/shard_map/ppermute | solution.py:45
  44.2 13.0 %collective-permute-start.10 = (bf16[512,256]{1,0:T(8,128)(2,1)S(1)}, bf16[512,256]{1,0:T(8,128)(2,1)S(1)}, u32[]{:S(2)}, u32[]{:S(2)}) collective-permute-start(bf16[512,256]{1,0:T(8,128)(2,1)S(1)} %pad_maximum_fusion.6), channel_id=1, source_target_pairs={{0,8},{4,12},{8,0},{12,4},{16,24},{20,28},{24,16},{28,20},{1,9},{5... | collective-permute-start | bytes 786440 | tf_op jit(solution)/shard_map/ppermute | solution.py:45
  61.4 21.1 %collective-permute-start.12 = (bf16[384,1024]{1,0:T(8,128)(2,1)}, bf16[384,1024]{1,0:T(8,128)(2,1)}, u32[]{:S(2)}, u32[]{:S(2)}) collective-permute-start(bf16[384,1024]{1,0:T(8,128)(2,1)} %collective-permute-done.8.refs_3_.refs_7_), channel_id=1, source_target_pairs={{0,1},{1,0},{2,3},{3,2},{4,5},{5,4},{6,7},{7,6},{8,9},{9,8},{10,11... | collective-permute-start | bytes 2359304 | tf_op jit(solution)/shard_map/ppermute | solution.py:45
  62.4 20.1 %collective-permute-start.14 = (bf16[256,1024]{1,0:T(8,128)(2,1)}, bf16[256,1024]{1,0:T(8,128)(2,1)}, u32[]{:S(2)}, u32[]{:S(2)}) collective-permute-start(bf16[256,1024]{1,0:T(8,128)(2,1)} %pad_maximum_fusion.3), channel_id=1, source_target_pairs={{0,8},{4,12},{8,0},{12,4},{16,24},{20,28},{24,16},{28,20},{1,9},{5... | collective-permute-start | bytes 1572872 | tf_op jit(solution)/shard_map/ppermute | solution.py:45
  62.8 19.8 %collective-permute-start.13 = (bf16[256,1024]{1,0:T(8,128)(2,1)}, bf16[256,1024]{1,0:T(8,128)(2,1)}, u32[]{:S(2)}, u32[]{:S(2)}) collective-permute-start(bf16[256,1024]{1,0:T(8,128)(2,1)} %slice.31), channel_id=1, source_target_pairs={{0,2},{1,3},{2,0},{3,1},{4,6},{5,7},{6,4},{7,5},{8,10},{9,11},{10,... | collective-permute-start | bytes 1572872 | tf_op jit(solution)/shard_map/ppermute | solution.py:45
  64.6 15.8 %collective-permute-start.15 = (bf16[128,1024]{1,0:T(8,128)(2,1)S(1)}, bf16[128,1024]{1,0:T(8,128)(2,1)}, u32[]{:S(2)}, u32[]{:S(2)}) collective-permute-start(bf16[128,1024]{1,0:T(8,128)(2,1)S(1)} %get-tuple-element.276.refs_14_), channel_id=1, source_target_pairs={{0,16},{4,20},{8,24},{12,28},{16,0},{20,4},{24,8},{28,12},{1,17},{... | collective-permute-start | bytes 786440 | tf_op jit(solution)/shard_map/ppermute | solution.py:45
  82.5 5.7 %collective-permute-start.16 = (bf16[256,1024]{1,0:T(8,128)(2,1)}, bf16[256,1024]{1,0:T(8,128)(2,1)S(1)}, u32[]{:S(2)}, u32[]{:S(2)}) collective-permute-start(bf16[256,1024]{1,0:T(8,128)(2,1)} %collective-permute-done.13.refs_4_.refs_8_), channel_id=1, source_target_pairs={{0,1},{1,0},{2,3},{3,2},{4,5},{5,4},{6,7},{7,6},{8,9},{9,8},{10,11... | collective-permute-start | bytes 1572872 | tf_op jit(solution)/shard_map/ppermute | solution.py:45
  83.6 14.4 %collective-permute-start.17 = (bf16[256,1024]{1,0:T(8,128)(2,1)S(1)}, bf16[256,1024]{1,0:T(8,128)(2,1)S(1)}, u32[]{:S(2)}, u32[]{:S(2)}) collective-permute-start(bf16[256,1024]{1,0:T(8,128)(2,1)S(1)} %pad_maximum_fusion.4), channel_id=1, source_target_pairs={{0,8},{4,12},{8,0},{12,4},{16,24},{20,28},{24,16},{28,20},{1,9},{5... | collective-permute-start | bytes 1572872 | tf_op jit(solution)/shard_map/ppermute | solution.py:45
  86.6 64.1 %collective-permute-start.18 = (bf16[512,1024]{1,0:T(8,128)(2,1)S(1)}, bf16[512,1024]{1,0:T(8,128)(2,1)S(1)}, u32[]{:S(2)}, u32[]{:S(2)}) collective-permute-start(bf16[512,1024]{1,0:T(8,128)(2,1)S(1)} %pad_maximum_fusion), channel_id=1, source_target_pairs={{0,4},{4,0},{8,12},{12,8},{16,20},{20,16},{24,28},{28,24},{1,5},{5... | collective-permute-start | bytes 3145736 | tf_op jit(solution)/shard_map/ppermute | solution.py:45
  88.3 69.1 %copy-start.22 = (bf16[256,1024]{1,0:T(8,128)(2,1)}, bf16[256,1024]{1,0:T(8,128)(2,1)S(1)}, u32[]{:S(2)}) copy-start(bf16[256,1024]{1,0:T(8,128)(2,1)S(1)} %collective-permute-done.16.refs_1_.refs_5_) | copy-start | bytes 1572868
  88.3 12.5 %copy-start.58 = (bf16[2560,256]{1,0:T(8,128)(2,1)S(1)}, bf16[2560,256]{1,0:T(8,128)(2,1)}, u32[]{:S(2)}) copy-start(bf16[2560,256]{1,0:T(8,128)(2,1)} %get-tuple-element.233.q_ref) | copy-start | bytes 3932164
  88.3 12.5 %copy-start.59 = (bf16[2560,256]{1,0:T(8,128)(2,1)S(1)}, bf16[2560,256]{1,0:T(8,128)(2,1)}, u32[]{:S(2)}) copy-start(bf16[2560,256]{1,0:T(8,128)(2,1)} %get-tuple-element.244.k_ref) | copy-start | bytes 3932164
  88.3 12.5 %copy-start.60 = (bf16[2560,256]{1,0:T(8,128)(2,1)S(1)}, bf16[2560,256]{1,0:T(8,128)(2,1)}, u32[]{:S(2)}) copy-start(bf16[2560,256]{1,0:T(8,128)(2,1)} %get-tuple-element.245.v_ref) | copy-start | bytes 3932164
  93.8 7.1 %copy-start.14 = (f32[1280,128]{1,0:T(8,128)S(1)}, f32[1280,128]{1,0:T(8,128)}, u32[]{:S(2)}) copy-start(f32[1280,128]{1,0:T(8,128)} %get-tuple-element.224.refs_12_.sine.refs_13_) | copy-start | bytes 1966084
  93.8 7.1 %copy-start.15 = (f32[1280,128]{1,0:T(8,128)S(1)}, f32[1280,128]{1,0:T(8,128)}, u32[]{:S(2)}) copy-start(f32[1280,128]{1,0:T(8,128)} %get-tuple-element.223.refs_11_.cos.refs_12_) | copy-start | bytes 1966084
  98.1 52.7 %copy-start.26 = (bf16[256,1024]{1,0:T(8,128)(2,1)}, bf16[256,1024]{1,0:T(8,128)(2,1)S(1)}, u32[]{:S(2)}) copy-start(bf16[256,1024]{1,0:T(8,128)(2,1)S(1)} %collective-permute-done.17.refs_16_) | copy-start | bytes 1572868
  99.2 52.5 %collective-permute-start.19 = (bf16[512,1024]{1,0:T(8,128)(2,1)S(1)}, bf16[512,1024]{1,0:T(8,128)(2,1)S(1)}, u32[]{:S(2)}, u32[]{:S(2)}) collective-permute-start(bf16[512,1024]{1,0:T(8,128)(2,1)S(1)} %pad_maximum_fusion.1), channel_id=1, source_target_pairs={{0,4},{4,0},{8,12},{12,8},{16,20},{20,16},{24,28},{28,24},{1,5},{5... | collective-permute-start | bytes 3145736 | tf_op jit(solution)/shard_map/ppermute | solution.py:45
  156.8 15.1 %collective-permute-start.20 = (bf16[1,640,1024]{2,1,0:T(8,128)(2,1)S(1)}, bf16[1,640,1024]{2,1,0:T(8,128)(2,1)S(1)}, u32[]{:S(2)}, u32[]{:S(2)}) collective-permute-start(bf16[1,640,1024]{2,1,0:T(8,128)(2,1)S(1)} %get-tuple-element.266), channel_id=1, source_target_pairs={{0,1},{1,0},{2,3},{3,2},{4,5},{5,4},{6,7},{7,6},{8,9},{9,8},{10,11... | collective-permute-start | bytes 3932168 | tf_op jit(solution)/shard_map/ppermute | solution.py:45
  156.9 15.0 %collective-permute-start.21 = (bf16[1,640,1024]{2,1,0:T(8,128)(2,1)S(1)}, bf16[1,640,1024]{2,1,0:T(8,128)(2,1)S(1)}, u32[]{:S(2)}, u32[]{:S(2)}) collective-permute-start(bf16[1,640,1024]{2,1,0:T(8,128)(2,1)S(1)} %get-tuple-element.267), channel_id=1, source_target_pairs={{0,1},{1,0},{2,3},{3,2},{4,5},{5,4},{6,7},{7,6},{8,9},{9,8},{10,11... | collective-permute-start | bytes 3932168 | tf_op jit(solution)/shard_map/ppermute | solution.py:45
  171.9 43.6 %collective-permute-start.23 = (bf16[4,128,512]{2,1,0:T(8,128)(2,1)}, bf16[4,128,512]{2,1,0:T(8,128)(2,1)S(1)}, u32[]{:S(2)}, u32[]{:S(2)}) collective-permute-start(bf16[4,128,512]{2,1,0:T(8,128)(2,1)} %get-tuple-element.291), channel_id=1, source_target_pairs={{0,4},{4,0},{8,12},{12,8},{16,20},{20,16},{24,28},{28,24},{1,5},{5... | collective-permute-start | bytes 1572872 | tf_op jit(solution)/shard_map/ppermute | solution.py:45
  172.4 43.1 %collective-permute-start.24 = (bf16[4,128,512]{2,1,0:T(8,128)(2,1)}, bf16[4,128,512]{2,1,0:T(8,128)(2,1)S(1)}, u32[]{:S(2)}, u32[]{:S(2)}) collective-permute-start(bf16[4,128,512]{2,1,0:T(8,128)(2,1)} %get-tuple-element.292), channel_id=1, source_target_pairs={{0,8},{4,12},{8,0},{12,4},{16,24},{20,28},{24,16},{28,20},{1,9},{5... | collective-permute-start | bytes 1572872 | tf_op jit(solution)/shard_map/ppermute | solution.py:45
  174.6 41.0 %collective-permute-start.22 = (bf16[1,640,1024]{2,1,0:T(8,128)(2,1)S(1)}, bf16[1,640,1024]{2,1,0:T(8,128)(2,1)S(1)}, u32[]{:S(2)}, u32[]{:S(2)}) collective-permute-start(bf16[1,640,1024]{2,1,0:T(8,128)(2,1)S(1)} %add_terms.3), channel_id=1, source_target_pairs={{0,2},{1,3},{2,0},{3,1},{4,6},{5,7},{6,4},{7,5},{8,10},{9,11},{10,... | collective-permute-start | bytes 3932168 | tf_op jit(solution)/shard_map/ppermute | solution.py:45
  215.6 4.2 %collective-permute-start.25 = (bf16[1,640,1024]{2,1,0:T(8,128)(2,1)S(1)}, bf16[1,640,1024]{2,1,0:T(8,128)(2,1)S(1)}, u32[]{:S(2)}, u32[]{:S(2)}) collective-permute-start(bf16[1,640,1024]{2,1,0:T(8,128)(2,1)S(1)} %get-tuple-element.295), channel_id=1, source_target_pairs={{0,1},{1,0},{2,3},{3,2},{4,5},{5,4},{6,7},{7,6},{8,9},{9,8},{10,11... | collective-permute-start | bytes 3932168 | tf_op jit(solution)/shard_map/ppermute | solution.py:45
  215.7 11.5 %collective-permute-start.26 = (bf16[1,640,1024]{2,1,0:T(8,128)(2,1)}, bf16[1,640,1024]{2,1,0:T(8,128)(2,1)S(1)}, u32[]{:S(2)}, u32[]{:S(2)}) collective-permute-start(bf16[1,640,1024]{2,1,0:T(8,128)(2,1)} %get-tuple-element.297), channel_id=1, source_target_pairs={{0,1},{1,0},{2,3},{3,2},{4,5},{5,4},{6,7},{7,6},{8,9},{9,8},{10,11... | collective-permute-start | bytes 3932168 | tf_op jit(solution)/shard_map/ppermute | solution.py:45
  222.2 32.7 %collective-permute-start.27 = (bf16[1,640,1024]{2,1,0:T(8,128)(2,1)S(1)}, bf16[1,640,1024]{2,1,0:T(8,128)(2,1)S(1)}, u32[]{:S(2)}, u32[]{:S(2)}) collective-permute-start(bf16[1,640,1024]{2,1,0:T(8,128)(2,1)S(1)} %add_terms.4), channel_id=1, source_target_pairs={{0,2},{1,3},{2,0},{3,1},{4,6},{5,7},{6,4},{7,5},{8,10},{9,11},{10,... | collective-permute-start | bytes 3932168 | tf_op jit(solution)/shard_map/ppermute | solution.py:45
  223.0 30.8 %collective-permute-start.30 = (bf16[4,128,1024]{2,1,0:T(8,128)(2,1)}, bf16[4,128,1024]{2,1,0:T(8,128)(2,1)S(1)}, u32[]{:S(2)}, u32[]{:S(2)}) collective-permute-start(bf16[4,128,1024]{2,1,0:T(8,128)(2,1)} %get-tuple-element.310), channel_id=1, source_target_pairs={{0,4},{4,0},{8,12},{12,8},{16,20},{20,16},{24,28},{28,24},{1,5},{5... | collective-permute-start | bytes 3145736 | tf_op jit(solution)/shard_map/ppermute | solution.py:45
  224.4 30.5 %collective-permute-start.31 = (bf16[4,128,1024]{2,1,0:T(8,128)(2,1)}, bf16[4,128,1024]{2,1,0:T(8,128)(2,1)S(1)}, u32[]{:S(2)}, u32[]{:S(2)}) collective-permute-start(bf16[4,128,1024]{2,1,0:T(8,128)(2,1)} %get-tuple-element.311), channel_id=1, source_target_pairs={{0,8},{4,12},{8,0},{12,4},{16,24},{20,28},{24,16},{28,20},{1,9},{5... | collective-permute-start | bytes 3145736 | tf_op jit(solution)/shard_map/ppermute | solution.py:45
  225.5 27.2 %collective-permute-start.28 = (bf16[2,128,512]{2,1,0:T(8,128)(2,1)}, bf16[2,128,512]{2,1,0:T(8,128)(2,1)S(1)}, u32[]{:S(2)}, u32[]{:S(2)}) collective-permute-start(bf16[2,128,512]{2,1,0:T(8,128)(2,1)} %get-tuple-element.308), channel_id=1, source_target_pairs={{0,16},{4,20},{8,24},{12,28},{16,0},{20,4},{24,8},{28,12},{1,17},{... | collective-permute-start | bytes 786440 | tf_op jit(solution)/shard_map/ppermute | solution.py:45
  227.2 26.6 %collective-permute-start.29 = (bf16[2,128,512]{2,1,0:T(8,128)(2,1)}, bf16[2,128,512]{2,1,0:T(8,128)(2,1)S(1)}, u32[]{:S(2)}, u32[]{:S(2)}) collective-permute-start(bf16[2,128,512]{2,1,0:T(8,128)(2,1)} %get-tuple-element.309), channel_id=1, source_target_pairs={{0,4},{4,0},{8,12},{12,8},{16,20},{20,16},{24,28},{28,24},{1,5},{5... | collective-permute-start | bytes 786440 | tf_op jit(solution)/shard_map/ppermute | solution.py:45
  254.8 3.0 collective-permute-start.32
  254.8 7.7 %collective-permute-start.33 = (bf16[1,640,1024]{2,1,0:T(8,128)(2,1)S(1)}, bf16[1,640,1024]{2,1,0:T(8,128)(2,1)S(1)}, u32[]{:S(2)}, u32[]{:S(2)}) collective-permute-start(bf16[1,640,1024]{2,1,0:T(8,128)(2,1)S(1)} %get-tuple-element.315), channel_id=1, source_target_pairs={{0,1},{1,0},{2,3},{3,2},{4,5},{5,4},{6,7},{7,6},{8,9},{9,8},{10,11... | collective-permute-start | bytes 3932168 | tf_op jit(solution)/shard_map/ppermute | solution.py:45
  258.3 35.9 %collective-permute-start.41 = (bf16[1,640,1024]{2,1,0:T(8,128)(2,1)S(1)}, bf16[1,640,1024]{2,1,0:T(8,128)(2,1)S(1)}, u32[]{:S(2)}, u32[]{:S(2)}) collective-permute-start(bf16[1,640,1024]{2,1,0:T(8,128)(2,1)S(1)} %add_terms.5), channel_id=1, source_target_pairs={{0,2},{1,3},{2,0},{3,1},{4,6},{5,7},{6,4},{7,5},{8,10},{9,11},{10,... | collective-permute-start | bytes 3932168 | tf_op jit(solution)/shard_map/ppermute | solution.py:45
  260.1 18.0 %collective-permute-start.36 = (bf16[2,128,1024]{2,1,0:T(8,128)(2,1)S(1)}, bf16[2,128,1024]{2,1,0:T(8,128)(2,1)S(1)}, u32[]{:S(2)}, u32[]{:S(2)}) collective-permute-start(bf16[2,128,1024]{2,1,0:T(8,128)(2,1)S(1)} %get-tuple-element.332), channel_id=1, source_target_pairs={{0,8},{4,12},{8,0},{12,4},{16,24},{20,28},{24,16},{28,20},{1,9},{5... | collective-permute-start | bytes 1572872 | tf_op jit(solution)/shard_map/ppermute | solution.py:45
  261.9 16.2 %collective-permute-start.37 = (bf16[2,128,1024]{2,1,0:T(8,128)(2,1)S(1)}, bf16[2,128,1024]{2,1,0:T(8,128)(2,1)S(1)}, u32[]{:S(2)}, u32[]{:S(2)}) collective-permute-start(bf16[2,128,1024]{2,1,0:T(8,128)(2,1)S(1)} %get-tuple-element.333), channel_id=1, source_target_pairs={{0,4},{4,0},{8,12},{12,8},{16,20},{20,16},{24,28},{28,24},{1,5},{5... | collective-permute-start | bytes 1572872 | tf_op jit(solution)/shard_map/ppermute | solution.py:45
  262.4 14.2 %collective-permute-start.38 = (bf16[1,128,512]{2,1,0:T(8,128)(2,1)S(1)}, bf16[1,128,512]{2,1,0:T(8,128)(2,1)S(1)}, u32[]{:S(2)}, u32[]{:S(2)}) collective-permute-start(bf16[1,128,512]{2,1,0:T(8,128)(2,1)S(1)} %get-tuple-element.334), channel_id=1, source_target_pairs={{0,16},{4,20},{8,24},{12,28},{16,0},{20,4},{24,8},{28,12},{1,17},{... | collective-permute-start | bytes 393224 | tf_op jit(solution)/shard_map/ppermute | solution.py:45
  267.6 1.3 collective-permute-start.34
  268.9 9.2 %collective-permute-start.35 = (f32[16,1024]{1,0:T(8,128)S(1)}, f32[16,1024]{1,0:T(8,128)S(1)}, u32[]{:S(2)}, u32[]{:S(2)}) collective-permute-start(f32[16,1024]{1,0:T(8,128)S(1)} %add.41), channel_id=1, source_target_pairs={{0,16},{4,20},{8,24},{12,28},{16,0},{20,4},{24,8},{28,12},{1,17},{... | collective-permute-start | bytes 196616 | tf_op jit(solution)/shard_map/ppermute | solution.py:45
  278.1 16.1 %copy-start.5 = (f32[640,1024]{1,0:T(8,128)S(1)}, f32[640,1024]{1,0:T(8,128)}, u32[]{:S(2)}) copy-start(f32[640,1024]{1,0:T(8,128)} %get-tuple-element.343.norm_ref) | copy-start | bytes 7864324
  278.1 16.1 %copy-start.31 = (f32[640,1]{1,0:T(8,128)S(1)}, f32[640,1]{1,0:T(8,128)}, u32[]{:S(2)}) copy-start(f32[640,1]{1,0:T(8,128)} %get-tuple-element.344.std_ref) | copy-start | bytes 7684
  278.3 20.4 %collective-permute-start.44 = (bf16[1,128,1024]{2,1,0:T(8,128)(2,1)S(1)}, bf16[1,128,1024]{2,1,0:T(8,128)(2,1)S(1)}, u32[]{:S(2)}, u32[]{:S(2)}) collective-permute-start(bf16[1,128,1024]{2,1,0:T(8,128)(2,1)S(1)} %get-tuple-element.353), channel_id=1, source_target_pairs={{0,16},{4,20},{8,24},{12,28},{16,0},{20,4},{24,8},{28,12},{1,17},{... | collective-permute-start | bytes 786440 | tf_op jit(solution)/shard_map/ppermute | solution.py:45
  281.0 22.3 %collective-permute-start.45 = (bf16[1,128,1024]{2,1,0:T(8,128)(2,1)S(1)}, bf16[1,128,1024]{2,1,0:T(8,128)(2,1)S(1)}, u32[]{:S(2)}, u32[]{:S(2)}) collective-permute-start(bf16[1,128,1024]{2,1,0:T(8,128)(2,1)S(1)} %get-tuple-element.354), channel_id=1, source_target_pairs={{0,16},{4,20},{8,24},{12,28},{16,0},{20,4},{24,8},{28,12},{1,17},{... | collective-permute-start | bytes 786440 | tf_op jit(solution)/shard_map/ppermute | solution.py:45
  281.3 4.3 %collective-permute-start.39 = (f32[16,1024]{1,0:T(8,128)S(1)}, f32[16,1024]{1,0:T(8,128)S(1)}, u32[]{:S(2)}, u32[]{:S(2)}) collective-permute-start(f32[16,1024]{1,0:T(8,128)S(1)} %add.42), channel_id=1, source_target_pairs={{0,4},{4,0},{8,12},{12,8},{16,20},{20,16},{24,28},{28,24},{1,5},{5... | collective-permute-start | bytes 196616 | tf_op jit(solution)/shard_map/ppermute | solution.py:45
  285.6 8.6 %collective-permute-start.40 = (f32[16,1024]{1,0:T(8,128)S(1)}, f32[16,1024]{1,0:T(8,128)S(1)}, u32[]{:S(2)}, u32[]{:S(2)}) collective-permute-start(f32[16,1024]{1,0:T(8,128)S(1)} %add.43), channel_id=1, source_target_pairs={{0,8},{4,12},{8,0},{12,4},{16,24},{20,28},{24,16},{28,20},{1,9},{5... | collective-permute-start | bytes 196616 | tf_op jit(solution)/shard_map/ppermute | solution.py:45
  286.9 10.9 %collective-permute-start.43 = (bf16[1,128,512]{2,1,0:T(8,128)(2,1)S(1)}, bf16[1,128,512]{2,1,0:T(8,128)(2,1)S(1)}, u32[]{:S(2)}, u32[]{:S(2)}) collective-permute-start(bf16[1,128,512]{2,1,0:T(8,128)(2,1)S(1)} %get-tuple-element.349), channel_id=1, source_target_pairs={{0,8},{4,12},{8,0},{12,4},{16,24},{20,28},{24,16},{28,20},{1,9},{5... | collective-permute-start | bytes 393224 | tf_op jit(solution)/shard_map/ppermute | solution.py:45
  297.1 7.4 %collective-permute-start.42 = (f32[16,1024]{1,0:T(8,128)S(1)}, f32[16,1024]{1,0:T(8,128)S(1)}, u32[]{:S(2)}, u32[]{:S(2)}) collective-permute-start(f32[16,1024]{1,0:T(8,128)S(1)} %add.44), channel_id=1, source_target_pairs={{0,2},{1,3},{2,0},{3,1},{4,6},{5,7},{6,4},{7,5},{8,10},{9,11},{10,... | collective-permute-start | bytes 196616 | tf_op jit(solution)/shard_map/ppermute | solution.py:45
  (48 other events, 165.3 us)

commit v14 on v13

--- a/solution.py
+++ b/solution.py
@@ -323,14 +323,14 @@
     rows, model = stream.shape
     block = 160
 
-    def kernel(stream_ref, sent_ref, norm_ref, std_ref):
+    def kernel(stream_ref, sent_ref, mean_ref, std_ref):
         field = stream_ref[...]
-        centred = field - jnp.sum(field, axis=1, keepdims=True) / model
+        mean = jnp.sum(field, axis=1, keepdims=True) / model
+        centred = field - mean
         variance = jnp.sum(centred * centred, axis=1, keepdims=True) / model
         scale = lax.rsqrt(variance + eps_norm)
-        norm = centred * scale
-        norm_ref[...] = norm
-        sent_ref[...] = norm.astype(bf16)
+        sent_ref[...] = (centred * scale).astype(bf16)
+        mean_ref[...] = mean
         std_ref[...] = scale
 
     return call(
@@ -340,8 +340,8 @@
         [],
         [stream],
         [step_block(block, model)],
-        [shaped(rows, model), shaped(rows, model, dtype=f32), shaped(rows, 1, dtype=f32)],
-        [step_block(block, model), step_block(block, model), step_block(block, 1)],
+        [shaped(rows, model), shaped(rows, 1, dtype=f32), shaped(rows, 1, dtype=f32)],
+        [step_block(block, model), step_block(block, 1), step_block(block, 1)],
         [],
         rows * model * 8,
         room=62,
@@ -454,16 +454,14 @@
     tree, step = pl.program_id(0), pl.program_id(1)
     width = q_ref.shape[1]
     heads = width // HD
-    lane_head = lax.broadcasted_iota(jnp.int32, (SEG, width), 1) // HD
+    both = 2 * SEG
+    lane_head = lax.broadcasted_iota(jnp.int32, (both, width), 1) // HD
 
     @pl.when(step == 0)
     def _():
         dk_sum[...] = jnp.zeros_like(dk_sum)
         dv_sum[...] = jnp.zeros_like(dv_sum)
 
-    first, second = info[tree, step, 0], info[tree, step, 1]
-    first_rows = pl.ds(pl.multiple_of(first * SEG, SEG), SEG)
-    second_rows = pl.ds(pl.multiple_of(second * SEG, SEG), SEG)
     queries, grads = q_ref[...], do_ref[...]
     zero = jnp.zeros_like(queries)
     q_rows = jnp.concatenate([jnp.where(lane_head == h, queries, zero) for h in range(heads)], axis=0)
@@ -472,14 +470,32 @@
     ahead = lax.broadcasted_iota(jnp.int32, (SEG, SEG), 1) - lax.broadcasted_iota(
         jnp.int32, (SEG, SEG), 0
     )
-    seen = jnp.concatenate([ahead <= info[tree, step, 2], ahead <= info[tree, step, 3]], axis=1)
-    seen = jnp.concatenate([seen] * heads, axis=0)
-    k_near = jnp.concatenate([k_ref[first_rows, :], k_ref[second_rows, :]], axis=0)
-    v_near = jnp.concatenate([v_ref[first_rows, :], v_ref[second_rows, :]], axis=0)
+    blocks = []
+    for at in range(2):
+        number = step * 2 + at
+        first, second = info[tree, number, 0], info[tree, number, 1]
+        rows = [pl.ds(pl.multiple_of(x * SEG, SEG), SEG) for x in (first, second)]
+        seen = [ahead <= info[tree, number, 2], ahead <= info[tree, number, 3]]
+        seen = jnp.concatenate([jnp.concatenate(seen, axis=1)] * heads, axis=0)
+        k_near = jnp.concatenate([k_ref[x, :] for x in rows], axis=0)
+        v_near = jnp.concatenate([v_ref[x, :] for x in rows], axis=0)
+        blocks.append((first, second, seen, k_near, v_near))
+
+    def of_block(stack, at):
+        cuts = [stack[h * both + at * SEG : h * both + (at + 1) * SEG] for h in range(heads)]
+        return jnp.concatenate(cuts, axis=0)
+
+    def by_block(parts):
+        cuts = [x[h * SEG : (h + 1) * SEG] for h in range(heads) for x in parts]
+        return jnp.concatenate(cuts, axis=0)
 
     def work(pairs):
-        count = pairs * 2 * SEG
-        near = jnp.where(seen, dot_nt(q_rows, k_near), masked_score)
+        count = pairs * both
+        near = [
+            jnp.where(seen, dot_nt(of_block(q_rows, at), k_near), masked_score)
+            for at, (_, _, seen, k_near, _) in enumerate(blocks)
+        ]
+        near = by_block(near)
         most = jnp.max(near, axis=1, keepdims=True)
         if count:
             k_far, v_far = k_ref[0:count, :], v_ref[0:count, :]
@@ -493,33 +509,41 @@
         scale = 1.0 / total
         near = near * scale
         near_low = near.astype(bf16)
-        context = dot_nn(near_low, v_near)
+        context = by_block([dot_nn(of_block(near_low, at), x[4]) for at, x in enumerate(blocks)])
         if count:
             far = far * scale
             far_low = far.astype(bf16)
             context = context + dot_nn(far_low, v_far)
         delta = jnp.sum(context * g_rows.astype(f32), axis=1, keepdims=True)
-        near = (near * (dot_nt(g_rows, v_near) - delta)).astype(bf16)
-        dq = dot_nn(near, k_near)
+        slope = by_block([dot_nt(of_block(g_rows, at), x[4]) for at, x in enumerate(blocks)])
+        near = (near * (slope - delta)).astype(bf16)
+        dq = by_block([dot_nn(of_block(near, at), x[3]) for at, x in enumerate(blocks)])
         if count:
             far = (far * (dot_nt(g_rows, v_far) - delta)).astype(bf16)
             dq = dq + dot_nn(far, k_far)
-        ctx_own, dq_own = context[0:SEG], dq[0:SEG]
+        ctx_own, dq_own = context[0:both], dq[0:both]
         for h in range(1, heads):
-            ctx_own = jnp.where(lane_head == h, context[h * SEG : (h + 1) * SEG], ctx_own)
-            dq_own = jnp.where(lane_head == h, dq[h * SEG : (h + 1) * SEG], dq_own)
+            ctx_own = jnp.where(lane_head == h, context[h * both : (h + 1) * both], ctx_own)
+            dq_own = jnp.where(lane_head == h, dq[h * both : (h + 1) * both], dq_own)
         ctx_ref[...] = ctx_own.astype(bf16)
-        dq_ref[...] = turn(dq_own * HD**-0.5, cos, sine, -1.0).astype(bf16)
+        for at in range(2):
+            table = pl.ds(pl.multiple_of(info[tree, step * 2 + at, 4] * SEG, SEG), SEG)
+            own = slice(at * SEG, (at + 1) * SEG)
+            turned = turn(dq_own[own] * HD**-0.5, cos[table, :], sine[table, :], -1.0)
+            dq_ref[own, :] = turned.astype(bf16)
         for h in range(heads):
-            own = slice(h * SEG, (h + 1) * SEG)
             part = slice(h * HD, (h + 1) * HD)
-            dk = dot_nn(q_turned[part], near[own])
-            dv = dot_nn(g_turned[part], near_low[own])
-            dk_sum[first, part, :] += dk[:, :SEG]
-            dv_sum[first, part, :] += dv[:, :SEG]
-            dk_sum[second, part, :] += dk[:, SEG:]
-            dv_sum[second, part, :] += dv[:, SEG:]
+            for at, (first, second, *_) in enumerate(blocks):
+                own = slice(h * both + at * SEG, h * both + (at + 1) * SEG)
+                columns = slice(at * SEG, (at + 1) * SEG)
+                dk = dot_nn(q_turned[part, columns], near[own])
+                dv = dot_nn(g_turned[part, columns], near_low[own])
+                dk_sum[first, part, :] += dk[:, :SEG]
+                dv_sum[first, part, :] += dv[:, :SEG]
+                dk_sum[second, part, :] += dk[:, SEG:]
+                dv_sum[second, part, :] += dv[:, SEG:]
             if count:
+                own = slice(h * both, (h + 1) * both)
                 dk = dot_nn(q_turned[part], far[own])
                 dv = dot_nn(g_turned[part], far_low[own])
                 for j in range(2 * pairs):
@@ -528,15 +552,15 @@
 
     for pairs in range(NT // 2):
 
-        @pl.when(step // 2 == pairs)
+        @pl.when(step == pairs)
         def _(pairs=pairs):
             work(pairs)
 
-    @pl.when(step >= NT)
+    @pl.when(step >= NT // 2)
     def _():
         work(NT // 2)
 
-    @pl.when(step == NB - 1)
+    @pl.when(step == NB // 2 - 1)
     def _():
         def finish(j, carry):
             rows = pl.ds(pl.multiple_of(j * SEG, SEG), SEG)
@@ -550,24 +574,22 @@
 def attention(info, tables, queries, keys, values, grads):
     total, width = queries.shape
     trees = total // TREE
-    table_width = tables[0].shape[1]
-    block = pl.BlockSpec((SEG, width), lambda t, b, info: (t * NB + b, 0))
+    block = pl.BlockSpec((2 * SEG, width), lambda t, b, info: (t * NB // 2 + b, 0))
     whole = pl.BlockSpec((TREE, width), lambda t, b, info: (t, 0))
-    table = pl.BlockSpec((SEG, table_width), lambda t, b, info: (info[t, b, 4], 0))
     scores = trees * (TREE - TRUNK) * (TRUNK + 2 * SEG) * (width // HD)
     return call(
         attention_kernel,
         "attention",
-        (trees, NB),
+        (trees, NB // 2),
         [info],
         [queries, grads, keys, values, *tables],
-        [block, block, whole, whole, table, table],
+        [block, block, whole, whole] + [resident(x.shape) for x in tables],
         [shaped(total, width)] * 4,
         [block, block, whole, whole],
         [pltpu.VMEM((NB, width, SEG), f32), pltpu.VMEM((NB, width, SEG), f32)],
         scores * width * 2 * 6 * 1.3,
         scores,
-        room=22,
+        room=20,
     )
 
 
@@ -1003,26 +1025,27 @@
     )
 
 
-def finish_grad(grad, normalized, inv_std, terms):
+def finish_grad(grad, stream, row_mean, inv_std, terms):
     rows, model = grad.shape
     block = 160
 
-    def kernel(grad_ref, norm_ref, std_ref, *refs):
+    def kernel(grad_ref, stream_ref, mean_ref, std_ref, *refs):
         term_refs, out_ref = refs[:-1], refs[-1]
         sent = sum(x[...].astype(f32) for x in term_refs)
-        norm = norm_ref[...]
+        norm = (stream_ref[...] - mean_ref[...]) * std_ref[...]
         mean = jnp.sum(sent, axis=1, keepdims=True) / model
         cross = jnp.sum(sent * norm, axis=1, keepdims=True) / model
         out_ref[...] = grad_ref[...].astype(f32) + std_ref[...] * (sent - mean - norm * cross)
 
-    operands = [grad, normalized, inv_std, *[x for x, _ in terms]]
+    operands = [grad, stream, row_mean, inv_std, *[x for x, _ in terms]]
     return call(
         kernel,
         "finish_grad",
         (rows // block,),
         [],
         operands,
-        [step_block(block, model), step_block(block, model), step_block(block, 1)]
+        [step_block(block, model)] * 2
+        + [step_block(block, 1)] * 2
         + taken(terms, block),
         [shaped(rows, model, dtype=f32)],
         [step_block(block, model)],
@@ -1137,7 +1160,7 @@
     fc_pack = Pack(blocks[2], "dp", rows_first)
     out_pack = Pack(blocks[3], "dp", rows_first)
 
-    sent_norm, normalized, inv_std = normalize(stream_in)
+    sent_norm, row_mean, inv_std = normalize(stream_in)
     sent = gather_far(sent_norm, "tensor", tensor_bits)
 
     info = tree_table(segment_ids, parent_ids)
@@ -1276,7 +1299,7 @@
         sums = sums + swap(sums, "dp", bit)
     sums, back_parts.got = tie(sums, back_parts.got)
     back_parts.add()
-    stream_grad = finish_grad(out_grad, normalized, inv_std, back_parts.terms)
+    stream_grad = finish_grad(out_grad, stream_in, row_mean, inv_std, back_parts.terms)
     sums, stream_grad = tie(sums, stream_grad)
     for bit in tensor_bits[1:]:
         sums = sums + swap(sums, "tensor", bit)

time: 309 us -> 317 us (1.026)
  Pallas kernels: 157 us -> 166 us
    pallas_call x19, Pallas kernels: 154 us -> 164 us  [call(): pl.pallas_call(kernel, grid_spec=pltpu.PrefetchScalarGridSpec(num_scalar_...]
  transfers between devices with their start and end apart: 46 -> 46, of which waited for: 21 -> 21; matrix products, arithmetic and copies ran while one was open for 4% -> 4% of each run, Pallas kernels for 50% -> 51%
where the time goes in v14:
time: 317 us; the launch traced here: 318 us
  Pallas kernels  166 us (52%)
  waiting for transfers between devices  69 us (22%)
  starting transfers between devices  49.3 us (16%)
  local copies, waits for them, and re-layouts  22.6 us (7%)
  other arithmetic  8.77 us (3%)
    pallas_call x19, Pallas kernels, call(): pl.pallas_call(kernel, grid_spec=pltpu.PrefetchScalarGridSpec(num_scalar_...  164 us
    ppermute x46, waiting for transfers between devices, swap(): return lax.ppermute(block, axis, [(i, i ^ bit) for i in range(size)])  69 us
    ppermute x46, starting transfers between devices, swap(): return lax.ppermute(block, axis, [(i, i ^ bit) for i in range(size)])  49.3 us
    unnamed x135, local copies, waits for them, and re-layouts  17.6 us
  transfers between devices with their start and end apart: 46, of which 21 were waited for; matrix products, arithmetic and copies ran while one was open for 4% of the time, Pallas kernels for 51%

profile of v14, /device:TPU:0, one launch (start us, length us, event | category | flops | bytes accessed | tf_op | source)
XLA Modules:
  0.0 317.5 jit_solution(225350055654660765)
XLA Ops:
  1.2 4.2 %normalize.1 = (bf16[640,1024]{1,0:T(8,128)(2,1)}, f32[640,1]{1,0:T(8,128)}, f32[640,1]{1,0:T(8,128)}) custom-call(f32[640,1024]{1,0:T(8,128)} %stream_ref.3), custom_call_target="tpu_custom_call" | custom-call | flops 5242880 | bytes 3937280 | tf_op jit(solution)/shard_map/normalize/pallas_call | solution.py:241
  5.4 2.5 collective-permute-start.4
  8.1 1.0 copy-done.23
  9.2 1.0 copy-done.24
  10.2 1.0 copy-done.27
  12.4 1.6 collective-permute-start.2
  14.0 2.6 collective-permute-start.1
  18.3 2.1 tree_table.1.info
  20.5 5.4 %collective-permute-done.1.refs_5_ = bf16[128,768]{1,0:T(8,128)(2,1)S(1)} collective-permute-done((bf16[128,768]{1,0:T(8,128)(2,1)S(1)}, bf16[128,768]{1,0:T(8,128)(2,1)S(1)}, u32[]{:S(2)}, u32[]{:S(2)}) %collective-permute-start.1) | collective-permute-done | bytes 196640 | tf_op jit(solution)/shard_map/ppermute | solution.py:45
  26.0 4.1 %collective-permute-start.5 = (bf16[256,768]{1,0:T(8,128)(2,1)S(1)}, bf16[256,768]{1,0:T(8,128)(2,1)S(1)}, u32[]{:S(2)}, u32[]{:S(2)}) collective-permute-start(bf16[256,768]{1,0:T(8,128)(2,1)S(1)} %pad_maximum_fusion.5), channel_id=1, source_target_pairs={{0,8},{4,12},{8,0},{12,4},{16,24},{20,28},{24,16},{28,20},{1,9},{5... | collective-permute-start | bytes 1179656 | tf_op jit(solution)/shard_map/ppermute | solution.py:45
  30.2 3.7 %fusion = (f32[1280,128]{1,0:T(8,128)}, f32[1280,128]{1,0:T(8,128)}) fusion(s32[128]{0:T(128)S(1)} %get-tuple-element.364, s32[128]{0:T(128)S(1)} %get-tuple-element.365, pred[128]{0:T(512)(128)(4,1)S(1)} %compare_and_fusion, f32[1280]{0:T(1024)S(1)} %convert_add_fusion), kind=kLoop, calls=%fused_computation.9 | loop fusion | flops 3112960 | bytes 1316992 | tf_op jit(solution)/shard_map/jit(_where)/select_n | solution.py:1103
  35.1 2.5 collective-permute-done.4.refs_2_
  37.7 2.9 collective-permute-done.5.refs_6_
  41.7 2.0 collective-permute-start.11
  43.8 1.6 collective-permute-start.10
  45.4 11.1 %collective-permute-done.11.refs_11_.refs_9_ = bf16[128,1024]{1,0:T(8,128)(2,1)S(1)} collective-permute-done((bf16[128,1024]{1,0:T(8,128)(2,1)S(1)}, bf16[128,1024]{1,0:T(8,128)(2,1)S(1)}, u32[]{:S(2)}, u32[]{:S(2)}) %collective-permute-start.11) | collective-permute-done | bytes 262176 | tf_op jit(solution)/shard_map/ppermute | solution.py:45
  56.8 3.8 %collective-permute-done.9.refs_7_ = bf16[512,768]{1,0:T(8,128)(2,1)S(1)} collective-permute-done((bf16[512,768]{1,0:T(8,128)(2,1)S(1)}, bf16[512,768]{1,0:T(8,128)(2,1)S(1)}, u32[]{:S(2)}, u32[]{:S(2)}) %collective-permute-start.9) | collective-permute-done | bytes 786464 | tf_op jit(solution)/shard_map/ppermute | solution.py:45
  62.2 1.2 collective-permute-start.13
  64.0 2.6 collective-permute-start.15
  66.6 11.1 %project_qkv.1 = (bf16[2560,256]{1,0:T(8,128)(2,1)}, bf16[2560,256]{1,0:T(8,128)(2,1)}, bf16[2560,256]{1,0:T(8,128)(2,1)}) custom-call(s32[6]{0:T(128)} %stack.11.ids, s32[1,20,5]{2,1,0:T(8,128)} %tree_table.1.info, bf16[640,1024]{1,0:T(8,128)(2,1)} %copy-done.42, bf16[640,1024]{1,0:T(8,128)(2,1)} %collective-permute-done.3.refs_1_, ...), custom_call_target="tpu_custom_call" | custom-call | flops 4026531840 | bytes 12079104 | tf_op jit(solution)/shard_map/project_qkv/pallas_call | solution.py:241
  77.7 2.1 collective-permute-done.15.refs_15_
  79.9 2.2 collective-permute-done.14.refs_12_.refs_10_
  82.1 1.0 pad_maximum_fusion.4
  83.2 1.9 collective-permute-start.17
  85.0 1.2 pad_maximum_fusion
  86.2 1.6 collective-permute-start.18
  87.9 5.4 %project_grad.1.do_ref = bf16[2560,256]{1,0:T(8,128)(2,1)S(1)} custom-call(s32[6]{0:T(128)S(1)} %copy-done.37, bf16[384,1024]{1,0:T(8,128)(2,1)} %collective-permute-done.12.refs_0_.refs_4_, bf16[256,1024]{1,0:T(8,128)(2,1)S(1)} %collective-permute-done.16.refs_1_.refs_5_, bf16[640,1024]{1,0:T(8,128)(2,1)} %collective-permute-done.refs_2_.refs_6_, ...), custom_call_target="tpu_custom_call" | custom-call | flops 1342177280 | bytes 7077888 | tf_op jit(solution)/shard_map/project_grad/pallas_call | solution.py:241
  93.3 4.3 %collective-permute-done.17.refs_16_ = bf16[256,1024]{1,0:T(8,128)(2,1)S(1)} collective-permute-done((bf16[256,1024]{1,0:T(8,128)(2,1)S(1)}, bf16[256,1024]{1,0:T(8,128)(2,1)S(1)}, u32[]{:S(2)}, u32[]{:S(2)}) %collective-permute-start.17) | collective-permute-done | bytes 524320 | tf_op jit(solution)/shard_map/ppermute | solution.py:45
  97.6 1.2 pad_maximum_fusion.1
  98.8 1.6 collective-permute-start.19
  100.4 60.3 %attention.1 = (bf16[2560,256]{1,0:T(8,128)(2,1)S(1)}, bf16[2560,256]{1,0:T(8,128)(2,1)S(1)}, bf16[2560,256]{1,0:T(8,128)(2,1)S(1)}, bf16[2560,256]{1,0:T(8,128)(2,1)S(1)}) custom-call(s32[1,20,5]{2,1,0:T(8,128)S(1)} %copy-done.36, bf16[2560,256]{1,0:T(8,128)(2,1)S(1)} %copy-done.58, bf16[2560,256]{1,0:T(8,128)(2,1)S(1)} %project_grad.1.do_ref, ...), custom_call_target="tpu_custom_call" | custom-call | flops 31406948352 | bytes 11796480 | tf_op jit(solution)/shard_map/attention/pallas_call | solution.py:241
  161.8 1.0 copy-done.48
  162.7 4.1 %project_context.1 = (bf16[1,640,1024]{2,1,0:T(8,128)(2,1)S(1)}, bf16[1,640,1024]{2,1,0:T(8,128)(2,1)S(1)}, bf16[2,640,1024]{2,1,0:T(8,128)(2,1)S(1)}) custom-call(s32[6]{0:T(128)S(1)} %copy-done.37, bf16[2560,256]{1,0:T(8,128)(2,1)S(1)} %get-tuple-element.256.ctx_ref.ctx, bf16[128,256]{1,0:T(8,128)(2,1)S(1)} %copy-done.16, bf16[128,256]{1,0:T(8,128)(2,1)S(1)} %copy-done.18, ...), custom_call_target="tpu_custom_call" | custom-call | flops 1342177280 | bytes 7077888 | tf_op jit(solution)/shard_map/project_context/pallas_call | solution.py:241
  167.4 12.3 %attention_weights.1 = (bf16[2560,768]{1,0:T(8,128)(2,1)S(1)}, f32[8,768]{1,0:T(8,128)S(1)}, bf16[4,128,512]{2,1,0:T(8,128)(2,1)}, bf16[4,128,512]{2,1,0:T(8,128...) custom-call(s32[6]{0:T(128)S(1)} %copy-done.37, s32[1,20,5]{2,1,0:T(8,128)S(1)} %copy-done.36, ...), custom_call_target="tpu_custom_call" | custom-call | flops 5368709120 | bytes 23101440 | tf_op jit(solution)/shard_map/attention_weights/pallas_call | solution.py:241
  179.7 2.0 copy-done.56
  182.2 1.7 collective-permute-start.24
  185.9 39.4 %mlp.1 = (bf16[1,640,1024]{2,1,0:T(8,128)(2,1)S(1)}, bf16[1,640,1024]{2,1,0:T(8,128)(2,1)}, bf16[2,640,1024]{2,1,0:T(8,128)(2,1)}, bf16[2560,1024]{1,0:T(8,128)(...) custom-call(s32[6]{0:T(128)S(1)} %copy-done.37, ...), custom_call_target="tpu_custom_call" | custom-call | flops 26843545600 | bytes 29417472 | tf_op jit(solution)/shard_map/mlp/pallas_call | solution.py:241
  225.9 3.6 %collective-permute-done.25.refs_1_ = bf16[1,640,1024]{2,1,0:T(8,128)(2,1)S(1)} collective-permute-done((bf16[1,640,1024]{2,1,0:T(8,128)(2,1)S(1)}, bf16[1,640,1024]{2,1,0:T(8,128)(2,1)S(1)}, u32[]{:S(2)}, u32[]{:S(2)}) %collective-permute-start.25) | collective-permute-done | bytes 1310752 | tf_op jit(solution)/shard_map/ppermute | solution.py:45
  229.5 1.7 copy-done.3
  232.5 1.3 collective-permute-start.30
  235.0 1.7 collective-permute-start.28
  237.4 2.1 copy-done.57
  239.5 2.5 copy-done.61
  242.0 15.9 %norm_backward.1 = (bf16[1,640,1024]{2,1,0:T(8,128)(2,1)S(1)}, bf16[1,640,1024]{2,1,0:T(8,128)(2,1)S(1)}, bf16[2,640,1024]{2,1,0:T(8,128)(2,1)S(1)}, f32[8,1024]{1,0:T(8,128)S(1)}) custom-call(s32[6]{0:T(128)S(1)} %copy-done.37, bf16[2560,768]{1,0:T(8,128)(2,1)S(1)} %copy-done.57, bf16[2560,1024]{1,0:T(8,128)(2,1)S(1)} %copy-done.61, ...), custom_call_target="tpu_custom_call" | custom-call | flops 9395240960 | bytes 23371776 | tf_op jit(solution)/shard_map/norm_backward/pallas_call | solution.py:241
  257.9 4.3 %collective-permute-done.28.refs_2_ = bf16[2,128,512]{2,1,0:T(8,128)(2,1)S(1)} collective-permute-done((bf16[2,128,512]{2,1,0:T(8,128)(2,1)}, bf16[2,128,512]{2,1,0:T(8,128)(2,1)S(1)}, u32[]{:S(2)}, u32[]{:S(2)}) %collective-permute-start.28) | collective-permute-done | bytes 262176 | tf_op jit(solution)/shard_map/ppermute | solution.py:45
  262.3 1.0 collective-permute-done.29.refs_5_.refs_6_
  263.3 1.0 collective-permute-done.31.refs_9_.refs_4_.refs_5_
  264.9 2.5 collective-permute-done.32.refs_1_
  267.8 1.5 collective-permute-start.41
  269.6 1.8 collective-permute-start.36
  272.1 1.3 copy-done.6
  273.4 3.7 %finish_output.1 = (f32[640,1024]{1,0:T(8,128)}, f32[16,1024]{1,0:T(8,128)S(1)}) custom-call(s32[6]{0:T(128)S(1)} %copy-done.37, f32[640,1024]{1,0:T(8,128)S(1)} %copy-done, bf16[640,1024]{1,0:T(8,128)(2,1)S(1)} %copy-done.2, bf16[2,640,1024]{2,1,0:T(8,128)(2,1)S(1)} %get-tuple-element.269.refs_0_, ...), custom_call_target="tpu_custom_call" | custom-call | flops 10485760 | bytes 17203200 | tf_op jit(solution)/shard_map/finish_output/pallas_call | solution.py:241
  277.1 1.3 collective-permute-done.34
  278.4 2.8 collective-permute-start.35
  281.2 4.9 %collective-permute-done.38.refs_7_ = bf16[1,128,512]{2,1,0:T(8,128)(2,1)S(1)} collective-permute-done((bf16[1,128,512]{2,1,0:T(8,128)(2,1)S(1)}, bf16[1,128,512]{2,1,0:T(8,128)(2,1)S(1)}, u32[]{:S(2)}, u32[]{:S(2)}) %collective-permute-start.38) | collective-permute-done | bytes 131104 | tf_op jit(solution)/shard_map/ppermute | solution.py:45
  286.1 1.4 collective-permute-done.36.refs_2_
  287.8 2.7 collective-permute-start.44
  290.8 1.7 collective-permute-start.39
  292.5 2.5 collective-permute-done.39
  295.1 1.3 collective-permute-start.40
  297.1 6.5 %collective-permute-done.40 = f32[16,1024]{1,0:T(8,128)S(1)} collective-permute-done((f32[16,1024]{1,0:T(8,128)S(1)}, f32[16,1024]{1,0:T(8,128)S(1)}, u32[]{:S(2)}, u32[]{:S(2)}) %collective-permute-start.40) | collective-permute-done | bytes 65568 | tf_op jit(solution)/shard_map/ppermute | solution.py:45
  303.7 2.8 finish_grad.1
  308.1 4.7 %collective-permute-done.45.refs_7_ = bf16[1,128,1024]{2,1,0:T(8,128)(2,1)S(1)} collective-permute-done((bf16[1,128,1024]{2,1,0:T(8,128)(2,1)S(1)}, bf16[1,128,1024]{2,1,0:T(8,128)(2,1)S(1)}, u32[]{:S(2)}, u32[]{:S(2)}) %collective-permute-start.45) | collective-permute-done | bytes 262176 | tf_op jit(solution)/shard_map/ppermute | solution.py:45
  312.8 1.2 finish_mlp_weights.1
  (212 shorter events, 24.4 us)
Async XLA Ops:
  0.6 25.3 %collective-permute-start = (bf16[640,1024]{1,0:T(8,128)(2,1)}, bf16[640,1024]{1,0:T(8,128)(2,1)}, u32[]{:S(2)}, u32[]{:S(2)}) collective-permute-start(bf16[640,1024]{1,0:T(8,128)(2,1)} %grad_ref.3), channel_id=1, source_target_pairs={{0,1},{1,0},{2,3},{3,2},{4,5},{5,4},{6,7},{7,6},{8,9},{9,8},{10,11... | collective-permute-start | bytes 3932168 | tf_op jit(solution)/shard_map/ppermute | solution.py:45
  5.4 11.2 %copy-start.1 = (bf16[640,1024]{1,0:T(8,128)(2,1)S(1)}, bf16[640,1024]{1,0:T(8,128)(2,1)}, u32[]{:S(2)}) copy-start(bf16[640,1024]{1,0:T(8,128)(2,1)} %grad_ref.3) | copy-start | bytes 3932164
  5.4 32.3 %collective-permute-start.4 = (bf16[640,1024]{1,0:T(8,128)(2,1)}, bf16[640,1024]{1,0:T(8,128)(2,1)}, u32[]{:S(2)}, u32[]{:S(2)}) collective-permute-start(bf16[640,1024]{1,0:T(8,128)(2,1)} %get-tuple-element.217.refs_3_), channel_id=1, source_target_pairs={{0,2},{1,3},{2,0},{3,1},{4,6},{5,7},{6,4},{7,5},{8,10},{9,11},{10,... | collective-permute-start | bytes 3932168 | tf_op jit(solution)/shard_map/ppermute | solution.py:45
  7.9 29.7 %collective-permute-start.3 = (bf16[640,1024]{1,0:T(8,128)(2,1)}, bf16[640,1024]{1,0:T(8,128)(2,1)}, u32[]{:S(2)}, u32[]{:S(2)}) collective-permute-start(bf16[640,1024]{1,0:T(8,128)(2,1)} %get-tuple-element.217.refs_3_), channel_id=1, source_target_pairs={{0,1},{1,0},{2,3},{3,2},{4,5},{5,4},{6,7},{7,6},{8,9},{9,8},{10,11... | collective-permute-start | bytes 3932168 | tf_op jit(solution)/shard_map/ppermute | solution.py:45
  12.4 28.2 %copy-start.9 = (bf16[128,768]{1,0:T(8,128)(2,1)}, bf16[128,768]{1,0:T(8,128)(2,1)S(1)}, u32[]{:S(2)}) copy-start(bf16[128,768]{1,0:T(8,128)(2,1)S(1)} %get-tuple-element.218.refs_4_) | copy-start | bytes 589828
  12.4 31.4 %copy-start.15 = (bf16[128,256]{1,0:T(8,128)(2,1)}, bf16[128,256]{1,0:T(8,128)(2,1)S(1)}, u32[]{:S(2)}) copy-start(bf16[128,256]{1,0:T(8,128)(2,1)S(1)} %get-tuple-element.237.refs_6_.refs_0_) | copy-start | bytes 196612
  12.4 8.1 %collective-permute-start.2 = (bf16[128,256]{1,0:T(8,128)(2,1)S(1)}, bf16[128,256]{1,0:T(8,128)(2,1)S(1)}, u32[]{:S(2)}, u32[]{:S(2)}) collective-permute-start(bf16[128,256]{1,0:T(8,128)(2,1)S(1)} %get-tuple-element.237.refs_6_.refs_0_), channel_id=1, source_target_pairs={{0,4},{4,0},{8,12},{12,8},{16,20},{20,16},{24,28},{28,24},{1,5},{5... | collective-permute-start | bytes 196616 | tf_op jit(solution)/shard_map/ppermute | solution.py:45
  14.0 11.9 %collective-permute-start.1 = (bf16[128,768]{1,0:T(8,128)(2,1)S(1)}, bf16[128,768]{1,0:T(8,128)(2,1)S(1)}, u32[]{:S(2)}, u32[]{:S(2)}) collective-permute-start(bf16[128,768]{1,0:T(8,128)(2,1)S(1)} %get-tuple-element.218.refs_4_), channel_id=1, source_target_pairs={{0,16},{4,20},{8,24},{12,28},{16,0},{20,4},{24,8},{28,12},{1,17},{... | collective-permute-start | bytes 589832 | tf_op jit(solution)/shard_map/ppermute | solution.py:45
  18.3 15.6 %copy-start.65 = (f32[3072]{0:T(1024)S(1)}, f32[3072]{0:T(1024)}, u32[]{:S(2)}) copy-start(f32[3072]{0:T(1024)} %param.24) | copy-start | bytes 36868
  18.3 16.2 %copy-start.64 = (f32[4096]{0:T(1024)S(1)}, f32[4096]{0:T(1024)}, u32[]{:S(2)}) copy-start(f32[4096]{0:T(1024)} %param.28) | copy-start | bytes 49156
  20.5 23.3 %copy-start.17 = (bf16[128,256]{1,0:T(8,128)(2,1)}, bf16[128,256]{1,0:T(8,128)(2,1)S(1)}, u32[]{:S(2)}) copy-start(bf16[128,256]{1,0:T(8,128)(2,1)S(1)} %collective-permute-done.2.refs_7_.refs_1_) | copy-start | bytes 196612
  25.9 14.7 %copy-start.11 = (bf16[128,768]{1,0:T(8,128)(2,1)}, bf16[128,768]{1,0:T(8,128)(2,1)S(1)}, u32[]{:S(2)}) copy-start(bf16[128,768]{1,0:T(8,128)(2,1)S(1)} %collective-permute-done.1.refs_5_) | copy-start | bytes 589828
  25.9 11.7 %collective-permute-start.6 = (bf16[256,256]{1,0:T(8,128)(2,1)S(1)}, bf16[256,256]{1,0:T(8,128)(2,1)S(1)}, u32[]{:S(2)}, u32[]{:S(2)}) collective-permute-start(bf16[256,256]{1,0:T(8,128)(2,1)S(1)} %pad_maximum_fusion.7), channel_id=1, source_target_pairs={{0,16},{4,20},{8,24},{12,28},{16,0},{20,4},{24,8},{28,12},{1,17},{... | collective-permute-start | bytes 393224 | tf_op jit(solution)/shard_map/ppermute | solution.py:45
  26.0 14.5 %collective-permute-start.5 = (bf16[256,768]{1,0:T(8,128)(2,1)S(1)}, bf16[256,768]{1,0:T(8,128)(2,1)S(1)}, u32[]{:S(2)}, u32[]{:S(2)}) collective-permute-start(bf16[256,768]{1,0:T(8,128)(2,1)S(1)} %pad_maximum_fusion.5), channel_id=1, source_target_pairs={{0,8},{4,12},{8,0},{12,4},{16,24},{20,28},{24,16},{28,20},{1,9},{5... | collective-permute-start | bytes 1179656 | tf_op jit(solution)/shard_map/ppermute | solution.py:45
  37.7 24.2 %copy-start.19 = (bf16[256,256]{1,0:T(8,128)(2,1)}, bf16[256,256]{1,0:T(8,128)(2,1)S(1)}, u32[]{:S(2)}) copy-start(bf16[256,256]{1,0:T(8,128)(2,1)S(1)} %collective-permute-done.6.refs_8_.refs_2_) | copy-start | bytes 393220
  40.6 21.3 %copy-start.28 = (bf16[256,768]{1,0:T(8,128)(2,1)}, bf16[256,768]{1,0:T(8,128)(2,1)S(1)}, u32[]{:S(2)}) copy-start(bf16[256,768]{1,0:T(8,128)(2,1)S(1)} %collective-permute-done.5.refs_6_) | copy-start | bytes 1179652
  40.6 20.4 %collective-permute-start.7 = (bf16[640,1024]{1,0:T(8,128)(2,1)}, bf16[640,1024]{1,0:T(8,128)(2,1)S(1)}, u32[]{:S(2)}, u32[]{:S(2)}) collective-permute-start(bf16[640,1024]{1,0:T(8,128)(2,1)} %collective-permute-done.4.refs_2_), channel_id=1, source_target_pairs={{0,1},{1,0},{2,3},{3,2},{4,5},{5,4},{6,7},{7,6},{8,9},{9,8},{10,11... | collective-permute-start | bytes 3932168 | tf_op jit(solution)/shard_map/ppermute | solution.py:45
  40.6 20.0 %collective-permute-start.9 = (bf16[512,768]{1,0:T(8,128)(2,1)S(1)}, bf16[512,768]{1,0:T(8,128)(2,1)S(1)}, u32[]{:S(2)}, u32[]{:S(2)}) collective-permute-start(bf16[512,768]{1,0:T(8,128)(2,1)S(1)} %pad_maximum_fusion.2), channel_id=1, source_target_pairs={{0,4},{4,0},{8,12},{12,8},{16,20},{20,16},{24,28},{28,24},{1,5},{5... | collective-permute-start | bytes 2359304 | tf_op jit(solution)/shard_map/ppermute | solution.py:45
  41.2 19.8 %collective-permute-start.8 = (bf16[384,1024]{1,0:T(8,128)(2,1)S(1)}, bf16[384,1024]{1,0:T(8,128)(2,1)}, u32[]{:S(2)}, u32[]{:S(2)}) collective-permute-start(bf16[384,1024]{1,0:T(8,128)(2,1)S(1)} %copy-done.62), channel_id=1, source_target_pairs={{0,2},{1,3},{2,0},{3,1},{4,6},{5,7},{6,4},{7,5},{8,10},{9,11},{10,... | collective-permute-start | bytes 2359304 | tf_op jit(solution)/shard_map/ppermute | solution.py:45
  41.7 14.8 %collective-permute-start.11 = (bf16[128,1024]{1,0:T(8,128)(2,1)S(1)}, bf16[128,1024]{1,0:T(8,128)(2,1)S(1)}, u32[]{:S(2)}, u32[]{:S(2)}) collective-permute-start(bf16[128,1024]{1,0:T(8,128)(2,1)S(1)} %get-tuple-element.272.refs_10_.refs_8_), channel_id=1, source_target_pairs={{0,16},{4,20},{8,24},{12,28},{16,0},{20,4},{24,8},{28,12},{1,17},{... | collective-permute-start | bytes 786440 | tf_op jit(solution)/shard_map/ppermute | solution.py:45
  43.8 13.0 %collective-permute-start.10 = (bf16[512,256]{1,0:T(8,128)(2,1)S(1)}, bf16[512,256]{1,0:T(8,128)(2,1)S(1)}, u32[]{:S(2)}, u32[]{:S(2)}) collective-permute-start(bf16[512,256]{1,0:T(8,128)(2,1)S(1)} %pad_maximum_fusion.6), channel_id=1, source_target_pairs={{0,8},{4,12},{8,0},{12,4},{16,24},{20,28},{24,16},{28,20},{1,9},{5... | collective-permute-start | bytes 786440 | tf_op jit(solution)/shard_map/ppermute | solution.py:45
  61.0 21.1 %collective-permute-start.12 = (bf16[384,1024]{1,0:T(8,128)(2,1)}, bf16[384,1024]{1,0:T(8,128)(2,1)}, u32[]{:S(2)}, u32[]{:S(2)}) collective-permute-start(bf16[384,1024]{1,0:T(8,128)(2,1)} %collective-permute-done.8.refs_3_.refs_7_), channel_id=1, source_target_pairs={{0,1},{1,0},{2,3},{3,2},{4,5},{5,4},{6,7},{7,6},{8,9},{9,8},{10,11... | collective-permute-start | bytes 2359304 | tf_op jit(solution)/shard_map/ppermute | solution.py:45
  61.9 20.2 %collective-permute-start.14 = (bf16[256,1024]{1,0:T(8,128)(2,1)}, bf16[256,1024]{1,0:T(8,128)(2,1)}, u32[]{:S(2)}, u32[]{:S(2)}) collective-permute-start(bf16[256,1024]{1,0:T(8,128)(2,1)} %pad_maximum_fusion.3), channel_id=1, source_target_pairs={{0,8},{4,12},{8,0},{12,4},{16,24},{20,28},{24,16},{28,20},{1,9},{5... | collective-permute-start | bytes 1572872 | tf_op jit(solution)/shard_map/ppermute | solution.py:45
  62.2 19.9 %collective-permute-start.13 = (bf16[256,1024]{1,0:T(8,128)(2,1)}, bf16[256,1024]{1,0:T(8,128)(2,1)}, u32[]{:S(2)}, u32[]{:S(2)}) collective-permute-start(bf16[256,1024]{1,0:T(8,128)(2,1)} %slice.31), channel_id=1, source_target_pairs={{0,2},{1,3},{2,0},{3,1},{4,6},{5,7},{6,4},{7,5},{8,10},{9,11},{10,... | collective-permute-start | bytes 1572872 | tf_op jit(solution)/shard_map/ppermute | solution.py:45
  64.0 15.8 %collective-permute-start.15 = (bf16[128,1024]{1,0:T(8,128)(2,1)S(1)}, bf16[128,1024]{1,0:T(8,128)(2,1)}, u32[]{:S(2)}, u32[]{:S(2)}) collective-permute-start(bf16[128,1024]{1,0:T(8,128)(2,1)S(1)} %get-tuple-element.276.refs_14_), channel_id=1, source_target_pairs={{0,16},{4,20},{8,24},{12,28},{16,0},{20,4},{24,8},{28,12},{1,17},{... | collective-permute-start | bytes 786440 | tf_op jit(solution)/shard_map/ppermute | solution.py:45
  82.1 5.7 %collective-permute-start.16 = (bf16[256,1024]{1,0:T(8,128)(2,1)}, bf16[256,1024]{1,0:T(8,128)(2,1)S(1)}, u32[]{:S(2)}, u32[]{:S(2)}) collective-permute-start(bf16[256,1024]{1,0:T(8,128)(2,1)} %collective-permute-done.13.refs_4_.refs_8_), channel_id=1, source_target_pairs={{0,1},{1,0},{2,3},{3,2},{4,5},{5,4},{6,7},{7,6},{8,9},{9,8},{10,11... | collective-permute-start | bytes 1572872 | tf_op jit(solution)/shard_map/ppermute | solution.py:45
  83.2 14.4 %collective-permute-start.17 = (bf16[256,1024]{1,0:T(8,128)(2,1)S(1)}, bf16[256,1024]{1,0:T(8,128)(2,1)S(1)}, u32[]{:S(2)}, u32[]{:S(2)}) collective-permute-start(bf16[256,1024]{1,0:T(8,128)(2,1)S(1)} %pad_maximum_fusion.4), channel_id=1, source_target_pairs={{0,8},{4,12},{8,0},{12,4},{16,24},{20,28},{24,16},{28,20},{1,9},{5... | collective-permute-start | bytes 1572872 | tf_op jit(solution)/shard_map/ppermute | solution.py:45
  86.2 74.6 %collective-permute-start.18 = (bf16[512,1024]{1,0:T(8,128)(2,1)S(1)}, bf16[512,1024]{1,0:T(8,128)(2,1)S(1)}, u32[]{:S(2)}, u32[]{:S(2)}) collective-permute-start(bf16[512,1024]{1,0:T(8,128)(2,1)S(1)} %pad_maximum_fusion), channel_id=1, source_target_pairs={{0,4},{4,0},{8,12},{12,8},{16,20},{20,16},{24,28},{28,24},{1,5},{5... | collective-permute-start | bytes 3145736 | tf_op jit(solution)/shard_map/ppermute | solution.py:45
  87.8 79.6 %copy-start.21 = (bf16[256,1024]{1,0:T(8,128)(2,1)}, bf16[256,1024]{1,0:T(8,128)(2,1)S(1)}, u32[]{:S(2)}) copy-start(bf16[256,1024]{1,0:T(8,128)(2,1)S(1)} %collective-permute-done.16.refs_1_.refs_5_) | copy-start | bytes 1572868
  87.8 12.5 %copy-start.58 = (bf16[2560,256]{1,0:T(8,128)(2,1)S(1)}, bf16[2560,256]{1,0:T(8,128)(2,1)}, u32[]{:S(2)}) copy-start(bf16[2560,256]{1,0:T(8,128)(2,1)} %get-tuple-element.233.q_ref) | copy-start | bytes 3932164
  87.8 12.5 %copy-start.59 = (bf16[2560,256]{1,0:T(8,128)(2,1)S(1)}, bf16[2560,256]{1,0:T(8,128)(2,1)}, u32[]{:S(2)}) copy-start(bf16[2560,256]{1,0:T(8,128)(2,1)} %get-tuple-element.244.k_ref) | copy-start | bytes 3932164
  87.9 12.5 %copy-start.60 = (bf16[2560,256]{1,0:T(8,128)(2,1)S(1)}, bf16[2560,256]{1,0:T(8,128)(2,1)}, u32[]{:S(2)}) copy-start(bf16[2560,256]{1,0:T(8,128)(2,1)} %get-tuple-element.245.v_ref) | copy-start | bytes 3932164
  93.3 7.1 %copy-start.13 = (f32[1280,128]{1,0:T(8,128)S(1)}, f32[1280,128]{1,0:T(8,128)}, u32[]{:S(2)}) copy-start(f32[1280,128]{1,0:T(8,128)} %get-tuple-element.224.refs_12_.sine.refs_13_) | copy-start | bytes 1966084
  93.3 7.1 %copy-start.14 = (f32[1280,128]{1,0:T(8,128)S(1)}, f32[1280,128]{1,0:T(8,128)}, u32[]{:S(2)}) copy-start(f32[1280,128]{1,0:T(8,128)} %get-tuple-element.223.refs_11_.cos.refs_12_) | copy-start | bytes 1966084
  97.6 63.2 %copy-start.25 = (bf16[256,1024]{1,0:T(8,128)(2,1)}, bf16[256,1024]{1,0:T(8,128)(2,1)S(1)}, u32[]{:S(2)}) copy-start(bf16[256,1024]{1,0:T(8,128)(2,1)S(1)} %collective-permute-done.17.refs_16_) | copy-start | bytes 1572868
  98.8 63.0 %collective-permute-start.19 = (bf16[512,1024]{1,0:T(8,128)(2,1)S(1)}, bf16[512,1024]{1,0:T(8,128)(2,1)S(1)}, u32[]{:S(2)}, u32[]{:S(2)}) collective-permute-start(bf16[512,1024]{1,0:T(8,128)(2,1)S(1)} %pad_maximum_fusion.1), channel_id=1, source_target_pairs={{0,4},{4,0},{8,12},{12,8},{16,20},{20,16},{24,28},{28,24},{1,5},{5... | collective-permute-start | bytes 3145736 | tf_op jit(solution)/shard_map/ppermute | solution.py:45
  166.8 14.9 %collective-permute-start.20 = (bf16[1,640,1024]{2,1,0:T(8,128)(2,1)S(1)}, bf16[1,640,1024]{2,1,0:T(8,128)(2,1)S(1)}, u32[]{:S(2)}, u32[]{:S(2)}) collective-permute-start(bf16[1,640,1024]{2,1,0:T(8,128)(2,1)S(1)} %get-tuple-element.266), channel_id=1, source_target_pairs={{0,1},{1,0},{2,3},{3,2},{4,5},{5,4},{6,7},{7,6},{8,9},{9,8},{10,11... | collective-permute-start | bytes 3932168 | tf_op jit(solution)/shard_map/ppermute | solution.py:45
  166.9 14.8 %collective-permute-start.21 = (bf16[1,640,1024]{2,1,0:T(8,128)(2,1)S(1)}, bf16[1,640,1024]{2,1,0:T(8,128)(2,1)S(1)}, u32[]{:S(2)}, u32[]{:S(2)}) collective-permute-start(bf16[1,640,1024]{2,1,0:T(8,128)(2,1)S(1)} %get-tuple-element.267), channel_id=1, source_target_pairs={{0,1},{1,0},{2,3},{3,2},{4,5},{5,4},{6,7},{7,6},{8,9},{9,8},{10,11... | collective-permute-start | bytes 3932168 | tf_op jit(solution)/shard_map/ppermute | solution.py:45
  181.7 43.6 %collective-permute-start.23 = (bf16[4,128,512]{2,1,0:T(8,128)(2,1)}, bf16[4,128,512]{2,1,0:T(8,128)(2,1)S(1)}, u32[]{:S(2)}, u32[]{:S(2)}) collective-permute-start(bf16[4,128,512]{2,1,0:T(8,128)(2,1)} %get-tuple-element.291), channel_id=1, source_target_pairs={{0,4},{4,0},{8,12},{12,8},{16,20},{20,16},{24,28},{28,24},{1,5},{5... | collective-permute-start | bytes 1572872 | tf_op jit(solution)/shard_map/ppermute | solution.py:45
  182.2 43.1 %collective-permute-start.24 = (bf16[4,128,512]{2,1,0:T(8,128)(2,1)}, bf16[4,128,512]{2,1,0:T(8,128)(2,1)S(1)}, u32[]{:S(2)}, u32[]{:S(2)}) collective-permute-start(bf16[4,128,512]{2,1,0:T(8,128)(2,1)} %get-tuple-element.292), channel_id=1, source_target_pairs={{0,8},{4,12},{8,0},{12,4},{16,24},{20,28},{24,16},{28,20},{1,9},{5... | collective-permute-start | bytes 1572872 | tf_op jit(solution)/shard_map/ppermute | solution.py:45
  184.3 41.0 %collective-permute-start.22 = (bf16[1,640,1024]{2,1,0:T(8,128)(2,1)S(1)}, bf16[1,640,1024]{2,1,0:T(8,128)(2,1)S(1)}, u32[]{:S(2)}, u32[]{:S(2)}) collective-permute-start(bf16[1,640,1024]{2,1,0:T(8,128)(2,1)S(1)} %add_terms.3), channel_id=1, source_target_pairs={{0,2},{1,3},{2,0},{3,1},{4,6},{5,7},{6,4},{7,5},{8,10},{9,11},{10,... | collective-permute-start | bytes 3932168 | tf_op jit(solution)/shard_map/ppermute | solution.py:45
  225.3 4.2 %collective-permute-start.25 = (bf16[1,640,1024]{2,1,0:T(8,128)(2,1)S(1)}, bf16[1,640,1024]{2,1,0:T(8,128)(2,1)S(1)}, u32[]{:S(2)}, u32[]{:S(2)}) collective-permute-start(bf16[1,640,1024]{2,1,0:T(8,128)(2,1)S(1)} %get-tuple-element.295), channel_id=1, source_target_pairs={{0,1},{1,0},{2,3},{3,2},{4,5},{5,4},{6,7},{7,6},{8,9},{9,8},{10,11... | collective-permute-start | bytes 3932168 | tf_op jit(solution)/shard_map/ppermute | solution.py:45
  225.4 11.3 %collective-permute-start.26 = (bf16[1,640,1024]{2,1,0:T(8,128)(2,1)}, bf16[1,640,1024]{2,1,0:T(8,128)(2,1)S(1)}, u32[]{:S(2)}, u32[]{:S(2)}) collective-permute-start(bf16[1,640,1024]{2,1,0:T(8,128)(2,1)} %get-tuple-element.297), channel_id=1, source_target_pairs={{0,1},{1,0},{2,3},{3,2},{4,5},{5,4},{6,7},{7,6},{8,9},{9,8},{10,11... | collective-permute-start | bytes 3932168 | tf_op jit(solution)/shard_map/ppermute | solution.py:45
  231.6 32.7 %collective-permute-start.27 = (bf16[1,640,1024]{2,1,0:T(8,128)(2,1)S(1)}, bf16[1,640,1024]{2,1,0:T(8,128)(2,1)S(1)}, u32[]{:S(2)}, u32[]{:S(2)}) collective-permute-start(bf16[1,640,1024]{2,1,0:T(8,128)(2,1)S(1)} %add_terms.4), channel_id=1, source_target_pairs={{0,2},{1,3},{2,0},{3,1},{4,6},{5,7},{6,4},{7,5},{8,10},{9,11},{10,... | collective-permute-start | bytes 3932168 | tf_op jit(solution)/shard_map/ppermute | solution.py:45
  232.5 30.8 %collective-permute-start.30 = (bf16[4,128,1024]{2,1,0:T(8,128)(2,1)}, bf16[4,128,1024]{2,1,0:T(8,128)(2,1)S(1)}, u32[]{:S(2)}, u32[]{:S(2)}) collective-permute-start(bf16[4,128,1024]{2,1,0:T(8,128)(2,1)} %get-tuple-element.310), channel_id=1, source_target_pairs={{0,4},{4,0},{8,12},{12,8},{16,20},{20,16},{24,28},{28,24},{1,5},{5... | collective-permute-start | bytes 3145736 | tf_op jit(solution)/shard_map/ppermute | solution.py:45
  233.9 30.5 %collective-permute-start.31 = (bf16[4,128,1024]{2,1,0:T(8,128)(2,1)}, bf16[4,128,1024]{2,1,0:T(8,128)(2,1)S(1)}, u32[]{:S(2)}, u32[]{:S(2)}) collective-permute-start(bf16[4,128,1024]{2,1,0:T(8,128)(2,1)} %get-tuple-element.311), channel_id=1, source_target_pairs={{0,8},{4,12},{8,0},{12,4},{16,24},{20,28},{24,16},{28,20},{1,9},{5... | collective-permute-start | bytes 3145736 | tf_op jit(solution)/shard_map/ppermute | solution.py:45
  235.0 27.2 %collective-permute-start.28 = (bf16[2,128,512]{2,1,0:T(8,128)(2,1)}, bf16[2,128,512]{2,1,0:T(8,128)(2,1)S(1)}, u32[]{:S(2)}, u32[]{:S(2)}) collective-permute-start(bf16[2,128,512]{2,1,0:T(8,128)(2,1)} %get-tuple-element.308), channel_id=1, source_target_pairs={{0,16},{4,20},{8,24},{12,28},{16,0},{20,4},{24,8},{28,12},{1,17},{... | collective-permute-start | bytes 786440 | tf_op jit(solution)/shard_map/ppermute | solution.py:45
  236.7 26.6 %collective-permute-start.29 = (bf16[2,128,512]{2,1,0:T(8,128)(2,1)}, bf16[2,128,512]{2,1,0:T(8,128)(2,1)S(1)}, u32[]{:S(2)}, u32[]{:S(2)}) collective-permute-start(bf16[2,128,512]{2,1,0:T(8,128)(2,1)} %get-tuple-element.309), channel_id=1, source_target_pairs={{0,4},{4,0},{8,12},{12,8},{16,20},{20,16},{24,28},{28,24},{1,5},{5... | collective-permute-start | bytes 786440 | tf_op jit(solution)/shard_map/ppermute | solution.py:45
  264.3 3.0 collective-permute-start.32
  264.3 7.7 %collective-permute-start.33 = (bf16[1,640,1024]{2,1,0:T(8,128)(2,1)S(1)}, bf16[1,640,1024]{2,1,0:T(8,128)(2,1)S(1)}, u32[]{:S(2)}, u32[]{:S(2)}) collective-permute-start(bf16[1,640,1024]{2,1,0:T(8,128)(2,1)S(1)} %get-tuple-element.315), channel_id=1, source_target_pairs={{0,1},{1,0},{2,3},{3,2},{4,5},{5,4},{6,7},{7,6},{8,9},{9,8},{10,11... | collective-permute-start | bytes 3932168 | tf_op jit(solution)/shard_map/ppermute | solution.py:45
  267.8 35.9 %collective-permute-start.41 = (bf16[1,640,1024]{2,1,0:T(8,128)(2,1)S(1)}, bf16[1,640,1024]{2,1,0:T(8,128)(2,1)S(1)}, u32[]{:S(2)}, u32[]{:S(2)}) collective-permute-start(bf16[1,640,1024]{2,1,0:T(8,128)(2,1)S(1)} %add_terms.5), channel_id=1, source_target_pairs={{0,2},{1,3},{2,0},{3,1},{4,6},{5,7},{6,4},{7,5},{8,10},{9,11},{10,... | collective-permute-start | bytes 3932168 | tf_op jit(solution)/shard_map/ppermute | solution.py:45
  269.6 18.0 %collective-permute-start.36 = (bf16[2,128,1024]{2,1,0:T(8,128)(2,1)S(1)}, bf16[2,128,1024]{2,1,0:T(8,128)(2,1)S(1)}, u32[]{:S(2)}, u32[]{:S(2)}) collective-permute-start(bf16[2,128,1024]{2,1,0:T(8,128)(2,1)S(1)} %get-tuple-element.332), channel_id=1, source_target_pairs={{0,8},{4,12},{8,0},{12,4},{16,24},{20,28},{24,16},{28,20},{1,9},{5... | collective-permute-start | bytes 1572872 | tf_op jit(solution)/shard_map/ppermute | solution.py:45
  271.4 16.2 %collective-permute-start.37 = (bf16[2,128,1024]{2,1,0:T(8,128)(2,1)S(1)}, bf16[2,128,1024]{2,1,0:T(8,128)(2,1)S(1)}, u32[]{:S(2)}, u32[]{:S(2)}) collective-permute-start(bf16[2,128,1024]{2,1,0:T(8,128)(2,1)S(1)} %get-tuple-element.333), channel_id=1, source_target_pairs={{0,4},{4,0},{8,12},{12,8},{16,20},{20,16},{24,28},{28,24},{1,5},{5... | collective-permute-start | bytes 1572872 | tf_op jit(solution)/shard_map/ppermute | solution.py:45
  271.9 14.2 %collective-permute-start.38 = (bf16[1,128,512]{2,1,0:T(8,128)(2,1)S(1)}, bf16[1,128,512]{2,1,0:T(8,128)(2,1)S(1)}, u32[]{:S(2)}, u32[]{:S(2)}) collective-permute-start(bf16[1,128,512]{2,1,0:T(8,128)(2,1)S(1)} %get-tuple-element.334), channel_id=1, source_target_pairs={{0,16},{4,20},{8,24},{12,28},{16,0},{20,4},{24,8},{28,12},{1,17},{... | collective-permute-start | bytes 393224 | tf_op jit(solution)/shard_map/ppermute | solution.py:45
  277.1 1.3 collective-permute-start.34
  278.4 9.2 %collective-permute-start.35 = (f32[16,1024]{1,0:T(8,128)S(1)}, f32[16,1024]{1,0:T(8,128)S(1)}, u32[]{:S(2)}, u32[]{:S(2)}) collective-permute-start(f32[16,1024]{1,0:T(8,128)S(1)} %add.41), channel_id=1, source_target_pairs={{0,16},{4,20},{8,24},{12,28},{16,0},{20,4},{24,8},{28,12},{1,17},{... | collective-permute-start | bytes 196616 | tf_op jit(solution)/shard_map/ppermute | solution.py:45
  287.6 16.1 %copy-start.30 = (f32[640,1]{1,0:T(8,128)S(1)}, f32[640,1]{1,0:T(8,128)}, u32[]{:S(2)}) copy-start(f32[640,1]{1,0:T(8,128)} %get-tuple-element.343.mean_ref) | copy-start | bytes 7684
  287.6 16.1 %copy-start.31 = (f32[640,1]{1,0:T(8,128)S(1)}, f32[640,1]{1,0:T(8,128)}, u32[]{:S(2)}) copy-start(f32[640,1]{1,0:T(8,128)} %get-tuple-element.344.std_ref) | copy-start | bytes 7684
  287.8 20.3 %collective-permute-start.44 = (bf16[1,128,1024]{2,1,0:T(8,128)(2,1)S(1)}, bf16[1,128,1024]{2,1,0:T(8,128)(2,1)S(1)}, u32[]{:S(2)}, u32[]{:S(2)}) collective-permute-start(bf16[1,128,1024]{2,1,0:T(8,128)(2,1)S(1)} %get-tuple-element.353), channel_id=1, source_target_pairs={{0,16},{4,20},{8,24},{12,28},{16,0},{20,4},{24,8},{28,12},{1,17},{... | collective-permute-start | bytes 786440 | tf_op jit(solution)/shard_map/ppermute | solution.py:45
  290.5 22.3 %collective-permute-start.45 = (bf16[1,128,1024]{2,1,0:T(8,128)(2,1)S(1)}, bf16[1,128,1024]{2,1,0:T(8,128)(2,1)S(1)}, u32[]{:S(2)}, u32[]{:S(2)}) collective-permute-start(bf16[1,128,1024]{2,1,0:T(8,128)(2,1)S(1)} %get-tuple-element.354), channel_id=1, source_target_pairs={{0,16},{4,20},{8,24},{12,28},{16,0},{20,4},{24,8},{28,12},{1,17},{... | collective-permute-start | bytes 786440 | tf_op jit(solution)/shard_map/ppermute | solution.py:45
  290.8 4.3 %collective-permute-start.39 = (f32[16,1024]{1,0:T(8,128)S(1)}, f32[16,1024]{1,0:T(8,128)S(1)}, u32[]{:S(2)}, u32[]{:S(2)}) collective-permute-start(f32[16,1024]{1,0:T(8,128)S(1)} %add.42), channel_id=1, source_target_pairs={{0,4},{4,0},{8,12},{12,8},{16,20},{20,16},{24,28},{28,24},{1,5},{5... | collective-permute-start | bytes 196616 | tf_op jit(solution)/shard_map/ppermute | solution.py:45
  295.1 8.6 %collective-permute-start.40 = (f32[16,1024]{1,0:T(8,128)S(1)}, f32[16,1024]{1,0:T(8,128)S(1)}, u32[]{:S(2)}, u32[]{:S(2)}) collective-permute-start(f32[16,1024]{1,0:T(8,128)S(1)} %add.43), channel_id=1, source_target_pairs={{0,8},{4,12},{8,0},{12,4},{16,24},{20,28},{24,16},{28,20},{1,9},{5... | collective-permute-start | bytes 196616 | tf_op jit(solution)/shard_map/ppermute | solution.py:45
  296.4 10.8 %collective-permute-start.43 = (bf16[1,128,512]{2,1,0:T(8,128)(2,1)S(1)}, bf16[1,128,512]{2,1,0:T(8,128)(2,1)S(1)}, u32[]{:S(2)}, u32[]{:S(2)}) collective-permute-start(bf16[1,128,512]{2,1,0:T(8,128)(2,1)S(1)} %get-tuple-element.349), channel_id=1, source_target_pairs={{0,8},{4,12},{8,0},{12,4},{16,24},{20,28},{24,16},{28,20},{1,9},{5... | collective-permute-start | bytes 393224 | tf_op jit(solution)/shard_map/ppermute | solution.py:45
  306.5 7.5 %collective-permute-start.42 = (f32[16,1024]{1,0:T(8,128)S(1)}, f32[16,1024]{1,0:T(8,128)S(1)}, u32[]{:S(2)}, u32[]{:S(2)}) collective-permute-start(f32[16,1024]{1,0:T(8,128)S(1)} %add.44), channel_id=1, source_target_pairs={{0,2},{1,3},{2,0},{3,1},{4,6},{5,7},{6,4},{7,5},{8,10},{9,11},{10,... | collective-permute-start | bytes 196616 | tf_op jit(solution)/shard_map/ppermute | solution.py:45
  (48 other events, 164.5 us)

commit v15 on v13

--- a/solution.py
+++ b/solution.py
@@ -316,6 +316,7 @@
         [resident(x.shape) for x in outs],
         [],
         rows * columns,
+        room=62,
     )
 
 
@@ -323,14 +324,14 @@
     rows, model = stream.shape
     block = 160
 
-    def kernel(stream_ref, sent_ref, norm_ref, std_ref):
+    def kernel(stream_ref, sent_ref, mean_ref, std_ref):
         field = stream_ref[...]
-        centred = field - jnp.sum(field, axis=1, keepdims=True) / model
+        mean = jnp.sum(field, axis=1, keepdims=True) / model
+        centred = field - mean
         variance = jnp.sum(centred * centred, axis=1, keepdims=True) / model
         scale = lax.rsqrt(variance + eps_norm)
-        norm = centred * scale
-        norm_ref[...] = norm
-        sent_ref[...] = norm.astype(bf16)
+        sent_ref[...] = (centred * scale).astype(bf16)
+        mean_ref[...] = mean
         std_ref[...] = scale
 
     return call(
@@ -340,8 +341,8 @@
         [],
         [stream],
         [step_block(block, model)],
-        [shaped(rows, model), shaped(rows, model, dtype=f32), shaped(rows, 1, dtype=f32)],
-        [step_block(block, model), step_block(block, model), step_block(block, 1)],
+        [shaped(rows, model), shaped(rows, 1, dtype=f32), shaped(rows, 1, dtype=f32)],
+        [step_block(block, model), step_block(block, 1), step_block(block, 1)],
         [],
         rows * model * 8,
         room=62,
@@ -705,7 +706,7 @@
 
         token, grads = block[step % 2], grad_block[step % 2]
         normed = shift_gain(token, gain, shift)
-        count = 2
+        count = 1
         parts = [slice(k * rows // count, (k + 1) * rows // count) for k in range(count)]
         added = bias[pl.ds(ids[0], 1), :]
         hidden = [dot_nn(normed[x], fc_whole[...]) + added for x in parts]
@@ -1003,26 +1004,27 @@
     )
 
 
-def finish_grad(grad, normalized, inv_std, terms):
+def finish_grad(grad, stream, row_mean, inv_std, terms):
     rows, model = grad.shape
     block = 160
 
-    def kernel(grad_ref, norm_ref, std_ref, *refs):
+    def kernel(grad_ref, stream_ref, mean_ref, std_ref, *refs):
         term_refs, out_ref = refs[:-1], refs[-1]
         sent = sum(x[...].astype(f32) for x in term_refs)
-        norm = norm_ref[...]
+        norm = (stream_ref[...] - mean_ref[...]) * std_ref[...]
         mean = jnp.sum(sent, axis=1, keepdims=True) / model
         cross = jnp.sum(sent * norm, axis=1, keepdims=True) / model
         out_ref[...] = grad_ref[...].astype(f32) + std_ref[...] * (sent - mean - norm * cross)
 
-    operands = [grad, normalized, inv_std, *[x for x, _ in terms]]
+    operands = [grad, stream, row_mean, inv_std, *[x for x, _ in terms]]
     return call(
         kernel,
         "finish_grad",
         (rows // block,),
         [],
         operands,
-        [step_block(block, model), step_block(block, model), step_block(block, 1)]
+        [step_block(block, model)] * 2
+        + [step_block(block, 1)] * 2
         + taken(terms, block),
         [shaped(rows, model, dtype=f32)],
         [step_block(block, model)],
@@ -1137,7 +1139,7 @@
     fc_pack = Pack(blocks[2], "dp", rows_first)
     out_pack = Pack(blocks[3], "dp", rows_first)
 
-    sent_norm, normalized, inv_std = normalize(stream_in)
+    sent_norm, row_mean, inv_std = normalize(stream_in)
     sent = gather_far(sent_norm, "tensor", tensor_bits)
 
     info = tree_table(segment_ids, parent_ids)
@@ -1276,7 +1278,7 @@
         sums = sums + swap(sums, "dp", bit)
     sums, back_parts.got = tie(sums, back_parts.got)
     back_parts.add()
-    stream_grad = finish_grad(out_grad, normalized, inv_std, back_parts.terms)
+    stream_grad = finish_grad(out_grad, stream_in, row_mean, inv_std, back_parts.terms)
     sums, stream_grad = tie(sums, stream_grad)
     for bit in tensor_bits[1:]:
         sums = sums + swap(sums, "tensor", bit)

time: 309 us -> 306 us (level)
  local copies, waits for them, and re-layouts: 22.6 us -> 18 us
  starting transfers between devices: 49.3 us -> 52.8 us
    unnamed x135 -> x123, local copies, waits for them, and re-layouts: 17.6 us -> 13 us
    ppermute x46, starting transfers between devices: 49.3 us -> 52.8 us  [swap(): return lax.ppermute(block, axis, [(i, i ^ bit) for i in range(size)])]
  transfers between devices with their start and end apart: 46 -> 46, of which waited for: 21 -> 22; matrix products, arithmetic and copies ran while one was open for 4% -> 4% of each run, Pallas kernels for 50% -> 50%
where the time goes in v15:
time: 306 us; the launch traced here: 305 us
  Pallas kernels  158 us (52%)
  waiting for transfers between devices  66.4 us (22%)
  starting transfers between devices  52.8 us (17%)
  local copies, waits for them, and re-layouts  18 us (6%)
  other arithmetic  8.71 us (3%)
    pallas_call x19, Pallas kernels, call(): pl.pallas_call(kernel, grid_spec=pltpu.PrefetchScalarGridSpec(num_scalar_...  155 us
    ppermute x46, waiting for transfers between devices, swap(): return lax.ppermute(block, axis, [(i, i ^ bit) for i in range(size)])  66.4 us
    ppermute x46, starting transfers between devices, swap(): return lax.ppermute(block, axis, [(i, i ^ bit) for i in range(size)])  52.8 us
    unnamed x123, local copies, waits for them, and re-layouts  13 us
  transfers between devices with their start and end apart: 46, of which 22 were waited for; matrix products, arithmetic and copies ran while one was open for 4% of the time, Pallas kernels for 50%

profile of v15, /device:TPU:0, one launch (start us, length us, event | category | flops | bytes accessed | tf_op | source)
XLA Modules:
  0.0 304.8 jit_solution(16688125923177822688)
XLA Ops:
  1.2 4.2 %normalize.1 = (bf16[640,1024]{1,0:T(8,128)(2,1)}, f32[640,1]{1,0:T(8,128)}, f32[640,1]{1,0:T(8,128)}) custom-call(f32[640,1024]{1,0:T(8,128)} %stream_ref.3), custom_call_target="tpu_custom_call" | custom-call | flops 5242880 | bytes 3937280 | tf_op jit(solution)/shard_map/normalize/pallas_call | solution.py:241
  5.4 2.5 collective-permute-start.4
  8.1 2.5 prepare_weights.1
  10.6 1.5 collective-permute-start.2
  12.1 2.6 collective-permute-start.1
  16.5 2.1 tree_table.1.info
  18.6 5.7 %collective-permute-done.1.refs_5_ = bf16[128,768]{1,0:T(8,128)(2,1)S(1)} collective-permute-done((bf16[128,768]{1,0:T(8,128)(2,1)}, bf16[128,768]{1,0:T(8,128)(2,1)S(1)}, u32[]{:S(2)}, u32[]{:S(2)}) %collective-permute-start.1) | collective-permute-done | bytes 196640 | tf_op jit(solution)/shard_map/ppermute | solution.py:45
  24.4 4.1 %collective-permute-start.5 = (bf16[256,768]{1,0:T(8,128)(2,1)S(1)}, bf16[256,768]{1,0:T(8,128)(2,1)S(1)}, u32[]{:S(2)}, u32[]{:S(2)}) collective-permute-start(bf16[256,768]{1,0:T(8,128)(2,1)S(1)} %pad_maximum_fusion.5), channel_id=1, source_target_pairs={{0,8},{4,12},{8,0},{12,4},{16,24},{20,28},{24,16},{28,20},{1,9},{5... | collective-permute-start | bytes 1179656 | tf_op jit(solution)/shard_map/ppermute | solution.py:45
  28.5 3.8 %fusion = (f32[1280,128]{1,0:T(8,128)}, f32[1280,128]{1,0:T(8,128)}) fusion(s32[128]{0:T(128)S(1)} %get-tuple-element.364, s32[128]{0:T(128)S(1)} %get-tuple-element.365, pred[128]{0:T(512)(128)(4,1)S(1)} %compare_and_fusion, f32[1280]{0:T(1024)S(1)} %convert_add_fusion), kind=kLoop, calls=%fused_computation.9 | loop fusion | flops 3112960 | bytes 1316992 | tf_op jit(solution)/shard_map/jit(_where)/select_n | solution.py:1082
  33.6 4.1 %collective-permute-done.4.refs_2_ = bf16[640,1024]{1,0:T(8,128)(2,1)} collective-permute-done((bf16[640,1024]{1,0:T(8,128)(2,1)}, bf16[640,1024]{1,0:T(8,128)(2,1)}, u32[]{:S(2)}, u32[]{:S(2)}) %collective-permute-start.4) | collective-permute-done | bytes 1310752 | tf_op jit(solution)/shard_map/ppermute | solution.py:45
  37.7 1.2 collective-permute-done.5.refs_6_
  39.7 1.5 collective-permute-start.8
  41.2 2.6 collective-permute-start.11
  43.8 1.6 collective-permute-start.10
  45.4 10.5 %collective-permute-done.11.refs_11_.refs_9_ = bf16[128,1024]{1,0:T(8,128)(2,1)S(1)} collective-permute-done((bf16[128,1024]{1,0:T(8,128)(2,1)S(1)}, bf16[128,1024]{1,0:T(8,128)(2,1)S(1)}, u32[]{:S(2)}, u32[]{:S(2)}) %collective-permute-start.11) | collective-permute-done | bytes 262176 | tf_op jit(solution)/shard_map/ppermute | solution.py:45
  56.2 2.8 collective-permute-done.9.refs_7_
  60.6 1.6 collective-permute-start.14
  62.2 1.5 collective-permute-start.13
  64.3 2.6 collective-permute-start.15
  66.8 11.1 %project_qkv.1 = (bf16[2560,256]{1,0:T(8,128)(2,1)}, bf16[2560,256]{1,0:T(8,128)(2,1)}, bf16[2560,256]{1,0:T(8,128)(2,1)}) custom-call(s32[6]{0:T(128)} %stack.11.ids, s32[1,20,5]{2,1,0:T(8,128)} %tree_table.1.info, bf16[640,1024]{1,0:T(8,128)(2,1)} %copy-done.37, bf16[640,1024]{1,0:T(8,128)(2,1)} %collective-permute-done.3.refs_1_, ...), custom_call_target="tpu_custom_call" | custom-call | flops 4026531840 | bytes 12079104 | tf_op jit(solution)/shard_map/project_qkv/pallas_call | solution.py:241
  78.0 1.8 collective-permute-done.15.refs_15_
  79.8 1.0 collective-permute-done.14.refs_12_.refs_10_
  81.8 2.7 collective-permute-start.17
  84.6 1.2 pad_maximum_fusion
  86.4 5.3 %project_grad.1.do_ref = bf16[2560,256]{1,0:T(8,128)(2,1)S(1)} custom-call(s32[6]{0:T(128)S(1)} %copy-done.32, bf16[384,1024]{1,0:T(8,128)(2,1)} %collective-permute-done.12.refs_0_.refs_4_, bf16[256,1024]{1,0:T(8,128)(2,1)S(1)} %collective-permute-done.16.refs_1_.refs_5_, bf16[640,1024]{1,0:T(8,128)(2,1)} %collective-permute-done.refs_2_.refs_6_, ...), custom_call_target="tpu_custom_call" | custom-call | flops 1342177280 | bytes 7077888 | tf_op jit(solution)/shard_map/project_grad/pallas_call | solution.py:241
  91.8 5.3 %collective-permute-done.17.refs_16_ = bf16[256,1024]{1,0:T(8,128)(2,1)S(1)} collective-permute-done((bf16[256,1024]{1,0:T(8,128)(2,1)S(1)}, bf16[256,1024]{1,0:T(8,128)(2,1)S(1)}, u32[]{:S(2)}, u32[]{:S(2)}) %collective-permute-start.17) | collective-permute-done | bytes 524320 | tf_op jit(solution)/shard_map/ppermute | solution.py:45
  97.2 1.0 pad_maximum_fusion.1
  98.8 49.9 %attention.1 = (bf16[2560,256]{1,0:T(8,128)(2,1)S(1)}, bf16[2560,256]{1,0:T(8,128)(2,1)S(1)}, bf16[2560,256]{1,0:T(8,128)(2,1)S(1)}, bf16[2560,256]{1,0:T(8,128)(2,1)S(1)}) custom-call(s32[1,20,5]{2,1,0:T(8,128)S(1)} %copy-done.31, bf16[2560,256]{1,0:T(8,128)(2,1)S(1)} %copy-done.53, bf16[2560,256]{1,0:T(8,128)(2,1)S(1)} %project_grad.1.do_ref, ...), custom_call_target="tpu_custom_call" | custom-call | flops 31406948352 | bytes 11796480 | tf_op jit(solution)/shard_map/attention/pallas_call | solution.py:241
  150.7 4.1 %project_context.1 = (bf16[1,640,1024]{2,1,0:T(8,128)(2,1)S(1)}, bf16[1,640,1024]{2,1,0:T(8,128)(2,1)S(1)}, bf16[2,640,1024]{2,1,0:T(8,128)(2,1)S(1)}) custom-call(s32[6]{0:T(128)S(1)} %copy-done.32, bf16[2560,256]{1,0:T(8,128)(2,1)S(1)} %get-tuple-element.256.ctx_ref.ctx, bf16[128,256]{1,0:T(8,128)(2,1)S(1)} %copy-done.19, bf16[128,256]{1,0:T(8,128)(2,1)S(1)} %copy-done.21, ...), custom_call_target="tpu_custom_call" | custom-call | flops 1342177280 | bytes 7077888 | tf_op jit(solution)/shard_map/project_context/pallas_call | solution.py:241
  155.4 12.4 %attention_weights.1 = (bf16[2560,768]{1,0:T(8,128)(2,1)S(1)}, f32[8,768]{1,0:T(8,128)S(1)}, bf16[4,128,512]{2,1,0:T(8,128)(2,1)}, bf16[4,128,512]{2,1,0:T(8,128...) custom-call(s32[6]{0:T(128)S(1)} %copy-done.32, s32[1,20,5]{2,1,0:T(8,128)S(1)} %copy-done.31, ...), custom_call_target="tpu_custom_call" | custom-call | flops 5368709120 | bytes 23101440 | tf_op jit(solution)/shard_map/attention_weights/pallas_call | solution.py:241
  167.8 2.0 copy-done.51
  169.8 1.5 collective-permute-start.23
  171.3 1.7 collective-permute-start.24
  173.4 1.5 collective-permute-start.22
  175.0 38.9 %mlp.1 = (bf16[1,640,1024]{2,1,0:T(8,128)(2,1)S(1)}, bf16[1,640,1024]{2,1,0:T(8,128)(2,1)}, bf16[2,640,1024]{2,1,0:T(8,128)(2,1)}, bf16[2560,1024]{1,0:T(8,128)(...) custom-call(s32[6]{0:T(128)S(1)} %copy-done.32, ...), custom_call_target="tpu_custom_call" | custom-call | flops 26843545600 | bytes 29417472 | tf_op jit(solution)/shard_map/mlp/pallas_call | solution.py:241
  214.5 3.6 %collective-permute-done.25.refs_1_ = bf16[1,640,1024]{2,1,0:T(8,128)(2,1)S(1)} collective-permute-done((bf16[1,640,1024]{2,1,0:T(8,128)(2,1)S(1)}, bf16[1,640,1024]{2,1,0:T(8,128)(2,1)S(1)}, u32[]{:S(2)}, u32[]{:S(2)}) %collective-permute-start.25) | collective-permute-done | bytes 1310752 | tf_op jit(solution)/shard_map/ppermute | solution.py:45
  218.1 1.7 copy-done.3
  220.3 1.2 collective-permute-start.27
  223.1 1.6 collective-permute-start.28
  224.7 1.5 collective-permute-start.29
  226.3 2.1 copy-done.52
  228.4 2.5 copy-done.56
  230.9 16.0 %norm_backward.1 = (bf16[1,640,1024]{2,1,0:T(8,128)(2,1)S(1)}, bf16[1,640,1024]{2,1,0:T(8,128)(2,1)S(1)}, bf16[2,640,1024]{2,1,0:T(8,128)(2,1)S(1)}, f32[8,1024]{1,0:T(8,128)S(1)}) custom-call(s32[6]{0:T(128)S(1)} %copy-done.32, bf16[2560,768]{1,0:T(8,128)(2,1)S(1)} %copy-done.52, bf16[2560,1024]{1,0:T(8,128)(2,1)S(1)} %copy-done.56, ...), custom_call_target="tpu_custom_call" | custom-call | flops 9395240960 | bytes 23371776 | tf_op jit(solution)/shard_map/norm_backward/pallas_call | solution.py:241
  246.9 3.4 %collective-permute-done.28.refs_2_ = bf16[2,128,512]{2,1,0:T(8,128)(2,1)S(1)} collective-permute-done((bf16[2,128,512]{2,1,0:T(8,128)(2,1)}, bf16[2,128,512]{2,1,0:T(8,128)(2,1)S(1)}, u32[]{:S(2)}, u32[]{:S(2)}) %collective-permute-start.28) | collective-permute-done | bytes 262176 | tf_op jit(solution)/shard_map/ppermute | solution.py:45
  250.3 1.9 collective-permute-done.29.refs_5_.refs_6_
  252.9 2.5 collective-permute-done.32.refs_1_
  257.2 1.7 collective-permute-start.36
  258.8 1.5 collective-permute-start.37
  260.7 1.3 copy-done.6
  262.0 3.7 %finish_output.1 = (f32[640,1024]{1,0:T(8,128)}, f32[16,1024]{1,0:T(8,128)S(1)}) custom-call(s32[6]{0:T(128)S(1)} %copy-done.32, f32[640,1024]{1,0:T(8,128)S(1)} %copy-done, bf16[640,1024]{1,0:T(8,128)(2,1)S(1)} %copy-done.2, bf16[2,640,1024]{2,1,0:T(8,128)(2,1)S(1)} %get-tuple-element.269.refs_0_, ...), custom_call_target="tpu_custom_call" | custom-call | flops 10485760 | bytes 17203200 | tf_op jit(solution)/shard_map/finish_output/pallas_call | solution.py:241
  265.7 1.3 collective-permute-done.34
  267.0 2.7 collective-permute-start.35
  269.6 4.0 %collective-permute-done.38.refs_7_ = bf16[1,128,512]{2,1,0:T(8,128)(2,1)S(1)} collective-permute-done((bf16[1,128,512]{2,1,0:T(8,128)(2,1)S(1)}, bf16[1,128,512]{2,1,0:T(8,128)(2,1)S(1)}, u32[]{:S(2)}, u32[]{:S(2)}) %collective-permute-start.38) | collective-permute-done | bytes 131104 | tf_op jit(solution)/shard_map/ppermute | solution.py:45
  273.6 1.3 collective-permute-done.36.refs_2_
  274.9 1.3 collective-permute-done.35
  276.5 1.5 collective-permute-start.44
  278.0 1.4 collective-permute-start.45
  279.9 3.9 %collective-permute-done.39 = f32[16,1024]{1,0:T(8,128)S(1)} collective-permute-done((f32[16,1024]{1,0:T(8,128)S(1)}, f32[16,1024]{1,0:T(8,128)S(1)}, u32[]{:S(2)}, u32[]{:S(2)}) %collective-permute-start.39) | collective-permute-done | bytes 65568 | tf_op jit(solution)/shard_map/ppermute | solution.py:45
  284.2 1.7 collective-permute-start.43
  285.8 5.3 %collective-permute-done.40 = f32[16,1024]{1,0:T(8,128)S(1)} collective-permute-done((f32[16,1024]{1,0:T(8,128)S(1)}, f32[16,1024]{1,0:T(8,128)S(1)}, u32[]{:S(2)}, u32[]{:S(2)}) %collective-permute-start.40) | collective-permute-done | bytes 65568 | tf_op jit(solution)/shard_map/ppermute | solution.py:45
  291.2 2.8 finish_grad.1
  294.0 1.1 collective-permute-start.42
  296.1 4.2 %collective-permute-done.45.refs_7_ = bf16[1,128,1024]{2,1,0:T(8,128)(2,1)S(1)} collective-permute-done((bf16[1,128,1024]{2,1,0:T(8,128)(2,1)S(1)}, bf16[1,128,1024]{2,1,0:T(8,128)(2,1)S(1)}, u32[]{:S(2)}, u32[]{:S(2)}) %collective-permute-start.45) | collective-permute-done | bytes 262176 | tf_op jit(solution)/shard_map/ppermute | solution.py:45
  300.3 1.2 finish_mlp_weights.1
  (200 shorter events, 22.8 us)
Async XLA Ops:
  0.6 23.6 %collective-permute-start = (bf16[640,1024]{1,0:T(8,128)(2,1)}, bf16[640,1024]{1,0:T(8,128)(2,1)}, u32[]{:S(2)}, u32[]{:S(2)}) collective-permute-start(bf16[640,1024]{1,0:T(8,128)(2,1)} %grad_ref.3), channel_id=1, source_target_pairs={{0,1},{1,0},{2,3},{3,2},{4,5},{5,4},{6,7},{7,6},{8,9},{9,8},{10,11... | collective-permute-start | bytes 3932168 | tf_op jit(solution)/shard_map/ppermute | solution.py:45
  5.4 9.3 %copy-start.1 = (bf16[640,1024]{1,0:T(8,128)(2,1)S(1)}, bf16[640,1024]{1,0:T(8,128)(2,1)}, u32[]{:S(2)}) copy-start(bf16[640,1024]{1,0:T(8,128)(2,1)} %grad_ref.3) | copy-start | bytes 3932164
  5.4 32.3 %collective-permute-start.4 = (bf16[640,1024]{1,0:T(8,128)(2,1)}, bf16[640,1024]{1,0:T(8,128)(2,1)}, u32[]{:S(2)}, u32[]{:S(2)}) collective-permute-start(bf16[640,1024]{1,0:T(8,128)(2,1)} %get-tuple-element.217.refs_3_), channel_id=1, source_target_pairs={{0,2},{1,3},{2,0},{3,1},{4,6},{5,7},{6,4},{7,5},{8,10},{9,11},{10,... | collective-permute-start | bytes 3932168 | tf_op jit(solution)/shard_map/ppermute | solution.py:45
  7.9 29.7 %collective-permute-start.3 = (bf16[640,1024]{1,0:T(8,128)(2,1)}, bf16[640,1024]{1,0:T(8,128)(2,1)}, u32[]{:S(2)}, u32[]{:S(2)}) collective-permute-start(bf16[640,1024]{1,0:T(8,128)(2,1)} %get-tuple-element.217.refs_3_), channel_id=1, source_target_pairs={{0,1},{1,0},{2,3},{3,2},{4,5},{5,4},{6,7},{7,6},{8,9},{9,8},{10,11... | collective-permute-start | bytes 3932168 | tf_op jit(solution)/shard_map/ppermute | solution.py:45
  10.6 8.0 %collective-permute-start.2 = (bf16[128,256]{1,0:T(8,128)(2,1)}, bf16[128,256]{1,0:T(8,128)(2,1)S(1)}, u32[]{:S(2)}, u32[]{:S(2)}) collective-permute-start(bf16[128,256]{1,0:T(8,128)(2,1)} %get-tuple-element.237.refs_6_.refs_0_), channel_id=1, source_target_pairs={{0,4},{4,0},{8,12},{12,8},{16,20},{20,16},{24,28},{28,24},{1,5},{5... | collective-permute-start | bytes 196616 | tf_op jit(solution)/shard_map/ppermute | solution.py:45
  12.1 12.2 %copy-start.18 = (bf16[128,256]{1,0:T(8,128)(2,1)S(1)}, bf16[128,256]{1,0:T(8,128)(2,1)}, u32[]{:S(2)}) copy-start(bf16[128,256]{1,0:T(8,128)(2,1)} %get-tuple-element.237.refs_6_.refs_0_) | copy-start | bytes 196612
  12.1 12.3 %copy-start.12 = (bf16[128,768]{1,0:T(8,128)(2,1)S(1)}, bf16[128,768]{1,0:T(8,128)(2,1)}, u32[]{:S(2)}) copy-start(bf16[128,768]{1,0:T(8,128)(2,1)} %get-tuple-element.218.refs_4_) | copy-start | bytes 589828
  12.1 12.2 %collective-permute-start.1 = (bf16[128,768]{1,0:T(8,128)(2,1)}, bf16[128,768]{1,0:T(8,128)(2,1)S(1)}, u32[]{:S(2)}, u32[]{:S(2)}) collective-permute-start(bf16[128,768]{1,0:T(8,128)(2,1)} %get-tuple-element.218.refs_4_), channel_id=1, source_target_pairs={{0,16},{4,20},{8,24},{12,28},{16,0},{20,4},{24,8},{28,12},{1,17},{... | collective-permute-start | bytes 589832 | tf_op jit(solution)/shard_map/ppermute | solution.py:45
  16.5 15.9 %copy-start.59 = (f32[3072]{0:T(1024)S(1)}, f32[3072]{0:T(1024)}, u32[]{:S(2)}) copy-start(f32[3072]{0:T(1024)} %param.24) | copy-start | bytes 36868
  16.5 16.5 %copy-start.58 = (f32[4096]{0:T(1024)S(1)}, f32[4096]{0:T(1024)}, u32[]{:S(2)}) copy-start(f32[4096]{0:T(1024)} %param.28) | copy-start | bytes 49156
  18.6 25.2 %copy-start.20 = (bf16[128,256]{1,0:T(8,128)(2,1)}, bf16[128,256]{1,0:T(8,128)(2,1)S(1)}, u32[]{:S(2)}) copy-start(bf16[128,256]{1,0:T(8,128)(2,1)S(1)} %collective-permute-done.2.refs_7_.refs_1_) | copy-start | bytes 196612
  24.3 14.7 %copy-start.14 = (bf16[128,768]{1,0:T(8,128)(2,1)}, bf16[128,768]{1,0:T(8,128)(2,1)S(1)}, u32[]{:S(2)}) copy-start(bf16[128,768]{1,0:T(8,128)(2,1)S(1)} %collective-permute-done.1.refs_5_) | copy-start | bytes 589828
  24.3 13.3 %collective-permute-start.6 = (bf16[256,256]{1,0:T(8,128)(2,1)S(1)}, bf16[256,256]{1,0:T(8,128)(2,1)S(1)}, u32[]{:S(2)}, u32[]{:S(2)}) collective-permute-start(bf16[256,256]{1,0:T(8,128)(2,1)S(1)} %pad_maximum_fusion.7), channel_id=1, source_target_pairs={{0,16},{4,20},{8,24},{12,28},{16,0},{20,4},{24,8},{28,12},{1,17},{... | collective-permute-start | bytes 393224 | tf_op jit(solution)/shard_map/ppermute | solution.py:45
  24.4 14.5 %collective-permute-start.5 = (bf16[256,768]{1,0:T(8,128)(2,1)S(1)}, bf16[256,768]{1,0:T(8,128)(2,1)S(1)}, u32[]{:S(2)}, u32[]{:S(2)}) collective-permute-start(bf16[256,768]{1,0:T(8,128)(2,1)S(1)} %pad_maximum_fusion.5), channel_id=1, source_target_pairs={{0,8},{4,12},{8,0},{12,4},{16,24},{20,28},{24,16},{28,20},{1,9},{5... | collective-permute-start | bytes 1179656 | tf_op jit(solution)/shard_map/ppermute | solution.py:45
  28.5 12.7 %copy-start.7 = (bf16[128,1024]{1,0:T(8,128)(2,1)S(1)}, bf16[128,1024]{1,0:T(8,128)(2,1)}, u32[]{:S(2)}) copy-start(bf16[128,1024]{1,0:T(8,128)(2,1)} %get-tuple-element.272.refs_10_.refs_8_) | copy-start | bytes 786436
  37.7 22.9 %copy-start.22 = (bf16[256,256]{1,0:T(8,128)(2,1)}, bf16[256,256]{1,0:T(8,128)(2,1)S(1)}, u32[]{:S(2)}) copy-start(bf16[256,256]{1,0:T(8,128)(2,1)S(1)} %collective-permute-done.6.refs_8_.refs_2_) | copy-start | bytes 393220
  38.9 21.7 %copy-start.24 = (bf16[256,768]{1,0:T(8,128)(2,1)}, bf16[256,768]{1,0:T(8,128)(2,1)S(1)}, u32[]{:S(2)}) copy-start(bf16[256,768]{1,0:T(8,128)(2,1)S(1)} %collective-permute-done.5.refs_6_) | copy-start | bytes 1179652
  38.9 25.3 %copy-start.8 = (bf16[128,1024]{1,0:T(8,128)(2,1)S(1)}, bf16[128,1024]{1,0:T(8,128)(2,1)}, u32[]{:S(2)}) copy-start(bf16[128,1024]{1,0:T(8,128)(2,1)} %get-tuple-element.276.refs_14_) | copy-start | bytes 786436
  38.9 20.7 %collective-permute-start.7 = (bf16[640,1024]{1,0:T(8,128)(2,1)}, bf16[640,1024]{1,0:T(8,128)(2,1)S(1)}, u32[]{:S(2)}, u32[]{:S(2)}) collective-permute-start(bf16[640,1024]{1,0:T(8,128)(2,1)} %collective-permute-done.4.refs_2_), channel_id=1, source_target_pairs={{0,1},{1,0},{2,3},{3,2},{4,5},{5,4},{6,7},{7,6},{8,9},{9,8},{10,11... | collective-permute-start | bytes 3932168 | tf_op jit(solution)/shard_map/ppermute | solution.py:45
  39.0 20.0 %collective-permute-start.9 = (bf16[512,768]{1,0:T(8,128)(2,1)S(1)}, bf16[512,768]{1,0:T(8,128)(2,1)S(1)}, u32[]{:S(2)}, u32[]{:S(2)}) collective-permute-start(bf16[512,768]{1,0:T(8,128)(2,1)S(1)} %pad_maximum_fusion.2), channel_id=1, source_target_pairs={{0,4},{4,0},{8,12},{12,8},{16,20},{20,16},{24,28},{28,24},{1,5},{5... | collective-permute-start | bytes 2359304 | tf_op jit(solution)/shard_map/ppermute | solution.py:45
  39.7 20.0 %collective-permute-start.8 = (bf16[384,1024]{1,0:T(8,128)(2,1)}, bf16[384,1024]{1,0:T(8,128)(2,1)}, u32[]{:S(2)}, u32[]{:S(2)}) collective-permute-start(bf16[384,1024]{1,0:T(8,128)(2,1)} %slice.30), channel_id=1, source_target_pairs={{0,2},{1,3},{2,0},{3,1},{4,6},{5,7},{6,4},{7,5},{8,10},{9,11},{10,... | collective-permute-start | bytes 2359304 | tf_op jit(solution)/shard_map/ppermute | solution.py:45
  41.2 14.8 %collective-permute-start.11 = (bf16[128,1024]{1,0:T(8,128)(2,1)S(1)}, bf16[128,1024]{1,0:T(8,128)(2,1)S(1)}, u32[]{:S(2)}, u32[]{:S(2)}) collective-permute-start(bf16[128,1024]{1,0:T(8,128)(2,1)S(1)} %copy-done.7), channel_id=1, source_target_pairs={{0,16},{4,20},{8,24},{12,28},{16,0},{20,4},{24,8},{28,12},{1,17},{... | collective-permute-start | bytes 786440 | tf_op jit(solution)/shard_map/ppermute | solution.py:45
  43.8 12.4 %collective-permute-start.10 = (bf16[512,256]{1,0:T(8,128)(2,1)S(1)}, bf16[512,256]{1,0:T(8,128)(2,1)S(1)}, u32[]{:S(2)}, u32[]{:S(2)}) collective-permute-start(bf16[512,256]{1,0:T(8,128)(2,1)S(1)} %pad_maximum_fusion.6), channel_id=1, source_target_pairs={{0,8},{4,12},{8,0},{12,4},{16,24},{20,28},{24,16},{28,20},{1,9},{5... | collective-permute-start | bytes 786440 | tf_op jit(solution)/shard_map/ppermute | solution.py:45
  56.2 7.4 %copy-start.28 = (bf16[512,256]{1,0:T(8,128)(2,1)}, bf16[512,256]{1,0:T(8,128)(2,1)S(1)}, u32[]{:S(2)}) copy-start(bf16[512,256]{1,0:T(8,128)(2,1)S(1)} %collective-permute-done.10.refs_9_.refs_3_) | copy-start | bytes 786436
  59.7 21.1 %collective-permute-start.12 = (bf16[384,1024]{1,0:T(8,128)(2,1)}, bf16[384,1024]{1,0:T(8,128)(2,1)}, u32[]{:S(2)}, u32[]{:S(2)}) collective-permute-start(bf16[384,1024]{1,0:T(8,128)(2,1)} %collective-permute-done.8.refs_3_.refs_7_), channel_id=1, source_target_pairs={{0,1},{1,0},{2,3},{3,2},{4,5},{5,4},{6,7},{7,6},{8,9},{9,8},{10,11... | collective-permute-start | bytes 2359304 | tf_op jit(solution)/shard_map/ppermute | solution.py:45
  60.6 20.2 %collective-permute-start.14 = (bf16[256,1024]{1,0:T(8,128)(2,1)}, bf16[256,1024]{1,0:T(8,128)(2,1)}, u32[]{:S(2)}, u32[]{:S(2)}) collective-permute-start(bf16[256,1024]{1,0:T(8,128)(2,1)} %pad_maximum_fusion.3), channel_id=1, source_target_pairs={{0,8},{4,12},{8,0},{12,4},{16,24},{20,28},{24,16},{28,20},{1,9},{5... | collective-permute-start | bytes 1572872 | tf_op jit(solution)/shard_map/ppermute | solution.py:45
  62.2 18.6 %collective-permute-start.13 = (bf16[256,1024]{1,0:T(8,128)(2,1)}, bf16[256,1024]{1,0:T(8,128)(2,1)}, u32[]{:S(2)}, u32[]{:S(2)}) collective-permute-start(bf16[256,1024]{1,0:T(8,128)(2,1)} %slice.31), channel_id=1, source_target_pairs={{0,2},{1,3},{2,0},{3,1},{4,6},{5,7},{6,4},{7,5},{8,10},{9,11},{10,... | collective-permute-start | bytes 1572872 | tf_op jit(solution)/shard_map/ppermute | solution.py:45
  64.3 15.5 %collective-permute-start.15 = (bf16[128,1024]{1,0:T(8,128)(2,1)S(1)}, bf16[128,1024]{1,0:T(8,128)(2,1)}, u32[]{:S(2)}, u32[]{:S(2)}) collective-permute-start(bf16[128,1024]{1,0:T(8,128)(2,1)S(1)} %copy-done.8), channel_id=1, source_target_pairs={{0,16},{4,20},{8,24},{12,28},{16,0},{20,4},{24,8},{28,12},{1,17},{... | collective-permute-start | bytes 786440 | tf_op jit(solution)/shard_map/ppermute | solution.py:45
  80.8 5.6 %collective-permute-start.16 = (bf16[256,1024]{1,0:T(8,128)(2,1)}, bf16[256,1024]{1,0:T(8,128)(2,1)S(1)}, u32[]{:S(2)}, u32[]{:S(2)}) collective-permute-start(bf16[256,1024]{1,0:T(8,128)(2,1)} %collective-permute-done.13.refs_4_.refs_8_), channel_id=1, source_target_pairs={{0,1},{1,0},{2,3},{3,2},{4,5},{5,4},{6,7},{7,6},{8,9},{9,8},{10,11... | collective-permute-start | bytes 1572872 | tf_op jit(solution)/shard_map/ppermute | solution.py:45
  81.8 15.3 %collective-permute-start.17 = (bf16[256,1024]{1,0:T(8,128)(2,1)S(1)}, bf16[256,1024]{1,0:T(8,128)(2,1)S(1)}, u32[]{:S(2)}, u32[]{:S(2)}) collective-permute-start(bf16[256,1024]{1,0:T(8,128)(2,1)S(1)} %pad_maximum_fusion.4), channel_id=1, source_target_pairs={{0,8},{4,12},{8,0},{12,4},{16,24},{20,28},{24,16},{28,20},{1,9},{5... | collective-permute-start | bytes 1572872 | tf_op jit(solution)/shard_map/ppermute | solution.py:45
  85.7 63.0 %collective-permute-start.18 = (bf16[512,1024]{1,0:T(8,128)(2,1)S(1)}, bf16[512,1024]{1,0:T(8,128)(2,1)S(1)}, u32[]{:S(2)}, u32[]{:S(2)}) collective-permute-start(bf16[512,1024]{1,0:T(8,128)(2,1)S(1)} %pad_maximum_fusion), channel_id=1, source_target_pairs={{0,4},{4,0},{8,12},{12,8},{16,20},{20,16},{24,28},{28,24},{1,5},{5... | collective-permute-start | bytes 3145736 | tf_op jit(solution)/shard_map/ppermute | solution.py:45
  86.4 12.4 %copy-start.53 = (bf16[2560,256]{1,0:T(8,128)(2,1)S(1)}, bf16[2560,256]{1,0:T(8,128)(2,1)}, u32[]{:S(2)}) copy-start(bf16[2560,256]{1,0:T(8,128)(2,1)} %get-tuple-element.233.q_ref) | copy-start | bytes 3932164
  86.4 12.4 %copy-start.54 = (bf16[2560,256]{1,0:T(8,128)(2,1)S(1)}, bf16[2560,256]{1,0:T(8,128)(2,1)}, u32[]{:S(2)}) copy-start(bf16[2560,256]{1,0:T(8,128)(2,1)} %get-tuple-element.244.k_ref) | copy-start | bytes 3932164
  86.4 12.4 %copy-start.55 = (bf16[2560,256]{1,0:T(8,128)(2,1)S(1)}, bf16[2560,256]{1,0:T(8,128)(2,1)}, u32[]{:S(2)}) copy-start(bf16[2560,256]{1,0:T(8,128)(2,1)} %get-tuple-element.245.v_ref) | copy-start | bytes 3932164
  91.8 7.0 %copy-start.16 = (f32[1280,128]{1,0:T(8,128)S(1)}, f32[1280,128]{1,0:T(8,128)}, u32[]{:S(2)}) copy-start(f32[1280,128]{1,0:T(8,128)} %get-tuple-element.224.refs_12_.sine.refs_13_) | copy-start | bytes 1966084
  98.2 51.6 %collective-permute-start.19 = (bf16[512,1024]{1,0:T(8,128)(2,1)S(1)}, bf16[512,1024]{1,0:T(8,128)(2,1)S(1)}, u32[]{:S(2)}, u32[]{:S(2)}) collective-permute-start(bf16[512,1024]{1,0:T(8,128)(2,1)S(1)} %pad_maximum_fusion.1), channel_id=1, source_target_pairs={{0,4},{4,0},{8,12},{12,8},{16,20},{20,16},{24,28},{28,24},{1,5},{5... | collective-permute-start | bytes 3145736 | tf_op jit(solution)/shard_map/ppermute | solution.py:45
  154.8 15.0 %collective-permute-start.20 = (bf16[1,640,1024]{2,1,0:T(8,128)(2,1)S(1)}, bf16[1,640,1024]{2,1,0:T(8,128)(2,1)S(1)}, u32[]{:S(2)}, u32[]{:S(2)}) collective-permute-start(bf16[1,640,1024]{2,1,0:T(8,128)(2,1)S(1)} %get-tuple-element.266), channel_id=1, source_target_pairs={{0,1},{1,0},{2,3},{3,2},{4,5},{5,4},{6,7},{7,6},{8,9},{9,8},{10,11... | collective-permute-start | bytes 3932168 | tf_op jit(solution)/shard_map/ppermute | solution.py:45
  154.9 14.9 %collective-permute-start.21 = (bf16[1,640,1024]{2,1,0:T(8,128)(2,1)S(1)}, bf16[1,640,1024]{2,1,0:T(8,128)(2,1)S(1)}, u32[]{:S(2)}, u32[]{:S(2)}) collective-permute-start(bf16[1,640,1024]{2,1,0:T(8,128)(2,1)S(1)} %get-tuple-element.267), channel_id=1, source_target_pairs={{0,1},{1,0},{2,3},{3,2},{4,5},{5,4},{6,7},{7,6},{8,9},{9,8},{10,11... | collective-permute-start | bytes 3932168 | tf_op jit(solution)/shard_map/ppermute | solution.py:45
  169.8 44.1 %collective-permute-start.23 = (bf16[4,128,512]{2,1,0:T(8,128)(2,1)}, bf16[4,128,512]{2,1,0:T(8,128)(2,1)S(1)}, u32[]{:S(2)}, u32[]{:S(2)}) collective-permute-start(bf16[4,128,512]{2,1,0:T(8,128)(2,1)} %get-tuple-element.291), channel_id=1, source_target_pairs={{0,4},{4,0},{8,12},{12,8},{16,20},{20,16},{24,28},{28,24},{1,5},{5... | collective-permute-start | bytes 1572872 | tf_op jit(solution)/shard_map/ppermute | solution.py:45
  171.3 42.7 %collective-permute-start.24 = (bf16[4,128,512]{2,1,0:T(8,128)(2,1)}, bf16[4,128,512]{2,1,0:T(8,128)(2,1)S(1)}, u32[]{:S(2)}, u32[]{:S(2)}) collective-permute-start(bf16[4,128,512]{2,1,0:T(8,128)(2,1)} %get-tuple-element.292), channel_id=1, source_target_pairs={{0,8},{4,12},{8,0},{12,4},{16,24},{20,28},{24,16},{28,20},{1,9},{5... | collective-permute-start | bytes 1572872 | tf_op jit(solution)/shard_map/ppermute | solution.py:45
  173.4 40.5 %collective-permute-start.22 = (bf16[1,640,1024]{2,1,0:T(8,128)(2,1)S(1)}, bf16[1,640,1024]{2,1,0:T(8,128)(2,1)S(1)}, u32[]{:S(2)}, u32[]{:S(2)}) collective-permute-start(bf16[1,640,1024]{2,1,0:T(8,128)(2,1)S(1)} %add_terms.3), channel_id=1, source_target_pairs={{0,2},{1,3},{2,0},{3,1},{4,6},{5,7},{6,4},{7,5},{8,10},{9,11},{10,... | collective-permute-start | bytes 3932168 | tf_op jit(solution)/shard_map/ppermute | solution.py:45
  213.9 4.2 %collective-permute-start.25 = (bf16[1,640,1024]{2,1,0:T(8,128)(2,1)S(1)}, bf16[1,640,1024]{2,1,0:T(8,128)(2,1)S(1)}, u32[]{:S(2)}, u32[]{:S(2)}) collective-permute-start(bf16[1,640,1024]{2,1,0:T(8,128)(2,1)S(1)} %get-tuple-element.295), channel_id=1, source_target_pairs={{0,1},{1,0},{2,3},{3,2},{4,5},{5,4},{6,7},{7,6},{8,9},{9,8},{10,11... | collective-permute-start | bytes 3932168 | tf_op jit(solution)/shard_map/ppermute | solution.py:45
  214.0 10.7 %collective-permute-start.26 = (bf16[1,640,1024]{2,1,0:T(8,128)(2,1)}, bf16[1,640,1024]{2,1,0:T(8,128)(2,1)S(1)}, u32[]{:S(2)}, u32[]{:S(2)}) collective-permute-start(bf16[1,640,1024]{2,1,0:T(8,128)(2,1)} %get-tuple-element.297), channel_id=1, source_target_pairs={{0,1},{1,0},{2,3},{3,2},{4,5},{5,4},{6,7},{7,6},{8,9},{9,8},{10,11... | collective-permute-start | bytes 3932168 | tf_op jit(solution)/shard_map/ppermute | solution.py:45
  220.3 32.2 %collective-permute-start.27 = (bf16[1,640,1024]{2,1,0:T(8,128)(2,1)S(1)}, bf16[1,640,1024]{2,1,0:T(8,128)(2,1)S(1)}, u32[]{:S(2)}, u32[]{:S(2)}) collective-permute-start(bf16[1,640,1024]{2,1,0:T(8,128)(2,1)S(1)} %add_terms.4), channel_id=1, source_target_pairs={{0,2},{1,3},{2,0},{3,1},{4,6},{5,7},{6,4},{7,5},{8,10},{9,11},{10,... | collective-permute-start | bytes 3932168 | tf_op jit(solution)/shard_map/ppermute | solution.py:45
  221.4 30.8 %collective-permute-start.30 = (bf16[4,128,1024]{2,1,0:T(8,128)(2,1)}, bf16[4,128,1024]{2,1,0:T(8,128)(2,1)S(1)}, u32[]{:S(2)}, u32[]{:S(2)}) collective-permute-start(bf16[4,128,1024]{2,1,0:T(8,128)(2,1)} %get-tuple-element.310), channel_id=1, source_target_pairs={{0,4},{4,0},{8,12},{12,8},{16,20},{20,16},{24,28},{28,24},{1,5},{5... | collective-permute-start | bytes 3145736 | tf_op jit(solution)/shard_map/ppermute | solution.py:45
  222.0 30.5 %collective-permute-start.31 = (bf16[4,128,1024]{2,1,0:T(8,128)(2,1)}, bf16[4,128,1024]{2,1,0:T(8,128)(2,1)S(1)}, u32[]{:S(2)}, u32[]{:S(2)}) collective-permute-start(bf16[4,128,1024]{2,1,0:T(8,128)(2,1)} %get-tuple-element.311), channel_id=1, source_target_pairs={{0,8},{4,12},{8,0},{12,4},{16,24},{20,28},{24,16},{28,20},{1,9},{5... | collective-permute-start | bytes 3145736 | tf_op jit(solution)/shard_map/ppermute | solution.py:45
  223.1 27.3 %collective-permute-start.28 = (bf16[2,128,512]{2,1,0:T(8,128)(2,1)}, bf16[2,128,512]{2,1,0:T(8,128)(2,1)S(1)}, u32[]{:S(2)}, u32[]{:S(2)}) collective-permute-start(bf16[2,128,512]{2,1,0:T(8,128)(2,1)} %get-tuple-element.308), channel_id=1, source_target_pairs={{0,16},{4,20},{8,24},{12,28},{16,0},{20,4},{24,8},{28,12},{1,17},{... | collective-permute-start | bytes 786440 | tf_op jit(solution)/shard_map/ppermute | solution.py:45
  224.7 27.5 %collective-permute-start.29 = (bf16[2,128,512]{2,1,0:T(8,128)(2,1)}, bf16[2,128,512]{2,1,0:T(8,128)(2,1)S(1)}, u32[]{:S(2)}, u32[]{:S(2)}) collective-permute-start(bf16[2,128,512]{2,1,0:T(8,128)(2,1)} %get-tuple-element.309), channel_id=1, source_target_pairs={{0,4},{4,0},{8,12},{12,8},{16,20},{20,16},{24,28},{28,24},{1,5},{5... | collective-permute-start | bytes 786440 | tf_op jit(solution)/shard_map/ppermute | solution.py:45
  252.4 3.0 collective-permute-start.32
  252.4 8.2 %collective-permute-start.33 = (bf16[1,640,1024]{2,1,0:T(8,128)(2,1)S(1)}, bf16[1,640,1024]{2,1,0:T(8,128)(2,1)S(1)}, u32[]{:S(2)}, u32[]{:S(2)}) collective-permute-start(bf16[1,640,1024]{2,1,0:T(8,128)(2,1)S(1)} %get-tuple-element.315), channel_id=1, source_target_pairs={{0,1},{1,0},{2,3},{3,2},{4,5},{5,4},{6,7},{7,6},{8,9},{9,8},{10,11... | collective-permute-start | bytes 3932168 | tf_op jit(solution)/shard_map/ppermute | solution.py:45
  255.9 35.3 %collective-permute-start.41 = (bf16[1,640,1024]{2,1,0:T(8,128)(2,1)S(1)}, bf16[1,640,1024]{2,1,0:T(8,128)(2,1)S(1)}, u32[]{:S(2)}, u32[]{:S(2)}) collective-permute-start(bf16[1,640,1024]{2,1,0:T(8,128)(2,1)S(1)} %add_terms.5), channel_id=1, source_target_pairs={{0,2},{1,3},{2,0},{3,1},{4,6},{5,7},{6,4},{7,5},{8,10},{9,11},{10,... | collective-permute-start | bytes 3932168 | tf_op jit(solution)/shard_map/ppermute | solution.py:45
  257.2 17.7 %collective-permute-start.36 = (bf16[2,128,1024]{2,1,0:T(8,128)(2,1)S(1)}, bf16[2,128,1024]{2,1,0:T(8,128)(2,1)S(1)}, u32[]{:S(2)}, u32[]{:S(2)}) collective-permute-start(bf16[2,128,1024]{2,1,0:T(8,128)(2,1)S(1)} %get-tuple-element.332), channel_id=1, source_target_pairs={{0,8},{4,12},{8,0},{12,4},{16,24},{20,28},{24,16},{28,20},{1,9},{5... | collective-permute-start | bytes 1572872 | tf_op jit(solution)/shard_map/ppermute | solution.py:45
  258.8 16.1 %collective-permute-start.37 = (bf16[2,128,1024]{2,1,0:T(8,128)(2,1)S(1)}, bf16[2,128,1024]{2,1,0:T(8,128)(2,1)S(1)}, u32[]{:S(2)}, u32[]{:S(2)}) collective-permute-start(bf16[2,128,1024]{2,1,0:T(8,128)(2,1)S(1)} %get-tuple-element.333), channel_id=1, source_target_pairs={{0,4},{4,0},{8,12},{12,8},{16,20},{20,16},{24,28},{28,24},{1,5},{5... | collective-permute-start | bytes 1572872 | tf_op jit(solution)/shard_map/ppermute | solution.py:45
  260.3 13.2 %collective-permute-start.38 = (bf16[1,128,512]{2,1,0:T(8,128)(2,1)S(1)}, bf16[1,128,512]{2,1,0:T(8,128)(2,1)S(1)}, u32[]{:S(2)}, u32[]{:S(2)}) collective-permute-start(bf16[1,128,512]{2,1,0:T(8,128)(2,1)S(1)} %get-tuple-element.334), channel_id=1, source_target_pairs={{0,16},{4,20},{8,24},{12,28},{16,0},{20,4},{24,8},{28,12},{1,17},{... | collective-permute-start | bytes 393224 | tf_op jit(solution)/shard_map/ppermute | solution.py:45
  265.7 1.3 collective-permute-start.34
  267.0 9.3 %collective-permute-start.35 = (f32[16,1024]{1,0:T(8,128)S(1)}, f32[16,1024]{1,0:T(8,128)S(1)}, u32[]{:S(2)}, u32[]{:S(2)}) collective-permute-start(f32[16,1024]{1,0:T(8,128)S(1)} %add.41), channel_id=1, source_target_pairs={{0,16},{4,20},{8,24},{12,28},{16,0},{20,4},{24,8},{28,12},{1,17},{... | collective-permute-start | bytes 196616 | tf_op jit(solution)/shard_map/ppermute | solution.py:45
  276.3 14.9 %copy-start.26 = (f32[640,1]{1,0:T(8,128)S(1)}, f32[640,1]{1,0:T(8,128)}, u32[]{:S(2)}) copy-start(f32[640,1]{1,0:T(8,128)} %get-tuple-element.343.mean_ref) | copy-start | bytes 7684
  276.3 14.9 %copy-start.27 = (f32[640,1]{1,0:T(8,128)S(1)}, f32[640,1]{1,0:T(8,128)}, u32[]{:S(2)}) copy-start(f32[640,1]{1,0:T(8,128)} %get-tuple-element.344.std_ref) | copy-start | bytes 7684
  276.5 19.6 %collective-permute-start.44 = (bf16[1,128,1024]{2,1,0:T(8,128)(2,1)S(1)}, bf16[1,128,1024]{2,1,0:T(8,128)(2,1)S(1)}, u32[]{:S(2)}, u32[]{:S(2)}) collective-permute-start(bf16[1,128,1024]{2,1,0:T(8,128)(2,1)S(1)} %get-tuple-element.353), channel_id=1, source_target_pairs={{0,16},{4,20},{8,24},{12,28},{16,0},{20,4},{24,8},{28,12},{1,17},{... | collective-permute-start | bytes 786440 | tf_op jit(solution)/shard_map/ppermute | solution.py:45
  278.0 22.3 %collective-permute-start.45 = (bf16[1,128,1024]{2,1,0:T(8,128)(2,1)S(1)}, bf16[1,128,1024]{2,1,0:T(8,128)(2,1)S(1)}, u32[]{:S(2)}, u32[]{:S(2)}) collective-permute-start(bf16[1,128,1024]{2,1,0:T(8,128)(2,1)S(1)} %get-tuple-element.354), channel_id=1, source_target_pairs={{0,16},{4,20},{8,24},{12,28},{16,0},{20,4},{24,8},{28,12},{1,17},{... | collective-permute-start | bytes 786440 | tf_op jit(solution)/shard_map/ppermute | solution.py:45
  279.5 4.3 %collective-permute-start.39 = (f32[16,1024]{1,0:T(8,128)S(1)}, f32[16,1024]{1,0:T(8,128)S(1)}, u32[]{:S(2)}, u32[]{:S(2)}) collective-permute-start(f32[16,1024]{1,0:T(8,128)S(1)} %add.42), channel_id=1, source_target_pairs={{0,4},{4,0},{8,12},{12,8},{16,20},{20,16},{24,28},{28,24},{1,5},{5... | collective-permute-start | bytes 196616 | tf_op jit(solution)/shard_map/ppermute | solution.py:45
  283.7 7.4 %collective-permute-start.40 = (f32[16,1024]{1,0:T(8,128)S(1)}, f32[16,1024]{1,0:T(8,128)S(1)}, u32[]{:S(2)}, u32[]{:S(2)}) collective-permute-start(f32[16,1024]{1,0:T(8,128)S(1)} %add.43), channel_id=1, source_target_pairs={{0,8},{4,12},{8,0},{12,4},{16,24},{20,28},{24,16},{28,20},{1,9},{5... | collective-permute-start | bytes 196616 | tf_op jit(solution)/shard_map/ppermute | solution.py:45
  284.2 11.0 %collective-permute-start.43 = (bf16[1,128,512]{2,1,0:T(8,128)(2,1)S(1)}, bf16[1,128,512]{2,1,0:T(8,128)(2,1)S(1)}, u32[]{:S(2)}, u32[]{:S(2)}) collective-permute-start(bf16[1,128,512]{2,1,0:T(8,128)(2,1)S(1)} %get-tuple-element.349), channel_id=1, source_target_pairs={{0,8},{4,12},{8,0},{12,4},{16,24},{20,28},{24,16},{28,20},{1,9},{5... | collective-permute-start | bytes 393224 | tf_op jit(solution)/shard_map/ppermute | solution.py:45
  294.0 7.5 %collective-permute-start.42 = (f32[16,1024]{1,0:T(8,128)S(1)}, f32[16,1024]{1,0:T(8,128)S(1)}, u32[]{:S(2)}, u32[]{:S(2)}) collective-permute-start(f32[16,1024]{1,0:T(8,128)S(1)} %add.44), channel_id=1, source_target_pairs={{0,2},{1,3},{2,0},{3,1},{4,6},{5,7},{6,4},{7,5},{8,10},{9,11},{10,... | collective-permute-start | bytes 196616 | tf_op jit(solution)/shard_map/ppermute | solution.py:45
  (42 other events, 167.1 us)

commit v16 on v15

--- a/solution.py
+++ b/solution.py
@@ -1192,11 +1192,10 @@
     late_near = [swap(x, "tensor", 1) for x in late_far]
     far = zip(zip(early_far, late_far), zip(early_near, late_near))
     grad = Tokens([(out_grad,), (near,), *[x for pair in far for x in pair]], order)
+    grad_context = project_grad(ids, grad, dense_pack, width)
+    fc_pack.double()
     while len(out_pack.bits) > 1:
         out_pack.double()
-    (grad_context,) = tie_packs(out_pack, beside=[project_grad(ids, grad, dense_pack, width)])
-    fc_pack.double()
-    out_pack.double()
     done = attention(info, tables, queries, keys, values, grad_context)
     context, dq, dk, dv = tie_packs(fc_pack, out_pack, beside=done)
     dp_orders = [halving_order(near_bits), halving_order(next_bits)]
@@ -1205,6 +1204,7 @@
         *project_context(ids, context, dense_pack, groups, model), "tensor", tensor_bits
     )
     attn_parts.begin()
+    out_pack.double()
     done = attention_weights(
         ids, info, tables, context, dq, dk, dv, sent, grad, gain_attn, shift_attn, qkv_orders
     )
@@ -1212,7 +1212,9 @@
     grads, qkv_bias_sums, *stacks = done
     attn_parts.middle()
     qkv_sums = [Halving(*stacks[:2], "dp", qkv_bits[0]), Halving(*stacks[2:], "dp", qkv_bits[1])]
-    sent.arrays[0], attn_parts.send = tie(sent.arrays[0], attn_parts.send)
+    sent.arrays[0], attn_parts.send = tie_packs(
+        out_pack, beside=[sent.arrays[0], attn_parts.send]
+    )
     attn_parts.swap()
     for parts in qkv_sums:
         parts.swap()

time: 306 us -> 310 us (1.013)
  waiting for transfers between devices: 66.4 us -> 71.5 us
    ppermute x46, waiting for transfers between devices: 66.4 us -> 71.5 us  [swap(): return lax.ppermute(block, axis, [(i, i ^ bit) for i in range(size)])]
where the time goes in v16:
time: 310 us; the launch traced here: 309 us
  Pallas kernels  157 us (51%)
  waiting for transfers between devices  71.5 us (23%)
  starting transfers between devices  50.8 us (16%)
  local copies, waits for them, and re-layouts  19.2 us (6%)
  other arithmetic  8.71 us (3%)
    pallas_call x19, Pallas kernels, call(): pl.pallas_call(kernel, grid_spec=pltpu.PrefetchScalarGridSpec(num_scalar_...  155 us
    ppermute x46, waiting for transfers between devices, swap(): return lax.ppermute(block, axis, [(i, i ^ bit) for i in range(size)])  71.5 us
    ppermute x46, starting transfers between devices, swap(): return lax.ppermute(block, axis, [(i, i ^ bit) for i in range(size)])  50.8 us
    unnamed x123, local copies, waits for them, and re-layouts  14.2 us
  transfers between devices with their start and end apart: 46, of which 22 were waited for; matrix products, arithmetic and copies ran while one was open for 4% of the time, Pallas kernels for 50%

profile of v16, /device:TPU:0, one launch (start us, length us, event | category | flops | bytes accessed | tf_op | source)
XLA Modules:
  0.0 309.1 jit_solution(3818221512740340460)
XLA Ops:
  1.2 4.2 %normalize.1 = (bf16[640,1024]{1,0:T(8,128)(2,1)}, f32[640,1]{1,0:T(8,128)}, f32[640,1]{1,0:T(8,128)}) custom-call(f32[640,1024]{1,0:T(8,128)} %stream_ref.3), custom_call_target="tpu_custom_call" | custom-call | flops 5242880 | bytes 3937280 | tf_op jit(solution)/shard_map/normalize/pallas_call | solution.py:241
  5.4 2.5 collective-permute-start.4
  8.1 2.5 prepare_weights.1
  10.6 1.5 collective-permute-start.2
  12.1 2.6 collective-permute-start.1
  16.5 2.1 tree_table.1.info
  18.6 5.7 %collective-permute-done.1.refs_5_ = bf16[128,768]{1,0:T(8,128)(2,1)S(1)} collective-permute-done((bf16[128,768]{1,0:T(8,128)(2,1)}, bf16[128,768]{1,0:T(8,128)(2,1)S(1)}, u32[]{:S(2)}, u32[]{:S(2)}) %collective-permute-start.1) | collective-permute-done | bytes 196640 | tf_op jit(solution)/shard_map/ppermute | solution.py:45
  24.4 4.1 %collective-permute-start.5 = (bf16[256,768]{1,0:T(8,128)(2,1)S(1)}, bf16[256,768]{1,0:T(8,128)(2,1)S(1)}, u32[]{:S(2)}, u32[]{:S(2)}) collective-permute-start(bf16[256,768]{1,0:T(8,128)(2,1)S(1)} %pad_maximum_fusion.5), channel_id=1, source_target_pairs={{0,8},{4,12},{8,0},{12,4},{16,24},{20,28},{24,16},{28,20},{1,9},{5... | collective-permute-start | bytes 1179656 | tf_op jit(solution)/shard_map/ppermute | solution.py:45
  28.5 3.8 %fusion = (f32[1280,128]{1,0:T(8,128)}, f32[1280,128]{1,0:T(8,128)}) fusion(s32[128]{0:T(128)S(1)} %get-tuple-element.362, s32[128]{0:T(128)S(1)} %get-tuple-element.363, pred[128]{0:T(512)(128)(4,1)S(1)} %compare_and_fusion, f32[1280]{0:T(1024)S(1)} %convert_add_fusion), kind=kLoop, calls=%fused_computation.9 | loop fusion | flops 3112960 | bytes 1316992 | tf_op jit(solution)/shard_map/jit(_where)/select_n | solution.py:1082
  33.6 4.1 %collective-permute-done.4.refs_2_ = bf16[640,1024]{1,0:T(8,128)(2,1)} collective-permute-done((bf16[640,1024]{1,0:T(8,128)(2,1)}, bf16[640,1024]{1,0:T(8,128)(2,1)}, u32[]{:S(2)}, u32[]{:S(2)}) %collective-permute-start.4) | collective-permute-done | bytes 1310752 | tf_op jit(solution)/shard_map/ppermute | solution.py:45
  37.7 1.2 collective-permute-done.5.refs_6_
  39.7 1.5 collective-permute-start.8
  41.2 2.6 collective-permute-start.11
  43.8 1.6 collective-permute-start.10
  45.4 10.5 %collective-permute-done.11.refs_11_.refs_9_ = bf16[128,1024]{1,0:T(8,128)(2,1)S(1)} collective-permute-done((bf16[128,1024]{1,0:T(8,128)(2,1)S(1)}, bf16[128,1024]{1,0:T(8,128)(2,1)S(1)}, u32[]{:S(2)}, u32[]{:S(2)}) %collective-permute-start.11) | collective-permute-done | bytes 262176 | tf_op jit(solution)/shard_map/ppermute | solution.py:45
  56.2 2.8 collective-permute-done.9.refs_7_
  60.6 1.6 collective-permute-start.14
  62.2 1.5 collective-permute-start.13
  64.3 2.6 collective-permute-start.15
  66.8 11.1 %project_qkv.1 = (bf16[2560,256]{1,0:T(8,128)(2,1)}, bf16[2560,256]{1,0:T(8,128)(2,1)}, bf16[2560,256]{1,0:T(8,128)(2,1)}) custom-call(s32[6]{0:T(128)} %stack.11.ids, s32[1,20,5]{2,1,0:T(8,128)} %tree_table.1.info, bf16[640,1024]{1,0:T(8,128)(2,1)} %copy-done.37, bf16[640,1024]{1,0:T(8,128)(2,1)} %collective-permute-done.3.refs_1_, ...), custom_call_target="tpu_custom_call" | custom-call | flops 4026531840 | bytes 12079104 | tf_op jit(solution)/shard_map/project_qkv/pallas_call | solution.py:241
  78.0 1.8 collective-permute-done.15.refs_15_
  79.8 1.0 collective-permute-done.14.refs_12_.refs_10_
  80.8 1.0 pad_maximum_fusion.4
  81.8 2.7 collective-permute-start.18
  84.6 1.2 pad_maximum_fusion
  86.5 5.3 %project_grad.1.do_ref = bf16[2560,256]{1,0:T(8,128)(2,1)S(1)} custom-call(s32[6]{0:T(128)S(1)} %copy-done.32, bf16[384,1024]{1,0:T(8,128)(2,1)} %collective-permute-done.12.refs_0_.refs_4_, bf16[256,1024]{1,0:T(8,128)(2,1)S(1)} %collective-permute-done.16.refs_1_.refs_5_, bf16[640,1024]{1,0:T(8,128)(2,1)} %collective-permute-done.refs_2_.refs_6_, ...), custom_call_target="tpu_custom_call" | custom-call | flops 1342177280 | bytes 7077888 | tf_op jit(solution)/shard_map/project_grad/pallas_call | solution.py:241
  91.9 49.9 %attention.1 = (bf16[2560,256]{1,0:T(8,128)(2,1)S(1)}, bf16[2560,256]{1,0:T(8,128)(2,1)S(1)}, bf16[2560,256]{1,0:T(8,128)(2,1)S(1)}, bf16[2560,256]{1,0:T(8,128)(2,1)S(1)}) custom-call(s32[1,20,5]{2,1,0:T(8,128)S(1)} %copy-done.31, bf16[2560,256]{1,0:T(8,128)(2,1)S(1)} %copy-done.53, bf16[2560,256]{1,0:T(8,128)(2,1)S(1)} %project_grad.1.do_ref, ...), custom_call_target="tpu_custom_call" | custom-call | flops 31406948352 | bytes 11796480 | tf_op jit(solution)/shard_map/attention/pallas_call | solution.py:241
  141.8 1.0 copy-done.40
  142.8 4.1 %project_context.1 = (bf16[1,640,1024]{2,1,0:T(8,128)(2,1)S(1)}, bf16[1,640,1024]{2,1,0:T(8,128)(2,1)S(1)}, bf16[2,640,1024]{2,1,0:T(8,128)(2,1)S(1)}) custom-call(s32[6]{0:T(128)S(1)} %copy-done.32, bf16[2560,256]{1,0:T(8,128)(2,1)S(1)} %get-tuple-element.251.ctx_ref.ctx, bf16[128,256]{1,0:T(8,128)(2,1)S(1)} %copy-done.19, bf16[128,256]{1,0:T(8,128)(2,1)S(1)} %copy-done.21, ...), custom_call_target="tpu_custom_call" | custom-call | flops 1342177280 | bytes 7077888 | tf_op jit(solution)/shard_map/project_context/pallas_call | solution.py:241
  147.5 1.0 pad_maximum_fusion.1
  148.5 1.5 collective-permute-start.21
  150.0 12.4 %attention_weights.1 = (bf16[2560,768]{1,0:T(8,128)(2,1)S(1)}, f32[8,768]{1,0:T(8,128)S(1)}, bf16[4,128,512]{2,1,0:T(8,128)(2,1)}, bf16[4,128,512]{2,1,0:T(8,128...) custom-call(s32[6]{0:T(128)S(1)} %copy-done.32, s32[1,20,5]{2,1,0:T(8,128)S(1)} %copy-done.31, ...), custom_call_target="tpu_custom_call" | custom-call | flops 5368709120 | bytes 23101440 | tf_op jit(solution)/shard_map/attention_weights/pallas_call | solution.py:241
  162.5 2.0 copy-done.51
  165.6 8.9 %collective-permute-done.21.refs_17_ = bf16[512,1024]{1,0:T(8,128)(2,1)S(1)} collective-permute-done((bf16[512,1024]{1,0:T(8,128)(2,1)S(1)}, bf16[512,1024]{1,0:T(8,128)(2,1)S(1)}, u32[]{:S(2)}, u32[]{:S(2)}) %collective-permute-start.21) | collective-permute-done | bytes 1048608 | tf_op jit(solution)/shard_map/ppermute | solution.py:45
  174.6 1.0 copy-done.43
  175.5 1.4 collective-permute-start.22
  177.0 1.2 copy-done.44
  178.2 38.9 %mlp.1 = (bf16[1,640,1024]{2,1,0:T(8,128)(2,1)S(1)}, bf16[1,640,1024]{2,1,0:T(8,128)(2,1)}, bf16[2,640,1024]{2,1,0:T(8,128)(2,1)}, bf16[2560,1024]{1,0:T(8,128)(...) custom-call(s32[6]{0:T(128)S(1)} %copy-done.32, ...), custom_call_target="tpu_custom_call" | custom-call | flops 26843545600 | bytes 29417472 | tf_op jit(solution)/shard_map/mlp/pallas_call | solution.py:241
  217.7 3.6 %collective-permute-done.25.refs_1_ = bf16[1,640,1024]{2,1,0:T(8,128)(2,1)S(1)} collective-permute-done((bf16[1,640,1024]{2,1,0:T(8,128)(2,1)S(1)}, bf16[1,640,1024]{2,1,0:T(8,128)(2,1)S(1)}, u32[]{:S(2)}, u32[]{:S(2)}) %collective-permute-start.25) | collective-permute-done | bytes 1310752 | tf_op jit(solution)/shard_map/ppermute | solution.py:45
  221.3 1.7 copy-done.3
  224.1 1.5 collective-permute-start.30
  226.5 1.8 collective-permute-start.28
  228.9 2.1 copy-done.52
  231.0 2.5 copy-done.56
  233.5 16.0 %norm_backward.1 = (bf16[1,640,1024]{2,1,0:T(8,128)(2,1)S(1)}, bf16[1,640,1024]{2,1,0:T(8,128)(2,1)S(1)}, bf16[2,640,1024]{2,1,0:T(8,128)(2,1)S(1)}, f32[8,1024]{1,0:T(8,128)S(1)}) custom-call(s32[6]{0:T(128)S(1)} %copy-done.32, bf16[2560,768]{1,0:T(8,128)(2,1)S(1)} %copy-done.52, bf16[2560,1024]{1,0:T(8,128)(2,1)S(1)} %copy-done.56, ...), custom_call_target="tpu_custom_call" | custom-call | flops 9395240960 | bytes 23371776 | tf_op jit(solution)/shard_map/norm_backward/pallas_call | solution.py:241
  249.5 4.5 %collective-permute-done.28.refs_2_ = bf16[2,128,512]{2,1,0:T(8,128)(2,1)S(1)} collective-permute-done((bf16[2,128,512]{2,1,0:T(8,128)(2,1)}, bf16[2,128,512]{2,1,0:T(8,128)(2,1)S(1)}, u32[]{:S(2)}, u32[]{:S(2)}) %collective-permute-start.28) | collective-permute-done | bytes 262176 | tf_op jit(solution)/shard_map/ppermute | solution.py:45
  254.9 1.2 collective-permute-done.31.refs_9_.refs_4_.refs_5_
  256.6 2.5 collective-permute-done.32.refs_1_
  259.5 1.6 collective-permute-start.41
  261.4 1.7 collective-permute-start.36
  263.9 1.3 copy-done.6
  265.2 3.7 %finish_output.1 = (f32[640,1024]{1,0:T(8,128)}, f32[16,1024]{1,0:T(8,128)S(1)}) custom-call(s32[6]{0:T(128)S(1)} %copy-done.32, f32[640,1024]{1,0:T(8,128)S(1)} %copy-done, bf16[640,1024]{1,0:T(8,128)(2,1)S(1)} %copy-done.2, bf16[2,640,1024]{2,1,0:T(8,128)(2,1)S(1)} %get-tuple-element.264.refs_0_, ...), custom_call_target="tpu_custom_call" | custom-call | flops 10485760 | bytes 17203200 | tf_op jit(solution)/shard_map/finish_output/pallas_call | solution.py:241
  268.9 1.3 collective-permute-done.34
  270.1 2.7 collective-permute-start.35
  272.8 4.9 %collective-permute-done.38.refs_7_ = bf16[1,128,512]{2,1,0:T(8,128)(2,1)S(1)} collective-permute-done((bf16[1,128,512]{2,1,0:T(8,128)(2,1)S(1)}, bf16[1,128,512]{2,1,0:T(8,128)(2,1)S(1)}, u32[]{:S(2)}, u32[]{:S(2)}) %collective-permute-start.38) | collective-permute-done | bytes 131104 | tf_op jit(solution)/shard_map/ppermute | solution.py:45
  277.7 1.6 collective-permute-done.36.refs_2_
  279.6 2.6 collective-permute-start.44
  282.6 1.6 collective-permute-start.39
  284.2 2.7 collective-permute-done.39
  286.8 1.3 collective-permute-start.40
  288.9 6.4 %collective-permute-done.40 = f32[16,1024]{1,0:T(8,128)S(1)} collective-permute-done((f32[16,1024]{1,0:T(8,128)S(1)}, f32[16,1024]{1,0:T(8,128)S(1)}, u32[]{:S(2)}, u32[]{:S(2)}) %collective-permute-start.40) | collective-permute-done | bytes 65568 | tf_op jit(solution)/shard_map/ppermute | solution.py:45
  295.4 2.8 finish_grad.1
  299.8 4.8 %collective-permute-done.45.refs_7_ = bf16[1,128,1024]{2,1,0:T(8,128)(2,1)S(1)} collective-permute-done((bf16[1,128,1024]{2,1,0:T(8,128)(2,1)S(1)}, bf16[1,128,1024]{2,1,0:T(8,128)(2,1)S(1)}, u32[]{:S(2)}, u32[]{:S(2)}) %collective-permute-start.45) | collective-permute-done | bytes 262176 | tf_op jit(solution)/shard_map/ppermute | solution.py:45
  304.6 1.2 finish_mlp_weights.1
  (200 shorter events, 21.8 us)
Async XLA Ops:
  0.6 23.6 %collective-permute-start = (bf16[640,1024]{1,0:T(8,128)(2,1)}, bf16[640,1024]{1,0:T(8,128)(2,1)}, u32[]{:S(2)}, u32[]{:S(2)}) collective-permute-start(bf16[640,1024]{1,0:T(8,128)(2,1)} %grad_ref.3), channel_id=1, source_target_pairs={{0,1},{1,0},{2,3},{3,2},{4,5},{5,4},{6,7},{7,6},{8,9},{9,8},{10,11... | collective-permute-start | bytes 3932168 | tf_op jit(solution)/shard_map/ppermute | solution.py:45
  5.4 9.3 %copy-start.1 = (bf16[640,1024]{1,0:T(8,128)(2,1)S(1)}, bf16[640,1024]{1,0:T(8,128)(2,1)}, u32[]{:S(2)}) copy-start(bf16[640,1024]{1,0:T(8,128)(2,1)} %grad_ref.3) | copy-start | bytes 3932164
  5.4 32.3 %collective-permute-start.4 = (bf16[640,1024]{1,0:T(8,128)(2,1)}, bf16[640,1024]{1,0:T(8,128)(2,1)}, u32[]{:S(2)}, u32[]{:S(2)}) collective-permute-start(bf16[640,1024]{1,0:T(8,128)(2,1)} %get-tuple-element.216.refs_3_), channel_id=1, source_target_pairs={{0,2},{1,3},{2,0},{3,1},{4,6},{5,7},{6,4},{7,5},{8,10},{9,11},{10,... | collective-permute-start | bytes 3932168 | tf_op jit(solution)/shard_map/ppermute | solution.py:45
  7.9 29.7 %collective-permute-start.3 = (bf16[640,1024]{1,0:T(8,128)(2,1)}, bf16[640,1024]{1,0:T(8,128)(2,1)}, u32[]{:S(2)}, u32[]{:S(2)}) collective-permute-start(bf16[640,1024]{1,0:T(8,128)(2,1)} %get-tuple-element.216.refs_3_), channel_id=1, source_target_pairs={{0,1},{1,0},{2,3},{3,2},{4,5},{5,4},{6,7},{7,6},{8,9},{9,8},{10,11... | collective-permute-start | bytes 3932168 | tf_op jit(solution)/shard_map/ppermute | solution.py:45
  10.6 8.0 %collective-permute-start.2 = (bf16[128,256]{1,0:T(8,128)(2,1)}, bf16[128,256]{1,0:T(8,128)(2,1)S(1)}, u32[]{:S(2)}, u32[]{:S(2)}) collective-permute-start(bf16[128,256]{1,0:T(8,128)(2,1)} %get-tuple-element.236.refs_6_.refs_0_), channel_id=1, source_target_pairs={{0,4},{4,0},{8,12},{12,8},{16,20},{20,16},{24,28},{28,24},{1,5},{5... | collective-permute-start | bytes 196616 | tf_op jit(solution)/shard_map/ppermute | solution.py:45
  12.1 12.2 %copy-start.18 = (bf16[128,256]{1,0:T(8,128)(2,1)S(1)}, bf16[128,256]{1,0:T(8,128)(2,1)}, u32[]{:S(2)}) copy-start(bf16[128,256]{1,0:T(8,128)(2,1)} %get-tuple-element.236.refs_6_.refs_0_) | copy-start | bytes 196612
  12.1 12.3 %copy-start.12 = (bf16[128,768]{1,0:T(8,128)(2,1)S(1)}, bf16[128,768]{1,0:T(8,128)(2,1)}, u32[]{:S(2)}) copy-start(bf16[128,768]{1,0:T(8,128)(2,1)} %get-tuple-element.217.refs_4_) | copy-start | bytes 589828
  12.1 12.2 %collective-permute-start.1 = (bf16[128,768]{1,0:T(8,128)(2,1)}, bf16[128,768]{1,0:T(8,128)(2,1)S(1)}, u32[]{:S(2)}, u32[]{:S(2)}) collective-permute-start(bf16[128,768]{1,0:T(8,128)(2,1)} %get-tuple-element.217.refs_4_), channel_id=1, source_target_pairs={{0,16},{4,20},{8,24},{12,28},{16,0},{20,4},{24,8},{28,12},{1,17},{... | collective-permute-start | bytes 589832 | tf_op jit(solution)/shard_map/ppermute | solution.py:45
  16.5 15.9 %copy-start.59 = (f32[3072]{0:T(1024)S(1)}, f32[3072]{0:T(1024)}, u32[]{:S(2)}) copy-start(f32[3072]{0:T(1024)} %param.24) | copy-start | bytes 36868
  16.5 16.5 %copy-start.58 = (f32[4096]{0:T(1024)S(1)}, f32[4096]{0:T(1024)}, u32[]{:S(2)}) copy-start(f32[4096]{0:T(1024)} %param.28) | copy-start | bytes 49156
  18.6 25.2 %copy-start.20 = (bf16[128,256]{1,0:T(8,128)(2,1)}, bf16[128,256]{1,0:T(8,128)(2,1)S(1)}, u32[]{:S(2)}) copy-start(bf16[128,256]{1,0:T(8,128)(2,1)S(1)} %collective-permute-done.2.refs_7_.refs_1_) | copy-start | bytes 196612
  24.3 14.7 %copy-start.14 = (bf16[128,768]{1,0:T(8,128)(2,1)}, bf16[128,768]{1,0:T(8,128)(2,1)S(1)}, u32[]{:S(2)}) copy-start(bf16[128,768]{1,0:T(8,128)(2,1)S(1)} %collective-permute-done.1.refs_5_) | copy-start | bytes 589828
  24.3 13.3 %collective-permute-start.6 = (bf16[256,256]{1,0:T(8,128)(2,1)S(1)}, bf16[256,256]{1,0:T(8,128)(2,1)S(1)}, u32[]{:S(2)}, u32[]{:S(2)}) collective-permute-start(bf16[256,256]{1,0:T(8,128)(2,1)S(1)} %pad_maximum_fusion.7), channel_id=1, source_target_pairs={{0,16},{4,20},{8,24},{12,28},{16,0},{20,4},{24,8},{28,12},{1,17},{... | collective-permute-start | bytes 393224 | tf_op jit(solution)/shard_map/ppermute | solution.py:45
  24.4 14.5 %collective-permute-start.5 = (bf16[256,768]{1,0:T(8,128)(2,1)S(1)}, bf16[256,768]{1,0:T(8,128)(2,1)S(1)}, u32[]{:S(2)}, u32[]{:S(2)}) collective-permute-start(bf16[256,768]{1,0:T(8,128)(2,1)S(1)} %pad_maximum_fusion.5), channel_id=1, source_target_pairs={{0,8},{4,12},{8,0},{12,4},{16,24},{20,28},{24,16},{28,20},{1,9},{5... | collective-permute-start | bytes 1179656 | tf_op jit(solution)/shard_map/ppermute | solution.py:45
  28.5 12.7 %copy-start.7 = (bf16[128,1024]{1,0:T(8,128)(2,1)S(1)}, bf16[128,1024]{1,0:T(8,128)(2,1)}, u32[]{:S(2)}) copy-start(bf16[128,1024]{1,0:T(8,128)(2,1)} %get-tuple-element.270.refs_10_.refs_8_) | copy-start | bytes 786436
  37.7 22.9 %copy-start.22 = (bf16[256,256]{1,0:T(8,128)(2,1)}, bf16[256,256]{1,0:T(8,128)(2,1)S(1)}, u32[]{:S(2)}) copy-start(bf16[256,256]{1,0:T(8,128)(2,1)S(1)} %collective-permute-done.6.refs_8_.refs_2_) | copy-start | bytes 393220
  38.9 21.7 %copy-start.24 = (bf16[256,768]{1,0:T(8,128)(2,1)}, bf16[256,768]{1,0:T(8,128)(2,1)S(1)}, u32[]{:S(2)}) copy-start(bf16[256,768]{1,0:T(8,128)(2,1)S(1)} %collective-permute-done.5.refs_6_) | copy-start | bytes 1179652
  38.9 25.3 %copy-start.8 = (bf16[128,1024]{1,0:T(8,128)(2,1)S(1)}, bf16[128,1024]{1,0:T(8,128)(2,1)}, u32[]{:S(2)}) copy-start(bf16[128,1024]{1,0:T(8,128)(2,1)} %get-tuple-element.274.refs_14_) | copy-start | bytes 786436
  38.9 20.7 %collective-permute-start.7 = (bf16[640,1024]{1,0:T(8,128)(2,1)}, bf16[640,1024]{1,0:T(8,128)(2,1)S(1)}, u32[]{:S(2)}, u32[]{:S(2)}) collective-permute-start(bf16[640,1024]{1,0:T(8,128)(2,1)} %collective-permute-done.4.refs_2_), channel_id=1, source_target_pairs={{0,1},{1,0},{2,3},{3,2},{4,5},{5,4},{6,7},{7,6},{8,9},{9,8},{10,11... | collective-permute-start | bytes 3932168 | tf_op jit(solution)/shard_map/ppermute | solution.py:45
  39.0 20.0 %collective-permute-start.9 = (bf16[512,768]{1,0:T(8,128)(2,1)S(1)}, bf16[512,768]{1,0:T(8,128)(2,1)S(1)}, u32[]{:S(2)}, u32[]{:S(2)}) collective-permute-start(bf16[512,768]{1,0:T(8,128)(2,1)S(1)} %pad_maximum_fusion.2), channel_id=1, source_target_pairs={{0,4},{4,0},{8,12},{12,8},{16,20},{20,16},{24,28},{28,24},{1,5},{5... | collective-permute-start | bytes 2359304 | tf_op jit(solution)/shard_map/ppermute | solution.py:45
  39.7 20.0 %collective-permute-start.8 = (bf16[384,1024]{1,0:T(8,128)(2,1)}, bf16[384,1024]{1,0:T(8,128)(2,1)}, u32[]{:S(2)}, u32[]{:S(2)}) collective-permute-start(bf16[384,1024]{1,0:T(8,128)(2,1)} %slice.30), channel_id=1, source_target_pairs={{0,2},{1,3},{2,0},{3,1},{4,6},{5,7},{6,4},{7,5},{8,10},{9,11},{10,... | collective-permute-start | bytes 2359304 | tf_op jit(solution)/shard_map/ppermute | solution.py:45
  41.2 14.8 %collective-permute-start.11 = (bf16[128,1024]{1,0:T(8,128)(2,1)S(1)}, bf16[128,1024]{1,0:T(8,128)(2,1)S(1)}, u32[]{:S(2)}, u32[]{:S(2)}) collective-permute-start(bf16[128,1024]{1,0:T(8,128)(2,1)S(1)} %copy-done.7), channel_id=1, source_target_pairs={{0,16},{4,20},{8,24},{12,28},{16,0},{20,4},{24,8},{28,12},{1,17},{... | collective-permute-start | bytes 786440 | tf_op jit(solution)/shard_map/ppermute | solution.py:45
  43.8 12.4 %collective-permute-start.10 = (bf16[512,256]{1,0:T(8,128)(2,1)S(1)}, bf16[512,256]{1,0:T(8,128)(2,1)S(1)}, u32[]{:S(2)}, u32[]{:S(2)}) collective-permute-start(bf16[512,256]{1,0:T(8,128)(2,1)S(1)} %pad_maximum_fusion.6), channel_id=1, source_target_pairs={{0,8},{4,12},{8,0},{12,4},{16,24},{20,28},{24,16},{28,20},{1,9},{5... | collective-permute-start | bytes 786440 | tf_op jit(solution)/shard_map/ppermute | solution.py:45
  59.7 21.1 %collective-permute-start.12 = (bf16[384,1024]{1,0:T(8,128)(2,1)}, bf16[384,1024]{1,0:T(8,128)(2,1)}, u32[]{:S(2)}, u32[]{:S(2)}) collective-permute-start(bf16[384,1024]{1,0:T(8,128)(2,1)} %collective-permute-done.8.refs_3_.refs_7_), channel_id=1, source_target_pairs={{0,1},{1,0},{2,3},{3,2},{4,5},{5,4},{6,7},{7,6},{8,9},{9,8},{10,11... | collective-permute-start | bytes 2359304 | tf_op jit(solution)/shard_map/ppermute | solution.py:45
  60.6 20.2 %collective-permute-start.14 = (bf16[256,1024]{1,0:T(8,128)(2,1)}, bf16[256,1024]{1,0:T(8,128)(2,1)}, u32[]{:S(2)}, u32[]{:S(2)}) collective-permute-start(bf16[256,1024]{1,0:T(8,128)(2,1)} %pad_maximum_fusion.3), channel_id=1, source_target_pairs={{0,8},{4,12},{8,0},{12,4},{16,24},{20,28},{24,16},{28,20},{1,9},{5... | collective-permute-start | bytes 1572872 | tf_op jit(solution)/shard_map/ppermute | solution.py:45
  62.2 18.6 %collective-permute-start.13 = (bf16[256,1024]{1,0:T(8,128)(2,1)}, bf16[256,1024]{1,0:T(8,128)(2,1)}, u32[]{:S(2)}, u32[]{:S(2)}) collective-permute-start(bf16[256,1024]{1,0:T(8,128)(2,1)} %slice.31), channel_id=1, source_target_pairs={{0,2},{1,3},{2,0},{3,1},{4,6},{5,7},{6,4},{7,5},{8,10},{9,11},{10,... | collective-permute-start | bytes 1572872 | tf_op jit(solution)/shard_map/ppermute | solution.py:45
  64.3 15.5 %collective-permute-start.15 = (bf16[128,1024]{1,0:T(8,128)(2,1)S(1)}, bf16[128,1024]{1,0:T(8,128)(2,1)}, u32[]{:S(2)}, u32[]{:S(2)}) collective-permute-start(bf16[128,1024]{1,0:T(8,128)(2,1)S(1)} %copy-done.8), channel_id=1, source_target_pairs={{0,16},{4,20},{8,24},{12,28},{16,0},{20,4},{24,8},{28,12},{1,17},{... | collective-permute-start | bytes 786440 | tf_op jit(solution)/shard_map/ppermute | solution.py:45
  80.8 5.6 %collective-permute-start.16 = (bf16[256,1024]{1,0:T(8,128)(2,1)}, bf16[256,1024]{1,0:T(8,128)(2,1)S(1)}, u32[]{:S(2)}, u32[]{:S(2)}) collective-permute-start(bf16[256,1024]{1,0:T(8,128)(2,1)} %collective-permute-done.13.refs_4_.refs_8_), channel_id=1, source_target_pairs={{0,1},{1,0},{2,3},{3,2},{4,5},{5,4},{6,7},{7,6},{8,9},{9,8},{10,11... | collective-permute-start | bytes 1572872 | tf_op jit(solution)/shard_map/ppermute | solution.py:45
  81.8 59.9 %collective-permute-start.18 = (bf16[256,1024]{1,0:T(8,128)(2,1)S(1)}, bf16[256,1024]{1,0:T(8,128)(2,1)S(1)}, u32[]{:S(2)}, u32[]{:S(2)}) collective-permute-start(bf16[256,1024]{1,0:T(8,128)(2,1)S(1)} %pad_maximum_fusion.4), channel_id=1, source_target_pairs={{0,8},{4,12},{8,0},{12,4},{16,24},{20,28},{24,16},{28,20},{1,9},{5... | collective-permute-start | bytes 1572872 | tf_op jit(solution)/shard_map/ppermute | solution.py:45
  85.8 56.0 %collective-permute-start.17 = (bf16[512,1024]{1,0:T(8,128)(2,1)S(1)}, bf16[512,1024]{1,0:T(8,128)(2,1)S(1)}, u32[]{:S(2)}, u32[]{:S(2)}) collective-permute-start(bf16[512,1024]{1,0:T(8,128)(2,1)S(1)} %pad_maximum_fusion), channel_id=1, source_target_pairs={{0,4},{4,0},{8,12},{12,8},{16,20},{20,16},{24,28},{28,24},{1,5},{5... | collective-permute-start | bytes 3145736 | tf_op jit(solution)/shard_map/ppermute | solution.py:45
  146.9 17.6 %collective-permute-start.19 = (bf16[1,640,1024]{2,1,0:T(8,128)(2,1)S(1)}, bf16[1,640,1024]{2,1,0:T(8,128)(2,1)S(1)}, u32[]{:S(2)}, u32[]{:S(2)}) collective-permute-start(bf16[1,640,1024]{2,1,0:T(8,128)(2,1)S(1)} %get-tuple-element.261), channel_id=1, source_target_pairs={{0,1},{1,0},{2,3},{3,2},{4,5},{5,4},{6,7},{7,6},{8,9},{9,8},{10,11... | collective-permute-start | bytes 3932168 | tf_op jit(solution)/shard_map/ppermute | solution.py:45
  147.0 17.5 %collective-permute-start.20 = (bf16[1,640,1024]{2,1,0:T(8,128)(2,1)S(1)}, bf16[1,640,1024]{2,1,0:T(8,128)(2,1)S(1)}, u32[]{:S(2)}, u32[]{:S(2)}) collective-permute-start(bf16[1,640,1024]{2,1,0:T(8,128)(2,1)S(1)} %get-tuple-element.262), channel_id=1, source_target_pairs={{0,1},{1,0},{2,3},{3,2},{4,5},{5,4},{6,7},{7,6},{8,9},{9,8},{10,11... | collective-permute-start | bytes 3932168 | tf_op jit(solution)/shard_map/ppermute | solution.py:45
  148.5 26.1 %collective-permute-start.21 = (bf16[512,1024]{1,0:T(8,128)(2,1)S(1)}, bf16[512,1024]{1,0:T(8,128)(2,1)S(1)}, u32[]{:S(2)}, u32[]{:S(2)}) collective-permute-start(bf16[512,1024]{1,0:T(8,128)(2,1)S(1)} %pad_maximum_fusion.1), channel_id=1, source_target_pairs={{0,4},{4,0},{8,12},{12,8},{16,20},{20,16},{24,28},{28,24},{1,5},{5... | collective-permute-start | bytes 3145736 | tf_op jit(solution)/shard_map/ppermute | solution.py:45
  164.4 52.7 %collective-permute-start.23 = (bf16[4,128,512]{2,1,0:T(8,128)(2,1)}, bf16[4,128,512]{2,1,0:T(8,128)(2,1)S(1)}, u32[]{:S(2)}, u32[]{:S(2)}) collective-permute-start(bf16[4,128,512]{2,1,0:T(8,128)(2,1)} %get-tuple-element.289), channel_id=1, source_target_pairs={{0,4},{4,0},{8,12},{12,8},{16,20},{20,16},{24,28},{28,24},{1,5},{5... | collective-permute-start | bytes 1572872 | tf_op jit(solution)/shard_map/ppermute | solution.py:45
  165.0 52.1 %collective-permute-start.24 = (bf16[4,128,512]{2,1,0:T(8,128)(2,1)}, bf16[4,128,512]{2,1,0:T(8,128)(2,1)S(1)}, u32[]{:S(2)}, u32[]{:S(2)}) collective-permute-start(bf16[4,128,512]{2,1,0:T(8,128)(2,1)} %get-tuple-element.290), channel_id=1, source_target_pairs={{0,8},{4,12},{8,0},{12,4},{16,24},{20,28},{24,16},{28,20},{1,9},{5... | collective-permute-start | bytes 1572872 | tf_op jit(solution)/shard_map/ppermute | solution.py:45
  165.2 11.7 %copy-start.10 = (bf16[128,1024]{1,0:T(8,128)(2,1)S(1)}, bf16[128,1024]{1,0:T(8,128)(2,1)}, u32[]{:S(2)}) copy-start(bf16[128,1024]{1,0:T(8,128)(2,1)} %copy-done.9) | copy-start | bytes 786436
  165.2 11.7 %copy-start.30 = (f32[4,1024]{1,0:T(4,128)S(1)}, f32[4,1024]{1,0:T(4,128)}, u32[]{:S(2)}) copy-start(f32[4,1024]{1,0:T(4,128)} %reshape.43.refs_20_) | copy-start | bytes 49156
  165.2 11.7 %copy-start.41 = (bf16[512,1024]{1,0:T(8,128)(2,1)S(1)}, bf16[512,1024]{1,0:T(8,128)(2,1)}, u32[]{:S(2)}) copy-start(bf16[512,1024]{1,0:T(8,128)(2,1)} %copy-done.40) | copy-start | bytes 3145732
  165.2 11.7 %copy-start.48 = (f32[1024]{0:T(1024)S(1)}, f32[1024]{0:T(1024)}, u32[]{:S(2)}) copy-start(f32[1024]{0:T(1024)} %param.22) | copy-start | bytes 12292
  165.3 11.7 %copy-start.50 = (f32[1024]{0:T(1024)S(1)}, f32[1024]{0:T(1024)}, u32[]{:S(2)}) copy-start(f32[1024]{0:T(1024)} %param.21) | copy-start | bytes 12292
  175.5 41.6 %collective-permute-start.22 = (bf16[1,640,1024]{2,1,0:T(8,128)(2,1)S(1)}, bf16[1,640,1024]{2,1,0:T(8,128)(2,1)S(1)}, u32[]{:S(2)}, u32[]{:S(2)}) collective-permute-start(bf16[1,640,1024]{2,1,0:T(8,128)(2,1)S(1)} %add_terms.3), channel_id=1, source_target_pairs={{0,2},{1,3},{2,0},{3,1},{4,6},{5,7},{6,4},{7,5},{8,10},{9,11},{10,... | collective-permute-start | bytes 3932168 | tf_op jit(solution)/shard_map/ppermute | solution.py:45
  217.1 4.2 %collective-permute-start.25 = (bf16[1,640,1024]{2,1,0:T(8,128)(2,1)S(1)}, bf16[1,640,1024]{2,1,0:T(8,128)(2,1)S(1)}, u32[]{:S(2)}, u32[]{:S(2)}) collective-permute-start(bf16[1,640,1024]{2,1,0:T(8,128)(2,1)S(1)} %get-tuple-element.293), channel_id=1, source_target_pairs={{0,1},{1,0},{2,3},{3,2},{4,5},{5,4},{6,7},{7,6},{8,9},{9,8},{10,11... | collective-permute-start | bytes 3932168 | tf_op jit(solution)/shard_map/ppermute | solution.py:45
  217.2 11.1 %collective-permute-start.26 = (bf16[1,640,1024]{2,1,0:T(8,128)(2,1)}, bf16[1,640,1024]{2,1,0:T(8,128)(2,1)S(1)}, u32[]{:S(2)}, u32[]{:S(2)}) collective-permute-start(bf16[1,640,1024]{2,1,0:T(8,128)(2,1)} %get-tuple-element.295), channel_id=1, source_target_pairs={{0,1},{1,0},{2,3},{3,2},{4,5},{5,4},{6,7},{7,6},{8,9},{9,8},{10,11... | collective-permute-start | bytes 3932168 | tf_op jit(solution)/shard_map/ppermute | solution.py:45
  223.5 32.6 %collective-permute-start.27 = (bf16[1,640,1024]{2,1,0:T(8,128)(2,1)S(1)}, bf16[1,640,1024]{2,1,0:T(8,128)(2,1)S(1)}, u32[]{:S(2)}, u32[]{:S(2)}) collective-permute-start(bf16[1,640,1024]{2,1,0:T(8,128)(2,1)S(1)} %add_terms.4), channel_id=1, source_target_pairs={{0,2},{1,3},{2,0},{3,1},{4,6},{5,7},{6,4},{7,5},{8,10},{9,11},{10,... | collective-permute-start | bytes 3932168 | tf_op jit(solution)/shard_map/ppermute | solution.py:45
  224.1 30.8 %collective-permute-start.30 = (bf16[4,128,1024]{2,1,0:T(8,128)(2,1)}, bf16[4,128,1024]{2,1,0:T(8,128)(2,1)S(1)}, u32[]{:S(2)}, u32[]{:S(2)}) collective-permute-start(bf16[4,128,1024]{2,1,0:T(8,128)(2,1)} %get-tuple-element.308), channel_id=1, source_target_pairs={{0,4},{4,0},{8,12},{12,8},{16,20},{20,16},{24,28},{28,24},{1,5},{5... | collective-permute-start | bytes 3145736 | tf_op jit(solution)/shard_map/ppermute | solution.py:45
  225.6 30.5 %collective-permute-start.31 = (bf16[4,128,1024]{2,1,0:T(8,128)(2,1)}, bf16[4,128,1024]{2,1,0:T(8,128)(2,1)S(1)}, u32[]{:S(2)}, u32[]{:S(2)}) collective-permute-start(bf16[4,128,1024]{2,1,0:T(8,128)(2,1)} %get-tuple-element.309), channel_id=1, source_target_pairs={{0,8},{4,12},{8,0},{12,4},{16,24},{20,28},{24,16},{28,20},{1,9},{5... | collective-permute-start | bytes 3145736 | tf_op jit(solution)/shard_map/ppermute | solution.py:45
  226.5 27.4 %collective-permute-start.28 = (bf16[2,128,512]{2,1,0:T(8,128)(2,1)}, bf16[2,128,512]{2,1,0:T(8,128)(2,1)S(1)}, u32[]{:S(2)}, u32[]{:S(2)}) collective-permute-start(bf16[2,128,512]{2,1,0:T(8,128)(2,1)} %get-tuple-element.306), channel_id=1, source_target_pairs={{0,16},{4,20},{8,24},{12,28},{16,0},{20,4},{24,8},{28,12},{1,17},{... | collective-permute-start | bytes 786440 | tf_op jit(solution)/shard_map/ppermute | solution.py:45
  228.3 26.5 %collective-permute-start.29 = (bf16[2,128,512]{2,1,0:T(8,128)(2,1)}, bf16[2,128,512]{2,1,0:T(8,128)(2,1)S(1)}, u32[]{:S(2)}, u32[]{:S(2)}) collective-permute-start(bf16[2,128,512]{2,1,0:T(8,128)(2,1)} %get-tuple-element.307), channel_id=1, source_target_pairs={{0,4},{4,0},{8,12},{12,8},{16,20},{20,16},{24,28},{28,24},{1,5},{5... | collective-permute-start | bytes 786440 | tf_op jit(solution)/shard_map/ppermute | solution.py:45
  256.1 3.0 collective-permute-start.32
  256.1 7.8 %collective-permute-start.33 = (bf16[1,640,1024]{2,1,0:T(8,128)(2,1)S(1)}, bf16[1,640,1024]{2,1,0:T(8,128)(2,1)S(1)}, u32[]{:S(2)}, u32[]{:S(2)}) collective-permute-start(bf16[1,640,1024]{2,1,0:T(8,128)(2,1)S(1)} %get-tuple-element.313), channel_id=1, source_target_pairs={{0,1},{1,0},{2,3},{3,2},{4,5},{5,4},{6,7},{7,6},{8,9},{9,8},{10,11... | collective-permute-start | bytes 3932168 | tf_op jit(solution)/shard_map/ppermute | solution.py:45
  259.5 35.9 %collective-permute-start.41 = (bf16[1,640,1024]{2,1,0:T(8,128)(2,1)S(1)}, bf16[1,640,1024]{2,1,0:T(8,128)(2,1)S(1)}, u32[]{:S(2)}, u32[]{:S(2)}) collective-permute-start(bf16[1,640,1024]{2,1,0:T(8,128)(2,1)S(1)} %add_terms.5), channel_id=1, source_target_pairs={{0,2},{1,3},{2,0},{3,1},{4,6},{5,7},{6,4},{7,5},{8,10},{9,11},{10,... | collective-permute-start | bytes 3932168 | tf_op jit(solution)/shard_map/ppermute | solution.py:45
  261.4 18.0 %collective-permute-start.36 = (bf16[2,128,1024]{2,1,0:T(8,128)(2,1)S(1)}, bf16[2,128,1024]{2,1,0:T(8,128)(2,1)S(1)}, u32[]{:S(2)}, u32[]{:S(2)}) collective-permute-start(bf16[2,128,1024]{2,1,0:T(8,128)(2,1)S(1)} %get-tuple-element.330), channel_id=1, source_target_pairs={{0,8},{4,12},{8,0},{12,4},{16,24},{20,28},{24,16},{28,20},{1,9},{5... | collective-permute-start | bytes 1572872 | tf_op jit(solution)/shard_map/ppermute | solution.py:45
  263.0 16.3 %collective-permute-start.37 = (bf16[2,128,1024]{2,1,0:T(8,128)(2,1)S(1)}, bf16[2,128,1024]{2,1,0:T(8,128)(2,1)S(1)}, u32[]{:S(2)}, u32[]{:S(2)}) collective-permute-start(bf16[2,128,1024]{2,1,0:T(8,128)(2,1)S(1)} %get-tuple-element.331), channel_id=1, source_target_pairs={{0,4},{4,0},{8,12},{12,8},{16,20},{20,16},{24,28},{28,24},{1,5},{5... | collective-permute-start | bytes 1572872 | tf_op jit(solution)/shard_map/ppermute | solution.py:45
  263.5 14.2 %collective-permute-start.38 = (bf16[1,128,512]{2,1,0:T(8,128)(2,1)S(1)}, bf16[1,128,512]{2,1,0:T(8,128)(2,1)S(1)}, u32[]{:S(2)}, u32[]{:S(2)}) collective-permute-start(bf16[1,128,512]{2,1,0:T(8,128)(2,1)S(1)} %get-tuple-element.332), channel_id=1, source_target_pairs={{0,16},{4,20},{8,24},{12,28},{16,0},{20,4},{24,8},{28,12},{1,17},{... | collective-permute-start | bytes 393224 | tf_op jit(solution)/shard_map/ppermute | solution.py:45
  268.9 1.3 collective-permute-start.34
  270.1 9.2 %collective-permute-start.35 = (f32[16,1024]{1,0:T(8,128)S(1)}, f32[16,1024]{1,0:T(8,128)S(1)}, u32[]{:S(2)}, u32[]{:S(2)}) collective-permute-start(f32[16,1024]{1,0:T(8,128)S(1)} %add.41), channel_id=1, source_target_pairs={{0,16},{4,20},{8,24},{12,28},{16,0},{20,4},{24,8},{28,12},{1,17},{... | collective-permute-start | bytes 196616 | tf_op jit(solution)/shard_map/ppermute | solution.py:45
  279.3 16.0 %copy-start.26 = (f32[640,1]{1,0:T(8,128)S(1)}, f32[640,1]{1,0:T(8,128)}, u32[]{:S(2)}) copy-start(f32[640,1]{1,0:T(8,128)} %get-tuple-element.341.mean_ref) | copy-start | bytes 7684
  279.4 16.0 %copy-start.27 = (f32[640,1]{1,0:T(8,128)S(1)}, f32[640,1]{1,0:T(8,128)}, u32[]{:S(2)}) copy-start(f32[640,1]{1,0:T(8,128)} %get-tuple-element.342.std_ref) | copy-start | bytes 7684
  279.6 20.3 %collective-permute-start.44 = (bf16[1,128,1024]{2,1,0:T(8,128)(2,1)S(1)}, bf16[1,128,1024]{2,1,0:T(8,128)(2,1)S(1)}, u32[]{:S(2)}, u32[]{:S(2)}) collective-permute-start(bf16[1,128,1024]{2,1,0:T(8,128)(2,1)S(1)} %get-tuple-element.351), channel_id=1, source_target_pairs={{0,16},{4,20},{8,24},{12,28},{16,0},{20,4},{24,8},{28,12},{1,17},{... | collective-permute-start | bytes 786440 | tf_op jit(solution)/shard_map/ppermute | solution.py:45
  282.1 22.5 %collective-permute-start.45 = (bf16[1,128,1024]{2,1,0:T(8,128)(2,1)S(1)}, bf16[1,128,1024]{2,1,0:T(8,128)(2,1)S(1)}, u32[]{:S(2)}, u32[]{:S(2)}) collective-permute-start(bf16[1,128,1024]{2,1,0:T(8,128)(2,1)S(1)} %get-tuple-element.352), channel_id=1, source_target_pairs={{0,16},{4,20},{8,24},{12,28},{16,0},{20,4},{24,8},{28,12},{1,17},{... | collective-permute-start | bytes 786440 | tf_op jit(solution)/shard_map/ppermute | solution.py:45
  282.6 4.3 %collective-permute-start.39 = (f32[16,1024]{1,0:T(8,128)S(1)}, f32[16,1024]{1,0:T(8,128)S(1)}, u32[]{:S(2)}, u32[]{:S(2)}) collective-permute-start(f32[16,1024]{1,0:T(8,128)S(1)} %add.42), channel_id=1, source_target_pairs={{0,4},{4,0},{8,12},{12,8},{16,20},{20,16},{24,28},{28,24},{1,5},{5... | collective-permute-start | bytes 196616 | tf_op jit(solution)/shard_map/ppermute | solution.py:45
  286.8 8.5 %collective-permute-start.40 = (f32[16,1024]{1,0:T(8,128)S(1)}, f32[16,1024]{1,0:T(8,128)S(1)}, u32[]{:S(2)}, u32[]{:S(2)}) collective-permute-start(f32[16,1024]{1,0:T(8,128)S(1)} %add.43), channel_id=1, source_target_pairs={{0,8},{4,12},{8,0},{12,4},{16,24},{20,28},{24,16},{28,20},{1,9},{5... | collective-permute-start | bytes 196616 | tf_op jit(solution)/shard_map/ppermute | solution.py:45
  288.2 10.5 %collective-permute-start.43 = (bf16[1,128,512]{2,1,0:T(8,128)(2,1)S(1)}, bf16[1,128,512]{2,1,0:T(8,128)(2,1)S(1)}, u32[]{:S(2)}, u32[]{:S(2)}) collective-permute-start(bf16[1,128,512]{2,1,0:T(8,128)(2,1)S(1)} %get-tuple-element.347), channel_id=1, source_target_pairs={{0,8},{4,12},{8,0},{12,4},{16,24},{20,28},{24,16},{28,20},{1,9},{5... | collective-permute-start | bytes 393224 | tf_op jit(solution)/shard_map/ppermute | solution.py:45
  298.2 7.6 %collective-permute-start.42 = (f32[16,1024]{1,0:T(8,128)S(1)}, f32[16,1024]{1,0:T(8,128)S(1)}, u32[]{:S(2)}, u32[]{:S(2)}) collective-permute-start(f32[16,1024]{1,0:T(8,128)S(1)} %add.44), channel_id=1, source_target_pairs={{0,2},{1,3},{2,0},{3,1},{4,6},{5,7},{6,4},{7,5},{8,10},{9,11},{10,... | collective-permute-start | bytes 196616 | tf_op jit(solution)/shard_map/ppermute | solution.py:45
  (42 other events, 176.7 us)
